TPU v7x, 128 devices: a whole 4x4x4 slice. The times are simulated.
128 devices in a mesh: pool: 2 (over x_lo), seq: 16 (over x_hi, y, core), head: 4 (over z).
Axes of the slice: x: 4 (x_hi: 2, x_lo: 2; x = x_hi * 2 + x_lo), y: 4, z: 4, core: 2. Of those that a mesh axis runs over, the one named last changes fastest.
Arguments:
- prompt: bfloat16 [8, 2048, 8192], P('pool', 'seq'), may hold values from -6 to 6
- key_value_weight: bfloat16 [8192, 2, 1024], P('seq', None, 'head'), may hold values from -0.0625 to 0.0625
- adapter_down_weight: bfloat16 [8192, 256], P('seq'), may hold values from -0.0625 to 0.0625
- adapter_up_weight: bfloat16 [8, 2, 16, 1024], P(None, None, None, 'head'), may hold values from -0.75 to 0.75
- request_adapter_index: int32 [8], P('pool'), may hold values from 0 to 7
- destination: int32 [8], replicated, may hold values from 0 to 15, as said below
- rotated_query: bfloat16 [1536, 8192], P(('pool', 'seq'), 'head'), may hold values from -150 to 150
- key_value_cache: bfloat16 [1536, 128, 2, 1024], P(('pool', 'seq'), None, None, 'head'), may hold values from -6 to 6
- current_key_value: bfloat16 [1536, 2, 1024], P(('pool', 'seq'), None, 'head'), may hold values from -6 to 6
- cached_length: int32 [1536], P(('pool', 'seq')), may hold values from 1 to 128
- row_adapter_index: int32 [1536], P('pool'), may hold values from 0 to 7
- output_weight: bfloat16 [8192, 8192], P('head', 'seq'), may hold values from -0.0625 to 0.0625
- output_down_weight: bfloat16 [8192, 8, 16], P('head'), may hold values from -0.0625 to 0.0625
- output_up_weight: bfloat16 [8, 16, 8192], P(None, None, 'seq'), may hold values from -3.59375 to 3.59375
Outputs:
- handed: bfloat16 [32, 2, 2048, 2, 1024], P(('pool', 'seq'), None, None, None, 'head')
- decoded: bfloat16 [1536, 8192], P(('pool', 'head'), 'seq')
Inputs may be any that keep to these rules, and one draw needn't show every extreme that they name: `destination`: among one pool's 4 requests no decode owner is named more than 2 times, and some owner exactly 2 times; in each pool owners 0 and 15 both receive requests.
All inputs are finite; a program needn't handle non-finite values.
Results may differ from a plain program's by a relative error of at most 0.0085.
Values may be sent and summed in bfloat16 or wider, within the bound.
No kernel may reach another device: no remote copies, remote signals or barrier semaphores. Data moves between devices by JAX's collectives and lax.ppermute only.
A program may use at most 128 MiB of HBM per device.

v0:
```python
import math

import jax
import jax.numpy as jnp
from jax import lax
from jax.sharding import PartitionSpec as P

HEAD_DIM = 128
ADAPTER_RANK = 16
ADAPTER_COUNT = 8
CAP = 2


def side_by_side(arrays, axis, dim, along):
    widths = [math.prod(a.shape[along:]) for a in arrays]
    both = jnp.concatenate(
        [a.reshape(*a.shape[:along], w) for a, w in zip(arrays, widths)], axis=along
    )
    result = lax.all_gather(both, axis, axis=dim, tiled=True)
    pieces = jnp.split(result, [sum(widths[:k]) for k in range(1, len(widths))], axis=along)
    return tuple(
        (b.reshape(*result.shape[:along], *a.shape[along:]) for a, b in zip(arrays, pieces))
    )


def swapped(value, axis, distance):
    mask = 2**distance
    pairs = [(source, source ^ mask) for source in range(lax.axis_size(axis))]
    return lax.ppermute(value, axis, pairs)


def attend_local(query_matrix, key_value_cache, prefill_state, lengths):
    decode_count = query_matrix.shape[0]
    kv_heads = key_value_cache.shape[-1] // HEAD_DIM
    query_groups = query_matrix.shape[1] // HEAD_DIM // kv_heads
    positions = key_value_cache.shape[1]
    query_batch = query_matrix.reshape(decode_count, kv_heads, query_groups, HEAD_DIM)
    key_matrix = key_value_cache[:, :, 0].reshape(decode_count, positions, kv_heads, HEAD_DIM)
    value_matrix = key_value_cache[:, :, 1].reshape(decode_count, positions, kv_heads, HEAD_DIM)
    prefill_key = prefill_state[:, 0].reshape(decode_count, kv_heads, HEAD_DIM)
    prefill_value = prefill_state[:, 1].reshape(decode_count, kv_heads, HEAD_DIM)
    factor = HEAD_DIM ** (-0.5)
    scores = (
        jnp.einsum("rkgd,rckd->rkgc", query_batch, key_matrix, preferred_element_type=jnp.float32)
        * factor
    )
    own_score = (
        jnp.einsum("rkgd,rkd->rkg", query_batch, prefill_key, preferred_element_type=jnp.float32)
        * factor
    )
    valid = (jnp.arange(positions, dtype=jnp.int32)[None, :] < lengths[:, None])[:, None, None, :]
    highest = jnp.maximum(jnp.max(jnp.where(valid, scores, -1e30), axis=-1), own_score)
    raw = jnp.where(valid, jnp.exp(scores - highest[..., None]), 0.0)
    own_raw = jnp.exp(own_score - highest)
    normer = jnp.sum(raw, axis=-1) + own_raw
    weights = (raw / normer[..., None]).astype(jnp.bfloat16)
    own_weight = (own_raw / normer).astype(jnp.bfloat16)
    mixed = jnp.einsum("rkgc,rckd->rkgd", weights, value_matrix, preferred_element_type=jnp.float32)
    mixed = (
        mixed
        + own_weight.astype(jnp.float32)[..., None]
        * prefill_value.astype(jnp.float32)[:, :, None, :]
    )
    return mixed.reshape(decode_count, kv_heads * query_groups * HEAD_DIM).astype(jnp.bfloat16)


def place_slots(owner_ids, block, decoders):
    requests = block.shape[0]
    order_index = jnp.arange(requests, dtype=jnp.int32)
    same_owner = owner_ids[:, None] == owner_ids[None, :]
    slot_of = jnp.sum(
        (same_owner & (order_index[None, :] < order_index[:, None])).astype(jnp.int32), axis=1
    )
    slot_hit = slot_of[None, :] == jnp.arange(CAP, dtype=jnp.int32)[:, None]
    owner_hit = owner_ids[None, :] == jnp.arange(decoders, dtype=jnp.int32)[:, None]
    placer = (slot_hit[:, None, :] & owner_hit[None, :, :]).astype(jnp.bfloat16)
    flat = block.reshape(requests, block.shape[1] * block.shape[2] * block.shape[3])
    outgoing = jnp.einsum("cdr,rx->cdx", placer, flat, preferred_element_type=jnp.float32)
    return outgoing.astype(jnp.bfloat16).reshape(
        CAP, decoders, block.shape[1], block.shape[2], block.shape[3]
    )


def body(
    prompt,
    key_value_weight,
    adapter_down_weight,
    adapter_up_weight,
    request_adapter_index,
    destination,
    rotated_query,
    key_value_cache,
    current_key_value,
    cached_length,
    row_adapter_index,
    output_weight,
    output_down_weight,
    output_up_weight,
):
    requests, tok_dev, model_width = prompt.shape
    key_value_width = key_value_weight.shape[2]
    token_matrix = prompt.reshape(requests * tok_dev, model_width)
    weight_rows, lowered_rows = side_by_side((key_value_weight, adapter_down_weight), "seq", 0, 1)
    decode_count = weight_rows.shape[0]
    base_part = jnp.dot(
        token_matrix,
        weight_rows.reshape(decode_count, 2 * key_value_width),
        preferred_element_type=jnp.float32,
    )
    low_part = jnp.dot(token_matrix, lowered_rows, preferred_element_type=jnp.float32)
    reduced_everything = low_part
    adapter_selector = (
        request_adapter_index[:, None] == jnp.arange(ADAPTER_COUNT, dtype=jnp.int32)[None, :]
    )
    reduced_everything = reduced_everything.reshape(
        requests, tok_dev, ADAPTER_COUNT, 2, ADAPTER_RANK
    )
    low_rank = jnp.sum(
        jnp.where(adapter_selector[:, None, :, None, None], reduced_everything, 0.0), axis=2
    )
    selected_up_weight = jnp.einsum(
        "um,mdzt->udzt",
        adapter_selector.astype(jnp.bfloat16),
        adapter_up_weight,
        preferred_element_type=jnp.float32,
    )
    correction = jnp.einsum("rtkq,rkqf->rtkf", low_rank, selected_up_weight)
    prefilled = (base_part.reshape(requests, tok_dev, 2, key_value_width) + correction).astype(
        jnp.bfloat16
    )
    decoders = lax.axis_size("seq")
    pool_index = lax.axis_index("pool")
    other_owners = lax.dynamic_slice_in_dim(destination, (1 - pool_index) * requests, requests)
    arrived = swapped(prefilled, "pool", 0)
    outgoing = place_slots(other_owners, arrived, decoders)
    handed = lax.all_to_all(outgoing, "seq", split_axis=1, concat_axis=1, tiled=True)
    handed = handed.reshape(1, CAP, decoders * tok_dev, 2, key_value_width)
    attended = attend_local(rotated_query, key_value_cache, current_key_value, cached_length)
    down_flat = output_down_weight.reshape(
        output_down_weight.shape[0], ADAPTER_COUNT * ADAPTER_RANK
    )
    up_flat = output_up_weight.reshape(
        ADAPTER_COUNT * ADAPTER_RANK, output_up_weight.shape[2]
    ).astype(jnp.float32)
    rank_owner = jnp.arange(ADAPTER_COUNT * ADAPTER_RANK, dtype=jnp.int32) // ADAPTER_RANK
    attn_rows = lax.all_gather(attended, "seq", axis=0, tiled=True)
    low_rows = jnp.dot(attn_rows, down_flat, preferred_element_type=jnp.float32)
    low_rows = jnp.where(row_adapter_index[:, None] == rank_owner[None, :], low_rows, 0.0)
    projected = jnp.dot(attn_rows, output_weight, preferred_element_type=jnp.float32)
    terms = projected + jnp.dot(low_rows, up_flat)
    decoded = lax.psum_scatter(terms, "head", scatter_dimension=0, tiled=True)
    return (handed, decoded.astype(jnp.bfloat16))


def solution(mesh):
    in_specs = (
        P("pool", "seq", None),
        P("seq", None, "head"),
        P("seq", None),
        P(None, None, None, "head"),
        P("pool"),
        P(),
        P(("pool", "seq"), "head"),
        P(("pool", "seq"), None, None, "head"),
        P(("pool", "seq"), None, "head"),
        P(("pool", "seq")),
        P("pool"),
        P("head", "seq"),
        P("head", None, None),
        P(None, None, "seq"),
    )
    out_specs = (P(("pool", "seq"), None, None, None, "head"), P(("pool", "head"), "seq"))
    return jax.shard_map(body, mesh=mesh, in_specs=in_specs, out_specs=out_specs, check_vma=False)
```

profile of v0, /device:TPU:27, one launch (start us, length us, event | category | flops | bytes accessed | tf_op | source)
XLA Modules:
  0.0 271.1 jit_solution(11845594747030804117)
XLA Ops:
  7.2 1.3 copy.101
  8.5 1.9 pad_maximum_fusion
  10.5 0.0 all-gather.5.cloned.1.call-start
  10.5 13.9 %fusion.39 = (bf16[48,128,1,256]{3,2,1,0:T(2,128)(2,1)}, bf16[48,128,1,256]{3,2,1,0:T(2,128)(2,1)}) fusion(bf16[48,128,2,256]{3,2,1,0:T(2,128)(2,1)} %param.21), kind=kLoop, calls=%fused_computation.61 | loop fusion | bytes 12582912 | tf_op jit(solution)/shard_map/slice | solution.py:38
  24.4 13.6 %copy.99 = bf16[48,128,1,256]{1,3,0,2:T(8,128)(2,1)} copy(bf16[48,128,1,256]{3,2,1,0:T(2,128)(2,1)} %get-tuple-element.10) | data formatting | bytes 6291456
  38.1 0.1 iota_compare_fusion
  38.1 2.9 %select_reduce_fusion.1 = (f32[48,2,8]{2,1,0:T(2,128)S(1)}, f32[48,2,8,128]{3,2,1,0:T(8,128)S(1)}) fusion(pred[48,128]{1,0:T(8,128)(4,1)S(1)} %iota_compare_fusion, bf16[48,2,8,128]{3,2,1,0:T(8,128)(2,1)S(1)} %bitcast.71, bf16[48,128,2,128]{1,3,2,0:T(8,128)(2,1)} %bitcast.68), kind=kOutput, calls=%fused_computation.19 | convolution fusion | flops 25459968 | bytes 3744768 | tf_op jit(solution)/shard_map/rkgd,rckd->rkgc/dot_general | solution.py:44
  41.1 0.1 copy.86
  41.1 0.2 fusion.26
  41.4 0.1 copy.97
  41.5 0.1 copy.87
  41.6 0.4 fusion.14
  42.0 0.1 copy.88
  42.0 0.1 copy.89
  42.2 0.1 copy.92
  42.3 13.6 %copy.100 = bf16[48,128,1,256]{1,3,0,2:T(8,128)(2,1)} copy(bf16[48,128,1,256]{3,2,1,0:T(2,128)(2,1)} %get-tuple-element.11) | data formatting | bytes 6291456
  55.9 0.1 slice_convert_fusion
  56.0 3.7 %fusion.12 = bf16[48,2,8,128]{3,2,1,0:T(8,128)(2,1)S(1)} fusion(bf16[48,128,2,128]{1,3,2,0:T(8,128)(2,1)} %bitcast.69, f32[48,2,8,128]{3,2,1,0:T(8,128)S(1)} %get-tuple-element.15, f32[48,2,128]{2,1,0:T(2,128)S(1)} %bitcast.79, f32[48,2,8]{2,1,0:T(2,128)S(1)} %copy.92, f32[48,2,8]{2,1,0:T(2,128)S(1)} %copy.89, f32[48,2,8]{2,1,0:T(2,128)S(1)} %copy.87, ...), kind=kOutput, calls=%fused_computation.14 | convolution fusion | flops 25853952 | bytes 3800064 | tf_op jit(solution)/shard_map/rkgc,rckd->rkgd/dot_general | solution.py:58
  59.7 0.7 copy.112
  60.5 0.1 iota_compare_fusion.1
  60.6 0.1 copy.77
  60.7 0.1 dynamic_slice.3
  60.7 0.2 convert_reduce_fusion
  60.9 0.2 fusion.23
  61.2 39.8 %all-gather.3.cloned.1.call-done = bf16[8192,768]{1,0:T(8,128)(2,1)} async-done(((bf16[512,768]{1,0:T(8,128)(2,1)}), bf16[8192,768]{1,0:T(8,128)(2,1)}) %all-gather.3.cloned.1.call-update) | async-done | bytes 12582928 | tf_op jit(solution)/shard_map/all_gather | solution.py:19
  101.0 11.3 %fusion.4 = f32[512,512]{0,1:T(8,128)} fusion(bf16[512,8192]{1,0:T(8,128)(2,1)} %bitcast.80, bf16[8192,768]{1,0:T(8,128)(2,1)} %all-gather.3.cloned.1.call-done), kind=kOutput, calls=%fused_computation.6 | convolution fusion | flops 4294967296 | bytes 17825792 | tf_op jit(solution)/shard_map/dot_general | solution.py:105
  112.3 1.6 reshape.136
  113.9 8.0 %fusion.9 = f32[512,256]{0,1:T(8,128)} fusion(bf16[512,8192]{1,0:T(8,128)(2,1)} %bitcast.81, bf16[8192,768]{1,0:T(8,128)(2,1)} %all-gather.3.cloned.1.call-done), kind=kOutput, calls=%fused_computation.10 | convolution fusion | flops 2147483648 | bytes 13107200 | tf_op jit(solution)/shard_map/dot_general | solution.py:110
  121.8 2.0 reshape.137
  123.8 1.2 select_reduce_fusion
  125.1 0.4 fusion.8
  125.4 1.2 collective-permute-start
  126.7 0.1 iota_compare_fusion.2
  126.7 14.3 %collective-permute-done = bf16[4,128,2,256]{1,3,2,0:T(8,128)(2,1)S(1)} collective-permute-done((bf16[4,128,2,256]{1,3,2,0:T(8,128)(2,1)S(1)}, bf16[4,128,2,256]{1,3,2,0:T(8,128)(2,1)S(1)}, u32[]{:S(2)}, u32[]{:S(2)}) %collective-permute-start) | collective-permute-done | bytes 524320 | tf_op jit(solution)/shard_map/ppermute | solution.py:29
  141.0 0.5 copy.81
  141.5 0.3 reshape.146
  141.8 3.1 %convolution_convert_fusion = bf16[2,16,65536]{2,1,0:T(8,128)(2,1)} fusion(bf16[4,65536,1]{1,0,2:T(4,128)(2,1)S(1)} %reshape.146, pred[16,4]{0,1:T(4,128)(4,1)S(1)} %iota_compare_fusion.2, pred[2,4]{1,0:T(4,128)(4,1)S(1)} %iota_compare_fusion.4), kind=kOutput, calls=%fused_computation | convolution fusion | flops 18874496 | bytes 4718664 | tf_op jit(solution)/shard_map/cdr,rx->cdx/dot_general | solution.py:78
  144.9 6.5 %reshape.139 = bf16[2,16,128,2,256]{4,3,2,1,0:T(2,128)(2,1)} reshape(bf16[2,16,65536]{2,1,0:T(8,128)(2,1)} %convolution_convert_fusion) | data formatting | bytes 8388608 | tf_op jit(solution)/shard_map/reshape | solution.py:79
  151.4 9.3 %copy.82 = bf16[2,16,128,2,256]{4,3,2,0,1:T(2,128)(2,1)} copy(bf16[2,16,128,2,256]{4,3,2,1,0:T(2,128)(2,1)} %reshape.139) | data formatting | bytes 8388608 | tf_op jit(solution)/shard_map/reshape | solution.py:79
  160.7 10.6 %all-to-all-start = ((bf16[2,16,128,2,256]{4,3,2,0,1:T(2,128)(2,1)}), bf16[2,16,128,2,256]{4,3,2,0,1:T(2,128)(2,1)}, u32[]{:S(2)}, u32[]{:S(2)}) async-start(bf16[2,16,128,2,256]{4,3,2,0,1:T(2,128)(2,1)} %copy.82), calls=%async_computation | async-start | bytes 8388608 | tf_op jit(solution)/shard_map/all_to_all | solution.py:136
  171.4 0.0 reduce-scatter.2.cloned.1.call-start
  171.4 4.9 %fusion.40 = f32[768,512]{1,0:T(8,128)} fusion(bf16[768,2048]{1,0:T(8,128)(2,1)} %all-gather.5.cloned.1.call-done, bf16[2048,512]{1,0:T(8,128)(2,1)S(1)} %copy-done), kind=kOutput, calls=%fused_computation.62 | convolution fusion | flops 1610612736 | bytes 6815744 | tf_op jit(solution)/shard_map/dot_general | solution.py:149
  176.4 5.0 %convolution_add_fusion = f32[768,512]{1,0:T(8,128)} fusion(f32[768,512]{1,0:T(8,128)} %fusion.40, bf16[128,512]{1,0:T(8,128)(2,1)S(1)} %bitcast.78, bf16[768,2048]{1,0:T(8,128)(2,1)} %all-gather.5.cloned.1.call-done, bf16[2048,128]{0,1:T(8,128)(2,1)S(1)} %bitcast.74, s32[128]{0:T(128)S(1)} %and_select_fusion, s32[768]{0:T(1024)S(1)} %copy-done.6), kind=kOutput, calls=%fused_computation.5 | convolution fusion | flops 503906304 | bytes 6950400 | tf_op jit(solution)/shard_map/dot_general | solution.py:150
  181.4 26.8 %reduce-scatter.2.cloned.1.call-done = f32[192,512]{1,0:T(8,128)} async-done(((f32[768,512]{1,0:T(8,128)}), f32[192,512]{1,0:T(8,128)}) %reduce-scatter.2.cloned.1.call-update) | async-done | bytes 393232 | tf_op jit(solution)/shard_map/reduce_scatter | solution.py:151
  208.3 1.7 convert_element_type.50
  210.0 24.1 %all-to-all-done = bf16[2,16,128,2,256]{4,3,2,0,1:T(2,128)(2,1)} async-done(((bf16[2,16,128,2,256]{4,3,2,0,1:T(2,128)(2,1)}), bf16[2,16,128,2,256]{4,3,2,0,1:T(2,128)(2,1)}, u32[]{:S(2)}, u32[]{:S(2)}) %all-to-all-start) | async-done | bytes 4194336 | tf_op jit(solution)/shard_map/all_to_all | solution.py:136
  234.0 3.0 %copy.83 = bf16[2,16,128,2,256]{4,2,1,3,0:T(8,128)(2,1)S(1)} copy(bf16[2,16,128,2,256]{4,3,2,0,1:T(2,128)(2,1)} %all-to-all-done) | data formatting | bytes 8388608 | tf_op jit(solution)/shard_map/all_to_all | solution.py:136
  237.1 27.5 %copy.93 = bf16[1,2,2048,2,256]{4,3,2,1,0:T(2,128)(2,1)} copy(bf16[1,2,2048,2,256]{4,2,3,1,0:T(8,128)(2,1)S(1)} %bitcast.67) | data formatting | bytes 8388608
  (30 shorter events, 0.2 us)
Async XLA Ops:
  7.2 164.3 %copy-start = (bf16[2048,512]{1,0:T(8,128)(2,1)S(1)}, bf16[2048,512]{1,0:T(8,128)(2,1)}, u32[]{:S(2)}) copy-start(bf16[2048,512]{1,0:T(8,128)(2,1)} %param.25) | copy-start | bytes 6291460
  7.2 93.8 %all-gather.3.cloned.1.call-start = ((), (), s32[]{:S(2)}) async-start(), calls=%async_computation.2 | async-start | bytes 13369344 | tf_op jit(solution)/shard_map/all_gather | solution.py:19
  10.5 161.0 %all-gather.5.cloned.1.call-start = ((), (), s32[]{:S(2)}) async-start(), calls=%async_computation.3 | async-start | bytes 3342336 | tf_op jit(solution)/shard_map/all_gather | solution.py:146
  24.4 13.6 %copy-start.2 = (bf16[48,2048]{1,0:T(8,128)(2,1)S(1)}, bf16[48,2048]{1,0:T(8,128)(2,1)}, u32[]{:S(2)}) copy-start(bf16[48,2048]{1,0:T(8,128)(2,1)} %param.20) | copy-start | bytes 589828
  24.4 13.7 %copy-start.8 = (s32[48]{0:T(128)S(1)}, s32[48]{0:T(128)}, u32[]{:S(2)}) copy-start(s32[48]{0:T(128)} %param.23) | copy-start | bytes 580
  38.0 3.1 %copy-start.5 = (bf16[48,2,256]{2,1,0:T(2,128)(2,1)S(1)}, bf16[48,2,256]{2,1,0:T(2,128)(2,1)}, u32[]{:S(2)}) copy-start(bf16[48,2,256]{2,1,0:T(2,128)(2,1)} %param.22) | copy-start | bytes 147460
  56.0 4.5 %copy-start.7 = (s32[4]{0:T(128)S(1)}, s32[4]{0:T(128)}, u32[]{:S(2)}) copy-start(s32[4]{0:T(128)} %param.18) | copy-start | bytes 52
  56.0 4.7 %copy-start.9 = (s32[8]{0:T(128)S(1)}, s32[8]{0:T(128)}, u32[]{:S(2)}) copy-start(s32[8]{0:T(128)} %param.19) | copy-start | bytes 100
  56.0 5.0 %copy-start.4 = (bf16[8,2,16,256]{3,2,1,0:T(8,128)(2,1)S(1)}, bf16[8,2,16,256]{3,2,1,0:T(8,128)(2,1)}, u32[]{:S(2)}) copy-start(bf16[8,2,16,256]{3,2,1,0:T(8,128)(2,1)} %param.17) | copy-start | bytes 393220
  125.4 15.6 %collective-permute-start = (bf16[4,128,2,256]{1,3,2,0:T(8,128)(2,1)S(1)}, bf16[4,128,2,256]{1,3,2,0:T(8,128)(2,1)S(1)}, u32[]{:S(2)}, u32[]{:S(2)}) collective-permute-start(bf16[4,128,2,256]{1,3,2,0:T(8,128)(2,1)S(1)} %fusion.8), channel_id=1, source_target_pairs={{0,64},{64,0},{1,65},{65,1},{2,66},{66,2},{3,67},{67,3},{4,68},{68... | collective-permute-start | bytes 1572872 | tf_op jit(solution)/shard_map/ppermute | solution.py:29
  160.7 73.3 %all-to-all-start = ((bf16[2,16,128,2,256]{4,3,2,0,1:T(2,128)(2,1)}), bf16[2,16,128,2,256]{4,3,2,0,1:T(2,128)(2,1)}, u32[]{:S(2)}, u32[]{:S(2)}) async-start(bf16[2,16,128,2,256]{4,3,2,0,1:T(2,128)(2,1)} %copy.82), calls=%async_computation | async-start | bytes 8388608 | tf_op jit(solution)/shard_map/all_to_all | solution.py:136
  171.3 5.0 %copy-start.1 = (bf16[2048,8,16]{0,2,1:T(8,128)(2,1)S(1)}, bf16[2048,8,16]{0,2,1:T(8,128)(2,1)}, u32[]{:S(2)}) copy-start(bf16[2048,8,16]{0,2,1:T(8,128)(2,1)} %param.26) | copy-start | bytes 1572868
  171.3 5.0 %copy-start.3 = (bf16[8,16,512]{2,1,0:T(8,128)(2,1)S(1)}, bf16[8,16,512]{2,1,0:T(8,128)(2,1)}, u32[]{:S(2)}) copy-start(bf16[8,16,512]{2,1,0:T(8,128)(2,1)} %param.27) | copy-start | bytes 393220
  171.3 5.0 %copy-start.6 = (s32[768]{0:T(1024)S(1)}, s32[768]{0:T(1024)}, u32[]{:S(2)}) copy-start(s32[768]{0:T(1024)} %param.24) | copy-start | bytes 9220
  171.4 36.9 %reduce-scatter.2.cloned.1.call-start = ((), (), s32[]{:S(2)}) async-start(), calls=%async_computation.4 | async-start | bytes 1966080 | tf_op jit(solution)/shard_map/reduce_scatter | solution.py:151
Sparse Core Ops, SparseCore 0:
  10.6 90.3 all-gather.2
  104.0 51.1 all-gather.4
  181.5 26.6 reduce-scatter.1
where the time goes:
time: 272 us; the launch traced here: 271 us
  waiting for transfers between devices  105 us (39%)
  local copies, waits for them, and re-layouts  94.6 us (35%)
  matrix products  39.8 us (15%)
  between operations  14 us (5%)
  starting transfers between devices  11.9 us (4%)
  other arithmetic  5.72 us (2%)
    unnamed x26, local copies, waits for them, and re-layouts  56.8 us
    all_gather x1, waiting for transfers between devices, side_by_side(): result = lax.all_gather(both, axis, axis=dim, tiled=True)  39.8 us
    reduce_scatter x1, waiting for transfers between devices, body(): decoded = lax.psum_scatter(terms, 'head', scatter_dimension=0, tiled=True)  26.8 us
    all_to_all x1, waiting for transfers between devices, body(): lax.all_to_all(outgoing, 'seq', split_axis=1, concat_axis=1, tiled=True)  24.1 us
    reshape x2, local copies, waits for them, and re-layouts, place_slots(): outgoing.astype(jnp.bfloat16)  15.8 us
    ppermute x1, waiting for transfers between devices, swapped(): return lax.ppermute(value, axis, pairs)  14.3 us
    slice x1, local copies, waits for them, and re-layouts, attend_local(): key_value_cache[:, :, 0]  13.9 us
    dot_general x1, matrix products, body(): jnp.dot(token_matrix, weight_rows.reshape(decode_count, 2 * key_value_wid...  11.3 us
  transfers between devices with their start and end apart: 5, of which 4 were waited for; matrix products, arithmetic and copies ran while one was open for 39% of the time, Pallas kernels for 0%

commit v1 on v0

v1 whole, which is shorter than its diff:
```python
import jax
import jax.numpy as jnp
from jax import lax
from jax.experimental import pallas as pl
from jax.experimental.pallas import tpu as pltpu
from jax.sharding import Mesh
from jax.sharding import PartitionSpec as P

HEAD_DIM = 128
RANK = 16
ADAPTERS = 8
CAP = 2
REQ_POOL = 4
X_SLOTS = 3
MIB = 2**20


def params(limit=48):
    return pltpu.CompilerParams(vmem_limit_bytes=limit * MIB)


def x_shift(value, k):
    pairs = []
    for x in range(4):
        t = (x + k) % 4
        pairs.append(((x % 2) * 2 + x // 2, (t % 2) * 2 + t // 2))
    return lax.ppermute(value, ("pool", "xh"), pairs)


def y_shift(value, k):
    return lax.ppermute(value, "y", [(i, (i + k) % 4) for i in range(4)])


def core_swap(value):
    return lax.ppermute(value, "core", [(0, 1), (1, 0)])


def pack_kernel(meta, adapter, w_ref, d_ref, k_ref, v_ref, t_ref):
    k_ref[...] = w_ref[:, 0, :]
    v_ref[...] = w_ref[:, 1, :]
    column = lax.broadcasted_iota(jnp.int32, (256, 128), 0)
    lane = lax.broadcasted_iota(jnp.int32, (256, 128), 1)
    wanted = jnp.zeros((256, 128), jnp.int32)
    for r in range(REQ_POOL):
        wanted = jnp.where((lane >> 5) == r, adapter[r] * 32 + (lane & 31), wanted)
    pick = (column == wanted).astype(jnp.bfloat16)
    t_ref[...] = lax.dot_general(
        pick, d_ref[...], (((0,), (1,)), ((), ())), preferred_element_type=jnp.float32
    ).astype(jnp.bfloat16)


def pack(meta, adapter, weight, down):
    rows, half = weight.shape[0], weight.shape[0] // 2
    bf = jnp.bfloat16
    return pl.pallas_call(
        pack_kernel,
        grid_spec=pltpu.PrefetchScalarGridSpec(
            num_scalar_prefetch=2,
            grid=(1,),
            in_specs=[
                pl.BlockSpec((half, 2, 256), lambda i, m, a: (m[0], 0, 0)),
                pl.BlockSpec((rows, 256), lambda i, m, a: (0, 0)),
            ],
            out_specs=[
                pl.BlockSpec((half, 256), lambda i, m, a: (0, 0)),
                pl.BlockSpec((half, 256), lambda i, m, a: (0, 0)),
                pl.BlockSpec((128, rows), lambda i, m, a: (0, 0)),
            ],
        ),
        out_shape=[
            jax.ShapeDtypeStruct((half, 256), bf),
            jax.ShapeDtypeStruct((half, 256), bf),
            jax.ShapeDtypeStruct((128, rows), bf),
        ],
        compiler_params=params(),
        name="pack",
    )(meta, adapter, weight, down)


ROWS_STEP = 8


def attend_kernel(len_ref, q_ref, kv_ref, cur_ref, o_ref):
    first = pl.program_id(0) * ROWS_STEP
    factor = HEAD_DIM**-0.5
    lane = lax.broadcasted_iota(jnp.int32, (8, 256), 1)
    is_key = (lane & 1) == 0
    scores, own = [], []
    for i in range(ROWS_STEP):
        n = len_ref[first + i]
        valid = is_key & (lane < 2 * n)
        for h in range(2):
            both = kv_ref[i, :, :, h * 128 : (h + 1) * 128].reshape(256, 128)
            q = q_ref[i, h * 8 : (h + 1) * 8, :]
            s = lax.dot_general(
                q, both, (((1,), (1,)), ((), ())), preferred_element_type=jnp.float32
            )
            scores.append(jnp.where(valid, s * factor, -1e30))
            k = cur_ref[i, 0:1, h * 128 : (h + 1) * 128].astype(jnp.float32)
            own.append(jnp.sum(q.astype(jnp.float32) * k, axis=-1, keepdims=True) * factor)
    s = jnp.concatenate(scores, 0)
    o = jnp.concatenate(own, 0)
    highest = jnp.maximum(jnp.max(s, axis=-1, keepdims=True), o)
    raw = jnp.exp(s - highest)
    own_raw = jnp.exp(o - highest)
    norm = jnp.sum(raw, axis=-1, keepdims=True) + own_raw
    weights = pltpu.roll(raw / norm, 1, 1).astype(jnp.bfloat16)
    own_weight = (own_raw / norm).astype(jnp.bfloat16).astype(jnp.float32)
    for i in range(ROWS_STEP):
        for h in range(2):
            both = kv_ref[i, :, :, h * 128 : (h + 1) * 128].reshape(256, 128)
            j = (i * 2 + h) * 8
            v = cur_ref[i, 1:2, h * 128 : (h + 1) * 128].astype(jnp.float32)
            mixed = jnp.dot(weights[j : j + 8], both, preferred_element_type=jnp.float32)
            mixed = mixed + own_weight[j : j + 8] * v
            o_ref[i, h * 8 : (h + 1) * 8, :] = mixed.astype(jnp.bfloat16)


def attend(query, cache, current, lengths):
    rows = query.shape[0]
    heads = query.shape[1] // HEAD_DIM
    out = pl.pallas_call(
        attend_kernel,
        grid_spec=pltpu.PrefetchScalarGridSpec(
            num_scalar_prefetch=1,
            grid=(rows // ROWS_STEP,),
            in_specs=[
                pl.BlockSpec((ROWS_STEP, heads, 128), lambda g, n: (g, 0, 0)),
                pl.BlockSpec((ROWS_STEP, 128, 2, 256), lambda g, n: (g, 0, 0, 0)),
                pl.BlockSpec((ROWS_STEP, 2, 256), lambda g, n: (g, 0, 0)),
            ],
            out_specs=pl.BlockSpec((ROWS_STEP, heads, 128), lambda g, n: (g, 0, 0)),
        ),
        out_shape=jax.ShapeDtypeStruct((rows, heads, 128), jnp.bfloat16),
        compiler_params=params(),
        name="attend",
    )(lengths, query.reshape(rows, heads, 128), cache, current)
    return out.reshape(rows, heads * 128)


def split_dot(low, up):
    high = low.astype(jnp.bfloat16)
    rest = (low - high.astype(jnp.float32)).astype(jnp.bfloat16)
    return jnp.dot(high, up, preferred_element_type=jnp.float32) + jnp.dot(
        rest, up, preferred_element_type=jnp.float32
    )


def x_order(x):
    return [x, (x + 3) & 3, (x + 2) & 3, (x + 1) & 3]


def prefill_kernel(meta, adapter, dest, *refs):
    n_blocks = 16
    prompt, down, up = refs[0:3]
    blocks = refs[3 : 3 + n_blocks]
    near_ref, far_ref = refs[3 + n_blocks : 5 + n_blocks]
    p_buf, d_buf, u_buf, w_buf, res, sems, osem = refs[5 + n_blocks :]
    pool, xh, y, core = meta[0], meta[1], meta[2], meta[3]
    x = 2 * xh + pool
    copies = [
        pltpu.make_async_copy(prompt, p_buf, sems.at[16]),
        pltpu.make_async_copy(down, d_buf, sems.at[17]),
        pltpu.make_async_copy(up, u_buf, sems.at[18]),
    ]
    wcopies = [pltpu.make_async_copy(blocks[b], w_buf.at[b], sems.at[b]) for b in range(n_blocks)]
    copies[0].start()
    for c in wcopies:
        c.start()
    copies[1].start()
    copies[2].start()
    copies[0].wait()
    acc = [None, None]
    for b in range(n_blocks):
        wcopies[b].wait()
        kv = (b // 4) % 2
        c_of = core if b < 8 else 1 - core
        j = b % 4
        for i in range(4):
            xi = x_order(x)[i if kv == 0 else j]
            yi = x_order(y)[j if kv == 0 else i]
            shard = (xi >> 1) * 8 + yi * 2 + c_of
            at = pl.multiple_of(shard * 512 + (xi & 1) * 256, 256)
            part = jnp.dot(
                p_buf[:, pl.ds(at, 256)],
                w_buf[b, i * 256 : (i + 1) * 256, :],
                preferred_element_type=jnp.float32,
            )
            acc[kv] = part if acc[kv] is None else acc[kv] + part
    copies[1].wait()
    copies[2].wait()
    outs = []
    for r in range(REQ_POOL):
        rows = slice(r * 128, (r + 1) * 128)
        low = None
        for s in range(16):
            part = lax.dot_general(
                p_buf[rows, s * 512 : (s + 1) * 512],
                d_buf[s * 128 + r * 32 : s * 128 + (r + 1) * 32, :],
                (((1,), (1,)), ((), ())),
                preferred_element_type=jnp.float32,
            )
            low = part if low is None else low + part
        a = adapter[r]
        both = []
        for kv in range(2):
            value = acc[kv][rows] + split_dot(low[:, kv * 16 : (kv + 1) * 16], u_buf[a, kv])
            both.append(value.astype(jnp.bfloat16))
        res[r] = jnp.stack(both, axis=1)
    base = pool * REQ_POOL
    sides = [dest[base + r] >> 3 for r in range(REQ_POOL)]
    for r in range(REQ_POOL):
        slot = jnp.int32(0)
        for q in range(r):
            slot = slot + (sides[q] == sides[r]).astype(jnp.int32)

        @pl.when(sides[r] == xh)
        def _():
            pltpu.make_async_copy(res.at[r], near_ref.at[slot], osem.at[r]).start()

        @pl.when(sides[r] != xh)
        def _():
            pltpu.make_async_copy(res.at[r], far_ref.at[slot], osem.at[r]).start()

    for r in range(REQ_POOL):
        pltpu.make_async_copy(res.at[r], near_ref.at[0], osem.at[r]).wait()


def prefill(meta, adapter, dest, prompt, down, up, blocks):
    bf = jnp.bfloat16
    tokens, width = prompt.shape
    any_spec = pl.BlockSpec(memory_space=pl.ANY)
    shape = jax.ShapeDtypeStruct((X_SLOTS, 128, 2, 256), bf)
    return pl.pallas_call(
        prefill_kernel,
        grid_spec=pltpu.PrefetchScalarGridSpec(
            num_scalar_prefetch=3,
            grid=(1,),
            in_specs=[any_spec] * (3 + len(blocks)),
            out_specs=[any_spec, any_spec],
            scratch_shapes=[
                pltpu.VMEM((tokens, width), bf),
                pltpu.VMEM(down.shape, bf),
                pltpu.VMEM(up.shape, bf),
                pltpu.VMEM((len(blocks),) + blocks[0].shape, bf),
                pltpu.VMEM((REQ_POOL, 128, 2, 256), bf),
                pltpu.SemaphoreType.DMA((19,)),
                pltpu.SemaphoreType.DMA((REQ_POOL,)),
            ],
        ),
        out_shape=[shape, shape],
        compiler_params=params(56),
        name="prefill",
    )(meta, adapter, dest, prompt, down, up, *blocks)


def choose_kernel(meta, dest, *refs):
    ins, out, sems = refs[:8], refs[8], refs[9]
    pool, xh, y, core = meta[0], meta[1], meta[2], meta[3]
    index = slots_of(dest, 1 - pool, xh, xh * 8 + y * 2 + (1 - core))[0]
    copies = []
    for j in range(CAP):
        for b in range(8):
            copies.append(
                pltpu.make_async_copy(ins[b].at[index[j]], out.at[j, b], sems.at[j * 8 + b])
            )
    for c in copies:
        c.start()
    for c in copies:
        c.wait()


def slots_of(dest, pool, xh, owner):
    owners = [dest[pool * REQ_POOL + r] for r in range(REQ_POOL)]
    index = [jnp.int32(0)] * CAP
    used = [jnp.int32(0)] * CAP
    place, mine = jnp.int32(0), jnp.int32(0)
    for r in range(REQ_POOL):
        hit = (owners[r] == owner).astype(jnp.int32)
        for j in range(CAP):
            here = hit * (mine == j).astype(jnp.int32)
            index[j] = index[j] + here * place
            used[j] = used[j] + here
        mine = mine + hit
        place = place + ((owners[r] >> 3) == xh).astype(jnp.int32)
    return index, used


def choose(meta, dest, parts):
    any_spec = pl.BlockSpec(memory_space=pl.ANY)
    return pl.pallas_call(
        choose_kernel,
        grid_spec=pltpu.PrefetchScalarGridSpec(
            num_scalar_prefetch=2,
            grid=(1,),
            in_specs=[any_spec] * 8,
            out_specs=any_spec,
            scratch_shapes=[pltpu.SemaphoreType.DMA((16,))],
        ),
        out_shape=jax.ShapeDtypeStruct((CAP, 8, 128, 2, 256), jnp.bfloat16),
        compiler_params=params(),
        name="choose",
    )(meta, dest, *parts)


def place_kernel(meta, dest, *refs):
    ins, other, out, zero, sems = refs[:8], refs[8], refs[9], refs[10], refs[11]
    pool, xh, y, core = meta[0], meta[1], meta[2], meta[3]
    zero[...] = jnp.zeros_like(zero)
    index, used = slots_of(dest, 1 - pool, xh, xh * 8 + y * 2 + core)
    for j in range(CAP):
        for b in range(8):
            side = xh if b < 4 else 1 - xh
            row = x_order(y)[b % 4]
            mine = pl.multiple_of((side * 8 + row * 2 + core) * 128, 128)
            theirs = pl.multiple_of((side * 8 + row * 2 + (1 - core)) * 128, 128)

            @pl.when(used[j] == 1)
            def _():
                pltpu.make_async_copy(
                    ins[b].at[index[j]], out.at[0, j, pl.ds(mine, 128)], sems.at[j * 16 + b]
                ).start()
                pltpu.make_async_copy(
                    other.at[j, b], out.at[0, j, pl.ds(theirs, 128)], sems.at[j * 16 + 8 + b]
                ).start()

            @pl.when(used[j] == 0)
            def _():
                pltpu.make_async_copy(
                    zero, out.at[0, j, pl.ds(mine, 128)], sems.at[j * 16 + b]
                ).start()
                pltpu.make_async_copy(
                    zero, out.at[0, j, pl.ds(theirs, 128)], sems.at[j * 16 + 8 + b]
                ).start()

    for j in range(CAP):
        for b in range(16):
            pltpu.make_async_copy(zero, out.at[0, j, pl.ds(0, 128)], sems.at[j * 16 + b]).wait()


def place(meta, dest, parts, other):
    any_spec = pl.BlockSpec(memory_space=pl.ANY)
    return pl.pallas_call(
        place_kernel,
        grid_spec=pltpu.PrefetchScalarGridSpec(
            num_scalar_prefetch=2,
            grid=(1,),
            in_specs=[any_spec] * 9,
            out_specs=any_spec,
            scratch_shapes=[
                pltpu.VMEM((128, 2, 256), jnp.bfloat16),
                pltpu.SemaphoreType.DMA((32,)),
            ],
        ),
        out_shape=jax.ShapeDtypeStruct((1, CAP, 2048, 2, 256), jnp.bfloat16),
        compiler_params=params(),
        name="place",
    )(meta, dest, *parts, other)


def project_kernel(meta, keep_ref, down_ref, up_ref, w_ref, *refs):
    ins, out_ref, rows, sems = refs[:8], refs[8], refs[9], refs[10]
    xh, y, core = meta[1], meta[2], meta[3]
    copies = []
    for b in range(8):
        row = x_order(y)[b % 4]
        c_of = core if b < 4 else 1 - core
        for i in range(2):
            side = xh if i == 0 else 1 - xh
            at = pl.multiple_of((side * 8 + row * 2 + c_of) * 48, 16)
            copies.append(
                pltpu.make_async_copy(
                    ins[b].at[pl.ds(i * 48, 48)], rows.at[pl.ds(at, 48)], sems.at[b * 2 + i]
                )
            )
    for c in copies:
        c.start()
    for c in copies:
        c.wait()
    value = rows[...]
    low = lax.dot_general(
        value, down_ref[...], (((1,), (1,)), ((), ())), preferred_element_type=jnp.float32
    )
    owner = lax.broadcasted_iota(jnp.int32, low.shape, 1) >> 4
    low = jnp.where(keep_ref[...] == owner, low, 0.0)
    out = jnp.dot(value, w_ref[...], preferred_element_type=jnp.float32)
    out_ref[...] = (out + split_dot(low, up_ref[...])).astype(jnp.bfloat16)


def project(meta, keep, down, up, weight, parts):
    any_spec = pl.BlockSpec(memory_space=pl.ANY)
    rows = 768

    def whole(shape):
        return pl.BlockSpec(shape, lambda i, m: (0,) * len(shape))

    return pl.pallas_call(
        project_kernel,
        grid_spec=pltpu.PrefetchScalarGridSpec(
            num_scalar_prefetch=1,
            grid=(1,),
            in_specs=[
                whole(keep.shape),
                whole(down.shape),
                whole(up.shape),
                whole(weight.shape),
            ]
            + [any_spec] * 8,
            out_specs=whole((rows, weight.shape[1])),
            scratch_shapes=[
                pltpu.VMEM((rows, weight.shape[0]), jnp.bfloat16),
                pltpu.SemaphoreType.DMA((16,)),
            ],
        ),
        out_shape=jax.ShapeDtypeStruct((rows, weight.shape[1]), jnp.bfloat16),
        compiler_params=params(),
        name="project",
    )(meta, keep, down, up, weight, *parts)


def ring(value, shift):
    return [value, shift(value, 1), shift(value, 2), shift(value, -1)]


def body(
    prompt,
    key_value_weight,
    adapter_down_weight,
    adapter_up_weight,
    request_adapter_index,
    destination,
    rotated_query,
    key_value_cache,
    current_key_value,
    cached_length,
    row_adapter_index,
    output_weight,
    output_down_weight,
    output_up_weight,
):
    meta = jnp.stack([lax.axis_index(a) for a in ("pool", "xh", "y", "core")]).astype(jnp.int32)
    keys, values, low_down = pack(
        meta, request_adapter_index, key_value_weight, adapter_down_weight
    )
    all_down = lax.all_gather(low_down, ("xh", "y", "core"), axis=0, tiled=True)
    key_rows = jnp.concatenate(ring(keys, x_shift), 0)
    value_rows = jnp.concatenate(ring(values, y_shift), 0)
    near = ring(key_rows, y_shift) + ring(value_rows, x_shift)
    blocks = near + [core_swap(b) for b in near]

    attended = attend(rotated_query, key_value_cache, current_key_value, cached_length)
    across = lax.ppermute(attended, "xh", [(0, 1), (1, 0)])
    mine = ring(jnp.concatenate([attended, across], 0), y_shift)
    parts = mine + [core_swap(b) for b in mine]
    ranks = ADAPTERS * RANK
    down = jnp.transpose(output_down_weight, (1, 2, 0)).reshape(ranks, -1)
    up = output_up_weight.reshape(ranks, -1)
    partial = project(meta, row_adapter_index[:, None], down, up, output_weight, parts)
    shares = lax.all_to_all(partial, "head", split_axis=0, concat_axis=0, tiled=True)
    shares = shares.reshape(4, -1, partial.shape[1]).astype(jnp.float32)
    decoded = (shares[0] + shares[1] + shares[2] + shares[3]).astype(jnp.bfloat16)

    tokens = prompt.reshape(-1, prompt.shape[2])
    same, other = prefill(
        meta, request_adapter_index, destination, tokens, all_down, adapter_up_weight, blocks
    )
    b0 = lax.ppermute(same, "pool", [(0, 1), (1, 0)])
    a0 = lax.ppermute(other, ("pool", "xh"), [(i, 3 - i) for i in range(4)])
    b1, b3 = y_shift(b0, 1), y_shift(b0, -1)
    a1, a3 = y_shift(a0, 1), y_shift(a0, -1)
    b2, a2 = y_shift(b1, 1), y_shift(a3, -1)
    held = [b0, b1, b2, b3, a0, a1, a2, a3]
    theirs = core_swap(choose(meta, destination, held))
    handed = place(meta, destination, held, theirs)
    return handed, decoded


def solution(mesh):
    fine = Mesh(mesh.devices.reshape(2, 2, 4, 2, 4), ("pool", "xh", "y", "core", "head"))
    seq = ("xh", "y", "core")
    every = ("pool",) + seq
    in_specs = (
        P("pool", seq, None),
        P(seq, None, "head"),
        P(seq, None),
        P(None, None, None, "head"),
        P("pool"),
        P(),
        P(every, "head"),
        P(every, None, None, "head"),
        P(every, None, "head"),
        P(every),
        P("pool"),
        P("head", seq),
        P("head", None, None),
        P(None, None, seq),
    )
    out_specs = (P(every, None, None, None, "head"), P(("pool", "head"), seq))
    return jax.shard_map(body, mesh=fine, in_specs=in_specs, out_specs=out_specs, check_vma=False)
```

time: 272 us -> 198 us (0.73)
  the two profiles are of different devices: /device:TPU:27 before, /device:TPU:1 now
where the time goes in v1:
time: 198 us; the launch traced here: 197 us
  waiting for transfers between devices  63.2 us (32%)
  starting transfers between devices  49.7 us (25%)
  Pallas kernels  49.6 us (25%)
  blocking collectives  15.4 us (8%)
  between operations  14.4 us (7%)
  local copies, waits for them, and re-layouts  3.96 us (2%)
    ppermute x15, waiting for transfers between devices, y_shift(): return lax.ppermute(value, 'y', [(i, (i + k) % 4) for i in range(4)])  24.6 us
    ppermute x15, starting transfers between devices, y_shift(): return lax.ppermute(value, 'y', [(i, (i + k) % 4) for i in range(4)])  21.5 us
    pallas_call x1, Pallas kernels, prefill(): pl.pallas_call(prefill_kernel, grid_spec=pltpu.PrefetchScalarGridSpec(num...  20.4 us
    ppermute x6, waiting for transfers between devices, x_shift(): return lax.ppermute(value, ('pool', 'xh'), pairs)  20.1 us
    ppermute x13, starting transfers between devices, core_swap(): return lax.ppermute(value, 'core', [(0, 1), (1, 0)])  16.5 us
    all_to_all x1, blocking collectives, body(): lax.all_to_all(partial, 'head', split_axis=0, concat_axis=0, tiled=True)  15.4 us
    pallas_call x1, Pallas kernels, project(): pl.pallas_call(project_kernel, grid_spec=pltpu.PrefetchScalarGridSpec(num...  11.5 us
    ppermute x1, waiting for transfers between devices, body(): b0 = lax.ppermute(same, 'pool', [(0, 1), (1, 0)])  9.67 us
  transfers between devices with their start and end apart: 38, of which 14 were waited for; matrix products, arithmetic and copies ran while one was open for 1% of the time, Pallas kernels for 12%

profile of v1, /device:TPU:1, one launch (start us, length us, event | category | flops | bytes accessed | tf_op | source)
XLA Modules:
  0.0 197.4 jit_solution(995764222194553010)
XLA Ops:
  7.3 1.0 copy-done.1
  8.3 0.9 copy-done.2
  9.9 2.2 %pack.1 = (bf16[256,256]{1,0:T(8,128)(2,1)S(1)}, bf16[256,256]{1,0:T(8,128)(2,1)S(1)}, bf16[128,512]{1,0:T(8,128)(2,1)}) custom-call(s32[4]{0:T(128)S(1)} %pad_add_fusion.meta, s32[4]{0:T(128)S(1)} %copy-done.8, bf16[512,2,256]{2,1,0:T(2,128)(2,1)S(1)} %copy-done.1, bf16[512,256]{1,0:T(8,128)(2,1)S(1)} %copy-done.2), custom_call_target="tpu_custom_call" | custom-call | tf_op jit(solution)/shard_map/pack/pallas_call | solution.py:55
  12.2 2.2 %collective-permute-start.6 = (bf16[256,256]{1,0:T(8,128)(2,1)S(1)}, bf16[256,256]{1,0:T(8,128)(2,1)S(1)}, u32[]{:S(2)}, u32[]{:S(2)}) collective-permute-start(bf16[256,256]{1,0:T(8,128)(2,1)S(1)} %get-tuple-element.9), channel_id=1, source_target_pairs={{0,8},{8,16},{16,24},{24,0},{1,9},{9,17},{17,25},{25,1},{2,10},{10... | collective-permute-start | bytes 393224 | tf_op jit(solution)/shard_map/ppermute | solution.py:31
  14.4 2.6 %collective-permute-start.7 = (bf16[256,256]{1,0:T(8,128)(2,1)S(1)}, bf16[256,256]{1,0:T(8,128)(2,1)S(1)}, u32[]{:S(2)}, u32[]{:S(2)}) collective-permute-start(bf16[256,256]{1,0:T(8,128)(2,1)S(1)} %get-tuple-element.9), channel_id=1, source_target_pairs={{0,16},{8,24},{16,0},{24,8},{1,17},{9,25},{17,1},{25,9},{2,18},{10... | collective-permute-start | bytes 393224 | tf_op jit(solution)/shard_map/ppermute | solution.py:31
  17.0 1.1 collective-permute-start.8
  18.0 1.2 collective-permute-start
  19.3 2.5 %collective-permute-start.1 = (bf16[256,256]{1,0:T(8,128)(2,1)S(1)}, bf16[256,256]{1,0:T(8,128)(2,1)S(1)}, u32[]{:S(2)}, u32[]{:S(2)}) collective-permute-start(bf16[256,256]{1,0:T(8,128)(2,1)S(1)} %get-tuple-element.8), channel_id=1, source_target_pairs={{0,32},{64,96},{32,0},{96,64},{1,33},{65,97},{33,1},{97,65},{2,34}... | collective-permute-start | bytes 393224 | tf_op jit(solution)/shard_map/ppermute | solution.py:27
  21.7 1.2 collective-permute-start.2
  23.0 1.0 collective-permute-start.9
  24.0 2.5 %collective-permute-start.10 = (bf16[1024,256]{1,0:T(8,128)(2,1)S(1)}, bf16[1024,256]{1,0:T(8,128)(2,1)S(1)}, u32[]{:S(2)}, u32[]{:S(2)}) collective-permute-start(bf16[1024,256]{1,0:T(8,128)(2,1)S(1)} %constant_dynamic-update-slice_fusion.4.refs_7_), channel_id=1, source_target_pairs={{0,32},{64,96},{32,0},{96,64},{1,33},{65,97},{33,1},{97,65},{2,34}... | collective-permute-start | bytes 1572872 | tf_op jit(solution)/shard_map/ppermute | solution.py:27
  26.5 1.2 collective-permute-start.11
  27.7 1.1 collective-permute-start.3
  28.8 2.3 %collective-permute-start.4 = (bf16[1024,256]{1,0:T(8,128)(2,1)S(1)}, bf16[1024,256]{1,0:T(8,128)(2,1)S(1)}, u32[]{:S(2)}, u32[]{:S(2)}) collective-permute-start(bf16[1024,256]{1,0:T(8,128)(2,1)S(1)} %constant_dynamic-update-slice_fusion.refs_3_), channel_id=1, source_target_pairs={{0,16},{8,24},{16,0},{24,8},{1,17},{9,25},{17,1},{25,9},{2,18},{10... | collective-permute-start | bytes 1572872 | tf_op jit(solution)/shard_map/ppermute | solution.py:31
  31.1 8.5 %collective-permute-done.9.refs_8_ = bf16[1024,256]{1,0:T(8,128)(2,1)S(1)} collective-permute-done((bf16[1024,256]{1,0:T(8,128)(2,1)S(1)}, bf16[1024,256]{1,0:T(8,128)(2,1)S(1)}, u32[]{:S(2)}, u32[]{:S(2)}) %collective-permute-start.9) | collective-permute-done | bytes 524320 | tf_op jit(solution)/shard_map/ppermute | solution.py:27
  39.7 11.5 %collective-permute-done.10.refs_9_ = bf16[1024,256]{1,0:T(8,128)(2,1)S(1)} collective-permute-done((bf16[1024,256]{1,0:T(8,128)(2,1)S(1)}, bf16[1024,256]{1,0:T(8,128)(2,1)S(1)}, u32[]{:S(2)}, u32[]{:S(2)}) %collective-permute-start.10) | collective-permute-done | bytes 524320 | tf_op jit(solution)/shard_map/ppermute | solution.py:27
  51.2 1.6 collective-permute-start.16
  53.4 3.3 %collective-permute-start.18 = (bf16[1024,256]{1,0:T(8,128)(2,1)S(1)}, bf16[1024,256]{1,0:T(8,128)(2,1)S(1)}, u32[]{:S(2)}, u32[]{:S(2)}) collective-permute-start(bf16[1024,256]{1,0:T(8,128)(2,1)S(1)} %collective-permute-done.10.refs_9_), channel_id=1, source_target_pairs={{0,4},{4,0},{1,5},{5,1},{2,6},{6,2},{3,7},{7,3},{8,12},{12,8},{9,1... | collective-permute-start | bytes 1572872 | tf_op jit(solution)/shard_map/ppermute | solution.py:35
  56.7 4.9 %collective-permute-start.19 = (bf16[1024,256]{1,0:T(8,128)(2,1)S(1)}, bf16[1024,256]{1,0:T(8,128)(2,1)S(1)}, u32[]{:S(2)}, u32[]{:S(2)}) collective-permute-start(bf16[1024,256]{1,0:T(8,128)(2,1)S(1)} %collective-permute-done.11.refs_10_), channel_id=1, source_target_pairs={{0,4},{4,0},{1,5},{5,1},{2,6},{6,2},{3,7},{7,3},{8,12},{12,8},{9,1... | collective-permute-start | bytes 1572872 | tf_op jit(solution)/shard_map/ppermute | solution.py:35
  62.4 0.7 collective-permute-done.19.refs_18_
  63.1 1.6 collective-permute-done.13.refs_12_
  64.7 0.8 collective-permute-done.14.refs_13_
  65.5 0.8 copy-done.24
  66.4 3.8 %all-gather.2.cloned.1.call-done.refs_1_ = bf16[2048,512]{1,0:T(8,128)(2,1)} async-done(((bf16[128,512]{1,0:T(8,128)(2,1)}), bf16[2048,512]{1,0:T(8,128)(2,1)}) %all-gather.2.cloned.1.call-update) | async-done | bytes 2097168 | tf_op jit(solution)/shard_map/all_gather | solution.py:445
  70.2 20.4 %prefill.1 = (bf16[3,128,2,256]{3,2,1,0:T(2,128)(2,1)}, bf16[3,128,2,256]{3,2,1,0:T(2,128)(2,1)}) custom-call(s32[4]{0:T(128)} %copy-done.5, s32[4]{0:T(128)} %adapter.3, s32[8]{0:T(128)} %dest.5, bf16[512,8192]{1,0:T(8,128)(2,1)} %bitcast.26, bf16[2048,512]{1,0:T(8,128)(2,1)} %all-gather.2.cloned.1.call-done.refs_1_, bf16[8,2,16,256]{3,2,1,0:T(8,128)(2,1)} %refs_2_.1, ...), custom_call_target="tpu_custom_call" | custom-call | tf_op jit(solution)/shard_map/prefill/pallas_call | solution.py:234
  91.0 0.7 collective-permute-start.24
  91.7 9.7 %collective-permute-done.20.refs_0_ = bf16[3,128,2,256]{3,2,1,0:T(2,128)(2,1)S(1)} collective-permute-done((bf16[3,128,2,256]{3,2,1,0:T(2,128)(2,1)}, bf16[3,128,2,256]{3,2,1,0:T(2,128)(2,1)S(1)}, u32[]{:S(2)}, u32[]{:S(2)}) %collective-permute-start.20) | collective-permute-done | bytes 393248 | tf_op jit(solution)/shard_map/ppermute | solution.py:467
  101.4 0.9 collective-permute-start.21
  102.6 2.1 %collective-permute-start.26 = (bf16[3,128,2,256]{3,2,1,0:T(2,128)(2,1)S(1)}, bf16[3,128,2,256]{3,2,1,0:T(2,128)(2,1)S(1)}, u32[]{:S(2)}, u32[]{:S(2)}) collective-permute-start(bf16[3,128,2,256]{3,2,1,0:T(2,128)(2,1)S(1)} %collective-permute-done.24.refs_4_), channel_id=1, source_target_pairs={{0,24},{8,0},{16,8},{24,16},{1,25},{9,1},{17,9},{25,17},{2,26},{10... | collective-permute-start | bytes 1179656 | tf_op jit(solution)/shard_map/ppermute | solution.py:31
  105.0 1.2 collective-permute-start.25
  106.1 6.0 %collective-permute-done.21.refs_1_ = bf16[3,128,2,256]{3,2,1,0:T(2,128)(2,1)S(1)} collective-permute-done((bf16[3,128,2,256]{3,2,1,0:T(2,128)(2,1)S(1)}, bf16[3,128,2,256]{3,2,1,0:T(2,128)(2,1)S(1)}, u32[]{:S(2)}, u32[]{:S(2)}) %collective-permute-start.21) | collective-permute-done | bytes 393248 | tf_op jit(solution)/shard_map/ppermute | solution.py:31
  112.1 3.0 %collective-permute-start.27 = (bf16[3,128,2,256]{3,2,1,0:T(2,128)(2,1)S(1)}, bf16[3,128,2,256]{3,2,1,0:T(2,128)(2,1)S(1)}, u32[]{:S(2)}, u32[]{:S(2)}) collective-permute-start(bf16[3,128,2,256]{3,2,1,0:T(2,128)(2,1)S(1)} %collective-permute-done.26.refs_7_), channel_id=1, source_target_pairs={{0,24},{8,0},{16,8},{24,16},{1,25},{9,1},{17,9},{25,17},{2,26},{10... | collective-permute-start | bytes 1179656 | tf_op jit(solution)/shard_map/ppermute | solution.py:31
  115.2 9.2 %attend.1 = bf16[48,16,128]{2,1,0:T(8,128)(2,1)S(1)} custom-call(s32[48]{0:T(128)S(1)} %copy-done.9, bf16[48,16,128]{2,1,0:T(8,128)(2,1)S(1)} %bitcast.23, bf16[48,128,2,256]{3,2,1,0:T(2,128)(2,1)} %kv_ref.1, bf16[48,2,256]{2,1,0:T(2,128)(2,1)S(1)} %copy-done.4), custom_call_target="tpu_custom_call" | custom-call | tf_op jit(solution)/shard_map/attend/pallas_call | solution.py:122
  124.5 1.1 collective-permute-start.29
  125.6 3.4 %collective-permute-done.22.refs_2_ = bf16[3,128,2,256]{3,2,1,0:T(2,128)(2,1)S(1)} collective-permute-done((bf16[3,128,2,256]{3,2,1,0:T(2,128)(2,1)S(1)}, bf16[3,128,2,256]{3,2,1,0:T(2,128)(2,1)S(1)}, u32[]{:S(2)}, u32[]{:S(2)}) %collective-permute-start.22) | collective-permute-done | bytes 393248 | tf_op jit(solution)/shard_map/ppermute | solution.py:31
  129.0 3.5 %choose.1 = bf16[2,8,128,2,256]{4,3,2,1,0:T(2,128)(2,1)S(1)} custom-call(s32[4]{0:T(128)S(1)} %copy-done.6, s32[8]{0:T(128)S(1)} %copy-done.7, bf16[3,128,2,256]{3,2,1,0:T(2,128)(2,1)S(1)} %collective-permute-done.20.refs_0_, bf16[3,128,2,256]{3,2,1,0:T(2,128)(2,1)S(1)} %collective-permute-done.21.refs_1_, ...), custom_call_target="tpu_custom_call" | custom-call | tf_op jit(solution)/shard_map/choose/pallas_call | solution.py:291
  132.5 2.1 %collective-permute-start.28 = (bf16[2,8,128,2,256]{4,3,2,1,0:T(2,128)(2,1)S(1)}, bf16[2,8,128,2,256]{4,3,2,1,0:T(2,128)(2,1)S(1)}, u32[]{:S(2)}, u32[]{:S(2)}) collective-permute-start(bf16[2,8,128,2,256]{4,3,2,1,0:T(2,128)(2,1)S(1)} %choose.1), channel_id=1, source_target_pairs={{0,4},{4,0},{1,5},{5,1},{2,6},{6,2},{3,7},{7,3},{8,12},{12,8},{9,1... | collective-permute-start | bytes 6291464 | tf_op jit(solution)/shard_map/ppermute | solution.py:35
  134.6 1.2 collective-permute-start.30
  135.8 3.6 %collective-permute-start.31 = (bf16[96,2048]{1,0:T(8,128)(2,1)S(1)}, bf16[96,2048]{1,0:T(8,128)(2,1)S(1)}, u32[]{:S(2)}, u32[]{:S(2)}) collective-permute-start(bf16[96,2048]{1,0:T(8,128)(2,1)S(1)} %constant_dynamic-update-slice_fusion.8.refs_0_), channel_id=1, source_target_pairs={{0,16},{8,24},{16,0},{24,8},{1,17},{9,25},{17,1},{25,9},{2,18},{10... | collective-permute-start | bytes 1179656 | tf_op jit(solution)/shard_map/ppermute | solution.py:31
  139.9 6.4 %collective-permute-done.30.refs_1_ = bf16[96,2048]{1,0:T(8,128)(2,1)S(1)} collective-permute-done((bf16[96,2048]{1,0:T(8,128)(2,1)S(1)}, bf16[96,2048]{1,0:T(8,128)(2,1)S(1)}, u32[]{:S(2)}, u32[]{:S(2)}) %collective-permute-start.30) | collective-permute-done | bytes 393248 | tf_op jit(solution)/shard_map/ppermute | solution.py:31
  146.3 2.0 collective-permute-start.34
  148.3 8.8 %collective-permute-done.31.refs_2_ = bf16[96,2048]{1,0:T(8,128)(2,1)S(1)} collective-permute-done((bf16[96,2048]{1,0:T(8,128)(2,1)S(1)}, bf16[96,2048]{1,0:T(8,128)(2,1)S(1)}, u32[]{:S(2)}, u32[]{:S(2)}) %collective-permute-start.31) | collective-permute-done | bytes 393248 | tf_op jit(solution)/shard_map/ppermute | solution.py:31
  157.1 0.8 collective-permute-start.35
  158.1 1.2 collective-permute-done.35.refs_6_
  159.8 11.5 %project.1 = bf16[768,512]{1,0:T(8,128)(2,1)S(1)} custom-call(s32[4]{0:T(128)S(1)} %copy-done.6, s32[768,1]{1,0:T(8,128)S(1)} %broadcast_in_dim.4.keep_ref, bf16[128,2048]{1,0:T(8,128)(2,1)S(1)} %bitcast.24, bf16[128,512]{1,0:T(8,128)(2,1)S(1)} %bitcast.25, bf16[2048,512]{1,0:T(8,128)(2,1)} %w_ref.3, ...), custom_call_target="tpu_custom_call" | custom-call | tf_op jit(solution)/shard_map/project/pallas_call | solution.py:397
  171.3 15.4 %all_to_all.9 = bf16[4,192,512]{2,1,0:T(8,128)(2,1)S(1)} all-to-all(bf16[4,192,512]{2,1,0:T(8,128)(2,1)S(1)} %bitcast.20), channel_id=1, replica_groups=mesh['pool'=2,'xh'=2,'y'=4,'core'=2,'head'=4] {'head'}, dimensions={0} | all-to-all | bytes 1572864 | tf_op jit(solution)/shard_map/all_to_all | solution.py:459
  186.9 0.8 fusion.1
  187.7 2.8 %place.1 = bf16[1,2,2048,2,256]{4,3,2,1,0:T(2,128)(2,1)} custom-call(s32[4]{0:T(128)S(1)} %copy-done.6, s32[8]{0:T(128)S(1)} %copy-done.7, bf16[3,128,2,256]{3,2,1,0:T(2,128)(2,1)S(1)} %collective-permute-done.20.refs_0_, bf16[3,128,2,256]{3,2,1,0:T(2,128)(2,1)S(1)} %collective-permute-done.21.refs_1_, ...), custom_call_target="tpu_custom_call" | custom-call | tf_op jit(solution)/shard_map/place/pallas_call | solution.py:343
  (106 shorter events, 5.0 us)
Async XLA Ops:
  7.2 63.0 %all-gather.2.cloned.1.call-start = ((), (), s32[]{:S(2)}) async-start(), calls=%async_computation.1 | async-start | bytes 2228224 | tf_op jit(solution)/shard_map/all_gather | solution.py:445
  9.9 60.2 %copy-start.5 = (s32[4]{0:T(128)}, s32[4]{0:T(128)S(1)}, u32[]{:S(2)}) copy-start(s32[4]{0:T(128)S(1)} %pad_add_fusion.meta) | copy-start | bytes 52
  12.2 9.6 %collective-permute-start.6 = (bf16[256,256]{1,0:T(8,128)(2,1)S(1)}, bf16[256,256]{1,0:T(8,128)(2,1)S(1)}, u32[]{:S(2)}, u32[]{:S(2)}) collective-permute-start(bf16[256,256]{1,0:T(8,128)(2,1)S(1)} %get-tuple-element.9), channel_id=1, source_target_pairs={{0,8},{8,16},{16,24},{24,0},{1,9},{9,17},{17,25},{25,1},{2,10},{10... | collective-permute-start | bytes 393224 | tf_op jit(solution)/shard_map/ppermute | solution.py:31
  14.4 8.6 %collective-permute-start.7 = (bf16[256,256]{1,0:T(8,128)(2,1)S(1)}, bf16[256,256]{1,0:T(8,128)(2,1)S(1)}, u32[]{:S(2)}, u32[]{:S(2)}) collective-permute-start(bf16[256,256]{1,0:T(8,128)(2,1)S(1)} %get-tuple-element.9), channel_id=1, source_target_pairs={{0,16},{8,24},{16,0},{24,8},{1,17},{9,25},{17,1},{25,9},{2,18},{10... | collective-permute-start | bytes 393224 | tf_op jit(solution)/shard_map/ppermute | solution.py:31
  17.0 6.0 %collective-permute-start.8 = (bf16[256,256]{1,0:T(8,128)(2,1)S(1)}, bf16[256,256]{1,0:T(8,128)(2,1)S(1)}, u32[]{:S(2)}, u32[]{:S(2)}) collective-permute-start(bf16[256,256]{1,0:T(8,128)(2,1)S(1)} %get-tuple-element.9), channel_id=1, source_target_pairs={{0,24},{8,0},{16,8},{24,16},{1,25},{9,1},{17,9},{25,17},{2,26},{10... | collective-permute-start | bytes 393224 | tf_op jit(solution)/shard_map/ppermute | solution.py:31
  18.0 8.4 %collective-permute-start = (bf16[256,256]{1,0:T(8,128)(2,1)S(1)}, bf16[256,256]{1,0:T(8,128)(2,1)S(1)}, u32[]{:S(2)}, u32[]{:S(2)}) collective-permute-start(bf16[256,256]{1,0:T(8,128)(2,1)S(1)} %get-tuple-element.8), channel_id=1, source_target_pairs={{0,64},{64,32},{32,96},{96,0},{1,65},{65,33},{33,97},{97,1},{2,66}... | collective-permute-start | bytes 393224 | tf_op jit(solution)/shard_map/ppermute | solution.py:27
  19.3 8.4 %collective-permute-start.1 = (bf16[256,256]{1,0:T(8,128)(2,1)S(1)}, bf16[256,256]{1,0:T(8,128)(2,1)S(1)}, u32[]{:S(2)}, u32[]{:S(2)}) collective-permute-start(bf16[256,256]{1,0:T(8,128)(2,1)S(1)} %get-tuple-element.8), channel_id=1, source_target_pairs={{0,32},{64,96},{32,0},{96,64},{1,33},{65,97},{33,1},{97,65},{2,34}... | collective-permute-start | bytes 393224 | tf_op jit(solution)/shard_map/ppermute | solution.py:27
  21.7 5.9 %collective-permute-start.2 = (bf16[256,256]{1,0:T(8,128)(2,1)S(1)}, bf16[256,256]{1,0:T(8,128)(2,1)S(1)}, u32[]{:S(2)}, u32[]{:S(2)}) collective-permute-start(bf16[256,256]{1,0:T(8,128)(2,1)S(1)} %get-tuple-element.8), channel_id=1, source_target_pairs={{0,96},{64,0},{32,64},{96,32},{1,97},{65,1},{33,65},{97,33},{2,98}... | collective-permute-start | bytes 393224 | tf_op jit(solution)/shard_map/ppermute | solution.py:27
  23.0 47.1 %copy-start.11 = (bf16[1024,256]{1,0:T(8,128)(2,1)}, bf16[1024,256]{1,0:T(8,128)(2,1)S(1)}, u32[]{:S(2)}) copy-start(bf16[1024,256]{1,0:T(8,128)(2,1)S(1)} %constant_dynamic-update-slice_fusion.4.refs_7_) | copy-start | bytes 1572868
  23.0 16.6 %collective-permute-start.9 = (bf16[1024,256]{1,0:T(8,128)(2,1)S(1)}, bf16[1024,256]{1,0:T(8,128)(2,1)S(1)}, u32[]{:S(2)}, u32[]{:S(2)}) collective-permute-start(bf16[1024,256]{1,0:T(8,128)(2,1)S(1)} %constant_dynamic-update-slice_fusion.4.refs_7_), channel_id=1, source_target_pairs={{0,64},{64,32},{32,96},{96,0},{1,65},{65,33},{33,97},{97,1},{2,66}... | collective-permute-start | bytes 1572872 | tf_op jit(solution)/shard_map/ppermute | solution.py:27
  24.0 27.2 %collective-permute-start.10 = (bf16[1024,256]{1,0:T(8,128)(2,1)S(1)}, bf16[1024,256]{1,0:T(8,128)(2,1)S(1)}, u32[]{:S(2)}, u32[]{:S(2)}) collective-permute-start(bf16[1024,256]{1,0:T(8,128)(2,1)S(1)} %constant_dynamic-update-slice_fusion.4.refs_7_), channel_id=1, source_target_pairs={{0,32},{64,96},{32,0},{96,64},{1,33},{65,97},{33,1},{97,65},{2,34}... | collective-permute-start | bytes 1572872 | tf_op jit(solution)/shard_map/ppermute | solution.py:27
  26.5 26.4 %collective-permute-start.11 = (bf16[1024,256]{1,0:T(8,128)(2,1)S(1)}, bf16[1024,256]{1,0:T(8,128)(2,1)S(1)}, u32[]{:S(2)}, u32[]{:S(2)}) collective-permute-start(bf16[1024,256]{1,0:T(8,128)(2,1)S(1)} %constant_dynamic-update-slice_fusion.4.refs_7_), channel_id=1, source_target_pairs={{0,96},{64,0},{32,64},{96,32},{1,97},{65,1},{33,65},{97,33},{2,98}... | collective-permute-start | bytes 1572872 | tf_op jit(solution)/shard_map/ppermute | solution.py:27
  27.7 42.5 %copy-start.10 = (bf16[1024,256]{1,0:T(8,128)(2,1)}, bf16[1024,256]{1,0:T(8,128)(2,1)S(1)}, u32[]{:S(2)}) copy-start(bf16[1024,256]{1,0:T(8,128)(2,1)S(1)} %constant_dynamic-update-slice_fusion.refs_3_) | copy-start | bytes 1572868
  27.7 25.3 %collective-permute-start.3 = (bf16[1024,256]{1,0:T(8,128)(2,1)S(1)}, bf16[1024,256]{1,0:T(8,128)(2,1)S(1)}, u32[]{:S(2)}, u32[]{:S(2)}) collective-permute-start(bf16[1024,256]{1,0:T(8,128)(2,1)S(1)} %constant_dynamic-update-slice_fusion.refs_3_), channel_id=1, source_target_pairs={{0,8},{8,16},{16,24},{24,0},{1,9},{9,17},{17,25},{25,1},{2,10},{10... | collective-permute-start | bytes 1572872 | tf_op jit(solution)/shard_map/ppermute | solution.py:31
  28.8 24.6 %collective-permute-start.4 = (bf16[1024,256]{1,0:T(8,128)(2,1)S(1)}, bf16[1024,256]{1,0:T(8,128)(2,1)S(1)}, u32[]{:S(2)}, u32[]{:S(2)}) collective-permute-start(bf16[1024,256]{1,0:T(8,128)(2,1)S(1)} %constant_dynamic-update-slice_fusion.refs_3_), channel_id=1, source_target_pairs={{0,16},{8,24},{16,0},{24,8},{1,17},{9,25},{17,1},{25,9},{2,18},{10... | collective-permute-start | bytes 1572872 | tf_op jit(solution)/shard_map/ppermute | solution.py:31
  39.6 30.5 %copy-start.12 = (bf16[1024,256]{1,0:T(8,128)(2,1)}, bf16[1024,256]{1,0:T(8,128)(2,1)S(1)}, u32[]{:S(2)}) copy-start(bf16[1024,256]{1,0:T(8,128)(2,1)S(1)} %collective-permute-done.9.refs_8_) | copy-start | bytes 1572868
  39.6 17.1 %collective-permute-start.5 = (bf16[1024,256]{1,0:T(8,128)(2,1)S(1)}, bf16[1024,256]{1,0:T(8,128)(2,1)S(1)}, u32[]{:S(2)}, u32[]{:S(2)}) collective-permute-start(bf16[1024,256]{1,0:T(8,128)(2,1)S(1)} %constant_dynamic-update-slice_fusion.refs_3_), channel_id=1, source_target_pairs={{0,24},{8,0},{16,8},{24,16},{1,25},{9,1},{17,9},{25,17},{2,26},{10... | collective-permute-start | bytes 1572872 | tf_op jit(solution)/shard_map/ppermute | solution.py:31
  51.2 10.3 %collective-permute-start.16 = (bf16[1024,256]{1,0:T(8,128)(2,1)S(1)}, bf16[1024,256]{1,0:T(8,128)(2,1)S(1)}, u32[]{:S(2)}, u32[]{:S(2)}) collective-permute-start(bf16[1024,256]{1,0:T(8,128)(2,1)S(1)} %constant_dynamic-update-slice_fusion.4.refs_7_), channel_id=1, source_target_pairs={{0,4},{4,0},{1,5},{5,1},{2,6},{6,2},{3,7},{7,3},{8,12},{12,8},{9,1... | collective-permute-start | bytes 1572872 | tf_op jit(solution)/shard_map/ppermute | solution.py:35
  52.8 8.8 %collective-permute-start.12 = (bf16[1024,256]{1,0:T(8,128)(2,1)S(1)}, bf16[1024,256]{1,0:T(8,128)(2,1)S(1)}, u32[]{:S(2)}, u32[]{:S(2)}) collective-permute-start(bf16[1024,256]{1,0:T(8,128)(2,1)S(1)} %constant_dynamic-update-slice_fusion.refs_3_), channel_id=1, source_target_pairs={{0,4},{4,0},{1,5},{5,1},{2,6},{6,2},{3,7},{7,3},{8,12},{12,8},{9,1... | collective-permute-start | bytes 1572872 | tf_op jit(solution)/shard_map/ppermute | solution.py:35
  53.0 9.1 %collective-permute-start.17 = (bf16[1024,256]{1,0:T(8,128)(2,1)S(1)}, bf16[1024,256]{1,0:T(8,128)(2,1)S(1)}, u32[]{:S(2)}, u32[]{:S(2)}) collective-permute-start(bf16[1024,256]{1,0:T(8,128)(2,1)S(1)} %collective-permute-done.9.refs_8_), channel_id=1, source_target_pairs={{0,4},{4,0},{1,5},{5,1},{2,6},{6,2},{3,7},{7,3},{8,12},{12,8},{9,1... | collective-permute-start | bytes 1572872 | tf_op jit(solution)/shard_map/ppermute | solution.py:35
  53.4 9.0 %collective-permute-start.18 = (bf16[1024,256]{1,0:T(8,128)(2,1)S(1)}, bf16[1024,256]{1,0:T(8,128)(2,1)S(1)}, u32[]{:S(2)}, u32[]{:S(2)}) collective-permute-start(bf16[1024,256]{1,0:T(8,128)(2,1)S(1)} %collective-permute-done.10.refs_9_), channel_id=1, source_target_pairs={{0,4},{4,0},{1,5},{5,1},{2,6},{6,2},{3,7},{7,3},{8,12},{12,8},{9,1... | collective-permute-start | bytes 1572872 | tf_op jit(solution)/shard_map/ppermute | solution.py:35
  56.7 6.4 %collective-permute-start.19 = (bf16[1024,256]{1,0:T(8,128)(2,1)S(1)}, bf16[1024,256]{1,0:T(8,128)(2,1)S(1)}, u32[]{:S(2)}, u32[]{:S(2)}) collective-permute-start(bf16[1024,256]{1,0:T(8,128)(2,1)S(1)} %collective-permute-done.11.refs_10_), channel_id=1, source_target_pairs={{0,4},{4,0},{1,5},{5,1},{2,6},{6,2},{3,7},{7,3},{8,12},{12,8},{9,1... | collective-permute-start | bytes 1572872 | tf_op jit(solution)/shard_map/ppermute | solution.py:35
  61.6 3.1 %collective-permute-start.13 = (bf16[1024,256]{1,0:T(8,128)(2,1)S(1)}, bf16[1024,256]{1,0:T(8,128)(2,1)S(1)}, u32[]{:S(2)}, u32[]{:S(2)}) collective-permute-start(bf16[1024,256]{1,0:T(8,128)(2,1)S(1)} %collective-permute-done.3.refs_4_), channel_id=1, source_target_pairs={{0,4},{4,0},{1,5},{5,1},{2,6},{6,2},{3,7},{7,3},{8,12},{12,8},{9,1... | collective-permute-start | bytes 1572872 | tf_op jit(solution)/shard_map/ppermute | solution.py:35
  61.7 3.8 %collective-permute-start.14 = (bf16[1024,256]{1,0:T(8,128)(2,1)S(1)}, bf16[1024,256]{1,0:T(8,128)(2,1)S(1)}, u32[]{:S(2)}, u32[]{:S(2)}) collective-permute-start(bf16[1024,256]{1,0:T(8,128)(2,1)S(1)} %collective-permute-done.4.refs_5_), channel_id=1, source_target_pairs={{0,4},{4,0},{1,5},{5,1},{2,6},{6,2},{3,7},{7,3},{8,12},{12,8},{9,1... | collective-permute-start | bytes 1572872 | tf_op jit(solution)/shard_map/ppermute | solution.py:35
  62.1 4.3 %collective-permute-start.15 = (bf16[1024,256]{1,0:T(8,128)(2,1)S(1)}, bf16[1024,256]{1,0:T(8,128)(2,1)}, u32[]{:S(2)}, u32[]{:S(2)}) collective-permute-start(bf16[1024,256]{1,0:T(8,128)(2,1)S(1)} %collective-permute-done.5.refs_6_), channel_id=1, source_target_pairs={{0,4},{4,0},{1,5},{5,1},{2,6},{6,2},{3,7},{7,3},{8,12},{12,8},{9,1... | collective-permute-start | bytes 1572872 | tf_op jit(solution)/shard_map/ppermute | solution.py:35
  70.2 44.9 %copy-start.25 = (bf16[48,2048]{1,0:T(8,128)(2,1)S(1)}, bf16[48,2048]{1,0:T(8,128)(2,1)}, u32[]{:S(2)}) copy-start(bf16[48,2048]{1,0:T(8,128)(2,1)} %param.20) | copy-start | bytes 589828
  70.2 44.9 %copy-start.4 = (bf16[48,2,256]{2,1,0:T(2,128)(2,1)S(1)}, bf16[48,2,256]{2,1,0:T(2,128)(2,1)}, u32[]{:S(2)}) copy-start(bf16[48,2,256]{2,1,0:T(2,128)(2,1)} %cur_ref.1) | copy-start | bytes 147460
  70.2 44.9 %copy-start.9 = (s32[48]{0:T(128)S(1)}, s32[48]{0:T(128)}, u32[]{:S(2)}) copy-start(s32[48]{0:T(128)} %len_ref.1) | copy-start | bytes 580
  90.6 10.8 %collective-permute-start.20 = (bf16[3,128,2,256]{3,2,1,0:T(2,128)(2,1)}, bf16[3,128,2,256]{3,2,1,0:T(2,128)(2,1)S(1)}, u32[]{:S(2)}, u32[]{:S(2)}) collective-permute-start(bf16[3,128,2,256]{3,2,1,0:T(2,128)(2,1)} %get-tuple-element.10), channel_id=1, source_target_pairs={{0,64},{64,0},{1,65},{65,1},{2,66},{66,2},{3,67},{67,3},{4,68},{68... | collective-permute-start | bytes 1179656 | tf_op jit(solution)/shard_map/ppermute | solution.py:467
  91.0 11.6 %collective-permute-start.24 = (bf16[3,128,2,256]{3,2,1,0:T(2,128)(2,1)}, bf16[3,128,2,256]{3,2,1,0:T(2,128)(2,1)S(1)}, u32[]{:S(2)}, u32[]{:S(2)}) collective-permute-start(bf16[3,128,2,256]{3,2,1,0:T(2,128)(2,1)} %get-tuple-element.11), channel_id=1, source_target_pairs={{0,96},{32,64},{64,32},{96,0},{1,97},{33,65},{65,33},{97,1},{2,98}... | collective-permute-start | bytes 1179656 | tf_op jit(solution)/shard_map/ppermute | solution.py:468
  101.4 10.7 %collective-permute-start.21 = (bf16[3,128,2,256]{3,2,1,0:T(2,128)(2,1)S(1)}, bf16[3,128,2,256]{3,2,1,0:T(2,128)(2,1)S(1)}, u32[]{:S(2)}, u32[]{:S(2)}) collective-permute-start(bf16[3,128,2,256]{3,2,1,0:T(2,128)(2,1)S(1)} %collective-permute-done.20.refs_0_), channel_id=1, source_target_pairs={{0,8},{8,16},{16,24},{24,0},{1,9},{9,17},{17,25},{25,1},{2,10},{10... | collective-permute-start | bytes 1179656 | tf_op jit(solution)/shard_map/ppermute | solution.py:31
  102.6 9.6 %collective-permute-start.26 = (bf16[3,128,2,256]{3,2,1,0:T(2,128)(2,1)S(1)}, bf16[3,128,2,256]{3,2,1,0:T(2,128)(2,1)S(1)}, u32[]{:S(2)}, u32[]{:S(2)}) collective-permute-start(bf16[3,128,2,256]{3,2,1,0:T(2,128)(2,1)S(1)} %collective-permute-done.24.refs_4_), channel_id=1, source_target_pairs={{0,24},{8,0},{16,8},{24,16},{1,25},{9,1},{17,9},{25,17},{2,26},{10... | collective-permute-start | bytes 1179656 | tf_op jit(solution)/shard_map/ppermute | solution.py:31
  104.7 20.9 %collective-permute-start.23 = (bf16[3,128,2,256]{3,2,1,0:T(2,128)(2,1)S(1)}, bf16[3,128,2,256]{3,2,1,0:T(2,128)(2,1)S(1)}, u32[]{:S(2)}, u32[]{:S(2)}) collective-permute-start(bf16[3,128,2,256]{3,2,1,0:T(2,128)(2,1)S(1)} %collective-permute-done.20.refs_0_), channel_id=1, source_target_pairs={{0,24},{8,0},{16,8},{24,16},{1,25},{9,1},{17,9},{25,17},{2,26},{10... | collective-permute-start | bytes 1179656 | tf_op jit(solution)/shard_map/ppermute | solution.py:31
  105.0 20.6 %collective-permute-start.25 = (bf16[3,128,2,256]{3,2,1,0:T(2,128)(2,1)S(1)}, bf16[3,128,2,256]{3,2,1,0:T(2,128)(2,1)S(1)}, u32[]{:S(2)}, u32[]{:S(2)}) collective-permute-start(bf16[3,128,2,256]{3,2,1,0:T(2,128)(2,1)S(1)} %collective-permute-done.24.refs_4_), channel_id=1, source_target_pairs={{0,8},{8,16},{16,24},{24,0},{1,9},{9,17},{17,25},{25,1},{2,10},{10... | collective-permute-start | bytes 1179656 | tf_op jit(solution)/shard_map/ppermute | solution.py:31
  112.1 16.9 %collective-permute-start.22 = (bf16[3,128,2,256]{3,2,1,0:T(2,128)(2,1)S(1)}, bf16[3,128,2,256]{3,2,1,0:T(2,128)(2,1)S(1)}, u32[]{:S(2)}, u32[]{:S(2)}) collective-permute-start(bf16[3,128,2,256]{3,2,1,0:T(2,128)(2,1)S(1)} %collective-permute-done.21.refs_1_), channel_id=1, source_target_pairs={{0,8},{8,16},{16,24},{24,0},{1,9},{9,17},{17,25},{25,1},{2,10},{10... | collective-permute-start | bytes 1179656 | tf_op jit(solution)/shard_map/ppermute | solution.py:31
  112.1 16.8 %collective-permute-start.27 = (bf16[3,128,2,256]{3,2,1,0:T(2,128)(2,1)S(1)}, bf16[3,128,2,256]{3,2,1,0:T(2,128)(2,1)S(1)}, u32[]{:S(2)}, u32[]{:S(2)}) collective-permute-start(bf16[3,128,2,256]{3,2,1,0:T(2,128)(2,1)S(1)} %collective-permute-done.26.refs_7_), channel_id=1, source_target_pairs={{0,24},{8,0},{16,8},{24,16},{1,25},{9,1},{17,9},{25,17},{2,26},{10... | collective-permute-start | bytes 1179656 | tf_op jit(solution)/shard_map/ppermute | solution.py:31
  124.4 33.4 %copy-start.26 = (s32[768]{0:T(1024)S(1)}, s32[768]{0:T(1024)}, u32[]{:S(2)}) copy-start(s32[768]{0:T(1024)} %param.24) | copy-start | bytes 9220
  124.4 35.3 %copy-start = (bf16[2048,8,16]{0,2,1:T(8,128)(2,1)S(1)}, bf16[2048,8,16]{0,2,1:T(8,128)(2,1)}, u32[]{:S(2)}) copy-start(bf16[2048,8,16]{0,2,1:T(8,128)(2,1)} %param.26) | copy-start | bytes 1572868
  124.4 35.3 %copy-start.3 = (bf16[8,16,512]{2,1,0:T(8,128)(2,1)S(1)}, bf16[8,16,512]{2,1,0:T(8,128)(2,1)}, u32[]{:S(2)}) copy-start(bf16[8,16,512]{2,1,0:T(8,128)(2,1)} %param.27) | copy-start | bytes 393220
  124.5 10.1 %collective-permute-start.29 = (bf16[48,2048]{1,0:T(8,128)(2,1)S(1)}, bf16[48,2048]{1,0:T(8,128)(2,1)S(1)}, u32[]{:S(2)}, u32[]{:S(2)}) collective-permute-start(bf16[48,2048]{1,0:T(8,128)(2,1)S(1)} %bitcast.28), channel_id=1, source_target_pairs={{0,32},{32,0},{1,33},{33,1},{2,34},{34,2},{3,35},{35,3},{4,36},{36... | collective-permute-start | bytes 589832 | tf_op jit(solution)/shard_map/ppermute | solution.py:452
  132.5 55.2 %collective-permute-start.28 = (bf16[2,8,128,2,256]{4,3,2,1,0:T(2,128)(2,1)S(1)}, bf16[2,8,128,2,256]{4,3,2,1,0:T(2,128)(2,1)S(1)}, u32[]{:S(2)}, u32[]{:S(2)}) collective-permute-start(bf16[2,8,128,2,256]{4,3,2,1,0:T(2,128)(2,1)S(1)} %choose.1), channel_id=1, source_target_pairs={{0,4},{4,0},{1,5},{5,1},{2,6},{6,2},{3,7},{7,3},{8,12},{12,8},{9,1... | collective-permute-start | bytes 6291464 | tf_op jit(solution)/shard_map/ppermute | solution.py:35
  134.6 11.7 %collective-permute-start.30 = (bf16[96,2048]{1,0:T(8,128)(2,1)S(1)}, bf16[96,2048]{1,0:T(8,128)(2,1)S(1)}, u32[]{:S(2)}, u32[]{:S(2)}) collective-permute-start(bf16[96,2048]{1,0:T(8,128)(2,1)S(1)} %constant_dynamic-update-slice_fusion.8.refs_0_), channel_id=1, source_target_pairs={{0,8},{8,16},{16,24},{24,0},{1,9},{9,17},{17,25},{25,1},{2,10},{10... | collective-permute-start | bytes 1179656 | tf_op jit(solution)/shard_map/ppermute | solution.py:31
  135.8 21.3 %collective-permute-start.31 = (bf16[96,2048]{1,0:T(8,128)(2,1)S(1)}, bf16[96,2048]{1,0:T(8,128)(2,1)S(1)}, u32[]{:S(2)}, u32[]{:S(2)}) collective-permute-start(bf16[96,2048]{1,0:T(8,128)(2,1)S(1)} %constant_dynamic-update-slice_fusion.8.refs_0_), channel_id=1, source_target_pairs={{0,16},{8,24},{16,0},{24,8},{1,17},{9,25},{17,1},{25,9},{2,18},{10... | collective-permute-start | bytes 1179656 | tf_op jit(solution)/shard_map/ppermute | solution.py:31
  139.4 18.5 %collective-permute-start.32 = (bf16[96,2048]{1,0:T(8,128)(2,1)S(1)}, bf16[96,2048]{1,0:T(8,128)(2,1)S(1)}, u32[]{:S(2)}, u32[]{:S(2)}) collective-permute-start(bf16[96,2048]{1,0:T(8,128)(2,1)S(1)} %constant_dynamic-update-slice_fusion.8.refs_0_), channel_id=1, source_target_pairs={{0,24},{8,0},{16,8},{24,16},{1,25},{9,1},{17,9},{25,17},{2,26},{10... | collective-permute-start | bytes 1179656 | tf_op jit(solution)/shard_map/ppermute | solution.py:31
  139.4 18.7 %collective-permute-start.33 = (bf16[96,2048]{1,0:T(8,128)(2,1)S(1)}, bf16[96,2048]{1,0:T(8,128)(2,1)S(1)}, u32[]{:S(2)}, u32[]{:S(2)}) collective-permute-start(bf16[96,2048]{1,0:T(8,128)(2,1)S(1)} %constant_dynamic-update-slice_fusion.8.refs_0_), channel_id=1, source_target_pairs={{0,4},{4,0},{1,5},{5,1},{2,6},{6,2},{3,7},{7,3},{8,12},{12,8},{9,1... | collective-permute-start | bytes 1179656 | tf_op jit(solution)/shard_map/ppermute | solution.py:35
  146.3 11.7 %collective-permute-start.34 = (bf16[96,2048]{1,0:T(8,128)(2,1)S(1)}, bf16[96,2048]{1,0:T(8,128)(2,1)S(1)}, u32[]{:S(2)}, u32[]{:S(2)}) collective-permute-start(bf16[96,2048]{1,0:T(8,128)(2,1)S(1)} %collective-permute-done.30.refs_1_), channel_id=1, source_target_pairs={{0,4},{4,0},{1,5},{5,1},{2,6},{6,2},{3,7},{7,3},{8,12},{12,8},{9,1... | collective-permute-start | bytes 1179656 | tf_op jit(solution)/shard_map/ppermute | solution.py:35
  157.1 2.2 %collective-permute-start.35 = (bf16[96,2048]{1,0:T(8,128)(2,1)S(1)}, bf16[96,2048]{1,0:T(8,128)(2,1)S(1)}, u32[]{:S(2)}, u32[]{:S(2)}) collective-permute-start(bf16[96,2048]{1,0:T(8,128)(2,1)S(1)} %collective-permute-done.31.refs_2_), channel_id=1, source_target_pairs={{0,4},{4,0},{1,5},{5,1},{2,6},{6,2},{3,7},{7,3},{8,12},{12,8},{9,1... | collective-permute-start | bytes 1179656 | tf_op jit(solution)/shard_map/ppermute | solution.py:35
  157.9 1.9 collective-permute-start.36
  (17 other events, 122.3 us)
Sparse Core Ops, SparseCore 0:
  12.3 57.8 all-gather.1

commit v2 on v1

--- a/solution.py
+++ b/solution.py
@@ -31,6 +31,14 @@
     return lax.ppermute(value, "y", [(i, (i + k) % 4) for i in range(4)])
 
 
+def xh_swap(value):
+    return lax.ppermute(value, "xh", [(0, 1), (1, 0)])
+
+
+def z_shift(value, k):
+    return lax.ppermute(value, "head", [(i, (i + k) % 4) for i in range(4)])
+
+
 def core_swap(value):
     return lax.ppermute(value, "core", [(0, 1), (1, 0)])
 
@@ -40,18 +48,26 @@
     v_ref[...] = w_ref[:, 1, :]
     column = lax.broadcasted_iota(jnp.int32, (256, 128), 0)
     lane = lax.broadcasted_iota(jnp.int32, (256, 128), 1)
-    wanted = jnp.zeros((256, 128), jnp.int32)
-    for r in range(REQ_POOL):
-        wanted = jnp.where((lane >> 5) == r, adapter[r] * 32 + (lane & 31), wanted)
-    pick = (column == wanted).astype(jnp.bfloat16)
-    t_ref[...] = lax.dot_general(
-        pick, d_ref[...], (((0,), (1,)), ((), ())), preferred_element_type=jnp.float32
+    pick = (column == adapter[meta[4]] * 32 + lane) & (lane < 32)
+    low = lax.dot_general(
+        pick.astype(jnp.bfloat16),
+        d_ref[...],
+        (((0,), (1,)), ((), ())),
+        preferred_element_type=jnp.float32,
     ).astype(jnp.bfloat16)
+    t_ref[0:32] = low[0:32, 0:256]
+    t_ref[32:64] = low[0:32, 256:512]
 
 
 def pack(meta, adapter, weight, down):
     rows, half = weight.shape[0], weight.shape[0] // 2
-    bf = jnp.bfloat16
+
+    def shape(n):
+        return jax.ShapeDtypeStruct((n, 256), jnp.bfloat16)
+
+    def spec(n):
+        return pl.BlockSpec((n, 256), lambda i, m, a: (0, 0))
+
     return pl.pallas_call(
         pack_kernel,
         grid_spec=pltpu.PrefetchScalarGridSpec(
@@ -61,17 +77,9 @@
                 pl.BlockSpec((half, 2, 256), lambda i, m, a: (m[0], 0, 0)),
                 pl.BlockSpec((rows, 256), lambda i, m, a: (0, 0)),
             ],
-            out_specs=[
-                pl.BlockSpec((half, 256), lambda i, m, a: (0, 0)),
-                pl.BlockSpec((half, 256), lambda i, m, a: (0, 0)),
-                pl.BlockSpec((128, rows), lambda i, m, a: (0, 0)),
-            ],
-        ),
-        out_shape=[
-            jax.ShapeDtypeStruct((half, 256), bf),
-            jax.ShapeDtypeStruct((half, 256), bf),
-            jax.ShapeDtypeStruct((128, rows), bf),
-        ],
+            out_specs=[spec(half), spec(half), spec(64)],
+        ),
+        out_shape=[shape(half), shape(half), shape(64)],
         compiler_params=params(),
         name="pack",
     )(meta, adapter, weight, down)
@@ -138,11 +146,11 @@
     return out.reshape(rows, heads * 128)
 
 
-def split_dot(low, up):
+def split_dot(low, up, dims=(((1,), (0,)), ((), ()))):
     high = low.astype(jnp.bfloat16)
     rest = (low - high.astype(jnp.float32)).astype(jnp.bfloat16)
-    return jnp.dot(high, up, preferred_element_type=jnp.float32) + jnp.dot(
-        rest, up, preferred_element_type=jnp.float32
+    return lax.dot_general(high, up, dims, preferred_element_type=jnp.float32) + lax.dot_general(
+        rest, up, dims, preferred_element_type=jnp.float32
     )
 
 
@@ -150,108 +158,181 @@
     return [x, (x + 3) & 3, (x + 2) & 3, (x + 1) & 3]
 
 
-def prefill_kernel(meta, adapter, dest, *refs):
-    n_blocks = 16
-    prompt, down, up = refs[0:3]
-    blocks = refs[3 : 3 + n_blocks]
-    near_ref, far_ref = refs[3 + n_blocks : 5 + n_blocks]
-    p_buf, d_buf, u_buf, w_buf, res, sems, osem = refs[5 + n_blocks :]
+def chunk_start(xi, yi, core):
+    return pl.multiple_of(((xi >> 1) * 8 + yi * 2 + core) * 512 + (xi & 1) * 256, 256)
+
+
+def low_kernel(meta, *refs):
+    prompt, blocks, out_ref = refs[0], refs[1:9], refs[9]
+    p_buf, d_buf, sems = refs[10:]
+    xh, y, core, z = meta[1], meta[2], meta[3], meta[4]
+    first = pltpu.make_async_copy(prompt.at[z], p_buf, sems.at[8])
+    first.start()
+    copies = [
+        pltpu.make_async_copy(blocks[n].at[pl.ds(1024, 128)], d_buf.at[n], sems.at[n])
+        for n in range(8)
+    ]
+    for c in copies:
+        c.start()
+    first.wait()
+    low = jnp.zeros((32, 128), jnp.float32)
+    for n in range(8):
+        copies[n].wait()
+        c_of = core if n < 4 else 1 - core
+        tokens = []
+        for i in range(4):
+            side = xh if i < 2 else 1 - xh
+            shard = side * 8 + x_order(y)[n % 4] * 2 + c_of
+            at = pl.multiple_of(shard * 512 + (i % 2) * 256, 256)
+            tokens.append(p_buf[:, pl.ds(at, 256)])
+        low = low + lax.dot_general(
+            jnp.concatenate([d_buf[n, i * 32 : (i + 1) * 32] for i in range(4)], 1),
+            jnp.concatenate(tokens, 1),
+            (((1,), (1,)), ((), ())),
+            preferred_element_type=jnp.float32,
+        )
+    out_ref[...] = low
+
+
+def low_rank(meta, prompt, blocks):
+    bf = jnp.bfloat16
+    any_spec = pl.BlockSpec(memory_space=pl.ANY)
+    return pl.pallas_call(
+        low_kernel,
+        grid_spec=pltpu.PrefetchScalarGridSpec(
+            num_scalar_prefetch=1,
+            grid=(1,),
+            in_specs=[any_spec] * 9,
+            out_specs=pl.BlockSpec((32, 128), lambda i, m: (0, 0)),
+            scratch_shapes=[
+                pltpu.VMEM(prompt.shape[1:], bf),
+                pltpu.VMEM((8, 128, 256), bf),
+                pltpu.SemaphoreType.DMA((9,)),
+            ],
+        ),
+        out_shape=jax.ShapeDtypeStruct((32, 128), jnp.float32),
+        compiler_params=params(),
+        name="low_rank",
+    )(meta, prompt, *blocks)
+
+
+def main_kernel(meta, *refs):
+    prompt, blocks, k_ref, v_ref = refs[0], refs[1:17], refs[17], refs[18]
+    p_buf, w_buf, sems = refs[19:]
     pool, xh, y, core = meta[0], meta[1], meta[2], meta[3]
     x = 2 * xh + pool
+    first = pltpu.make_async_copy(prompt, p_buf, sems.at[16])
+    first.start()
     copies = [
-        pltpu.make_async_copy(prompt, p_buf, sems.at[16]),
-        pltpu.make_async_copy(down, d_buf, sems.at[17]),
-        pltpu.make_async_copy(up, u_buf, sems.at[18]),
+        pltpu.make_async_copy(blocks[b].at[pl.ds(0, 1024)], w_buf.at[b], sems.at[b])
+        for b in range(16)
     ]
-    wcopies = [pltpu.make_async_copy(blocks[b], w_buf.at[b], sems.at[b]) for b in range(n_blocks)]
-    copies[0].start()
-    for c in wcopies:
+    for c in copies:
         c.start()
-    copies[1].start()
-    copies[2].start()
-    copies[0].wait()
-    acc = [None, None]
-    for b in range(n_blocks):
-        wcopies[b].wait()
+    first.wait()
+    for b in range(16):
+        copies[b].wait()
         kv = (b // 4) % 2
         c_of = core if b < 8 else 1 - core
         j = b % 4
+        tokens = []
         for i in range(4):
             xi = x_order(x)[i if kv == 0 else j]
             yi = x_order(y)[j if kv == 0 else i]
-            shard = (xi >> 1) * 8 + yi * 2 + c_of
-            at = pl.multiple_of(shard * 512 + (xi & 1) * 256, 256)
-            part = jnp.dot(
-                p_buf[:, pl.ds(at, 256)],
-                w_buf[b, i * 256 : (i + 1) * 256, :],
-                preferred_element_type=jnp.float32,
-            )
-            acc[kv] = part if acc[kv] is None else acc[kv] + part
-    copies[1].wait()
-    copies[2].wait()
-    outs = []
-    for r in range(REQ_POOL):
-        rows = slice(r * 128, (r + 1) * 128)
-        low = None
-        for s in range(16):
-            part = lax.dot_general(
-                p_buf[rows, s * 512 : (s + 1) * 512],
-                d_buf[s * 128 + r * 32 : s * 128 + (r + 1) * 32, :],
-                (((1,), (1,)), ((), ())),
-                preferred_element_type=jnp.float32,
-            )
-            low = part if low is None else low + part
+            tokens.append(p_buf[:, pl.ds(chunk_start(xi, yi, c_of), 256)])
+        part = jnp.dot(
+            jnp.concatenate(tokens, 1),
+            w_buf[b],
+            preferred_element_type=jnp.float32,
+        )
+        out_ref = v_ref if kv else k_ref
+        if b == 4 * kv:
+            out_ref[...] = part
+        else:
+            out_ref[...] += part
+
+
+def main_product(meta, tokens, blocks):
+    bf = jnp.bfloat16
+    any_spec = pl.BlockSpec(memory_space=pl.ANY)
+    shape = jax.ShapeDtypeStruct((tokens.shape[0], 256), jnp.float32)
+    return pl.pallas_call(
+        main_kernel,
+        grid_spec=pltpu.PrefetchScalarGridSpec(
+            num_scalar_prefetch=1,
+            grid=(1,),
+            in_specs=[any_spec] * 17,
+            out_specs=[pl.BlockSpec(shape.shape, lambda i, m: (0, 0))] * 2,
+            scratch_shapes=[
+                pltpu.VMEM(tokens.shape, bf),
+                pltpu.VMEM((16, 1024, 256), bf),
+                pltpu.SemaphoreType.DMA((17,)),
+            ],
+        ),
+        out_shape=[shape, shape],
+        compiler_params=params(56),
+        name="main_product",
+    )(meta, tokens, *blocks)
+
+
+def finish_kernel(meta, adapter, dest, *refs):
+    lows, k_ref, v_ref, up_ref = refs[0:4], refs[4], refs[5], refs[6]
+    near_ref, far_ref, res, sems = refs[7:]
+    pool, xh, z = meta[0], meta[1], meta[4]
+    owners = [dest[pool * REQ_POOL + r] for r in range(REQ_POOL)]
+    dims = (((0,), (0,)), ((), ()))
+    for n in range(REQ_POOL):
+        r = x_order(z)[n]
         a = adapter[r]
+        rows = pl.ds(pl.multiple_of(r * 128, 128), 128)
+        low = lows[n][...]
         both = []
-        for kv in range(2):
-            value = acc[kv][rows] + split_dot(low[:, kv * 16 : (kv + 1) * 16], u_buf[a, kv])
+        for kv, ref in enumerate((k_ref, v_ref)):
+            value = ref[rows, :] + split_dot(low[kv * 16 : (kv + 1) * 16], up_ref[a, kv], dims)
             both.append(value.astype(jnp.bfloat16))
-        res[r] = jnp.stack(both, axis=1)
-    base = pool * REQ_POOL
-    sides = [dest[base + r] >> 3 for r in range(REQ_POOL)]
-    for r in range(REQ_POOL):
+        res[n] = jnp.stack(both, axis=1)
+        owner = dest[pool * REQ_POOL + r]
         slot = jnp.int32(0)
-        for q in range(r):
-            slot = slot + (sides[q] == sides[r]).astype(jnp.int32)
-
-        @pl.when(sides[r] == xh)
+        for q in range(REQ_POOL):
+            slot = slot + (((owners[q] >> 3) == (owner >> 3)) & (q < r)).astype(jnp.int32)
+
+        @pl.when((owner >> 3) == xh)
         def _():
-            pltpu.make_async_copy(res.at[r], near_ref.at[slot], osem.at[r]).start()
-
-        @pl.when(sides[r] != xh)
+            pltpu.make_async_copy(res.at[n], near_ref.at[slot], sems.at[n]).start()
+
+        @pl.when((owner >> 3) != xh)
         def _():
-            pltpu.make_async_copy(res.at[r], far_ref.at[slot], osem.at[r]).start()
-
-    for r in range(REQ_POOL):
-        pltpu.make_async_copy(res.at[r], near_ref.at[0], osem.at[r]).wait()
-
-
-def prefill(meta, adapter, dest, prompt, down, up, blocks):
+            pltpu.make_async_copy(res.at[n], far_ref.at[slot], sems.at[n]).start()
+
+    for n in range(REQ_POOL):
+        pltpu.make_async_copy(res.at[n], near_ref.at[0], sems.at[n]).wait()
+
+
+def finish(meta, adapters, dest, lows, keys, values, up):
     bf = jnp.bfloat16
-    tokens, width = prompt.shape
     any_spec = pl.BlockSpec(memory_space=pl.ANY)
     shape = jax.ShapeDtypeStruct((X_SLOTS, 128, 2, 256), bf)
+
+    def whole(a):
+        return pl.BlockSpec(a.shape, lambda i, m, b, d: (0,) * a.ndim)
+
+    ins = [*lows, keys, values, up]
     return pl.pallas_call(
-        prefill_kernel,
+        finish_kernel,
         grid_spec=pltpu.PrefetchScalarGridSpec(
             num_scalar_prefetch=3,
             grid=(1,),
-            in_specs=[any_spec] * (3 + len(blocks)),
+            in_specs=[whole(a) for a in ins],
             out_specs=[any_spec, any_spec],
             scratch_shapes=[
-                pltpu.VMEM((tokens, width), bf),
-                pltpu.VMEM(down.shape, bf),
-                pltpu.VMEM(up.shape, bf),
-                pltpu.VMEM((len(blocks),) + blocks[0].shape, bf),
                 pltpu.VMEM((REQ_POOL, 128, 2, 256), bf),
-                pltpu.SemaphoreType.DMA((19,)),
                 pltpu.SemaphoreType.DMA((REQ_POOL,)),
             ],
         ),
         out_shape=[shape, shape],
         compiler_params=params(56),
-        name="prefill",
-    )(meta, adapter, dest, prompt, down, up, *blocks)
+        name="finish",
+    )(meta, adapters, dest, *ins)
 
 
 def choose_kernel(meta, dest, *refs):
@@ -359,8 +440,8 @@
 
 
 def project_kernel(meta, keep_ref, down_ref, up_ref, w_ref, *refs):
-    ins, out_ref, rows, sems = refs[:8], refs[8], refs[9], refs[10]
-    xh, y, core = meta[1], meta[2], meta[3]
+    ins, outs, rows, sems = refs[:8], refs[8:12], refs[12], refs[13]
+    xh, y, core, z = meta[1], meta[2], meta[3], meta[4]
     copies = []
     for b in range(8):
         row = x_order(y)[b % 4]
@@ -377,14 +458,16 @@
         c.start()
     for c in copies:
         c.wait()
-    value = rows[...]
-    low = lax.dot_general(
-        value, down_ref[...], (((1,), (1,)), ((), ())), preferred_element_type=jnp.float32
-    )
-    owner = lax.broadcasted_iota(jnp.int32, low.shape, 1) >> 4
-    low = jnp.where(keep_ref[...] == owner, low, 0.0)
-    out = jnp.dot(value, w_ref[...], preferred_element_type=jnp.float32)
-    out_ref[...] = (out + split_dot(low, up_ref[...])).astype(jnp.bfloat16)
+    for n in range(4):
+        at = pl.ds(pl.multiple_of(((z + n) & 3) * 192, 64), 192)
+        value = rows[at, :]
+        low = lax.dot_general(
+            value, down_ref[...], (((1,), (1,)), ((), ())), preferred_element_type=jnp.float32
+        )
+        owner = lax.broadcasted_iota(jnp.int32, low.shape, 1) >> 4
+        low = jnp.where(keep_ref[at, :] == owner, low, 0.0)
+        out = jnp.dot(value, w_ref[...], preferred_element_type=jnp.float32)
+        outs[n][...] = (out + split_dot(low, up_ref[...])).astype(jnp.bfloat16)
 
 
 def project(meta, keep, down, up, weight, parts):
@@ -406,13 +489,13 @@
                 whole(weight.shape),
             ]
             + [any_spec] * 8,
-            out_specs=whole((rows, weight.shape[1])),
+            out_specs=[whole((rows // 4, weight.shape[1]))] * 4,
             scratch_shapes=[
                 pltpu.VMEM((rows, weight.shape[0]), jnp.bfloat16),
                 pltpu.SemaphoreType.DMA((16,)),
             ],
         ),
-        out_shape=jax.ShapeDtypeStruct((rows, weight.shape[1]), jnp.bfloat16),
+        out_shape=[jax.ShapeDtypeStruct((rows // 4, weight.shape[1]), jnp.bfloat16)] * 4,
         compiler_params=params(),
         name="project",
     )(meta, keep, down, up, weight, *parts)
@@ -438,38 +521,58 @@
     output_down_weight,
     output_up_weight,
 ):
-    meta = jnp.stack([lax.axis_index(a) for a in ("pool", "xh", "y", "core")]).astype(jnp.int32)
+    axes = ("pool", "xh", "y", "core", "head")
+    meta = jnp.stack([lax.axis_index(a) for a in axes]).astype(jnp.int32)
     keys, values, low_down = pack(
         meta, request_adapter_index, key_value_weight, adapter_down_weight
     )
-    all_down = lax.all_gather(low_down, ("xh", "y", "core"), axis=0, tiled=True)
-    key_rows = jnp.concatenate(ring(keys, x_shift), 0)
-    value_rows = jnp.concatenate(ring(values, y_shift), 0)
+    key_ring = ring(keys, x_shift)
+    value_ring = ring(values, y_shift)
+    attended = attend(rotated_query, key_value_cache, current_key_value, cached_length)
+    key_rows, value_rows, attended = lax.optimization_barrier(
+        (
+            jnp.concatenate(key_ring + [low_down, xh_swap(low_down)], 0),
+            jnp.concatenate(value_ring, 0),
+            attended,
+        )
+    )
     near = ring(key_rows, y_shift) + ring(value_rows, x_shift)
+    across = xh_swap(attended)
     blocks = near + [core_swap(b) for b in near]
 
-    attended = attend(rotated_query, key_value_cache, current_key_value, cached_length)
-    across = lax.ppermute(attended, "xh", [(0, 1), (1, 0)])
-    mine = ring(jnp.concatenate([attended, across], 0), y_shift)
+    blocks, across = lax.optimization_barrier((blocks, across))
+    pair = jnp.concatenate([attended, across], 0)
+    low = low_rank(meta, prompt, blocks[0:4] + blocks[8:12])
+    lows = ring(low, z_shift)
+    mine = ring(pair, y_shift)
+    tokens = prompt.reshape(-1, prompt.shape[2])
+    base_keys, base_values = main_product(meta, tokens, blocks)
+    base_keys, base_values, mine[1], mine[3] = lax.optimization_barrier(
+        (base_keys, base_values, mine[1], mine[3])
+    )
+    same, other = finish(
+        meta, request_adapter_index, destination, lows, base_keys, base_values, adapter_up_weight
+    )
+    b0 = lax.ppermute(same, "pool", [(0, 1), (1, 0)])
+    a0 = lax.ppermute(other, ("pool", "xh"), [(i, 3 - i) for i in range(4)])
+    b0, a0, mine[2] = lax.optimization_barrier((b0, a0, mine[2]))
+    b1, b3 = y_shift(b0, 1), y_shift(b0, -1)
+    a1, a3 = y_shift(a0, 1), y_shift(a0, -1)
+
     parts = mine + [core_swap(b) for b in mine]
     ranks = ADAPTERS * RANK
     down = jnp.transpose(output_down_weight, (1, 2, 0)).reshape(ranks, -1)
     up = output_up_weight.reshape(ranks, -1)
-    partial = project(meta, row_adapter_index[:, None], down, up, output_weight, parts)
-    shares = lax.all_to_all(partial, "head", split_axis=0, concat_axis=0, tiled=True)
-    shares = shares.reshape(4, -1, partial.shape[1]).astype(jnp.float32)
-    decoded = (shares[0] + shares[1] + shares[2] + shares[3]).astype(jnp.bfloat16)
-
-    tokens = prompt.reshape(-1, prompt.shape[2])
-    same, other = prefill(
-        meta, request_adapter_index, destination, tokens, all_down, adapter_up_weight, blocks
-    )
-    b0 = lax.ppermute(same, "pool", [(0, 1), (1, 0)])
-    a0 = lax.ppermute(other, ("pool", "xh"), [(i, 3 - i) for i in range(4)])
-    b1, b3 = y_shift(b0, 1), y_shift(b0, -1)
-    a1, a3 = y_shift(a0, 1), y_shift(a0, -1)
+    shares = project(meta, row_adapter_index[:, None], down, up, output_weight, parts)
+    b1, b3, a1, a3, shares = lax.optimization_barrier((b1, b3, a1, a3, shares))
     b2, a2 = y_shift(b1, 1), y_shift(a3, -1)
+    decoded = shares[0].astype(jnp.float32)
+    for k, share in ((1, shares[1]), (2, shares[2]), (-1, shares[3])):
+        decoded = decoded + z_shift(share, k).astype(jnp.float32)
+    decoded = decoded.astype(jnp.bfloat16)
+
     held = [b0, b1, b2, b3, a0, a1, a2, a3]
+    held, decoded = lax.optimization_barrier((held, decoded))
     theirs = core_swap(choose(meta, destination, held))
     handed = place(meta, destination, held, theirs)
     return handed, decoded

time: 198 us -> 185 us (0.934)
  starting transfers between devices: 49.7 us -> 74.2 us
  blocking collectives: 15.4 us -> 0 us
  between operations: 14.4 us -> 1.3 us
  waiting for transfers between devices: 63.2 us -> 52.4 us
  local copies, waits for them, and re-layouts: 3.96 us -> 6.69 us
    ppermute x1 -> x8, waiting for transfers between devices: 0.01 us -> 28.9 us  [the longest x2 20.4 us: xh_swap(): return lax.ppermute(value, 'xh', [(0, 1), (1, 0)])]
    ppermute x6, waiting for transfers between devices: 20.1 us -> 0.02 us  [x_shift(): return lax.ppermute(value, ('pool', 'xh'), pairs)]
    all_to_all x1 -> x0, blocking collectives: 15.4 us -> none  [body(): lax.all_to_all(partial, 'head', split_axis=0, concat_axis=0, tiled=True)]
    ppermute x13, starting transfers between devices: 16.5 us -> 30.9 us  [core_swap(): return lax.ppermute(value, 'core', [(0, 1), (1, 0)])]
    ppermute x15, waiting for transfers between devices: 24.6 us -> 11.7 us  [y_shift(): return lax.ppermute(value, 'y', [(i, (i + k) % 4) for i in range(4)])]
    ppermute x1 -> x8, starting transfers between devices: 1.12 us -> 13 us  [the longest x6 10.1 us: z_shift(): return lax.ppermute(value, 'head', [(i, (i + k) % 4) for i in range(4)])]
    ppermute x1, waiting for transfers between devices: 9.67 us -> 3.07 us  [body(): b0 = lax.ppermute(same, 'pool', [(0, 1), (1, 0)])]
    all_gather x1 -> x0, waiting for transfers between devices: 3.78 us -> none  [body(): all_down = lax.all_gather(low_down, ('xh', 'y', 'core'), axis=0, tiled=True)]
  transfers between devices with their start and end apart: 38 -> 44, of which waited for: 14 -> 13; matrix products, arithmetic and copies ran while one was open for 1% -> 1% of each run, Pallas kernels for 12% -> 22%
where the time goes in v2:
time: 185 us
  starting transfers between devices  74.2 us (40%)
  waiting for transfers between devices  52.4 us (28%)
  Pallas kernels  49.4 us (27%)
  local copies, waits for them, and re-layouts  6.69 us (4%)
    ppermute x13, starting transfers between devices, core_swap(): return lax.ppermute(value, 'core', [(0, 1), (1, 0)])  30.9 us
    ppermute x2, waiting for transfers between devices, xh_swap(): return lax.ppermute(value, 'xh', [(0, 1), (1, 0)])  20.4 us
    ppermute x15, starting transfers between devices, y_shift(): return lax.ppermute(value, 'y', [(i, (i + k) % 4) for i in range(4)])  18.9 us
    pallas_call x1, Pallas kernels, main_product(): pl.pallas_call(main_kernel, grid_spec=pltpu.PrefetchScalarGridSpec(num_sc...  14.6 us
    ppermute x15, waiting for transfers between devices, y_shift(): return lax.ppermute(value, 'y', [(i, (i + k) % 4) for i in range(4)])  11.7 us
    pallas_call x1, Pallas kernels, project(): pl.pallas_call(project_kernel, grid_spec=pltpu.PrefetchScalarGridSpec(num...  10.2 us
    ppermute x6, starting transfers between devices, z_shift(): return lax.ppermute(value, 'head', [(i, (i + k) % 4) for i in range(4)])  10.1 us
    pallas_call x1, Pallas kernels, attend(): pl.pallas_call(attend_kernel, grid_spec=pltpu.PrefetchScalarGridSpec(num_...  9.19 us
  transfers between devices with their start and end apart: 44, of which 13 were waited for; matrix products, arithmetic and copies ran while one was open for 1% of the time, Pallas kernels for 22%

profile of v2, /device:TPU:1, one launch (start us, length us, event | category | flops | bytes accessed | tf_op | source)
XLA Modules:
  0.0 184.8 jit_solution(5975317294446408934)
XLA Ops:
  0.7 1.0 copy-done.9
  1.8 0.9 copy-done.10
  3.4 1.5 pack.1
  4.9 2.1 %collective-permute-start = (bf16[256,256]{1,0:T(8,128)(2,1)S(1)}, bf16[256,256]{1,0:T(8,128)(2,1)S(1)}, u32[]{:S(2)}, u32[]{:S(2)}) collective-permute-start(bf16[256,256]{1,0:T(8,128)(2,1)S(1)} %get-tuple-element.57), channel_id=1, source_target_pairs={{0,64},{64,32},{32,96},{96,0},{1,65},{65,33},{33,97},{97,1},{2,66}... | collective-permute-start | bytes 393224 | tf_op jit(solution)/shard_map/ppermute | solution.py:27
  7.0 2.5 %collective-permute-start.1 = (bf16[256,256]{1,0:T(8,128)(2,1)S(1)}, bf16[256,256]{1,0:T(8,128)(2,1)S(1)}, u32[]{:S(2)}, u32[]{:S(2)}) collective-permute-start(bf16[256,256]{1,0:T(8,128)(2,1)S(1)} %get-tuple-element.57), channel_id=1, source_target_pairs={{0,32},{64,96},{32,0},{96,64},{1,33},{65,97},{33,1},{97,65},{2,34}... | collective-permute-start | bytes 393224 | tf_op jit(solution)/shard_map/ppermute | solution.py:27
  9.4 1.2 collective-permute-start.2
  10.6 2.7 %collective-permute-start.6 = (bf16[256,256]{1,0:T(8,128)(2,1)S(1)}, bf16[256,256]{1,0:T(8,128)(2,1)S(1)}, u32[]{:S(2)}, u32[]{:S(2)}) collective-permute-start(bf16[256,256]{1,0:T(8,128)(2,1)S(1)} %get-tuple-element.59), channel_id=1, source_target_pairs={{0,24},{8,0},{16,8},{24,16},{1,25},{9,1},{17,9},{25,17},{2,26},{10... | collective-permute-start | bytes 393224 | tf_op jit(solution)/shard_map/ppermute | solution.py:31
  13.7 1.0 copy.17
  16.1 9.2 %attend.1 = bf16[48,16,128]{2,1,0:T(8,128)(2,1)S(1)} custom-call(s32[48]{0:T(128)S(1)} %copy-done.18, bf16[48,16,128]{2,1,0:T(8,128)(2,1)S(1)} %bitcast.17, bf16[48,128,2,256]{3,2,1,0:T(2,128)(2,1)} %kv_ref.1, bf16[48,2,256]{2,1,0:T(2,128)(2,1)S(1)} %copy-done.13), custom_call_target="tpu_custom_call" | custom-call | tf_op jit(solution)/shard_map/attend/pallas_call | solution.py:130
  26.5 4.0 %collective-permute-done.3 = bf16[64,256]{1,0:T(8,128)(2,1)S(1)} collective-permute-done((bf16[64,256]{1,0:T(8,128)(2,1)S(1)}, bf16[64,256]{1,0:T(8,128)(2,1)S(1)}, u32[]{:S(2)}, u32[]{:S(2)}) %collective-permute-start.3) | collective-permute-done | bytes 32800 | tf_op jit(solution)/shard_map/ppermute | solution.py:35
  31.0 0.9 collective-permute-start.11
  31.9 1.6 collective-permute-start.12
  33.5 4.3 %collective-permute-start.17 = (bf16[1024,256]{1,0:T(8,128)(2,1)S(1)}, bf16[1024,256]{1,0:T(8,128)(2,1)S(1)}, u32[]{:S(2)}, u32[]{:S(2)}) collective-permute-start(bf16[1024,256]{1,0:T(8,128)(2,1)S(1)} %pad_maximum_fusion.refs_5_), channel_id=1, source_target_pairs={{0,4},{4,0},{1,5},{5,1},{2,6},{6,2},{3,7},{7,3},{8,12},{12,8},{9,1... | collective-permute-start | bytes 1572872 | tf_op jit(solution)/shard_map/ppermute | solution.py:43
  37.8 2.6 %collective-permute-start.21 = (bf16[48,2048]{1,0:T(8,128)(2,1)S(1)}, bf16[48,2048]{1,0:T(8,128)(2,1)S(1)}, u32[]{:S(2)}, u32[]{:S(2)}) collective-permute-start(bf16[48,2048]{1,0:T(8,128)(2,1)S(1)} %bitcast.21), channel_id=1, source_target_pairs={{0,32},{32,0},{1,33},{33,1},{2,34},{34,2},{3,35},{35,3},{4,36},{36... | collective-permute-start | bytes 589832 | tf_op jit(solution)/shard_map/ppermute | solution.py:35
  40.4 16.4 %collective-permute-done.21 = bf16[48,2048]{1,0:T(8,128)(2,1)S(1)} collective-permute-done((bf16[48,2048]{1,0:T(8,128)(2,1)S(1)}, bf16[48,2048]{1,0:T(8,128)(2,1)S(1)}, u32[]{:S(2)}, u32[]{:S(2)}) %collective-permute-start.21) | collective-permute-done | bytes 196640 | tf_op jit(solution)/shard_map/ppermute | solution.py:35
  56.8 1.6 collective-permute-start.7
  58.4 1.6 collective-permute-start.8
  60.0 0.9 collective-permute-start.9
  60.9 5.4 %collective-permute-start.13 = (bf16[1152,256]{1,0:T(8,128)(2,1)S(1)}, bf16[1152,256]{1,0:T(8,128)(2,1)S(1)}, u32[]{:S(2)}, u32[]{:S(2)}) collective-permute-start(bf16[1152,256]{1,0:T(8,128)(2,1)S(1)} %constant_dynamic-update-slice_fusion.refs_1_), channel_id=1, source_target_pairs={{0,4},{4,0},{1,5},{5,1},{2,6},{6,2},{3,7},{7,3},{8,12},{12,8},{9,1... | collective-permute-start | bytes 1769480 | tf_op jit(solution)/shard_map/ppermute | solution.py:43
  66.4 2.6 %collective-permute-done.7.refs_2_ = bf16[1152,256]{1,0:T(8,128)(2,1)S(1)} collective-permute-done((bf16[1152,256]{1,0:T(8,128)(2,1)S(1)}, bf16[1152,256]{1,0:T(8,128)(2,1)S(1)}, u32[]{:S(2)}, u32[]{:S(2)}) %collective-permute-start.7) | collective-permute-done | bytes 589856 | tf_op jit(solution)/shard_map/ppermute | solution.py:31
  69.0 8.7 %collective-permute-start.14 = (bf16[1152,256]{1,0:T(8,128)(2,1)S(1)}, bf16[1152,256]{1,0:T(8,128)(2,1)S(1)}, u32[]{:S(2)}, u32[]{:S(2)}) collective-permute-start(bf16[1152,256]{1,0:T(8,128)(2,1)S(1)} %collective-permute-done.7.refs_2_), channel_id=1, source_target_pairs={{0,4},{4,0},{1,5},{5,1},{2,6},{6,2},{3,7},{7,3},{8,12},{12,8},{9,1... | collective-permute-start | bytes 1769480 | tf_op jit(solution)/shard_map/ppermute | solution.py:43
  77.6 4.5 %collective-permute-done.8.refs_3_ = bf16[1152,256]{1,0:T(8,128)(2,1)S(1)} collective-permute-done((bf16[1152,256]{1,0:T(8,128)(2,1)S(1)}, bf16[1152,256]{1,0:T(8,128)(2,1)S(1)}, u32[]{:S(2)}, u32[]{:S(2)}) %collective-permute-start.8) | collective-permute-done | bytes 589856 | tf_op jit(solution)/shard_map/ppermute | solution.py:31
  82.1 4.8 %collective-permute-start.15 = (bf16[1152,256]{1,0:T(8,128)(2,1)S(1)}, bf16[1152,256]{1,0:T(8,128)(2,1)S(1)}, u32[]{:S(2)}, u32[]{:S(2)}) collective-permute-start(bf16[1152,256]{1,0:T(8,128)(2,1)S(1)} %collective-permute-done.8.refs_3_), channel_id=1, source_target_pairs={{0,4},{4,0},{1,5},{5,1},{2,6},{6,2},{3,7},{7,3},{8,12},{12,8},{9,1... | collective-permute-start | bytes 1769480 | tf_op jit(solution)/shard_map/ppermute | solution.py:43
  87.5 2.5 %collective-permute-done.19.refs_15_ = bf16[1024,256]{1,0:T(8,128)(2,1)S(1)} collective-permute-done((bf16[1024,256]{1,0:T(8,128)(2,1)S(1)}, bf16[1024,256]{1,0:T(8,128)(2,1)S(1)}, u32[]{:S(2)}, u32[]{:S(2)}) %collective-permute-start.19) | collective-permute-done | bytes 524320 | tf_op jit(solution)/shard_map/ppermute | solution.py:43
  91.7 2.0 %collective-permute-start.26 = (bf16[96,2048]{1,0:T(8,128)(2,1)S(1)}, bf16[96,2048]{1,0:T(8,128)(2,1)S(1)}, u32[]{:S(2)}, u32[]{:S(2)}) collective-permute-start(bf16[96,2048]{1,0:T(8,128)(2,1)S(1)} %constant_dynamic-update-slice_fusion.6.refs_0_), channel_id=1, source_target_pairs={{0,24},{8,0},{16,8},{24,16},{1,25},{9,1},{17,9},{25,17},{2,26},{10... | collective-permute-start | bytes 1179656 | tf_op jit(solution)/shard_map/ppermute | solution.py:31
  93.9 3.6 %low_rank.1.refs_0_ = f32[32,128]{1,0:T(8,128)S(1)} custom-call(s32[5]{0:T(128)S(1)} %stack.23.meta, bf16[4,128,8192]{2,1,0:T(8,128)(2,1)} %refs_0_.1, bf16[1152,256]{1,0:T(8,128)(2,1)S(1)} %constant_dynamic-update-slice_fusion.refs_1_, bf16[1152,256]{1,0:T(8,128)(2,1)S(1)} %collective-permute-done.7.refs_2_, ...), custom_call_target="tpu_custom_call" | custom-call | tf_op jit(solution)/shard_map/low_rank/pallas_call | solution.py:200
  97.7 1.7 collective-permute-start.22
  99.4 3.3 %collective-permute-start.23 = (f32[32,128]{1,0:T(8,128)S(1)}, f32[32,128]{1,0:T(8,128)S(1)}, u32[]{:S(2)}, u32[]{:S(2)}) collective-permute-start(f32[32,128]{1,0:T(8,128)S(1)} %low_rank.1.refs_0_), channel_id=1, source_target_pairs={{0,2},{1,3},{2,0},{3,1},{4,6},{5,7},{6,4},{7,5},{8,10},{9,11},{10,... | collective-permute-start | bytes 49160 | tf_op jit(solution)/shard_map/ppermute | solution.py:39
  102.7 3.6 %collective-permute-start.24 = (f32[32,128]{1,0:T(8,128)S(1)}, f32[32,128]{1,0:T(8,128)S(1)}, u32[]{:S(2)}, u32[]{:S(2)}) collective-permute-start(f32[32,128]{1,0:T(8,128)S(1)} %low_rank.1.refs_0_), channel_id=1, source_target_pairs={{0,3},{1,0},{2,1},{3,2},{4,7},{5,4},{6,5},{7,6},{8,11},{9,8},{10,9... | collective-permute-start | bytes 49160 | tf_op jit(solution)/shard_map/ppermute | solution.py:39
  106.3 14.6 %main_product.1 = (f32[512,256]{1,0:T(8,128)}, f32[512,256]{1,0:T(8,128)}) custom-call(s32[5]{0:T(128)} %copy-done.14, bf16[512,8192]{1,0:T(8,128)(2,1)} %bitcast.20, bf16[1152,256]{1,0:T(8,128)(2,1)} %copy-done, bf16[1152,256]{1,0:T(8,128)(2,1)} %copy-done.1, bf16[1152,256]{1,0:T(8,128)(2,1)} %copy-done.2, bf16[1152,256]{1,0:T(8,128)(2,1)} %copy-done.3, ...), custom_call_target="tpu_custom_call" | custom-call | tf_op jit(solution)/shard_map/main_product/pallas_call | solution.py:259
  122.2 3.9 %finish.1 = (bf16[3,128,2,256]{3,2,1,0:T(2,128)(2,1)}, bf16[3,128,2,256]{3,2,1,0:T(2,128)(2,1)}) custom-call(s32[5]{0:T(128)} %copy-done.14, s32[4]{0:T(128)} %adapter.3, s32[8]{0:T(128)} %dest.5, f32[32,128]{1,0:T(8,128)} %copy-done.12, f32[32,128]{1,0:T(8,128)} %copy-done.27, f32[32,128]{1,0:T(8,128)} %copy-done.28, f32[32,128]{1,0:T(8,128)} %copy-done.29, ...), custom_call_target="tpu_custom_call" | custom-call | tf_op jit(solution)/shard_map/finish/pallas_call | solution.py:320
  126.9 2.0 %collective-permute-start.28 = (bf16[3,128,2,256]{3,2,1,0:T(2,128)(2,1)}, bf16[3,128,2,256]{3,2,1,0:T(2,128)(2,1)S(1)}, u32[]{:S(2)}, u32[]{:S(2)}) collective-permute-start(bf16[3,128,2,256]{3,2,1,0:T(2,128)(2,1)} %get-tuple-element.85), channel_id=1, source_target_pairs={{0,96},{32,64},{64,32},{96,0},{1,97},{33,65},{65,33},{97,1},{2,98}... | collective-permute-start | bytes 1179656 | tf_op jit(solution)/shard_map/ppermute | solution.py:557
  128.9 2.4 %collective-permute-start.34 = (bf16[96,2048]{1,0:T(8,128)(2,1)S(1)}, bf16[96,2048]{1,0:T(8,128)(2,1)S(1)}, u32[]{:S(2)}, u32[]{:S(2)}) collective-permute-start(bf16[96,2048]{1,0:T(8,128)(2,1)S(1)} %constant_dynamic-update-slice_fusion.6.refs_0_), channel_id=1, source_target_pairs={{0,4},{4,0},{1,5},{5,1},{2,6},{6,2},{3,7},{7,3},{8,12},{12,8},{9,1... | collective-permute-start | bytes 1179656 | tf_op jit(solution)/shard_map/ppermute | solution.py:43
  131.8 3.1 %collective-permute-done.27.refs_0_ = bf16[3,128,2,256]{3,2,1,0:T(2,128)(2,1)S(1)} collective-permute-done((bf16[3,128,2,256]{3,2,1,0:T(2,128)(2,1)}, bf16[3,128,2,256]{3,2,1,0:T(2,128)(2,1)S(1)}, u32[]{:S(2)}, u32[]{:S(2)}) %collective-permute-start.27) | collective-permute-done | bytes 393248 | tf_op jit(solution)/shard_map/ppermute | solution.py:556
  134.9 1.6 collective-permute-done.28.refs_4_
  136.5 3.3 %collective-permute-start.36 = (bf16[96,2048]{1,0:T(8,128)(2,1)S(1)}, bf16[96,2048]{1,0:T(8,128)(2,1)S(1)}, u32[]{:S(2)}, u32[]{:S(2)}) collective-permute-start(bf16[96,2048]{1,0:T(8,128)(2,1)S(1)} %collective-permute-done.29.refs_2_), channel_id=1, source_target_pairs={{0,4},{4,0},{1,5},{5,1},{2,6},{6,2},{3,7},{7,3},{8,12},{12,8},{9,1... | collective-permute-start | bytes 1179656 | tf_op jit(solution)/shard_map/ppermute | solution.py:43
  139.9 2.7 %collective-permute-start.31 = (bf16[3,128,2,256]{3,2,1,0:T(2,128)(2,1)S(1)}, bf16[3,128,2,256]{3,2,1,0:T(2,128)(2,1)S(1)}, u32[]{:S(2)}, u32[]{:S(2)}) collective-permute-start(bf16[3,128,2,256]{3,2,1,0:T(2,128)(2,1)S(1)} %collective-permute-done.27.refs_0_), channel_id=1, source_target_pairs={{0,24},{8,0},{16,8},{24,16},{1,25},{9,1},{17,9},{25,17},{2,26},{10... | collective-permute-start | bytes 1179656 | tf_op jit(solution)/shard_map/ppermute | solution.py:31
  142.6 2.7 %collective-permute-start.33 = (bf16[3,128,2,256]{3,2,1,0:T(2,128)(2,1)S(1)}, bf16[3,128,2,256]{3,2,1,0:T(2,128)(2,1)S(1)}, u32[]{:S(2)}, u32[]{:S(2)}) collective-permute-start(bf16[3,128,2,256]{3,2,1,0:T(2,128)(2,1)S(1)} %collective-permute-done.28.refs_4_), channel_id=1, source_target_pairs={{0,24},{8,0},{16,8},{24,16},{1,25},{9,1},{17,9},{25,17},{2,26},{10... | collective-permute-start | bytes 1179656 | tf_op jit(solution)/shard_map/ppermute | solution.py:31
  145.4 10.2 %project.1 = (bf16[192,512]{1,0:T(8,128)(2,1)S(1)}, bf16[192,512]{1,0:T(8,128)(2,1)S(1)}, bf16[192,512]{1,0:T(8,128)(2,1)S(1)}, bf16[192,512]{1,0:T(8,128)(2,1)S(1)}) custom-call(s32[5]{0:T(128)S(1)} %copy-done.15, s32[768,1]{1,0:T(8,128)S(1)} %broadcast_in_dim.4.keep_ref, bf16[128,2048]{1,0:T(8,128)(2,1)S(1)} %bitcast.18, bf16[128,512]{1,0:T(8,128)(2,1)S(1)} %bitcast.19, ...), custom_call_target="tpu_custom_call" | custom-call | tf_op jit(solution)/shard_map/project/pallas_call | solution.py:480
  155.7 4.6 %collective-permute-done.32.refs_5_ = bf16[3,128,2,256]{3,2,1,0:T(2,128)(2,1)S(1)} collective-permute-done((bf16[3,128,2,256]{3,2,1,0:T(2,128)(2,1)S(1)}, bf16[3,128,2,256]{3,2,1,0:T(2,128)(2,1)S(1)}, u32[]{:S(2)}, u32[]{:S(2)}) %collective-permute-start.32) | collective-permute-done | bytes 393248 | tf_op jit(solution)/shard_map/ppermute | solution.py:31
  160.4 1.3 collective-permute-start.40
  161.7 2.7 %collective-permute-start.39 = (bf16[3,128,2,256]{3,2,1,0:T(2,128)(2,1)S(1)}, bf16[3,128,2,256]{3,2,1,0:T(2,128)(2,1)S(1)}, u32[]{:S(2)}, u32[]{:S(2)}) collective-permute-start(bf16[3,128,2,256]{3,2,1,0:T(2,128)(2,1)S(1)} %collective-permute-done.33.refs_7_), channel_id=1, source_target_pairs={{0,24},{8,0},{16,8},{24,16},{1,25},{9,1},{17,9},{25,17},{2,26},{10... | collective-permute-start | bytes 1179656 | tf_op jit(solution)/shard_map/ppermute | solution.py:31
  164.4 1.5 collective-permute-done.42
  165.9 1.4 collective-permute-done.41
  167.3 5.7 %collective-permute-done.40 = bf16[192,512]{1,0:T(8,128)(2,1)S(1)} collective-permute-done((bf16[192,512]{1,0:T(8,128)(2,1)S(1)}, bf16[192,512]{1,0:T(8,128)(2,1)S(1)}, u32[]{:S(2)}, u32[]{:S(2)}) %collective-permute-start.40) | collective-permute-done | bytes 196640 | tf_op jit(solution)/shard_map/ppermute | solution.py:39
  173.7 3.5 %choose.1 = bf16[2,8,128,2,256]{4,3,2,1,0:T(2,128)(2,1)S(1)} custom-call(s32[5]{0:T(128)S(1)} %copy-done.15, s32[8]{0:T(128)S(1)} %copy-done.16, bf16[3,128,2,256]{3,2,1,0:T(2,128)(2,1)S(1)} %collective-permute-done.27.refs_0_, bf16[3,128,2,256]{3,2,1,0:T(2,128)(2,1)S(1)} %collective-permute-done.30.refs_1_, ...), custom_call_target="tpu_custom_call" | custom-call | tf_op jit(solution)/shard_map/choose/pallas_call | solution.py:372
  178.0 3.8 %collective-permute-done.43.refs_8_ = bf16[2,8,128,2,256]{4,3,2,1,0:T(2,128)(2,1)S(1)} collective-permute-done((bf16[2,8,128,2,256]{4,3,2,1,0:T(2,128)(2,1)S(1)}, bf16[2,8,128,2,256]{4,3,2,1,0:T(2,128)(2,1)S(1)}, u32[]{:S(2)}, u32[]{:S(2)}) %collective-permute-start.43) | collective-permute-done | bytes 2097184 | tf_op jit(solution)/shard_map/ppermute | solution.py:43
  181.8 2.8 %place.1 = bf16[1,2,2048,2,256]{4,3,2,1,0:T(2,128)(2,1)} custom-call(s32[5]{0:T(128)S(1)} %copy-done.15, s32[8]{0:T(128)S(1)} %copy-done.16, bf16[3,128,2,256]{3,2,1,0:T(2,128)(2,1)S(1)} %collective-permute-done.27.refs_0_, bf16[3,128,2,256]{3,2,1,0:T(2,128)(2,1)S(1)} %collective-permute-done.30.refs_1_, ...), custom_call_target="tpu_custom_call" | custom-call | tf_op jit(solution)/shard_map/place/pallas_call | solution.py:424
  (124 shorter events, 11.1 us)
Async XLA Ops:
  3.4 90.5 %copy-start.14 = (s32[5]{0:T(128)}, s32[5]{0:T(128)S(1)}, u32[]{:S(2)}) copy-start(s32[5]{0:T(128)S(1)} %stack.23.meta) | copy-start | bytes 64
  4.9 20.5 %collective-permute-start = (bf16[256,256]{1,0:T(8,128)(2,1)S(1)}, bf16[256,256]{1,0:T(8,128)(2,1)S(1)}, u32[]{:S(2)}, u32[]{:S(2)}) collective-permute-start(bf16[256,256]{1,0:T(8,128)(2,1)S(1)} %get-tuple-element.57), channel_id=1, source_target_pairs={{0,64},{64,32},{32,96},{96,0},{1,65},{65,33},{33,97},{97,1},{2,66}... | collective-permute-start | bytes 393224 | tf_op jit(solution)/shard_map/ppermute | solution.py:27
  7.0 19.2 %collective-permute-start.1 = (bf16[256,256]{1,0:T(8,128)(2,1)S(1)}, bf16[256,256]{1,0:T(8,128)(2,1)S(1)}, u32[]{:S(2)}, u32[]{:S(2)}) collective-permute-start(bf16[256,256]{1,0:T(8,128)(2,1)S(1)} %get-tuple-element.57), channel_id=1, source_target_pairs={{0,32},{64,96},{32,0},{96,64},{1,33},{65,97},{33,1},{97,65},{2,34}... | collective-permute-start | bytes 393224 | tf_op jit(solution)/shard_map/ppermute | solution.py:27
  9.4 17.0 %collective-permute-start.2 = (bf16[256,256]{1,0:T(8,128)(2,1)S(1)}, bf16[256,256]{1,0:T(8,128)(2,1)S(1)}, u32[]{:S(2)}, u32[]{:S(2)}) collective-permute-start(bf16[256,256]{1,0:T(8,128)(2,1)S(1)} %get-tuple-element.57), channel_id=1, source_target_pairs={{0,96},{64,0},{32,64},{96,32},{1,97},{65,1},{33,65},{97,33},{2,98}... | collective-permute-start | bytes 393224 | tf_op jit(solution)/shard_map/ppermute | solution.py:27
  10.6 19.9 %collective-permute-start.6 = (bf16[256,256]{1,0:T(8,128)(2,1)S(1)}, bf16[256,256]{1,0:T(8,128)(2,1)S(1)}, u32[]{:S(2)}, u32[]{:S(2)}) collective-permute-start(bf16[256,256]{1,0:T(8,128)(2,1)S(1)} %get-tuple-element.59), channel_id=1, source_target_pairs={{0,24},{8,0},{16,8},{24,16},{1,25},{9,1},{17,9},{25,17},{2,26},{10... | collective-permute-start | bytes 393224 | tf_op jit(solution)/shard_map/ppermute | solution.py:31
  13.3 17.2 %collective-permute-start.5 = (bf16[256,256]{1,0:T(8,128)(2,1)S(1)}, bf16[256,256]{1,0:T(8,128)(2,1)S(1)}, u32[]{:S(2)}, u32[]{:S(2)}) collective-permute-start(bf16[256,256]{1,0:T(8,128)(2,1)S(1)} %get-tuple-element.59), channel_id=1, source_target_pairs={{0,16},{8,24},{16,0},{24,8},{1,17},{9,25},{17,1},{25,9},{2,18},{10... | collective-permute-start | bytes 393224 | tf_op jit(solution)/shard_map/ppermute | solution.py:31
  25.4 5.2 %collective-permute-start.4 = (bf16[256,256]{1,0:T(8,128)(2,1)S(1)}, bf16[256,256]{1,0:T(8,128)(2,1)S(1)}, u32[]{:S(2)}, u32[]{:S(2)}) collective-permute-start(bf16[256,256]{1,0:T(8,128)(2,1)S(1)} %get-tuple-element.59), channel_id=1, source_target_pairs={{0,8},{8,16},{16,24},{24,0},{1,9},{9,17},{17,25},{25,1},{2,10},{10... | collective-permute-start | bytes 393224 | tf_op jit(solution)/shard_map/ppermute | solution.py:31
  26.2 4.3 %collective-permute-start.3 = (bf16[64,256]{1,0:T(8,128)(2,1)S(1)}, bf16[64,256]{1,0:T(8,128)(2,1)S(1)}, u32[]{:S(2)}, u32[]{:S(2)}) collective-permute-start(bf16[64,256]{1,0:T(8,128)(2,1)S(1)} %get-tuple-element.58), channel_id=1, source_target_pairs={{0,32},{32,0},{1,33},{33,1},{2,34},{34,2},{3,35},{35,3},{4,36},{36... | collective-permute-start | bytes 98312 | tf_op jit(solution)/shard_map/ppermute | solution.py:35
  30.5 67.0 %copy-start = (bf16[1152,256]{1,0:T(8,128)(2,1)}, bf16[1152,256]{1,0:T(8,128)(2,1)S(1)}, u32[]{:S(2)}) copy-start(bf16[1152,256]{1,0:T(8,128)(2,1)S(1)} %constant_dynamic-update-slice_fusion.refs_1_) | copy-start | bytes 1769476
  30.6 66.9 %copy-start.19 = (bf16[1024,256]{1,0:T(8,128)(2,1)}, bf16[1024,256]{1,0:T(8,128)(2,1)S(1)}, u32[]{:S(2)}) copy-start(bf16[1024,256]{1,0:T(8,128)(2,1)S(1)} %pad_maximum_fusion.refs_5_) | copy-start | bytes 1572868
  30.6 27.8 %collective-permute-start.10 = (bf16[1024,256]{1,0:T(8,128)(2,1)S(1)}, bf16[1024,256]{1,0:T(8,128)(2,1)S(1)}, u32[]{:S(2)}, u32[]{:S(2)}) collective-permute-start(bf16[1024,256]{1,0:T(8,128)(2,1)S(1)} %pad_maximum_fusion.refs_5_), channel_id=1, source_target_pairs={{0,64},{64,32},{32,96},{96,0},{1,65},{65,33},{33,97},{97,1},{2,66}... | collective-permute-start | bytes 1572872 | tf_op jit(solution)/shard_map/ppermute | solution.py:27
  31.0 29.0 %collective-permute-start.11 = (bf16[1024,256]{1,0:T(8,128)(2,1)S(1)}, bf16[1024,256]{1,0:T(8,128)(2,1)S(1)}, u32[]{:S(2)}, u32[]{:S(2)}) collective-permute-start(bf16[1024,256]{1,0:T(8,128)(2,1)S(1)} %pad_maximum_fusion.refs_5_), channel_id=1, source_target_pairs={{0,32},{64,96},{32,0},{96,64},{1,33},{65,97},{33,1},{97,65},{2,34}... | collective-permute-start | bytes 1572872 | tf_op jit(solution)/shard_map/ppermute | solution.py:27
  31.9 29.0 %collective-permute-start.12 = (bf16[1024,256]{1,0:T(8,128)(2,1)S(1)}, bf16[1024,256]{1,0:T(8,128)(2,1)S(1)}, u32[]{:S(2)}, u32[]{:S(2)}) collective-permute-start(bf16[1024,256]{1,0:T(8,128)(2,1)S(1)} %pad_maximum_fusion.refs_5_), channel_id=1, source_target_pairs={{0,96},{64,0},{32,64},{96,32},{1,97},{65,1},{33,65},{97,33},{2,98}... | collective-permute-start | bytes 1572872 | tf_op jit(solution)/shard_map/ppermute | solution.py:27
  33.5 32.8 %collective-permute-start.17 = (bf16[1024,256]{1,0:T(8,128)(2,1)S(1)}, bf16[1024,256]{1,0:T(8,128)(2,1)S(1)}, u32[]{:S(2)}, u32[]{:S(2)}) collective-permute-start(bf16[1024,256]{1,0:T(8,128)(2,1)S(1)} %pad_maximum_fusion.refs_5_), channel_id=1, source_target_pairs={{0,4},{4,0},{1,5},{5,1},{2,6},{6,2},{3,7},{7,3},{8,12},{12,8},{9,1... | collective-permute-start | bytes 1572872 | tf_op jit(solution)/shard_map/ppermute | solution.py:43
  37.8 19.0 %collective-permute-start.21 = (bf16[48,2048]{1,0:T(8,128)(2,1)S(1)}, bf16[48,2048]{1,0:T(8,128)(2,1)S(1)}, u32[]{:S(2)}, u32[]{:S(2)}) collective-permute-start(bf16[48,2048]{1,0:T(8,128)(2,1)S(1)} %bitcast.21), channel_id=1, source_target_pairs={{0,32},{32,0},{1,33},{33,1},{2,34},{34,2},{3,35},{35,3},{4,36},{36... | collective-permute-start | bytes 589832 | tf_op jit(solution)/shard_map/ppermute | solution.py:35
  56.8 12.2 %collective-permute-start.7 = (bf16[1152,256]{1,0:T(8,128)(2,1)S(1)}, bf16[1152,256]{1,0:T(8,128)(2,1)S(1)}, u32[]{:S(2)}, u32[]{:S(2)}) collective-permute-start(bf16[1152,256]{1,0:T(8,128)(2,1)S(1)} %constant_dynamic-update-slice_fusion.refs_1_), channel_id=1, source_target_pairs={{0,8},{8,16},{16,24},{24,0},{1,9},{9,17},{17,25},{25,1},{2,10},{10... | collective-permute-start | bytes 1769480 | tf_op jit(solution)/shard_map/ppermute | solution.py:31
  58.4 23.7 %collective-permute-start.8 = (bf16[1152,256]{1,0:T(8,128)(2,1)S(1)}, bf16[1152,256]{1,0:T(8,128)(2,1)S(1)}, u32[]{:S(2)}, u32[]{:S(2)}) collective-permute-start(bf16[1152,256]{1,0:T(8,128)(2,1)S(1)} %constant_dynamic-update-slice_fusion.refs_1_), channel_id=1, source_target_pairs={{0,16},{8,24},{16,0},{24,8},{1,17},{9,25},{17,1},{25,9},{2,18},{10... | collective-permute-start | bytes 1769480 | tf_op jit(solution)/shard_map/ppermute | solution.py:31
  60.0 26.9 %collective-permute-start.9 = (bf16[1152,256]{1,0:T(8,128)(2,1)S(1)}, bf16[1152,256]{1,0:T(8,128)(2,1)S(1)}, u32[]{:S(2)}, u32[]{:S(2)}) collective-permute-start(bf16[1152,256]{1,0:T(8,128)(2,1)S(1)} %constant_dynamic-update-slice_fusion.refs_1_), channel_id=1, source_target_pairs={{0,24},{8,0},{16,8},{24,16},{1,25},{9,1},{17,9},{25,17},{2,26},{10... | collective-permute-start | bytes 1769480 | tf_op jit(solution)/shard_map/ppermute | solution.py:31
  60.9 26.1 %collective-permute-start.13 = (bf16[1152,256]{1,0:T(8,128)(2,1)S(1)}, bf16[1152,256]{1,0:T(8,128)(2,1)S(1)}, u32[]{:S(2)}, u32[]{:S(2)}) collective-permute-start(bf16[1152,256]{1,0:T(8,128)(2,1)S(1)} %constant_dynamic-update-slice_fusion.refs_1_), channel_id=1, source_target_pairs={{0,4},{4,0},{1,5},{5,1},{2,6},{6,2},{3,7},{7,3},{8,12},{12,8},{9,1... | collective-permute-start | bytes 1769480 | tf_op jit(solution)/shard_map/ppermute | solution.py:43
  66.3 21.1 %collective-permute-start.18 = (bf16[1024,256]{1,0:T(8,128)(2,1)S(1)}, bf16[1024,256]{1,0:T(8,128)(2,1)S(1)}, u32[]{:S(2)}, u32[]{:S(2)}) collective-permute-start(bf16[1024,256]{1,0:T(8,128)(2,1)S(1)} %collective-permute-done.10.refs_6_), channel_id=1, source_target_pairs={{0,4},{4,0},{1,5},{5,1},{2,6},{6,2},{3,7},{7,3},{8,12},{12,8},{9,1... | collective-permute-start | bytes 1572872 | tf_op jit(solution)/shard_map/ppermute | solution.py:43
  69.0 21.9 %collective-permute-start.14 = (bf16[1152,256]{1,0:T(8,128)(2,1)S(1)}, bf16[1152,256]{1,0:T(8,128)(2,1)S(1)}, u32[]{:S(2)}, u32[]{:S(2)}) collective-permute-start(bf16[1152,256]{1,0:T(8,128)(2,1)S(1)} %collective-permute-done.7.refs_2_), channel_id=1, source_target_pairs={{0,4},{4,0},{1,5},{5,1},{2,6},{6,2},{3,7},{7,3},{8,12},{12,8},{9,1... | collective-permute-start | bytes 1769480 | tf_op jit(solution)/shard_map/ppermute | solution.py:43
  82.1 8.8 %collective-permute-start.15 = (bf16[1152,256]{1,0:T(8,128)(2,1)S(1)}, bf16[1152,256]{1,0:T(8,128)(2,1)S(1)}, u32[]{:S(2)}, u32[]{:S(2)}) collective-permute-start(bf16[1152,256]{1,0:T(8,128)(2,1)S(1)} %collective-permute-done.8.refs_3_), channel_id=1, source_target_pairs={{0,4},{4,0},{1,5},{5,1},{2,6},{6,2},{3,7},{7,3},{8,12},{12,8},{9,1... | collective-permute-start | bytes 1769480 | tf_op jit(solution)/shard_map/ppermute | solution.py:43
  86.9 4.0 %collective-permute-start.16 = (bf16[1152,256]{1,0:T(8,128)(2,1)S(1)}, bf16[1152,256]{1,0:T(8,128)(2,1)S(1)}, u32[]{:S(2)}, u32[]{:S(2)}) collective-permute-start(bf16[1152,256]{1,0:T(8,128)(2,1)S(1)} %collective-permute-done.9.refs_4_), channel_id=1, source_target_pairs={{0,4},{4,0},{1,5},{5,1},{2,6},{6,2},{3,7},{7,3},{8,12},{12,8},{9,1... | collective-permute-start | bytes 1769480 | tf_op jit(solution)/shard_map/ppermute | solution.py:43
  87.0 3.1 %collective-permute-start.19 = (bf16[1024,256]{1,0:T(8,128)(2,1)S(1)}, bf16[1024,256]{1,0:T(8,128)(2,1)S(1)}, u32[]{:S(2)}, u32[]{:S(2)}) collective-permute-start(bf16[1024,256]{1,0:T(8,128)(2,1)S(1)} %collective-permute-done.11.refs_7_), channel_id=1, source_target_pairs={{0,4},{4,0},{1,5},{5,1},{2,6},{6,2},{3,7},{7,3},{8,12},{12,8},{9,1... | collective-permute-start | bytes 1572872 | tf_op jit(solution)/shard_map/ppermute | solution.py:43
  87.4 3.4 %collective-permute-start.20 = (bf16[1024,256]{1,0:T(8,128)(2,1)S(1)}, bf16[1024,256]{1,0:T(8,128)(2,1)S(1)}, u32[]{:S(2)}, u32[]{:S(2)}) collective-permute-start(bf16[1024,256]{1,0:T(8,128)(2,1)S(1)} %collective-permute-done.12.refs_8_), channel_id=1, source_target_pairs={{0,4},{4,0},{1,5},{5,1},{2,6},{6,2},{3,7},{7,3},{8,12},{12,8},{9,1... | collective-permute-start | bytes 1572872 | tf_op jit(solution)/shard_map/ppermute | solution.py:43
  90.9 11.8 %collective-permute-start.25 = (bf16[96,2048]{1,0:T(8,128)(2,1)S(1)}, bf16[96,2048]{1,0:T(8,128)(2,1)S(1)}, u32[]{:S(2)}, u32[]{:S(2)}) collective-permute-start(bf16[96,2048]{1,0:T(8,128)(2,1)S(1)} %constant_dynamic-update-slice_fusion.6.refs_0_), channel_id=1, source_target_pairs={{0,8},{8,16},{16,24},{24,0},{1,9},{9,17},{17,25},{25,1},{2,10},{10... | collective-permute-start | bytes 1179656 | tf_op jit(solution)/shard_map/ppermute | solution.py:31
  91.7 29.3 %collective-permute-start.26 = (bf16[96,2048]{1,0:T(8,128)(2,1)S(1)}, bf16[96,2048]{1,0:T(8,128)(2,1)S(1)}, u32[]{:S(2)}, u32[]{:S(2)}) collective-permute-start(bf16[96,2048]{1,0:T(8,128)(2,1)S(1)} %constant_dynamic-update-slice_fusion.6.refs_0_), channel_id=1, source_target_pairs={{0,24},{8,0},{16,8},{24,16},{1,25},{9,1},{17,9},{25,17},{2,26},{10... | collective-permute-start | bytes 1179656 | tf_op jit(solution)/shard_map/ppermute | solution.py:31
  93.7 37.6 %collective-permute-start.29 = (bf16[96,2048]{1,0:T(8,128)(2,1)S(1)}, bf16[96,2048]{1,0:T(8,128)(2,1)S(1)}, u32[]{:S(2)}, u32[]{:S(2)}) collective-permute-start(bf16[96,2048]{1,0:T(8,128)(2,1)S(1)} %constant_dynamic-update-slice_fusion.6.refs_0_), channel_id=1, source_target_pairs={{0,16},{8,24},{16,0},{24,8},{1,17},{9,25},{17,1},{25,9},{2,18},{10... | collective-permute-start | bytes 1179656 | tf_op jit(solution)/shard_map/ppermute | solution.py:31
  97.7 23.3 %collective-permute-start.22 = (f32[32,128]{1,0:T(8,128)S(1)}, f32[32,128]{1,0:T(8,128)S(1)}, u32[]{:S(2)}, u32[]{:S(2)}) collective-permute-start(f32[32,128]{1,0:T(8,128)S(1)} %low_rank.1.refs_0_), channel_id=1, source_target_pairs={{0,1},{1,2},{2,3},{3,0},{4,5},{5,6},{6,7},{7,4},{8,9},{9,10},{10,1... | collective-permute-start | bytes 49160 | tf_op jit(solution)/shard_map/ppermute | solution.py:39
  99.4 21.6 %collective-permute-start.23 = (f32[32,128]{1,0:T(8,128)S(1)}, f32[32,128]{1,0:T(8,128)S(1)}, u32[]{:S(2)}, u32[]{:S(2)}) collective-permute-start(f32[32,128]{1,0:T(8,128)S(1)} %low_rank.1.refs_0_), channel_id=1, source_target_pairs={{0,2},{1,3},{2,0},{3,1},{4,6},{5,7},{6,4},{7,5},{8,10},{9,11},{10,... | collective-permute-start | bytes 49160 | tf_op jit(solution)/shard_map/ppermute | solution.py:39
  102.7 18.3 %collective-permute-start.24 = (f32[32,128]{1,0:T(8,128)S(1)}, f32[32,128]{1,0:T(8,128)S(1)}, u32[]{:S(2)}, u32[]{:S(2)}) collective-permute-start(f32[32,128]{1,0:T(8,128)S(1)} %low_rank.1.refs_0_), channel_id=1, source_target_pairs={{0,3},{1,0},{2,1},{3,2},{4,7},{5,4},{6,5},{7,6},{8,11},{9,8},{10,9... | collective-permute-start | bytes 49160 | tf_op jit(solution)/shard_map/ppermute | solution.py:39
  121.0 52.7 %copy-start.16 = (s32[8]{0:T(128)S(1)}, s32[8]{0:T(128)}, u32[]{:S(2)}) copy-start(s32[8]{0:T(128)} %dest.5) | copy-start | bytes 100
  126.1 8.8 %collective-permute-start.27 = (bf16[3,128,2,256]{3,2,1,0:T(2,128)(2,1)}, bf16[3,128,2,256]{3,2,1,0:T(2,128)(2,1)S(1)}, u32[]{:S(2)}, u32[]{:S(2)}) collective-permute-start(bf16[3,128,2,256]{3,2,1,0:T(2,128)(2,1)} %get-tuple-element.84), channel_id=1, source_target_pairs={{0,64},{64,0},{1,65},{65,1},{2,66},{66,2},{3,67},{67,3},{4,68},{68... | collective-permute-start | bytes 1179656 | tf_op jit(solution)/shard_map/ppermute | solution.py:556
  126.9 9.6 %collective-permute-start.28 = (bf16[3,128,2,256]{3,2,1,0:T(2,128)(2,1)}, bf16[3,128,2,256]{3,2,1,0:T(2,128)(2,1)S(1)}, u32[]{:S(2)}, u32[]{:S(2)}) collective-permute-start(bf16[3,128,2,256]{3,2,1,0:T(2,128)(2,1)} %get-tuple-element.85), channel_id=1, source_target_pairs={{0,96},{32,64},{64,32},{96,0},{1,97},{33,65},{65,33},{97,1},{2,98}... | collective-permute-start | bytes 1179656 | tf_op jit(solution)/shard_map/ppermute | solution.py:557
  128.9 11.0 %collective-permute-start.34 = (bf16[96,2048]{1,0:T(8,128)(2,1)S(1)}, bf16[96,2048]{1,0:T(8,128)(2,1)S(1)}, u32[]{:S(2)}, u32[]{:S(2)}) collective-permute-start(bf16[96,2048]{1,0:T(8,128)(2,1)S(1)} %constant_dynamic-update-slice_fusion.6.refs_0_), channel_id=1, source_target_pairs={{0,4},{4,0},{1,5},{5,1},{2,6},{6,2},{3,7},{7,3},{8,12},{12,8},{9,1... | collective-permute-start | bytes 1179656 | tf_op jit(solution)/shard_map/ppermute | solution.py:43
  131.3 11.2 %collective-permute-start.35 = (bf16[96,2048]{1,0:T(8,128)(2,1)S(1)}, bf16[96,2048]{1,0:T(8,128)(2,1)S(1)}, u32[]{:S(2)}, u32[]{:S(2)}) collective-permute-start(bf16[96,2048]{1,0:T(8,128)(2,1)S(1)} %collective-permute-done.25.refs_1_), channel_id=1, source_target_pairs={{0,4},{4,0},{1,5},{5,1},{2,6},{6,2},{3,7},{7,3},{8,12},{12,8},{9,1... | collective-permute-start | bytes 1179656 | tf_op jit(solution)/shard_map/ppermute | solution.py:43
  131.3 11.2 %collective-permute-start.37 = (bf16[96,2048]{1,0:T(8,128)(2,1)S(1)}, bf16[96,2048]{1,0:T(8,128)(2,1)S(1)}, u32[]{:S(2)}, u32[]{:S(2)}) collective-permute-start(bf16[96,2048]{1,0:T(8,128)(2,1)S(1)} %collective-permute-done.26.refs_3_), channel_id=1, source_target_pairs={{0,4},{4,0},{1,5},{5,1},{2,6},{6,2},{3,7},{7,3},{8,12},{12,8},{9,1... | collective-permute-start | bytes 1179656 | tf_op jit(solution)/shard_map/ppermute | solution.py:43
  136.5 8.9 %collective-permute-start.36 = (bf16[96,2048]{1,0:T(8,128)(2,1)S(1)}, bf16[96,2048]{1,0:T(8,128)(2,1)S(1)}, u32[]{:S(2)}, u32[]{:S(2)}) collective-permute-start(bf16[96,2048]{1,0:T(8,128)(2,1)S(1)} %collective-permute-done.29.refs_2_), channel_id=1, source_target_pairs={{0,4},{4,0},{1,5},{5,1},{2,6},{6,2},{3,7},{7,3},{8,12},{12,8},{9,1... | collective-permute-start | bytes 1179656 | tf_op jit(solution)/shard_map/ppermute | solution.py:43
  139.9 15.8 %collective-permute-start.30 = (bf16[3,128,2,256]{3,2,1,0:T(2,128)(2,1)S(1)}, bf16[3,128,2,256]{3,2,1,0:T(2,128)(2,1)S(1)}, u32[]{:S(2)}, u32[]{:S(2)}) collective-permute-start(bf16[3,128,2,256]{3,2,1,0:T(2,128)(2,1)S(1)} %collective-permute-done.27.refs_0_), channel_id=1, source_target_pairs={{0,8},{8,16},{16,24},{24,0},{1,9},{9,17},{17,25},{25,1},{2,10},{10... | collective-permute-start | bytes 1179656 | tf_op jit(solution)/shard_map/ppermute | solution.py:31
  139.9 15.8 %collective-permute-start.31 = (bf16[3,128,2,256]{3,2,1,0:T(2,128)(2,1)S(1)}, bf16[3,128,2,256]{3,2,1,0:T(2,128)(2,1)S(1)}, u32[]{:S(2)}, u32[]{:S(2)}) collective-permute-start(bf16[3,128,2,256]{3,2,1,0:T(2,128)(2,1)S(1)} %collective-permute-done.27.refs_0_), channel_id=1, source_target_pairs={{0,24},{8,0},{16,8},{24,16},{1,25},{9,1},{17,9},{25,17},{2,26},{10... | collective-permute-start | bytes 1179656 | tf_op jit(solution)/shard_map/ppermute | solution.py:31
  142.6 17.7 %collective-permute-start.32 = (bf16[3,128,2,256]{3,2,1,0:T(2,128)(2,1)S(1)}, bf16[3,128,2,256]{3,2,1,0:T(2,128)(2,1)S(1)}, u32[]{:S(2)}, u32[]{:S(2)}) collective-permute-start(bf16[3,128,2,256]{3,2,1,0:T(2,128)(2,1)S(1)} %collective-permute-done.28.refs_4_), channel_id=1, source_target_pairs={{0,8},{8,16},{16,24},{24,0},{1,9},{9,17},{17,25},{25,1},{2,10},{10... | collective-permute-start | bytes 1179656 | tf_op jit(solution)/shard_map/ppermute | solution.py:31
  142.6 17.7 %collective-permute-start.33 = (bf16[3,128,2,256]{3,2,1,0:T(2,128)(2,1)S(1)}, bf16[3,128,2,256]{3,2,1,0:T(2,128)(2,1)S(1)}, u32[]{:S(2)}, u32[]{:S(2)}) collective-permute-start(bf16[3,128,2,256]{3,2,1,0:T(2,128)(2,1)S(1)} %collective-permute-done.28.refs_4_), channel_id=1, source_target_pairs={{0,24},{8,0},{16,8},{24,16},{1,25},{9,1},{17,9},{25,17},{2,26},{10... | collective-permute-start | bytes 1179656 | tf_op jit(solution)/shard_map/ppermute | solution.py:31
  160.3 5.6 %collective-permute-start.42 = (bf16[192,512]{1,0:T(8,128)(2,1)S(1)}, bf16[192,512]{1,0:T(8,128)(2,1)S(1)}, u32[]{:S(2)}, u32[]{:S(2)}) collective-permute-start(bf16[192,512]{1,0:T(8,128)(2,1)S(1)} %get-tuple-element.102), channel_id=1, source_target_pairs={{0,3},{1,0},{2,1},{3,2},{4,7},{5,4},{6,5},{7,6},{8,11},{9,8},{10,9... | collective-permute-start | bytes 589832 | tf_op jit(solution)/shard_map/ppermute | solution.py:39
  160.4 6.9 %collective-permute-start.41 = (bf16[192,512]{1,0:T(8,128)(2,1)S(1)}, bf16[192,512]{1,0:T(8,128)(2,1)S(1)}, u32[]{:S(2)}, u32[]{:S(2)}) collective-permute-start(bf16[192,512]{1,0:T(8,128)(2,1)S(1)} %get-tuple-element.101), channel_id=1, source_target_pairs={{0,2},{1,3},{2,0},{3,1},{4,6},{5,7},{6,4},{7,5},{8,10},{9,11},{10,... | collective-permute-start | bytes 589832 | tf_op jit(solution)/shard_map/ppermute | solution.py:39
  160.4 12.5 %collective-permute-start.40 = (bf16[192,512]{1,0:T(8,128)(2,1)S(1)}, bf16[192,512]{1,0:T(8,128)(2,1)S(1)}, u32[]{:S(2)}, u32[]{:S(2)}) collective-permute-start(bf16[192,512]{1,0:T(8,128)(2,1)S(1)} %get-tuple-element.100), channel_id=1, source_target_pairs={{0,1},{1,2},{2,3},{3,0},{4,5},{5,6},{6,7},{7,4},{8,9},{9,10},{10,1... | collective-permute-start | bytes 589832 | tf_op jit(solution)/shard_map/ppermute | solution.py:39
  161.7 12.0 %collective-permute-start.38 = (bf16[3,128,2,256]{3,2,1,0:T(2,128)(2,1)S(1)}, bf16[3,128,2,256]{3,2,1,0:T(2,128)(2,1)S(1)}, u32[]{:S(2)}, u32[]{:S(2)}) collective-permute-start(bf16[3,128,2,256]{3,2,1,0:T(2,128)(2,1)S(1)} %collective-permute-done.30.refs_1_), channel_id=1, source_target_pairs={{0,8},{8,16},{16,24},{24,0},{1,9},{9,17},{17,25},{25,1},{2,10},{10... | collective-permute-start | bytes 1179656 | tf_op jit(solution)/shard_map/ppermute | solution.py:31
  161.7 12.0 %collective-permute-start.39 = (bf16[3,128,2,256]{3,2,1,0:T(2,128)(2,1)S(1)}, bf16[3,128,2,256]{3,2,1,0:T(2,128)(2,1)S(1)}, u32[]{:S(2)}, u32[]{:S(2)}) collective-permute-start(bf16[3,128,2,256]{3,2,1,0:T(2,128)(2,1)S(1)} %collective-permute-done.33.refs_7_), channel_id=1, source_target_pairs={{0,24},{8,0},{16,8},{24,16},{1,25},{9,1},{17,9},{25,17},{2,26},{10... | collective-permute-start | bytes 1179656 | tf_op jit(solution)/shard_map/ppermute | solution.py:31
  177.2 4.6 %collective-permute-start.43 = (bf16[2,8,128,2,256]{4,3,2,1,0:T(2,128)(2,1)S(1)}, bf16[2,8,128,2,256]{4,3,2,1,0:T(2,128)(2,1)S(1)}, u32[]{:S(2)}, u32[]{:S(2)}) collective-permute-start(bf16[2,8,128,2,256]{4,3,2,1,0:T(2,128)(2,1)S(1)} %choose.1), channel_id=1, source_target_pairs={{0,4},{4,0},{1,5},{5,1},{2,6},{6,2},{3,7},{7,3},{8,12},{12,8},{9,1... | collective-permute-start | bytes 6291464 | tf_op jit(solution)/shard_map/ppermute | solution.py:43
  (27 other events, 427.1 us)

commit v3 on v2

v3 whole, which is shorter than its diff:
```python
import functools

import jax
import jax.numpy as jnp
from jax import lax
from jax.experimental import pallas as pl
from jax.experimental.pallas import tpu as pltpu
from jax.sharding import Mesh
from jax.sharding import PartitionSpec as P

HEAD_DIM = 128
RANK = 16
ADAPTERS = 8
CAP = 2
REQ_POOL = 4
X_SLOTS = 3
MIB = 2**20


POOL, XH, Y, CORE, HEAD, DEST, ADAPTER = 0, 1, 2, 3, 4, 5, 13
VMEM = pl.BlockSpec(memory_space=pltpu.VMEM)
SMEM = pl.BlockSpec(memory_space=pltpu.SMEM)
ANY = pl.BlockSpec(memory_space=pl.ANY)


def params(limit=48):
    return pltpu.CompilerParams(vmem_limit_bytes=limit * MIB)


def x_shift(value, k):
    pairs = []
    for x in range(4):
        t = (x + k) % 4
        pairs.append(((x % 2) * 2 + x // 2, (t % 2) * 2 + t // 2))
    return lax.ppermute(value, ("pool", "xh"), pairs)


def y_shift(value, k):
    return lax.ppermute(value, "y", [(i, (i + k) % 4) for i in range(4)])


def xh_swap(value):
    return lax.ppermute(value, "xh", [(0, 1), (1, 0)])


def z_shift(value, k):
    return lax.ppermute(value, "head", [(i, (i + k) % 4) for i in range(4)])


def core_swap(value):
    return lax.ppermute(value, "core", [(0, 1), (1, 0)])


def pack_kernel(info, w_ref, d_ref, k_ref, v_ref):
    half = pl.ds(pl.multiple_of(info[POOL] * 256, 256), 256)
    k_ref[...] = w_ref[half, 0, :]
    v_ref[0:256] = w_ref[half, 1, :]
    column = lax.broadcasted_iota(jnp.int32, (256, 128), 0)
    lane = lax.broadcasted_iota(jnp.int32, (256, 128), 1)
    pick = (column == info[ADAPTER + info[HEAD]] * 32 + lane) & (lane < 32)
    low = lax.dot_general(
        pick.astype(jnp.bfloat16),
        d_ref[...],
        (((0,), (1,)), ((), ())),
        preferred_element_type=jnp.float32,
    ).astype(jnp.bfloat16)
    v_ref[256:288] = low[0:32, 0:256]
    v_ref[288:320] = low[0:32, 256:512]


def pack(info, weight, down):
    return pl.pallas_call(
        pack_kernel,
        in_specs=[SMEM, VMEM, VMEM],
        out_specs=[VMEM, VMEM],
        out_shape=[
            jax.ShapeDtypeStruct((256, 256), jnp.bfloat16),
            jax.ShapeDtypeStruct((320, 256), jnp.bfloat16),
        ],
        compiler_params=params(),
        name="pack",
    )(info, weight, down)


ROWS_STEP = 8


def attend_kernel(offset, len_ref, q_ref, kv_ref, cur_ref, o_ref):
    first = pl.program_id(0) * ROWS_STEP + offset
    factor = HEAD_DIM**-0.5
    lane = lax.broadcasted_iota(jnp.int32, (8, 256), 1)
    is_key = (lane & 1) == 0
    scores, own = [], []
    for i in range(ROWS_STEP):
        n = len_ref[first + i]
        valid = is_key & (lane < 2 * n)
        for h in range(2):
            both = kv_ref[i, :, :, h * 128 : (h + 1) * 128].reshape(256, 128)
            q = q_ref[i, h * 8 : (h + 1) * 8, :]
            s = lax.dot_general(
                q, both, (((1,), (1,)), ((), ())), preferred_element_type=jnp.float32
            )
            scores.append(jnp.where(valid, s * factor, -1e30))
            k = cur_ref[i, 0:1, h * 128 : (h + 1) * 128].astype(jnp.float32)
            own.append(jnp.sum(q.astype(jnp.float32) * k, axis=-1, keepdims=True) * factor)
    s = jnp.concatenate(scores, 0)
    o = jnp.concatenate(own, 0)
    highest = jnp.maximum(jnp.max(s, axis=-1, keepdims=True), o)
    raw = jnp.exp(s - highest)
    own_raw = jnp.exp(o - highest)
    norm = jnp.sum(raw, axis=-1, keepdims=True) + own_raw
    weights = pltpu.roll(raw / norm, 1, 1).astype(jnp.bfloat16)
    own_weight = (own_raw / norm).astype(jnp.bfloat16).astype(jnp.float32)
    for i in range(ROWS_STEP):
        for h in range(2):
            both = kv_ref[i, :, :, h * 128 : (h + 1) * 128].reshape(256, 128)
            j = (i * 2 + h) * 8
            v = cur_ref[i, 1:2, h * 128 : (h + 1) * 128].astype(jnp.float32)
            mixed = jnp.dot(weights[j : j + 8], both, preferred_element_type=jnp.float32)
            mixed = mixed + own_weight[j : j + 8] * v
            o_ref[i, h * 8 : (h + 1) * 8, :] = mixed.astype(jnp.bfloat16)


def attend(query, cache, current, lengths, part, parts):
    rows, heads = query.shape[0] // parts, query.shape[1]
    first = part * (rows // ROWS_STEP)
    return pl.pallas_call(
        functools.partial(attend_kernel, first * ROWS_STEP),
        grid_spec=pltpu.PrefetchScalarGridSpec(
            num_scalar_prefetch=1,
            grid=(rows // ROWS_STEP,),
            in_specs=[
                pl.BlockSpec((ROWS_STEP, heads, 128), lambda g, n: (g + first, 0, 0)),
                pl.BlockSpec((ROWS_STEP, 128, 2, 256), lambda g, n: (g + first, 0, 0, 0)),
                pl.BlockSpec((ROWS_STEP, 2, 256), lambda g, n: (g + first, 0, 0)),
            ],
            out_specs=pl.BlockSpec((ROWS_STEP, heads, 128), lambda g, n: (g, 0, 0)),
        ),
        out_shape=jax.ShapeDtypeStruct((rows, heads, 128), jnp.bfloat16),
        compiler_params=params(),
        name="attend",
    )(lengths, query, cache, current)


def split_dot(low, up, dims=(((1,), (0,)), ((), ()))):
    high = low.astype(jnp.bfloat16)
    rest = (low - high.astype(jnp.float32)).astype(jnp.bfloat16)
    return lax.dot_general(high, up, dims, preferred_element_type=jnp.float32) + lax.dot_general(
        rest, up, dims, preferred_element_type=jnp.float32
    )


def x_order(x):
    return [x, (x + 3) & 3, (x + 2) & 3, (x + 1) & 3]


def chunk_start(xi, yi, core):
    return pl.multiple_of(((xi >> 1) * 8 + yi * 2 + core) * 512 + (xi & 1) * 256, 256)


def low_kernel(info, prompt, own_ref, other_ref, out_ref):
    xh, y, core = info[XH], info[Y], info[CORE]
    rows = pl.ds(pl.multiple_of(info[HEAD] * 128, 128), 128)
    low = jnp.zeros((32, 128), jnp.float32)
    for n in range(2):
        ref, c_of = ((own_ref, core), (other_ref, 1 - core))[n]
        downs, tokens = [], []
        for i in range(16):
            side = xh if i < 8 else 1 - xh
            shard = side * 8 + x_order(y)[(i // 2) % 4] * 2 + c_of
            at = pl.multiple_of(shard * 512 + (i % 2) * 256, 256)
            tokens.append(prompt[rows, pl.ds(at, 256)])
            downs.append(ref[i * 32 : (i + 1) * 32])
        low = low + lax.dot_general(
            jnp.concatenate(downs, 1),
            jnp.concatenate(tokens, 1),
            (((1,), (1,)), ((), ())),
            preferred_element_type=jnp.float32,
        )
    out_ref[...] = low


def low_rank(info, tokens, own, other):
    return pl.pallas_call(
        low_kernel,
        in_specs=[SMEM, VMEM, VMEM, VMEM],
        out_specs=VMEM,
        out_shape=jax.ShapeDtypeStruct((32, 128), jnp.float32),
        compiler_params=params(),
        name="low_rank",
    )(info, tokens, own, other)


def main_kernel(kinds, fresh, info, prompt, *refs):
    n = len(kinds)
    blocks, sums, outs = refs[:n], refs[n:-2], refs[-2:]
    pool, xh, y, core = info[POOL], info[XH], info[Y], info[CORE]
    x = 2 * xh + pool
    done = [fresh, fresh]
    for (kv, j, partner), ref in zip(kinds, blocks):
        c_of = 1 - core if partner else core
        tokens = []
        for i in range(4):
            xi = x_order(x)[i if kv == 0 else j]
            yi = x_order(y)[j if kv == 0 else i]
            tokens.append(prompt[:, pl.ds(chunk_start(xi, yi, c_of), 256)])
        part = jnp.dot(
            jnp.concatenate(tokens, 1), ref[...], preferred_element_type=jnp.float32
        )
        if done[kv] is True:
            outs[kv][...] = part
        elif done[kv] is False:
            outs[kv][...] = sums[kv][...] + part
        else:
            outs[kv][...] += part
        done[kv] = None


def main_product(info, tokens, kinds, blocks, sums=()):
    shape = jax.ShapeDtypeStruct((tokens.shape[0], 256), jnp.float32)
    return pl.pallas_call(
        functools.partial(main_kernel, kinds, not sums),
        in_specs=[SMEM] + [VMEM] * (1 + len(blocks) + len(sums)),
        out_specs=[VMEM, VMEM],
        out_shape=[shape, shape],
        compiler_params=params(),
        name="main_product",
    )(info, tokens, *blocks, *sums)


def finish_kernel(info, *refs):
    lows, k_ref, v_ref, up_ref, near_ref, far_ref = refs[0:4], *refs[4:]
    pool, xh, z = info[POOL], info[XH], info[HEAD]
    owners = [info[DEST + pool * REQ_POOL + r] for r in range(REQ_POOL)]
    dims = (((0,), (0,)), ((), ()))
    for n in range(REQ_POOL):
        r = x_order(z)[n]
        a = info[ADAPTER + r]
        rows = pl.ds(pl.multiple_of(r * 128, 128), 128)
        low = lows[n][...]
        both = []
        for kv, ref in enumerate((k_ref, v_ref)):
            value = ref[rows, :] + split_dot(low[kv * 16 : (kv + 1) * 16], up_ref[a, kv], dims)
            both.append(value.astype(jnp.bfloat16))
        result = jnp.stack(both, axis=1)
        owner = info[DEST + pool * REQ_POOL + r]
        slot = jnp.int32(0)
        for q in range(REQ_POOL):
            slot = slot + (((owners[q] >> 3) == (owner >> 3)) & (q < r)).astype(jnp.int32)

        @pl.when((owner >> 3) == xh)
        def _():
            near_ref[slot] = result

        @pl.when((owner >> 3) != xh)
        def _():
            far_ref[slot] = result


def finish(info, lows, sums, up):
    shape = jax.ShapeDtypeStruct((X_SLOTS, 128, 2, 256), jnp.bfloat16)
    return pl.pallas_call(
        finish_kernel,
        in_specs=[SMEM] + [VMEM] * 7,
        out_specs=[VMEM, VMEM],
        out_shape=[shape, shape],
        compiler_params=params(),
        name="finish",
    )(info, *lows, *sums, up)


def slots_of(info, pool, xh, owner):
    owners = [info[DEST + pool * REQ_POOL + r] for r in range(REQ_POOL)]
    index = [jnp.int32(0)] * CAP
    used = [jnp.int32(0)] * CAP
    place, mine = jnp.int32(0), jnp.int32(0)
    for r in range(REQ_POOL):
        hit = (owners[r] == owner).astype(jnp.int32)
        for j in range(CAP):
            here = hit * (mine == j).astype(jnp.int32)
            index[j] = index[j] + here * place
            used[j] = used[j] + here
        mine = mine + hit
        place = place + ((owners[r] >> 3) == xh).astype(jnp.int32)
    return index, used


def choose_kernel(info, *refs):
    ins, out, sems = refs[:-2], refs[-2], refs[-1]
    xh = info[XH]
    owner = xh * 8 + info[Y] * 2 + (1 - info[CORE])
    index = slots_of(info, 1 - info[POOL], xh, owner)[0]
    n = len(ins)
    copies = [
        pltpu.make_async_copy(ins[b].at[index[j]], out.at[j, b], sems.at[j * n + b])
        for j in range(CAP)
        for b in range(n)
    ]
    for c in copies:
        c.start()
    for c in copies:
        c.wait()


def choose(info, parts):
    n = len(parts)
    return pl.pallas_call(
        choose_kernel,
        in_specs=[SMEM] + [VMEM] * n,
        out_specs=VMEM,
        out_shape=jax.ShapeDtypeStruct((CAP, n, 128, 2, 256), jnp.bfloat16),
        scratch_shapes=[pltpu.SemaphoreType.DMA((CAP * n,))],
        compiler_params=params(),
        name="choose",
    )(info, *parts)


def place_kernel(kinds, rest, info, *refs):
    n = len(kinds)
    ins, others = refs[:n], refs[n]
    out, zero, sems = refs[-3], refs[-2], refs[-1]
    xh, y, core = info[XH], info[Y], info[CORE]
    index, used = slots_of(info, 1 - info[POOL], xh, xh * 8 + y * 2 + core)
    if rest:
        zero[...] = jnp.zeros_like(zero)

    def spot(j, kind, c_of):
        side = xh if kind[0] == 0 else 1 - xh
        at = (side * 8 + x_order(y)[kind[1]] * 2 + c_of) * 128
        return out.at[0, j, pl.ds(pl.multiple_of(at, 128), 128)]

    def transfers(j):
        full = []
        for b, kind in enumerate(kinds):
            full.append((ins[b].at[index[j]], spot(j, kind, core)))
            full.append((others.at[j, b], spot(j, kind, 1 - core)))
        return [
            pltpu.make_async_copy(src, dst, sems.at[j, i]) for i, (src, dst) in enumerate(full)
        ]

    def clears(j):
        spots = [spot(j, kind, c) for kind in kinds + rest for c in (core, 1 - core)]
        return [pltpu.make_async_copy(zero, dst, sems.at[j, i]) for i, dst in enumerate(spots)]

    for step in ("start", "wait"):
        for j in range(CAP):

            @pl.when(used[j] == 1)
            def _():
                for c in transfers(j):
                    getattr(c, step)()

            if rest:

                @pl.when(used[j] == 0)
                def _():
                    for c in clears(j):
                        getattr(c, step)()


def place(info, kinds, rest, parts, others, out=None):
    shape = jax.ShapeDtypeStruct((1, CAP, 2048, 2, 256), jnp.bfloat16)
    ins = [info, *parts, others] + ([] if out is None else [out])
    return pl.pallas_call(
        functools.partial(place_kernel, kinds, rest),
        in_specs=[SMEM] + [VMEM] * (len(parts) + 1) + ([] if out is None else [ANY]),
        out_specs=ANY,
        out_shape=shape,
        scratch_shapes=[
            pltpu.VMEM((128, 2, 256), jnp.bfloat16),
            pltpu.SemaphoreType.DMA((CAP, 16)),
        ],
        input_output_aliases={} if out is None else {len(ins) - 1: 0},
        compiler_params=params(),
        name="place",
    )(*ins)


def project_kernel(info, keep, down, up, w_ref, *refs):
    ins, outs, res = refs[:8], refs[8:12], refs[12]
    xh, y, core, z = info[XH], info[Y], info[CORE], info[HEAD]
    value = jnp.concatenate([ref[...] for ref in ins], 0)
    out = jnp.dot(value, w_ref[...], preferred_element_type=jnp.float32)
    low = lax.dot_general(
        value, down[...], (((1,), (1,)), ((), ())), preferred_element_type=jnp.float32
    )
    owner = lax.broadcasted_iota(jnp.int32, (48, ADAPTERS * RANK), 1) >> 4
    spots, lows = [], []
    for b in range(8):
        row, c_of = x_order(y)[b % 4], core if b < 4 else 1 - core
        for i in range(2):
            side = xh if i == 0 else 1 - xh
            at = pl.ds(pl.multiple_of((side * 8 + row * 2 + c_of) * 48, 16), 48)
            n = b * 96 + i * 48
            spots.append(at)
            lows.append(jnp.where(keep[at, :] == owner, low[n : n + 48], 0.0))
    out = (out + split_dot(jnp.concatenate(lows, 0), up[...])).astype(jnp.bfloat16)
    for n in range(16):
        res[spots[n], :] = out[n * 48 : (n + 1) * 48]
    for n in range(4):
        outs[n][...] = res[pl.ds(pl.multiple_of(((z + n) & 3) * 192, 64), 192), :]


def project(info, keep, down, up, weight, parts):
    rows, width = 768, weight.shape[1]
    return pl.pallas_call(
        project_kernel,
        in_specs=[SMEM] + [VMEM] * 12,
        out_specs=[VMEM] * 4,
        out_shape=[jax.ShapeDtypeStruct((rows // 4, width), jnp.bfloat16)] * 4,
        scratch_shapes=[pltpu.VMEM((rows, width), jnp.bfloat16)],
        compiler_params=params(),
        name="project",
    )(info, keep, down, up, weight, *parts)


def ring(value, shift):
    return [value, shift(value, 1), shift(value, 2), shift(value, -1)]


def body(
    prompt,
    key_value_weight,
    adapter_down_weight,
    adapter_up_weight,
    request_adapter_index,
    destination,
    rotated_query,
    key_value_cache,
    current_key_value,
    cached_length,
    row_adapter_index,
    output_weight,
    output_down_weight,
    output_up_weight,
):
    barrier = lax.optimization_barrier
    axes = ("pool", "xh", "y", "core", "head")
    place_of = jnp.stack([lax.axis_index(a) for a in axes]).astype(jnp.int32)
    info = jnp.concatenate([place_of, destination, request_adapter_index])
    tokens = prompt.reshape(-1, prompt.shape[2])
    rows, heads = rotated_query.shape[0], rotated_query.shape[1] // HEAD_DIM
    query = rotated_query.reshape(rows, heads, HEAD_DIM)

    keys, values = pack(info, key_value_weight, adapter_down_weight)
    kx1, kx2, kx3 = x_shift(keys, 1), x_shift(keys, 2), x_shift(keys, -1)
    vy1, vy3 = y_shift(values, 1), y_shift(values, -1)
    att0 = attend(query, key_value_cache, current_key_value, cached_length, 0, 2)
    keys, kx1, kx2, kx3, values, vy1, vy3, att0, cached_length = barrier(
        (keys, kx1, kx2, kx3, values, vy1, vy3, att0, cached_length)
    )
    vy2 = y_shift(values, 2)
    key0 = jnp.concatenate([keys, kx1, kx2, kx3], 0)
    key1, key3 = y_shift(key0, 1), y_shift(key0, -1)
    att1 = attend(query, key_value_cache, current_key_value, cached_length, 1, 2)
    vy2, att1 = barrier((vy2, att1))
    both = [values, vy1, vy2, vy3]
    value0 = jnp.concatenate([v[:256] for v in both], 0)
    value1, value3 = x_shift(value0, 1), x_shift(value0, -1)
    down0 = jnp.concatenate([v[256:] for v in both], 0)
    down_own = jnp.concatenate([down0, xh_swap(down0)], 0)
    sums = main_product(info, tokens, ((0, 0, 0), (1, 0, 0)), (key0, value0))
    attended = jnp.concatenate([att0, att1], 0).reshape(rows, heads * HEAD_DIM)
    key0, value0, key1, key3, value1, value3, down_own, sums, attended = barrier(
        (key0, value0, key1, key3, value1, value3, down_own, sums, attended)
    )
    key2, value2 = y_shift(key0, 2), x_shift(value0, 2)
    low = low_rank(info, tokens, down_own, core_swap(down_own))
    kinds = ((0, 1, 0), (0, 3, 0), (1, 1, 0), (1, 3, 0))
    sums = main_product(info, tokens, kinds, (key1, key3, value1, value3), tuple(sums))
    ready = [core_swap(b) for b in (key0, value0, key1, key3, value1, value3)]
    across = xh_swap(attended)
    lows = ring(low, z_shift)
    key2, value2, ready, sums, across, lows, attended = barrier(
        (key2, value2, ready, sums, across, lows, attended)
    )
    mine = ring(jnp.concatenate([attended, across], 0), y_shift)
    last = [key2, value2, core_swap(key2), core_swap(value2)]
    kinds = ((0, 0, 1), (1, 0, 1), (0, 1, 1), (0, 3, 1), (1, 1, 1), (1, 3, 1))
    sums = main_product(info, tokens, kinds, ready, tuple(sums))
    kinds = ((0, 2, 0), (1, 2, 0), (0, 2, 1), (1, 2, 1))
    sums = main_product(info, tokens, kinds, last, tuple(sums))
    same, other = finish(info, lows, sums, adapter_up_weight)

    b0 = lax.ppermute(same, "pool", [(0, 1), (1, 0)])
    a0 = lax.ppermute(other, ("pool", "xh"), [(i, 3 - i) for i in range(4)])
    b0, a0, mine = barrier((b0, a0, mine))
    b1, b3 = y_shift(b0, 1), y_shift(b0, -1)
    a1, a3 = y_shift(a0, 1), y_shift(a0, -1)
    parts = mine + [core_swap(b) for b in mine]
    ranks = ADAPTERS * RANK
    down = jnp.transpose(output_down_weight, (1, 2, 0)).reshape(ranks, -1)
    up = output_up_weight.reshape(ranks, -1)
    shares = project(info, row_adapter_index[:, None], down, up, output_weight, parts)
    theirs0 = core_swap(choose(info, [b0, a0]))
    b0, a0, b1, b3, a1, a3, shares, theirs0 = barrier((b0, a0, b1, b3, a1, a3, shares, theirs0))
    b2, a2 = y_shift(b1, 1), y_shift(a3, -1)
    decoded = shares[0].astype(jnp.float32)
    for k, share in ((1, shares[1]), (2, shares[2]), (-1, shares[3])):
        decoded = decoded + z_shift(share, k).astype(jnp.float32)
    decoded = decoded.astype(jnp.bfloat16)
    theirs1 = core_swap(choose(info, [b1, b3, a1, a3]))
    theirs = jnp.concatenate([theirs0, theirs1], 1)
    kinds = ((0, 0), (1, 0), (0, 1), (0, 3), (1, 1), (1, 3))
    rest = ((0, 2), (1, 2))
    handed = place(info, kinds, rest, [b0, a0, b1, b3, a1, a3], theirs)
    b2, a2, decoded, handed = barrier((b2, a2, decoded, handed))
    theirs2 = core_swap(choose(info, [b2, a2]))
    handed = place(info, rest, (), [b2, a2], theirs2, handed)
    return handed, decoded


def solution(mesh):
    fine = Mesh(mesh.devices.reshape(2, 2, 4, 2, 4), ("pool", "xh", "y", "core", "head"))
    seq = ("xh", "y", "core")
    every = ("pool",) + seq
    in_specs = (
        P("pool", seq, None),
        P(seq, None, "head"),
        P(seq, None),
        P(None, None, None, "head"),
        P("pool"),
        P(),
        P(every, "head"),
        P(every, None, None, "head"),
        P(every, None, "head"),
        P(every),
        P("pool"),
        P("head", seq),
        P("head", None, None),
        P(None, None, seq),
    )
    out_specs = (P(every, None, None, None, "head"), P(("pool", "head"), seq))
    return jax.shard_map(body, mesh=fine, in_specs=in_specs, out_specs=out_specs, check_vma=False)
```

time: 185 us -> 165 us (0.89); the launches traced: 185 us -> 162 us
  starting transfers between devices: 74.2 us -> 54.6 us
  waiting for transfers between devices: 52.4 us -> 45.1 us
  Pallas kernels: 49.4 us -> 52.4 us
  other arithmetic: 0.82 us -> 2.87 us
    ppermute x13 -> x16, starting transfers between devices: 30.9 us -> 17.5 us  [core_swap(): return lax.ppermute(value, 'core', [(0, 1), (1, 0)])]
    ppermute x2, waiting for transfers between devices: 20.4 us -> 7.47 us  [xh_swap(): return lax.ppermute(value, 'xh', [(0, 1), (1, 0)])]
    ppermute x15, waiting for transfers between devices: 11.7 us -> 17 us  [y_shift(): return lax.ppermute(value, 'y', [(i, (i + k) % 4) for i in range(4)])]
    ppermute x13 -> x16, waiting for transfers between devices: 7.11 us -> 2.9 us  [core_swap(): return lax.ppermute(value, 'core', [(0, 1), (1, 0)])]
    ppermute x6, waiting for transfers between devices: 0.02 us -> 4.15 us  [x_shift(): return lax.ppermute(value, ('pool', 'xh'), pairs)]
    pallas_call x8 -> x15, Pallas kernels: 49.4 us -> 52.4 us  [the longest x4 18.6 us: main_product(): pl.pallas_call(functools.partial(main_kernel, kinds, not sums), in_specs=...]
    concatenate x1 -> x4, other arithmetic: 0.04 us -> 2.09 us  [the longest x1 2.03 us: body(): theirs = jnp.concatenate([theirs0, theirs1], 1)]
    ppermute x15, starting transfers between devices: 18.9 us -> 16.9 us  [y_shift(): return lax.ppermute(value, 'y', [(i, (i + k) % 4) for i in range(4)])]
  transfers between devices with their start and end apart: 44 -> 47, of which waited for: 13 -> 16; matrix products, arithmetic and copies ran while one was open for 1% -> 3% of each run, Pallas kernels for 22% -> 29%
where the time goes in v3:
time: 165 us; the launch traced here: 162 us
  starting transfers between devices  54.6 us (33%)
  Pallas kernels  52.4 us (32%)
  waiting for transfers between devices  45.1 us (27%)
  local copies, waits for them, and re-layouts  5.53 us (3%)
  other arithmetic  2.87 us (2%)
    pallas_call x4, Pallas kernels, main_product(): pl.pallas_call(functools.partial(main_kernel, kinds, not sums), in_specs=...  18.6 us
    ppermute x16, starting transfers between devices, core_swap(): return lax.ppermute(value, 'core', [(0, 1), (1, 0)])  17.5 us
    ppermute x15, waiting for transfers between devices, y_shift(): return lax.ppermute(value, 'y', [(i, (i + k) % 4) for i in range(4)])  17 us
    ppermute x15, starting transfers between devices, y_shift(): return lax.ppermute(value, 'y', [(i, (i + k) % 4) for i in range(4)])  16.9 us
    pallas_call x2, Pallas kernels, attend(): pl.pallas_call(functools.partial(attend_kernel, first * ROWS_STEP), grid_...  11 us
    ppermute x6, waiting for transfers between devices, z_shift(): return lax.ppermute(value, 'head', [(i, (i + k) % 4) for i in range(4)])  10.2 us
    ppermute x6, starting transfers between devices, z_shift(): return lax.ppermute(value, 'head', [(i, (i + k) % 4) for i in range(4)])  9.99 us
    ppermute x2, waiting for transfers between devices, xh_swap(): return lax.ppermute(value, 'xh', [(0, 1), (1, 0)])  7.47 us
  transfers between devices with their start and end apart: 47, of which 16 were waited for; matrix products, arithmetic and copies ran while one was open for 3% of the time, Pallas kernels for 29%

profile of v3, /device:TPU:1, one launch (start us, length us, event | category | flops | bytes accessed | tf_op | source)
XLA Modules:
  0.0 161.8 jit_solution(6369430882262666082)
XLA Ops:
  3.4 1.5 pack.1
  4.9 3.6 %collective-permute-start.4 = (bf16[320,256]{1,0:T(8,128)(2,1)S(1)}, bf16[320,256]{1,0:T(8,128)(2,1)S(1)}, u32[]{:S(2)}, u32[]{:S(2)}) collective-permute-start(bf16[320,256]{1,0:T(8,128)(2,1)S(1)} %get-tuple-element.82), channel_id=1, source_target_pairs={{0,24},{8,0},{16,8},{24,16},{1,25},{9,1},{17,9},{25,17},{2,26},{10... | collective-permute-start | bytes 491528 | tf_op jit(solution)/shard_map/ppermute | solution.py:39
  8.5 2.5 %collective-permute-start.2 = (bf16[256,256]{1,0:T(8,128)(2,1)S(1)}, bf16[256,256]{1,0:T(8,128)(2,1)S(1)}, u32[]{:S(2)}, u32[]{:S(2)}) collective-permute-start(bf16[256,256]{1,0:T(8,128)(2,1)S(1)} %get-tuple-element.78), channel_id=1, source_target_pairs={{0,96},{64,0},{32,64},{96,32},{1,97},{65,1},{33,65},{97,33},{2,98}... | collective-permute-start | bytes 393224 | tf_op jit(solution)/shard_map/ppermute | solution.py:35
  14.6 5.5 %attend.2 = bf16[24,16,128]{2,1,0:T(8,128)(2,1)S(1)} custom-call(s32[48]{0:T(128)S(1)} %copy-done.7, bf16[48,16,128]{2,1,0:T(8,128)(2,1)S(1)} %bitcast.16, bf16[48,128,2,256]{3,2,1,0:T(2,128)(2,1)} %kv_ref.3, bf16[48,2,256]{2,1,0:T(2,128)(2,1)S(1)} %copy-done.3), custom_call_target="tpu_custom_call" | custom-call | tf_op jit(solution)/shard_map/attend/pallas_call | solution.py:127
  20.2 1.6 collective-permute-start.5
  23.7 5.5 %attend.3 = bf16[24,16,128]{2,1,0:T(8,128)(2,1)S(1)} custom-call(s32[48]{0:T(128)S(1)} %copy-done.7, bf16[48,16,128]{2,1,0:T(8,128)(2,1)S(1)} %bitcast.17, bf16[48,128,2,256]{3,2,1,0:T(2,128)(2,1)} %kv_ref.3, bf16[48,2,256]{2,1,0:T(2,128)(2,1)S(1)} %copy-done.4), custom_call_target="tpu_custom_call" | custom-call | tf_op jit(solution)/shard_map/attend/pallas_call | solution.py:127
  29.3 2.1 %collective-permute-start.9 = (bf16[1024,256]{1,0:T(8,128)(2,1)S(1)}, bf16[1024,256]{1,0:T(8,128)(2,1)S(1)}, u32[]{:S(2)}, u32[]{:S(2)}) collective-permute-start(bf16[1024,256]{1,0:T(8,128)(2,1)S(1)} %pad_maximum_fusion.1.refs_1_), channel_id=1, source_target_pairs={{0,96},{64,0},{32,64},{96,32},{1,97},{65,1},{33,65},{97,33},{2,98}... | collective-permute-start | bytes 1572872 | tf_op jit(solution)/shard_map/ppermute | solution.py:35
  31.5 1.3 collective-permute-start.10
  32.9 4.1 %main_product.4 = (f32[512,256]{1,0:T(8,128)S(1)}, f32[512,256]{1,0:T(8,128)S(1)}) custom-call(s32[17]{0:T(128)S(1)} %concatenate.25.info, bf16[512,8192]{1,0:T(8,128)(2,1)} %bitcast.20, bf16[1024,256]{1,0:T(8,128)(2,1)S(1)} %constant_dynamic-update-slice_fusion.refs_0_, bf16[1024,256]{1,0:T(8,128)(2,1)S(1)} %pad_maximum_fusion.1.refs_1_), custom_call_target="tpu_custom_call" | custom-call | tf_op jit(solution)/shard_map/main_product/pallas_call | solution.py:221
  37.0 7.5 %collective-permute-done.10 = bf16[256,256]{1,0:T(8,128)(2,1)S(1)} collective-permute-done((bf16[256,256]{1,0:T(8,128)(2,1)S(1)}, bf16[256,256]{1,0:T(8,128)(2,1)S(1)}, u32[]{:S(2)}, u32[]{:S(2)}) %collective-permute-start.10) | collective-permute-done | bytes 131104 | tf_op jit(solution)/shard_map/ppermute | solution.py:43
  44.5 5.3 %collective-permute-start.13 = (bf16[1024,256]{1,0:T(8,128)(2,1)S(1)}, bf16[1024,256]{1,0:T(8,128)(2,1)S(1)}, u32[]{:S(2)}, u32[]{:S(2)}) collective-permute-start(bf16[1024,256]{1,0:T(8,128)(2,1)S(1)} %constant_dynamic-update-slice_fusion.refs_0_), channel_id=1, source_target_pairs={{0,4},{4,0},{1,5},{5,1},{2,6},{6,2},{3,7},{7,3},{8,12},{12,8},{9,1... | collective-permute-start | bytes 1572872 | tf_op jit(solution)/shard_map/ppermute | solution.py:51
  49.8 1.7 %collective-permute-start.11 = (bf16[1024,256]{1,0:T(8,128)(2,1)S(1)}, bf16[1024,256]{1,0:T(8,128)(2,1)S(1)}, u32[]{:S(2)}, u32[]{:S(2)}) collective-permute-start(bf16[1024,256]{1,0:T(8,128)(2,1)S(1)} %constant_dynamic-update-slice_fusion.refs_0_), channel_id=1, source_target_pairs={{0,16},{8,24},{16,0},{24,8},{1,17},{9,25},{17,1},{25,9},{2,18},{10... | collective-permute-start | bytes 1572872 | tf_op jit(solution)/shard_map/ppermute | solution.py:39
  52.4 1.3 collective-permute-done.20.other_ref
  53.8 4.2 %low_rank.1.refs_0_ = f32[32,128]{1,0:T(8,128)S(1)} custom-call(s32[17]{0:T(128)S(1)} %concatenate.25.info, bf16[512,8192]{1,0:T(8,128)(2,1)} %bitcast.21, bf16[512,256]{1,0:T(8,128)(2,1)S(1)} %constant_dynamic-update-slice_fusion.4.own_ref, bf16[512,256]{1,0:T(8,128)(2,1)S(1)} %collective-permute-done.20.other_ref), custom_call_target="tpu_custom_call" | custom-call | tf_op jit(solution)/shard_map/low_rank/pallas_call | solution.py:184
  58.0 3.8 %collective-permute-start.23 = (f32[32,128]{1,0:T(8,128)S(1)}, f32[32,128]{1,0:T(8,128)S(1)}, u32[]{:S(2)}, u32[]{:S(2)}) collective-permute-start(f32[32,128]{1,0:T(8,128)S(1)} %low_rank.1.refs_0_), channel_id=1, source_target_pairs={{0,3},{1,0},{2,1},{3,2},{4,7},{5,4},{6,5},{7,6},{8,11},{9,8},{10,9... | collective-permute-start | bytes 49160 | tf_op jit(solution)/shard_map/ppermute | solution.py:47
  61.8 1.5 collective-permute-start.22
  64.0 1.8 %collective-permute-done.22.refs_2_ = f32[32,128]{1,0:T(8,128)S(1)} collective-permute-done((f32[32,128]{1,0:T(8,128)S(1)}, f32[32,128]{1,0:T(8,128)S(1)}, u32[]{:S(2)}, u32[]{:S(2)}) %collective-permute-start.22) | collective-permute-done | bytes 16416 | tf_op jit(solution)/shard_map/ppermute | solution.py:47
  65.9 1.2 collective-permute-start.12
  67.2 2.4 %collective-permute-start.15 = (bf16[1024,256]{1,0:T(8,128)(2,1)S(1)}, bf16[1024,256]{1,0:T(8,128)(2,1)S(1)}, u32[]{:S(2)}, u32[]{:S(2)}) collective-permute-start(bf16[1024,256]{1,0:T(8,128)(2,1)S(1)} %collective-permute-done.6.refs_0_), channel_id=1, source_target_pairs={{0,4},{4,0},{1,5},{5,1},{2,6},{6,2},{3,7},{7,3},{8,12},{12,8},{9,1... | collective-permute-start | bytes 1572872 | tf_op jit(solution)/shard_map/ppermute | solution.py:51
  70.4 4.7 %main_product.5 = (f32[512,256]{1,0:T(8,128)S(1)}, f32[512,256]{1,0:T(8,128)S(1)}) custom-call(s32[17]{0:T(128)S(1)} %concatenate.25.info, bf16[512,8192]{1,0:T(8,128)(2,1)} %bitcast.22, bf16[1024,256]{1,0:T(8,128)(2,1)S(1)} %collective-permute-done.6.refs_0_, bf16[1024,256]{1,0:T(8,128)(2,1)S(1)} %collective-permute-done.7.refs_1_, ...), custom_call_target="tpu_custom_call" | custom-call | tf_op jit(solution)/shard_map/main_product/pallas_call | solution.py:221
  75.1 4.0 %collective-permute-done.12.refs_1_ = bf16[1024,256]{1,0:T(8,128)(2,1)S(1)} collective-permute-done((bf16[1024,256]{1,0:T(8,128)(2,1)S(1)}, bf16[1024,256]{1,0:T(8,128)(2,1)S(1)}, u32[]{:S(2)}, u32[]{:S(2)}) %collective-permute-start.12) | collective-permute-done | bytes 524320 | tf_op jit(solution)/shard_map/ppermute | solution.py:35
  79.1 2.7 %collective-permute-start.24 = (bf16[1024,256]{1,0:T(8,128)(2,1)S(1)}, bf16[1024,256]{1,0:T(8,128)(2,1)S(1)}, u32[]{:S(2)}, u32[]{:S(2)}) collective-permute-start(bf16[1024,256]{1,0:T(8,128)(2,1)S(1)} %collective-permute-done.11.refs_0_), channel_id=1, source_target_pairs={{0,4},{4,0},{1,5},{5,1},{2,6},{6,2},{3,7},{7,3},{8,12},{12,8},{9,1... | collective-permute-start | bytes 1572872 | tf_op jit(solution)/shard_map/ppermute | solution.py:51
  82.0 2.1 %collective-permute-start.30 = (bf16[96,2048]{1,0:T(8,128)(2,1)S(1)}, bf16[96,2048]{1,0:T(8,128)(2,1)S(1)}, u32[]{:S(2)}, u32[]{:S(2)}) collective-permute-start(bf16[96,2048]{1,0:T(8,128)(2,1)S(1)} %constant_dynamic-update-slice_fusion.9.refs_0_), channel_id=1, source_target_pairs={{0,24},{8,0},{16,8},{24,16},{1,25},{9,1},{17,9},{25,17},{2,26},{10... | collective-permute-start | bytes 1179656 | tf_op jit(solution)/shard_map/ppermute | solution.py:39
  84.8 5.2 %main_product.6 = (f32[512,256]{1,0:T(8,128)S(1)}, f32[512,256]{1,0:T(8,128)S(1)}) custom-call(s32[17]{0:T(128)S(1)} %concatenate.25.info, bf16[512,8192]{1,0:T(8,128)(2,1)} %bitcast.23, bf16[1024,256]{1,0:T(8,128)(2,1)S(1)} %collective-permute-done.13.refs_0_, bf16[1024,256]{1,0:T(8,128)(2,1)S(1)} %collective-permute-done.14.refs_1_, ...), custom_call_target="tpu_custom_call" | custom-call | tf_op jit(solution)/shard_map/main_product/pallas_call | solution.py:221
  90.0 4.7 %main_product.7 = (f32[512,256]{1,0:T(8,128)S(1)}, f32[512,256]{1,0:T(8,128)S(1)}) custom-call(s32[17]{0:T(128)S(1)} %concatenate.25.info, bf16[512,8192]{1,0:T(8,128)(2,1)} %bitcast.24, bf16[1024,256]{1,0:T(8,128)(2,1)S(1)} %collective-permute-done.11.refs_0_, bf16[1024,256]{1,0:T(8,128)(2,1)S(1)} %collective-permute-done.12.refs_1_, ...), custom_call_target="tpu_custom_call" | custom-call | tf_op jit(solution)/shard_map/main_product/pallas_call | solution.py:221
  94.7 2.6 %finish.1 = (bf16[3,128,2,256]{3,2,1,0:T(2,128)(2,1)S(1)}, bf16[3,128,2,256]{3,2,1,0:T(2,128)(2,1)S(1)}) custom-call(s32[17]{0:T(128)S(1)} %concatenate.25.info, f32[32,128]{1,0:T(8,128)S(1)} %low_rank.1.refs_0_, f32[32,128]{1,0:T(8,128)S(1)} %collective-permute-done.21.refs_1_, f32[32,128]{1,0:T(8,128)S(1)} %collective-permute-done.22.refs_2_, ...), custom_call_target="tpu_custom_call" | custom-call | tf_op jit(solution)/shard_map/finish/pallas_call | solution.py:262
  97.5 1.5 collective-permute-start.27
  98.9 6.1 %collective-permute-done.28.refs_1_ = bf16[96,2048]{1,0:T(8,128)(2,1)S(1)} collective-permute-done((bf16[96,2048]{1,0:T(8,128)(2,1)S(1)}, bf16[96,2048]{1,0:T(8,128)(2,1)S(1)}, u32[]{:S(2)}, u32[]{:S(2)}) %collective-permute-start.28) | collective-permute-done | bytes 393248 | tf_op jit(solution)/shard_map/ppermute | solution.py:39
  105.1 2.0 %collective-permute-done.26.refs_0_ = bf16[3,128,2,256]{3,2,1,0:T(2,128)(2,1)S(1)} collective-permute-done((bf16[3,128,2,256]{3,2,1,0:T(2,128)(2,1)S(1)}, bf16[3,128,2,256]{3,2,1,0:T(2,128)(2,1)S(1)}, u32[]{:S(2)}, u32[]{:S(2)}) %collective-permute-start.26) | collective-permute-done | bytes 393248 | tf_op jit(solution)/shard_map/ppermute | solution.py:485
  107.1 1.3 collective-permute-done.27.refs_1_
  108.4 1.9 %collective-permute-start.35 = (bf16[96,2048]{1,0:T(8,128)(2,1)S(1)}, bf16[96,2048]{1,0:T(8,128)(2,1)S(1)}, u32[]{:S(2)}, u32[]{:S(2)}) collective-permute-start(bf16[96,2048]{1,0:T(8,128)(2,1)S(1)} %constant_dynamic-update-slice_fusion.9.refs_0_), channel_id=1, source_target_pairs={{0,4},{4,0},{1,5},{5,1},{2,6},{6,2},{3,7},{7,3},{8,12},{12,8},{9,1... | collective-permute-start | bytes 1179656 | tf_op jit(solution)/shard_map/ppermute | solution.py:51
  110.8 1.3 choose.3
  112.7 2.7 %collective-permute-start.32 = (bf16[3,128,2,256]{3,2,1,0:T(2,128)(2,1)S(1)}, bf16[3,128,2,256]{3,2,1,0:T(2,128)(2,1)S(1)}, u32[]{:S(2)}, u32[]{:S(2)}) collective-permute-start(bf16[3,128,2,256]{3,2,1,0:T(2,128)(2,1)S(1)} %collective-permute-done.26.refs_0_), channel_id=1, source_target_pairs={{0,24},{8,0},{16,8},{24,16},{1,25},{9,1},{17,9},{25,17},{2,26},{10... | collective-permute-start | bytes 1179656 | tf_op jit(solution)/shard_map/ppermute | solution.py:39
  115.3 2.7 %collective-permute-start.34 = (bf16[3,128,2,256]{3,2,1,0:T(2,128)(2,1)S(1)}, bf16[3,128,2,256]{3,2,1,0:T(2,128)(2,1)S(1)}, u32[]{:S(2)}, u32[]{:S(2)}) collective-permute-start(bf16[3,128,2,256]{3,2,1,0:T(2,128)(2,1)S(1)} %collective-permute-done.27.refs_1_), channel_id=1, source_target_pairs={{0,24},{8,0},{16,8},{24,16},{1,25},{9,1},{17,9},{25,17},{2,26},{10... | collective-permute-start | bytes 1179656 | tf_op jit(solution)/shard_map/ppermute | solution.py:39
  118.2 6.2 %project.1 = (bf16[192,512]{1,0:T(8,128)(2,1)S(1)}, bf16[192,512]{1,0:T(8,128)(2,1)S(1)}, bf16[192,512]{1,0:T(8,128)(2,1)S(1)}, bf16[192,512]{1,0:T(8,128)(2,1)S(1)}) custom-call(s32[17]{0:T(128)S(1)} %concatenate.25.info, s32[768,1]{1,0:T(8,128)S(1)} %broadcast_in_dim.4.keep, bf16[128,2048]{1,0:T(8,128)(2,1)S(1)} %bitcast.18, ...), custom_call_target="tpu_custom_call" | custom-call | tf_op jit(solution)/shard_map/project/pallas_call | solution.py:406
  124.4 2.5 %collective-permute-done.31.refs_0_.refs_2_ = bf16[3,128,2,256]{3,2,1,0:T(2,128)(2,1)S(1)} collective-permute-done((bf16[3,128,2,256]{3,2,1,0:T(2,128)(2,1)S(1)}, bf16[3,128,2,256]{3,2,1,0:T(2,128)(2,1)S(1)}, u32[]{:S(2)}, u32[]{:S(2)}) %collective-permute-start.31) | collective-permute-done | bytes 393248 | tf_op jit(solution)/shard_map/ppermute | solution.py:39
  126.9 5.6 %collective-permute-done.34.refs_3_.refs_5_ = bf16[3,128,2,256]{3,2,1,0:T(2,128)(2,1)S(1)} collective-permute-done((bf16[3,128,2,256]{3,2,1,0:T(2,128)(2,1)S(1)}, bf16[3,128,2,256]{3,2,1,0:T(2,128)(2,1)S(1)}, u32[]{:S(2)}, u32[]{:S(2)}) %collective-permute-start.34) | collective-permute-done | bytes 393248 | tf_op jit(solution)/shard_map/ppermute | solution.py:39
  132.5 2.8 %collective-permute-done.33.refs_2_.refs_4_ = bf16[3,128,2,256]{3,2,1,0:T(2,128)(2,1)S(1)} collective-permute-done((bf16[3,128,2,256]{3,2,1,0:T(2,128)(2,1)S(1)}, bf16[3,128,2,256]{3,2,1,0:T(2,128)(2,1)S(1)}, u32[]{:S(2)}, u32[]{:S(2)}) %collective-permute-start.33) | collective-permute-done | bytes 393248 | tf_op jit(solution)/shard_map/ppermute | solution.py:39
  135.3 2.0 %choose.4 = bf16[2,4,128,2,256]{4,3,2,1,0:T(2,128)(2,1)S(1)} custom-call(s32[17]{0:T(128)S(1)} %concatenate.25.info, bf16[3,128,2,256]{3,2,1,0:T(2,128)(2,1)S(1)} %collective-permute-done.31.refs_0_.refs_2_, bf16[3,128,2,256]{3,2,1,0:T(2,128)(2,1)S(1)} %collective-permute-done.32.refs_1_.refs_3_, ...), custom_call_target="tpu_custom_call" | custom-call | tf_op jit(solution)/shard_map/choose/pallas_call | solution.py:307
  137.3 1.3 collective-permute-start.45
  138.6 2.9 %collective-permute-start.43 = (bf16[192,512]{1,0:T(8,128)(2,1)S(1)}, bf16[192,512]{1,0:T(8,128)(2,1)S(1)}, u32[]{:S(2)}, u32[]{:S(2)}) collective-permute-start(bf16[192,512]{1,0:T(8,128)(2,1)S(1)} %get-tuple-element.139), channel_id=1, source_target_pairs={{0,2},{1,3},{2,0},{3,1},{4,6},{5,7},{6,4},{7,5},{8,10},{9,11},{10,... | collective-permute-start | bytes 589832 | tf_op jit(solution)/shard_map/ppermute | solution.py:47
  142.5 3.8 %collective-permute-done.42 = bf16[192,512]{1,0:T(8,128)(2,1)S(1)} collective-permute-done((bf16[192,512]{1,0:T(8,128)(2,1)S(1)}, bf16[192,512]{1,0:T(8,128)(2,1)S(1)}, u32[]{:S(2)}, u32[]{:S(2)}) %collective-permute-start.42) | collective-permute-done | bytes 196640 | tf_op jit(solution)/shard_map/ppermute | solution.py:47
  146.3 4.4 %collective-permute-done.43 = bf16[192,512]{1,0:T(8,128)(2,1)S(1)} collective-permute-done((bf16[192,512]{1,0:T(8,128)(2,1)S(1)}, bf16[192,512]{1,0:T(8,128)(2,1)S(1)}, u32[]{:S(2)}, u32[]{:S(2)}) %collective-permute-start.43) | collective-permute-done | bytes 196640 | tf_op jit(solution)/shard_map/ppermute | solution.py:47
  151.6 2.0 %pad_maximum_fusion.refs_6_ = bf16[2,6,128,2,256]{4,3,2,1,0:T(2,128)(2,1)S(1)} fusion(bf16[2,4,128,2,256]{4,3,2,1,0:T(2,128)(2,1)S(1)} %collective-permute-done.45, bf16[2,2,128,2,256]{4,3,2,1,0:T(2,128)(2,1)S(1)} %collective-permute-done.39), kind=kLoop, calls=%fused_computation | loop fusion | flops 786432 | bytes 3145728 | tf_op jit(solution)/shard_map/concatenate | solution.py:503
  153.6 2.9 %place.2.refs_3_ = bf16[1,2,2048,2,256]{4,3,2,1,0:T(2,128)(2,1)} custom-call(s32[17]{0:T(128)S(1)} %concatenate.25.info, bf16[3,128,2,256]{3,2,1,0:T(2,128)(2,1)S(1)} %collective-permute-done.26.refs_0_, bf16[3,128,2,256]{3,2,1,0:T(2,128)(2,1)S(1)} %collective-permute-done.27.refs_1_, bf16[3,128,2,256]{3,2,1,0:T(2,128)(2,1)S(1)} %collective-permute-done.31.refs_0_.refs_2_, ...), custom_call_target="tpu_custom_call" | custom-call | tf_op jit(solution)/shard_map/place/pallas_call | solution.py:364
  156.5 1.3 choose.5
  157.8 1.4 collective-permute-start.46
  159.2 1.5 collective-permute-done.46.refs_2_
  (103 shorter events, 16.1 us)
Async XLA Ops:
  4.9 15.3 %collective-permute-start.4 = (bf16[320,256]{1,0:T(8,128)(2,1)S(1)}, bf16[320,256]{1,0:T(8,128)(2,1)S(1)}, u32[]{:S(2)}, u32[]{:S(2)}) collective-permute-start(bf16[320,256]{1,0:T(8,128)(2,1)S(1)} %get-tuple-element.82), channel_id=1, source_target_pairs={{0,24},{8,0},{16,8},{24,16},{1,25},{9,1},{17,9},{25,17},{2,26},{10... | collective-permute-start | bytes 491528 | tf_op jit(solution)/shard_map/ppermute | solution.py:39
  8.5 11.7 %collective-permute-start.3 = (bf16[320,256]{1,0:T(8,128)(2,1)S(1)}, bf16[320,256]{1,0:T(8,128)(2,1)S(1)}, u32[]{:S(2)}, u32[]{:S(2)}) collective-permute-start(bf16[320,256]{1,0:T(8,128)(2,1)S(1)} %get-tuple-element.82), channel_id=1, source_target_pairs={{0,8},{8,16},{16,24},{24,0},{1,9},{9,17},{17,25},{25,1},{2,10},{10... | collective-permute-start | bytes 491528 | tf_op jit(solution)/shard_map/ppermute | solution.py:39
  8.5 11.5 %collective-permute-start.2 = (bf16[256,256]{1,0:T(8,128)(2,1)S(1)}, bf16[256,256]{1,0:T(8,128)(2,1)S(1)}, u32[]{:S(2)}, u32[]{:S(2)}) collective-permute-start(bf16[256,256]{1,0:T(8,128)(2,1)S(1)} %get-tuple-element.78), channel_id=1, source_target_pairs={{0,96},{64,0},{32,64},{96,32},{1,97},{65,1},{33,65},{97,33},{2,98}... | collective-permute-start | bytes 393224 | tf_op jit(solution)/shard_map/ppermute | solution.py:35
  11.0 9.0 %collective-permute-start.1 = (bf16[256,256]{1,0:T(8,128)(2,1)S(1)}, bf16[256,256]{1,0:T(8,128)(2,1)S(1)}, u32[]{:S(2)}, u32[]{:S(2)}) collective-permute-start(bf16[256,256]{1,0:T(8,128)(2,1)S(1)} %get-tuple-element.78), channel_id=1, source_target_pairs={{0,32},{64,96},{32,0},{96,64},{1,33},{65,97},{33,1},{97,65},{2,34}... | collective-permute-start | bytes 393224 | tf_op jit(solution)/shard_map/ppermute | solution.py:35
  11.5 8.7 %collective-permute-start = (bf16[256,256]{1,0:T(8,128)(2,1)S(1)}, bf16[256,256]{1,0:T(8,128)(2,1)S(1)}, u32[]{:S(2)}, u32[]{:S(2)}) collective-permute-start(bf16[256,256]{1,0:T(8,128)(2,1)S(1)} %get-tuple-element.78), channel_id=1, source_target_pairs={{0,64},{64,32},{32,96},{96,0},{1,65},{65,33},{33,97},{97,1},{2,66}... | collective-permute-start | bytes 393224 | tf_op jit(solution)/shard_map/ppermute | solution.py:35
  20.2 9.0 %collective-permute-start.5 = (bf16[320,256]{1,0:T(8,128)(2,1)S(1)}, bf16[320,256]{1,0:T(8,128)(2,1)S(1)}, u32[]{:S(2)}, u32[]{:S(2)}) collective-permute-start(bf16[320,256]{1,0:T(8,128)(2,1)S(1)} %get-tuple-element.82), channel_id=1, source_target_pairs={{0,16},{8,24},{16,0},{24,8},{1,17},{9,25},{17,1},{25,9},{2,18},{10... | collective-permute-start | bytes 491528 | tf_op jit(solution)/shard_map/ppermute | solution.py:39
  21.9 22.6 %collective-permute-start.7 = (bf16[1024,256]{1,0:T(8,128)(2,1)S(1)}, bf16[1024,256]{1,0:T(8,128)(2,1)S(1)}, u32[]{:S(2)}, u32[]{:S(2)}) collective-permute-start(bf16[1024,256]{1,0:T(8,128)(2,1)S(1)} %constant_dynamic-update-slice_fusion.refs_0_), channel_id=1, source_target_pairs={{0,24},{8,0},{16,8},{24,16},{1,25},{9,1},{17,9},{25,17},{2,26},{10... | collective-permute-start | bytes 1572872 | tf_op jit(solution)/shard_map/ppermute | solution.py:39
  23.0 21.4 %collective-permute-start.6 = (bf16[1024,256]{1,0:T(8,128)(2,1)S(1)}, bf16[1024,256]{1,0:T(8,128)(2,1)S(1)}, u32[]{:S(2)}, u32[]{:S(2)}) collective-permute-start(bf16[1024,256]{1,0:T(8,128)(2,1)S(1)} %constant_dynamic-update-slice_fusion.refs_0_), channel_id=1, source_target_pairs={{0,8},{8,16},{16,24},{24,0},{1,9},{9,17},{17,25},{25,1},{2,10},{10... | collective-permute-start | bytes 1572872 | tf_op jit(solution)/shard_map/ppermute | solution.py:39
  29.3 15.2 %collective-permute-start.9 = (bf16[1024,256]{1,0:T(8,128)(2,1)S(1)}, bf16[1024,256]{1,0:T(8,128)(2,1)S(1)}, u32[]{:S(2)}, u32[]{:S(2)}) collective-permute-start(bf16[1024,256]{1,0:T(8,128)(2,1)S(1)} %pad_maximum_fusion.1.refs_1_), channel_id=1, source_target_pairs={{0,96},{64,0},{32,64},{96,32},{1,97},{65,1},{33,65},{97,33},{2,98}... | collective-permute-start | bytes 1572872 | tf_op jit(solution)/shard_map/ppermute | solution.py:35
  31.4 13.1 %collective-permute-start.8 = (bf16[1024,256]{1,0:T(8,128)(2,1)S(1)}, bf16[1024,256]{1,0:T(8,128)(2,1)S(1)}, u32[]{:S(2)}, u32[]{:S(2)}) collective-permute-start(bf16[1024,256]{1,0:T(8,128)(2,1)S(1)} %pad_maximum_fusion.1.refs_1_), channel_id=1, source_target_pairs={{0,64},{64,32},{32,96},{96,0},{1,65},{65,33},{33,97},{97,1},{2,66}... | collective-permute-start | bytes 1572872 | tf_op jit(solution)/shard_map/ppermute | solution.py:35
  31.5 13.0 %collective-permute-start.10 = (bf16[256,256]{1,0:T(8,128)(2,1)S(1)}, bf16[256,256]{1,0:T(8,128)(2,1)S(1)}, u32[]{:S(2)}, u32[]{:S(2)}) collective-permute-start(bf16[256,256]{1,0:T(8,128)(2,1)S(1)} %pad_maximum_fusion.3), channel_id=1, source_target_pairs={{0,32},{32,0},{1,33},{33,1},{2,34},{34,2},{3,35},{35,3},{4,36},{36... | collective-permute-start | bytes 393224 | tf_op jit(solution)/shard_map/ppermute | solution.py:43
  44.5 25.1 %collective-permute-start.13 = (bf16[1024,256]{1,0:T(8,128)(2,1)S(1)}, bf16[1024,256]{1,0:T(8,128)(2,1)S(1)}, u32[]{:S(2)}, u32[]{:S(2)}) collective-permute-start(bf16[1024,256]{1,0:T(8,128)(2,1)S(1)} %constant_dynamic-update-slice_fusion.refs_0_), channel_id=1, source_target_pairs={{0,4},{4,0},{1,5},{5,1},{2,6},{6,2},{3,7},{7,3},{8,12},{12,8},{9,1... | collective-permute-start | bytes 1572872 | tf_op jit(solution)/shard_map/ppermute | solution.py:51
  49.8 19.9 %collective-permute-start.11 = (bf16[1024,256]{1,0:T(8,128)(2,1)S(1)}, bf16[1024,256]{1,0:T(8,128)(2,1)S(1)}, u32[]{:S(2)}, u32[]{:S(2)}) collective-permute-start(bf16[1024,256]{1,0:T(8,128)(2,1)S(1)} %constant_dynamic-update-slice_fusion.refs_0_), channel_id=1, source_target_pairs={{0,16},{8,24},{16,0},{24,8},{1,17},{9,25},{17,1},{25,9},{2,18},{10... | collective-permute-start | bytes 1572872 | tf_op jit(solution)/shard_map/ppermute | solution.py:39
  51.5 18.7 %collective-permute-start.14 = (bf16[1024,256]{1,0:T(8,128)(2,1)S(1)}, bf16[1024,256]{1,0:T(8,128)(2,1)S(1)}, u32[]{:S(2)}, u32[]{:S(2)}) collective-permute-start(bf16[1024,256]{1,0:T(8,128)(2,1)S(1)} %pad_maximum_fusion.1.refs_1_), channel_id=1, source_target_pairs={{0,4},{4,0},{1,5},{5,1},{2,6},{6,2},{3,7},{7,3},{8,12},{12,8},{9,1... | collective-permute-start | bytes 1572872 | tf_op jit(solution)/shard_map/ppermute | solution.py:51
  51.8 2.0 %collective-permute-start.20 = (bf16[512,256]{1,0:T(8,128)(2,1)S(1)}, bf16[512,256]{1,0:T(8,128)(2,1)S(1)}, u32[]{:S(2)}, u32[]{:S(2)}) collective-permute-start(bf16[512,256]{1,0:T(8,128)(2,1)S(1)} %constant_dynamic-update-slice_fusion.4.own_ref), channel_id=1, source_target_pairs={{0,4},{4,0},{1,5},{5,1},{2,6},{6,2},{3,7},{7,3},{8,12},{12,8},{9,1... | collective-permute-start | bytes 786440 | tf_op jit(solution)/shard_map/ppermute | solution.py:51
  52.0 9.8 %collective-permute-start.19 = (bf16[48,2048]{1,0:T(8,128)(2,1)S(1)}, bf16[48,2048]{1,0:T(8,128)(2,1)S(1)}, u32[]{:S(2)}, u32[]{:S(2)}) collective-permute-start(bf16[48,2048]{1,0:T(8,128)(2,1)S(1)} %bitcast.25), channel_id=1, source_target_pairs={{0,32},{32,0},{1,33},{33,1},{2,34},{34,2},{3,35},{35,3},{4,36},{36... | collective-permute-start | bytes 589832 | tf_op jit(solution)/shard_map/ppermute | solution.py:43
  58.0 5.4 %collective-permute-start.23 = (f32[32,128]{1,0:T(8,128)S(1)}, f32[32,128]{1,0:T(8,128)S(1)}, u32[]{:S(2)}, u32[]{:S(2)}) collective-permute-start(f32[32,128]{1,0:T(8,128)S(1)} %low_rank.1.refs_0_), channel_id=1, source_target_pairs={{0,3},{1,0},{2,1},{3,2},{4,7},{5,4},{6,5},{7,6},{8,11},{9,8},{10,9... | collective-permute-start | bytes 49160 | tf_op jit(solution)/shard_map/ppermute | solution.py:47
  61.8 4.1 %collective-permute-start.22 = (f32[32,128]{1,0:T(8,128)S(1)}, f32[32,128]{1,0:T(8,128)S(1)}, u32[]{:S(2)}, u32[]{:S(2)}) collective-permute-start(f32[32,128]{1,0:T(8,128)S(1)} %low_rank.1.refs_0_), channel_id=1, source_target_pairs={{0,2},{1,3},{2,0},{3,1},{4,6},{5,7},{6,4},{7,5},{8,10},{9,11},{10,... | collective-permute-start | bytes 49160 | tf_op jit(solution)/shard_map/ppermute | solution.py:47
  63.3 3.9 %collective-permute-start.21 = (f32[32,128]{1,0:T(8,128)S(1)}, f32[32,128]{1,0:T(8,128)S(1)}, u32[]{:S(2)}, u32[]{:S(2)}) collective-permute-start(f32[32,128]{1,0:T(8,128)S(1)} %low_rank.1.refs_0_), channel_id=1, source_target_pairs={{0,1},{1,2},{2,3},{3,0},{4,5},{5,6},{6,7},{7,4},{8,9},{9,10},{10,1... | collective-permute-start | bytes 49160 | tf_op jit(solution)/shard_map/ppermute | solution.py:47
  65.9 13.2 %collective-permute-start.12 = (bf16[1024,256]{1,0:T(8,128)(2,1)S(1)}, bf16[1024,256]{1,0:T(8,128)(2,1)S(1)}, u32[]{:S(2)}, u32[]{:S(2)}) collective-permute-start(bf16[1024,256]{1,0:T(8,128)(2,1)S(1)} %pad_maximum_fusion.1.refs_1_), channel_id=1, source_target_pairs={{0,32},{64,96},{32,0},{96,64},{1,33},{65,97},{33,1},{97,65},{2,34}... | collective-permute-start | bytes 1572872 | tf_op jit(solution)/shard_map/ppermute | solution.py:35
  67.2 11.9 %collective-permute-start.15 = (bf16[1024,256]{1,0:T(8,128)(2,1)S(1)}, bf16[1024,256]{1,0:T(8,128)(2,1)S(1)}, u32[]{:S(2)}, u32[]{:S(2)}) collective-permute-start(bf16[1024,256]{1,0:T(8,128)(2,1)S(1)} %collective-permute-done.6.refs_0_), channel_id=1, source_target_pairs={{0,4},{4,0},{1,5},{5,1},{2,6},{6,2},{3,7},{7,3},{8,12},{12,8},{9,1... | collective-permute-start | bytes 1572872 | tf_op jit(solution)/shard_map/ppermute | solution.py:51
  69.6 9.4 %collective-permute-start.16 = (bf16[1024,256]{1,0:T(8,128)(2,1)S(1)}, bf16[1024,256]{1,0:T(8,128)(2,1)S(1)}, u32[]{:S(2)}, u32[]{:S(2)}) collective-permute-start(bf16[1024,256]{1,0:T(8,128)(2,1)S(1)} %collective-permute-done.7.refs_1_), channel_id=1, source_target_pairs={{0,4},{4,0},{1,5},{5,1},{2,6},{6,2},{3,7},{7,3},{8,12},{12,8},{9,1... | collective-permute-start | bytes 1572872 | tf_op jit(solution)/shard_map/ppermute | solution.py:51
  69.7 9.4 %collective-permute-start.17 = (bf16[1024,256]{1,0:T(8,128)(2,1)S(1)}, bf16[1024,256]{1,0:T(8,128)(2,1)S(1)}, u32[]{:S(2)}, u32[]{:S(2)}) collective-permute-start(bf16[1024,256]{1,0:T(8,128)(2,1)S(1)} %collective-permute-done.8.refs_2_), channel_id=1, source_target_pairs={{0,4},{4,0},{1,5},{5,1},{2,6},{6,2},{3,7},{7,3},{8,12},{12,8},{9,1... | collective-permute-start | bytes 1572872 | tf_op jit(solution)/shard_map/ppermute | solution.py:51
  70.2 8.9 %collective-permute-start.18 = (bf16[1024,256]{1,0:T(8,128)(2,1)S(1)}, bf16[1024,256]{1,0:T(8,128)(2,1)S(1)}, u32[]{:S(2)}, u32[]{:S(2)}) collective-permute-start(bf16[1024,256]{1,0:T(8,128)(2,1)S(1)} %collective-permute-done.9.refs_3_), channel_id=1, source_target_pairs={{0,4},{4,0},{1,5},{5,1},{2,6},{6,2},{3,7},{7,3},{8,12},{12,8},{9,1... | collective-permute-start | bytes 1572872 | tf_op jit(solution)/shard_map/ppermute | solution.py:51
  79.1 10.9 %collective-permute-start.24 = (bf16[1024,256]{1,0:T(8,128)(2,1)S(1)}, bf16[1024,256]{1,0:T(8,128)(2,1)S(1)}, u32[]{:S(2)}, u32[]{:S(2)}) collective-permute-start(bf16[1024,256]{1,0:T(8,128)(2,1)S(1)} %collective-permute-done.11.refs_0_), channel_id=1, source_target_pairs={{0,4},{4,0},{1,5},{5,1},{2,6},{6,2},{3,7},{7,3},{8,12},{12,8},{9,1... | collective-permute-start | bytes 1572872 | tf_op jit(solution)/shard_map/ppermute | solution.py:51
  81.8 8.2 %collective-permute-start.25 = (bf16[1024,256]{1,0:T(8,128)(2,1)S(1)}, bf16[1024,256]{1,0:T(8,128)(2,1)S(1)}, u32[]{:S(2)}, u32[]{:S(2)}) collective-permute-start(bf16[1024,256]{1,0:T(8,128)(2,1)S(1)} %collective-permute-done.12.refs_1_), channel_id=1, source_target_pairs={{0,4},{4,0},{1,5},{5,1},{2,6},{6,2},{3,7},{7,3},{8,12},{12,8},{9,1... | collective-permute-start | bytes 1572872 | tf_op jit(solution)/shard_map/ppermute | solution.py:51
  82.0 17.0 %collective-permute-start.30 = (bf16[96,2048]{1,0:T(8,128)(2,1)S(1)}, bf16[96,2048]{1,0:T(8,128)(2,1)S(1)}, u32[]{:S(2)}, u32[]{:S(2)}) collective-permute-start(bf16[96,2048]{1,0:T(8,128)(2,1)S(1)} %constant_dynamic-update-slice_fusion.9.refs_0_), channel_id=1, source_target_pairs={{0,24},{8,0},{16,8},{24,16},{1,25},{9,1},{17,9},{25,17},{2,26},{10... | collective-permute-start | bytes 1179656 | tf_op jit(solution)/shard_map/ppermute | solution.py:39
  84.1 14.8 %collective-permute-start.29 = (bf16[96,2048]{1,0:T(8,128)(2,1)S(1)}, bf16[96,2048]{1,0:T(8,128)(2,1)S(1)}, u32[]{:S(2)}, u32[]{:S(2)}) collective-permute-start(bf16[96,2048]{1,0:T(8,128)(2,1)S(1)} %constant_dynamic-update-slice_fusion.9.refs_0_), channel_id=1, source_target_pairs={{0,16},{8,24},{16,0},{24,8},{1,17},{9,25},{17,1},{25,9},{2,18},{10... | collective-permute-start | bytes 1179656 | tf_op jit(solution)/shard_map/ppermute | solution.py:39
  84.7 20.3 %collective-permute-start.28 = (bf16[96,2048]{1,0:T(8,128)(2,1)S(1)}, bf16[96,2048]{1,0:T(8,128)(2,1)S(1)}, u32[]{:S(2)}, u32[]{:S(2)}) collective-permute-start(bf16[96,2048]{1,0:T(8,128)(2,1)S(1)} %constant_dynamic-update-slice_fusion.9.refs_0_), channel_id=1, source_target_pairs={{0,8},{8,16},{16,24},{24,0},{1,9},{9,17},{17,25},{25,1},{2,10},{10... | collective-permute-start | bytes 1179656 | tf_op jit(solution)/shard_map/ppermute | solution.py:39
  94.7 23.5 %copy-start = (bf16[2048,8,16]{0,2,1:T(8,128)(2,1)S(1)}, bf16[2048,8,16]{0,2,1:T(8,128)(2,1)}, u32[]{:S(2)}) copy-start(bf16[2048,8,16]{0,2,1:T(8,128)(2,1)} %param.26) | copy-start | bytes 1572868
  97.4 9.7 %collective-permute-start.26 = (bf16[3,128,2,256]{3,2,1,0:T(2,128)(2,1)S(1)}, bf16[3,128,2,256]{3,2,1,0:T(2,128)(2,1)S(1)}, u32[]{:S(2)}, u32[]{:S(2)}) collective-permute-start(bf16[3,128,2,256]{3,2,1,0:T(2,128)(2,1)S(1)} %get-tuple-element.121), channel_id=1, source_target_pairs={{0,64},{64,0},{1,65},{65,1},{2,66},{66,2},{3,67},{67,3},{4,68},{68... | collective-permute-start | bytes 1179656 | tf_op jit(solution)/shard_map/ppermute | solution.py:485
  97.5 10.9 %collective-permute-start.27 = (bf16[3,128,2,256]{3,2,1,0:T(2,128)(2,1)S(1)}, bf16[3,128,2,256]{3,2,1,0:T(2,128)(2,1)S(1)}, u32[]{:S(2)}, u32[]{:S(2)}) collective-permute-start(bf16[3,128,2,256]{3,2,1,0:T(2,128)(2,1)S(1)} %get-tuple-element.122), channel_id=1, source_target_pairs={{0,96},{32,64},{64,32},{96,0},{1,97},{33,65},{65,33},{97,1},{2,98}... | collective-permute-start | bytes 1179656 | tf_op jit(solution)/shard_map/ppermute | solution.py:486
  108.4 4.3 %collective-permute-start.35 = (bf16[96,2048]{1,0:T(8,128)(2,1)S(1)}, bf16[96,2048]{1,0:T(8,128)(2,1)S(1)}, u32[]{:S(2)}, u32[]{:S(2)}) collective-permute-start(bf16[96,2048]{1,0:T(8,128)(2,1)S(1)} %constant_dynamic-update-slice_fusion.9.refs_0_), channel_id=1, source_target_pairs={{0,4},{4,0},{1,5},{5,1},{2,6},{6,2},{3,7},{7,3},{8,12},{12,8},{9,1... | collective-permute-start | bytes 1179656 | tf_op jit(solution)/shard_map/ppermute | solution.py:51
  110.3 5.0 %collective-permute-start.36 = (bf16[96,2048]{1,0:T(8,128)(2,1)S(1)}, bf16[96,2048]{1,0:T(8,128)(2,1)S(1)}, u32[]{:S(2)}, u32[]{:S(2)}) collective-permute-start(bf16[96,2048]{1,0:T(8,128)(2,1)S(1)} %collective-permute-done.28.refs_1_), channel_id=1, source_target_pairs={{0,4},{4,0},{1,5},{5,1},{2,6},{6,2},{3,7},{7,3},{8,12},{12,8},{9,1... | collective-permute-start | bytes 1179656 | tf_op jit(solution)/shard_map/ppermute | solution.py:51
  110.3 5.1 %collective-permute-start.37 = (bf16[96,2048]{1,0:T(8,128)(2,1)S(1)}, bf16[96,2048]{1,0:T(8,128)(2,1)S(1)}, u32[]{:S(2)}, u32[]{:S(2)}) collective-permute-start(bf16[96,2048]{1,0:T(8,128)(2,1)S(1)} %collective-permute-done.29.refs_2_), channel_id=1, source_target_pairs={{0,4},{4,0},{1,5},{5,1},{2,6},{6,2},{3,7},{7,3},{8,12},{12,8},{9,1... | collective-permute-start | bytes 1179656 | tf_op jit(solution)/shard_map/ppermute | solution.py:51
  110.8 7.2 %collective-permute-start.38 = (bf16[96,2048]{1,0:T(8,128)(2,1)S(1)}, bf16[96,2048]{1,0:T(8,128)(2,1)S(1)}, u32[]{:S(2)}, u32[]{:S(2)}) collective-permute-start(bf16[96,2048]{1,0:T(8,128)(2,1)S(1)} %collective-permute-done.30.refs_3_), channel_id=1, source_target_pairs={{0,4},{4,0},{1,5},{5,1},{2,6},{6,2},{3,7},{7,3},{8,12},{12,8},{9,1... | collective-permute-start | bytes 1179656 | tf_op jit(solution)/shard_map/ppermute | solution.py:51
  112.1 23.2 %collective-permute-start.39 = (bf16[2,2,128,2,256]{4,3,2,1,0:T(2,128)(2,1)S(1)}, bf16[2,2,128,2,256]{4,3,2,1,0:T(2,128)(2,1)S(1)}, u32[]{:S(2)}, u32[]{:S(2)}) collective-permute-start(bf16[2,2,128,2,256]{4,3,2,1,0:T(2,128)(2,1)S(1)} %choose.3), channel_id=1, source_target_pairs={{0,4},{4,0},{1,5},{5,1},{2,6},{6,2},{3,7},{7,3},{8,12},{12,8},{9,1... | collective-permute-start | bytes 1572872 | tf_op jit(solution)/shard_map/ppermute | solution.py:51
  112.7 11.8 %collective-permute-start.32 = (bf16[3,128,2,256]{3,2,1,0:T(2,128)(2,1)S(1)}, bf16[3,128,2,256]{3,2,1,0:T(2,128)(2,1)S(1)}, u32[]{:S(2)}, u32[]{:S(2)}) collective-permute-start(bf16[3,128,2,256]{3,2,1,0:T(2,128)(2,1)S(1)} %collective-permute-done.26.refs_0_), channel_id=1, source_target_pairs={{0,24},{8,0},{16,8},{24,16},{1,25},{9,1},{17,9},{25,17},{2,26},{10... | collective-permute-start | bytes 1179656 | tf_op jit(solution)/shard_map/ppermute | solution.py:39
  115.3 11.6 %collective-permute-start.31 = (bf16[3,128,2,256]{3,2,1,0:T(2,128)(2,1)S(1)}, bf16[3,128,2,256]{3,2,1,0:T(2,128)(2,1)S(1)}, u32[]{:S(2)}, u32[]{:S(2)}) collective-permute-start(bf16[3,128,2,256]{3,2,1,0:T(2,128)(2,1)S(1)} %collective-permute-done.26.refs_0_), channel_id=1, source_target_pairs={{0,8},{8,16},{16,24},{24,0},{1,9},{9,17},{17,25},{25,1},{2,10},{10... | collective-permute-start | bytes 1179656 | tf_op jit(solution)/shard_map/ppermute | solution.py:39
  115.3 17.1 %collective-permute-start.34 = (bf16[3,128,2,256]{3,2,1,0:T(2,128)(2,1)S(1)}, bf16[3,128,2,256]{3,2,1,0:T(2,128)(2,1)S(1)}, u32[]{:S(2)}, u32[]{:S(2)}) collective-permute-start(bf16[3,128,2,256]{3,2,1,0:T(2,128)(2,1)S(1)} %collective-permute-done.27.refs_1_), channel_id=1, source_target_pairs={{0,24},{8,0},{16,8},{24,16},{1,25},{9,1},{17,9},{25,17},{2,26},{10... | collective-permute-start | bytes 1179656 | tf_op jit(solution)/shard_map/ppermute | solution.py:39
  118.0 17.3 %collective-permute-start.33 = (bf16[3,128,2,256]{3,2,1,0:T(2,128)(2,1)S(1)}, bf16[3,128,2,256]{3,2,1,0:T(2,128)(2,1)S(1)}, u32[]{:S(2)}, u32[]{:S(2)}) collective-permute-start(bf16[3,128,2,256]{3,2,1,0:T(2,128)(2,1)S(1)} %collective-permute-done.27.refs_1_), channel_id=1, source_target_pairs={{0,8},{8,16},{16,24},{24,0},{1,9},{9,17},{17,25},{25,1},{2,10},{10... | collective-permute-start | bytes 1179656 | tf_op jit(solution)/shard_map/ppermute | solution.py:39
  137.3 14.2 %collective-permute-start.45 = (bf16[2,4,128,2,256]{4,3,2,1,0:T(2,128)(2,1)S(1)}, bf16[2,4,128,2,256]{4,3,2,1,0:T(2,128)(2,1)S(1)}, u32[]{:S(2)}, u32[]{:S(2)}) collective-permute-start(bf16[2,4,128,2,256]{4,3,2,1,0:T(2,128)(2,1)S(1)} %choose.4), channel_id=1, source_target_pairs={{0,4},{4,0},{1,5},{5,1},{2,6},{6,2},{3,7},{7,3},{8,12},{12,8},{9,1... | collective-permute-start | bytes 3145736 | tf_op jit(solution)/shard_map/ppermute | solution.py:51
  138.6 7.7 %collective-permute-start.42 = (bf16[192,512]{1,0:T(8,128)(2,1)S(1)}, bf16[192,512]{1,0:T(8,128)(2,1)S(1)}, u32[]{:S(2)}, u32[]{:S(2)}) collective-permute-start(bf16[192,512]{1,0:T(8,128)(2,1)S(1)} %get-tuple-element.138), channel_id=1, source_target_pairs={{0,1},{1,2},{2,3},{3,0},{4,5},{5,6},{6,7},{7,4},{8,9},{9,10},{10,1... | collective-permute-start | bytes 589832 | tf_op jit(solution)/shard_map/ppermute | solution.py:47
  138.6 12.1 %collective-permute-start.43 = (bf16[192,512]{1,0:T(8,128)(2,1)S(1)}, bf16[192,512]{1,0:T(8,128)(2,1)S(1)}, u32[]{:S(2)}, u32[]{:S(2)}) collective-permute-start(bf16[192,512]{1,0:T(8,128)(2,1)S(1)} %get-tuple-element.139), channel_id=1, source_target_pairs={{0,2},{1,3},{2,0},{3,1},{4,6},{5,7},{6,4},{7,5},{8,10},{9,11},{10,... | collective-permute-start | bytes 589832 | tf_op jit(solution)/shard_map/ppermute | solution.py:47
  141.5 9.3 %collective-permute-start.44 = (bf16[192,512]{1,0:T(8,128)(2,1)S(1)}, bf16[192,512]{1,0:T(8,128)(2,1)S(1)}, u32[]{:S(2)}, u32[]{:S(2)}) collective-permute-start(bf16[192,512]{1,0:T(8,128)(2,1)S(1)} %get-tuple-element.140), channel_id=1, source_target_pairs={{0,3},{1,0},{2,1},{3,2},{4,7},{5,4},{6,5},{7,6},{8,11},{9,8},{10,9... | collective-permute-start | bytes 589832 | tf_op jit(solution)/shard_map/ppermute | solution.py:47
  142.5 14.0 %collective-permute-start.40 = (bf16[3,128,2,256]{3,2,1,0:T(2,128)(2,1)S(1)}, bf16[3,128,2,256]{3,2,1,0:T(2,128)(2,1)S(1)}, u32[]{:S(2)}, u32[]{:S(2)}) collective-permute-start(bf16[3,128,2,256]{3,2,1,0:T(2,128)(2,1)S(1)} %collective-permute-done.31.refs_0_.refs_2_), channel_id=1, source_target_pairs={{0,8},{8,16},{16,24},{24,0},{1,9},{9,17},{17,25},{25,1},{2,10},{10... | collective-permute-start | bytes 1179656 | tf_op jit(solution)/shard_map/ppermute | solution.py:39
  146.3 10.2 %collective-permute-start.41 = (bf16[3,128,2,256]{3,2,1,0:T(2,128)(2,1)S(1)}, bf16[3,128,2,256]{3,2,1,0:T(2,128)(2,1)S(1)}, u32[]{:S(2)}, u32[]{:S(2)}) collective-permute-start(bf16[3,128,2,256]{3,2,1,0:T(2,128)(2,1)S(1)} %collective-permute-done.34.refs_3_.refs_5_), channel_id=1, source_target_pairs={{0,24},{8,0},{16,8},{24,16},{1,25},{9,1},{17,9},{25,17},{2,26},{10... | collective-permute-start | bytes 1179656 | tf_op jit(solution)/shard_map/ppermute | solution.py:39
  157.8 2.9 %collective-permute-start.46 = (bf16[2,2,128,2,256]{4,3,2,1,0:T(2,128)(2,1)S(1)}, bf16[2,2,128,2,256]{4,3,2,1,0:T(2,128)(2,1)S(1)}, u32[]{:S(2)}, u32[]{:S(2)}) collective-permute-start(bf16[2,2,128,2,256]{4,3,2,1,0:T(2,128)(2,1)S(1)} %choose.5), channel_id=1, source_target_pairs={{0,4},{4,0},{1,5},{5,1},{2,6},{6,2},{3,7},{7,3},{8,12},{12,8},{9,1... | collective-permute-start | bytes 1572872 | tf_op jit(solution)/shard_map/ppermute | solution.py:51
  (8 other events, 64.1 us)

commit v4 on v3

--- a/solution.py
+++ b/solution.py
@@ -23,7 +23,7 @@
 ANY = pl.BlockSpec(memory_space=pl.ANY)
 
 
-def params(limit=48):
+def params(limit=8):
     return pltpu.CompilerParams(vmem_limit_bytes=limit * MIB)
 
 
@@ -45,6 +45,10 @@
 
 def z_shift(value, k):
     return lax.ppermute(value, "head", [(i, (i + k) % 4) for i in range(4)])
+
+
+def z_flip(value, mask):
+    return lax.ppermute(value, "head", [(i, i ^ mask) for i in range(4)])
 
 
 def core_swap(value):
@@ -192,12 +196,12 @@
 
 
 def main_kernel(kinds, fresh, info, prompt, *refs):
-    n = len(kinds)
+    n = max(kind[3] for kind in kinds) + 1
     blocks, sums, outs = refs[:n], refs[n:-2], refs[-2:]
     pool, xh, y, core = info[POOL], info[XH], info[Y], info[CORE]
     x = 2 * xh + pool
     done = [fresh, fresh]
-    for (kv, j, partner), ref in zip(kinds, blocks):
+    for kv, j, partner, which, block in kinds:
         c_of = 1 - core if partner else core
         tokens = []
         for i in range(4):
@@ -205,7 +209,9 @@
             yi = x_order(y)[j if kv == 0 else i]
             tokens.append(prompt[:, pl.ds(chunk_start(xi, yi, c_of), 256)])
         part = jnp.dot(
-            jnp.concatenate(tokens, 1), ref[...], preferred_element_type=jnp.float32
+            jnp.concatenate(tokens, 1),
+            blocks[which][block * 1024 : (block + 1) * 1024],
+            preferred_element_type=jnp.float32,
         )
         if done[kv] is True:
             outs[kv][...] = part
@@ -229,15 +235,15 @@
 
 
 def finish_kernel(info, *refs):
-    lows, k_ref, v_ref, up_ref, near_ref, far_ref = refs[0:4], *refs[4:]
+    lows, k_ref, v_ref, up_ref, near_ref, far_ref = refs
     pool, xh, z = info[POOL], info[XH], info[HEAD]
     owners = [info[DEST + pool * REQ_POOL + r] for r in range(REQ_POOL)]
     dims = (((0,), (0,)), ((), ()))
     for n in range(REQ_POOL):
-        r = x_order(z)[n]
+        r = z ^ n
         a = info[ADAPTER + r]
         rows = pl.ds(pl.multiple_of(r * 128, 128), 128)
-        low = lows[n][...]
+        low = lows[n * 32 : (n + 1) * 32]
         both = []
         for kv, ref in enumerate((k_ref, v_ref)):
             value = ref[rows, :] + split_dot(low[kv * 16 : (kv + 1) * 16], up_ref[a, kv], dims)
@@ -261,12 +267,12 @@
     shape = jax.ShapeDtypeStruct((X_SLOTS, 128, 2, 256), jnp.bfloat16)
     return pl.pallas_call(
         finish_kernel,
-        in_specs=[SMEM] + [VMEM] * 7,
+        in_specs=[SMEM] + [VMEM] * 4,
         out_specs=[VMEM, VMEM],
         out_shape=[shape, shape],
         compiler_params=params(),
         name="finish",
-    )(info, *lows, *sums, up)
+    )(info, lows, *sums, up)
 
 
 def slots_of(info, pool, xh, owner):
@@ -285,39 +291,10 @@
     return index, used
 
 
-def choose_kernel(info, *refs):
-    ins, out, sems = refs[:-2], refs[-2], refs[-1]
-    xh = info[XH]
-    owner = xh * 8 + info[Y] * 2 + (1 - info[CORE])
-    index = slots_of(info, 1 - info[POOL], xh, owner)[0]
-    n = len(ins)
-    copies = [
-        pltpu.make_async_copy(ins[b].at[index[j]], out.at[j, b], sems.at[j * n + b])
-        for j in range(CAP)
-        for b in range(n)
-    ]
-    for c in copies:
-        c.start()
-    for c in copies:
-        c.wait()
-
-
-def choose(info, parts):
-    n = len(parts)
-    return pl.pallas_call(
-        choose_kernel,
-        in_specs=[SMEM] + [VMEM] * n,
-        out_specs=VMEM,
-        out_shape=jax.ShapeDtypeStruct((CAP, n, 128, 2, 256), jnp.bfloat16),
-        scratch_shapes=[pltpu.SemaphoreType.DMA((CAP * n,))],
-        compiler_params=params(),
-        name="choose",
-    )(info, *parts)
-
-
-def place_kernel(kinds, rest, info, *refs):
-    n = len(kinds)
-    ins, others = refs[:n], refs[n]
+def place_kernel(kinds, rest, sizes, info, *refs):
+    n = len(sizes)
+    at = [(i, b) for i, size in enumerate(sizes) for b in range(size)]
+    ins, others = refs[:n], refs[n : 2 * n]
     out, zero, sems = refs[-3], refs[-2], refs[-1]
     xh, y, core = info[XH], info[Y], info[CORE]
     index, used = slots_of(info, 1 - info[POOL], xh, xh * 8 + y * 2 + core)
@@ -326,14 +303,15 @@
 
     def spot(j, kind, c_of):
         side = xh if kind[0] == 0 else 1 - xh
-        at = (side * 8 + x_order(y)[kind[1]] * 2 + c_of) * 128
-        return out.at[0, j, pl.ds(pl.multiple_of(at, 128), 128)]
+        token = (side * 8 + x_order(y)[kind[1]] * 2 + c_of) * 128
+        return out.at[0, j, pl.ds(pl.multiple_of(token, 128), 128)]
 
     def transfers(j):
         full = []
         for b, kind in enumerate(kinds):
-            full.append((ins[b].at[index[j]], spot(j, kind, core)))
-            full.append((others.at[j, b], spot(j, kind, 1 - core)))
+            i, k = at[b]
+            full.append((ins[i].at[k, index[j]], spot(j, kind, core)))
+            full.append((others[i].at[k, index[j]], spot(j, kind, 1 - core)))
         return [
             pltpu.make_async_copy(src, dst, sems.at[j, i]) for i, (src, dst) in enumerate(full)
         ]
@@ -360,10 +338,10 @@
 
 def place(info, kinds, rest, parts, others, out=None):
     shape = jax.ShapeDtypeStruct((1, CAP, 2048, 2, 256), jnp.bfloat16)
-    ins = [info, *parts, others] + ([] if out is None else [out])
-    return pl.pallas_call(
-        functools.partial(place_kernel, kinds, rest),
-        in_specs=[SMEM] + [VMEM] * (len(parts) + 1) + ([] if out is None else [ANY]),
+    ins = [info, *parts, *others] + ([] if out is None else [out])
+    return pl.pallas_call(
+        functools.partial(place_kernel, kinds, rest, tuple(p.shape[0] for p in parts)),
+        in_specs=[SMEM] + [VMEM] * (len(parts) + len(others)) + ([] if out is None else [ANY]),
         out_specs=ANY,
         out_shape=shape,
         scratch_shapes=[
@@ -377,7 +355,7 @@
 
 
 def project_kernel(info, keep, down, up, w_ref, *refs):
-    ins, outs, res = refs[:8], refs[8:12], refs[12]
+    ins, outs, res = refs[:2], refs[2:6], refs[6]
     xh, y, core, z = info[XH], info[Y], info[CORE], info[HEAD]
     value = jnp.concatenate([ref[...] for ref in ins], 0)
     out = jnp.dot(value, w_ref[...], preferred_element_type=jnp.float32)
@@ -405,7 +383,7 @@
     rows, width = 768, weight.shape[1]
     return pl.pallas_call(
         project_kernel,
-        in_specs=[SMEM] + [VMEM] * 12,
+        in_specs=[SMEM] + [VMEM] * 6,
         out_specs=[VMEM] * 4,
         out_shape=[jax.ShapeDtypeStruct((rows // 4, width), jnp.bfloat16)] * 4,
         scratch_shapes=[pltpu.VMEM((rows, width), jnp.bfloat16)],
@@ -439,6 +417,7 @@
     place_of = jnp.stack([lax.axis_index(a) for a in axes]).astype(jnp.int32)
     info = jnp.concatenate([place_of, destination, request_adapter_index])
     tokens = prompt.reshape(-1, prompt.shape[2])
+    tokens = pltpu.with_memory_space_constraint(tokens, pltpu.VMEM)
     rows, heads = rotated_query.shape[0], rotated_query.shape[1] // HEAD_DIM
     query = rotated_query.reshape(rows, heads, HEAD_DIM)
 
@@ -446,67 +425,69 @@
     kx1, kx2, kx3 = x_shift(keys, 1), x_shift(keys, 2), x_shift(keys, -1)
     vy1, vy3 = y_shift(values, 1), y_shift(values, -1)
     att0 = attend(query, key_value_cache, current_key_value, cached_length, 0, 2)
-    keys, kx1, kx2, kx3, values, vy1, vy3, att0, cached_length = barrier(
-        (keys, kx1, kx2, kx3, values, vy1, vy3, att0, cached_length)
+    keys, kx1, kx2, kx3, values, vy1, vy3, att0 = barrier(
+        (keys, kx1, kx2, kx3, values, vy1, vy3, att0)
     )
     vy2 = y_shift(values, 2)
     key0 = jnp.concatenate([keys, kx1, kx2, kx3], 0)
     key1, key3 = y_shift(key0, 1), y_shift(key0, -1)
-    att1 = attend(query, key_value_cache, current_key_value, cached_length, 1, 2)
-    vy2, att1 = barrier((vy2, att1))
+    vy2, cached_length = barrier((vy2, cached_length))
     both = [values, vy1, vy2, vy3]
     value0 = jnp.concatenate([v[:256] for v in both], 0)
     value1, value3 = x_shift(value0, 1), x_shift(value0, -1)
     down0 = jnp.concatenate([v[256:] for v in both], 0)
     down_own = jnp.concatenate([down0, xh_swap(down0)], 0)
-    sums = main_product(info, tokens, ((0, 0, 0), (1, 0, 0)), (key0, value0))
+    att1 = attend(query, key_value_cache, current_key_value, cached_length, 1, 2)
     attended = jnp.concatenate([att0, att1], 0).reshape(rows, heads * HEAD_DIM)
-    key0, value0, key1, key3, value1, value3, down_own, sums, attended = barrier(
-        (key0, value0, key1, key3, value1, value3, down_own, sums, attended)
+    low = low_rank(info, tokens, down_own, core_swap(down_own))
+    key0, value0, key1, key3, value1, value3, low, attended = barrier(
+        (key0, value0, key1, key3, value1, value3, low, attended)
     )
+    first = [key0, value0, key1, key3, value1, value3]
     key2, value2 = y_shift(key0, 2), x_shift(value0, 2)
-    low = low_rank(info, tokens, down_own, core_swap(down_own))
-    kinds = ((0, 1, 0), (0, 3, 0), (1, 1, 0), (1, 3, 0))
-    sums = main_product(info, tokens, kinds, (key1, key3, value1, value3), tuple(sums))
-    ready = [core_swap(b) for b in (key0, value0, key1, key3, value1, value3)]
+    theirs = core_swap(jnp.concatenate(first, 0))
     across = xh_swap(attended)
-    lows = ring(low, z_shift)
-    key2, value2, ready, sums, across, lows, attended = barrier(
-        (key2, value2, ready, sums, across, lows, attended)
+    pair = jnp.concatenate([low, z_flip(low, 1)], 0)
+    lows = jnp.concatenate([pair, z_flip(pair, 2)], 0)
+    key2, value2, theirs, across, lows, attended = barrier(
+        (key2, value2, theirs, across, lows, attended)
     )
     mine = ring(jnp.concatenate([attended, across], 0), y_shift)
-    last = [key2, value2, core_swap(key2), core_swap(value2)]
-    kinds = ((0, 0, 1), (1, 0, 1), (0, 1, 1), (0, 3, 1), (1, 1, 1), (1, 3, 1))
-    sums = main_product(info, tokens, kinds, ready, tuple(sums))
-    kinds = ((0, 2, 0), (1, 2, 0), (0, 2, 1), (1, 2, 1))
-    sums = main_product(info, tokens, kinds, last, tuple(sums))
+    last = [core_swap(key2), core_swap(value2)]
+    order = ((0, 0), (1, 0), (0, 1), (0, 3), (1, 1), (1, 3))
+    kinds = tuple((kv, j, 0, n, 0) for n, (kv, j) in enumerate(order))
+    kinds += ((0, 2, 0, 6, 0), (1, 2, 0, 7, 0))
+    kinds += tuple((kv, j, 1, 8, n) for n, (kv, j) in enumerate(order))
+    sums = main_product(info, tokens, kinds, first + [key2, value2, theirs])
+    sums = main_product(info, tokens, ((0, 2, 1, 0, 0), (1, 2, 1, 1, 0)), last, tuple(sums))
     same, other = finish(info, lows, sums, adapter_up_weight)
 
     b0 = lax.ppermute(same, "pool", [(0, 1), (1, 0)])
     a0 = lax.ppermute(other, ("pool", "xh"), [(i, 3 - i) for i in range(4)])
-    b0, a0, mine = barrier((b0, a0, mine))
-    b1, b3 = y_shift(b0, 1), y_shift(b0, -1)
-    a1, a3 = y_shift(a0, 1), y_shift(a0, -1)
-    parts = mine + [core_swap(b) for b in mine]
+    mine = jnp.concatenate(mine, 0)
+    partner = core_swap(mine)
+    b0, a0, mine, partner = barrier((b0, a0, mine, partner))
+    both0 = jnp.stack([b0, a0])
+    both1, both3 = y_shift(both0, 1), y_shift(both0, -1)
     ranks = ADAPTERS * RANK
     down = jnp.transpose(output_down_weight, (1, 2, 0)).reshape(ranks, -1)
     up = output_up_weight.reshape(ranks, -1)
-    shares = project(info, row_adapter_index[:, None], down, up, output_weight, parts)
-    theirs0 = core_swap(choose(info, [b0, a0]))
-    b0, a0, b1, b3, a1, a3, shares, theirs0 = barrier((b0, a0, b1, b3, a1, a3, shares, theirs0))
-    b2, a2 = y_shift(b1, 1), y_shift(a3, -1)
+    keep = row_adapter_index[:, None]
+    shares = project(info, keep, down, up, output_weight, [mine, partner])
     decoded = shares[0].astype(jnp.float32)
     for k, share in ((1, shares[1]), (2, shares[2]), (-1, shares[3])):
         decoded = decoded + z_shift(share, k).astype(jnp.float32)
     decoded = decoded.astype(jnp.bfloat16)
-    theirs1 = core_swap(choose(info, [b1, b3, a1, a3]))
-    theirs = jnp.concatenate([theirs0, theirs1], 1)
-    kinds = ((0, 0), (1, 0), (0, 1), (0, 3), (1, 1), (1, 3))
+    both0, both1, both3, decoded = barrier((both0, both1, both3, decoded))
+    b2, a2 = y_shift(both1[0], 1), y_shift(both3[1], -1)
+    middle = [both0, both1, both3]
+    theirs = [core_swap(v) for v in middle]
+    b2, a2, theirs = barrier((b2, a2, theirs))
+    theirs2 = [core_swap(b2), core_swap(a2)]
+    kinds = ((0, 0), (1, 0), (0, 1), (1, 1), (0, 3), (1, 3))
     rest = ((0, 2), (1, 2))
-    handed = place(info, kinds, rest, [b0, a0, b1, b3, a1, a3], theirs)
-    b2, a2, decoded, handed = barrier((b2, a2, decoded, handed))
-    theirs2 = core_swap(choose(info, [b2, a2]))
-    handed = place(info, rest, (), [b2, a2], theirs2, handed)
+    handed = place(info, kinds, rest, middle, theirs)
+    handed = place(info, rest, (), [b2[None], a2[None]], [v[None] for v in theirs2], handed)
     return handed, decoded
 
 

time: 165 us -> 162 us (0.982); the launches traced: 162 us -> 162 us
  Pallas kernels: 52.4 us -> 28.7 us
  waiting for transfers between devices: 45.1 us -> 67.6 us
  local copies, waits for them, and re-layouts: 5.53 us -> 9.2 us
  starting transfers between devices: 54.6 us -> 52.8 us
    pallas_call x4 -> x2, Pallas kernels: 18.6 us -> 5.79 us  [main_product(): pl.pallas_call(functools.partial(main_kernel, kinds, not sums), in_specs=...]
    ppermute x15 -> x13, waiting for transfers between devices: 17 us -> 27.2 us  [y_shift(): return lax.ppermute(value, 'y', [(i, (i + k) % 4) for i in range(4)])]
    ppermute x2, waiting for transfers between devices: 7.47 us -> 16.6 us  [xh_swap(): return lax.ppermute(value, 'xh', [(0, 1), (1, 0)])]
    ppermute x16 -> x10, starting transfers between devices: 17.5 us -> 10.6 us  [core_swap(): return lax.ppermute(value, 'core', [(0, 1), (1, 0)])]
    ppermute x1, waiting for transfers between devices: 2.02 us -> 8.25 us  [body(): b0 = lax.ppermute(same, 'pool', [(0, 1), (1, 0)])]
    pallas_call x7 -> x4, Pallas kernels: 17.1 us -> 11.5 us  [the longest x1 5.15 us: project(): pl.pallas_call(project_kernel, in_specs=[SMEM] + [VMEM] * 6, out_specs=[V...]
    ppermute x6 -> x3, starting transfers between devices: 9.99 us -> 4.53 us  [z_shift(): return lax.ppermute(value, 'head', [(i, (i + k) % 4) for i in range(4)])]
    ppermute x0 -> x2, starting transfers between devices: none -> 5.06 us  [z_flip(): return lax.ppermute(value, 'head', [(i, i ^ mask) for i in range(4)])]
  transfers between devices with their start and end apart: 47 -> 38, of which waited for: 16 -> 13; matrix products, arithmetic and copies ran while one was open for 3% -> 2% of each run, Pallas kernels for 29% -> 16%
where the time goes in v4:
time: 162 us
  waiting for transfers between devices  67.6 us (42%)
  starting transfers between devices  52.8 us (33%)
  Pallas kernels  28.7 us (18%)
  local copies, waits for them, and re-layouts  9.2 us (6%)
  other arithmetic  1.97 us (1%)
    ppermute x13, waiting for transfers between devices, y_shift(): return lax.ppermute(value, 'y', [(i, (i + k) % 4) for i in range(4)])  27.2 us
    ppermute x13, starting transfers between devices, y_shift(): return lax.ppermute(value, 'y', [(i, (i + k) % 4) for i in range(4)])  18.8 us
    ppermute x2, waiting for transfers between devices, xh_swap(): return lax.ppermute(value, 'xh', [(0, 1), (1, 0)])  16.6 us
    ppermute x3, waiting for transfers between devices, z_shift(): return lax.ppermute(value, 'head', [(i, (i + k) % 4) for i in range(4)])  11.2 us
    ppermute x10, starting transfers between devices, core_swap(): return lax.ppermute(value, 'core', [(0, 1), (1, 0)])  10.6 us
    ppermute x6, starting transfers between devices, x_shift(): return lax.ppermute(value, ('pool', 'xh'), pairs)  9.55 us
    pallas_call x2, Pallas kernels, attend(): pl.pallas_call(functools.partial(attend_kernel, first * ROWS_STEP), grid_...  8.54 us
    ppermute x1, waiting for transfers between devices, body(): b0 = lax.ppermute(same, 'pool', [(0, 1), (1, 0)])  8.25 us
  transfers between devices with their start and end apart: 38, of which 13 were waited for; matrix products, arithmetic and copies ran while one was open for 2% of the time, Pallas kernels for 16%

profile of v4, /device:TPU:1, one launch (start us, length us, event | category | flops | bytes accessed | tf_op | source)
XLA Modules:
  0.0 161.6 jit_solution(1010490922689440794)
XLA Ops:
  1.4 1.0 copy-done.4
  2.4 0.9 copy-done.5
  3.4 1.5 pack.1
  4.9 2.2 %collective-permute-start.3 = (bf16[320,256]{1,0:T(8,128)(2,1)S(1)}, bf16[320,256]{1,0:T(8,128)(2,1)S(1)}, u32[]{:S(2)}, u32[]{:S(2)}) collective-permute-start(bf16[320,256]{1,0:T(8,128)(2,1)S(1)} %get-tuple-element.57), channel_id=1, source_target_pairs={{0,8},{8,16},{16,24},{24,0},{1,9},{9,17},{17,25},{25,1},{2,10},{10... | collective-permute-start | bytes 491528 | tf_op jit(solution)/shard_map/ppermute | solution.py:39
  7.1 1.5 collective-permute-start.4
  8.6 1.2 collective-permute-start
  9.8 2.5 %collective-permute-start.1 = (bf16[256,256]{1,0:T(8,128)(2,1)S(1)}, bf16[256,256]{1,0:T(8,128)(2,1)S(1)}, u32[]{:S(2)}, u32[]{:S(2)}) collective-permute-start(bf16[256,256]{1,0:T(8,128)(2,1)S(1)} %get-tuple-element.53), channel_id=1, source_target_pairs={{0,32},{64,96},{32,0},{96,64},{1,33},{65,97},{33,1},{97,65},{2,34}... | collective-permute-start | bytes 393224 | tf_op jit(solution)/shard_map/ppermute | solution.py:35
  12.3 1.2 collective-permute-start.2
  13.4 1.0 copy.18
  14.4 2.8 %copy-done = bf16[48,128,2,256]{3,2,1,0:T(2,128)(2,1)S(1)} copy-done((bf16[48,128,2,256]{3,2,1,0:T(2,128)(2,1)S(1)}, bf16[48,128,2,256]{3,2,1,0:T(2,128)(2,1)}, u32[]{:S(2)}) %copy-start) | copy-done | bytes 6291480
  18.6 4.3 %attend.2 = bf16[24,16,128]{2,1,0:T(8,128)(2,1)S(1)} custom-call(s32[48]{0:T(128)S(1)} %copy-done.9, bf16[48,16,128]{2,1,0:T(8,128)(2,1)S(1)} %bitcast.31, bf16[48,128,2,256]{3,2,1,0:T(2,128)(2,1)S(1)} %copy-done, bf16[48,2,256]{2,1,0:T(2,128)(2,1)S(1)} %copy-done.6), custom_call_target="tpu_custom_call" | custom-call | tf_op jit(solution)/shard_map/attend/pallas_call | solution.py:131
  23.0 1.6 %collective-permute-start.5 = (bf16[320,256]{1,0:T(8,128)(2,1)S(1)}, bf16[320,256]{1,0:T(8,128)(2,1)S(1)}, u32[]{:S(2)}, u32[]{:S(2)}) collective-permute-start(bf16[320,256]{1,0:T(8,128)(2,1)S(1)} %get-tuple-element.57), channel_id=1, source_target_pairs={{0,16},{8,24},{16,0},{24,8},{1,17},{9,25},{17,1},{25,9},{2,18},{10... | collective-permute-start | bytes 491528 | tf_op jit(solution)/shard_map/ppermute | solution.py:39
  25.2 2.3 %collective-permute-start.7 = (bf16[1024,256]{1,0:T(8,128)(2,1)S(1)}, bf16[1024,256]{1,0:T(8,128)(2,1)S(1)}, u32[]{:S(2)}, u32[]{:S(2)}) collective-permute-start(bf16[1024,256]{1,0:T(8,128)(2,1)S(1)} %constant_dynamic-update-slice_fusion.refs_0_), channel_id=1, source_target_pairs={{0,24},{8,0},{16,8},{24,16},{1,25},{9,1},{17,9},{25,17},{2,26},{10... | collective-permute-start | bytes 1572872 | tf_op jit(solution)/shard_map/ppermute | solution.py:39
  27.5 1.3 collective-permute-done.5
  29.2 2.4 %collective-permute-start.9 = (bf16[1024,256]{1,0:T(8,128)(2,1)S(1)}, bf16[1024,256]{1,0:T(8,128)(2,1)S(1)}, u32[]{:S(2)}, u32[]{:S(2)}) collective-permute-start(bf16[1024,256]{1,0:T(8,128)(2,1)S(1)} %pad_maximum_fusion.1.refs_1_), channel_id=1, source_target_pairs={{0,96},{64,0},{32,64},{96,32},{1,97},{65,1},{33,65},{97,33},{2,98}... | collective-permute-start | bytes 1572872 | tf_op jit(solution)/shard_map/ppermute | solution.py:35
  31.7 8.3 %collective-permute-done.10 = bf16[256,256]{1,0:T(8,128)(2,1)S(1)} collective-permute-done((bf16[256,256]{1,0:T(8,128)(2,1)S(1)}, bf16[256,256]{1,0:T(8,128)(2,1)S(1)}, u32[]{:S(2)}, u32[]{:S(2)}) %collective-permute-start.10) | collective-permute-done | bytes 131104 | tf_op jit(solution)/shard_map/ppermute | solution.py:43
  40.0 6.0 %collective-permute-start.11 = (bf16[512,256]{1,0:T(8,128)(2,1)S(1)}, bf16[512,256]{1,0:T(8,128)(2,1)S(1)}, u32[]{:S(2)}, u32[]{:S(2)}) collective-permute-start(bf16[512,256]{1,0:T(8,128)(2,1)S(1)} %constant_dynamic-update-slice_fusion.4.own_ref), channel_id=1, source_target_pairs={{0,4},{4,0},{1,5},{5,1},{2,6},{6,2},{3,7},{7,3},{8,12},{12,8},{9,1... | collective-permute-start | bytes 786440 | tf_op jit(solution)/shard_map/ppermute | solution.py:55
  46.0 4.3 %attend.3 = bf16[24,16,128]{2,1,0:T(8,128)(2,1)S(1)} custom-call(s32[48]{0:T(128)S(1)} %copy-done.10, bf16[48,16,128]{2,1,0:T(8,128)(2,1)S(1)} %bitcast.32, bf16[48,128,2,256]{3,2,1,0:T(2,128)(2,1)S(1)} %copy-done.1, bf16[48,2,256]{2,1,0:T(2,128)(2,1)S(1)} %copy-done.6), custom_call_target="tpu_custom_call" | custom-call | tf_op jit(solution)/shard_map/attend/pallas_call | solution.py:131
  50.4 1.3 low_rank.1
  52.1 1.7 %collective-permute-start.12 = (bf16[1024,256]{1,0:T(8,128)(2,1)S(1)}, bf16[1024,256]{1,0:T(8,128)(2,1)S(1)}, u32[]{:S(2)}, u32[]{:S(2)}) collective-permute-start(bf16[1024,256]{1,0:T(8,128)(2,1)S(1)} %constant_dynamic-update-slice_fusion.refs_0_), channel_id=1, source_target_pairs={{0,16},{8,24},{16,0},{24,8},{1,17},{9,25},{17,1},{25,9},{2,18},{10... | collective-permute-start | bytes 1572872 | tf_op jit(solution)/shard_map/ppermute | solution.py:39
  53.8 2.0 %collective-permute-start.13 = (bf16[1024,256]{1,0:T(8,128)(2,1)S(1)}, bf16[1024,256]{1,0:T(8,128)(2,1)S(1)}, u32[]{:S(2)}, u32[]{:S(2)}) collective-permute-start(bf16[1024,256]{1,0:T(8,128)(2,1)S(1)} %pad_maximum_fusion.1.refs_1_), channel_id=1, source_target_pairs={{0,32},{64,96},{32,0},{96,64},{1,33},{65,97},{33,1},{97,65},{2,34}... | collective-permute-start | bytes 1572872 | tf_op jit(solution)/shard_map/ppermute | solution.py:35
  55.8 1.6 %collective-permute-start.16 = (f32[32,128]{1,0:T(8,128)S(1)}, f32[32,128]{1,0:T(8,128)S(1)}, u32[]{:S(2)}, u32[]{:S(2)}) collective-permute-start(f32[32,128]{1,0:T(8,128)S(1)} %low_rank.1), channel_id=1, source_target_pairs={{0,1},{1,0},{2,3},{3,2},{4,5},{5,4},{6,7},{7,6},{8,9},{9,8},{10,11... | collective-permute-start | bytes 49160 | tf_op jit(solution)/shard_map/ppermute | solution.py:51
  57.4 1.0 collective-permute-start.15
  58.9 3.4 %collective-permute-start.17 = (f32[64,128]{1,0:T(8,128)S(1)}, f32[64,128]{1,0:T(8,128)S(1)}, u32[]{:S(2)}, u32[]{:S(2)}) collective-permute-start(f32[64,128]{1,0:T(8,128)S(1)} %pad_maximum_fusion.5), channel_id=1, source_target_pairs={{0,2},{1,3},{2,0},{3,1},{4,6},{5,7},{6,4},{7,5},{8,10},{9,11},{10,... | collective-permute-start | bytes 98312 | tf_op jit(solution)/shard_map/ppermute | solution.py:51
  62.3 1.7 %collective-permute-done.17 = f32[64,128]{1,0:T(8,128)S(1)} collective-permute-done((f32[64,128]{1,0:T(8,128)S(1)}, f32[64,128]{1,0:T(8,128)S(1)}, u32[]{:S(2)}, u32[]{:S(2)}) %collective-permute-start.17) | collective-permute-done | bytes 32800 | tf_op jit(solution)/shard_map/ppermute | solution.py:51
  64.0 8.3 %collective-permute-done.15 = bf16[48,2048]{1,0:T(8,128)(2,1)S(1)} collective-permute-done((bf16[48,2048]{1,0:T(8,128)(2,1)S(1)}, bf16[48,2048]{1,0:T(8,128)(2,1)S(1)}, u32[]{:S(2)}, u32[]{:S(2)}) %collective-permute-start.15) | collective-permute-done | bytes 196640 | tf_op jit(solution)/shard_map/ppermute | solution.py:43
  72.7 1.6 collective-permute-start.23
  74.3 1.5 collective-permute-start.24
  75.9 7.6 %collective-permute-done.22 = bf16[96,2048]{1,0:T(8,128)(2,1)S(1)} collective-permute-done((bf16[96,2048]{1,0:T(8,128)(2,1)S(1)}, bf16[96,2048]{1,0:T(8,128)(2,1)S(1)}, u32[]{:S(2)}, u32[]{:S(2)}) %collective-permute-start.22) | collective-permute-done | bytes 393248 | tf_op jit(solution)/shard_map/ppermute | solution.py:39
  83.5 6.9 %collective-permute-done.23 = bf16[96,2048]{1,0:T(8,128)(2,1)S(1)} collective-permute-done((bf16[96,2048]{1,0:T(8,128)(2,1)S(1)}, bf16[96,2048]{1,0:T(8,128)(2,1)S(1)}, u32[]{:S(2)}, u32[]{:S(2)}) %collective-permute-start.23) | collective-permute-done | bytes 393248 | tf_op jit(solution)/shard_map/ppermute | solution.py:39
  90.4 2.3 %collective-permute-done.24 = bf16[96,2048]{1,0:T(8,128)(2,1)S(1)} collective-permute-done((bf16[96,2048]{1,0:T(8,128)(2,1)S(1)}, bf16[96,2048]{1,0:T(8,128)(2,1)S(1)}, u32[]{:S(2)}, u32[]{:S(2)}) %collective-permute-start.24) | collective-permute-done | bytes 393248 | tf_op jit(solution)/shard_map/ppermute | solution.py:39
  92.7 1.6 %collective-permute-start.25 = (bf16[384,2048]{1,0:T(8,128)(2,1)S(1)}, bf16[384,2048]{1,0:T(8,128)(2,1)S(1)}, u32[]{:S(2)}, u32[]{:S(2)}) collective-permute-start(bf16[384,2048]{1,0:T(8,128)(2,1)S(1)} %constant_dynamic-update-slice_fusion.17.refs_0_), channel_id=1, source_target_pairs={{0,4},{4,0},{1,5},{5,1},{2,6},{6,2},{3,7},{7,3},{8,12},{12,8},{9,1... | collective-permute-start | bytes 4718600 | tf_op jit(solution)/shard_map/ppermute | solution.py:55
  94.9 4.5 %main_product.2 = (f32[512,256]{1,0:T(8,128)S(1)}, f32[512,256]{1,0:T(8,128)S(1)}) custom-call(s32[17]{0:T(128)S(1)} %concatenate.36.info, bf16[512,8192]{1,0:T(8,128)(2,1)S(1)} %bitcast.29, bf16[1024,256]{1,0:T(8,128)(2,1)S(1)} %constant_dynamic-update-slice_fusion.refs_0_, bf16[1024,256]{1,0:T(8,128)(2,1)S(1)} %pad_maximum_fusion.1.refs_1_, ...), custom_call_target="tpu_custom_call" | custom-call | tf_op jit(solution)/shard_map/main_product/pallas_call | solution.py:227
  99.5 1.3 main_product.3
  100.8 2.6 %finish.1 = (bf16[3,128,2,256]{3,2,1,0:T(2,128)(2,1)S(1)}, bf16[3,128,2,256]{3,2,1,0:T(2,128)(2,1)S(1)}) custom-call(s32[17]{0:T(128)S(1)} %concatenate.36.info, f32[128,128]{1,0:T(8,128)S(1)} %pad_maximum_fusion.4.refs_0_, f32[512,256]{1,0:T(8,128)S(1)} %get-tuple-element.77.refs_1_, f32[512,256]{1,0:T(8,128)S(1)} %get-tuple-element.78.refs_2_, ...), custom_call_target="tpu_custom_call" | custom-call | tf_op jit(solution)/shard_map/finish/pallas_call | solution.py:268
  103.4 2.1 %collective-permute-start.20 = (bf16[3,128,2,256]{3,2,1,0:T(2,128)(2,1)S(1)}, bf16[3,128,2,256]{3,2,1,0:T(2,128)(2,1)S(1)}, u32[]{:S(2)}, u32[]{:S(2)}) collective-permute-start(bf16[3,128,2,256]{3,2,1,0:T(2,128)(2,1)S(1)} %get-tuple-element.79), channel_id=1, source_target_pairs={{0,64},{64,0},{1,65},{65,1},{2,66},{66,2},{3,67},{67,3},{4,68},{68... | collective-permute-start | bytes 1179656 | tf_op jit(solution)/shard_map/ppermute | solution.py:465
  105.5 1.1 collective-permute-start.21
  106.6 8.3 %collective-permute-done.20 = bf16[3,128,2,256]{3,2,1,0:T(2,128)(2,1)S(1)} collective-permute-done((bf16[3,128,2,256]{3,2,1,0:T(2,128)(2,1)S(1)}, bf16[3,128,2,256]{3,2,1,0:T(2,128)(2,1)S(1)}, u32[]{:S(2)}, u32[]{:S(2)}) %collective-permute-start.20) | collective-permute-done | bytes 393248 | tf_op jit(solution)/shard_map/ppermute | solution.py:465
  114.8 2.2 %collective-permute-done.21 = bf16[3,128,2,256]{3,2,1,0:T(2,128)(2,1)S(1)} collective-permute-done((bf16[3,128,2,256]{3,2,1,0:T(2,128)(2,1)S(1)}, bf16[3,128,2,256]{3,2,1,0:T(2,128)(2,1)S(1)}, u32[]{:S(2)}, u32[]{:S(2)}) %collective-permute-start.21) | collective-permute-done | bytes 393248 | tf_op jit(solution)/shard_map/ppermute | solution.py:466
  117.0 1.1 pad_maximum_fusion.refs_0_
  118.9 2.0 %collective-permute-start.27 = (bf16[2,3,128,2,256]{4,3,2,1,0:T(2,128)(2,1)S(1)}, bf16[2,3,128,2,256]{4,3,2,1,0:T(2,128)(2,1)S(1)}, u32[]{:S(2)}, u32[]{:S(2)}) collective-permute-start(bf16[2,3,128,2,256]{4,3,2,1,0:T(2,128)(2,1)S(1)} %pad_maximum_fusion.refs_0_), channel_id=1, source_target_pairs={{0,24},{8,0},{16,8},{24,16},{1,25},{9,1},{17,9},{25,17},{2,26},{10... | collective-permute-start | bytes 2359304 | tf_op jit(solution)/shard_map/ppermute | solution.py:39
  121.1 5.2 %project.1 = (bf16[192,512]{1,0:T(8,128)(2,1)S(1)}, bf16[192,512]{1,0:T(8,128)(2,1)S(1)}, bf16[192,512]{1,0:T(8,128)(2,1)S(1)}, bf16[192,512]{1,0:T(8,128)(2,1)S(1)}) custom-call(s32[17]{0:T(128)S(1)} %concatenate.36.info, s32[768,1]{1,0:T(8,128)S(1)} %broadcast_in_dim.20.keep, bf16[128,2048]{1,0:T(8,128)(2,1)S(1)} %bitcast.33, ...), custom_call_target="tpu_custom_call" | custom-call | tf_op jit(solution)/shard_map/project/pallas_call | solution.py:384
  126.2 3.8 %collective-permute-start.30 = (bf16[192,512]{1,0:T(8,128)(2,1)S(1)}, bf16[192,512]{1,0:T(8,128)(2,1)S(1)}, u32[]{:S(2)}, u32[]{:S(2)}) collective-permute-start(bf16[192,512]{1,0:T(8,128)(2,1)S(1)} %get-tuple-element.90), channel_id=1, source_target_pairs={{0,3},{1,0},{2,1},{3,2},{4,7},{5,4},{6,5},{7,6},{8,11},{9,8},{10,9... | collective-permute-start | bytes 589832 | tf_op jit(solution)/shard_map/ppermute | solution.py:47
  130.8 6.7 %collective-permute-done.30 = bf16[192,512]{1,0:T(8,128)(2,1)S(1)} collective-permute-done((bf16[192,512]{1,0:T(8,128)(2,1)S(1)}, bf16[192,512]{1,0:T(8,128)(2,1)S(1)}, u32[]{:S(2)}, u32[]{:S(2)}) %collective-permute-start.30) | collective-permute-done | bytes 196640 | tf_op jit(solution)/shard_map/ppermute | solution.py:47
  137.5 4.5 %collective-permute-done.28 = bf16[192,512]{1,0:T(8,128)(2,1)S(1)} collective-permute-done((bf16[192,512]{1,0:T(8,128)(2,1)S(1)}, bf16[192,512]{1,0:T(8,128)(2,1)S(1)}, u32[]{:S(2)}, u32[]{:S(2)}) %collective-permute-start.28) | collective-permute-done | bytes 196640 | tf_op jit(solution)/shard_map/ppermute | solution.py:47
  144.7 2.7 %collective-permute-start.32 = (bf16[3,128,2,256]{3,2,1,0:T(2,128)(2,1)S(1)}, bf16[3,128,2,256]{3,2,1,0:T(2,128)(2,1)S(1)}, u32[]{:S(2)}, u32[]{:S(2)}) collective-permute-start(bf16[3,128,2,256]{3,2,1,0:T(2,128)(2,1)S(1)} %slice_bitcast_fusion), channel_id=1, source_target_pairs={{0,24},{8,0},{16,8},{24,16},{1,25},{9,1},{17,9},{25,17},{2,26},{10... | collective-permute-start | bytes 1179656 | tf_op jit(solution)/shard_map/ppermute | solution.py:39
  147.4 9.2 %collective-permute-done.31 = bf16[3,128,2,256]{3,2,1,0:T(2,128)(2,1)S(1)} collective-permute-done((bf16[3,128,2,256]{3,2,1,0:T(2,128)(2,1)S(1)}, bf16[3,128,2,256]{3,2,1,0:T(2,128)(2,1)S(1)}, u32[]{:S(2)}, u32[]{:S(2)}) %collective-permute-start.31) | collective-permute-done | bytes 393248 | tf_op jit(solution)/shard_map/ppermute | solution.py:39
  157.7 2.9 %place.2.refs_4_ = bf16[1,2,2048,2,256]{4,3,2,1,0:T(2,128)(2,1)} custom-call(s32[17]{0:T(128)S(1)} %concatenate.36.info, bf16[2,3,128,2,256]{4,3,2,1,0:T(2,128)(2,1)S(1)} %pad_maximum_fusion.refs_0_, bf16[2,3,128,2,256]{4,3,2,1,0:T(2,128)(2,1)S(1)} %collective-permute-done.26.refs_1_, bf16[2,3,128,2,256]{4,3,2,1,0:T(2,128)(2,1)S(1)} %collective-permute-done.27.refs_2_, ...), custom_call_target="tpu_custom_call" | custom-call | tf_op jit(solution)/shard_map/place/pallas_call | solution.py:342
  (104 shorter events, 11.6 us)
Async XLA Ops:
  4.9 18.0 %collective-permute-start.3 = (bf16[320,256]{1,0:T(8,128)(2,1)S(1)}, bf16[320,256]{1,0:T(8,128)(2,1)S(1)}, u32[]{:S(2)}, u32[]{:S(2)}) collective-permute-start(bf16[320,256]{1,0:T(8,128)(2,1)S(1)} %get-tuple-element.57), channel_id=1, source_target_pairs={{0,8},{8,16},{16,24},{24,0},{1,9},{9,17},{17,25},{25,1},{2,10},{10... | collective-permute-start | bytes 491528 | tf_op jit(solution)/shard_map/ppermute | solution.py:39
  7.1 15.9 %collective-permute-start.4 = (bf16[320,256]{1,0:T(8,128)(2,1)S(1)}, bf16[320,256]{1,0:T(8,128)(2,1)S(1)}, u32[]{:S(2)}, u32[]{:S(2)}) collective-permute-start(bf16[320,256]{1,0:T(8,128)(2,1)S(1)} %get-tuple-element.57), channel_id=1, source_target_pairs={{0,24},{8,0},{16,8},{24,16},{1,25},{9,1},{17,9},{25,17},{2,26},{10... | collective-permute-start | bytes 491528 | tf_op jit(solution)/shard_map/ppermute | solution.py:39
  8.6 14.3 %collective-permute-start = (bf16[256,256]{1,0:T(8,128)(2,1)S(1)}, bf16[256,256]{1,0:T(8,128)(2,1)S(1)}, u32[]{:S(2)}, u32[]{:S(2)}) collective-permute-start(bf16[256,256]{1,0:T(8,128)(2,1)S(1)} %get-tuple-element.53), channel_id=1, source_target_pairs={{0,64},{64,32},{32,96},{96,0},{1,65},{65,33},{33,97},{97,1},{2,66}... | collective-permute-start | bytes 393224 | tf_op jit(solution)/shard_map/ppermute | solution.py:35
  9.8 13.1 %collective-permute-start.1 = (bf16[256,256]{1,0:T(8,128)(2,1)S(1)}, bf16[256,256]{1,0:T(8,128)(2,1)S(1)}, u32[]{:S(2)}, u32[]{:S(2)}) collective-permute-start(bf16[256,256]{1,0:T(8,128)(2,1)S(1)} %get-tuple-element.53), channel_id=1, source_target_pairs={{0,32},{64,96},{32,0},{96,64},{1,33},{65,97},{33,1},{97,65},{2,34}... | collective-permute-start | bytes 393224 | tf_op jit(solution)/shard_map/ppermute | solution.py:35
  12.3 10.7 %collective-permute-start.2 = (bf16[256,256]{1,0:T(8,128)(2,1)S(1)}, bf16[256,256]{1,0:T(8,128)(2,1)S(1)}, u32[]{:S(2)}, u32[]{:S(2)}) collective-permute-start(bf16[256,256]{1,0:T(8,128)(2,1)S(1)} %get-tuple-element.53), channel_id=1, source_target_pairs={{0,96},{64,0},{32,64},{96,32},{1,97},{65,1},{33,65},{97,33},{2,98}... | collective-permute-start | bytes 393224 | tf_op jit(solution)/shard_map/ppermute | solution.py:35
  14.4 2.8 %copy-start = (bf16[48,128,2,256]{3,2,1,0:T(2,128)(2,1)S(1)}, bf16[48,128,2,256]{3,2,1,0:T(2,128)(2,1)}, u32[]{:S(2)}) copy-start(bf16[48,128,2,256]{3,2,1,0:T(2,128)(2,1)} %kv_ref.3) | copy-start | bytes 18874372
  18.6 27.3 %copy-start.1 = (bf16[48,128,2,256]{3,2,1,0:T(2,128)(2,1)S(1)}, bf16[48,128,2,256]{3,2,1,0:T(2,128)(2,1)}, u32[]{:S(2)}) copy-start(bf16[48,128,2,256]{3,2,1,0:T(2,128)(2,1)} %kv_ref.3) | copy-start | bytes 18874372
  18.6 31.7 %slice-start = ((s8[8388608]{0:T(1024)(128)(4,1)}), s8[4194304]{0:T(1024)(128)(4,1)S(1)}, s32[]{:S(2)}) async-start(s8[8388608]{0:T(1024)(128)(4,1)} %bitcast.26), calls=%async_computation | async-start | bytes 8388608
  22.9 23.1 %copy-start.10 = (s32[48]{0:T(128)S(1)}, s32[48]{0:T(128)}, u32[]{:S(2)}) copy-start(s32[48]{0:T(128)} %len_ref.2) | copy-start | bytes 580
  23.0 5.8 %collective-permute-start.5 = (bf16[320,256]{1,0:T(8,128)(2,1)S(1)}, bf16[320,256]{1,0:T(8,128)(2,1)S(1)}, u32[]{:S(2)}, u32[]{:S(2)}) collective-permute-start(bf16[320,256]{1,0:T(8,128)(2,1)S(1)} %get-tuple-element.57), channel_id=1, source_target_pairs={{0,16},{8,24},{16,0},{24,8},{1,17},{9,25},{17,1},{25,9},{2,18},{10... | collective-permute-start | bytes 491528 | tf_op jit(solution)/shard_map/ppermute | solution.py:39
  24.7 27.0 %collective-permute-start.6 = (bf16[1024,256]{1,0:T(8,128)(2,1)S(1)}, bf16[1024,256]{1,0:T(8,128)(2,1)S(1)}, u32[]{:S(2)}, u32[]{:S(2)}) collective-permute-start(bf16[1024,256]{1,0:T(8,128)(2,1)S(1)} %constant_dynamic-update-slice_fusion.refs_0_), channel_id=1, source_target_pairs={{0,8},{8,16},{16,24},{24,0},{1,9},{9,17},{17,25},{25,1},{2,10},{10... | collective-permute-start | bytes 1572872 | tf_op jit(solution)/shard_map/ppermute | solution.py:39
  25.2 26.6 %collective-permute-start.7 = (bf16[1024,256]{1,0:T(8,128)(2,1)S(1)}, bf16[1024,256]{1,0:T(8,128)(2,1)S(1)}, u32[]{:S(2)}, u32[]{:S(2)}) collective-permute-start(bf16[1024,256]{1,0:T(8,128)(2,1)S(1)} %constant_dynamic-update-slice_fusion.refs_0_), channel_id=1, source_target_pairs={{0,24},{8,0},{16,8},{24,16},{1,25},{9,1},{17,9},{25,17},{2,26},{10... | collective-permute-start | bytes 1572872 | tf_op jit(solution)/shard_map/ppermute | solution.py:39
  28.8 21.6 %slice-start.1 = ((s8[8388608]{0:T(1024)(128)(4,1)}), s8[4194304]{0:T(1024)(128)(4,1)S(1)}, s32[]{:S(2)}) async-start(s8[8388608]{0:T(1024)(128)(4,1)} %bitcast.26), calls=%async_computation.1 | async-start | bytes 8388608
  28.8 22.9 %collective-permute-start.8 = (bf16[1024,256]{1,0:T(8,128)(2,1)S(1)}, bf16[1024,256]{1,0:T(8,128)(2,1)S(1)}, u32[]{:S(2)}, u32[]{:S(2)}) collective-permute-start(bf16[1024,256]{1,0:T(8,128)(2,1)S(1)} %pad_maximum_fusion.1.refs_1_), channel_id=1, source_target_pairs={{0,64},{64,32},{32,96},{96,0},{1,65},{65,33},{33,97},{97,1},{2,66}... | collective-permute-start | bytes 1572872 | tf_op jit(solution)/shard_map/ppermute | solution.py:35
  29.2 22.5 %collective-permute-start.9 = (bf16[1024,256]{1,0:T(8,128)(2,1)S(1)}, bf16[1024,256]{1,0:T(8,128)(2,1)S(1)}, u32[]{:S(2)}, u32[]{:S(2)}) collective-permute-start(bf16[1024,256]{1,0:T(8,128)(2,1)S(1)} %pad_maximum_fusion.1.refs_1_), channel_id=1, source_target_pairs={{0,96},{64,0},{32,64},{96,32},{1,97},{65,1},{33,65},{97,33},{2,98}... | collective-permute-start | bytes 1572872 | tf_op jit(solution)/shard_map/ppermute | solution.py:35
  31.6 8.4 %collective-permute-start.10 = (bf16[256,256]{1,0:T(8,128)(2,1)S(1)}, bf16[256,256]{1,0:T(8,128)(2,1)S(1)}, u32[]{:S(2)}, u32[]{:S(2)}) collective-permute-start(bf16[256,256]{1,0:T(8,128)(2,1)S(1)} %pad_maximum_fusion.3), channel_id=1, source_target_pairs={{0,32},{32,0},{1,33},{33,1},{2,34},{34,2},{3,35},{35,3},{4,36},{36... | collective-permute-start | bytes 393224 | tf_op jit(solution)/shard_map/ppermute | solution.py:43
  40.0 10.4 %collective-permute-start.11 = (bf16[512,256]{1,0:T(8,128)(2,1)S(1)}, bf16[512,256]{1,0:T(8,128)(2,1)S(1)}, u32[]{:S(2)}, u32[]{:S(2)}) collective-permute-start(bf16[512,256]{1,0:T(8,128)(2,1)S(1)} %constant_dynamic-update-slice_fusion.4.own_ref), channel_id=1, source_target_pairs={{0,4},{4,0},{1,5},{5,1},{2,6},{6,2},{3,7},{7,3},{8,12},{12,8},{9,1... | collective-permute-start | bytes 786440 | tf_op jit(solution)/shard_map/ppermute | solution.py:55
  52.0 20.3 %collective-permute-start.14 = (bf16[6144,256]{1,0:T(8,128)(2,1)S(1)}, bf16[6144,256]{1,0:T(8,128)(2,1)S(1)}, u32[]{:S(2)}, u32[]{:S(2)}) collective-permute-start(bf16[6144,256]{1,0:T(8,128)(2,1)S(1)} %constant_dynamic-update-slice_fusion.9), channel_id=1, source_target_pairs={{0,4},{4,0},{1,5},{5,1},{2,6},{6,2},{3,7},{7,3},{8,12},{12,8},{9,1... | collective-permute-start | bytes 9437192 | tf_op jit(solution)/shard_map/ppermute | solution.py:55
  52.1 20.2 %collective-permute-start.12 = (bf16[1024,256]{1,0:T(8,128)(2,1)S(1)}, bf16[1024,256]{1,0:T(8,128)(2,1)S(1)}, u32[]{:S(2)}, u32[]{:S(2)}) collective-permute-start(bf16[1024,256]{1,0:T(8,128)(2,1)S(1)} %constant_dynamic-update-slice_fusion.refs_0_), channel_id=1, source_target_pairs={{0,16},{8,24},{16,0},{24,8},{1,17},{9,25},{17,1},{25,9},{2,18},{10... | collective-permute-start | bytes 1572872 | tf_op jit(solution)/shard_map/ppermute | solution.py:39
  53.8 18.5 %collective-permute-start.13 = (bf16[1024,256]{1,0:T(8,128)(2,1)S(1)}, bf16[1024,256]{1,0:T(8,128)(2,1)S(1)}, u32[]{:S(2)}, u32[]{:S(2)}) collective-permute-start(bf16[1024,256]{1,0:T(8,128)(2,1)S(1)} %pad_maximum_fusion.1.refs_1_), channel_id=1, source_target_pairs={{0,32},{64,96},{32,0},{96,64},{1,33},{65,97},{33,1},{97,65},{2,34}... | collective-permute-start | bytes 1572872 | tf_op jit(solution)/shard_map/ppermute | solution.py:35
  55.8 3.1 %collective-permute-start.16 = (f32[32,128]{1,0:T(8,128)S(1)}, f32[32,128]{1,0:T(8,128)S(1)}, u32[]{:S(2)}, u32[]{:S(2)}) collective-permute-start(f32[32,128]{1,0:T(8,128)S(1)} %low_rank.1), channel_id=1, source_target_pairs={{0,1},{1,0},{2,3},{3,2},{4,5},{5,4},{6,7},{7,6},{8,9},{9,8},{10,11... | collective-permute-start | bytes 49160 | tf_op jit(solution)/shard_map/ppermute | solution.py:51
  57.4 14.9 %collective-permute-start.15 = (bf16[48,2048]{1,0:T(8,128)(2,1)S(1)}, bf16[48,2048]{1,0:T(8,128)(2,1)S(1)}, u32[]{:S(2)}, u32[]{:S(2)}) collective-permute-start(bf16[48,2048]{1,0:T(8,128)(2,1)S(1)} %bitcast.40), channel_id=1, source_target_pairs={{0,32},{32,0},{1,33},{33,1},{2,34},{34,2},{3,35},{35,3},{4,36},{36... | collective-permute-start | bytes 589832 | tf_op jit(solution)/shard_map/ppermute | solution.py:43
  58.9 5.1 %collective-permute-start.17 = (f32[64,128]{1,0:T(8,128)S(1)}, f32[64,128]{1,0:T(8,128)S(1)}, u32[]{:S(2)}, u32[]{:S(2)}) collective-permute-start(f32[64,128]{1,0:T(8,128)S(1)} %pad_maximum_fusion.5), channel_id=1, source_target_pairs={{0,2},{1,3},{2,0},{3,1},{4,6},{5,7},{6,4},{7,5},{8,10},{9,11},{10,... | collective-permute-start | bytes 98312 | tf_op jit(solution)/shard_map/ppermute | solution.py:51
  72.4 11.1 %collective-permute-start.22 = (bf16[96,2048]{1,0:T(8,128)(2,1)S(1)}, bf16[96,2048]{1,0:T(8,128)(2,1)S(1)}, u32[]{:S(2)}, u32[]{:S(2)}) collective-permute-start(bf16[96,2048]{1,0:T(8,128)(2,1)S(1)} %get-tuple-element.100), channel_id=1, source_target_pairs={{0,8},{8,16},{16,24},{24,0},{1,9},{9,17},{17,25},{25,1},{2,10},{10... | collective-permute-start | bytes 1179656 | tf_op jit(solution)/shard_map/ppermute | solution.py:39
  72.7 17.6 %collective-permute-start.23 = (bf16[96,2048]{1,0:T(8,128)(2,1)S(1)}, bf16[96,2048]{1,0:T(8,128)(2,1)S(1)}, u32[]{:S(2)}, u32[]{:S(2)}) collective-permute-start(bf16[96,2048]{1,0:T(8,128)(2,1)S(1)} %get-tuple-element.100), channel_id=1, source_target_pairs={{0,16},{8,24},{16,0},{24,8},{1,17},{9,25},{17,1},{25,9},{2,18},{10... | collective-permute-start | bytes 1179656 | tf_op jit(solution)/shard_map/ppermute | solution.py:39
  74.3 18.3 %collective-permute-start.24 = (bf16[96,2048]{1,0:T(8,128)(2,1)S(1)}, bf16[96,2048]{1,0:T(8,128)(2,1)S(1)}, u32[]{:S(2)}, u32[]{:S(2)}) collective-permute-start(bf16[96,2048]{1,0:T(8,128)(2,1)S(1)} %get-tuple-element.100), channel_id=1, source_target_pairs={{0,24},{8,0},{16,8},{24,16},{1,25},{9,1},{17,9},{25,17},{2,26},{10... | collective-permute-start | bytes 1179656 | tf_op jit(solution)/shard_map/ppermute | solution.py:39
  92.7 24.3 %collective-permute-start.25 = (bf16[384,2048]{1,0:T(8,128)(2,1)S(1)}, bf16[384,2048]{1,0:T(8,128)(2,1)S(1)}, u32[]{:S(2)}, u32[]{:S(2)}) collective-permute-start(bf16[384,2048]{1,0:T(8,128)(2,1)S(1)} %constant_dynamic-update-slice_fusion.17.refs_0_), channel_id=1, source_target_pairs={{0,4},{4,0},{1,5},{5,1},{2,6},{6,2},{3,7},{7,3},{8,12},{12,8},{9,1... | collective-permute-start | bytes 4718600 | tf_op jit(solution)/shard_map/ppermute | solution.py:55
  94.3 5.1 %collective-permute-start.18 = (bf16[1024,256]{1,0:T(8,128)(2,1)S(1)}, bf16[1024,256]{1,0:T(8,128)(2,1)S(1)}, u32[]{:S(2)}, u32[]{:S(2)}) collective-permute-start(bf16[1024,256]{1,0:T(8,128)(2,1)S(1)} %collective-permute-done.12.refs_6_), channel_id=1, source_target_pairs={{0,4},{4,0},{1,5},{5,1},{2,6},{6,2},{3,7},{7,3},{8,12},{12,8},{9,1... | collective-permute-start | bytes 1572872 | tf_op jit(solution)/shard_map/ppermute | solution.py:55
  94.4 5.0 %collective-permute-start.19 = (bf16[1024,256]{1,0:T(8,128)(2,1)S(1)}, bf16[1024,256]{1,0:T(8,128)(2,1)S(1)}, u32[]{:S(2)}, u32[]{:S(2)}) collective-permute-start(bf16[1024,256]{1,0:T(8,128)(2,1)S(1)} %collective-permute-done.13.refs_7_), channel_id=1, source_target_pairs={{0,4},{4,0},{1,5},{5,1},{2,6},{6,2},{3,7},{7,3},{8,12},{12,8},{9,1... | collective-permute-start | bytes 1572872 | tf_op jit(solution)/shard_map/ppermute | solution.py:55
  99.4 1.3 copy-start.7
  99.4 21.4 %copy-start.11 = (s32[768]{0:T(1024)S(1)}, s32[768]{0:T(1024)}, u32[]{:S(2)}) copy-start(s32[768]{0:T(1024)} %param.24) | copy-start | bytes 9220
  100.7 20.3 %copy-start.2 = (bf16[2048,512]{1,0:T(8,128)(2,1)S(1)}, bf16[2048,512]{1,0:T(8,128)(2,1)}, u32[]{:S(2)}) copy-start(bf16[2048,512]{1,0:T(8,128)(2,1)} %w_ref.3) | copy-start | bytes 6291460
  100.7 20.3 %copy-start.3 = (bf16[2048,8,16]{0,2,1:T(8,128)(2,1)S(1)}, bf16[2048,8,16]{0,2,1:T(8,128)(2,1)}, u32[]{:S(2)}) copy-start(bf16[2048,8,16]{0,2,1:T(8,128)(2,1)} %param.26) | copy-start | bytes 1572868
  100.7 20.3 %copy-start.8 = (bf16[8,16,512]{2,1,0:T(8,128)(2,1)S(1)}, bf16[8,16,512]{2,1,0:T(8,128)(2,1)}, u32[]{:S(2)}) copy-start(bf16[8,16,512]{2,1,0:T(8,128)(2,1)} %param.27) | copy-start | bytes 393220
  103.4 11.4 %collective-permute-start.20 = (bf16[3,128,2,256]{3,2,1,0:T(2,128)(2,1)S(1)}, bf16[3,128,2,256]{3,2,1,0:T(2,128)(2,1)S(1)}, u32[]{:S(2)}, u32[]{:S(2)}) collective-permute-start(bf16[3,128,2,256]{3,2,1,0:T(2,128)(2,1)S(1)} %get-tuple-element.79), channel_id=1, source_target_pairs={{0,64},{64,0},{1,65},{65,1},{2,66},{66,2},{3,67},{67,3},{4,68},{68... | collective-permute-start | bytes 1179656 | tf_op jit(solution)/shard_map/ppermute | solution.py:465
  105.5 11.6 %collective-permute-start.21 = (bf16[3,128,2,256]{3,2,1,0:T(2,128)(2,1)S(1)}, bf16[3,128,2,256]{3,2,1,0:T(2,128)(2,1)S(1)}, u32[]{:S(2)}, u32[]{:S(2)}) collective-permute-start(bf16[3,128,2,256]{3,2,1,0:T(2,128)(2,1)S(1)} %get-tuple-element.80), channel_id=1, source_target_pairs={{0,96},{32,64},{64,32},{96,0},{1,97},{33,65},{65,33},{97,1},{2,98}... | collective-permute-start | bytes 1179656 | tf_op jit(solution)/shard_map/ppermute | solution.py:466
  118.1 24.6 %collective-permute-start.26 = (bf16[2,3,128,2,256]{4,3,2,1,0:T(2,128)(2,1)S(1)}, bf16[2,3,128,2,256]{4,3,2,1,0:T(2,128)(2,1)S(1)}, u32[]{:S(2)}, u32[]{:S(2)}) collective-permute-start(bf16[2,3,128,2,256]{4,3,2,1,0:T(2,128)(2,1)S(1)} %pad_maximum_fusion.refs_0_), channel_id=1, source_target_pairs={{0,8},{8,16},{16,24},{24,0},{1,9},{9,17},{17,25},{25,1},{2,10},{10... | collective-permute-start | bytes 2359304 | tf_op jit(solution)/shard_map/ppermute | solution.py:39
  118.9 23.9 %collective-permute-start.27 = (bf16[2,3,128,2,256]{4,3,2,1,0:T(2,128)(2,1)S(1)}, bf16[2,3,128,2,256]{4,3,2,1,0:T(2,128)(2,1)S(1)}, u32[]{:S(2)}, u32[]{:S(2)}) collective-permute-start(bf16[2,3,128,2,256]{4,3,2,1,0:T(2,128)(2,1)S(1)} %pad_maximum_fusion.refs_0_), channel_id=1, source_target_pairs={{0,24},{8,0},{16,8},{24,16},{1,25},{9,1},{17,9},{25,17},{2,26},{10... | collective-permute-start | bytes 2359304 | tf_op jit(solution)/shard_map/ppermute | solution.py:39
  126.2 11.3 %collective-permute-start.30 = (bf16[192,512]{1,0:T(8,128)(2,1)S(1)}, bf16[192,512]{1,0:T(8,128)(2,1)S(1)}, u32[]{:S(2)}, u32[]{:S(2)}) collective-permute-start(bf16[192,512]{1,0:T(8,128)(2,1)S(1)} %get-tuple-element.90), channel_id=1, source_target_pairs={{0,3},{1,0},{2,1},{3,2},{4,7},{5,4},{6,5},{7,6},{8,11},{9,8},{10,9... | collective-permute-start | bytes 589832 | tf_op jit(solution)/shard_map/ppermute | solution.py:47
  130.0 7.4 %collective-permute-start.29 = (bf16[192,512]{1,0:T(8,128)(2,1)S(1)}, bf16[192,512]{1,0:T(8,128)(2,1)S(1)}, u32[]{:S(2)}, u32[]{:S(2)}) collective-permute-start(bf16[192,512]{1,0:T(8,128)(2,1)S(1)} %get-tuple-element.89), channel_id=1, source_target_pairs={{0,2},{1,3},{2,0},{3,1},{4,6},{5,7},{6,4},{7,5},{8,10},{9,11},{10,... | collective-permute-start | bytes 589832 | tf_op jit(solution)/shard_map/ppermute | solution.py:47
  130.1 11.9 %collective-permute-start.28 = (bf16[192,512]{1,0:T(8,128)(2,1)S(1)}, bf16[192,512]{1,0:T(8,128)(2,1)S(1)}, u32[]{:S(2)}, u32[]{:S(2)}) collective-permute-start(bf16[192,512]{1,0:T(8,128)(2,1)S(1)} %get-tuple-element.88), channel_id=1, source_target_pairs={{0,1},{1,2},{2,3},{3,0},{4,5},{5,6},{6,7},{7,4},{8,9},{9,10},{10,1... | collective-permute-start | bytes 589832 | tf_op jit(solution)/shard_map/ppermute | solution.py:47
  142.7 13.9 %collective-permute-start.33 = (bf16[2,3,128,2,256]{4,3,2,1,0:T(2,128)(2,1)S(1)}, bf16[2,3,128,2,256]{4,3,2,1,0:T(2,128)(2,1)S(1)}, u32[]{:S(2)}, u32[]{:S(2)}) collective-permute-start(bf16[2,3,128,2,256]{4,3,2,1,0:T(2,128)(2,1)S(1)} %pad_maximum_fusion.refs_0_), channel_id=1, source_target_pairs={{0,4},{4,0},{1,5},{5,1},{2,6},{6,2},{3,7},{7,3},{8,12},{12,8},{9,1... | collective-permute-start | bytes 2359304 | tf_op jit(solution)/shard_map/ppermute | solution.py:55
  143.6 13.0 %collective-permute-start.34 = (bf16[2,3,128,2,256]{4,3,2,1,0:T(2,128)(2,1)S(1)}, bf16[2,3,128,2,256]{4,3,2,1,0:T(2,128)(2,1)S(1)}, u32[]{:S(2)}, u32[]{:S(2)}) collective-permute-start(bf16[2,3,128,2,256]{4,3,2,1,0:T(2,128)(2,1)S(1)} %collective-permute-done.26.refs_1_), channel_id=1, source_target_pairs={{0,4},{4,0},{1,5},{5,1},{2,6},{6,2},{3,7},{7,3},{8,12},{12,8},{9,1... | collective-permute-start | bytes 2359304 | tf_op jit(solution)/shard_map/ppermute | solution.py:55
  143.7 13.0 %collective-permute-start.35 = (bf16[2,3,128,2,256]{4,3,2,1,0:T(2,128)(2,1)S(1)}, bf16[2,3,128,2,256]{4,3,2,1,0:T(2,128)(2,1)S(1)}, u32[]{:S(2)}, u32[]{:S(2)}) collective-permute-start(bf16[2,3,128,2,256]{4,3,2,1,0:T(2,128)(2,1)S(1)} %collective-permute-done.27.refs_2_), channel_id=1, source_target_pairs={{0,4},{4,0},{1,5},{5,1},{2,6},{6,2},{3,7},{7,3},{8,12},{12,8},{9,1... | collective-permute-start | bytes 2359304 | tf_op jit(solution)/shard_map/ppermute | solution.py:55
  144.6 12.0 %collective-permute-start.31 = (bf16[3,128,2,256]{3,2,1,0:T(2,128)(2,1)S(1)}, bf16[3,128,2,256]{3,2,1,0:T(2,128)(2,1)S(1)}, u32[]{:S(2)}, u32[]{:S(2)}) collective-permute-start(bf16[3,128,2,256]{3,2,1,0:T(2,128)(2,1)S(1)} %slice_bitcast_fusion.1), channel_id=1, source_target_pairs={{0,8},{8,16},{16,24},{24,0},{1,9},{9,17},{17,25},{25,1},{2,10},{10... | collective-permute-start | bytes 1179656 | tf_op jit(solution)/shard_map/ppermute | solution.py:39
  144.7 11.9 %collective-permute-start.32 = (bf16[3,128,2,256]{3,2,1,0:T(2,128)(2,1)S(1)}, bf16[3,128,2,256]{3,2,1,0:T(2,128)(2,1)S(1)}, u32[]{:S(2)}, u32[]{:S(2)}) collective-permute-start(bf16[3,128,2,256]{3,2,1,0:T(2,128)(2,1)S(1)} %slice_bitcast_fusion), channel_id=1, source_target_pairs={{0,24},{8,0},{16,8},{24,16},{1,25},{9,1},{17,9},{25,17},{2,26},{10... | collective-permute-start | bytes 1179656 | tf_op jit(solution)/shard_map/ppermute | solution.py:39
  156.6 3.9 %collective-permute-start.36 = (bf16[3,128,2,256]{3,2,1,0:T(2,128)(2,1)S(1)}, bf16[3,128,2,256]{3,2,1,0:T(2,128)(2,1)S(1)}, u32[]{:S(2)}, u32[]{:S(2)}) collective-permute-start(bf16[3,128,2,256]{3,2,1,0:T(2,128)(2,1)S(1)} %collective-permute-done.31), channel_id=1, source_target_pairs={{0,4},{4,0},{1,5},{5,1},{2,6},{6,2},{3,7},{7,3},{8,12},{12,8},{9,1... | collective-permute-start | bytes 1179656 | tf_op jit(solution)/shard_map/ppermute | solution.py:55
  157.6 3.0 %collective-permute-start.37 = (bf16[3,128,2,256]{3,2,1,0:T(2,128)(2,1)S(1)}, bf16[3,128,2,256]{3,2,1,0:T(2,128)(2,1)S(1)}, u32[]{:S(2)}, u32[]{:S(2)}) collective-permute-start(bf16[3,128,2,256]{3,2,1,0:T(2,128)(2,1)S(1)} %collective-permute-done.32), channel_id=1, source_target_pairs={{0,4},{4,0},{1,5},{5,1},{2,6},{6,2},{3,7},{7,3},{8,12},{12,8},{9,1... | collective-permute-start | bytes 1179656 | tf_op jit(solution)/shard_map/ppermute | solution.py:55
  (4 other events, 3.4 us)

commit v5 on v4

--- a/solution.py
+++ b/solution.py
@@ -424,10 +424,7 @@
     keys, values = pack(info, key_value_weight, adapter_down_weight)
     kx1, kx2, kx3 = x_shift(keys, 1), x_shift(keys, 2), x_shift(keys, -1)
     vy1, vy3 = y_shift(values, 1), y_shift(values, -1)
-    att0 = attend(query, key_value_cache, current_key_value, cached_length, 0, 2)
-    keys, kx1, kx2, kx3, values, vy1, vy3, att0 = barrier(
-        (keys, kx1, kx2, kx3, values, vy1, vy3, att0)
-    )
+    keys, kx1, kx2, kx3, values, vy1, vy3 = barrier((keys, kx1, kx2, kx3, values, vy1, vy3))
     vy2 = y_shift(values, 2)
     key0 = jnp.concatenate([keys, kx1, kx2, kx3], 0)
     key1, key3 = y_shift(key0, 1), y_shift(key0, -1)
@@ -437,16 +434,16 @@
     value1, value3 = x_shift(value0, 1), x_shift(value0, -1)
     down0 = jnp.concatenate([v[256:] for v in both], 0)
     down_own = jnp.concatenate([down0, xh_swap(down0)], 0)
-    att1 = attend(query, key_value_cache, current_key_value, cached_length, 1, 2)
-    attended = jnp.concatenate([att0, att1], 0).reshape(rows, heads * HEAD_DIM)
-    low = low_rank(info, tokens, down_own, core_swap(down_own))
-    key0, value0, key1, key3, value1, value3, low, attended = barrier(
-        (key0, value0, key1, key3, value1, value3, low, attended)
+    attended = attend(query, key_value_cache, current_key_value, cached_length, 0, 1)
+    attended = attended.reshape(rows, heads * HEAD_DIM)
+    key0, value0, key1, key3, value1, value3, down_own, attended = barrier(
+        (key0, value0, key1, key3, value1, value3, down_own, attended)
     )
     first = [key0, value0, key1, key3, value1, value3]
     key2, value2 = y_shift(key0, 2), x_shift(value0, 2)
     theirs = core_swap(jnp.concatenate(first, 0))
     across = xh_swap(attended)
+    low = low_rank(info, tokens, down_own, core_swap(down_own))
     pair = jnp.concatenate([low, z_flip(low, 1)], 0)
     lows = jnp.concatenate([pair, z_flip(pair, 2)], 0)
     key2, value2, theirs, across, lows, attended = barrier(
@@ -464,9 +461,9 @@
 
     b0 = lax.ppermute(same, "pool", [(0, 1), (1, 0)])
     a0 = lax.ppermute(other, ("pool", "xh"), [(i, 3 - i) for i in range(4)])
+    b0, a0, mine = barrier((b0, a0, mine))
     mine = jnp.concatenate(mine, 0)
     partner = core_swap(mine)
-    b0, a0, mine, partner = barrier((b0, a0, mine, partner))
     both0 = jnp.stack([b0, a0])
     both1, both3 = y_shift(both0, 1), y_shift(both0, -1)
     ranks = ADAPTERS * RANK

time: 162 us -> 136 us (0.84)
  waiting for transfers between devices: 67.6 us -> 40.4 us
  starting transfers between devices: 52.8 us -> 56.7 us
  local copies, waits for them, and re-layouts: 9.2 us -> 6.83 us
    ppermute x2, waiting for transfers between devices: 16.6 us -> 4.69 us  [xh_swap(): return lax.ppermute(value, 'xh', [(0, 1), (1, 0)])]
    ppermute x13, waiting for transfers between devices: 27.2 us -> 17 us  [y_shift(): return lax.ppermute(value, 'y', [(i, (i + k) % 4) for i in range(4)])]
    ppermute x1, waiting for transfers between devices: 8.25 us -> 1.19 us  [body(): b0 = lax.ppermute(same, 'pool', [(0, 1), (1, 0)])]
    ppermute x6, waiting for transfers between devices: 0.02 us -> 4.37 us  [x_shift(): return lax.ppermute(value, ('pool', 'xh'), pairs)]
    ppermute x3, waiting for transfers between devices: 11.2 us -> 7.89 us  [z_shift(): return lax.ppermute(value, 'head', [(i, (i + k) % 4) for i in range(4)])]
    ppermute x10, starting transfers between devices: 10.6 us -> 13 us  [core_swap(): return lax.ppermute(value, 'core', [(0, 1), (1, 0)])]
    unnamed x41 -> x40, local copies, waits for them, and re-layouts: 7.58 us -> 5.22 us
    ppermute x10, waiting for transfers between devices: 0.03 us -> 2.17 us  [core_swap(): return lax.ppermute(value, 'core', [(0, 1), (1, 0)])]
  transfers between devices with their start and end apart: 38 -> 38, of which waited for: 13 -> 14; matrix products, arithmetic and copies ran while one was open for 2% -> 2% of each run, Pallas kernels for 16% -> 19%
where the time goes in v5:
time: 136 us; the launch traced here: 135 us
  starting transfers between devices  56.7 us (42%)
  waiting for transfers between devices  40.4 us (30%)
  Pallas kernels  28.1 us (21%)
  local copies, waits for them, and re-layouts  6.83 us (5%)
  other arithmetic  1.95 us (1%)
    ppermute x13, starting transfers between devices, y_shift(): return lax.ppermute(value, 'y', [(i, (i + k) % 4) for i in range(4)])  18.3 us
    ppermute x13, waiting for transfers between devices, y_shift(): return lax.ppermute(value, 'y', [(i, (i + k) % 4) for i in range(4)])  17 us
    ppermute x10, starting transfers between devices, core_swap(): return lax.ppermute(value, 'core', [(0, 1), (1, 0)])  13 us
    ppermute x6, starting transfers between devices, x_shift(): return lax.ppermute(value, ('pool', 'xh'), pairs)  9.42 us
    pallas_call x1, Pallas kernels, attend(): pl.pallas_call(functools.partial(attend_kernel, first * ROWS_STEP), grid_...  7.99 us
    ppermute x3, waiting for transfers between devices, z_shift(): return lax.ppermute(value, 'head', [(i, (i + k) % 4) for i in range(4)])  7.89 us
    ppermute x3, starting transfers between devices, z_shift(): return lax.ppermute(value, 'head', [(i, (i + k) % 4) for i in range(4)])  5.83 us
    pallas_call x2, Pallas kernels, main_product(): pl.pallas_call(functools.partial(main_kernel, kinds, not sums), in_specs=...  5.78 us
  transfers between devices with their start and end apart: 38, of which 14 were waited for; matrix products, arithmetic and copies ran while one was open for 2% of the time, Pallas kernels for 19%

profile of v5, /device:TPU:1, one launch (start us, length us, event | category | flops | bytes accessed | tf_op | source)
XLA Modules:
  0.0 135.3 jit_solution(13210044564782005098)
XLA Ops:
  1.4 1.0 copy-done.3
  3.4 1.5 %pack.1 = (bf16[256,256]{1,0:T(8,128)(2,1)S(1)}, bf16[320,256]{1,0:T(8,128)(2,1)S(1)}) custom-call(s32[17]{0:T(128)S(1)} %concatenate.32.info, bf16[512,2,256]{2,1,0:T(2,128)(2,1)S(1)} %copy-done.3, bf16[512,256]{1,0:T(8,128)(2,1)S(1)} %copy-done.4), custom_call_target="tpu_custom_call" | custom-call | tf_op jit(solution)/shard_map/pack/pallas_call | solution.py:76
  4.9 2.2 %collective-permute-start.3 = (bf16[320,256]{1,0:T(8,128)(2,1)S(1)}, bf16[320,256]{1,0:T(8,128)(2,1)S(1)}, u32[]{:S(2)}, u32[]{:S(2)}) collective-permute-start(bf16[320,256]{1,0:T(8,128)(2,1)S(1)} %get-tuple-element.58), channel_id=1, source_target_pairs={{0,8},{8,16},{16,24},{24,0},{1,9},{9,17},{17,25},{25,1},{2,10},{10... | collective-permute-start | bytes 491528 | tf_op jit(solution)/shard_map/ppermute | solution.py:39
  7.1 1.5 %collective-permute-start.4 = (bf16[320,256]{1,0:T(8,128)(2,1)S(1)}, bf16[320,256]{1,0:T(8,128)(2,1)S(1)}, u32[]{:S(2)}, u32[]{:S(2)}) collective-permute-start(bf16[320,256]{1,0:T(8,128)(2,1)S(1)} %get-tuple-element.58), channel_id=1, source_target_pairs={{0,24},{8,0},{16,8},{24,16},{1,25},{9,1},{17,9},{25,17},{2,26},{10... | collective-permute-start | bytes 491528 | tf_op jit(solution)/shard_map/ppermute | solution.py:39
  8.6 1.2 collective-permute-start
  9.8 2.5 %collective-permute-start.1 = (bf16[256,256]{1,0:T(8,128)(2,1)S(1)}, bf16[256,256]{1,0:T(8,128)(2,1)S(1)}, u32[]{:S(2)}, u32[]{:S(2)}) collective-permute-start(bf16[256,256]{1,0:T(8,128)(2,1)S(1)} %get-tuple-element.54), channel_id=1, source_target_pairs={{0,32},{64,96},{32,0},{96,64},{1,33},{65,97},{33,1},{97,65},{2,34}... | collective-permute-start | bytes 393224 | tf_op jit(solution)/shard_map/ppermute | solution.py:35
  12.3 1.2 collective-permute-start.2
  13.7 3.6 %collective-permute-done.1 = bf16[256,256]{1,0:T(8,128)(2,1)S(1)} collective-permute-done((bf16[256,256]{1,0:T(8,128)(2,1)S(1)}, bf16[256,256]{1,0:T(8,128)(2,1)S(1)}, u32[]{:S(2)}, u32[]{:S(2)}) %collective-permute-start.1) | collective-permute-done | bytes 131104 | tf_op jit(solution)/shard_map/ppermute | solution.py:35
  17.8 1.2 collective-permute-start.5
  19.6 2.3 %collective-permute-start.7 = (bf16[1024,256]{1,0:T(8,128)(2,1)S(1)}, bf16[1024,256]{1,0:T(8,128)(2,1)S(1)}, u32[]{:S(2)}, u32[]{:S(2)}) collective-permute-start(bf16[1024,256]{1,0:T(8,128)(2,1)S(1)} %constant_dynamic-update-slice_fusion.refs_0_), channel_id=1, source_target_pairs={{0,24},{8,0},{16,8},{24,16},{1,25},{9,1},{17,9},{25,17},{2,26},{10... | collective-permute-start | bytes 1572872 | tf_op jit(solution)/shard_map/ppermute | solution.py:39
  22.0 1.7 %collective-permute-done.5 = bf16[320,256]{1,0:T(8,128)(2,1)S(1)} collective-permute-done((bf16[320,256]{1,0:T(8,128)(2,1)S(1)}, bf16[320,256]{1,0:T(8,128)(2,1)S(1)}, u32[]{:S(2)}, u32[]{:S(2)}) %collective-permute-start.5) | collective-permute-done | bytes 163872 | tf_op jit(solution)/shard_map/ppermute | solution.py:39
  24.7 1.7 %collective-permute-start.9 = (bf16[1024,256]{1,0:T(8,128)(2,1)S(1)}, bf16[1024,256]{1,0:T(8,128)(2,1)S(1)}, u32[]{:S(2)}, u32[]{:S(2)}) collective-permute-start(bf16[1024,256]{1,0:T(8,128)(2,1)S(1)} %pad_maximum_fusion.1.refs_1_), channel_id=1, source_target_pairs={{0,96},{64,0},{32,64},{96,32},{1,97},{65,1},{33,65},{97,33},{2,98}... | collective-permute-start | bytes 1572872 | tf_op jit(solution)/shard_map/ppermute | solution.py:35
  26.5 1.1 collective-permute-start.10
  27.7 2.8 %copy-done = bf16[48,128,2,256]{3,2,1,0:T(2,128)(2,1)S(1)} copy-done((bf16[48,128,2,256]{3,2,1,0:T(2,128)(2,1)S(1)}, bf16[48,128,2,256]{3,2,1,0:T(2,128)(2,1)}, u32[]{:S(2)}) %copy-start) | copy-done | bytes 6291480
  30.5 8.0 %attend.1 = bf16[48,16,128]{2,1,0:T(8,128)(2,1)S(1)} custom-call(s32[48]{0:T(128)S(1)} %copy-done.8, bf16[48,16,128]{2,1,0:T(8,128)(2,1)S(1)} %bitcast.32, bf16[48,128,2,256]{3,2,1,0:T(2,128)(2,1)S(1)} %copy-done, bf16[48,2,256]{2,1,0:T(2,128)(2,1)S(1)} %copy-done.7), custom_call_target="tpu_custom_call" | custom-call | tf_op jit(solution)/shard_map/attend/pallas_call | solution.py:131
  38.9 5.7 %collective-permute-start.13 = (bf16[6144,256]{1,0:T(8,128)(2,1)S(1)}, bf16[6144,256]{1,0:T(8,128)(2,1)S(1)}, u32[]{:S(2)}, u32[]{:S(2)}) collective-permute-start(bf16[6144,256]{1,0:T(8,128)(2,1)S(1)} %constant_dynamic-update-slice_fusion.9), channel_id=1, source_target_pairs={{0,4},{4,0},{1,5},{5,1},{2,6},{6,2},{3,7},{7,3},{8,12},{12,8},{9,1... | collective-permute-start | bytes 9437192 | tf_op jit(solution)/shard_map/ppermute | solution.py:55
  44.6 1.6 %collective-permute-start.11 = (bf16[1024,256]{1,0:T(8,128)(2,1)S(1)}, bf16[1024,256]{1,0:T(8,128)(2,1)S(1)}, u32[]{:S(2)}, u32[]{:S(2)}) collective-permute-start(bf16[1024,256]{1,0:T(8,128)(2,1)S(1)} %constant_dynamic-update-slice_fusion.refs_0_), channel_id=1, source_target_pairs={{0,16},{8,24},{16,0},{24,8},{1,17},{9,25},{17,1},{25,9},{2,18},{10... | collective-permute-start | bytes 1572872 | tf_op jit(solution)/shard_map/ppermute | solution.py:39
  46.2 1.9 %collective-permute-start.12 = (bf16[1024,256]{1,0:T(8,128)(2,1)S(1)}, bf16[1024,256]{1,0:T(8,128)(2,1)S(1)}, u32[]{:S(2)}, u32[]{:S(2)}) collective-permute-start(bf16[1024,256]{1,0:T(8,128)(2,1)S(1)} %pad_maximum_fusion.1.refs_1_), channel_id=1, source_target_pairs={{0,32},{64,96},{32,0},{96,64},{1,33},{65,97},{33,1},{97,65},{2,34}... | collective-permute-start | bytes 1572872 | tf_op jit(solution)/shard_map/ppermute | solution.py:35
  48.1 2.1 %collective-permute-done.15.other_ref = bf16[512,256]{1,0:T(8,128)(2,1)S(1)} collective-permute-done((bf16[512,256]{1,0:T(8,128)(2,1)S(1)}, bf16[512,256]{1,0:T(8,128)(2,1)S(1)}, u32[]{:S(2)}, u32[]{:S(2)}) %collective-permute-start.15) | collective-permute-done | bytes 262176 | tf_op jit(solution)/shard_map/ppermute | solution.py:55
  50.2 1.3 low_rank.1
  51.5 1.7 %collective-permute-start.16 = (f32[32,128]{1,0:T(8,128)S(1)}, f32[32,128]{1,0:T(8,128)S(1)}, u32[]{:S(2)}, u32[]{:S(2)}) collective-permute-start(f32[32,128]{1,0:T(8,128)S(1)} %low_rank.1), channel_id=1, source_target_pairs={{0,1},{1,0},{2,3},{3,2},{4,5},{5,4},{6,7},{7,6},{8,9},{9,8},{10,11... | collective-permute-start | bytes 49160 | tf_op jit(solution)/shard_map/ppermute | solution.py:51
  53.3 1.8 %collective-permute-start.14 = (bf16[48,2048]{1,0:T(8,128)(2,1)S(1)}, bf16[48,2048]{1,0:T(8,128)(2,1)S(1)}, u32[]{:S(2)}, u32[]{:S(2)}) collective-permute-start(bf16[48,2048]{1,0:T(8,128)(2,1)S(1)} %bitcast.39), channel_id=1, source_target_pairs={{0,32},{32,0},{1,33},{33,1},{2,34},{34,2},{3,35},{35,3},{4,36},{36... | collective-permute-start | bytes 589832 | tf_op jit(solution)/shard_map/ppermute | solution.py:43
  55.1 3.3 %collective-permute-start.17 = (f32[64,128]{1,0:T(8,128)S(1)}, f32[64,128]{1,0:T(8,128)S(1)}, u32[]{:S(2)}, u32[]{:S(2)}) collective-permute-start(f32[64,128]{1,0:T(8,128)S(1)} %pad_maximum_fusion.4), channel_id=1, source_target_pairs={{0,2},{1,3},{2,0},{3,1},{4,6},{5,7},{6,4},{7,5},{8,10},{9,11},{10,... | collective-permute-start | bytes 98312 | tf_op jit(solution)/shard_map/ppermute | solution.py:51
  58.4 1.6 %collective-permute-done.17 = f32[64,128]{1,0:T(8,128)S(1)} collective-permute-done((f32[64,128]{1,0:T(8,128)S(1)}, f32[64,128]{1,0:T(8,128)S(1)}, u32[]{:S(2)}, u32[]{:S(2)}) %collective-permute-start.17) | collective-permute-done | bytes 32800 | tf_op jit(solution)/shard_map/ppermute | solution.py:51
  60.0 4.7 %collective-permute-done.14 = bf16[48,2048]{1,0:T(8,128)(2,1)S(1)} collective-permute-done((bf16[48,2048]{1,0:T(8,128)(2,1)S(1)}, bf16[48,2048]{1,0:T(8,128)(2,1)S(1)}, u32[]{:S(2)}, u32[]{:S(2)}) %collective-permute-start.14) | collective-permute-done | bytes 196640 | tf_op jit(solution)/shard_map/ppermute | solution.py:43
  64.7 1.7 %collective-permute-start.18 = (bf16[1024,256]{1,0:T(8,128)(2,1)S(1)}, bf16[1024,256]{1,0:T(8,128)(2,1)S(1)}, u32[]{:S(2)}, u32[]{:S(2)}) collective-permute-start(bf16[1024,256]{1,0:T(8,128)(2,1)S(1)} %collective-permute-done.11.refs_6_), channel_id=1, source_target_pairs={{0,4},{4,0},{1,5},{5,1},{2,6},{6,2},{3,7},{7,3},{8,12},{12,8},{9,1... | collective-permute-start | bytes 1572872 | tf_op jit(solution)/shard_map/ppermute | solution.py:55
  67.0 1.5 %collective-permute-start.23 = (bf16[96,2048]{1,0:T(8,128)(2,1)S(1)}, bf16[96,2048]{1,0:T(8,128)(2,1)S(1)}, u32[]{:S(2)}, u32[]{:S(2)}) collective-permute-start(bf16[96,2048]{1,0:T(8,128)(2,1)S(1)} %constant_dynamic-update-slice_fusion.15), channel_id=1, source_target_pairs={{0,16},{8,24},{16,0},{24,8},{1,17},{9,25},{17,1},{25,9},{2,18},{10... | collective-permute-start | bytes 1179656 | tf_op jit(solution)/shard_map/ppermute | solution.py:39
  68.4 1.6 %collective-permute-start.24 = (bf16[96,2048]{1,0:T(8,128)(2,1)S(1)}, bf16[96,2048]{1,0:T(8,128)(2,1)S(1)}, u32[]{:S(2)}, u32[]{:S(2)}) collective-permute-start(bf16[96,2048]{1,0:T(8,128)(2,1)S(1)} %constant_dynamic-update-slice_fusion.15), channel_id=1, source_target_pairs={{0,24},{8,0},{16,8},{24,16},{1,25},{9,1},{17,9},{25,17},{2,26},{10... | collective-permute-start | bytes 1179656 | tf_op jit(solution)/shard_map/ppermute | solution.py:39
  70.0 4.5 %main_product.2 = (f32[512,256]{1,0:T(8,128)S(1)}, f32[512,256]{1,0:T(8,128)S(1)}) custom-call(s32[17]{0:T(128)S(1)} %concatenate.32.info, bf16[512,8192]{1,0:T(8,128)(2,1)S(1)} %bitcast.29, bf16[1024,256]{1,0:T(8,128)(2,1)S(1)} %constant_dynamic-update-slice_fusion.refs_0_, bf16[1024,256]{1,0:T(8,128)(2,1)S(1)} %pad_maximum_fusion.1.refs_1_, ...), custom_call_target="tpu_custom_call" | custom-call | tf_op jit(solution)/shard_map/main_product/pallas_call | solution.py:227
  74.6 1.3 main_product.3
  75.9 2.6 %finish.1 = (bf16[3,128,2,256]{3,2,1,0:T(2,128)(2,1)S(1)}, bf16[3,128,2,256]{3,2,1,0:T(2,128)(2,1)S(1)}) custom-call(s32[17]{0:T(128)S(1)} %concatenate.32.info, f32[128,128]{1,0:T(8,128)S(1)} %pad_maximum_fusion.3.refs_0_, f32[512,256]{1,0:T(8,128)S(1)} %get-tuple-element.77.refs_1_, f32[512,256]{1,0:T(8,128)S(1)} %get-tuple-element.78.refs_2_, ...), custom_call_target="tpu_custom_call" | custom-call | tf_op jit(solution)/shard_map/finish/pallas_call | solution.py:268
  79.2 1.6 %collective-permute-start.21 = (bf16[3,128,2,256]{3,2,1,0:T(2,128)(2,1)S(1)}, bf16[3,128,2,256]{3,2,1,0:T(2,128)(2,1)S(1)}, u32[]{:S(2)}, u32[]{:S(2)}) collective-permute-start(bf16[3,128,2,256]{3,2,1,0:T(2,128)(2,1)S(1)} %get-tuple-element.80), channel_id=1, source_target_pairs={{0,96},{32,64},{64,32},{96,0},{1,97},{33,65},{65,33},{97,1},{2,98}... | collective-permute-start | bytes 1179656 | tf_op jit(solution)/shard_map/ppermute | solution.py:463
  80.7 5.0 %collective-permute-done.23 = bf16[96,2048]{1,0:T(8,128)(2,1)S(1)} collective-permute-done((bf16[96,2048]{1,0:T(8,128)(2,1)S(1)}, bf16[96,2048]{1,0:T(8,128)(2,1)S(1)}, u32[]{:S(2)}, u32[]{:S(2)}) %collective-permute-start.23) | collective-permute-done | bytes 393248 | tf_op jit(solution)/shard_map/ppermute | solution.py:39
  85.7 1.1 collective-permute-done.24
  86.8 1.2 collective-permute-done.20
  88.0 1.5 %collective-permute-done.21 = bf16[3,128,2,256]{3,2,1,0:T(2,128)(2,1)S(1)} collective-permute-done((bf16[3,128,2,256]{3,2,1,0:T(2,128)(2,1)S(1)}, bf16[3,128,2,256]{3,2,1,0:T(2,128)(2,1)S(1)}, u32[]{:S(2)}, u32[]{:S(2)}) %collective-permute-start.21) | collective-permute-done | bytes 393248 | tf_op jit(solution)/shard_map/ppermute | solution.py:463
  89.6 2.5 %collective-permute-start.27 = (bf16[384,2048]{1,0:T(8,128)(2,1)S(1)}, bf16[384,2048]{1,0:T(8,128)(2,1)S(1)}, u32[]{:S(2)}, u32[]{:S(2)}) collective-permute-start(bf16[384,2048]{1,0:T(8,128)(2,1)S(1)} %constant_dynamic-update-slice_fusion.17.refs_0_), channel_id=1, source_target_pairs={{0,4},{4,0},{1,5},{5,1},{2,6},{6,2},{3,7},{7,3},{8,12},{12,8},{9,1... | collective-permute-start | bytes 4718600 | tf_op jit(solution)/shard_map/ppermute | solution.py:55
  92.1 1.1 pad_maximum_fusion.refs_0_
  93.3 2.7 %collective-permute-start.26 = (bf16[2,3,128,2,256]{4,3,2,1,0:T(2,128)(2,1)S(1)}, bf16[2,3,128,2,256]{4,3,2,1,0:T(2,128)(2,1)S(1)}, u32[]{:S(2)}, u32[]{:S(2)}) collective-permute-start(bf16[2,3,128,2,256]{4,3,2,1,0:T(2,128)(2,1)S(1)} %pad_maximum_fusion.refs_0_), channel_id=1, source_target_pairs={{0,24},{8,0},{16,8},{24,16},{1,25},{9,1},{17,9},{25,17},{2,26},{10... | collective-permute-start | bytes 2359304 | tf_op jit(solution)/shard_map/ppermute | solution.py:39
  96.2 5.2 %project.1 = (bf16[192,512]{1,0:T(8,128)(2,1)S(1)}, bf16[192,512]{1,0:T(8,128)(2,1)S(1)}, bf16[192,512]{1,0:T(8,128)(2,1)S(1)}, bf16[192,512]{1,0:T(8,128)(2,1)S(1)}) custom-call(s32[17]{0:T(128)S(1)} %concatenate.32.info, s32[768,1]{1,0:T(8,128)S(1)} %broadcast_in_dim.20.keep, bf16[128,2048]{1,0:T(8,128)(2,1)S(1)} %bitcast.33, ...), custom_call_target="tpu_custom_call" | custom-call | tf_op jit(solution)/shard_map/project/pallas_call | solution.py:384
  101.3 1.8 %collective-permute-start.28 = (bf16[192,512]{1,0:T(8,128)(2,1)S(1)}, bf16[192,512]{1,0:T(8,128)(2,1)S(1)}, u32[]{:S(2)}, u32[]{:S(2)}) collective-permute-start(bf16[192,512]{1,0:T(8,128)(2,1)S(1)} %get-tuple-element.90), channel_id=1, source_target_pairs={{0,1},{1,2},{2,3},{3,0},{4,5},{5,6},{6,7},{7,4},{8,9},{9,10},{10,1... | collective-permute-start | bytes 589832 | tf_op jit(solution)/shard_map/ppermute | solution.py:47
  103.1 3.3 %collective-permute-start.29 = (bf16[192,512]{1,0:T(8,128)(2,1)S(1)}, bf16[192,512]{1,0:T(8,128)(2,1)S(1)}, u32[]{:S(2)}, u32[]{:S(2)}) collective-permute-start(bf16[192,512]{1,0:T(8,128)(2,1)S(1)} %get-tuple-element.91), channel_id=1, source_target_pairs={{0,2},{1,3},{2,0},{3,1},{4,6},{5,7},{6,4},{7,5},{8,10},{9,11},{10,... | collective-permute-start | bytes 589832 | tf_op jit(solution)/shard_map/ppermute | solution.py:47
  107.2 2.8 %collective-permute-done.28 = bf16[192,512]{1,0:T(8,128)(2,1)S(1)} collective-permute-done((bf16[192,512]{1,0:T(8,128)(2,1)S(1)}, bf16[192,512]{1,0:T(8,128)(2,1)S(1)}, u32[]{:S(2)}, u32[]{:S(2)}) %collective-permute-start.28) | collective-permute-done | bytes 196640 | tf_op jit(solution)/shard_map/ppermute | solution.py:47
  110.0 5.1 %collective-permute-done.29 = bf16[192,512]{1,0:T(8,128)(2,1)S(1)} collective-permute-done((bf16[192,512]{1,0:T(8,128)(2,1)S(1)}, bf16[192,512]{1,0:T(8,128)(2,1)S(1)}, u32[]{:S(2)}, u32[]{:S(2)}) %collective-permute-start.29) | collective-permute-done | bytes 196640 | tf_op jit(solution)/shard_map/ppermute | solution.py:47
  115.9 1.4 %collective-permute-start.33 = (bf16[2,3,128,2,256]{4,3,2,1,0:T(2,128)(2,1)S(1)}, bf16[2,3,128,2,256]{4,3,2,1,0:T(2,128)(2,1)S(1)}, u32[]{:S(2)}, u32[]{:S(2)}) collective-permute-start(bf16[2,3,128,2,256]{4,3,2,1,0:T(2,128)(2,1)S(1)} %pad_maximum_fusion.refs_0_), channel_id=1, source_target_pairs={{0,4},{4,0},{1,5},{5,1},{2,6},{6,2},{3,7},{7,3},{8,12},{12,8},{9,1... | collective-permute-start | bytes 2359304 | tf_op jit(solution)/shard_map/ppermute | solution.py:55
  118.4 2.7 %collective-permute-start.32 = (bf16[3,128,2,256]{3,2,1,0:T(2,128)(2,1)S(1)}, bf16[3,128,2,256]{3,2,1,0:T(2,128)(2,1)S(1)}, u32[]{:S(2)}, u32[]{:S(2)}) collective-permute-start(bf16[3,128,2,256]{3,2,1,0:T(2,128)(2,1)S(1)} %slice_bitcast_fusion), channel_id=1, source_target_pairs={{0,24},{8,0},{16,8},{24,16},{1,25},{9,1},{17,9},{25,17},{2,26},{10... | collective-permute-start | bytes 1179656 | tf_op jit(solution)/shard_map/ppermute | solution.py:39
  121.1 9.2 %collective-permute-done.31 = bf16[3,128,2,256]{3,2,1,0:T(2,128)(2,1)S(1)} collective-permute-done((bf16[3,128,2,256]{3,2,1,0:T(2,128)(2,1)S(1)}, bf16[3,128,2,256]{3,2,1,0:T(2,128)(2,1)S(1)}, u32[]{:S(2)}, u32[]{:S(2)}) %collective-permute-start.31) | collective-permute-done | bytes 393248 | tf_op jit(solution)/shard_map/ppermute | solution.py:39
  131.4 2.9 %place.2.refs_4_ = bf16[1,2,2048,2,256]{4,3,2,1,0:T(2,128)(2,1)} custom-call(s32[17]{0:T(128)S(1)} %concatenate.32.info, bf16[2,3,128,2,256]{4,3,2,1,0:T(2,128)(2,1)S(1)} %pad_maximum_fusion.refs_0_, bf16[2,3,128,2,256]{4,3,2,1,0:T(2,128)(2,1)S(1)} %collective-permute-done.25.refs_1_, bf16[2,3,128,2,256]{4,3,2,1,0:T(2,128)(2,1)S(1)} %collective-permute-done.26.refs_2_, ...), custom_call_target="tpu_custom_call" | custom-call | tf_op jit(solution)/shard_map/place/pallas_call | solution.py:342
  (101 shorter events, 10.8 us)
Async XLA Ops:
  0.6 27.0 %copy-start.8 = (s32[48]{0:T(128)S(1)}, s32[48]{0:T(128)}, u32[]{:S(2)}) copy-start(s32[48]{0:T(128)} %len_ref) | copy-start | bytes 580
  3.4 24.2 %copy-start.9 = (bf16[48,2048]{1,0:T(8,128)(2,1)S(1)}, bf16[48,2048]{1,0:T(8,128)(2,1)}, u32[]{:S(2)}) copy-start(bf16[48,2048]{1,0:T(8,128)(2,1)} %param.20) | copy-start | bytes 589828
  3.4 24.3 %copy-start.7 = (bf16[48,2,256]{2,1,0:T(2,128)(2,1)S(1)}, bf16[48,2,256]{2,1,0:T(2,128)(2,1)}, u32[]{:S(2)}) copy-start(bf16[48,2,256]{2,1,0:T(2,128)(2,1)} %cur_ref.1) | copy-start | bytes 147460
  4.9 12.9 %collective-permute-start.3 = (bf16[320,256]{1,0:T(8,128)(2,1)S(1)}, bf16[320,256]{1,0:T(8,128)(2,1)S(1)}, u32[]{:S(2)}, u32[]{:S(2)}) collective-permute-start(bf16[320,256]{1,0:T(8,128)(2,1)S(1)} %get-tuple-element.58), channel_id=1, source_target_pairs={{0,8},{8,16},{16,24},{24,0},{1,9},{9,17},{17,25},{25,1},{2,10},{10... | collective-permute-start | bytes 491528 | tf_op jit(solution)/shard_map/ppermute | solution.py:39
  7.1 10.7 %collective-permute-start.4 = (bf16[320,256]{1,0:T(8,128)(2,1)S(1)}, bf16[320,256]{1,0:T(8,128)(2,1)S(1)}, u32[]{:S(2)}, u32[]{:S(2)}) collective-permute-start(bf16[320,256]{1,0:T(8,128)(2,1)S(1)} %get-tuple-element.58), channel_id=1, source_target_pairs={{0,24},{8,0},{16,8},{24,16},{1,25},{9,1},{17,9},{25,17},{2,26},{10... | collective-permute-start | bytes 491528 | tf_op jit(solution)/shard_map/ppermute | solution.py:39
  8.6 5.0 %collective-permute-start = (bf16[256,256]{1,0:T(8,128)(2,1)S(1)}, bf16[256,256]{1,0:T(8,128)(2,1)S(1)}, u32[]{:S(2)}, u32[]{:S(2)}) collective-permute-start(bf16[256,256]{1,0:T(8,128)(2,1)S(1)} %get-tuple-element.54), channel_id=1, source_target_pairs={{0,64},{64,32},{32,96},{96,0},{1,65},{65,33},{33,97},{97,1},{2,66}... | collective-permute-start | bytes 393224 | tf_op jit(solution)/shard_map/ppermute | solution.py:35
  9.8 7.4 %collective-permute-start.1 = (bf16[256,256]{1,0:T(8,128)(2,1)S(1)}, bf16[256,256]{1,0:T(8,128)(2,1)S(1)}, u32[]{:S(2)}, u32[]{:S(2)}) collective-permute-start(bf16[256,256]{1,0:T(8,128)(2,1)S(1)} %get-tuple-element.54), channel_id=1, source_target_pairs={{0,32},{64,96},{32,0},{96,64},{1,33},{65,97},{33,1},{97,65},{2,34}... | collective-permute-start | bytes 393224 | tf_op jit(solution)/shard_map/ppermute | solution.py:35
  12.3 5.5 %collective-permute-start.2 = (bf16[256,256]{1,0:T(8,128)(2,1)S(1)}, bf16[256,256]{1,0:T(8,128)(2,1)S(1)}, u32[]{:S(2)}, u32[]{:S(2)}) collective-permute-start(bf16[256,256]{1,0:T(8,128)(2,1)S(1)} %get-tuple-element.54), channel_id=1, source_target_pairs={{0,96},{64,0},{32,64},{96,32},{1,97},{65,1},{33,65},{97,33},{2,98}... | collective-permute-start | bytes 393224 | tf_op jit(solution)/shard_map/ppermute | solution.py:35
  17.8 5.8 %collective-permute-start.5 = (bf16[320,256]{1,0:T(8,128)(2,1)S(1)}, bf16[320,256]{1,0:T(8,128)(2,1)S(1)}, u32[]{:S(2)}, u32[]{:S(2)}) collective-permute-start(bf16[320,256]{1,0:T(8,128)(2,1)S(1)} %get-tuple-element.58), channel_id=1, source_target_pairs={{0,16},{8,24},{16,0},{24,8},{1,17},{9,25},{17,1},{25,9},{2,18},{10... | collective-permute-start | bytes 491528 | tf_op jit(solution)/shard_map/ppermute | solution.py:39
  19.2 19.4 %collective-permute-start.6 = (bf16[1024,256]{1,0:T(8,128)(2,1)S(1)}, bf16[1024,256]{1,0:T(8,128)(2,1)S(1)}, u32[]{:S(2)}, u32[]{:S(2)}) collective-permute-start(bf16[1024,256]{1,0:T(8,128)(2,1)S(1)} %constant_dynamic-update-slice_fusion.refs_0_), channel_id=1, source_target_pairs={{0,8},{8,16},{16,24},{24,0},{1,9},{9,17},{17,25},{25,1},{2,10},{10... | collective-permute-start | bytes 1572872 | tf_op jit(solution)/shard_map/ppermute | solution.py:39
  19.6 18.9 %collective-permute-start.7 = (bf16[1024,256]{1,0:T(8,128)(2,1)S(1)}, bf16[1024,256]{1,0:T(8,128)(2,1)S(1)}, u32[]{:S(2)}, u32[]{:S(2)}) collective-permute-start(bf16[1024,256]{1,0:T(8,128)(2,1)S(1)} %constant_dynamic-update-slice_fusion.refs_0_), channel_id=1, source_target_pairs={{0,24},{8,0},{16,8},{24,16},{1,25},{9,1},{17,9},{25,17},{2,26},{10... | collective-permute-start | bytes 1572872 | tf_op jit(solution)/shard_map/ppermute | solution.py:39
  23.7 26.5 %slice-start = ((s8[8388608]{0:T(1024)(128)(4,1)}), s8[4194304]{0:T(1024)(128)(4,1)S(1)}, s32[]{:S(2)}) async-start(s8[8388608]{0:T(1024)(128)(4,1)} %bitcast.26), calls=%async_computation | async-start | bytes 8388608
  23.7 14.9 %collective-permute-start.8 = (bf16[1024,256]{1,0:T(8,128)(2,1)S(1)}, bf16[1024,256]{1,0:T(8,128)(2,1)S(1)}, u32[]{:S(2)}, u32[]{:S(2)}) collective-permute-start(bf16[1024,256]{1,0:T(8,128)(2,1)S(1)} %pad_maximum_fusion.1.refs_1_), channel_id=1, source_target_pairs={{0,64},{64,32},{32,96},{96,0},{1,65},{65,33},{33,97},{97,1},{2,66}... | collective-permute-start | bytes 1572872 | tf_op jit(solution)/shard_map/ppermute | solution.py:35
  24.7 13.9 %collective-permute-start.9 = (bf16[1024,256]{1,0:T(8,128)(2,1)S(1)}, bf16[1024,256]{1,0:T(8,128)(2,1)S(1)}, u32[]{:S(2)}, u32[]{:S(2)}) collective-permute-start(bf16[1024,256]{1,0:T(8,128)(2,1)S(1)} %pad_maximum_fusion.1.refs_1_), channel_id=1, source_target_pairs={{0,96},{64,0},{32,64},{96,32},{1,97},{65,1},{33,65},{97,33},{2,98}... | collective-permute-start | bytes 1572872 | tf_op jit(solution)/shard_map/ppermute | solution.py:35
  26.5 12.0 %collective-permute-start.10 = (bf16[256,256]{1,0:T(8,128)(2,1)S(1)}, bf16[256,256]{1,0:T(8,128)(2,1)S(1)}, u32[]{:S(2)}, u32[]{:S(2)}) collective-permute-start(bf16[256,256]{1,0:T(8,128)(2,1)S(1)} %pad_maximum_fusion.2), channel_id=1, source_target_pairs={{0,32},{32,0},{1,33},{33,1},{2,34},{34,2},{3,35},{35,3},{4,36},{36... | collective-permute-start | bytes 393224 | tf_op jit(solution)/shard_map/ppermute | solution.py:43
  27.7 2.8 %copy-start = (bf16[48,128,2,256]{3,2,1,0:T(2,128)(2,1)S(1)}, bf16[48,128,2,256]{3,2,1,0:T(2,128)(2,1)}, u32[]{:S(2)}) copy-start(bf16[48,128,2,256]{3,2,1,0:T(2,128)(2,1)} %kv_ref.1) | copy-start | bytes 18874372
  30.5 19.7 %slice-start.1 = ((s8[8388608]{0:T(1024)(128)(4,1)}), s8[4194304]{0:T(1024)(128)(4,1)S(1)}, s32[]{:S(2)}) async-start(s8[8388608]{0:T(1024)(128)(4,1)} %bitcast.26), calls=%async_computation.1 | async-start | bytes 8388608
  38.9 25.8 %collective-permute-start.13 = (bf16[6144,256]{1,0:T(8,128)(2,1)S(1)}, bf16[6144,256]{1,0:T(8,128)(2,1)S(1)}, u32[]{:S(2)}, u32[]{:S(2)}) collective-permute-start(bf16[6144,256]{1,0:T(8,128)(2,1)S(1)} %constant_dynamic-update-slice_fusion.9), channel_id=1, source_target_pairs={{0,4},{4,0},{1,5},{5,1},{2,6},{6,2},{3,7},{7,3},{8,12},{12,8},{9,1... | collective-permute-start | bytes 9437192 | tf_op jit(solution)/shard_map/ppermute | solution.py:55
  44.5 5.7 %collective-permute-start.15 = (bf16[512,256]{1,0:T(8,128)(2,1)S(1)}, bf16[512,256]{1,0:T(8,128)(2,1)S(1)}, u32[]{:S(2)}, u32[]{:S(2)}) collective-permute-start(bf16[512,256]{1,0:T(8,128)(2,1)S(1)} %constant_dynamic-update-slice_fusion.4.own_ref), channel_id=1, source_target_pairs={{0,4},{4,0},{1,5},{5,1},{2,6},{6,2},{3,7},{7,3},{8,12},{12,8},{9,1... | collective-permute-start | bytes 786440 | tf_op jit(solution)/shard_map/ppermute | solution.py:55
  44.6 20.0 %collective-permute-start.11 = (bf16[1024,256]{1,0:T(8,128)(2,1)S(1)}, bf16[1024,256]{1,0:T(8,128)(2,1)S(1)}, u32[]{:S(2)}, u32[]{:S(2)}) collective-permute-start(bf16[1024,256]{1,0:T(8,128)(2,1)S(1)} %constant_dynamic-update-slice_fusion.refs_0_), channel_id=1, source_target_pairs={{0,16},{8,24},{16,0},{24,8},{1,17},{9,25},{17,1},{25,9},{2,18},{10... | collective-permute-start | bytes 1572872 | tf_op jit(solution)/shard_map/ppermute | solution.py:39
  46.2 18.5 %collective-permute-start.12 = (bf16[1024,256]{1,0:T(8,128)(2,1)S(1)}, bf16[1024,256]{1,0:T(8,128)(2,1)S(1)}, u32[]{:S(2)}, u32[]{:S(2)}) collective-permute-start(bf16[1024,256]{1,0:T(8,128)(2,1)S(1)} %pad_maximum_fusion.1.refs_1_), channel_id=1, source_target_pairs={{0,32},{64,96},{32,0},{96,64},{1,33},{65,97},{33,1},{97,65},{2,34}... | collective-permute-start | bytes 1572872 | tf_op jit(solution)/shard_map/ppermute | solution.py:35
  51.5 3.5 %collective-permute-start.16 = (f32[32,128]{1,0:T(8,128)S(1)}, f32[32,128]{1,0:T(8,128)S(1)}, u32[]{:S(2)}, u32[]{:S(2)}) collective-permute-start(f32[32,128]{1,0:T(8,128)S(1)} %low_rank.1), channel_id=1, source_target_pairs={{0,1},{1,0},{2,3},{3,2},{4,5},{5,4},{6,7},{7,6},{8,9},{9,8},{10,11... | collective-permute-start | bytes 49160 | tf_op jit(solution)/shard_map/ppermute | solution.py:51
  53.3 11.4 %collective-permute-start.14 = (bf16[48,2048]{1,0:T(8,128)(2,1)S(1)}, bf16[48,2048]{1,0:T(8,128)(2,1)S(1)}, u32[]{:S(2)}, u32[]{:S(2)}) collective-permute-start(bf16[48,2048]{1,0:T(8,128)(2,1)S(1)} %bitcast.39), channel_id=1, source_target_pairs={{0,32},{32,0},{1,33},{33,1},{2,34},{34,2},{3,35},{35,3},{4,36},{36... | collective-permute-start | bytes 589832 | tf_op jit(solution)/shard_map/ppermute | solution.py:43
  55.1 4.9 %collective-permute-start.17 = (f32[64,128]{1,0:T(8,128)S(1)}, f32[64,128]{1,0:T(8,128)S(1)}, u32[]{:S(2)}, u32[]{:S(2)}) collective-permute-start(f32[64,128]{1,0:T(8,128)S(1)} %pad_maximum_fusion.4), channel_id=1, source_target_pairs={{0,2},{1,3},{2,0},{3,1},{4,6},{5,7},{6,4},{7,5},{8,10},{9,11},{10,... | collective-permute-start | bytes 98312 | tf_op jit(solution)/shard_map/ppermute | solution.py:51
  64.7 9.9 %collective-permute-start.18 = (bf16[1024,256]{1,0:T(8,128)(2,1)S(1)}, bf16[1024,256]{1,0:T(8,128)(2,1)S(1)}, u32[]{:S(2)}, u32[]{:S(2)}) collective-permute-start(bf16[1024,256]{1,0:T(8,128)(2,1)S(1)} %collective-permute-done.11.refs_6_), channel_id=1, source_target_pairs={{0,4},{4,0},{1,5},{5,1},{2,6},{6,2},{3,7},{7,3},{8,12},{12,8},{9,1... | collective-permute-start | bytes 1572872 | tf_op jit(solution)/shard_map/ppermute | solution.py:55
  66.3 8.2 %collective-permute-start.19 = (bf16[1024,256]{1,0:T(8,128)(2,1)S(1)}, bf16[1024,256]{1,0:T(8,128)(2,1)S(1)}, u32[]{:S(2)}, u32[]{:S(2)}) collective-permute-start(bf16[1024,256]{1,0:T(8,128)(2,1)S(1)} %collective-permute-done.12.refs_7_), channel_id=1, source_target_pairs={{0,4},{4,0},{1,5},{5,1},{2,6},{6,2},{3,7},{7,3},{8,12},{12,8},{9,1... | collective-permute-start | bytes 1572872 | tf_op jit(solution)/shard_map/ppermute | solution.py:55
  66.5 14.2 %collective-permute-start.22 = (bf16[96,2048]{1,0:T(8,128)(2,1)S(1)}, bf16[96,2048]{1,0:T(8,128)(2,1)S(1)}, u32[]{:S(2)}, u32[]{:S(2)}) collective-permute-start(bf16[96,2048]{1,0:T(8,128)(2,1)S(1)} %constant_dynamic-update-slice_fusion.15), channel_id=1, source_target_pairs={{0,8},{8,16},{16,24},{24,0},{1,9},{9,17},{17,25},{25,1},{2,10},{10... | collective-permute-start | bytes 1179656 | tf_op jit(solution)/shard_map/ppermute | solution.py:39
  67.0 18.7 %collective-permute-start.23 = (bf16[96,2048]{1,0:T(8,128)(2,1)S(1)}, bf16[96,2048]{1,0:T(8,128)(2,1)S(1)}, u32[]{:S(2)}, u32[]{:S(2)}) collective-permute-start(bf16[96,2048]{1,0:T(8,128)(2,1)S(1)} %constant_dynamic-update-slice_fusion.15), channel_id=1, source_target_pairs={{0,16},{8,24},{16,0},{24,8},{1,17},{9,25},{17,1},{25,9},{2,18},{10... | collective-permute-start | bytes 1179656 | tf_op jit(solution)/shard_map/ppermute | solution.py:39
  68.4 18.4 %collective-permute-start.24 = (bf16[96,2048]{1,0:T(8,128)(2,1)S(1)}, bf16[96,2048]{1,0:T(8,128)(2,1)S(1)}, u32[]{:S(2)}, u32[]{:S(2)}) collective-permute-start(bf16[96,2048]{1,0:T(8,128)(2,1)S(1)} %constant_dynamic-update-slice_fusion.15), channel_id=1, source_target_pairs={{0,24},{8,0},{16,8},{24,16},{1,25},{9,1},{17,9},{25,17},{2,26},{10... | collective-permute-start | bytes 1179656 | tf_op jit(solution)/shard_map/ppermute | solution.py:39
  75.9 20.1 %copy-start.10 = (s32[768]{0:T(1024)S(1)}, s32[768]{0:T(1024)}, u32[]{:S(2)}) copy-start(s32[768]{0:T(1024)} %param.24) | copy-start | bytes 9220
  75.9 20.3 %copy-start.1 = (bf16[2048,512]{1,0:T(8,128)(2,1)S(1)}, bf16[2048,512]{1,0:T(8,128)(2,1)}, u32[]{:S(2)}) copy-start(bf16[2048,512]{1,0:T(8,128)(2,1)} %w_ref.3) | copy-start | bytes 6291460
  75.9 20.3 %copy-start.2 = (bf16[2048,8,16]{0,2,1:T(8,128)(2,1)S(1)}, bf16[2048,8,16]{0,2,1:T(8,128)(2,1)}, u32[]{:S(2)}) copy-start(bf16[2048,8,16]{0,2,1:T(8,128)(2,1)} %param.26) | copy-start | bytes 1572868
  75.9 20.3 %copy-start.6 = (bf16[8,16,512]{2,1,0:T(8,128)(2,1)S(1)}, bf16[8,16,512]{2,1,0:T(8,128)(2,1)}, u32[]{:S(2)}) copy-start(bf16[8,16,512]{2,1,0:T(8,128)(2,1)} %param.27) | copy-start | bytes 393220
  78.6 9.4 %collective-permute-start.20 = (bf16[3,128,2,256]{3,2,1,0:T(2,128)(2,1)S(1)}, bf16[3,128,2,256]{3,2,1,0:T(2,128)(2,1)S(1)}, u32[]{:S(2)}, u32[]{:S(2)}) collective-permute-start(bf16[3,128,2,256]{3,2,1,0:T(2,128)(2,1)S(1)} %get-tuple-element.79), channel_id=1, source_target_pairs={{0,64},{64,0},{1,65},{65,1},{2,66},{66,2},{3,67},{67,3},{4,68},{68... | collective-permute-start | bytes 1179656 | tf_op jit(solution)/shard_map/ppermute | solution.py:462
  79.2 10.3 %collective-permute-start.21 = (bf16[3,128,2,256]{3,2,1,0:T(2,128)(2,1)S(1)}, bf16[3,128,2,256]{3,2,1,0:T(2,128)(2,1)S(1)}, u32[]{:S(2)}, u32[]{:S(2)}) collective-permute-start(bf16[3,128,2,256]{3,2,1,0:T(2,128)(2,1)S(1)} %get-tuple-element.80), channel_id=1, source_target_pairs={{0,96},{32,64},{64,32},{96,0},{1,97},{33,65},{65,33},{97,1},{2,98}... | collective-permute-start | bytes 1179656 | tf_op jit(solution)/shard_map/ppermute | solution.py:463
  89.6 6.6 %collective-permute-start.27 = (bf16[384,2048]{1,0:T(8,128)(2,1)S(1)}, bf16[384,2048]{1,0:T(8,128)(2,1)S(1)}, u32[]{:S(2)}, u32[]{:S(2)}) collective-permute-start(bf16[384,2048]{1,0:T(8,128)(2,1)S(1)} %constant_dynamic-update-slice_fusion.17.refs_0_), channel_id=1, source_target_pairs={{0,4},{4,0},{1,5},{5,1},{2,6},{6,2},{3,7},{7,3},{8,12},{12,8},{9,1... | collective-permute-start | bytes 4718600 | tf_op jit(solution)/shard_map/ppermute | solution.py:55
  93.2 22.6 %collective-permute-start.25 = (bf16[2,3,128,2,256]{4,3,2,1,0:T(2,128)(2,1)S(1)}, bf16[2,3,128,2,256]{4,3,2,1,0:T(2,128)(2,1)S(1)}, u32[]{:S(2)}, u32[]{:S(2)}) collective-permute-start(bf16[2,3,128,2,256]{4,3,2,1,0:T(2,128)(2,1)S(1)} %pad_maximum_fusion.refs_0_), channel_id=1, source_target_pairs={{0,8},{8,16},{16,24},{24,0},{1,9},{9,17},{17,25},{25,1},{2,10},{10... | collective-permute-start | bytes 2359304 | tf_op jit(solution)/shard_map/ppermute | solution.py:39
  93.3 22.5 %collective-permute-start.26 = (bf16[2,3,128,2,256]{4,3,2,1,0:T(2,128)(2,1)S(1)}, bf16[2,3,128,2,256]{4,3,2,1,0:T(2,128)(2,1)S(1)}, u32[]{:S(2)}, u32[]{:S(2)}) collective-permute-start(bf16[2,3,128,2,256]{4,3,2,1,0:T(2,128)(2,1)S(1)} %pad_maximum_fusion.refs_0_), channel_id=1, source_target_pairs={{0,24},{8,0},{16,8},{24,16},{1,25},{9,1},{17,9},{25,17},{2,26},{10... | collective-permute-start | bytes 2359304 | tf_op jit(solution)/shard_map/ppermute | solution.py:39
  101.3 8.7 %collective-permute-start.28 = (bf16[192,512]{1,0:T(8,128)(2,1)S(1)}, bf16[192,512]{1,0:T(8,128)(2,1)S(1)}, u32[]{:S(2)}, u32[]{:S(2)}) collective-permute-start(bf16[192,512]{1,0:T(8,128)(2,1)S(1)} %get-tuple-element.90), channel_id=1, source_target_pairs={{0,1},{1,2},{2,3},{3,0},{4,5},{5,6},{6,7},{7,4},{8,9},{9,10},{10,1... | collective-permute-start | bytes 589832 | tf_op jit(solution)/shard_map/ppermute | solution.py:47
  103.1 11.9 %collective-permute-start.29 = (bf16[192,512]{1,0:T(8,128)(2,1)S(1)}, bf16[192,512]{1,0:T(8,128)(2,1)S(1)}, u32[]{:S(2)}, u32[]{:S(2)}) collective-permute-start(bf16[192,512]{1,0:T(8,128)(2,1)S(1)} %get-tuple-element.91), channel_id=1, source_target_pairs={{0,2},{1,3},{2,0},{3,1},{4,6},{5,7},{6,4},{7,5},{8,10},{9,11},{10,... | collective-permute-start | bytes 589832 | tf_op jit(solution)/shard_map/ppermute | solution.py:47
  106.4 8.6 %collective-permute-start.30 = (bf16[192,512]{1,0:T(8,128)(2,1)S(1)}, bf16[192,512]{1,0:T(8,128)(2,1)S(1)}, u32[]{:S(2)}, u32[]{:S(2)}) collective-permute-start(bf16[192,512]{1,0:T(8,128)(2,1)S(1)} %get-tuple-element.92), channel_id=1, source_target_pairs={{0,3},{1,0},{2,1},{3,2},{4,7},{5,4},{6,5},{7,6},{8,11},{9,8},{10,9... | collective-permute-start | bytes 589832 | tf_op jit(solution)/shard_map/ppermute | solution.py:47
  115.9 14.5 %collective-permute-start.33 = (bf16[2,3,128,2,256]{4,3,2,1,0:T(2,128)(2,1)S(1)}, bf16[2,3,128,2,256]{4,3,2,1,0:T(2,128)(2,1)S(1)}, u32[]{:S(2)}, u32[]{:S(2)}) collective-permute-start(bf16[2,3,128,2,256]{4,3,2,1,0:T(2,128)(2,1)S(1)} %pad_maximum_fusion.refs_0_), channel_id=1, source_target_pairs={{0,4},{4,0},{1,5},{5,1},{2,6},{6,2},{3,7},{7,3},{8,12},{12,8},{9,1... | collective-permute-start | bytes 2359304 | tf_op jit(solution)/shard_map/ppermute | solution.py:55
  117.3 13.0 %collective-permute-start.34 = (bf16[2,3,128,2,256]{4,3,2,1,0:T(2,128)(2,1)S(1)}, bf16[2,3,128,2,256]{4,3,2,1,0:T(2,128)(2,1)S(1)}, u32[]{:S(2)}, u32[]{:S(2)}) collective-permute-start(bf16[2,3,128,2,256]{4,3,2,1,0:T(2,128)(2,1)S(1)} %collective-permute-done.25.refs_1_), channel_id=1, source_target_pairs={{0,4},{4,0},{1,5},{5,1},{2,6},{6,2},{3,7},{7,3},{8,12},{12,8},{9,1... | collective-permute-start | bytes 2359304 | tf_op jit(solution)/shard_map/ppermute | solution.py:55
  117.4 13.0 %collective-permute-start.35 = (bf16[2,3,128,2,256]{4,3,2,1,0:T(2,128)(2,1)S(1)}, bf16[2,3,128,2,256]{4,3,2,1,0:T(2,128)(2,1)S(1)}, u32[]{:S(2)}, u32[]{:S(2)}) collective-permute-start(bf16[2,3,128,2,256]{4,3,2,1,0:T(2,128)(2,1)S(1)} %collective-permute-done.26.refs_2_), channel_id=1, source_target_pairs={{0,4},{4,0},{1,5},{5,1},{2,6},{6,2},{3,7},{7,3},{8,12},{12,8},{9,1... | collective-permute-start | bytes 2359304 | tf_op jit(solution)/shard_map/ppermute | solution.py:55
  118.4 12.0 %collective-permute-start.31 = (bf16[3,128,2,256]{3,2,1,0:T(2,128)(2,1)S(1)}, bf16[3,128,2,256]{3,2,1,0:T(2,128)(2,1)S(1)}, u32[]{:S(2)}, u32[]{:S(2)}) collective-permute-start(bf16[3,128,2,256]{3,2,1,0:T(2,128)(2,1)S(1)} %slice_bitcast_fusion.1), channel_id=1, source_target_pairs={{0,8},{8,16},{16,24},{24,0},{1,9},{9,17},{17,25},{25,1},{2,10},{10... | collective-permute-start | bytes 1179656 | tf_op jit(solution)/shard_map/ppermute | solution.py:39
  118.4 11.9 %collective-permute-start.32 = (bf16[3,128,2,256]{3,2,1,0:T(2,128)(2,1)S(1)}, bf16[3,128,2,256]{3,2,1,0:T(2,128)(2,1)S(1)}, u32[]{:S(2)}, u32[]{:S(2)}) collective-permute-start(bf16[3,128,2,256]{3,2,1,0:T(2,128)(2,1)S(1)} %slice_bitcast_fusion), channel_id=1, source_target_pairs={{0,24},{8,0},{16,8},{24,16},{1,25},{9,1},{17,9},{25,17},{2,26},{10... | collective-permute-start | bytes 1179656 | tf_op jit(solution)/shard_map/ppermute | solution.py:39
  130.3 3.9 %collective-permute-start.36 = (bf16[3,128,2,256]{3,2,1,0:T(2,128)(2,1)S(1)}, bf16[3,128,2,256]{3,2,1,0:T(2,128)(2,1)S(1)}, u32[]{:S(2)}, u32[]{:S(2)}) collective-permute-start(bf16[3,128,2,256]{3,2,1,0:T(2,128)(2,1)S(1)} %collective-permute-done.31), channel_id=1, source_target_pairs={{0,4},{4,0},{1,5},{5,1},{2,6},{6,2},{3,7},{7,3},{8,12},{12,8},{9,1... | collective-permute-start | bytes 1179656 | tf_op jit(solution)/shard_map/ppermute | solution.py:55
  131.3 3.0 %collective-permute-start.37 = (bf16[3,128,2,256]{3,2,1,0:T(2,128)(2,1)S(1)}, bf16[3,128,2,256]{3,2,1,0:T(2,128)(2,1)S(1)}, u32[]{:S(2)}, u32[]{:S(2)}) collective-permute-start(bf16[3,128,2,256]{3,2,1,0:T(2,128)(2,1)S(1)} %collective-permute-done.32), channel_id=1, source_target_pairs={{0,4},{4,0},{1,5},{5,1},{2,6},{6,2},{3,7},{7,3},{8,12},{12,8},{9,1... | collective-permute-start | bytes 1179656 | tf_op jit(solution)/shard_map/ppermute | solution.py:55
  (3 other events, 3.3 us)

commit v6 on v5

--- a/solution.py
+++ b/solution.py
@@ -27,12 +27,8 @@
     return pltpu.CompilerParams(vmem_limit_bytes=limit * MIB)
 
 
-def x_shift(value, k):
-    pairs = []
-    for x in range(4):
-        t = (x + k) % 4
-        pairs.append(((x % 2) * 2 + x // 2, (t % 2) * 2 + t // 2))
-    return lax.ppermute(value, ("pool", "xh"), pairs)
+def x_mirror(value):
+    return lax.ppermute(value, ("pool", "xh"), [(i, 3 - i) for i in range(4)])
 
 
 def y_shift(value, k):
@@ -56,9 +52,8 @@
 
 
 def pack_kernel(info, w_ref, d_ref, k_ref, v_ref):
-    half = pl.ds(pl.multiple_of(info[POOL] * 256, 256), 256)
-    k_ref[...] = w_ref[half, 0, :]
-    v_ref[0:256] = w_ref[half, 1, :]
+    k_ref[...] = w_ref[:, 0, :]
+    v_ref[0:512] = w_ref[:, 1, :]
     column = lax.broadcasted_iota(jnp.int32, (256, 128), 0)
     lane = lax.broadcasted_iota(jnp.int32, (256, 128), 1)
     pick = (column == info[ADAPTER + info[HEAD]] * 32 + lane) & (lane < 32)
@@ -68,8 +63,8 @@
         (((0,), (1,)), ((), ())),
         preferred_element_type=jnp.float32,
     ).astype(jnp.bfloat16)
-    v_ref[256:288] = low[0:32, 0:256]
-    v_ref[288:320] = low[0:32, 256:512]
+    v_ref[512:544] = low[0:32, 0:256]
+    v_ref[544:576] = low[0:32, 256:512]
 
 
 def pack(info, weight, down):
@@ -78,8 +73,8 @@
         in_specs=[SMEM, VMEM, VMEM],
         out_specs=[VMEM, VMEM],
         out_shape=[
-            jax.ShapeDtypeStruct((256, 256), jnp.bfloat16),
-            jax.ShapeDtypeStruct((320, 256), jnp.bfloat16),
+            jax.ShapeDtypeStruct((512, 256), jnp.bfloat16),
+            jax.ShapeDtypeStruct((576, 256), jnp.bfloat16),
         ],
         compiler_params=params(),
         name="pack",
@@ -158,10 +153,6 @@
     return [x, (x + 3) & 3, (x + 2) & 3, (x + 1) & 3]
 
 
-def chunk_start(xi, yi, core):
-    return pl.multiple_of(((xi >> 1) * 8 + yi * 2 + core) * 512 + (xi & 1) * 256, 256)
-
-
 def low_kernel(info, prompt, own_ref, other_ref, out_ref):
     xh, y, core = info[XH], info[Y], info[CORE]
     rows = pl.ds(pl.multiple_of(info[HEAD] * 128, 128), 128)
@@ -195,48 +186,65 @@
     )(info, tokens, own, other)
 
 
-def main_kernel(kinds, fresh, info, prompt, *refs):
-    n = max(kind[3] for kind in kinds) + 1
-    blocks, sums, outs = refs[:n], refs[n:-2], refs[-2:]
-    pool, xh, y, core = info[POOL], info[XH], info[Y], info[CORE]
-    x = 2 * xh + pool
-    done = [fresh, fresh]
-    for kv, j, partner, which, block in kinds:
+def add_products(pieces, fresh, info, prompt, blocks, outs):
+    xh, y, core = info[XH], info[Y], info[CORE]
+    fresh = [fresh, fresh]
+    for kv, partner, which, row, shards in pieces:
         c_of = 1 - core if partner else core
         tokens = []
-        for i in range(4):
-            xi = x_order(x)[i if kv == 0 else j]
-            yi = x_order(y)[j if kv == 0 else i]
-            tokens.append(prompt[:, pl.ds(chunk_start(xi, yi, c_of), 256)])
+        for other, j in shards:
+            side = 1 - xh if other else xh
+            at = pl.multiple_of((side * 8 + x_order(y)[j] * 2 + c_of) * 512, 512)
+            tokens.append(prompt[:, pl.ds(at, 512)])
         part = jnp.dot(
             jnp.concatenate(tokens, 1),
-            blocks[which][block * 1024 : (block + 1) * 1024],
+            blocks[which][row : row + 512 * len(shards)],
             preferred_element_type=jnp.float32,
         )
-        if done[kv] is True:
+        if fresh[kv]:
             outs[kv][...] = part
-        elif done[kv] is False:
-            outs[kv][...] = sums[kv][...] + part
         else:
             outs[kv][...] += part
-        done[kv] = None
-
-
-def main_product(info, tokens, kinds, blocks, sums=()):
+        fresh[kv] = False
+
+
+def key_piece(partner, which, row, j):
+    return (0, partner, which, row, ((0, j), (1, j)))
+
+
+def value_pieces(partner, which, row, other):
+    return tuple(
+        (1, partner, which, row + 1024 * n, ((other, 2 * n), (other, 2 * n + 1))) for n in range(2)
+    )
+
+
+def main_kernel(pieces, info, prompt, *refs):
+    add_products(pieces, True, info, prompt, refs[:-2], refs[-2:])
+
+
+def main_product(info, tokens, pieces, blocks):
     shape = jax.ShapeDtypeStruct((tokens.shape[0], 256), jnp.float32)
     return pl.pallas_call(
-        functools.partial(main_kernel, kinds, not sums),
-        in_specs=[SMEM] + [VMEM] * (1 + len(blocks) + len(sums)),
+        functools.partial(main_kernel, pieces),
+        in_specs=[SMEM] + [VMEM] * (1 + len(blocks)),
         out_specs=[VMEM, VMEM],
         out_shape=[shape, shape],
         compiler_params=params(),
         name="main_product",
-    )(info, tokens, *blocks, *sums)
-
-
-def finish_kernel(info, *refs):
-    lows, k_ref, v_ref, up_ref, near_ref, far_ref = refs
+    )(info, tokens, *blocks)
+
+
+def finish_kernel(pieces, n_sums, info, prompt, *refs):
+    n = len(refs) - 6 - 2 * n_sums
+    blocks, sums = refs[:n], refs[n : n + 2 * n_sums]
+    lows, up_ref, near_ref, far_ref, k_ref, v_ref = refs[n + 2 * n_sums :]
     pool, xh, z = info[POOL], info[XH], info[HEAD]
+    for kv, ref in enumerate((k_ref, v_ref)):
+        total = sums[kv][...]
+        for m in range(1, n_sums):
+            total = total + sums[2 * m + kv][...]
+        ref[...] = total
+    add_products(pieces, False, info, prompt, blocks, (k_ref, v_ref))
     owners = [info[DEST + pool * REQ_POOL + r] for r in range(REQ_POOL)]
     dims = (((0,), (0,)), ((), ()))
     for n in range(REQ_POOL):
@@ -263,16 +271,19 @@
             far_ref[slot] = result
 
 
-def finish(info, lows, sums, up):
+def finish(info, tokens, pieces, blocks, sums, lows, up):
     shape = jax.ShapeDtypeStruct((X_SLOTS, 128, 2, 256), jnp.bfloat16)
-    return pl.pallas_call(
-        finish_kernel,
-        in_specs=[SMEM] + [VMEM] * 4,
+    total = pltpu.VMEM((tokens.shape[0], 256), jnp.float32)
+    flat = [v for pair in sums for v in pair]
+    return pl.pallas_call(
+        functools.partial(finish_kernel, pieces, len(sums)),
+        in_specs=[SMEM] + [VMEM] * (3 + len(blocks) + len(flat)),
         out_specs=[VMEM, VMEM],
         out_shape=[shape, shape],
+        scratch_shapes=[total, total],
         compiler_params=params(),
         name="finish",
-    )(info, lows, *sums, up)
+    )(info, tokens, *blocks, *flat, lows, up)
 
 
 def slots_of(info, pool, xh, owner):
@@ -422,45 +433,49 @@
     query = rotated_query.reshape(rows, heads, HEAD_DIM)
 
     keys, values = pack(info, key_value_weight, adapter_down_weight)
-    kx1, kx2, kx3 = x_shift(keys, 1), x_shift(keys, 2), x_shift(keys, -1)
-    vy1, vy3 = y_shift(values, 1), y_shift(values, -1)
-    keys, kx1, kx2, kx3, values, vy1, vy3 = barrier((keys, kx1, kx2, kx3, values, vy1, vy3))
-    vy2 = y_shift(values, 2)
-    key0 = jnp.concatenate([keys, kx1, kx2, kx3], 0)
+    keys_across = x_mirror(keys)
+    ring_values = ring(values, y_shift)
+    keys, keys_across, ring_values, cached_length = barrier(
+        (keys, keys_across, ring_values, cached_length)
+    )
+    key0 = jnp.concatenate([keys, keys_across], 0)
+    value0 = jnp.concatenate([v[:512] for v in ring_values], 0)
+    down0 = jnp.concatenate([v[512:] for v in ring_values], 0)
     key1, key3 = y_shift(key0, 1), y_shift(key0, -1)
-    vy2, cached_length = barrier((vy2, cached_length))
-    both = [values, vy1, vy2, vy3]
-    value0 = jnp.concatenate([v[:256] for v in both], 0)
-    value1, value3 = x_shift(value0, 1), x_shift(value0, -1)
-    down0 = jnp.concatenate([v[256:] for v in both], 0)
+    value1 = xh_swap(value0)
     down_own = jnp.concatenate([down0, xh_swap(down0)], 0)
     attended = attend(query, key_value_cache, current_key_value, cached_length, 0, 1)
     attended = attended.reshape(rows, heads * HEAD_DIM)
-    key0, value0, key1, key3, value1, value3, down_own, attended = barrier(
-        (key0, value0, key1, key3, value1, value3, down_own, attended)
-    )
-    first = [key0, value0, key1, key3, value1, value3]
-    key2, value2 = y_shift(key0, 2), x_shift(value0, 2)
-    theirs = core_swap(jnp.concatenate(first, 0))
+    down_own, attended = barrier((down_own, attended))
+    low = low_rank(info, tokens, down_own, core_swap(down_own))
+    pieces = (key_piece(0, 0, 0, 0),) + value_pieces(0, 1, 0, 0)
+    first = main_product(info, tokens, pieces, [key0, value0])
+    own = core_swap(jnp.concatenate([key0, value0], 0))
+    pieces = (key_piece(1, 0, 0, 0),) + value_pieces(1, 0, 1024, 0)
+    second = main_product(info, tokens, pieces, [own])
+    key0, key1, key3, low, attended, first, second = barrier(
+        (key0, key1, key3, low, attended, first, second)
+    )
+    key2 = y_shift(key0, 2)
     across = xh_swap(attended)
-    low = low_rank(info, tokens, down_own, core_swap(down_own))
     pair = jnp.concatenate([low, z_flip(low, 1)], 0)
     lows = jnp.concatenate([pair, z_flip(pair, 2)], 0)
-    key2, value2, theirs, across, lows, attended = barrier(
-        (key2, value2, theirs, across, lows, attended)
+    key1, key2, key3, value1, across, attended, lows = barrier(
+        (key1, key2, key3, value1, across, attended, lows)
     )
     mine = ring(jnp.concatenate([attended, across], 0), y_shift)
-    last = [core_swap(key2), core_swap(value2)]
-    order = ((0, 0), (1, 0), (0, 1), (0, 3), (1, 1), (1, 3))
-    kinds = tuple((kv, j, 0, n, 0) for n, (kv, j) in enumerate(order))
-    kinds += ((0, 2, 0, 6, 0), (1, 2, 0, 7, 0))
-    kinds += tuple((kv, j, 1, 8, n) for n, (kv, j) in enumerate(order))
-    sums = main_product(info, tokens, kinds, first + [key2, value2, theirs])
-    sums = main_product(info, tokens, ((0, 2, 1, 0, 0), (1, 2, 1, 1, 0)), last, tuple(sums))
-    same, other = finish(info, lows, sums, adapter_up_weight)
+    theirs_k = core_swap(jnp.concatenate([key1, key2, key3], 0))
+    theirs_v = core_swap(value1)
+    pieces = tuple(key_piece(0, n, 0, n + 1) for n in range(3)) + value_pieces(0, 3, 0, 1)
+    third = main_product(info, tokens, pieces, [key1, key2, key3, value1])
+    pieces = tuple(key_piece(1, 0, 1024 * n, n + 1) for n in range(3)) + value_pieces(1, 1, 0, 1)
+    sums = [first, second, third]
+    same, other = finish(
+        info, tokens, pieces, [theirs_k, theirs_v], sums, lows, adapter_up_weight
+    )
 
     b0 = lax.ppermute(same, "pool", [(0, 1), (1, 0)])
-    a0 = lax.ppermute(other, ("pool", "xh"), [(i, 3 - i) for i in range(4)])
+    a0 = x_mirror(other)
     b0, a0, mine = barrier((b0, a0, mine))
     mine = jnp.concatenate(mine, 0)
     partner = core_swap(mine)

time: 136 us -> 148 us (1.088)
  waiting for transfers between devices: 40.4 us -> 68.1 us
  starting transfers between devices: 56.7 us -> 42.6 us
  local copies, waits for them, and re-layouts: 6.83 us -> 3.97 us
  Pallas kernels: 28.1 us -> 29.8 us
    ppermute x13, waiting for transfers between devices: 17 us -> 35.4 us  [y_shift(): return lax.ppermute(value, 'y', [(i, (i + k) % 4) for i in range(4)])]
    ppermute x2 -> x3, waiting for transfers between devices: 4.69 us -> 17.8 us  [xh_swap(): return lax.ppermute(value, 'xh', [(0, 1), (1, 0)])]
    ppermute x7 -> x2, starting transfers between devices: 11 us -> 4.29 us  [x_mirror(): return lax.ppermute(value, ('pool', 'xh'), [(i, 3 - i) for i in range(4)])]
    ppermute x10, starting transfers between devices: 13 us -> 6.91 us  [core_swap(): return lax.ppermute(value, 'core', [(0, 1), (1, 0)])]
    ppermute x13, starting transfers between devices: 18.3 us -> 13.6 us  [y_shift(): return lax.ppermute(value, 'y', [(i, (i + k) % 4) for i in range(4)])]
    ppermute x2 -> x3, starting transfers between devices: 2.95 us -> 5.88 us  [xh_swap(): return lax.ppermute(value, 'xh', [(0, 1), (1, 0)])]
    unnamed x40 -> x37, local copies, waits for them, and re-layouts: 5.22 us -> 2.41 us
    ppermute x10, waiting for transfers between devices: 2.17 us -> 0.04 us  [core_swap(): return lax.ppermute(value, 'core', [(0, 1), (1, 0)])]
  transfers between devices with their start and end apart: 38 -> 34, of which waited for: 14 -> 12; matrix products, arithmetic and copies ran while one was open for 2% -> 2% of each run, Pallas kernels for 19% -> 18%
where the time goes in v6:
time: 148 us
  waiting for transfers between devices  68.1 us (46%)
  starting transfers between devices  42.6 us (29%)
  Pallas kernels  29.8 us (20%)
  local copies, waits for them, and re-layouts  3.97 us (3%)
  other arithmetic  2.08 us (1%)
    ppermute x13, waiting for transfers between devices, y_shift(): return lax.ppermute(value, 'y', [(i, (i + k) % 4) for i in range(4)])  35.4 us
    ppermute x3, waiting for transfers between devices, xh_swap(): return lax.ppermute(value, 'xh', [(0, 1), (1, 0)])  17.8 us
    ppermute x13, starting transfers between devices, y_shift(): return lax.ppermute(value, 'y', [(i, (i + k) % 4) for i in range(4)])  13.6 us
    ppermute x3, waiting for transfers between devices, z_shift(): return lax.ppermute(value, 'head', [(i, (i + k) % 4) for i in range(4)])  8.21 us
    pallas_call x1, Pallas kernels, attend(): pl.pallas_call(functools.partial(attend_kernel, first * ROWS_STEP), grid_...  8.01 us
    ppermute x10, starting transfers between devices, core_swap(): return lax.ppermute(value, 'core', [(0, 1), (1, 0)])  6.91 us
    ppermute x3, starting transfers between devices, xh_swap(): return lax.ppermute(value, 'xh', [(0, 1), (1, 0)])  5.88 us
    ppermute x3, starting transfers between devices, z_shift(): return lax.ppermute(value, 'head', [(i, (i + k) % 4) for i in range(4)])  5.75 us
  transfers between devices with their start and end apart: 34, of which 12 were waited for; matrix products, arithmetic and copies ran while one was open for 2% of the time, Pallas kernels for 18%

profile of v6, /device:TPU:1, one launch (start us, length us, event | category | flops | bytes accessed | tf_op | source)
XLA Modules:
  0.0 147.8 jit_solution(2134416731043716927)
XLA Ops:
  0.6 0.8 concatenate.36.info
  1.4 1.0 copy-done.3
  2.4 0.9 copy-done.4
  3.4 2.3 %pack.1 = (bf16[512,256]{1,0:T(8,128)(2,1)S(1)}, bf16[576,256]{1,0:T(8,128)(2,1)S(1)}) custom-call(s32[17]{0:T(128)S(1)} %concatenate.36.info, bf16[512,2,256]{2,1,0:T(2,128)(2,1)S(1)} %copy-done.3, bf16[512,256]{1,0:T(8,128)(2,1)S(1)} %copy-done.4), custom_call_target="tpu_custom_call" | custom-call | tf_op jit(solution)/shard_map/pack/pallas_call | solution.py:71
  5.7 3.6 %collective-permute-start.3 = (bf16[576,256]{1,0:T(8,128)(2,1)S(1)}, bf16[576,256]{1,0:T(8,128)(2,1)S(1)}, u32[]{:S(2)}, u32[]{:S(2)}) collective-permute-start(bf16[576,256]{1,0:T(8,128)(2,1)S(1)} %get-tuple-element.60), channel_id=1, source_target_pairs={{0,24},{8,0},{16,8},{24,16},{1,25},{9,1},{17,9},{25,17},{2,26},{10... | collective-permute-start | bytes 884744 | tf_op jit(solution)/shard_map/ppermute | solution.py:35
  10.3 2.5 %collective-permute-start = (bf16[512,256]{1,0:T(8,128)(2,1)S(1)}, bf16[512,256]{1,0:T(8,128)(2,1)S(1)}, u32[]{:S(2)}, u32[]{:S(2)}) collective-permute-start(bf16[512,256]{1,0:T(8,128)(2,1)S(1)} %get-tuple-element.58), channel_id=1, source_target_pairs={{0,96},{32,64},{64,32},{96,0},{1,97},{33,65},{65,33},{97,1},{2,98}... | collective-permute-start | bytes 786440 | tf_op jit(solution)/shard_map/ppermute | solution.py:31
  12.8 5.0 %collective-permute-done = bf16[512,256]{1,0:T(8,128)(2,1)S(1)} collective-permute-done((bf16[512,256]{1,0:T(8,128)(2,1)S(1)}, bf16[512,256]{1,0:T(8,128)(2,1)S(1)}, u32[]{:S(2)}, u32[]{:S(2)}) %collective-permute-start) | collective-permute-done | bytes 262176 | tf_op jit(solution)/shard_map/ppermute | solution.py:31
  17.8 3.3 %collective-permute-done.3 = bf16[576,256]{1,0:T(8,128)(2,1)S(1)} collective-permute-done((bf16[576,256]{1,0:T(8,128)(2,1)S(1)}, bf16[576,256]{1,0:T(8,128)(2,1)S(1)}, u32[]{:S(2)}, u32[]{:S(2)}) %collective-permute-start.3) | collective-permute-done | bytes 294944 | tf_op jit(solution)/shard_map/ppermute | solution.py:35
  21.2 4.9 %collective-permute-done.1 = bf16[576,256]{1,0:T(8,128)(2,1)S(1)} collective-permute-done((bf16[576,256]{1,0:T(8,128)(2,1)S(1)}, bf16[576,256]{1,0:T(8,128)(2,1)S(1)}, u32[]{:S(2)}, u32[]{:S(2)}) %collective-permute-start.1) | collective-permute-done | bytes 294944 | tf_op jit(solution)/shard_map/ppermute | solution.py:35
  26.2 1.5 collective-permute-start.4
  27.8 1.1 collective-permute-start.8
  29.0 2.8 %collective-permute-start.10 = (bf16[2048,256]{1,0:T(8,128)(2,1)S(1)}, bf16[2048,256]{1,0:T(8,128)(2,1)S(1)}, u32[]{:S(2)}, u32[]{:S(2)}) collective-permute-start(bf16[2048,256]{1,0:T(8,128)(2,1)S(1)} %pad_maximum_fusion.1.refs_1_), channel_id=1, source_target_pairs={{0,32},{32,0},{1,33},{33,1},{2,34},{34,2},{3,35},{35,3},{4,36},{36... | collective-permute-start | bytes 3145736 | tf_op jit(solution)/shard_map/ppermute | solution.py:39
  32.3 8.0 %attend.1 = bf16[48,16,128]{2,1,0:T(8,128)(2,1)S(1)} custom-call(s32[48]{0:T(128)S(1)} %copy-done.8, bf16[48,16,128]{2,1,0:T(8,128)(2,1)S(1)} %bitcast.34, bf16[48,128,2,256]{3,2,1,0:T(2,128)(2,1)S(1)} %copy-done, bf16[48,2,256]{2,1,0:T(2,128)(2,1)S(1)} %copy-done.7), custom_call_target="tpu_custom_call" | custom-call | tf_op jit(solution)/shard_map/attend/pallas_call | solution.py:126
  40.4 17.8 %collective-permute-done.6 = bf16[256,256]{1,0:T(8,128)(2,1)S(1)} collective-permute-done((bf16[256,256]{1,0:T(8,128)(2,1)S(1)}, bf16[256,256]{1,0:T(8,128)(2,1)S(1)}, u32[]{:S(2)}, u32[]{:S(2)}) %collective-permute-start.6) | collective-permute-done | bytes 131104 | tf_op jit(solution)/shard_map/ppermute | solution.py:39
  58.2 0.9 collective-permute-start.7
  59.1 1.5 %main_product.3 = (f32[512,256]{1,0:T(8,128)S(1)}, f32[512,256]{1,0:T(8,128)S(1)}) custom-call(s32[17]{0:T(128)S(1)} %concatenate.36.info, bf16[512,8192]{1,0:T(8,128)(2,1)S(1)} %bitcast.28, bf16[1024,256]{1,0:T(8,128)(2,1)S(1)} %get-tuple-element.72.refs_0_, bf16[2048,256]{1,0:T(8,128)(2,1)S(1)} %pad_maximum_fusion.1.refs_1_), custom_call_target="tpu_custom_call" | custom-call | tf_op jit(solution)/shard_map/main_product/pallas_call | solution.py:227
  60.7 1.3 low_rank.1
  62.0 1.5 %main_product.4 = (f32[512,256]{1,0:T(8,128)S(1)}, f32[512,256]{1,0:T(8,128)S(1)}) custom-call(s32[17]{0:T(128)S(1)} %concatenate.36.info, bf16[512,8192]{1,0:T(8,128)(2,1)S(1)} %bitcast.30, bf16[3072,256]{1,0:T(8,128)(2,1)S(1)} %collective-permute-done.8.refs_0_), custom_call_target="tpu_custom_call" | custom-call | tf_op jit(solution)/shard_map/main_product/pallas_call | solution.py:227
  64.0 1.6 %collective-permute-start.12 = (f32[32,128]{1,0:T(8,128)S(1)}, f32[32,128]{1,0:T(8,128)S(1)}, u32[]{:S(2)}, u32[]{:S(2)}) collective-permute-start(f32[32,128]{1,0:T(8,128)S(1)} %low_rank.1), channel_id=1, source_target_pairs={{0,1},{1,0},{2,3},{3,2},{4,5},{5,4},{6,7},{7,6},{8,9},{9,8},{10,11... | collective-permute-start | bytes 49160 | tf_op jit(solution)/shard_map/ppermute | solution.py:47
  65.6 2.7 %collective-permute-start.11 = (bf16[48,2048]{1,0:T(8,128)(2,1)S(1)}, bf16[48,2048]{1,0:T(8,128)(2,1)S(1)}, u32[]{:S(2)}, u32[]{:S(2)}) collective-permute-start(bf16[48,2048]{1,0:T(8,128)(2,1)S(1)} %bitcast.41), channel_id=1, source_target_pairs={{0,32},{32,0},{1,33},{33,1},{2,34},{34,2},{3,35},{35,3},{4,36},{36... | collective-permute-start | bytes 589832 | tf_op jit(solution)/shard_map/ppermute | solution.py:39
  68.4 3.3 %collective-permute-start.13 = (f32[64,128]{1,0:T(8,128)S(1)}, f32[64,128]{1,0:T(8,128)S(1)}, u32[]{:S(2)}, u32[]{:S(2)}) collective-permute-start(f32[64,128]{1,0:T(8,128)S(1)} %pad_maximum_fusion.5), channel_id=1, source_target_pairs={{0,2},{1,3},{2,0},{3,1},{4,6},{5,7},{6,4},{7,5},{8,10},{9,11},{10,... | collective-permute-start | bytes 98312 | tf_op jit(solution)/shard_map/ppermute | solution.py:47
  71.7 1.6 %collective-permute-done.13 = f32[64,128]{1,0:T(8,128)S(1)} collective-permute-done((f32[64,128]{1,0:T(8,128)S(1)}, f32[64,128]{1,0:T(8,128)S(1)}, u32[]{:S(2)}, u32[]{:S(2)}) %collective-permute-start.13) | collective-permute-done | bytes 32800 | tf_op jit(solution)/shard_map/ppermute | solution.py:47
  73.3 5.4 %collective-permute-done.9.refs_1_ = bf16[1024,256]{1,0:T(8,128)(2,1)S(1)} collective-permute-done((bf16[1024,256]{1,0:T(8,128)(2,1)S(1)}, bf16[1024,256]{1,0:T(8,128)(2,1)S(1)}, u32[]{:S(2)}, u32[]{:S(2)}) %collective-permute-start.9) | collective-permute-done | bytes 524320 | tf_op jit(solution)/shard_map/ppermute | solution.py:35
  78.8 0.9 collective-permute-start.14
  79.8 1.6 %collective-permute-start.20 = (bf16[96,2048]{1,0:T(8,128)(2,1)S(1)}, bf16[96,2048]{1,0:T(8,128)(2,1)S(1)}, u32[]{:S(2)}, u32[]{:S(2)}) collective-permute-start(bf16[96,2048]{1,0:T(8,128)(2,1)S(1)} %constant_dynamic-update-slice_fusion.13), channel_id=1, source_target_pairs={{0,24},{8,0},{16,8},{24,16},{1,25},{9,1},{17,9},{25,17},{2,26},{10... | collective-permute-start | bytes 1179656 | tf_op jit(solution)/shard_map/ppermute | solution.py:35
  82.1 2.1 %main_product.5 = (f32[512,256]{1,0:T(8,128)S(1)}, f32[512,256]{1,0:T(8,128)S(1)}) custom-call(s32[17]{0:T(128)S(1)} %concatenate.36.info, bf16[512,8192]{1,0:T(8,128)(2,1)S(1)} %bitcast.31, bf16[1024,256]{1,0:T(8,128)(2,1)S(1)} %collective-permute-done.4.refs_0_, bf16[1024,256]{1,0:T(8,128)(2,1)S(1)} %collective-permute-done.9.refs_1_, ...), custom_call_target="tpu_custom_call" | custom-call | tf_op jit(solution)/shard_map/main_product/pallas_call | solution.py:227
  84.2 4.2 %finish.1 = (bf16[3,128,2,256]{3,2,1,0:T(2,128)(2,1)S(1)}, bf16[3,128,2,256]{3,2,1,0:T(2,128)(2,1)S(1)}) custom-call(s32[17]{0:T(128)S(1)} %concatenate.36.info, bf16[512,8192]{1,0:T(8,128)(2,1)S(1)} %bitcast.32, bf16[3072,256]{1,0:T(8,128)(2,1)S(1)} %collective-permute-done.14.refs_0_, bf16[2048,256]{1,0:T(8,128)(2,1)S(1)} %collective-permute-done.15.refs_1_, ...), custom_call_target="tpu_custom_call" | custom-call | tf_op jit(solution)/shard_map/finish/pallas_call | solution.py:278
  88.4 1.3 collective-permute-start.16
  89.7 1.8 %collective-permute-start.17 = (bf16[3,128,2,256]{3,2,1,0:T(2,128)(2,1)S(1)}, bf16[3,128,2,256]{3,2,1,0:T(2,128)(2,1)S(1)}, u32[]{:S(2)}, u32[]{:S(2)}) collective-permute-start(bf16[3,128,2,256]{3,2,1,0:T(2,128)(2,1)S(1)} %get-tuple-element.88), channel_id=1, source_target_pairs={{0,96},{32,64},{64,32},{96,0},{1,97},{33,65},{65,33},{97,1},{2,98}... | collective-permute-start | bytes 1179656 | tf_op jit(solution)/shard_map/ppermute | solution.py:31
  91.5 1.4 collective-permute-done.19
  93.0 8.8 %collective-permute-done.18 = bf16[96,2048]{1,0:T(8,128)(2,1)S(1)} collective-permute-done((bf16[96,2048]{1,0:T(8,128)(2,1)S(1)}, bf16[96,2048]{1,0:T(8,128)(2,1)S(1)}, u32[]{:S(2)}, u32[]{:S(2)}) %collective-permute-start.18) | collective-permute-done | bytes 393248 | tf_op jit(solution)/shard_map/ppermute | solution.py:35
  102.0 0.9 collective-permute-start.23
  102.9 1.1 pad_maximum_fusion.2.refs_0_
  104.0 1.9 %collective-permute-start.22 = (bf16[2,3,128,2,256]{4,3,2,1,0:T(2,128)(2,1)S(1)}, bf16[2,3,128,2,256]{4,3,2,1,0:T(2,128)(2,1)S(1)}, u32[]{:S(2)}, u32[]{:S(2)}) collective-permute-start(bf16[2,3,128,2,256]{4,3,2,1,0:T(2,128)(2,1)S(1)} %pad_maximum_fusion.2.refs_0_), channel_id=1, source_target_pairs={{0,24},{8,0},{16,8},{24,16},{1,25},{9,1},{17,9},{25,17},{2,26},{10... | collective-permute-start | bytes 2359304 | tf_op jit(solution)/shard_map/ppermute | solution.py:35
  106.2 5.2 %project.1 = (bf16[192,512]{1,0:T(8,128)(2,1)S(1)}, bf16[192,512]{1,0:T(8,128)(2,1)S(1)}, bf16[192,512]{1,0:T(8,128)(2,1)S(1)}, bf16[192,512]{1,0:T(8,128)(2,1)S(1)}) custom-call(s32[17]{0:T(128)S(1)} %concatenate.36.info, s32[768,1]{1,0:T(8,128)S(1)} %broadcast_in_dim.20.keep, bf16[128,2048]{1,0:T(8,128)(2,1)S(1)} %bitcast.35, ...), custom_call_target="tpu_custom_call" | custom-call | tf_op jit(solution)/shard_map/project/pallas_call | solution.py:395
  111.3 1.7 %collective-permute-start.24 = (bf16[192,512]{1,0:T(8,128)(2,1)S(1)}, bf16[192,512]{1,0:T(8,128)(2,1)S(1)}, u32[]{:S(2)}, u32[]{:S(2)}) collective-permute-start(bf16[192,512]{1,0:T(8,128)(2,1)S(1)} %get-tuple-element.98), channel_id=1, source_target_pairs={{0,1},{1,2},{2,3},{3,0},{4,5},{5,6},{6,7},{7,4},{8,9},{9,10},{10,1... | collective-permute-start | bytes 589832 | tf_op jit(solution)/shard_map/ppermute | solution.py:43
  113.0 3.3 %collective-permute-start.25 = (bf16[192,512]{1,0:T(8,128)(2,1)S(1)}, bf16[192,512]{1,0:T(8,128)(2,1)S(1)}, u32[]{:S(2)}, u32[]{:S(2)}) collective-permute-start(bf16[192,512]{1,0:T(8,128)(2,1)S(1)} %get-tuple-element.99), channel_id=1, source_target_pairs={{0,2},{1,3},{2,0},{3,1},{4,6},{5,7},{6,4},{7,5},{8,10},{9,11},{10,... | collective-permute-start | bytes 589832 | tf_op jit(solution)/shard_map/ppermute | solution.py:43
  116.3 0.7 collective-permute-start.26
  117.1 3.1 %collective-permute-done.24 = bf16[192,512]{1,0:T(8,128)(2,1)S(1)} collective-permute-done((bf16[192,512]{1,0:T(8,128)(2,1)S(1)}, bf16[192,512]{1,0:T(8,128)(2,1)S(1)}, u32[]{:S(2)}, u32[]{:S(2)}) %collective-permute-start.24) | collective-permute-done | bytes 196640 | tf_op jit(solution)/shard_map/ppermute | solution.py:43
  120.2 5.1 %collective-permute-done.25 = bf16[192,512]{1,0:T(8,128)(2,1)S(1)} collective-permute-done((bf16[192,512]{1,0:T(8,128)(2,1)S(1)}, bf16[192,512]{1,0:T(8,128)(2,1)S(1)}, u32[]{:S(2)}, u32[]{:S(2)}) %collective-permute-start.25) | collective-permute-done | bytes 196640 | tf_op jit(solution)/shard_map/ppermute | solution.py:43
  125.3 0.8 add_convert_fusion
  126.1 1.1 collective-permute-start.29
  128.3 2.7 %collective-permute-start.28 = (bf16[3,128,2,256]{3,2,1,0:T(2,128)(2,1)S(1)}, bf16[3,128,2,256]{3,2,1,0:T(2,128)(2,1)S(1)}, u32[]{:S(2)}, u32[]{:S(2)}) collective-permute-start(bf16[3,128,2,256]{3,2,1,0:T(2,128)(2,1)S(1)} %slice_bitcast_fusion), channel_id=1, source_target_pairs={{0,24},{8,0},{16,8},{24,16},{1,25},{9,1},{17,9},{25,17},{2,26},{10... | collective-permute-start | bytes 1179656 | tf_op jit(solution)/shard_map/ppermute | solution.py:35
  131.0 8.5 %collective-permute-done.28 = bf16[3,128,2,256]{3,2,1,0:T(2,128)(2,1)S(1)} collective-permute-done((bf16[3,128,2,256]{3,2,1,0:T(2,128)(2,1)S(1)}, bf16[3,128,2,256]{3,2,1,0:T(2,128)(2,1)S(1)}, u32[]{:S(2)}, u32[]{:S(2)}) %collective-permute-start.28) | collective-permute-done | bytes 393248 | tf_op jit(solution)/shard_map/ppermute | solution.py:35
  139.4 3.1 %collective-permute-done.27 = bf16[3,128,2,256]{3,2,1,0:T(2,128)(2,1)S(1)} collective-permute-done((bf16[3,128,2,256]{3,2,1,0:T(2,128)(2,1)S(1)}, bf16[3,128,2,256]{3,2,1,0:T(2,128)(2,1)S(1)}, u32[]{:S(2)}, u32[]{:S(2)}) %collective-permute-start.27) | collective-permute-done | bytes 393248 | tf_op jit(solution)/shard_map/ppermute | solution.py:35
  142.5 1.3 collective-permute-start.32
  143.9 2.9 %place.2.refs_4_ = bf16[1,2,2048,2,256]{4,3,2,1,0:T(2,128)(2,1)} custom-call(s32[17]{0:T(128)S(1)} %concatenate.36.info, bf16[2,3,128,2,256]{4,3,2,1,0:T(2,128)(2,1)S(1)} %pad_maximum_fusion.2.refs_0_, bf16[2,3,128,2,256]{4,3,2,1,0:T(2,128)(2,1)S(1)} %collective-permute-done.21.refs_1_, bf16[2,3,128,2,256]{4,3,2,1,0:T(2,128)(2,1)S(1)} %collective-permute-done.22.refs_2_, ...), custom_call_target="tpu_custom_call" | custom-call | tf_op jit(solution)/shard_map/place/pallas_call | solution.py:353
  146.8 0.9 place.3
  (87 shorter events, 4.8 us)
Async XLA Ops:
  1.4 1.0 copy-start.3
  2.4 0.9 copy-start.4
  3.4 28.9 %copy-start.9 = (bf16[48,2048]{1,0:T(8,128)(2,1)S(1)}, bf16[48,2048]{1,0:T(8,128)(2,1)}, u32[]{:S(2)}) copy-start(bf16[48,2048]{1,0:T(8,128)(2,1)} %param.20) | copy-start | bytes 589828
  3.4 28.9 %copy-start = (bf16[48,128,2,256]{3,2,1,0:T(2,128)(2,1)S(1)}, bf16[48,128,2,256]{3,2,1,0:T(2,128)(2,1)}, u32[]{:S(2)}) copy-start(bf16[48,128,2,256]{3,2,1,0:T(2,128)(2,1)} %kv_ref.1) | copy-start | bytes 18874372
  3.4 28.9 %copy-start.7 = (bf16[48,2,256]{2,1,0:T(2,128)(2,1)S(1)}, bf16[48,2,256]{2,1,0:T(2,128)(2,1)}, u32[]{:S(2)}) copy-start(bf16[48,2,256]{2,1,0:T(2,128)(2,1)} %cur_ref.1) | copy-start | bytes 147460
  3.4 28.9 %copy-start.8 = (s32[48]{0:T(128)S(1)}, s32[48]{0:T(128)}, u32[]{:S(2)}) copy-start(s32[48]{0:T(128)} %len_ref) | copy-start | bytes 580
  5.7 15.5 %collective-permute-start.3 = (bf16[576,256]{1,0:T(8,128)(2,1)S(1)}, bf16[576,256]{1,0:T(8,128)(2,1)S(1)}, u32[]{:S(2)}, u32[]{:S(2)}) collective-permute-start(bf16[576,256]{1,0:T(8,128)(2,1)S(1)} %get-tuple-element.60), channel_id=1, source_target_pairs={{0,24},{8,0},{16,8},{24,16},{1,25},{9,1},{17,9},{25,17},{2,26},{10... | collective-permute-start | bytes 884744 | tf_op jit(solution)/shard_map/ppermute | solution.py:35
  9.3 11.9 %collective-permute-start.2 = (bf16[576,256]{1,0:T(8,128)(2,1)S(1)}, bf16[576,256]{1,0:T(8,128)(2,1)S(1)}, u32[]{:S(2)}, u32[]{:S(2)}) collective-permute-start(bf16[576,256]{1,0:T(8,128)(2,1)S(1)} %get-tuple-element.60), channel_id=1, source_target_pairs={{0,16},{8,24},{16,0},{24,8},{1,17},{9,25},{17,1},{25,9},{2,18},{10... | collective-permute-start | bytes 884744 | tf_op jit(solution)/shard_map/ppermute | solution.py:35
  9.6 16.4 %collective-permute-start.1 = (bf16[576,256]{1,0:T(8,128)(2,1)S(1)}, bf16[576,256]{1,0:T(8,128)(2,1)S(1)}, u32[]{:S(2)}, u32[]{:S(2)}) collective-permute-start(bf16[576,256]{1,0:T(8,128)(2,1)S(1)} %get-tuple-element.60), channel_id=1, source_target_pairs={{0,8},{8,16},{16,24},{24,0},{1,9},{9,17},{17,25},{25,1},{2,10},{10... | collective-permute-start | bytes 884744 | tf_op jit(solution)/shard_map/ppermute | solution.py:35
  10.3 7.5 %collective-permute-start = (bf16[512,256]{1,0:T(8,128)(2,1)S(1)}, bf16[512,256]{1,0:T(8,128)(2,1)S(1)}, u32[]{:S(2)}, u32[]{:S(2)}) collective-permute-start(bf16[512,256]{1,0:T(8,128)(2,1)S(1)} %get-tuple-element.58), channel_id=1, source_target_pairs={{0,96},{32,64},{64,32},{96,0},{1,97},{33,65},{65,33},{97,1},{2,98}... | collective-permute-start | bytes 786440 | tf_op jit(solution)/shard_map/ppermute | solution.py:31
  26.1 33.1 %slice-start = ((s8[8388608]{0:T(1024)(128)(4,1)}), s8[4194304]{0:T(1024)(128)(4,1)S(1)}, s32[]{:S(2)}) async-start(s8[8388608]{0:T(1024)(128)(4,1)} %bitcast.26), calls=%async_computation | async-start | bytes 8388608
  26.1 37.4 %collective-permute-start.5 = (bf16[1024,256]{1,0:T(8,128)(2,1)S(1)}, bf16[1024,256]{1,0:T(8,128)(2,1)S(1)}, u32[]{:S(2)}, u32[]{:S(2)}) collective-permute-start(bf16[1024,256]{1,0:T(8,128)(2,1)S(1)} %get-tuple-element.72.refs_0_), channel_id=1, source_target_pairs={{0,24},{8,0},{16,8},{24,16},{1,25},{9,1},{17,9},{25,17},{2,26},{10... | collective-permute-start | bytes 1572872 | tf_op jit(solution)/shard_map/ppermute | solution.py:35
  26.2 37.3 %collective-permute-start.4 = (bf16[1024,256]{1,0:T(8,128)(2,1)S(1)}, bf16[1024,256]{1,0:T(8,128)(2,1)S(1)}, u32[]{:S(2)}, u32[]{:S(2)}) collective-permute-start(bf16[1024,256]{1,0:T(8,128)(2,1)S(1)} %get-tuple-element.72.refs_0_), channel_id=1, source_target_pairs={{0,8},{8,16},{16,24},{24,0},{1,9},{9,17},{17,25},{25,1},{2,10},{10... | collective-permute-start | bytes 1572872 | tf_op jit(solution)/shard_map/ppermute | solution.py:35
  27.8 34.2 %collective-permute-start.8 = (bf16[3072,256]{1,0:T(8,128)(2,1)S(1)}, bf16[3072,256]{1,0:T(8,128)(2,1)S(1)}, u32[]{:S(2)}, u32[]{:S(2)}) collective-permute-start(bf16[3072,256]{1,0:T(8,128)(2,1)S(1)} %get-tuple-element.110), channel_id=1, source_target_pairs={{0,4},{4,0},{1,5},{5,1},{2,6},{6,2},{3,7},{7,3},{8,12},{12,8},{9,1... | collective-permute-start | bytes 4718600 | tf_op jit(solution)/shard_map/ppermute | solution.py:51
  29.0 44.3 %collective-permute-start.10 = (bf16[2048,256]{1,0:T(8,128)(2,1)S(1)}, bf16[2048,256]{1,0:T(8,128)(2,1)S(1)}, u32[]{:S(2)}, u32[]{:S(2)}) collective-permute-start(bf16[2048,256]{1,0:T(8,128)(2,1)S(1)} %pad_maximum_fusion.1.refs_1_), channel_id=1, source_target_pairs={{0,32},{32,0},{1,33},{33,1},{2,34},{34,2},{3,35},{35,3},{4,36},{36... | collective-permute-start | bytes 3145736 | tf_op jit(solution)/shard_map/ppermute | solution.py:39
  31.9 26.3 %collective-permute-start.6 = (bf16[256,256]{1,0:T(8,128)(2,1)S(1)}, bf16[256,256]{1,0:T(8,128)(2,1)S(1)}, u32[]{:S(2)}, u32[]{:S(2)}) collective-permute-start(bf16[256,256]{1,0:T(8,128)(2,1)S(1)} %pad_maximum_fusion.3), channel_id=1, source_target_pairs={{0,32},{32,0},{1,33},{33,1},{2,34},{34,2},{3,35},{35,3},{4,36},{36... | collective-permute-start | bytes 393224 | tf_op jit(solution)/shard_map/ppermute | solution.py:39
  32.2 26.9 %slice-start.1 = ((s8[8388608]{0:T(1024)(128)(4,1)}), s8[4194304]{0:T(1024)(128)(4,1)S(1)}, s32[]{:S(2)}) async-start(s8[8388608]{0:T(1024)(128)(4,1)} %bitcast.26), calls=%async_computation.1 | async-start | bytes 8388608
  58.2 2.4 %collective-permute-start.7 = (bf16[512,256]{1,0:T(8,128)(2,1)S(1)}, bf16[512,256]{1,0:T(8,128)(2,1)S(1)}, u32[]{:S(2)}, u32[]{:S(2)}) collective-permute-start(bf16[512,256]{1,0:T(8,128)(2,1)S(1)} %constant_dynamic-update-slice_fusion.2.own_ref), channel_id=1, source_target_pairs={{0,4},{4,0},{1,5},{5,1},{2,6},{6,2},{3,7},{7,3},{8,12},{12,8},{9,1... | collective-permute-start | bytes 786440 | tf_op jit(solution)/shard_map/ppermute | solution.py:51
  63.6 15.1 %collective-permute-start.9 = (bf16[1024,256]{1,0:T(8,128)(2,1)S(1)}, bf16[1024,256]{1,0:T(8,128)(2,1)S(1)}, u32[]{:S(2)}, u32[]{:S(2)}) collective-permute-start(bf16[1024,256]{1,0:T(8,128)(2,1)S(1)} %get-tuple-element.72.refs_0_), channel_id=1, source_target_pairs={{0,16},{8,24},{16,0},{24,8},{1,17},{9,25},{17,1},{25,9},{2,18},{10... | collective-permute-start | bytes 1572872 | tf_op jit(solution)/shard_map/ppermute | solution.py:35
  64.0 4.4 %collective-permute-start.12 = (f32[32,128]{1,0:T(8,128)S(1)}, f32[32,128]{1,0:T(8,128)S(1)}, u32[]{:S(2)}, u32[]{:S(2)}) collective-permute-start(f32[32,128]{1,0:T(8,128)S(1)} %low_rank.1), channel_id=1, source_target_pairs={{0,1},{1,0},{2,3},{3,2},{4,5},{5,4},{6,7},{7,6},{8,9},{9,8},{10,11... | collective-permute-start | bytes 49160 | tf_op jit(solution)/shard_map/ppermute | solution.py:47
  65.6 7.7 %collective-permute-start.11 = (bf16[48,2048]{1,0:T(8,128)(2,1)S(1)}, bf16[48,2048]{1,0:T(8,128)(2,1)S(1)}, u32[]{:S(2)}, u32[]{:S(2)}) collective-permute-start(bf16[48,2048]{1,0:T(8,128)(2,1)S(1)} %bitcast.41), channel_id=1, source_target_pairs={{0,32},{32,0},{1,33},{33,1},{2,34},{34,2},{3,35},{35,3},{4,36},{36... | collective-permute-start | bytes 589832 | tf_op jit(solution)/shard_map/ppermute | solution.py:39
  68.4 4.9 %collective-permute-start.13 = (f32[64,128]{1,0:T(8,128)S(1)}, f32[64,128]{1,0:T(8,128)S(1)}, u32[]{:S(2)}, u32[]{:S(2)}) collective-permute-start(f32[64,128]{1,0:T(8,128)S(1)} %pad_maximum_fusion.5), channel_id=1, source_target_pairs={{0,2},{1,3},{2,0},{3,1},{4,6},{5,7},{6,4},{7,5},{8,10},{9,11},{10,... | collective-permute-start | bytes 98312 | tf_op jit(solution)/shard_map/ppermute | solution.py:47
  78.8 5.4 %collective-permute-start.14 = (bf16[3072,256]{1,0:T(8,128)(2,1)S(1)}, bf16[3072,256]{1,0:T(8,128)(2,1)S(1)}, u32[]{:S(2)}, u32[]{:S(2)}) collective-permute-start(bf16[3072,256]{1,0:T(8,128)(2,1)S(1)} %pad_maximum_fusion), channel_id=1, source_target_pairs={{0,4},{4,0},{1,5},{5,1},{2,6},{6,2},{3,7},{7,3},{8,12},{12,8},{9,1... | collective-permute-start | bytes 4718600 | tf_op jit(solution)/shard_map/ppermute | solution.py:51
  79.7 4.5 %collective-permute-start.15 = (bf16[2048,256]{1,0:T(8,128)(2,1)S(1)}, bf16[2048,256]{1,0:T(8,128)(2,1)S(1)}, u32[]{:S(2)}, u32[]{:S(2)}) collective-permute-start(bf16[2048,256]{1,0:T(8,128)(2,1)S(1)} %collective-permute-done.10.refs_3_), channel_id=1, source_target_pairs={{0,4},{4,0},{1,5},{5,1},{2,6},{6,2},{3,7},{7,3},{8,12},{12,8},{9,1... | collective-permute-start | bytes 3145736 | tf_op jit(solution)/shard_map/ppermute | solution.py:51
  79.8 4.4 %copy-start.5 = (bf16[8,2,16,256]{3,2,1,0:T(8,128)(2,1)S(1)}, bf16[8,2,16,256]{3,2,1,0:T(8,128)(2,1)}, u32[]{:S(2)}) copy-start(bf16[8,2,16,256]{3,2,1,0:T(8,128)(2,1)} %refs_9_.1) | copy-start | bytes 393220
  79.8 11.7 %collective-permute-start.20 = (bf16[96,2048]{1,0:T(8,128)(2,1)S(1)}, bf16[96,2048]{1,0:T(8,128)(2,1)S(1)}, u32[]{:S(2)}, u32[]{:S(2)}) collective-permute-start(bf16[96,2048]{1,0:T(8,128)(2,1)S(1)} %constant_dynamic-update-slice_fusion.13), channel_id=1, source_target_pairs={{0,24},{8,0},{16,8},{24,16},{1,25},{9,1},{17,9},{25,17},{2,26},{10... | collective-permute-start | bytes 1179656 | tf_op jit(solution)/shard_map/ppermute | solution.py:35
  81.4 11.5 %collective-permute-start.19 = (bf16[96,2048]{1,0:T(8,128)(2,1)S(1)}, bf16[96,2048]{1,0:T(8,128)(2,1)S(1)}, u32[]{:S(2)}, u32[]{:S(2)}) collective-permute-start(bf16[96,2048]{1,0:T(8,128)(2,1)S(1)} %constant_dynamic-update-slice_fusion.13), channel_id=1, source_target_pairs={{0,16},{8,24},{16,0},{24,8},{1,17},{9,25},{17,1},{25,9},{2,18},{10... | collective-permute-start | bytes 1179656 | tf_op jit(solution)/shard_map/ppermute | solution.py:35
  81.4 20.3 %collective-permute-start.18 = (bf16[96,2048]{1,0:T(8,128)(2,1)S(1)}, bf16[96,2048]{1,0:T(8,128)(2,1)S(1)}, u32[]{:S(2)}, u32[]{:S(2)}) collective-permute-start(bf16[96,2048]{1,0:T(8,128)(2,1)S(1)} %constant_dynamic-update-slice_fusion.13), channel_id=1, source_target_pairs={{0,8},{8,16},{16,24},{24,0},{1,9},{9,17},{17,25},{25,1},{2,10},{10... | collective-permute-start | bytes 1179656 | tf_op jit(solution)/shard_map/ppermute | solution.py:35
  88.4 13.3 %collective-permute-start.16 = (bf16[3,128,2,256]{3,2,1,0:T(2,128)(2,1)S(1)}, bf16[3,128,2,256]{3,2,1,0:T(2,128)(2,1)S(1)}, u32[]{:S(2)}, u32[]{:S(2)}) collective-permute-start(bf16[3,128,2,256]{3,2,1,0:T(2,128)(2,1)S(1)} %get-tuple-element.87), channel_id=1, source_target_pairs={{0,64},{64,0},{1,65},{65,1},{2,66},{66,2},{3,67},{67,3},{4,68},{68... | collective-permute-start | bytes 1179656 | tf_op jit(solution)/shard_map/ppermute | solution.py:477
  89.7 12.1 %collective-permute-start.17 = (bf16[3,128,2,256]{3,2,1,0:T(2,128)(2,1)S(1)}, bf16[3,128,2,256]{3,2,1,0:T(2,128)(2,1)S(1)}, u32[]{:S(2)}, u32[]{:S(2)}) collective-permute-start(bf16[3,128,2,256]{3,2,1,0:T(2,128)(2,1)S(1)} %get-tuple-element.88), channel_id=1, source_target_pairs={{0,96},{32,64},{64,32},{96,0},{1,97},{33,65},{65,33},{97,1},{2,98}... | collective-permute-start | bytes 1179656 | tf_op jit(solution)/shard_map/ppermute | solution.py:31
  101.8 4.1 %copy-start.10 = (s32[768]{0:T(1024)S(1)}, s32[768]{0:T(1024)}, u32[]{:S(2)}) copy-start(s32[768]{0:T(1024)} %param.24) | copy-start | bytes 9220
  101.9 4.3 %copy-start.1 = (bf16[2048,512]{1,0:T(8,128)(2,1)S(1)}, bf16[2048,512]{1,0:T(8,128)(2,1)}, u32[]{:S(2)}) copy-start(bf16[2048,512]{1,0:T(8,128)(2,1)} %w_ref.3) | copy-start | bytes 6291460
  101.9 4.3 %copy-start.2 = (bf16[2048,8,16]{0,2,1:T(8,128)(2,1)S(1)}, bf16[2048,8,16]{0,2,1:T(8,128)(2,1)}, u32[]{:S(2)}) copy-start(bf16[2048,8,16]{0,2,1:T(8,128)(2,1)} %param.26) | copy-start | bytes 1572868
  101.9 4.2 %copy-start.6 = (bf16[8,16,512]{2,1,0:T(8,128)(2,1)S(1)}, bf16[8,16,512]{2,1,0:T(8,128)(2,1)}, u32[]{:S(2)}) copy-start(bf16[8,16,512]{2,1,0:T(8,128)(2,1)} %param.27) | copy-start | bytes 393220
  102.0 4.2 %collective-permute-start.23 = (bf16[384,2048]{1,0:T(8,128)(2,1)S(1)}, bf16[384,2048]{1,0:T(8,128)(2,1)S(1)}, u32[]{:S(2)}, u32[]{:S(2)}) collective-permute-start(bf16[384,2048]{1,0:T(8,128)(2,1)S(1)} %constant_dynamic-update-slice_fusion.15.refs_0_), channel_id=1, source_target_pairs={{0,4},{4,0},{1,5},{5,1},{2,6},{6,2},{3,7},{7,3},{8,12},{12,8},{9,1... | collective-permute-start | bytes 4718600 | tf_op jit(solution)/shard_map/ppermute | solution.py:51
  104.0 22.1 %collective-permute-start.22 = (bf16[2,3,128,2,256]{4,3,2,1,0:T(2,128)(2,1)S(1)}, bf16[2,3,128,2,256]{4,3,2,1,0:T(2,128)(2,1)S(1)}, u32[]{:S(2)}, u32[]{:S(2)}) collective-permute-start(bf16[2,3,128,2,256]{4,3,2,1,0:T(2,128)(2,1)S(1)} %pad_maximum_fusion.2.refs_0_), channel_id=1, source_target_pairs={{0,24},{8,0},{16,8},{24,16},{1,25},{9,1},{17,9},{25,17},{2,26},{10... | collective-permute-start | bytes 2359304 | tf_op jit(solution)/shard_map/ppermute | solution.py:35
  105.9 20.2 %collective-permute-start.21 = (bf16[2,3,128,2,256]{4,3,2,1,0:T(2,128)(2,1)S(1)}, bf16[2,3,128,2,256]{4,3,2,1,0:T(2,128)(2,1)S(1)}, u32[]{:S(2)}, u32[]{:S(2)}) collective-permute-start(bf16[2,3,128,2,256]{4,3,2,1,0:T(2,128)(2,1)S(1)} %pad_maximum_fusion.2.refs_0_), channel_id=1, source_target_pairs={{0,8},{8,16},{16,24},{24,0},{1,9},{9,17},{17,25},{25,1},{2,10},{10... | collective-permute-start | bytes 2359304 | tf_op jit(solution)/shard_map/ppermute | solution.py:35
  111.3 8.9 %collective-permute-start.24 = (bf16[192,512]{1,0:T(8,128)(2,1)S(1)}, bf16[192,512]{1,0:T(8,128)(2,1)S(1)}, u32[]{:S(2)}, u32[]{:S(2)}) collective-permute-start(bf16[192,512]{1,0:T(8,128)(2,1)S(1)} %get-tuple-element.98), channel_id=1, source_target_pairs={{0,1},{1,2},{2,3},{3,0},{4,5},{5,6},{6,7},{7,4},{8,9},{9,10},{10,1... | collective-permute-start | bytes 589832 | tf_op jit(solution)/shard_map/ppermute | solution.py:43
  113.0 12.2 %collective-permute-start.25 = (bf16[192,512]{1,0:T(8,128)(2,1)S(1)}, bf16[192,512]{1,0:T(8,128)(2,1)S(1)}, u32[]{:S(2)}, u32[]{:S(2)}) collective-permute-start(bf16[192,512]{1,0:T(8,128)(2,1)S(1)} %get-tuple-element.99), channel_id=1, source_target_pairs={{0,2},{1,3},{2,0},{3,1},{4,6},{5,7},{6,4},{7,5},{8,10},{9,11},{10,... | collective-permute-start | bytes 589832 | tf_op jit(solution)/shard_map/ppermute | solution.py:43
  116.3 8.9 %collective-permute-start.26 = (bf16[192,512]{1,0:T(8,128)(2,1)S(1)}, bf16[192,512]{1,0:T(8,128)(2,1)S(1)}, u32[]{:S(2)}, u32[]{:S(2)}) collective-permute-start(bf16[192,512]{1,0:T(8,128)(2,1)S(1)} %get-tuple-element.100), channel_id=1, source_target_pairs={{0,3},{1,0},{2,1},{3,2},{4,7},{5,4},{6,5},{7,6},{8,11},{9,8},{10,9... | collective-permute-start | bytes 589832 | tf_op jit(solution)/shard_map/ppermute | solution.py:43
  126.1 16.5 %collective-permute-start.29 = (bf16[2,3,128,2,256]{4,3,2,1,0:T(2,128)(2,1)S(1)}, bf16[2,3,128,2,256]{4,3,2,1,0:T(2,128)(2,1)S(1)}, u32[]{:S(2)}, u32[]{:S(2)}) collective-permute-start(bf16[2,3,128,2,256]{4,3,2,1,0:T(2,128)(2,1)S(1)} %pad_maximum_fusion.2.refs_0_), channel_id=1, source_target_pairs={{0,4},{4,0},{1,5},{5,1},{2,6},{6,2},{3,7},{7,3},{8,12},{12,8},{9,1... | collective-permute-start | bytes 2359304 | tf_op jit(solution)/shard_map/ppermute | solution.py:51
  127.2 15.3 %collective-permute-start.30 = (bf16[2,3,128,2,256]{4,3,2,1,0:T(2,128)(2,1)S(1)}, bf16[2,3,128,2,256]{4,3,2,1,0:T(2,128)(2,1)S(1)}, u32[]{:S(2)}, u32[]{:S(2)}) collective-permute-start(bf16[2,3,128,2,256]{4,3,2,1,0:T(2,128)(2,1)S(1)} %collective-permute-done.21.refs_1_), channel_id=1, source_target_pairs={{0,4},{4,0},{1,5},{5,1},{2,6},{6,2},{3,7},{7,3},{8,12},{12,8},{9,1... | collective-permute-start | bytes 2359304 | tf_op jit(solution)/shard_map/ppermute | solution.py:51
  127.3 15.2 %collective-permute-start.31 = (bf16[2,3,128,2,256]{4,3,2,1,0:T(2,128)(2,1)S(1)}, bf16[2,3,128,2,256]{4,3,2,1,0:T(2,128)(2,1)S(1)}, u32[]{:S(2)}, u32[]{:S(2)}) collective-permute-start(bf16[2,3,128,2,256]{4,3,2,1,0:T(2,128)(2,1)S(1)} %collective-permute-done.22.refs_2_), channel_id=1, source_target_pairs={{0,4},{4,0},{1,5},{5,1},{2,6},{6,2},{3,7},{7,3},{8,12},{12,8},{9,1... | collective-permute-start | bytes 2359304 | tf_op jit(solution)/shard_map/ppermute | solution.py:51
  128.3 11.2 %collective-permute-start.28 = (bf16[3,128,2,256]{3,2,1,0:T(2,128)(2,1)S(1)}, bf16[3,128,2,256]{3,2,1,0:T(2,128)(2,1)S(1)}, u32[]{:S(2)}, u32[]{:S(2)}) collective-permute-start(bf16[3,128,2,256]{3,2,1,0:T(2,128)(2,1)S(1)} %slice_bitcast_fusion), channel_id=1, source_target_pairs={{0,24},{8,0},{16,8},{24,16},{1,25},{9,1},{17,9},{25,17},{2,26},{10... | collective-permute-start | bytes 1179656 | tf_op jit(solution)/shard_map/ppermute | solution.py:35
  131.0 11.6 %collective-permute-start.27 = (bf16[3,128,2,256]{3,2,1,0:T(2,128)(2,1)S(1)}, bf16[3,128,2,256]{3,2,1,0:T(2,128)(2,1)S(1)}, u32[]{:S(2)}, u32[]{:S(2)}) collective-permute-start(bf16[3,128,2,256]{3,2,1,0:T(2,128)(2,1)S(1)} %slice_bitcast_fusion.1), channel_id=1, source_target_pairs={{0,8},{8,16},{16,24},{24,0},{1,9},{9,17},{17,25},{25,1},{2,10},{10... | collective-permute-start | bytes 1179656 | tf_op jit(solution)/shard_map/ppermute | solution.py:35
  142.5 4.2 %collective-permute-start.32 = (bf16[3,128,2,256]{3,2,1,0:T(2,128)(2,1)S(1)}, bf16[3,128,2,256]{3,2,1,0:T(2,128)(2,1)S(1)}, u32[]{:S(2)}, u32[]{:S(2)}) collective-permute-start(bf16[3,128,2,256]{3,2,1,0:T(2,128)(2,1)S(1)} %collective-permute-done.27), channel_id=1, source_target_pairs={{0,4},{4,0},{1,5},{5,1},{2,6},{6,2},{3,7},{7,3},{8,12},{12,8},{9,1... | collective-permute-start | bytes 1179656 | tf_op jit(solution)/shard_map/ppermute | solution.py:51
  143.8 3.0 %collective-permute-start.33 = (bf16[3,128,2,256]{3,2,1,0:T(2,128)(2,1)S(1)}, bf16[3,128,2,256]{3,2,1,0:T(2,128)(2,1)S(1)}, u32[]{:S(2)}, u32[]{:S(2)}) collective-permute-start(bf16[3,128,2,256]{3,2,1,0:T(2,128)(2,1)S(1)} %collective-permute-done.28), channel_id=1, source_target_pairs={{0,4},{4,0},{1,5},{5,1},{2,6},{6,2},{3,7},{7,3},{8,12},{12,8},{9,1... | collective-permute-start | bytes 1179656 | tf_op jit(solution)/shard_map/ppermute | solution.py:51

commit v7 on v6

--- a/solution.py
+++ b/solution.py
@@ -31,6 +31,14 @@
     return lax.ppermute(value, ("pool", "xh"), [(i, 3 - i) for i in range(4)])
 
 
+def x_shift(value, k):
+    pairs = []
+    for x in range(4):
+        t = (x + k) % 4
+        pairs.append(((x % 2) * 2 + x // 2, (t % 2) * 2 + t // 2))
+    return lax.ppermute(value, ("pool", "xh"), pairs)
+
+
 def y_shift(value, k):
     return lax.ppermute(value, "y", [(i, (i + k) % 4) for i in range(4)])
 
@@ -53,7 +61,7 @@
 
 def pack_kernel(info, w_ref, d_ref, k_ref, v_ref):
     k_ref[...] = w_ref[:, 0, :]
-    v_ref[0:512] = w_ref[:, 1, :]
+    v_ref[0:256] = w_ref[pl.ds(pl.multiple_of(info[POOL] * 256, 256), 256), 1, :]
     column = lax.broadcasted_iota(jnp.int32, (256, 128), 0)
     lane = lax.broadcasted_iota(jnp.int32, (256, 128), 1)
     pick = (column == info[ADAPTER + info[HEAD]] * 32 + lane) & (lane < 32)
@@ -63,8 +71,8 @@
         (((0,), (1,)), ((), ())),
         preferred_element_type=jnp.float32,
     ).astype(jnp.bfloat16)
-    v_ref[512:544] = low[0:32, 0:256]
-    v_ref[544:576] = low[0:32, 256:512]
+    v_ref[256:288] = low[0:32, 0:256]
+    v_ref[288:320] = low[0:32, 256:512]
 
 
 def pack(info, weight, down):
@@ -74,7 +82,7 @@
         out_specs=[VMEM, VMEM],
         out_shape=[
             jax.ShapeDtypeStruct((512, 256), jnp.bfloat16),
-            jax.ShapeDtypeStruct((576, 256), jnp.bfloat16),
+            jax.ShapeDtypeStruct((320, 256), jnp.bfloat16),
         ],
         compiler_params=params(),
         name="pack",
@@ -187,18 +195,23 @@
 
 
 def add_products(pieces, fresh, info, prompt, blocks, outs):
-    xh, y, core = info[XH], info[Y], info[CORE]
+    pool, xh, y, core = info[POOL], info[XH], info[Y], info[CORE]
     fresh = [fresh, fresh]
-    for kv, partner, which, row, shards in pieces:
+    for kv, partner, which, row, j in pieces:
         c_of = 1 - core if partner else core
         tokens = []
-        for other, j in shards:
-            side = 1 - xh if other else xh
-            at = pl.multiple_of((side * 8 + x_order(y)[j] * 2 + c_of) * 512, 512)
-            tokens.append(prompt[:, pl.ds(at, 512)])
+        if kv == 0:
+            for side in (xh, 1 - xh):
+                at = pl.multiple_of((side * 8 + x_order(y)[j] * 2 + c_of) * 512, 512)
+                tokens.append(prompt[:, pl.ds(at, 512)])
+        else:
+            xi = x_order(2 * xh + pool)[j]
+            for yi in x_order(y):
+                at = ((xi >> 1) * 8 + yi * 2 + c_of) * 512 + (xi & 1) * 256
+                tokens.append(prompt[:, pl.ds(pl.multiple_of(at, 256), 256)])
         part = jnp.dot(
             jnp.concatenate(tokens, 1),
-            blocks[which][row : row + 512 * len(shards)],
+            blocks[which][row : row + 1024],
             preferred_element_type=jnp.float32,
         )
         if fresh[kv]:
@@ -206,16 +219,6 @@
         else:
             outs[kv][...] += part
         fresh[kv] = False
-
-
-def key_piece(partner, which, row, j):
-    return (0, partner, which, row, ((0, j), (1, j)))
-
-
-def value_pieces(partner, which, row, other):
-    return tuple(
-        (1, partner, which, row + 1024 * n, ((other, 2 * n), (other, 2 * n + 1))) for n in range(2)
-    )
 
 
 def main_kernel(pieces, info, prompt, *refs):
@@ -439,40 +442,35 @@
         (keys, keys_across, ring_values, cached_length)
     )
     key0 = jnp.concatenate([keys, keys_across], 0)
-    value0 = jnp.concatenate([v[:512] for v in ring_values], 0)
-    down0 = jnp.concatenate([v[512:] for v in ring_values], 0)
+    value0 = jnp.concatenate([v[:256] for v in ring_values], 0)
+    down0 = jnp.concatenate([v[256:] for v in ring_values], 0)
     key1, key3 = y_shift(key0, 1), y_shift(key0, -1)
-    value1 = xh_swap(value0)
+    value1, value3 = x_shift(value0, 1), x_shift(value0, -1)
     down_own = jnp.concatenate([down0, xh_swap(down0)], 0)
     attended = attend(query, key_value_cache, current_key_value, cached_length, 0, 1)
     attended = attended.reshape(rows, heads * HEAD_DIM)
-    down_own, attended = barrier((down_own, attended))
+    key0, value0, key1, key3, value1, value3, down_own, attended = barrier(
+        (key0, value0, key1, key3, value1, value3, down_own, attended)
+    )
+    key2, value2 = y_shift(key0, 2), x_shift(value0, 2)
+    blocks = [key0, value0, key1, key3, value1, value3]
+    order = ((0, 0), (1, 0), (0, 1), (0, 3), (1, 1), (1, 3))
+    theirs = core_swap(jnp.concatenate(blocks, 0))
+    across = xh_swap(attended)
     low = low_rank(info, tokens, down_own, core_swap(down_own))
-    pieces = (key_piece(0, 0, 0, 0),) + value_pieces(0, 1, 0, 0)
-    first = main_product(info, tokens, pieces, [key0, value0])
-    own = core_swap(jnp.concatenate([key0, value0], 0))
-    pieces = (key_piece(1, 0, 0, 0),) + value_pieces(1, 0, 1024, 0)
-    second = main_product(info, tokens, pieces, [own])
-    key0, key1, key3, low, attended, first, second = barrier(
-        (key0, key1, key3, low, attended, first, second)
-    )
-    key2 = y_shift(key0, 2)
-    across = xh_swap(attended)
     pair = jnp.concatenate([low, z_flip(low, 1)], 0)
     lows = jnp.concatenate([pair, z_flip(pair, 2)], 0)
-    key1, key2, key3, value1, across, attended, lows = barrier(
-        (key1, key2, key3, value1, across, attended, lows)
+    pieces = tuple((kv, 0, n, 0, j) for n, (kv, j) in enumerate(order))
+    first = main_product(info, tokens, pieces, blocks)
+    pieces = tuple((kv, 1, 0, 1024 * n, j) for n, (kv, j) in enumerate(order))
+    second = main_product(info, tokens, pieces, [theirs])
+    key2, value2, first, second, across, lows, attended = barrier(
+        (key2, value2, first, second, across, lows, attended)
     )
     mine = ring(jnp.concatenate([attended, across], 0), y_shift)
-    theirs_k = core_swap(jnp.concatenate([key1, key2, key3], 0))
-    theirs_v = core_swap(value1)
-    pieces = tuple(key_piece(0, n, 0, n + 1) for n in range(3)) + value_pieces(0, 3, 0, 1)
-    third = main_product(info, tokens, pieces, [key1, key2, key3, value1])
-    pieces = tuple(key_piece(1, 0, 1024 * n, n + 1) for n in range(3)) + value_pieces(1, 1, 0, 1)
-    sums = [first, second, third]
-    same, other = finish(
-        info, tokens, pieces, [theirs_k, theirs_v], sums, lows, adapter_up_weight
-    )
+    last = [key2, value2, core_swap(key2), core_swap(value2)]
+    pieces = ((0, 0, 0, 0, 2), (1, 0, 1, 0, 2), (0, 1, 2, 0, 2), (1, 1, 3, 0, 2))
+    same, other = finish(info, tokens, pieces, last, [first, second], lows, adapter_up_weight)
 
     b0 = lax.ppermute(same, "pool", [(0, 1), (1, 0)])
     a0 = x_mirror(other)

time: 148 us -> 126 us (0.85)
  waiting for transfers between devices: 68.1 us -> 35 us
  starting transfers between devices: 42.6 us -> 51.8 us
  local copies, waits for them, and re-layouts: 3.97 us -> 6.83 us
    ppermute x3 -> x2, waiting for transfers between devices: 17.8 us -> 0.01 us  [xh_swap(): return lax.ppermute(value, 'xh', [(0, 1), (1, 0)])]
    ppermute x13, waiting for transfers between devices: 35.4 us -> 25.9 us  [y_shift(): return lax.ppermute(value, 'y', [(i, (i + k) % 4) for i in range(4)])]
    ppermute x0 -> x3, starting transfers between devices: none -> 5.96 us  [x_shift(): return lax.ppermute(value, ('pool', 'xh'), pairs)]
    ppermute x2, waiting for transfers between devices: 5.01 us -> 0.01 us  [x_mirror(): return lax.ppermute(value, ('pool', 'xh'), [(i, 3 - i) for i in range(4)])]
    ppermute x13, starting transfers between devices: 13.6 us -> 17.7 us  [y_shift(): return lax.ppermute(value, 'y', [(i, (i + k) % 4) for i in range(4)])]
    unnamed x37 -> x38, local copies, waits for them, and re-layouts: 2.41 us -> 5.21 us
    ppermute x3 -> x2, starting transfers between devices: 5.88 us -> 3.31 us  [xh_swap(): return lax.ppermute(value, 'xh', [(0, 1), (1, 0)])]
    ppermute x10, starting transfers between devices: 6.91 us -> 9.17 us  [core_swap(): return lax.ppermute(value, 'core', [(0, 1), (1, 0)])]
  transfers between devices with their start and end apart: 34 -> 36, of which waited for: 12 -> 9; matrix products, arithmetic and copies ran while one was open for 2% -> 2% of each run, Pallas kernels for 18% -> 21%
where the time goes in v7:
time: 126 us; the launch traced here: 125 us
  starting transfers between devices  51.8 us (41%)
  waiting for transfers between devices  35 us (28%)
  Pallas kernels  28.5 us (23%)
  local copies, waits for them, and re-layouts  6.83 us (5%)
  other arithmetic  1.95 us (2%)
  between operations  1.37 us (1%)
    ppermute x13, waiting for transfers between devices, y_shift(): return lax.ppermute(value, 'y', [(i, (i + k) % 4) for i in range(4)])  25.9 us
    ppermute x13, starting transfers between devices, y_shift(): return lax.ppermute(value, 'y', [(i, (i + k) % 4) for i in range(4)])  17.7 us
    ppermute x10, starting transfers between devices, core_swap(): return lax.ppermute(value, 'core', [(0, 1), (1, 0)])  9.17 us
    pallas_call x1, Pallas kernels, attend(): pl.pallas_call(functools.partial(attend_kernel, first * ROWS_STEP), grid_...  7.99 us
    ppermute x3, waiting for transfers between devices, z_shift(): return lax.ppermute(value, 'head', [(i, (i + k) % 4) for i in range(4)])  7.76 us
    ppermute x3, starting transfers between devices, x_shift(): return lax.ppermute(value, ('pool', 'xh'), pairs)  5.96 us
    ppermute x2, starting transfers between devices, x_mirror(): return lax.ppermute(value, ('pool', 'xh'), [(i, 3 - i) for i in range(4)])  5.67 us
    unnamed x38, local copies, waits for them, and re-layouts  5.21 us
  transfers between devices with their start and end apart: 36, of which 9 were waited for; matrix products, arithmetic and copies ran while one was open for 2% of the time, Pallas kernels for 21%

profile of v7, /device:TPU:1, one launch (start us, length us, event | category | flops | bytes accessed | tf_op | source)
XLA Modules:
  0.0 125.4 jit_solution(11180269572141717372)
XLA Ops:
  0.6 0.8 concatenate.32.info
  1.4 1.0 copy-done.3
  2.4 0.9 copy-done.4
  3.4 1.9 %pack.1 = (bf16[512,256]{1,0:T(8,128)(2,1)S(1)}, bf16[320,256]{1,0:T(8,128)(2,1)S(1)}) custom-call(s32[17]{0:T(128)S(1)} %concatenate.32.info, bf16[512,2,256]{2,1,0:T(2,128)(2,1)S(1)} %copy-done.3, bf16[512,256]{1,0:T(8,128)(2,1)S(1)} %copy-done.4), custom_call_target="tpu_custom_call" | custom-call | tf_op jit(solution)/shard_map/pack/pallas_call | solution.py:79
  5.3 3.4 %collective-permute-start = (bf16[512,256]{1,0:T(8,128)(2,1)S(1)}, bf16[512,256]{1,0:T(8,128)(2,1)S(1)}, u32[]{:S(2)}, u32[]{:S(2)}) collective-permute-start(bf16[512,256]{1,0:T(8,128)(2,1)S(1)} %get-tuple-element.55), channel_id=1, source_target_pairs={{0,96},{32,64},{64,32},{96,0},{1,97},{33,65},{65,33},{97,1},{2,98}... | collective-permute-start | bytes 786440 | tf_op jit(solution)/shard_map/ppermute | solution.py:31
  8.7 1.3 %collective-permute-start.1 = (bf16[320,256]{1,0:T(8,128)(2,1)S(1)}, bf16[320,256]{1,0:T(8,128)(2,1)S(1)}, u32[]{:S(2)}, u32[]{:S(2)}) collective-permute-start(bf16[320,256]{1,0:T(8,128)(2,1)S(1)} %get-tuple-element.57), channel_id=1, source_target_pairs={{0,8},{8,16},{16,24},{24,0},{1,9},{9,17},{17,25},{25,1},{2,10},{10... | collective-permute-start | bytes 491528 | tf_op jit(solution)/shard_map/ppermute | solution.py:43
  10.0 2.6 %collective-permute-start.2 = (bf16[320,256]{1,0:T(8,128)(2,1)S(1)}, bf16[320,256]{1,0:T(8,128)(2,1)S(1)}, u32[]{:S(2)}, u32[]{:S(2)}) collective-permute-start(bf16[320,256]{1,0:T(8,128)(2,1)S(1)} %get-tuple-element.57), channel_id=1, source_target_pairs={{0,16},{8,24},{16,0},{24,8},{1,17},{9,25},{17,1},{25,9},{2,18},{10... | collective-permute-start | bytes 491528 | tf_op jit(solution)/shard_map/ppermute | solution.py:43
  12.6 1.1 collective-permute-start.3
  13.7 1.1 collective-permute-done.1
  14.8 4.6 %collective-permute-done.2 = bf16[320,256]{1,0:T(8,128)(2,1)S(1)} collective-permute-done((bf16[320,256]{1,0:T(8,128)(2,1)S(1)}, bf16[320,256]{1,0:T(8,128)(2,1)S(1)}, u32[]{:S(2)}, u32[]{:S(2)}) %collective-permute-start.2) | collective-permute-done | bytes 163872 | tf_op jit(solution)/shard_map/ppermute | solution.py:43
  19.6 2.7 %collective-permute-start.7 = (bf16[1024,256]{1,0:T(8,128)(2,1)S(1)}, bf16[1024,256]{1,0:T(8,128)(2,1)S(1)}, u32[]{:S(2)}, u32[]{:S(2)}) collective-permute-start(bf16[1024,256]{1,0:T(8,128)(2,1)S(1)} %pad_maximum_fusion.1.refs_1_), channel_id=1, source_target_pairs={{0,96},{64,0},{32,64},{96,32},{1,97},{65,1},{33,65},{97,33},{2,98}... | collective-permute-start | bytes 1572872 | tf_op jit(solution)/shard_map/ppermute | solution.py:39
  22.3 1.4 %collective-permute-start.4 = (bf16[1024,256]{1,0:T(8,128)(2,1)S(1)}, bf16[1024,256]{1,0:T(8,128)(2,1)S(1)}, u32[]{:S(2)}, u32[]{:S(2)}) collective-permute-start(bf16[1024,256]{1,0:T(8,128)(2,1)S(1)} %constant_dynamic-update-slice_fusion.refs_0_), channel_id=1, source_target_pairs={{0,8},{8,16},{16,24},{24,0},{1,9},{9,17},{17,25},{25,1},{2,10},{10... | collective-permute-start | bytes 1572872 | tf_op jit(solution)/shard_map/ppermute | solution.py:43
  23.8 1.3 %collective-permute-start.5 = (bf16[1024,256]{1,0:T(8,128)(2,1)S(1)}, bf16[1024,256]{1,0:T(8,128)(2,1)S(1)}, u32[]{:S(2)}, u32[]{:S(2)}) collective-permute-start(bf16[1024,256]{1,0:T(8,128)(2,1)S(1)} %constant_dynamic-update-slice_fusion.refs_0_), channel_id=1, source_target_pairs={{0,24},{8,0},{16,8},{24,16},{1,25},{9,1},{17,9},{25,17},{2,26},{10... | collective-permute-start | bytes 1572872 | tf_op jit(solution)/shard_map/ppermute | solution.py:43
  25.3 2.8 %copy-done = bf16[48,128,2,256]{3,2,1,0:T(2,128)(2,1)S(1)} copy-done((bf16[48,128,2,256]{3,2,1,0:T(2,128)(2,1)S(1)}, bf16[48,128,2,256]{3,2,1,0:T(2,128)(2,1)}, u32[]{:S(2)}) %copy-start) | copy-done | bytes 6291480
  28.1 8.0 %attend.1 = bf16[48,16,128]{2,1,0:T(8,128)(2,1)S(1)} custom-call(s32[48]{0:T(128)S(1)} %copy-done.8, bf16[48,16,128]{2,1,0:T(8,128)(2,1)S(1)} %bitcast.33, bf16[48,128,2,256]{3,2,1,0:T(2,128)(2,1)S(1)} %copy-done, bf16[48,2,256]{2,1,0:T(2,128)(2,1)S(1)} %copy-done.7), custom_call_target="tpu_custom_call" | custom-call | tf_op jit(solution)/shard_map/attend/pallas_call | solution.py:134
  36.5 3.1 %collective-permute-start.11 = (bf16[6144,256]{1,0:T(8,128)(2,1)S(1)}, bf16[6144,256]{1,0:T(8,128)(2,1)S(1)}, u32[]{:S(2)}, u32[]{:S(2)}) collective-permute-start(bf16[6144,256]{1,0:T(8,128)(2,1)S(1)} %constant_dynamic-update-slice_fusion.7), channel_id=1, source_target_pairs={{0,4},{4,0},{1,5},{5,1},{2,6},{6,2},{3,7},{7,3},{8,12},{12,8},{9,1... | collective-permute-start | bytes 9437192 | tf_op jit(solution)/shard_map/ppermute | solution.py:59
  39.6 3.2 %collective-permute-start.10 = (bf16[1024,256]{1,0:T(8,128)(2,1)S(1)}, bf16[1024,256]{1,0:T(8,128)(2,1)S(1)}, u32[]{:S(2)}, u32[]{:S(2)}) collective-permute-start(bf16[1024,256]{1,0:T(8,128)(2,1)S(1)} %pad_maximum_fusion.1.refs_1_), channel_id=1, source_target_pairs={{0,32},{64,96},{32,0},{96,64},{1,33},{65,97},{33,1},{97,65},{2,34}... | collective-permute-start | bytes 1572872 | tf_op jit(solution)/shard_map/ppermute | solution.py:39
  42.8 1.1 collective-permute-start.9
  43.9 1.3 %collective-permute-done.13.other_ref = bf16[512,256]{1,0:T(8,128)(2,1)S(1)} collective-permute-done((bf16[512,256]{1,0:T(8,128)(2,1)S(1)}, bf16[512,256]{1,0:T(8,128)(2,1)S(1)}, u32[]{:S(2)}, u32[]{:S(2)}) %collective-permute-start.13) | collective-permute-done | bytes 262176 | tf_op jit(solution)/shard_map/ppermute | solution.py:59
  45.2 1.3 %low_rank.1 = f32[32,128]{1,0:T(8,128)S(1)} custom-call(s32[17]{0:T(128)S(1)} %concatenate.32.info, bf16[512,8192]{1,0:T(8,128)(2,1)S(1)} %bitcast.28, bf16[512,256]{1,0:T(8,128)(2,1)S(1)} %constant_dynamic-update-slice_fusion.2.own_ref, bf16[512,256]{1,0:T(8,128)(2,1)S(1)} %collective-permute-done.13.other_ref), custom_call_target="tpu_custom_call" | custom-call | tf_op jit(solution)/shard_map/low_rank/pallas_call | solution.py:187
  46.5 1.7 %collective-permute-start.14 = (f32[32,128]{1,0:T(8,128)S(1)}, f32[32,128]{1,0:T(8,128)S(1)}, u32[]{:S(2)}, u32[]{:S(2)}) collective-permute-start(f32[32,128]{1,0:T(8,128)S(1)} %low_rank.1), channel_id=1, source_target_pairs={{0,1},{1,0},{2,3},{3,2},{4,5},{5,4},{6,7},{7,6},{8,9},{9,8},{10,11... | collective-permute-start | bytes 49160 | tf_op jit(solution)/shard_map/ppermute | solution.py:55
  48.2 3.2 %collective-permute-start.12 = (bf16[48,2048]{1,0:T(8,128)(2,1)S(1)}, bf16[48,2048]{1,0:T(8,128)(2,1)S(1)}, u32[]{:S(2)}, u32[]{:S(2)}) collective-permute-start(bf16[48,2048]{1,0:T(8,128)(2,1)S(1)} %bitcast.40), channel_id=1, source_target_pairs={{0,32},{32,0},{1,33},{33,1},{2,34},{34,2},{3,35},{35,3},{4,36},{36... | collective-permute-start | bytes 589832 | tf_op jit(solution)/shard_map/ppermute | solution.py:47
  51.5 3.3 %collective-permute-start.15 = (f32[64,128]{1,0:T(8,128)S(1)}, f32[64,128]{1,0:T(8,128)S(1)}, u32[]{:S(2)}, u32[]{:S(2)}) collective-permute-start(f32[64,128]{1,0:T(8,128)S(1)} %pad_maximum_fusion.4), channel_id=1, source_target_pairs={{0,2},{1,3},{2,0},{3,1},{4,6},{5,7},{6,4},{7,5},{8,10},{9,11},{10,... | collective-permute-start | bytes 98312 | tf_op jit(solution)/shard_map/ppermute | solution.py:55
  54.8 2.4 %main_product.2 = (f32[512,256]{1,0:T(8,128)S(1)}, f32[512,256]{1,0:T(8,128)S(1)}) custom-call(s32[17]{0:T(128)S(1)} %concatenate.32.info, bf16[512,8192]{1,0:T(8,128)(2,1)S(1)} %bitcast.29, bf16[1024,256]{1,0:T(8,128)(2,1)S(1)} %constant_dynamic-update-slice_fusion.refs_0_, bf16[1024,256]{1,0:T(8,128)(2,1)S(1)} %pad_maximum_fusion.1.refs_1_, ...), custom_call_target="tpu_custom_call" | custom-call | tf_op jit(solution)/shard_map/main_product/pallas_call | solution.py:230
  57.2 2.3 %main_product.3 = (f32[512,256]{1,0:T(8,128)S(1)}, f32[512,256]{1,0:T(8,128)S(1)}) custom-call(s32[17]{0:T(128)S(1)} %concatenate.32.info, bf16[512,8192]{1,0:T(8,128)(2,1)S(1)} %bitcast.30, bf16[6144,256]{1,0:T(8,128)(2,1)S(1)} %collective-permute-done.11.refs_0_), custom_call_target="tpu_custom_call" | custom-call | tf_op jit(solution)/shard_map/main_product/pallas_call | solution.py:230
  59.6 1.3 %collective-permute-start.16 = (bf16[1024,256]{1,0:T(8,128)(2,1)S(1)}, bf16[1024,256]{1,0:T(8,128)(2,1)S(1)}, u32[]{:S(2)}, u32[]{:S(2)}) collective-permute-start(bf16[1024,256]{1,0:T(8,128)(2,1)S(1)} %collective-permute-done.9.refs_0_), channel_id=1, source_target_pairs={{0,4},{4,0},{1,5},{5,1},{2,6},{6,2},{3,7},{7,3},{8,12},{12,8},{9,1... | collective-permute-start | bytes 1572872 | tf_op jit(solution)/shard_map/ppermute | solution.py:59
  61.3 1.7 %collective-permute-start.21 = (bf16[96,2048]{1,0:T(8,128)(2,1)S(1)}, bf16[96,2048]{1,0:T(8,128)(2,1)S(1)}, u32[]{:S(2)}, u32[]{:S(2)}) collective-permute-start(bf16[96,2048]{1,0:T(8,128)(2,1)S(1)} %constant_dynamic-update-slice_fusion.13), channel_id=1, source_target_pairs={{0,16},{8,24},{16,0},{24,8},{1,17},{9,25},{17,1},{25,9},{2,18},{10... | collective-permute-start | bytes 1179656 | tf_op jit(solution)/shard_map/ppermute | solution.py:43
  63.0 1.4 %collective-permute-start.22 = (bf16[96,2048]{1,0:T(8,128)(2,1)S(1)}, bf16[96,2048]{1,0:T(8,128)(2,1)S(1)}, u32[]{:S(2)}, u32[]{:S(2)}) collective-permute-start(bf16[96,2048]{1,0:T(8,128)(2,1)S(1)} %constant_dynamic-update-slice_fusion.13), channel_id=1, source_target_pairs={{0,24},{8,0},{16,8},{24,16},{1,25},{9,1},{17,9},{25,17},{2,26},{10... | collective-permute-start | bytes 1179656 | tf_op jit(solution)/shard_map/ppermute | solution.py:43
  64.4 3.7 %finish.1 = (bf16[3,128,2,256]{3,2,1,0:T(2,128)(2,1)S(1)}, bf16[3,128,2,256]{3,2,1,0:T(2,128)(2,1)S(1)}) custom-call(s32[17]{0:T(128)S(1)} %concatenate.32.info, bf16[512,8192]{1,0:T(8,128)(2,1)S(1)} %bitcast.31, bf16[1024,256]{1,0:T(8,128)(2,1)S(1)} %collective-permute-done.9.refs_0_, bf16[1024,256]{1,0:T(8,128)(2,1)S(1)} %collective-permute-done.10.refs_1_, ...), custom_call_target="tpu_custom_call" | custom-call | tf_op jit(solution)/shard_map/finish/pallas_call | solution.py:281
  68.3 2.3 %collective-permute-start.19 = (bf16[3,128,2,256]{3,2,1,0:T(2,128)(2,1)S(1)}, bf16[3,128,2,256]{3,2,1,0:T(2,128)(2,1)S(1)}, u32[]{:S(2)}, u32[]{:S(2)}) collective-permute-start(bf16[3,128,2,256]{3,2,1,0:T(2,128)(2,1)S(1)} %get-tuple-element.82), channel_id=1, source_target_pairs={{0,96},{32,64},{64,32},{96,0},{1,97},{33,65},{65,33},{97,1},{2,98}... | collective-permute-start | bytes 1179656 | tf_op jit(solution)/shard_map/ppermute | solution.py:31
  70.6 3.1 %collective-permute-done.20 = bf16[96,2048]{1,0:T(8,128)(2,1)S(1)} collective-permute-done((bf16[96,2048]{1,0:T(8,128)(2,1)S(1)}, bf16[96,2048]{1,0:T(8,128)(2,1)S(1)}, u32[]{:S(2)}, u32[]{:S(2)}) %collective-permute-start.20) | collective-permute-done | bytes 393248 | tf_op jit(solution)/shard_map/ppermute | solution.py:43
  73.6 6.7 %collective-permute-done.21 = bf16[96,2048]{1,0:T(8,128)(2,1)S(1)} collective-permute-done((bf16[96,2048]{1,0:T(8,128)(2,1)S(1)}, bf16[96,2048]{1,0:T(8,128)(2,1)S(1)}, u32[]{:S(2)}, u32[]{:S(2)}) %collective-permute-start.21) | collective-permute-done | bytes 393248 | tf_op jit(solution)/shard_map/ppermute | solution.py:43
  80.3 1.2 collective-permute-done.22
  81.7 1.6 %collective-permute-start.25 = (bf16[384,2048]{1,0:T(8,128)(2,1)S(1)}, bf16[384,2048]{1,0:T(8,128)(2,1)S(1)}, u32[]{:S(2)}, u32[]{:S(2)}) collective-permute-start(bf16[384,2048]{1,0:T(8,128)(2,1)S(1)} %constant_dynamic-update-slice_fusion.15.refs_0_), channel_id=1, source_target_pairs={{0,4},{4,0},{1,5},{5,1},{2,6},{6,2},{3,7},{7,3},{8,12},{12,8},{9,1... | collective-permute-start | bytes 4718600 | tf_op jit(solution)/shard_map/ppermute | solution.py:59
  83.3 1.1 pad_maximum_fusion.refs_0_
  84.9 2.2 %collective-permute-start.24 = (bf16[2,3,128,2,256]{4,3,2,1,0:T(2,128)(2,1)S(1)}, bf16[2,3,128,2,256]{4,3,2,1,0:T(2,128)(2,1)S(1)}, u32[]{:S(2)}, u32[]{:S(2)}) collective-permute-start(bf16[2,3,128,2,256]{4,3,2,1,0:T(2,128)(2,1)S(1)} %pad_maximum_fusion.refs_0_), channel_id=1, source_target_pairs={{0,24},{8,0},{16,8},{24,16},{1,25},{9,1},{17,9},{25,17},{2,26},{10... | collective-permute-start | bytes 2359304 | tf_op jit(solution)/shard_map/ppermute | solution.py:43
  87.4 5.2 %project.1 = (bf16[192,512]{1,0:T(8,128)(2,1)S(1)}, bf16[192,512]{1,0:T(8,128)(2,1)S(1)}, bf16[192,512]{1,0:T(8,128)(2,1)S(1)}, bf16[192,512]{1,0:T(8,128)(2,1)S(1)}) custom-call(s32[17]{0:T(128)S(1)} %concatenate.32.info, s32[768,1]{1,0:T(8,128)S(1)} %broadcast_in_dim.20.keep, bf16[128,2048]{1,0:T(8,128)(2,1)S(1)} %bitcast.34, ...), custom_call_target="tpu_custom_call" | custom-call | tf_op jit(solution)/shard_map/project/pallas_call | solution.py:398
  93.3 3.3 %collective-permute-start.27 = (bf16[192,512]{1,0:T(8,128)(2,1)S(1)}, bf16[192,512]{1,0:T(8,128)(2,1)S(1)}, u32[]{:S(2)}, u32[]{:S(2)}) collective-permute-start(bf16[192,512]{1,0:T(8,128)(2,1)S(1)} %get-tuple-element.93), channel_id=1, source_target_pairs={{0,2},{1,3},{2,0},{3,1},{4,6},{5,7},{6,4},{7,5},{8,10},{9,11},{10,... | collective-permute-start | bytes 589832 | tf_op jit(solution)/shard_map/ppermute | solution.py:51
  96.6 0.9 collective-permute-start.28
  97.4 2.5 %collective-permute-done.26 = bf16[192,512]{1,0:T(8,128)(2,1)S(1)} collective-permute-done((bf16[192,512]{1,0:T(8,128)(2,1)S(1)}, bf16[192,512]{1,0:T(8,128)(2,1)S(1)}, u32[]{:S(2)}, u32[]{:S(2)}) %collective-permute-start.26) | collective-permute-done | bytes 196640 | tf_op jit(solution)/shard_map/ppermute | solution.py:51
  99.9 5.2 %collective-permute-done.27 = bf16[192,512]{1,0:T(8,128)(2,1)S(1)} collective-permute-done((bf16[192,512]{1,0:T(8,128)(2,1)S(1)}, bf16[192,512]{1,0:T(8,128)(2,1)S(1)}, u32[]{:S(2)}, u32[]{:S(2)}) %collective-permute-start.27) | collective-permute-done | bytes 196640 | tf_op jit(solution)/shard_map/ppermute | solution.py:51
  105.2 0.8 add_convert_fusion
  106.0 1.4 %collective-permute-start.31 = (bf16[2,3,128,2,256]{4,3,2,1,0:T(2,128)(2,1)S(1)}, bf16[2,3,128,2,256]{4,3,2,1,0:T(2,128)(2,1)S(1)}, u32[]{:S(2)}, u32[]{:S(2)}) collective-permute-start(bf16[2,3,128,2,256]{4,3,2,1,0:T(2,128)(2,1)S(1)} %pad_maximum_fusion.refs_0_), channel_id=1, source_target_pairs={{0,4},{4,0},{1,5},{5,1},{2,6},{6,2},{3,7},{7,3},{8,12},{12,8},{9,1... | collective-permute-start | bytes 2359304 | tf_op jit(solution)/shard_map/ppermute | solution.py:59
  108.6 2.7 %collective-permute-start.30 = (bf16[3,128,2,256]{3,2,1,0:T(2,128)(2,1)S(1)}, bf16[3,128,2,256]{3,2,1,0:T(2,128)(2,1)S(1)}, u32[]{:S(2)}, u32[]{:S(2)}) collective-permute-start(bf16[3,128,2,256]{3,2,1,0:T(2,128)(2,1)S(1)} %slice_bitcast_fusion), channel_id=1, source_target_pairs={{0,24},{8,0},{16,8},{24,16},{1,25},{9,1},{17,9},{25,17},{2,26},{10... | collective-permute-start | bytes 1179656 | tf_op jit(solution)/shard_map/ppermute | solution.py:43
  111.3 9.2 %collective-permute-done.29 = bf16[3,128,2,256]{3,2,1,0:T(2,128)(2,1)S(1)} collective-permute-done((bf16[3,128,2,256]{3,2,1,0:T(2,128)(2,1)S(1)}, bf16[3,128,2,256]{3,2,1,0:T(2,128)(2,1)S(1)}, u32[]{:S(2)}, u32[]{:S(2)}) %collective-permute-start.29) | collective-permute-done | bytes 393248 | tf_op jit(solution)/shard_map/ppermute | solution.py:43
  120.5 0.9 collective-permute-start.34
  121.5 2.9 %place.2.refs_4_ = bf16[1,2,2048,2,256]{4,3,2,1,0:T(2,128)(2,1)} custom-call(s32[17]{0:T(128)S(1)} %concatenate.32.info, bf16[2,3,128,2,256]{4,3,2,1,0:T(2,128)(2,1)S(1)} %pad_maximum_fusion.refs_0_, bf16[2,3,128,2,256]{4,3,2,1,0:T(2,128)(2,1)S(1)} %collective-permute-done.23.refs_1_, bf16[2,3,128,2,256]{4,3,2,1,0:T(2,128)(2,1)S(1)} %collective-permute-done.24.refs_2_, ...), custom_call_target="tpu_custom_call" | custom-call | tf_op jit(solution)/shard_map/place/pallas_call | solution.py:356
  124.4 0.9 place.3
  (95 shorter events, 4.1 us)
Async XLA Ops:
  0.6 24.6 %copy-start.8 = (s32[48]{0:T(128)S(1)}, s32[48]{0:T(128)}, u32[]{:S(2)}) copy-start(s32[48]{0:T(128)} %len_ref) | copy-start | bytes 580
  1.4 1.0 copy-start.3
  3.4 21.8 %copy-start.9 = (bf16[48,2048]{1,0:T(8,128)(2,1)S(1)}, bf16[48,2048]{1,0:T(8,128)(2,1)}, u32[]{:S(2)}) copy-start(bf16[48,2048]{1,0:T(8,128)(2,1)} %param.20) | copy-start | bytes 589828
  3.4 21.9 %copy-start.7 = (bf16[48,2,256]{2,1,0:T(2,128)(2,1)S(1)}, bf16[48,2,256]{2,1,0:T(2,128)(2,1)}, u32[]{:S(2)}) copy-start(bf16[48,2,256]{2,1,0:T(2,128)(2,1)} %cur_ref.1) | copy-start | bytes 147460
  5.3 14.1 %collective-permute-start = (bf16[512,256]{1,0:T(8,128)(2,1)S(1)}, bf16[512,256]{1,0:T(8,128)(2,1)S(1)}, u32[]{:S(2)}, u32[]{:S(2)}) collective-permute-start(bf16[512,256]{1,0:T(8,128)(2,1)S(1)} %get-tuple-element.55), channel_id=1, source_target_pairs={{0,96},{32,64},{64,32},{96,0},{1,97},{33,65},{65,33},{97,1},{2,98}... | collective-permute-start | bytes 786440 | tf_op jit(solution)/shard_map/ppermute | solution.py:31
  8.7 6.1 %collective-permute-start.1 = (bf16[320,256]{1,0:T(8,128)(2,1)S(1)}, bf16[320,256]{1,0:T(8,128)(2,1)S(1)}, u32[]{:S(2)}, u32[]{:S(2)}) collective-permute-start(bf16[320,256]{1,0:T(8,128)(2,1)S(1)} %get-tuple-element.57), channel_id=1, source_target_pairs={{0,8},{8,16},{16,24},{24,0},{1,9},{9,17},{17,25},{25,1},{2,10},{10... | collective-permute-start | bytes 491528 | tf_op jit(solution)/shard_map/ppermute | solution.py:43
  10.0 9.4 %collective-permute-start.2 = (bf16[320,256]{1,0:T(8,128)(2,1)S(1)}, bf16[320,256]{1,0:T(8,128)(2,1)S(1)}, u32[]{:S(2)}, u32[]{:S(2)}) collective-permute-start(bf16[320,256]{1,0:T(8,128)(2,1)S(1)} %get-tuple-element.57), channel_id=1, source_target_pairs={{0,16},{8,24},{16,0},{24,8},{1,17},{9,25},{17,1},{25,9},{2,18},{10... | collective-permute-start | bytes 491528 | tf_op jit(solution)/shard_map/ppermute | solution.py:43
  12.6 6.8 %collective-permute-start.3 = (bf16[320,256]{1,0:T(8,128)(2,1)S(1)}, bf16[320,256]{1,0:T(8,128)(2,1)S(1)}, u32[]{:S(2)}, u32[]{:S(2)}) collective-permute-start(bf16[320,256]{1,0:T(8,128)(2,1)S(1)} %get-tuple-element.57), channel_id=1, source_target_pairs={{0,24},{8,0},{16,8},{24,16},{1,25},{9,1},{17,9},{25,17},{2,26},{10... | collective-permute-start | bytes 491528 | tf_op jit(solution)/shard_map/ppermute | solution.py:43
  19.5 16.6 %collective-permute-start.6 = (bf16[1024,256]{1,0:T(8,128)(2,1)S(1)}, bf16[1024,256]{1,0:T(8,128)(2,1)S(1)}, u32[]{:S(2)}, u32[]{:S(2)}) collective-permute-start(bf16[1024,256]{1,0:T(8,128)(2,1)S(1)} %pad_maximum_fusion.1.refs_1_), channel_id=1, source_target_pairs={{0,64},{64,32},{32,96},{96,0},{1,65},{65,33},{33,97},{97,1},{2,66}... | collective-permute-start | bytes 1572872 | tf_op jit(solution)/shard_map/ppermute | solution.py:39
  19.6 16.6 %collective-permute-start.7 = (bf16[1024,256]{1,0:T(8,128)(2,1)S(1)}, bf16[1024,256]{1,0:T(8,128)(2,1)S(1)}, u32[]{:S(2)}, u32[]{:S(2)}) collective-permute-start(bf16[1024,256]{1,0:T(8,128)(2,1)S(1)} %pad_maximum_fusion.1.refs_1_), channel_id=1, source_target_pairs={{0,96},{64,0},{32,64},{96,32},{1,97},{65,1},{33,65},{97,33},{2,98}... | collective-permute-start | bytes 1572872 | tf_op jit(solution)/shard_map/ppermute | solution.py:39
  22.3 22.9 %slice-start = ((s8[8388608]{0:T(1024)(128)(4,1)}), s8[4194304]{0:T(1024)(128)(4,1)S(1)}, s32[]{:S(2)}) async-start(s8[8388608]{0:T(1024)(128)(4,1)} %bitcast.26), calls=%async_computation | async-start | bytes 8388608
  22.3 13.9 %collective-permute-start.4 = (bf16[1024,256]{1,0:T(8,128)(2,1)S(1)}, bf16[1024,256]{1,0:T(8,128)(2,1)S(1)}, u32[]{:S(2)}, u32[]{:S(2)}) collective-permute-start(bf16[1024,256]{1,0:T(8,128)(2,1)S(1)} %constant_dynamic-update-slice_fusion.refs_0_), channel_id=1, source_target_pairs={{0,8},{8,16},{16,24},{24,0},{1,9},{9,17},{17,25},{25,1},{2,10},{10... | collective-permute-start | bytes 1572872 | tf_op jit(solution)/shard_map/ppermute | solution.py:43
  23.8 12.4 %collective-permute-start.5 = (bf16[1024,256]{1,0:T(8,128)(2,1)S(1)}, bf16[1024,256]{1,0:T(8,128)(2,1)S(1)}, u32[]{:S(2)}, u32[]{:S(2)}) collective-permute-start(bf16[1024,256]{1,0:T(8,128)(2,1)S(1)} %constant_dynamic-update-slice_fusion.refs_0_), channel_id=1, source_target_pairs={{0,24},{8,0},{16,8},{24,16},{1,25},{9,1},{17,9},{25,17},{2,26},{10... | collective-permute-start | bytes 1572872 | tf_op jit(solution)/shard_map/ppermute | solution.py:43
  25.1 11.0 %collective-permute-start.8 = (bf16[256,256]{1,0:T(8,128)(2,1)S(1)}, bf16[256,256]{1,0:T(8,128)(2,1)S(1)}, u32[]{:S(2)}, u32[]{:S(2)}) collective-permute-start(bf16[256,256]{1,0:T(8,128)(2,1)S(1)} %pad_maximum_fusion.2), channel_id=1, source_target_pairs={{0,32},{32,0},{1,33},{33,1},{2,34},{34,2},{3,35},{35,3},{4,36},{36... | collective-permute-start | bytes 393224 | tf_op jit(solution)/shard_map/ppermute | solution.py:47
  25.3 2.8 %copy-start = (bf16[48,128,2,256]{3,2,1,0:T(2,128)(2,1)S(1)}, bf16[48,128,2,256]{3,2,1,0:T(2,128)(2,1)}, u32[]{:S(2)}) copy-start(bf16[48,128,2,256]{3,2,1,0:T(2,128)(2,1)} %kv_ref.1) | copy-start | bytes 18874372
  28.1 17.1 %slice-start.1 = ((s8[8388608]{0:T(1024)(128)(4,1)}), s8[4194304]{0:T(1024)(128)(4,1)S(1)}, s32[]{:S(2)}) async-start(s8[8388608]{0:T(1024)(128)(4,1)} %bitcast.26), calls=%async_computation.1 | async-start | bytes 8388608
  36.5 20.7 %collective-permute-start.11 = (bf16[6144,256]{1,0:T(8,128)(2,1)S(1)}, bf16[6144,256]{1,0:T(8,128)(2,1)S(1)}, u32[]{:S(2)}, u32[]{:S(2)}) collective-permute-start(bf16[6144,256]{1,0:T(8,128)(2,1)S(1)} %constant_dynamic-update-slice_fusion.7), channel_id=1, source_target_pairs={{0,4},{4,0},{1,5},{5,1},{2,6},{6,2},{3,7},{7,3},{8,12},{12,8},{9,1... | collective-permute-start | bytes 9437192 | tf_op jit(solution)/shard_map/ppermute | solution.py:59
  39.5 5.7 %collective-permute-start.13 = (bf16[512,256]{1,0:T(8,128)(2,1)S(1)}, bf16[512,256]{1,0:T(8,128)(2,1)S(1)}, u32[]{:S(2)}, u32[]{:S(2)}) collective-permute-start(bf16[512,256]{1,0:T(8,128)(2,1)S(1)} %constant_dynamic-update-slice_fusion.2.own_ref), channel_id=1, source_target_pairs={{0,4},{4,0},{1,5},{5,1},{2,6},{6,2},{3,7},{7,3},{8,12},{12,8},{9,1... | collective-permute-start | bytes 786440 | tf_op jit(solution)/shard_map/ppermute | solution.py:59
  39.6 20.0 %collective-permute-start.10 = (bf16[1024,256]{1,0:T(8,128)(2,1)S(1)}, bf16[1024,256]{1,0:T(8,128)(2,1)S(1)}, u32[]{:S(2)}, u32[]{:S(2)}) collective-permute-start(bf16[1024,256]{1,0:T(8,128)(2,1)S(1)} %pad_maximum_fusion.1.refs_1_), channel_id=1, source_target_pairs={{0,32},{64,96},{32,0},{96,64},{1,33},{65,97},{33,1},{97,65},{2,34}... | collective-permute-start | bytes 1572872 | tf_op jit(solution)/shard_map/ppermute | solution.py:39
  42.8 16.7 %collective-permute-start.9 = (bf16[1024,256]{1,0:T(8,128)(2,1)S(1)}, bf16[1024,256]{1,0:T(8,128)(2,1)S(1)}, u32[]{:S(2)}, u32[]{:S(2)}) collective-permute-start(bf16[1024,256]{1,0:T(8,128)(2,1)S(1)} %constant_dynamic-update-slice_fusion.refs_0_), channel_id=1, source_target_pairs={{0,16},{8,24},{16,0},{24,8},{1,17},{9,25},{17,1},{25,9},{2,18},{10... | collective-permute-start | bytes 1572872 | tf_op jit(solution)/shard_map/ppermute | solution.py:43
  46.5 4.9 %collective-permute-start.14 = (f32[32,128]{1,0:T(8,128)S(1)}, f32[32,128]{1,0:T(8,128)S(1)}, u32[]{:S(2)}, u32[]{:S(2)}) collective-permute-start(f32[32,128]{1,0:T(8,128)S(1)} %low_rank.1), channel_id=1, source_target_pairs={{0,1},{1,0},{2,3},{3,2},{4,5},{5,4},{6,7},{7,6},{8,9},{9,8},{10,11... | collective-permute-start | bytes 49160 | tf_op jit(solution)/shard_map/ppermute | solution.py:55
  48.2 11.3 %collective-permute-start.12 = (bf16[48,2048]{1,0:T(8,128)(2,1)S(1)}, bf16[48,2048]{1,0:T(8,128)(2,1)S(1)}, u32[]{:S(2)}, u32[]{:S(2)}) collective-permute-start(bf16[48,2048]{1,0:T(8,128)(2,1)S(1)} %bitcast.40), channel_id=1, source_target_pairs={{0,32},{32,0},{1,33},{33,1},{2,34},{34,2},{3,35},{35,3},{4,36},{36... | collective-permute-start | bytes 589832 | tf_op jit(solution)/shard_map/ppermute | solution.py:47
  51.5 5.7 %collective-permute-start.15 = (f32[64,128]{1,0:T(8,128)S(1)}, f32[64,128]{1,0:T(8,128)S(1)}, u32[]{:S(2)}, u32[]{:S(2)}) collective-permute-start(f32[64,128]{1,0:T(8,128)S(1)} %pad_maximum_fusion.4), channel_id=1, source_target_pairs={{0,2},{1,3},{2,0},{3,1},{4,6},{5,7},{6,4},{7,5},{8,10},{9,11},{10,... | collective-permute-start | bytes 98312 | tf_op jit(solution)/shard_map/ppermute | solution.py:55
  57.2 7.2 %copy-start.5 = (bf16[8,2,16,256]{3,2,1,0:T(8,128)(2,1)S(1)}, bf16[8,2,16,256]{3,2,1,0:T(8,128)(2,1)}, u32[]{:S(2)}) copy-start(bf16[8,2,16,256]{3,2,1,0:T(8,128)(2,1)} %refs_9_.1) | copy-start | bytes 393220
  59.6 4.8 %collective-permute-start.16 = (bf16[1024,256]{1,0:T(8,128)(2,1)S(1)}, bf16[1024,256]{1,0:T(8,128)(2,1)S(1)}, u32[]{:S(2)}, u32[]{:S(2)}) collective-permute-start(bf16[1024,256]{1,0:T(8,128)(2,1)S(1)} %collective-permute-done.9.refs_0_), channel_id=1, source_target_pairs={{0,4},{4,0},{1,5},{5,1},{2,6},{6,2},{3,7},{7,3},{8,12},{12,8},{9,1... | collective-permute-start | bytes 1572872 | tf_op jit(solution)/shard_map/ppermute | solution.py:59
  60.9 3.5 %collective-permute-start.17 = (bf16[1024,256]{1,0:T(8,128)(2,1)S(1)}, bf16[1024,256]{1,0:T(8,128)(2,1)S(1)}, u32[]{:S(2)}, u32[]{:S(2)}) collective-permute-start(bf16[1024,256]{1,0:T(8,128)(2,1)S(1)} %collective-permute-done.10.refs_1_), channel_id=1, source_target_pairs={{0,4},{4,0},{1,5},{5,1},{2,6},{6,2},{3,7},{7,3},{8,12},{12,8},{9,1... | collective-permute-start | bytes 1572872 | tf_op jit(solution)/shard_map/ppermute | solution.py:59
  61.0 12.6 %collective-permute-start.20 = (bf16[96,2048]{1,0:T(8,128)(2,1)S(1)}, bf16[96,2048]{1,0:T(8,128)(2,1)S(1)}, u32[]{:S(2)}, u32[]{:S(2)}) collective-permute-start(bf16[96,2048]{1,0:T(8,128)(2,1)S(1)} %constant_dynamic-update-slice_fusion.13), channel_id=1, source_target_pairs={{0,8},{8,16},{16,24},{24,0},{1,9},{9,17},{17,25},{25,1},{2,10},{10... | collective-permute-start | bytes 1179656 | tf_op jit(solution)/shard_map/ppermute | solution.py:43
  61.3 19.0 %collective-permute-start.21 = (bf16[96,2048]{1,0:T(8,128)(2,1)S(1)}, bf16[96,2048]{1,0:T(8,128)(2,1)S(1)}, u32[]{:S(2)}, u32[]{:S(2)}) collective-permute-start(bf16[96,2048]{1,0:T(8,128)(2,1)S(1)} %constant_dynamic-update-slice_fusion.13), channel_id=1, source_target_pairs={{0,16},{8,24},{16,0},{24,8},{1,17},{9,25},{17,1},{25,9},{2,18},{10... | collective-permute-start | bytes 1179656 | tf_op jit(solution)/shard_map/ppermute | solution.py:43
  63.0 18.5 %collective-permute-start.22 = (bf16[96,2048]{1,0:T(8,128)(2,1)S(1)}, bf16[96,2048]{1,0:T(8,128)(2,1)S(1)}, u32[]{:S(2)}, u32[]{:S(2)}) collective-permute-start(bf16[96,2048]{1,0:T(8,128)(2,1)S(1)} %constant_dynamic-update-slice_fusion.13), channel_id=1, source_target_pairs={{0,24},{8,0},{16,8},{24,16},{1,25},{9,1},{17,9},{25,17},{2,26},{10... | collective-permute-start | bytes 1179656 | tf_op jit(solution)/shard_map/ppermute | solution.py:43
  68.1 19.0 %copy-start.10 = (s32[768]{0:T(1024)S(1)}, s32[768]{0:T(1024)}, u32[]{:S(2)}) copy-start(s32[768]{0:T(1024)} %param.24) | copy-start | bytes 9220
  68.1 19.2 %copy-start.1 = (bf16[2048,512]{1,0:T(8,128)(2,1)S(1)}, bf16[2048,512]{1,0:T(8,128)(2,1)}, u32[]{:S(2)}) copy-start(bf16[2048,512]{1,0:T(8,128)(2,1)} %w_ref.3) | copy-start | bytes 6291460
  68.2 19.2 %copy-start.2 = (bf16[2048,8,16]{0,2,1:T(8,128)(2,1)S(1)}, bf16[2048,8,16]{0,2,1:T(8,128)(2,1)}, u32[]{:S(2)}) copy-start(bf16[2048,8,16]{0,2,1:T(8,128)(2,1)} %param.26) | copy-start | bytes 1572868
  68.2 19.2 %copy-start.6 = (bf16[8,16,512]{2,1,0:T(8,128)(2,1)S(1)}, bf16[8,16,512]{2,1,0:T(8,128)(2,1)}, u32[]{:S(2)}) copy-start(bf16[8,16,512]{2,1,0:T(8,128)(2,1)} %param.27) | copy-start | bytes 393220
  68.2 13.3 %collective-permute-start.18 = (bf16[3,128,2,256]{3,2,1,0:T(2,128)(2,1)S(1)}, bf16[3,128,2,256]{3,2,1,0:T(2,128)(2,1)S(1)}, u32[]{:S(2)}, u32[]{:S(2)}) collective-permute-start(bf16[3,128,2,256]{3,2,1,0:T(2,128)(2,1)S(1)} %get-tuple-element.81), channel_id=1, source_target_pairs={{0,64},{64,0},{1,65},{65,1},{2,66},{66,2},{3,67},{67,3},{4,68},{68... | collective-permute-start | bytes 1179656 | tf_op jit(solution)/shard_map/ppermute | solution.py:475
  68.3 13.2 %collective-permute-start.19 = (bf16[3,128,2,256]{3,2,1,0:T(2,128)(2,1)S(1)}, bf16[3,128,2,256]{3,2,1,0:T(2,128)(2,1)S(1)}, u32[]{:S(2)}, u32[]{:S(2)}) collective-permute-start(bf16[3,128,2,256]{3,2,1,0:T(2,128)(2,1)S(1)} %get-tuple-element.82), channel_id=1, source_target_pairs={{0,96},{32,64},{64,32},{96,0},{1,97},{33,65},{65,33},{97,1},{2,98}... | collective-permute-start | bytes 1179656 | tf_op jit(solution)/shard_map/ppermute | solution.py:31
  81.7 5.7 %collective-permute-start.25 = (bf16[384,2048]{1,0:T(8,128)(2,1)S(1)}, bf16[384,2048]{1,0:T(8,128)(2,1)S(1)}, u32[]{:S(2)}, u32[]{:S(2)}) collective-permute-start(bf16[384,2048]{1,0:T(8,128)(2,1)S(1)} %constant_dynamic-update-slice_fusion.15.refs_0_), channel_id=1, source_target_pairs={{0,4},{4,0},{1,5},{5,1},{2,6},{6,2},{3,7},{7,3},{8,12},{12,8},{9,1... | collective-permute-start | bytes 4718600 | tf_op jit(solution)/shard_map/ppermute | solution.py:59
  84.4 21.6 %collective-permute-start.23 = (bf16[2,3,128,2,256]{4,3,2,1,0:T(2,128)(2,1)S(1)}, bf16[2,3,128,2,256]{4,3,2,1,0:T(2,128)(2,1)S(1)}, u32[]{:S(2)}, u32[]{:S(2)}) collective-permute-start(bf16[2,3,128,2,256]{4,3,2,1,0:T(2,128)(2,1)S(1)} %pad_maximum_fusion.refs_0_), channel_id=1, source_target_pairs={{0,8},{8,16},{16,24},{24,0},{1,9},{9,17},{17,25},{25,1},{2,10},{10... | collective-permute-start | bytes 2359304 | tf_op jit(solution)/shard_map/ppermute | solution.py:43
  84.9 21.1 %collective-permute-start.24 = (bf16[2,3,128,2,256]{4,3,2,1,0:T(2,128)(2,1)S(1)}, bf16[2,3,128,2,256]{4,3,2,1,0:T(2,128)(2,1)S(1)}, u32[]{:S(2)}, u32[]{:S(2)}) collective-permute-start(bf16[2,3,128,2,256]{4,3,2,1,0:T(2,128)(2,1)S(1)} %pad_maximum_fusion.refs_0_), channel_id=1, source_target_pairs={{0,24},{8,0},{16,8},{24,16},{1,25},{9,1},{17,9},{25,17},{2,26},{10... | collective-permute-start | bytes 2359304 | tf_op jit(solution)/shard_map/ppermute | solution.py:43
  92.5 7.4 %collective-permute-start.26 = (bf16[192,512]{1,0:T(8,128)(2,1)S(1)}, bf16[192,512]{1,0:T(8,128)(2,1)S(1)}, u32[]{:S(2)}, u32[]{:S(2)}) collective-permute-start(bf16[192,512]{1,0:T(8,128)(2,1)S(1)} %get-tuple-element.92), channel_id=1, source_target_pairs={{0,1},{1,2},{2,3},{3,0},{4,5},{5,6},{6,7},{7,4},{8,9},{9,10},{10,1... | collective-permute-start | bytes 589832 | tf_op jit(solution)/shard_map/ppermute | solution.py:51
  93.3 11.9 %collective-permute-start.27 = (bf16[192,512]{1,0:T(8,128)(2,1)S(1)}, bf16[192,512]{1,0:T(8,128)(2,1)S(1)}, u32[]{:S(2)}, u32[]{:S(2)}) collective-permute-start(bf16[192,512]{1,0:T(8,128)(2,1)S(1)} %get-tuple-element.93), channel_id=1, source_target_pairs={{0,2},{1,3},{2,0},{3,1},{4,6},{5,7},{6,4},{7,5},{8,10},{9,11},{10,... | collective-permute-start | bytes 589832 | tf_op jit(solution)/shard_map/ppermute | solution.py:51
  96.6 8.6 %collective-permute-start.28 = (bf16[192,512]{1,0:T(8,128)(2,1)S(1)}, bf16[192,512]{1,0:T(8,128)(2,1)S(1)}, u32[]{:S(2)}, u32[]{:S(2)}) collective-permute-start(bf16[192,512]{1,0:T(8,128)(2,1)S(1)} %get-tuple-element.94), channel_id=1, source_target_pairs={{0,3},{1,0},{2,1},{3,2},{4,7},{5,4},{6,5},{7,6},{8,11},{9,8},{10,9... | collective-permute-start | bytes 589832 | tf_op jit(solution)/shard_map/ppermute | solution.py:51
  106.0 14.5 %collective-permute-start.31 = (bf16[2,3,128,2,256]{4,3,2,1,0:T(2,128)(2,1)S(1)}, bf16[2,3,128,2,256]{4,3,2,1,0:T(2,128)(2,1)S(1)}, u32[]{:S(2)}, u32[]{:S(2)}) collective-permute-start(bf16[2,3,128,2,256]{4,3,2,1,0:T(2,128)(2,1)S(1)} %pad_maximum_fusion.refs_0_), channel_id=1, source_target_pairs={{0,4},{4,0},{1,5},{5,1},{2,6},{6,2},{3,7},{7,3},{8,12},{12,8},{9,1... | collective-permute-start | bytes 2359304 | tf_op jit(solution)/shard_map/ppermute | solution.py:59
  107.4 13.0 %collective-permute-start.32 = (bf16[2,3,128,2,256]{4,3,2,1,0:T(2,128)(2,1)S(1)}, bf16[2,3,128,2,256]{4,3,2,1,0:T(2,128)(2,1)S(1)}, u32[]{:S(2)}, u32[]{:S(2)}) collective-permute-start(bf16[2,3,128,2,256]{4,3,2,1,0:T(2,128)(2,1)S(1)} %collective-permute-done.23.refs_1_), channel_id=1, source_target_pairs={{0,4},{4,0},{1,5},{5,1},{2,6},{6,2},{3,7},{7,3},{8,12},{12,8},{9,1... | collective-permute-start | bytes 2359304 | tf_op jit(solution)/shard_map/ppermute | solution.py:59
  107.5 13.0 %collective-permute-start.33 = (bf16[2,3,128,2,256]{4,3,2,1,0:T(2,128)(2,1)S(1)}, bf16[2,3,128,2,256]{4,3,2,1,0:T(2,128)(2,1)S(1)}, u32[]{:S(2)}, u32[]{:S(2)}) collective-permute-start(bf16[2,3,128,2,256]{4,3,2,1,0:T(2,128)(2,1)S(1)} %collective-permute-done.24.refs_2_), channel_id=1, source_target_pairs={{0,4},{4,0},{1,5},{5,1},{2,6},{6,2},{3,7},{7,3},{8,12},{12,8},{9,1... | collective-permute-start | bytes 2359304 | tf_op jit(solution)/shard_map/ppermute | solution.py:59
  108.5 12.0 %collective-permute-start.29 = (bf16[3,128,2,256]{3,2,1,0:T(2,128)(2,1)S(1)}, bf16[3,128,2,256]{3,2,1,0:T(2,128)(2,1)S(1)}, u32[]{:S(2)}, u32[]{:S(2)}) collective-permute-start(bf16[3,128,2,256]{3,2,1,0:T(2,128)(2,1)S(1)} %slice_bitcast_fusion.1), channel_id=1, source_target_pairs={{0,8},{8,16},{16,24},{24,0},{1,9},{9,17},{17,25},{25,1},{2,10},{10... | collective-permute-start | bytes 1179656 | tf_op jit(solution)/shard_map/ppermute | solution.py:43
  108.6 11.9 %collective-permute-start.30 = (bf16[3,128,2,256]{3,2,1,0:T(2,128)(2,1)S(1)}, bf16[3,128,2,256]{3,2,1,0:T(2,128)(2,1)S(1)}, u32[]{:S(2)}, u32[]{:S(2)}) collective-permute-start(bf16[3,128,2,256]{3,2,1,0:T(2,128)(2,1)S(1)} %slice_bitcast_fusion), channel_id=1, source_target_pairs={{0,24},{8,0},{16,8},{24,16},{1,25},{9,1},{17,9},{25,17},{2,26},{10... | collective-permute-start | bytes 1179656 | tf_op jit(solution)/shard_map/ppermute | solution.py:43
  120.5 3.9 %collective-permute-start.34 = (bf16[3,128,2,256]{3,2,1,0:T(2,128)(2,1)S(1)}, bf16[3,128,2,256]{3,2,1,0:T(2,128)(2,1)S(1)}, u32[]{:S(2)}, u32[]{:S(2)}) collective-permute-start(bf16[3,128,2,256]{3,2,1,0:T(2,128)(2,1)S(1)} %collective-permute-done.29), channel_id=1, source_target_pairs={{0,4},{4,0},{1,5},{5,1},{2,6},{6,2},{3,7},{7,3},{8,12},{12,8},{9,1... | collective-permute-start | bytes 1179656 | tf_op jit(solution)/shard_map/ppermute | solution.py:59
  121.4 3.0 %collective-permute-start.35 = (bf16[3,128,2,256]{3,2,1,0:T(2,128)(2,1)S(1)}, bf16[3,128,2,256]{3,2,1,0:T(2,128)(2,1)S(1)}, u32[]{:S(2)}, u32[]{:S(2)}) collective-permute-start(bf16[3,128,2,256]{3,2,1,0:T(2,128)(2,1)S(1)} %collective-permute-done.30), channel_id=1, source_target_pairs={{0,4},{4,0},{1,5},{5,1},{2,6},{6,2},{3,7},{7,3},{8,12},{12,8},{9,1... | collective-permute-start | bytes 1179656 | tf_op jit(solution)/shard_map/ppermute | solution.py:59
  (1 other events, 0.9 us)

commit v8 on v7

--- a/solution.py
+++ b/solution.py
@@ -21,6 +21,7 @@
 VMEM = pl.BlockSpec(memory_space=pltpu.VMEM)
 SMEM = pl.BlockSpec(memory_space=pltpu.SMEM)
 ANY = pl.BlockSpec(memory_space=pl.ANY)
+HBM = pl.BlockSpec(memory_space=pltpu.HBM)
 
 
 def params(limit=8):
@@ -59,12 +60,18 @@
     return lax.ppermute(value, "core", [(0, 1), (1, 0)])
 
 
-def pack_kernel(info, w_ref, d_ref, k_ref, v_ref):
+def pack_kernel(info, w_hbm, d_hbm, k_ref, v_ref, w_ref, d_ref, sems):
+    weight = pltpu.make_async_copy(w_hbm, w_ref, sems.at[0])
+    down = pltpu.make_async_copy(d_hbm, d_ref, sems.at[1])
+    weight.start()
+    down.start()
+    weight.wait()
     k_ref[...] = w_ref[:, 0, :]
     v_ref[0:256] = w_ref[pl.ds(pl.multiple_of(info[POOL] * 256, 256), 256), 1, :]
     column = lax.broadcasted_iota(jnp.int32, (256, 128), 0)
     lane = lax.broadcasted_iota(jnp.int32, (256, 128), 1)
     pick = (column == info[ADAPTER + info[HEAD]] * 32 + lane) & (lane < 32)
+    down.wait()
     low = lax.dot_general(
         pick.astype(jnp.bfloat16),
         d_ref[...],
@@ -78,18 +85,23 @@
 def pack(info, weight, down):
     return pl.pallas_call(
         pack_kernel,
-        in_specs=[SMEM, VMEM, VMEM],
+        in_specs=[SMEM, HBM, HBM],
         out_specs=[VMEM, VMEM],
         out_shape=[
             jax.ShapeDtypeStruct((512, 256), jnp.bfloat16),
             jax.ShapeDtypeStruct((320, 256), jnp.bfloat16),
         ],
+        scratch_shapes=[
+            pltpu.VMEM(weight.shape, weight.dtype),
+            pltpu.VMEM(down.shape, down.dtype),
+            pltpu.SemaphoreType.DMA((2,)),
+        ],
         compiler_params=params(),
         name="pack",
     )(info, weight, down)
 
 
-ROWS_STEP = 8
+ROWS_STEP = 12
 
 
 def attend_kernel(offset, len_ref, q_ref, kv_ref, cur_ref, o_ref):
@@ -435,7 +447,12 @@
     rows, heads = rotated_query.shape[0], rotated_query.shape[1] // HEAD_DIM
     query = rotated_query.reshape(rows, heads, HEAD_DIM)
 
-    keys, values = pack(info, key_value_weight, adapter_down_weight)
+    cache = pltpu.with_memory_space_constraint(key_value_cache, pltpu.HBM)
+    keys, values = pack(
+        info,
+        pltpu.with_memory_space_constraint(key_value_weight, pltpu.HBM),
+        pltpu.with_memory_space_constraint(adapter_down_weight, pltpu.HBM),
+    )
     keys_across = x_mirror(keys)
     ring_values = ring(values, y_shift)
     keys, keys_across, ring_values, cached_length = barrier(
@@ -447,7 +464,7 @@
     key1, key3 = y_shift(key0, 1), y_shift(key0, -1)
     value1, value3 = x_shift(value0, 1), x_shift(value0, -1)
     down_own = jnp.concatenate([down0, xh_swap(down0)], 0)
-    attended = attend(query, key_value_cache, current_key_value, cached_length, 0, 1)
+    attended = attend(query, cache, current_key_value, cached_length, 0, 1)
     attended = attended.reshape(rows, heads * HEAD_DIM)
     key0, value0, key1, key3, value1, value3, down_own, attended = barrier(
         (key0, value0, key1, key3, value1, value3, down_own, attended)
@@ -488,9 +505,9 @@
     for k, share in ((1, shares[1]), (2, shares[2]), (-1, shares[3])):
         decoded = decoded + z_shift(share, k).astype(jnp.float32)
     decoded = decoded.astype(jnp.bfloat16)
-    both0, both1, both3, decoded = barrier((both0, both1, both3, decoded))
+    both1, both3 = barrier((both1, both3))
     b2, a2 = y_shift(both1[0], 1), y_shift(both3[1], -1)
-    middle = [both0, both1, both3]
+    middle, decoded = barrier(([both0, both1, both3], decoded))
     theirs = [core_swap(v) for v in middle]
     b2, a2, theirs = barrier((b2, a2, theirs))
     theirs2 = [core_swap(b2), core_swap(a2)]

time: 126 us -> 124 us (0.984)
  local copies, waits for them, and re-layouts: 6.83 us -> 2.12 us
  waiting for transfers between devices: 35 us -> 37 us
  Pallas kernels: 28.5 us -> 29.8 us
    ppermute x13, waiting for transfers between devices: 25.9 us -> 33.1 us  [y_shift(): return lax.ppermute(value, 'y', [(i, (i + k) % 4) for i in range(4)])]
    ppermute x3, waiting for transfers between devices: 7.76 us -> 1.31 us  [z_shift(): return lax.ppermute(value, 'head', [(i, (i + k) % 4) for i in range(4)])]
    unnamed x38 -> x32, local copies, waits for them, and re-layouts: 5.21 us -> 0.44 us
  transfers between devices with their start and end apart: 36 -> 36, of which waited for: 9 -> 11; matrix products, arithmetic and copies ran while one was open for 2% -> 2% of each run, Pallas kernels for 21% -> 21%
where the time goes in v8:
time: 124 us; the launch traced here: 123 us
  starting transfers between devices  51.2 us (41%)
  waiting for transfers between devices  37 us (30%)
  Pallas kernels  29.8 us (24%)
  local copies, waits for them, and re-layouts  2.12 us (2%)
  other arithmetic  1.95 us (2%)
  between operations  1.34 us (1%)
    ppermute x13, waiting for transfers between devices, y_shift(): return lax.ppermute(value, 'y', [(i, (i + k) % 4) for i in range(4)])  33.1 us
    ppermute x13, starting transfers between devices, y_shift(): return lax.ppermute(value, 'y', [(i, (i + k) % 4) for i in range(4)])  18.6 us
    ppermute x10, starting transfers between devices, core_swap(): return lax.ppermute(value, 'core', [(0, 1), (1, 0)])  8.91 us
    pallas_call x1, Pallas kernels, attend(): pl.pallas_call(functools.partial(attend_kernel, first * ROWS_STEP), grid_...  8.47 us
    ppermute x3, starting transfers between devices, z_shift(): return lax.ppermute(value, 'head', [(i, (i + k) % 4) for i in range(4)])  5.75 us
    pallas_call x1, Pallas kernels, project(): pl.pallas_call(project_kernel, in_specs=[SMEM] + [VMEM] * 6, out_specs=[V...  5.15 us
    ppermute x2, starting transfers between devices, z_flip(): return lax.ppermute(value, 'head', [(i, i ^ mask) for i in range(4)])  5.02 us
    ppermute x2, starting transfers between devices, x_mirror(): return lax.ppermute(value, ('pool', 'xh'), [(i, 3 - i) for i in range(4)])  4.92 us
  transfers between devices with their start and end apart: 36, of which 11 were waited for; matrix products, arithmetic and copies ran while one was open for 2% of the time, Pallas kernels for 21%

profile of v8, /device:TPU:1, one launch (start us, length us, event | category | flops | bytes accessed | tf_op | source)
XLA Modules:
  0.0 123.4 jit_solution(779127213677738328)
XLA Ops:
  0.7 0.8 concatenate.32.info
  1.5 2.8 %pack.1 = (bf16[512,256]{1,0:T(8,128)(2,1)S(1)}, bf16[320,256]{1,0:T(8,128)(2,1)S(1)}) custom-call(s32[17]{0:T(128)S(1)} %concatenate.32.info, bf16[512,2,256]{2,1,0:T(2,128)(2,1)} %w_hbm.1, bf16[512,256]{1,0:T(8,128)(2,1)} %d_hbm.1), custom_call_target="tpu_custom_call" | custom-call | tf_op jit(solution)/shard_map/pack/pallas_call | solution.py:86
  4.2 3.4 %collective-permute-start = (bf16[512,256]{1,0:T(8,128)(2,1)S(1)}, bf16[512,256]{1,0:T(8,128)(2,1)S(1)}, u32[]{:S(2)}, u32[]{:S(2)}) collective-permute-start(bf16[512,256]{1,0:T(8,128)(2,1)S(1)} %get-tuple-element.57), channel_id=1, source_target_pairs={{0,96},{32,64},{64,32},{96,0},{1,97},{33,65},{65,33},{97,1},{2,98}... | collective-permute-start | bytes 786440 | tf_op jit(solution)/shard_map/ppermute | solution.py:32
  7.6 1.3 %collective-permute-start.1 = (bf16[320,256]{1,0:T(8,128)(2,1)S(1)}, bf16[320,256]{1,0:T(8,128)(2,1)S(1)}, u32[]{:S(2)}, u32[]{:S(2)}) collective-permute-start(bf16[320,256]{1,0:T(8,128)(2,1)S(1)} %get-tuple-element.59), channel_id=1, source_target_pairs={{0,8},{8,16},{16,24},{24,0},{1,9},{9,17},{17,25},{25,1},{2,10},{10... | collective-permute-start | bytes 491528 | tf_op jit(solution)/shard_map/ppermute | solution.py:44
  8.9 2.6 %collective-permute-start.2 = (bf16[320,256]{1,0:T(8,128)(2,1)S(1)}, bf16[320,256]{1,0:T(8,128)(2,1)S(1)}, u32[]{:S(2)}, u32[]{:S(2)}) collective-permute-start(bf16[320,256]{1,0:T(8,128)(2,1)S(1)} %get-tuple-element.59), channel_id=1, source_target_pairs={{0,16},{8,24},{16,0},{24,8},{1,17},{9,25},{17,1},{25,9},{2,18},{10... | collective-permute-start | bytes 491528 | tf_op jit(solution)/shard_map/ppermute | solution.py:44
  11.5 1.1 collective-permute-start.3
  12.6 1.1 collective-permute-done.1
  13.7 4.6 %collective-permute-done.2 = bf16[320,256]{1,0:T(8,128)(2,1)S(1)} collective-permute-done((bf16[320,256]{1,0:T(8,128)(2,1)S(1)}, bf16[320,256]{1,0:T(8,128)(2,1)S(1)}, u32[]{:S(2)}, u32[]{:S(2)}) %collective-permute-start.2) | collective-permute-done | bytes 163872 | tf_op jit(solution)/shard_map/ppermute | solution.py:44
  18.5 2.7 %collective-permute-start.7 = (bf16[1024,256]{1,0:T(8,128)(2,1)S(1)}, bf16[1024,256]{1,0:T(8,128)(2,1)S(1)}, u32[]{:S(2)}, u32[]{:S(2)}) collective-permute-start(bf16[1024,256]{1,0:T(8,128)(2,1)S(1)} %pad_maximum_fusion.1.refs_1_), channel_id=1, source_target_pairs={{0,96},{64,0},{32,64},{96,32},{1,97},{65,1},{33,65},{97,33},{2,98}... | collective-permute-start | bytes 1572872 | tf_op jit(solution)/shard_map/ppermute | solution.py:40
  21.3 1.5 %collective-permute-start.4 = (bf16[1024,256]{1,0:T(8,128)(2,1)S(1)}, bf16[1024,256]{1,0:T(8,128)(2,1)S(1)}, u32[]{:S(2)}, u32[]{:S(2)}) collective-permute-start(bf16[1024,256]{1,0:T(8,128)(2,1)S(1)} %constant_dynamic-update-slice_fusion.refs_0_), channel_id=1, source_target_pairs={{0,8},{8,16},{16,24},{24,0},{1,9},{9,17},{17,25},{25,1},{2,10},{10... | collective-permute-start | bytes 1572872 | tf_op jit(solution)/shard_map/ppermute | solution.py:44
  22.7 1.3 %collective-permute-start.5 = (bf16[1024,256]{1,0:T(8,128)(2,1)S(1)}, bf16[1024,256]{1,0:T(8,128)(2,1)S(1)}, u32[]{:S(2)}, u32[]{:S(2)}) collective-permute-start(bf16[1024,256]{1,0:T(8,128)(2,1)S(1)} %constant_dynamic-update-slice_fusion.refs_0_), channel_id=1, source_target_pairs={{0,24},{8,0},{16,8},{24,16},{1,25},{9,1},{17,9},{25,17},{2,26},{10... | collective-permute-start | bytes 1572872 | tf_op jit(solution)/shard_map/ppermute | solution.py:44
  24.2 8.5 %attend.1 = bf16[48,16,128]{2,1,0:T(8,128)(2,1)S(1)} custom-call(s32[48]{0:T(128)S(1)} %copy-done.5, bf16[48,16,128]{2,1,0:T(8,128)(2,1)S(1)} %bitcast.33, bf16[48,128,2,256]{3,2,1,0:T(2,128)(2,1)} %kv_ref.1, bf16[48,2,256]{2,1,0:T(2,128)(2,1)S(1)} %copy-done.4), custom_call_target="tpu_custom_call" | custom-call | tf_op jit(solution)/shard_map/attend/pallas_call | solution.py:146
  32.8 0.7 collective-permute-done.4.refs_2_
  34.2 3.2 %collective-permute-start.11 = (bf16[6144,256]{1,0:T(8,128)(2,1)S(1)}, bf16[6144,256]{1,0:T(8,128)(2,1)S(1)}, u32[]{:S(2)}, u32[]{:S(2)}) collective-permute-start(bf16[6144,256]{1,0:T(8,128)(2,1)S(1)} %constant_dynamic-update-slice_fusion.7), channel_id=1, source_target_pairs={{0,4},{4,0},{1,5},{5,1},{2,6},{6,2},{3,7},{7,3},{8,12},{12,8},{9,1... | collective-permute-start | bytes 9437192 | tf_op jit(solution)/shard_map/ppermute | solution.py:60
  37.5 2.0 %collective-permute-start.10 = (bf16[1024,256]{1,0:T(8,128)(2,1)S(1)}, bf16[1024,256]{1,0:T(8,128)(2,1)S(1)}, u32[]{:S(2)}, u32[]{:S(2)}) collective-permute-start(bf16[1024,256]{1,0:T(8,128)(2,1)S(1)} %pad_maximum_fusion.1.refs_1_), channel_id=1, source_target_pairs={{0,32},{64,96},{32,0},{96,64},{1,33},{65,97},{33,1},{97,65},{2,34}... | collective-permute-start | bytes 1572872 | tf_op jit(solution)/shard_map/ppermute | solution.py:40
  39.5 1.1 collective-permute-start.9
  40.6 2.5 %collective-permute-done.13.other_ref = bf16[512,256]{1,0:T(8,128)(2,1)S(1)} collective-permute-done((bf16[512,256]{1,0:T(8,128)(2,1)S(1)}, bf16[512,256]{1,0:T(8,128)(2,1)S(1)}, u32[]{:S(2)}, u32[]{:S(2)}) %collective-permute-start.13) | collective-permute-done | bytes 262176 | tf_op jit(solution)/shard_map/ppermute | solution.py:60
  43.1 1.3 %low_rank.1 = f32[32,128]{1,0:T(8,128)S(1)} custom-call(s32[17]{0:T(128)S(1)} %concatenate.32.info, bf16[512,8192]{1,0:T(8,128)(2,1)S(1)} %bitcast.28, bf16[512,256]{1,0:T(8,128)(2,1)S(1)} %constant_dynamic-update-slice_fusion.2.own_ref, bf16[512,256]{1,0:T(8,128)(2,1)S(1)} %collective-permute-done.13.other_ref), custom_call_target="tpu_custom_call" | custom-call | tf_op jit(solution)/shard_map/low_rank/pallas_call | solution.py:199
  44.4 1.7 %collective-permute-start.14 = (f32[32,128]{1,0:T(8,128)S(1)}, f32[32,128]{1,0:T(8,128)S(1)}, u32[]{:S(2)}, u32[]{:S(2)}) collective-permute-start(f32[32,128]{1,0:T(8,128)S(1)} %low_rank.1), channel_id=1, source_target_pairs={{0,1},{1,0},{2,3},{3,2},{4,5},{5,4},{6,7},{7,6},{8,9},{9,8},{10,11... | collective-permute-start | bytes 49160 | tf_op jit(solution)/shard_map/ppermute | solution.py:56
  46.1 2.0 %collective-permute-start.12 = (bf16[48,2048]{1,0:T(8,128)(2,1)S(1)}, bf16[48,2048]{1,0:T(8,128)(2,1)S(1)}, u32[]{:S(2)}, u32[]{:S(2)}) collective-permute-start(bf16[48,2048]{1,0:T(8,128)(2,1)S(1)} %bitcast.40), channel_id=1, source_target_pairs={{0,32},{32,0},{1,33},{33,1},{2,34},{34,2},{3,35},{35,3},{4,36},{36... | collective-permute-start | bytes 589832 | tf_op jit(solution)/shard_map/ppermute | solution.py:48
  48.1 3.3 %collective-permute-start.15 = (f32[64,128]{1,0:T(8,128)S(1)}, f32[64,128]{1,0:T(8,128)S(1)}, u32[]{:S(2)}, u32[]{:S(2)}) collective-permute-start(f32[64,128]{1,0:T(8,128)S(1)} %pad_maximum_fusion.4), channel_id=1, source_target_pairs={{0,2},{1,3},{2,0},{3,1},{4,6},{5,7},{6,4},{7,5},{8,10},{9,11},{10,... | collective-permute-start | bytes 98312 | tf_op jit(solution)/shard_map/ppermute | solution.py:56
  51.4 2.4 %main_product.2 = (f32[512,256]{1,0:T(8,128)S(1)}, f32[512,256]{1,0:T(8,128)S(1)}) custom-call(s32[17]{0:T(128)S(1)} %concatenate.32.info, bf16[512,8192]{1,0:T(8,128)(2,1)S(1)} %bitcast.29, bf16[1024,256]{1,0:T(8,128)(2,1)S(1)} %constant_dynamic-update-slice_fusion.refs_0_, bf16[1024,256]{1,0:T(8,128)(2,1)S(1)} %pad_maximum_fusion.1.refs_1_, ...), custom_call_target="tpu_custom_call" | custom-call | tf_op jit(solution)/shard_map/main_product/pallas_call | solution.py:242
  53.9 2.3 %main_product.3 = (f32[512,256]{1,0:T(8,128)S(1)}, f32[512,256]{1,0:T(8,128)S(1)}) custom-call(s32[17]{0:T(128)S(1)} %concatenate.32.info, bf16[512,8192]{1,0:T(8,128)(2,1)S(1)} %bitcast.30, bf16[6144,256]{1,0:T(8,128)(2,1)S(1)} %collective-permute-done.11.refs_0_), custom_call_target="tpu_custom_call" | custom-call | tf_op jit(solution)/shard_map/main_product/pallas_call | solution.py:242
  56.3 1.3 %collective-permute-start.16 = (bf16[1024,256]{1,0:T(8,128)(2,1)S(1)}, bf16[1024,256]{1,0:T(8,128)(2,1)S(1)}, u32[]{:S(2)}, u32[]{:S(2)}) collective-permute-start(bf16[1024,256]{1,0:T(8,128)(2,1)S(1)} %collective-permute-done.9.refs_0_), channel_id=1, source_target_pairs={{0,4},{4,0},{1,5},{5,1},{2,6},{6,2},{3,7},{7,3},{8,12},{12,8},{9,1... | collective-permute-start | bytes 1572872 | tf_op jit(solution)/shard_map/ppermute | solution.py:60
  57.7 1.4 %collective-permute-start.20 = (bf16[96,2048]{1,0:T(8,128)(2,1)S(1)}, bf16[96,2048]{1,0:T(8,128)(2,1)S(1)}, u32[]{:S(2)}, u32[]{:S(2)}) collective-permute-start(bf16[96,2048]{1,0:T(8,128)(2,1)S(1)} %constant_dynamic-update-slice_fusion.13), channel_id=1, source_target_pairs={{0,8},{8,16},{16,24},{24,0},{1,9},{9,17},{17,25},{25,1},{2,10},{10... | collective-permute-start | bytes 1179656 | tf_op jit(solution)/shard_map/ppermute | solution.py:44
  59.2 2.5 %collective-permute-start.21 = (bf16[96,2048]{1,0:T(8,128)(2,1)S(1)}, bf16[96,2048]{1,0:T(8,128)(2,1)S(1)}, u32[]{:S(2)}, u32[]{:S(2)}) collective-permute-start(bf16[96,2048]{1,0:T(8,128)(2,1)S(1)} %constant_dynamic-update-slice_fusion.13), channel_id=1, source_target_pairs={{0,16},{8,24},{16,0},{24,8},{1,17},{9,25},{17,1},{25,9},{2,18},{10... | collective-permute-start | bytes 1179656 | tf_op jit(solution)/shard_map/ppermute | solution.py:44
  62.1 3.7 %finish.1 = (bf16[3,128,2,256]{3,2,1,0:T(2,128)(2,1)S(1)}, bf16[3,128,2,256]{3,2,1,0:T(2,128)(2,1)S(1)}) custom-call(s32[17]{0:T(128)S(1)} %concatenate.32.info, bf16[512,8192]{1,0:T(8,128)(2,1)S(1)} %bitcast.31, bf16[1024,256]{1,0:T(8,128)(2,1)S(1)} %collective-permute-done.9.refs_0_, bf16[1024,256]{1,0:T(8,128)(2,1)S(1)} %collective-permute-done.10.refs_1_, ...), custom_call_target="tpu_custom_call" | custom-call | tf_op jit(solution)/shard_map/finish/pallas_call | solution.py:293
  65.8 1.2 collective-permute-start.18
  67.0 1.5 %collective-permute-start.19 = (bf16[3,128,2,256]{3,2,1,0:T(2,128)(2,1)S(1)}, bf16[3,128,2,256]{3,2,1,0:T(2,128)(2,1)S(1)}, u32[]{:S(2)}, u32[]{:S(2)}) collective-permute-start(bf16[3,128,2,256]{3,2,1,0:T(2,128)(2,1)S(1)} %get-tuple-element.84), channel_id=1, source_target_pairs={{0,96},{32,64},{64,32},{96,0},{1,97},{33,65},{65,33},{97,1},{2,98}... | collective-permute-start | bytes 1179656 | tf_op jit(solution)/shard_map/ppermute | solution.py:32
  68.5 1.0 collective-permute-done.20
  69.5 9.4 %collective-permute-done.21 = bf16[96,2048]{1,0:T(8,128)(2,1)S(1)} collective-permute-done((bf16[96,2048]{1,0:T(8,128)(2,1)S(1)}, bf16[96,2048]{1,0:T(8,128)(2,1)S(1)}, u32[]{:S(2)}, u32[]{:S(2)}) %collective-permute-start.21) | collective-permute-done | bytes 393248 | tf_op jit(solution)/shard_map/ppermute | solution.py:44
  79.0 1.3 %collective-permute-start.27 = (bf16[384,2048]{1,0:T(8,128)(2,1)S(1)}, bf16[384,2048]{1,0:T(8,128)(2,1)S(1)}, u32[]{:S(2)}, u32[]{:S(2)}) collective-permute-start(bf16[384,2048]{1,0:T(8,128)(2,1)S(1)} %constant_dynamic-update-slice_fusion.15.refs_0_), channel_id=1, source_target_pairs={{0,4},{4,0},{1,5},{5,1},{2,6},{6,2},{3,7},{7,3},{8,12},{12,8},{9,1... | collective-permute-start | bytes 4718600 | tf_op jit(solution)/shard_map/ppermute | solution.py:60
  80.3 1.1 pad_maximum_fusion.refs_0_
  81.5 1.1 collective-permute-start.23
  82.5 1.7 %collective-permute-start.24 = (bf16[2,3,128,2,256]{4,3,2,1,0:T(2,128)(2,1)S(1)}, bf16[2,3,128,2,256]{4,3,2,1,0:T(2,128)(2,1)S(1)}, u32[]{:S(2)}, u32[]{:S(2)}) collective-permute-start(bf16[2,3,128,2,256]{4,3,2,1,0:T(2,128)(2,1)S(1)} %pad_maximum_fusion.refs_0_), channel_id=1, source_target_pairs={{0,24},{8,0},{16,8},{24,16},{1,25},{9,1},{17,9},{25,17},{2,26},{10... | collective-permute-start | bytes 2359304 | tf_op jit(solution)/shard_map/ppermute | solution.py:44
  84.4 5.2 %project.1 = (bf16[192,512]{1,0:T(8,128)(2,1)S(1)}, bf16[192,512]{1,0:T(8,128)(2,1)S(1)}, bf16[192,512]{1,0:T(8,128)(2,1)S(1)}, bf16[192,512]{1,0:T(8,128)(2,1)S(1)}) custom-call(s32[17]{0:T(128)S(1)} %concatenate.32.info, s32[768,1]{1,0:T(8,128)S(1)} %broadcast_in_dim.20.keep, bf16[128,2048]{1,0:T(8,128)(2,1)S(1)} %bitcast.34, ...), custom_call_target="tpu_custom_call" | custom-call | tf_op jit(solution)/shard_map/project/pallas_call | solution.py:410
  89.6 1.7 %collective-permute-start.28 = (bf16[192,512]{1,0:T(8,128)(2,1)S(1)}, bf16[192,512]{1,0:T(8,128)(2,1)S(1)}, u32[]{:S(2)}, u32[]{:S(2)}) collective-permute-start(bf16[192,512]{1,0:T(8,128)(2,1)S(1)} %get-tuple-element.96), channel_id=1, source_target_pairs={{0,1},{1,2},{2,3},{3,0},{4,5},{5,6},{6,7},{7,4},{8,9},{9,10},{10,1... | collective-permute-start | bytes 589832 | tf_op jit(solution)/shard_map/ppermute | solution.py:52
  91.3 3.3 %collective-permute-start.29 = (bf16[192,512]{1,0:T(8,128)(2,1)S(1)}, bf16[192,512]{1,0:T(8,128)(2,1)S(1)}, u32[]{:S(2)}, u32[]{:S(2)}) collective-permute-start(bf16[192,512]{1,0:T(8,128)(2,1)S(1)} %get-tuple-element.97), channel_id=1, source_target_pairs={{0,2},{1,3},{2,0},{3,1},{4,6},{5,7},{6,4},{7,5},{8,10},{9,11},{10,... | collective-permute-start | bytes 589832 | tf_op jit(solution)/shard_map/ppermute | solution.py:52
  94.6 0.7 collective-permute-start.30
  95.3 6.6 %collective-permute-done.23.refs_1_ = bf16[2,3,128,2,256]{4,3,2,1,0:T(2,128)(2,1)S(1)} collective-permute-done((bf16[2,3,128,2,256]{4,3,2,1,0:T(2,128)(2,1)S(1)}, bf16[2,3,128,2,256]{4,3,2,1,0:T(2,128)(2,1)S(1)}, u32[]{:S(2)}, u32[]{:S(2)}) %collective-permute-start.23) | collective-permute-done | bytes 786464 | tf_op jit(solution)/shard_map/ppermute | solution.py:44
  101.9 1.3 %collective-permute-done.29 = bf16[192,512]{1,0:T(8,128)(2,1)S(1)} collective-permute-done((bf16[192,512]{1,0:T(8,128)(2,1)S(1)}, bf16[192,512]{1,0:T(8,128)(2,1)S(1)}, u32[]{:S(2)}, u32[]{:S(2)}) %collective-permute-start.29) | collective-permute-done | bytes 196640 | tf_op jit(solution)/shard_map/ppermute | solution.py:52
  103.2 0.8 add_convert_fusion
  104.0 1.4 %collective-permute-start.31 = (bf16[2,3,128,2,256]{4,3,2,1,0:T(2,128)(2,1)S(1)}, bf16[2,3,128,2,256]{4,3,2,1,0:T(2,128)(2,1)S(1)}, u32[]{:S(2)}, u32[]{:S(2)}) collective-permute-start(bf16[2,3,128,2,256]{4,3,2,1,0:T(2,128)(2,1)S(1)} %pad_maximum_fusion.refs_0_), channel_id=1, source_target_pairs={{0,4},{4,0},{1,5},{5,1},{2,6},{6,2},{3,7},{7,3},{8,12},{12,8},{9,1... | collective-permute-start | bytes 2359304 | tf_op jit(solution)/shard_map/ppermute | solution.py:60
  106.6 2.7 %collective-permute-start.26 = (bf16[3,128,2,256]{3,2,1,0:T(2,128)(2,1)S(1)}, bf16[3,128,2,256]{3,2,1,0:T(2,128)(2,1)S(1)}, u32[]{:S(2)}, u32[]{:S(2)}) collective-permute-start(bf16[3,128,2,256]{3,2,1,0:T(2,128)(2,1)S(1)} %slice_bitcast_fusion), channel_id=1, source_target_pairs={{0,24},{8,0},{16,8},{24,16},{1,25},{9,1},{17,9},{25,17},{2,26},{10... | collective-permute-start | bytes 1179656 | tf_op jit(solution)/shard_map/ppermute | solution.py:44
  109.3 9.3 %collective-permute-done.25 = bf16[3,128,2,256]{3,2,1,0:T(2,128)(2,1)S(1)} collective-permute-done((bf16[3,128,2,256]{3,2,1,0:T(2,128)(2,1)S(1)}, bf16[3,128,2,256]{3,2,1,0:T(2,128)(2,1)S(1)}, u32[]{:S(2)}, u32[]{:S(2)}) %collective-permute-start.25) | collective-permute-done | bytes 393248 | tf_op jit(solution)/shard_map/ppermute | solution.py:44
  118.6 0.9 collective-permute-start.34
  119.5 2.9 %place.2.refs_4_ = bf16[1,2,2048,2,256]{4,3,2,1,0:T(2,128)(2,1)} custom-call(s32[17]{0:T(128)S(1)} %concatenate.32.info, bf16[2,3,128,2,256]{4,3,2,1,0:T(2,128)(2,1)S(1)} %pad_maximum_fusion.refs_0_, bf16[2,3,128,2,256]{4,3,2,1,0:T(2,128)(2,1)S(1)} %collective-permute-done.23.refs_1_, bf16[2,3,128,2,256]{4,3,2,1,0:T(2,128)(2,1)S(1)} %collective-permute-done.24.refs_2_, ...), custom_call_target="tpu_custom_call" | custom-call | tf_op jit(solution)/shard_map/place/pallas_call | solution.py:368
  122.4 0.9 place.3
  (89 shorter events, 3.4 us)
Async XLA Ops:
  0.6 23.6 %copy-start.5 = (s32[48]{0:T(128)S(1)}, s32[48]{0:T(128)}, u32[]{:S(2)}) copy-start(s32[48]{0:T(128)} %len_ref) | copy-start | bytes 580
  0.6 23.5 %copy-start.6 = (bf16[48,2048]{1,0:T(8,128)(2,1)S(1)}, bf16[48,2048]{1,0:T(8,128)(2,1)}, u32[]{:S(2)}) copy-start(bf16[48,2048]{1,0:T(8,128)(2,1)} %param.20) | copy-start | bytes 589828
  0.7 23.6 %copy-start.4 = (bf16[48,2,256]{2,1,0:T(2,128)(2,1)S(1)}, bf16[48,2,256]{2,1,0:T(2,128)(2,1)}, u32[]{:S(2)}) copy-start(bf16[48,2,256]{2,1,0:T(2,128)(2,1)} %cur_ref.1) | copy-start | bytes 147460
  4.2 14.1 %collective-permute-start = (bf16[512,256]{1,0:T(8,128)(2,1)S(1)}, bf16[512,256]{1,0:T(8,128)(2,1)S(1)}, u32[]{:S(2)}, u32[]{:S(2)}) collective-permute-start(bf16[512,256]{1,0:T(8,128)(2,1)S(1)} %get-tuple-element.57), channel_id=1, source_target_pairs={{0,96},{32,64},{64,32},{96,0},{1,97},{33,65},{65,33},{97,1},{2,98}... | collective-permute-start | bytes 786440 | tf_op jit(solution)/shard_map/ppermute | solution.py:32
  7.6 6.1 %collective-permute-start.1 = (bf16[320,256]{1,0:T(8,128)(2,1)S(1)}, bf16[320,256]{1,0:T(8,128)(2,1)S(1)}, u32[]{:S(2)}, u32[]{:S(2)}) collective-permute-start(bf16[320,256]{1,0:T(8,128)(2,1)S(1)} %get-tuple-element.59), channel_id=1, source_target_pairs={{0,8},{8,16},{16,24},{24,0},{1,9},{9,17},{17,25},{25,1},{2,10},{10... | collective-permute-start | bytes 491528 | tf_op jit(solution)/shard_map/ppermute | solution.py:44
  8.9 9.4 %collective-permute-start.2 = (bf16[320,256]{1,0:T(8,128)(2,1)S(1)}, bf16[320,256]{1,0:T(8,128)(2,1)S(1)}, u32[]{:S(2)}, u32[]{:S(2)}) collective-permute-start(bf16[320,256]{1,0:T(8,128)(2,1)S(1)} %get-tuple-element.59), channel_id=1, source_target_pairs={{0,16},{8,24},{16,0},{24,8},{1,17},{9,25},{17,1},{25,9},{2,18},{10... | collective-permute-start | bytes 491528 | tf_op jit(solution)/shard_map/ppermute | solution.py:44
  11.5 6.8 %collective-permute-start.3 = (bf16[320,256]{1,0:T(8,128)(2,1)S(1)}, bf16[320,256]{1,0:T(8,128)(2,1)S(1)}, u32[]{:S(2)}, u32[]{:S(2)}) collective-permute-start(bf16[320,256]{1,0:T(8,128)(2,1)S(1)} %get-tuple-element.59), channel_id=1, source_target_pairs={{0,24},{8,0},{16,8},{24,16},{1,25},{9,1},{17,9},{25,17},{2,26},{10... | collective-permute-start | bytes 491528 | tf_op jit(solution)/shard_map/ppermute | solution.py:44
  18.5 14.3 %collective-permute-start.6 = (bf16[1024,256]{1,0:T(8,128)(2,1)S(1)}, bf16[1024,256]{1,0:T(8,128)(2,1)S(1)}, u32[]{:S(2)}, u32[]{:S(2)}) collective-permute-start(bf16[1024,256]{1,0:T(8,128)(2,1)S(1)} %pad_maximum_fusion.1.refs_1_), channel_id=1, source_target_pairs={{0,64},{64,32},{32,96},{96,0},{1,65},{65,33},{33,97},{97,1},{2,66}... | collective-permute-start | bytes 1572872 | tf_op jit(solution)/shard_map/ppermute | solution.py:40
  18.5 14.3 %collective-permute-start.7 = (bf16[1024,256]{1,0:T(8,128)(2,1)S(1)}, bf16[1024,256]{1,0:T(8,128)(2,1)S(1)}, u32[]{:S(2)}, u32[]{:S(2)}) collective-permute-start(bf16[1024,256]{1,0:T(8,128)(2,1)S(1)} %pad_maximum_fusion.1.refs_1_), channel_id=1, source_target_pairs={{0,96},{64,0},{32,64},{96,32},{1,97},{65,1},{33,65},{97,33},{2,98}... | collective-permute-start | bytes 1572872 | tf_op jit(solution)/shard_map/ppermute | solution.py:40
  21.2 21.8 %slice-start = ((s8[8388608]{0:T(1024)(128)(4,1)}), s8[4194304]{0:T(1024)(128)(4,1)S(1)}, s32[]{:S(2)}) async-start(s8[8388608]{0:T(1024)(128)(4,1)} %bitcast.26), calls=%async_computation | async-start | bytes 8388608
  21.3 12.3 %collective-permute-start.4 = (bf16[1024,256]{1,0:T(8,128)(2,1)S(1)}, bf16[1024,256]{1,0:T(8,128)(2,1)S(1)}, u32[]{:S(2)}, u32[]{:S(2)}) collective-permute-start(bf16[1024,256]{1,0:T(8,128)(2,1)S(1)} %constant_dynamic-update-slice_fusion.refs_0_), channel_id=1, source_target_pairs={{0,8},{8,16},{16,24},{24,0},{1,9},{9,17},{17,25},{25,1},{2,10},{10... | collective-permute-start | bytes 1572872 | tf_op jit(solution)/shard_map/ppermute | solution.py:44
  22.7 11.2 %collective-permute-start.5 = (bf16[1024,256]{1,0:T(8,128)(2,1)S(1)}, bf16[1024,256]{1,0:T(8,128)(2,1)S(1)}, u32[]{:S(2)}, u32[]{:S(2)}) collective-permute-start(bf16[1024,256]{1,0:T(8,128)(2,1)S(1)} %constant_dynamic-update-slice_fusion.refs_0_), channel_id=1, source_target_pairs={{0,24},{8,0},{16,8},{24,16},{1,25},{9,1},{17,9},{25,17},{2,26},{10... | collective-permute-start | bytes 1572872 | tf_op jit(solution)/shard_map/ppermute | solution.py:44
  24.1 8.7 %collective-permute-start.8 = (bf16[256,256]{1,0:T(8,128)(2,1)S(1)}, bf16[256,256]{1,0:T(8,128)(2,1)S(1)}, u32[]{:S(2)}, u32[]{:S(2)}) collective-permute-start(bf16[256,256]{1,0:T(8,128)(2,1)S(1)} %pad_maximum_fusion.2), channel_id=1, source_target_pairs={{0,32},{32,0},{1,33},{33,1},{2,34},{34,2},{3,35},{35,3},{4,36},{36... | collective-permute-start | bytes 393224 | tf_op jit(solution)/shard_map/ppermute | solution.py:48
  24.2 18.8 %slice-start.1 = ((s8[8388608]{0:T(1024)(128)(4,1)}), s8[4194304]{0:T(1024)(128)(4,1)S(1)}, s32[]{:S(2)}) async-start(s8[8388608]{0:T(1024)(128)(4,1)} %bitcast.26), calls=%async_computation.1 | async-start | bytes 8388608
  34.2 19.6 %collective-permute-start.11 = (bf16[6144,256]{1,0:T(8,128)(2,1)S(1)}, bf16[6144,256]{1,0:T(8,128)(2,1)S(1)}, u32[]{:S(2)}, u32[]{:S(2)}) collective-permute-start(bf16[6144,256]{1,0:T(8,128)(2,1)S(1)} %constant_dynamic-update-slice_fusion.7), channel_id=1, source_target_pairs={{0,4},{4,0},{1,5},{5,1},{2,6},{6,2},{3,7},{7,3},{8,12},{12,8},{9,1... | collective-permute-start | bytes 9437192 | tf_op jit(solution)/shard_map/ppermute | solution.py:60
  37.4 5.7 %collective-permute-start.13 = (bf16[512,256]{1,0:T(8,128)(2,1)S(1)}, bf16[512,256]{1,0:T(8,128)(2,1)S(1)}, u32[]{:S(2)}, u32[]{:S(2)}) collective-permute-start(bf16[512,256]{1,0:T(8,128)(2,1)S(1)} %constant_dynamic-update-slice_fusion.2.own_ref), channel_id=1, source_target_pairs={{0,4},{4,0},{1,5},{5,1},{2,6},{6,2},{3,7},{7,3},{8,12},{12,8},{9,1... | collective-permute-start | bytes 786440 | tf_op jit(solution)/shard_map/ppermute | solution.py:60
  37.5 18.8 %collective-permute-start.10 = (bf16[1024,256]{1,0:T(8,128)(2,1)S(1)}, bf16[1024,256]{1,0:T(8,128)(2,1)S(1)}, u32[]{:S(2)}, u32[]{:S(2)}) collective-permute-start(bf16[1024,256]{1,0:T(8,128)(2,1)S(1)} %pad_maximum_fusion.1.refs_1_), channel_id=1, source_target_pairs={{0,32},{64,96},{32,0},{96,64},{1,33},{65,97},{33,1},{97,65},{2,34}... | collective-permute-start | bytes 1572872 | tf_op jit(solution)/shard_map/ppermute | solution.py:40
  39.5 16.8 %collective-permute-start.9 = (bf16[1024,256]{1,0:T(8,128)(2,1)S(1)}, bf16[1024,256]{1,0:T(8,128)(2,1)S(1)}, u32[]{:S(2)}, u32[]{:S(2)}) collective-permute-start(bf16[1024,256]{1,0:T(8,128)(2,1)S(1)} %constant_dynamic-update-slice_fusion.refs_0_), channel_id=1, source_target_pairs={{0,16},{8,24},{16,0},{24,8},{1,17},{9,25},{17,1},{25,9},{2,18},{10... | collective-permute-start | bytes 1572872 | tf_op jit(solution)/shard_map/ppermute | solution.py:44
  44.4 3.7 %collective-permute-start.14 = (f32[32,128]{1,0:T(8,128)S(1)}, f32[32,128]{1,0:T(8,128)S(1)}, u32[]{:S(2)}, u32[]{:S(2)}) collective-permute-start(f32[32,128]{1,0:T(8,128)S(1)} %low_rank.1), channel_id=1, source_target_pairs={{0,1},{1,0},{2,3},{3,2},{4,5},{5,4},{6,7},{7,6},{8,9},{9,8},{10,11... | collective-permute-start | bytes 49160 | tf_op jit(solution)/shard_map/ppermute | solution.py:56
  46.1 10.2 %collective-permute-start.12 = (bf16[48,2048]{1,0:T(8,128)(2,1)S(1)}, bf16[48,2048]{1,0:T(8,128)(2,1)S(1)}, u32[]{:S(2)}, u32[]{:S(2)}) collective-permute-start(bf16[48,2048]{1,0:T(8,128)(2,1)S(1)} %bitcast.40), channel_id=1, source_target_pairs={{0,32},{32,0},{1,33},{33,1},{2,34},{34,2},{3,35},{35,3},{4,36},{36... | collective-permute-start | bytes 589832 | tf_op jit(solution)/shard_map/ppermute | solution.py:48
  48.1 5.7 %collective-permute-start.15 = (f32[64,128]{1,0:T(8,128)S(1)}, f32[64,128]{1,0:T(8,128)S(1)}, u32[]{:S(2)}, u32[]{:S(2)}) collective-permute-start(f32[64,128]{1,0:T(8,128)S(1)} %pad_maximum_fusion.4), channel_id=1, source_target_pairs={{0,2},{1,3},{2,0},{3,1},{4,6},{5,7},{6,4},{7,5},{8,10},{9,11},{10,... | collective-permute-start | bytes 98312 | tf_op jit(solution)/shard_map/ppermute | solution.py:56
  53.9 8.2 %copy-start.2 = (bf16[8,2,16,256]{3,2,1,0:T(8,128)(2,1)S(1)}, bf16[8,2,16,256]{3,2,1,0:T(8,128)(2,1)}, u32[]{:S(2)}) copy-start(bf16[8,2,16,256]{3,2,1,0:T(8,128)(2,1)} %refs_9_.1) | copy-start | bytes 393220
  56.3 5.8 %collective-permute-start.16 = (bf16[1024,256]{1,0:T(8,128)(2,1)S(1)}, bf16[1024,256]{1,0:T(8,128)(2,1)S(1)}, u32[]{:S(2)}, u32[]{:S(2)}) collective-permute-start(bf16[1024,256]{1,0:T(8,128)(2,1)S(1)} %collective-permute-done.9.refs_0_), channel_id=1, source_target_pairs={{0,4},{4,0},{1,5},{5,1},{2,6},{6,2},{3,7},{7,3},{8,12},{12,8},{9,1... | collective-permute-start | bytes 1572872 | tf_op jit(solution)/shard_map/ppermute | solution.py:60
  57.6 4.5 %collective-permute-start.17 = (bf16[1024,256]{1,0:T(8,128)(2,1)S(1)}, bf16[1024,256]{1,0:T(8,128)(2,1)S(1)}, u32[]{:S(2)}, u32[]{:S(2)}) collective-permute-start(bf16[1024,256]{1,0:T(8,128)(2,1)S(1)} %collective-permute-done.10.refs_1_), channel_id=1, source_target_pairs={{0,4},{4,0},{1,5},{5,1},{2,6},{6,2},{3,7},{7,3},{8,12},{12,8},{9,1... | collective-permute-start | bytes 1572872 | tf_op jit(solution)/shard_map/ppermute | solution.py:60
  57.7 11.7 %collective-permute-start.20 = (bf16[96,2048]{1,0:T(8,128)(2,1)S(1)}, bf16[96,2048]{1,0:T(8,128)(2,1)S(1)}, u32[]{:S(2)}, u32[]{:S(2)}) collective-permute-start(bf16[96,2048]{1,0:T(8,128)(2,1)S(1)} %constant_dynamic-update-slice_fusion.13), channel_id=1, source_target_pairs={{0,8},{8,16},{16,24},{24,0},{1,9},{9,17},{17,25},{25,1},{2,10},{10... | collective-permute-start | bytes 1179656 | tf_op jit(solution)/shard_map/ppermute | solution.py:44
  59.2 19.7 %collective-permute-start.21 = (bf16[96,2048]{1,0:T(8,128)(2,1)S(1)}, bf16[96,2048]{1,0:T(8,128)(2,1)S(1)}, u32[]{:S(2)}, u32[]{:S(2)}) collective-permute-start(bf16[96,2048]{1,0:T(8,128)(2,1)S(1)} %constant_dynamic-update-slice_fusion.13), channel_id=1, source_target_pairs={{0,16},{8,24},{16,0},{24,8},{1,17},{9,25},{17,1},{25,9},{2,18},{10... | collective-permute-start | bytes 1179656 | tf_op jit(solution)/shard_map/ppermute | solution.py:44
  61.6 17.2 %collective-permute-start.22 = (bf16[96,2048]{1,0:T(8,128)(2,1)S(1)}, bf16[96,2048]{1,0:T(8,128)(2,1)S(1)}, u32[]{:S(2)}, u32[]{:S(2)}) collective-permute-start(bf16[96,2048]{1,0:T(8,128)(2,1)S(1)} %constant_dynamic-update-slice_fusion.13), channel_id=1, source_target_pairs={{0,24},{8,0},{16,8},{24,16},{1,25},{9,1},{17,9},{25,17},{2,26},{10... | collective-permute-start | bytes 1179656 | tf_op jit(solution)/shard_map/ppermute | solution.py:44
  65.8 18.4 %copy-start.7 = (s32[768]{0:T(1024)S(1)}, s32[768]{0:T(1024)}, u32[]{:S(2)}) copy-start(s32[768]{0:T(1024)} %param.24) | copy-start | bytes 9220
  65.8 18.6 %copy-start = (bf16[2048,512]{1,0:T(8,128)(2,1)S(1)}, bf16[2048,512]{1,0:T(8,128)(2,1)}, u32[]{:S(2)}) copy-start(bf16[2048,512]{1,0:T(8,128)(2,1)} %w_ref.1) | copy-start | bytes 6291460
  65.8 18.6 %copy-start.1 = (bf16[2048,8,16]{0,2,1:T(8,128)(2,1)S(1)}, bf16[2048,8,16]{0,2,1:T(8,128)(2,1)}, u32[]{:S(2)}) copy-start(bf16[2048,8,16]{0,2,1:T(8,128)(2,1)} %param.26) | copy-start | bytes 1572868
  65.8 18.6 %copy-start.3 = (bf16[8,16,512]{2,1,0:T(8,128)(2,1)S(1)}, bf16[8,16,512]{2,1,0:T(8,128)(2,1)}, u32[]{:S(2)}) copy-start(bf16[8,16,512]{2,1,0:T(8,128)(2,1)} %param.27) | copy-start | bytes 393220
  65.8 13.0 %collective-permute-start.18 = (bf16[3,128,2,256]{3,2,1,0:T(2,128)(2,1)S(1)}, bf16[3,128,2,256]{3,2,1,0:T(2,128)(2,1)S(1)}, u32[]{:S(2)}, u32[]{:S(2)}) collective-permute-start(bf16[3,128,2,256]{3,2,1,0:T(2,128)(2,1)S(1)} %get-tuple-element.83), channel_id=1, source_target_pairs={{0,64},{64,0},{1,65},{65,1},{2,66},{66,2},{3,67},{67,3},{4,68},{68... | collective-permute-start | bytes 1179656 | tf_op jit(solution)/shard_map/ppermute | solution.py:492
  67.0 11.9 %collective-permute-start.19 = (bf16[3,128,2,256]{3,2,1,0:T(2,128)(2,1)S(1)}, bf16[3,128,2,256]{3,2,1,0:T(2,128)(2,1)S(1)}, u32[]{:S(2)}, u32[]{:S(2)}) collective-permute-start(bf16[3,128,2,256]{3,2,1,0:T(2,128)(2,1)S(1)} %get-tuple-element.84), channel_id=1, source_target_pairs={{0,96},{32,64},{64,32},{96,0},{1,97},{33,65},{65,33},{97,1},{2,98}... | collective-permute-start | bytes 1179656 | tf_op jit(solution)/shard_map/ppermute | solution.py:32
  79.0 5.4 %collective-permute-start.27 = (bf16[384,2048]{1,0:T(8,128)(2,1)S(1)}, bf16[384,2048]{1,0:T(8,128)(2,1)S(1)}, u32[]{:S(2)}, u32[]{:S(2)}) collective-permute-start(bf16[384,2048]{1,0:T(8,128)(2,1)S(1)} %constant_dynamic-update-slice_fusion.15.refs_0_), channel_id=1, source_target_pairs={{0,4},{4,0},{1,5},{5,1},{2,6},{6,2},{3,7},{7,3},{8,12},{12,8},{9,1... | collective-permute-start | bytes 4718600 | tf_op jit(solution)/shard_map/ppermute | solution.py:60
  81.5 20.4 %collective-permute-start.23 = (bf16[2,3,128,2,256]{4,3,2,1,0:T(2,128)(2,1)S(1)}, bf16[2,3,128,2,256]{4,3,2,1,0:T(2,128)(2,1)S(1)}, u32[]{:S(2)}, u32[]{:S(2)}) collective-permute-start(bf16[2,3,128,2,256]{4,3,2,1,0:T(2,128)(2,1)S(1)} %pad_maximum_fusion.refs_0_), channel_id=1, source_target_pairs={{0,8},{8,16},{16,24},{24,0},{1,9},{9,17},{17,25},{25,1},{2,10},{10... | collective-permute-start | bytes 2359304 | tf_op jit(solution)/shard_map/ppermute | solution.py:44
  82.5 19.4 %collective-permute-start.24 = (bf16[2,3,128,2,256]{4,3,2,1,0:T(2,128)(2,1)S(1)}, bf16[2,3,128,2,256]{4,3,2,1,0:T(2,128)(2,1)S(1)}, u32[]{:S(2)}, u32[]{:S(2)}) collective-permute-start(bf16[2,3,128,2,256]{4,3,2,1,0:T(2,128)(2,1)S(1)} %pad_maximum_fusion.refs_0_), channel_id=1, source_target_pairs={{0,24},{8,0},{16,8},{24,16},{1,25},{9,1},{17,9},{25,17},{2,26},{10... | collective-permute-start | bytes 2359304 | tf_op jit(solution)/shard_map/ppermute | solution.py:44
  89.6 12.3 %collective-permute-start.28 = (bf16[192,512]{1,0:T(8,128)(2,1)S(1)}, bf16[192,512]{1,0:T(8,128)(2,1)S(1)}, u32[]{:S(2)}, u32[]{:S(2)}) collective-permute-start(bf16[192,512]{1,0:T(8,128)(2,1)S(1)} %get-tuple-element.96), channel_id=1, source_target_pairs={{0,1},{1,2},{2,3},{3,0},{4,5},{5,6},{6,7},{7,4},{8,9},{9,10},{10,1... | collective-permute-start | bytes 589832 | tf_op jit(solution)/shard_map/ppermute | solution.py:52
  91.3 11.9 %collective-permute-start.29 = (bf16[192,512]{1,0:T(8,128)(2,1)S(1)}, bf16[192,512]{1,0:T(8,128)(2,1)S(1)}, u32[]{:S(2)}, u32[]{:S(2)}) collective-permute-start(bf16[192,512]{1,0:T(8,128)(2,1)S(1)} %get-tuple-element.97), channel_id=1, source_target_pairs={{0,2},{1,3},{2,0},{3,1},{4,6},{5,7},{6,4},{7,5},{8,10},{9,11},{10,... | collective-permute-start | bytes 589832 | tf_op jit(solution)/shard_map/ppermute | solution.py:52
  94.6 8.6 %collective-permute-start.30 = (bf16[192,512]{1,0:T(8,128)(2,1)S(1)}, bf16[192,512]{1,0:T(8,128)(2,1)S(1)}, u32[]{:S(2)}, u32[]{:S(2)}) collective-permute-start(bf16[192,512]{1,0:T(8,128)(2,1)S(1)} %get-tuple-element.98), channel_id=1, source_target_pairs={{0,3},{1,0},{2,1},{3,2},{4,7},{5,4},{6,5},{7,6},{8,11},{9,8},{10,9... | collective-permute-start | bytes 589832 | tf_op jit(solution)/shard_map/ppermute | solution.py:52
  104.0 14.5 %collective-permute-start.31 = (bf16[2,3,128,2,256]{4,3,2,1,0:T(2,128)(2,1)S(1)}, bf16[2,3,128,2,256]{4,3,2,1,0:T(2,128)(2,1)S(1)}, u32[]{:S(2)}, u32[]{:S(2)}) collective-permute-start(bf16[2,3,128,2,256]{4,3,2,1,0:T(2,128)(2,1)S(1)} %pad_maximum_fusion.refs_0_), channel_id=1, source_target_pairs={{0,4},{4,0},{1,5},{5,1},{2,6},{6,2},{3,7},{7,3},{8,12},{12,8},{9,1... | collective-permute-start | bytes 2359304 | tf_op jit(solution)/shard_map/ppermute | solution.py:60
  105.4 13.1 %collective-permute-start.32 = (bf16[2,3,128,2,256]{4,3,2,1,0:T(2,128)(2,1)S(1)}, bf16[2,3,128,2,256]{4,3,2,1,0:T(2,128)(2,1)S(1)}, u32[]{:S(2)}, u32[]{:S(2)}) collective-permute-start(bf16[2,3,128,2,256]{4,3,2,1,0:T(2,128)(2,1)S(1)} %collective-permute-done.23.refs_1_), channel_id=1, source_target_pairs={{0,4},{4,0},{1,5},{5,1},{2,6},{6,2},{3,7},{7,3},{8,12},{12,8},{9,1... | collective-permute-start | bytes 2359304 | tf_op jit(solution)/shard_map/ppermute | solution.py:60
  105.4 13.1 %collective-permute-start.33 = (bf16[2,3,128,2,256]{4,3,2,1,0:T(2,128)(2,1)S(1)}, bf16[2,3,128,2,256]{4,3,2,1,0:T(2,128)(2,1)S(1)}, u32[]{:S(2)}, u32[]{:S(2)}) collective-permute-start(bf16[2,3,128,2,256]{4,3,2,1,0:T(2,128)(2,1)S(1)} %collective-permute-done.24.refs_2_), channel_id=1, source_target_pairs={{0,4},{4,0},{1,5},{5,1},{2,6},{6,2},{3,7},{7,3},{8,12},{12,8},{9,1... | collective-permute-start | bytes 2359304 | tf_op jit(solution)/shard_map/ppermute | solution.py:60
  106.5 12.0 %collective-permute-start.25 = (bf16[3,128,2,256]{3,2,1,0:T(2,128)(2,1)S(1)}, bf16[3,128,2,256]{3,2,1,0:T(2,128)(2,1)S(1)}, u32[]{:S(2)}, u32[]{:S(2)}) collective-permute-start(bf16[3,128,2,256]{3,2,1,0:T(2,128)(2,1)S(1)} %slice_bitcast_fusion.1), channel_id=1, source_target_pairs={{0,8},{8,16},{16,24},{24,0},{1,9},{9,17},{17,25},{25,1},{2,10},{10... | collective-permute-start | bytes 1179656 | tf_op jit(solution)/shard_map/ppermute | solution.py:44
  106.6 11.9 %collective-permute-start.26 = (bf16[3,128,2,256]{3,2,1,0:T(2,128)(2,1)S(1)}, bf16[3,128,2,256]{3,2,1,0:T(2,128)(2,1)S(1)}, u32[]{:S(2)}, u32[]{:S(2)}) collective-permute-start(bf16[3,128,2,256]{3,2,1,0:T(2,128)(2,1)S(1)} %slice_bitcast_fusion), channel_id=1, source_target_pairs={{0,24},{8,0},{16,8},{24,16},{1,25},{9,1},{17,9},{25,17},{2,26},{10... | collective-permute-start | bytes 1179656 | tf_op jit(solution)/shard_map/ppermute | solution.py:44
  118.6 3.8 %collective-permute-start.34 = (bf16[3,128,2,256]{3,2,1,0:T(2,128)(2,1)S(1)}, bf16[3,128,2,256]{3,2,1,0:T(2,128)(2,1)S(1)}, u32[]{:S(2)}, u32[]{:S(2)}) collective-permute-start(bf16[3,128,2,256]{3,2,1,0:T(2,128)(2,1)S(1)} %collective-permute-done.25), channel_id=1, source_target_pairs={{0,4},{4,0},{1,5},{5,1},{2,6},{6,2},{3,7},{7,3},{8,12},{12,8},{9,1... | collective-permute-start | bytes 1179656 | tf_op jit(solution)/shard_map/ppermute | solution.py:60
  119.4 3.0 %collective-permute-start.35 = (bf16[3,128,2,256]{3,2,1,0:T(2,128)(2,1)S(1)}, bf16[3,128,2,256]{3,2,1,0:T(2,128)(2,1)S(1)}, u32[]{:S(2)}, u32[]{:S(2)}) collective-permute-start(bf16[3,128,2,256]{3,2,1,0:T(2,128)(2,1)S(1)} %collective-permute-done.26), channel_id=1, source_target_pairs={{0,4},{4,0},{1,5},{5,1},{2,6},{6,2},{3,7},{7,3},{8,12},{12,8},{9,1... | collective-permute-start | bytes 1179656 | tf_op jit(solution)/shard_map/ppermute | solution.py:60

commit v9 on v8

--- a/solution.py
+++ b/solution.py
@@ -380,42 +380,50 @@
     )(*ins)
 
 
-def project_kernel(info, keep, down, up, w_ref, *refs):
-    ins, outs, res = refs[:2], refs[2:6], refs[6]
+def project_kernel(last, info, keep, down, up, w_ref, rows_ref, *refs):
     xh, y, core, z = info[XH], info[Y], info[CORE], info[HEAD]
-    value = jnp.concatenate([ref[...] for ref in ins], 0)
+    value = rows_ref[...]
     out = jnp.dot(value, w_ref[...], preferred_element_type=jnp.float32)
     low = lax.dot_general(
         value, down[...], (((1,), (1,)), ((), ())), preferred_element_type=jnp.float32
     )
     owner = lax.broadcasted_iota(jnp.int32, (48, ADAPTERS * RANK), 1) >> 4
-    spots, lows = [], []
+
+    def spot(b, c_of):
+        side = 1 - xh if b % 2 else xh
+        at = (side * 8 + x_order(y)[b // 2] * 2 + c_of) * 48
+        return pl.ds(pl.multiple_of(at, 16), 48)
+
+    c_of = 1 - core if last else core
+    lows = [
+        jnp.where(keep[spot(b, c_of), :] == owner, low[b * 48 : (b + 1) * 48], 0.0)
+        for b in range(8)
+    ]
+    out = (out + split_dot(jnp.concatenate(lows, 0), up[...])).astype(jnp.bfloat16)
+    if not last:
+        refs[0][...] = out
+        return
+    first, outs, res = refs[0], refs[1:5], refs[5]
     for b in range(8):
-        row, c_of = x_order(y)[b % 4], core if b < 4 else 1 - core
-        for i in range(2):
-            side = xh if i == 0 else 1 - xh
-            at = pl.ds(pl.multiple_of((side * 8 + row * 2 + c_of) * 48, 16), 48)
-            n = b * 96 + i * 48
-            spots.append(at)
-            lows.append(jnp.where(keep[at, :] == owner, low[n : n + 48], 0.0))
-    out = (out + split_dot(jnp.concatenate(lows, 0), up[...])).astype(jnp.bfloat16)
-    for n in range(16):
-        res[spots[n], :] = out[n * 48 : (n + 1) * 48]
+        res[spot(b, core), :] = first[b * 48 : (b + 1) * 48]
+        res[spot(b, 1 - core), :] = out[b * 48 : (b + 1) * 48]
     for n in range(4):
         outs[n][...] = res[pl.ds(pl.multiple_of(((z + n) & 3) * 192, 64), 192), :]
 
 
-def project(info, keep, down, up, weight, parts):
-    rows, width = 768, weight.shape[1]
-    return pl.pallas_call(
-        project_kernel,
-        in_specs=[SMEM] + [VMEM] * 6,
-        out_specs=[VMEM] * 4,
-        out_shape=[jax.ShapeDtypeStruct((rows // 4, width), jnp.bfloat16)] * 4,
-        scratch_shapes=[pltpu.VMEM((rows, width), jnp.bfloat16)],
+def project(info, keep, down, up, weight, rows, first=None):
+    last, bf = first is not None, jnp.bfloat16
+    count, width = rows.shape[0], weight.shape[1]
+    shares = [jax.ShapeDtypeStruct((count // 2, width), bf)] * 4
+    return pl.pallas_call(
+        functools.partial(project_kernel, last),
+        in_specs=[SMEM] + [VMEM] * (6 if last else 5),
+        out_specs=[VMEM] * 4 if last else VMEM,
+        out_shape=shares if last else jax.ShapeDtypeStruct((count, width), bf),
+        scratch_shapes=[pltpu.VMEM((2 * count, width), bf)] if last else [],
         compiler_params=params(),
         name="project",
-    )(info, keep, down, up, weight, *parts)
+    )(info, keep, down, up, weight, rows, *([first] if last else []))
 
 
 def ring(value, shift):
@@ -500,7 +508,8 @@
     down = jnp.transpose(output_down_weight, (1, 2, 0)).reshape(ranks, -1)
     up = output_up_weight.reshape(ranks, -1)
     keep = row_adapter_index[:, None]
-    shares = project(info, keep, down, up, output_weight, [mine, partner])
+    shares = project(info, keep, down, up, output_weight, mine)
+    shares = project(info, keep, down, up, output_weight, partner, shares)
     decoded = shares[0].astype(jnp.float32)
     for k, share in ((1, shares[1]), (2, shares[2]), (-1, shares[3])):
         decoded = decoded + z_shift(share, k).astype(jnp.float32)

time: 124 us -> 124 us (level)
    pallas_call x1 -> x2, Pallas kernels: 5.15 us -> 6.02 us  [project(): pl.pallas_call(functools.partial(project_kernel, last), in_specs=[SMEM] +...]
  transfers between devices with their start and end apart: 36 -> 36, of which waited for: 11 -> 11; matrix products, arithmetic and copies ran while one was open for 2% -> 2% of each run, Pallas kernels for 21% -> 22%
where the time goes in v9:
time: 124 us
  starting transfers between devices  51.2 us (41%)
  waiting for transfers between devices  37 us (30%)
  Pallas kernels  30.7 us (25%)
  local copies, waits for them, and re-layouts  2.12 us (2%)
  other arithmetic  1.95 us (2%)
  between operations  1.33 us (1%)
    ppermute x13, waiting for transfers between devices, y_shift(): return lax.ppermute(value, 'y', [(i, (i + k) % 4) for i in range(4)])  32.2 us
    ppermute x13, starting transfers between devices, y_shift(): return lax.ppermute(value, 'y', [(i, (i + k) % 4) for i in range(4)])  18.6 us
    ppermute x10, starting transfers between devices, core_swap(): return lax.ppermute(value, 'core', [(0, 1), (1, 0)])  8.91 us
    pallas_call x1, Pallas kernels, attend(): pl.pallas_call(functools.partial(attend_kernel, first * ROWS_STEP), grid_...  8.47 us
    pallas_call x2, Pallas kernels, project(): pl.pallas_call(functools.partial(project_kernel, last), in_specs=[SMEM] +...  6.02 us
    ppermute x3, starting transfers between devices, z_shift(): return lax.ppermute(value, 'head', [(i, (i + k) % 4) for i in range(4)])  5.75 us
    ppermute x2, starting transfers between devices, z_flip(): return lax.ppermute(value, 'head', [(i, i ^ mask) for i in range(4)])  5.02 us
    ppermute x2, starting transfers between devices, x_mirror(): return lax.ppermute(value, ('pool', 'xh'), [(i, 3 - i) for i in range(4)])  4.92 us
  transfers between devices with their start and end apart: 36, of which 11 were waited for; matrix products, arithmetic and copies ran while one was open for 2% of the time, Pallas kernels for 22%

profile of v9, /device:TPU:1, one launch (start us, length us, event | category | flops | bytes accessed | tf_op | source)
XLA Modules:
  0.0 124.3 jit_solution(5882465362770800334)
XLA Ops:
  0.7 0.8 concatenate.32.info
  1.5 2.8 %pack.1 = (bf16[512,256]{1,0:T(8,128)(2,1)S(1)}, bf16[320,256]{1,0:T(8,128)(2,1)S(1)}) custom-call(s32[17]{0:T(128)S(1)} %concatenate.32.info, bf16[512,2,256]{2,1,0:T(2,128)(2,1)} %w_hbm.1, bf16[512,256]{1,0:T(8,128)(2,1)} %d_hbm.1), custom_call_target="tpu_custom_call" | custom-call | tf_op jit(solution)/shard_map/pack/pallas_call | solution.py:86
  4.2 3.4 %collective-permute-start = (bf16[512,256]{1,0:T(8,128)(2,1)S(1)}, bf16[512,256]{1,0:T(8,128)(2,1)S(1)}, u32[]{:S(2)}, u32[]{:S(2)}) collective-permute-start(bf16[512,256]{1,0:T(8,128)(2,1)S(1)} %get-tuple-element.57), channel_id=1, source_target_pairs={{0,96},{32,64},{64,32},{96,0},{1,97},{33,65},{65,33},{97,1},{2,98}... | collective-permute-start | bytes 786440 | tf_op jit(solution)/shard_map/ppermute | solution.py:32
  7.6 1.3 %collective-permute-start.1 = (bf16[320,256]{1,0:T(8,128)(2,1)S(1)}, bf16[320,256]{1,0:T(8,128)(2,1)S(1)}, u32[]{:S(2)}, u32[]{:S(2)}) collective-permute-start(bf16[320,256]{1,0:T(8,128)(2,1)S(1)} %get-tuple-element.59), channel_id=1, source_target_pairs={{0,8},{8,16},{16,24},{24,0},{1,9},{9,17},{17,25},{25,1},{2,10},{10... | collective-permute-start | bytes 491528 | tf_op jit(solution)/shard_map/ppermute | solution.py:44
  8.9 2.6 %collective-permute-start.2 = (bf16[320,256]{1,0:T(8,128)(2,1)S(1)}, bf16[320,256]{1,0:T(8,128)(2,1)S(1)}, u32[]{:S(2)}, u32[]{:S(2)}) collective-permute-start(bf16[320,256]{1,0:T(8,128)(2,1)S(1)} %get-tuple-element.59), channel_id=1, source_target_pairs={{0,16},{8,24},{16,0},{24,8},{1,17},{9,25},{17,1},{25,9},{2,18},{10... | collective-permute-start | bytes 491528 | tf_op jit(solution)/shard_map/ppermute | solution.py:44
  11.5 1.1 collective-permute-start.3
  12.6 1.1 collective-permute-done.1
  13.7 4.6 %collective-permute-done.2 = bf16[320,256]{1,0:T(8,128)(2,1)S(1)} collective-permute-done((bf16[320,256]{1,0:T(8,128)(2,1)S(1)}, bf16[320,256]{1,0:T(8,128)(2,1)S(1)}, u32[]{:S(2)}, u32[]{:S(2)}) %collective-permute-start.2) | collective-permute-done | bytes 163872 | tf_op jit(solution)/shard_map/ppermute | solution.py:44
  18.5 2.7 %collective-permute-start.7 = (bf16[1024,256]{1,0:T(8,128)(2,1)S(1)}, bf16[1024,256]{1,0:T(8,128)(2,1)S(1)}, u32[]{:S(2)}, u32[]{:S(2)}) collective-permute-start(bf16[1024,256]{1,0:T(8,128)(2,1)S(1)} %pad_maximum_fusion.1.refs_1_), channel_id=1, source_target_pairs={{0,96},{64,0},{32,64},{96,32},{1,97},{65,1},{33,65},{97,33},{2,98}... | collective-permute-start | bytes 1572872 | tf_op jit(solution)/shard_map/ppermute | solution.py:40
  21.3 1.5 %collective-permute-start.4 = (bf16[1024,256]{1,0:T(8,128)(2,1)S(1)}, bf16[1024,256]{1,0:T(8,128)(2,1)S(1)}, u32[]{:S(2)}, u32[]{:S(2)}) collective-permute-start(bf16[1024,256]{1,0:T(8,128)(2,1)S(1)} %constant_dynamic-update-slice_fusion.refs_0_), channel_id=1, source_target_pairs={{0,8},{8,16},{16,24},{24,0},{1,9},{9,17},{17,25},{25,1},{2,10},{10... | collective-permute-start | bytes 1572872 | tf_op jit(solution)/shard_map/ppermute | solution.py:44
  22.7 1.3 %collective-permute-start.5 = (bf16[1024,256]{1,0:T(8,128)(2,1)S(1)}, bf16[1024,256]{1,0:T(8,128)(2,1)S(1)}, u32[]{:S(2)}, u32[]{:S(2)}) collective-permute-start(bf16[1024,256]{1,0:T(8,128)(2,1)S(1)} %constant_dynamic-update-slice_fusion.refs_0_), channel_id=1, source_target_pairs={{0,24},{8,0},{16,8},{24,16},{1,25},{9,1},{17,9},{25,17},{2,26},{10... | collective-permute-start | bytes 1572872 | tf_op jit(solution)/shard_map/ppermute | solution.py:44
  24.2 8.5 %attend.1 = bf16[48,16,128]{2,1,0:T(8,128)(2,1)S(1)} custom-call(s32[48]{0:T(128)S(1)} %copy-done.5, bf16[48,16,128]{2,1,0:T(8,128)(2,1)S(1)} %bitcast.35, bf16[48,128,2,256]{3,2,1,0:T(2,128)(2,1)} %kv_ref.1, bf16[48,2,256]{2,1,0:T(2,128)(2,1)S(1)} %copy-done.4), custom_call_target="tpu_custom_call" | custom-call | tf_op jit(solution)/shard_map/attend/pallas_call | solution.py:146
  34.2 3.2 %collective-permute-start.11 = (bf16[6144,256]{1,0:T(8,128)(2,1)S(1)}, bf16[6144,256]{1,0:T(8,128)(2,1)S(1)}, u32[]{:S(2)}, u32[]{:S(2)}) collective-permute-start(bf16[6144,256]{1,0:T(8,128)(2,1)S(1)} %constant_dynamic-update-slice_fusion.7), channel_id=1, source_target_pairs={{0,4},{4,0},{1,5},{5,1},{2,6},{6,2},{3,7},{7,3},{8,12},{12,8},{9,1... | collective-permute-start | bytes 9437192 | tf_op jit(solution)/shard_map/ppermute | solution.py:60
  37.5 2.0 %collective-permute-start.10 = (bf16[1024,256]{1,0:T(8,128)(2,1)S(1)}, bf16[1024,256]{1,0:T(8,128)(2,1)S(1)}, u32[]{:S(2)}, u32[]{:S(2)}) collective-permute-start(bf16[1024,256]{1,0:T(8,128)(2,1)S(1)} %pad_maximum_fusion.1.refs_1_), channel_id=1, source_target_pairs={{0,32},{64,96},{32,0},{96,64},{1,33},{65,97},{33,1},{97,65},{2,34}... | collective-permute-start | bytes 1572872 | tf_op jit(solution)/shard_map/ppermute | solution.py:40
  39.5 1.1 collective-permute-start.9
  40.6 2.5 %collective-permute-done.13.other_ref = bf16[512,256]{1,0:T(8,128)(2,1)S(1)} collective-permute-done((bf16[512,256]{1,0:T(8,128)(2,1)S(1)}, bf16[512,256]{1,0:T(8,128)(2,1)S(1)}, u32[]{:S(2)}, u32[]{:S(2)}) %collective-permute-start.13) | collective-permute-done | bytes 262176 | tf_op jit(solution)/shard_map/ppermute | solution.py:60
  43.1 1.3 %low_rank.1 = f32[32,128]{1,0:T(8,128)S(1)} custom-call(s32[17]{0:T(128)S(1)} %concatenate.32.info, bf16[512,8192]{1,0:T(8,128)(2,1)S(1)} %bitcast.28, bf16[512,256]{1,0:T(8,128)(2,1)S(1)} %constant_dynamic-update-slice_fusion.2.own_ref, bf16[512,256]{1,0:T(8,128)(2,1)S(1)} %collective-permute-done.13.other_ref), custom_call_target="tpu_custom_call" | custom-call | tf_op jit(solution)/shard_map/low_rank/pallas_call | solution.py:199
  44.4 1.7 %collective-permute-start.14 = (f32[32,128]{1,0:T(8,128)S(1)}, f32[32,128]{1,0:T(8,128)S(1)}, u32[]{:S(2)}, u32[]{:S(2)}) collective-permute-start(f32[32,128]{1,0:T(8,128)S(1)} %low_rank.1), channel_id=1, source_target_pairs={{0,1},{1,0},{2,3},{3,2},{4,5},{5,4},{6,7},{7,6},{8,9},{9,8},{10,11... | collective-permute-start | bytes 49160 | tf_op jit(solution)/shard_map/ppermute | solution.py:56
  46.1 2.0 %collective-permute-start.12 = (bf16[48,2048]{1,0:T(8,128)(2,1)S(1)}, bf16[48,2048]{1,0:T(8,128)(2,1)S(1)}, u32[]{:S(2)}, u32[]{:S(2)}) collective-permute-start(bf16[48,2048]{1,0:T(8,128)(2,1)S(1)} %bitcast.42), channel_id=1, source_target_pairs={{0,32},{32,0},{1,33},{33,1},{2,34},{34,2},{3,35},{35,3},{4,36},{36... | collective-permute-start | bytes 589832 | tf_op jit(solution)/shard_map/ppermute | solution.py:48
  48.1 3.3 %collective-permute-start.15 = (f32[64,128]{1,0:T(8,128)S(1)}, f32[64,128]{1,0:T(8,128)S(1)}, u32[]{:S(2)}, u32[]{:S(2)}) collective-permute-start(f32[64,128]{1,0:T(8,128)S(1)} %pad_maximum_fusion.4), channel_id=1, source_target_pairs={{0,2},{1,3},{2,0},{3,1},{4,6},{5,7},{6,4},{7,5},{8,10},{9,11},{10,... | collective-permute-start | bytes 98312 | tf_op jit(solution)/shard_map/ppermute | solution.py:56
  51.4 2.4 %main_product.2 = (f32[512,256]{1,0:T(8,128)S(1)}, f32[512,256]{1,0:T(8,128)S(1)}) custom-call(s32[17]{0:T(128)S(1)} %concatenate.32.info, bf16[512,8192]{1,0:T(8,128)(2,1)S(1)} %bitcast.29, bf16[1024,256]{1,0:T(8,128)(2,1)S(1)} %constant_dynamic-update-slice_fusion.refs_0_, bf16[1024,256]{1,0:T(8,128)(2,1)S(1)} %pad_maximum_fusion.1.refs_1_, ...), custom_call_target="tpu_custom_call" | custom-call | tf_op jit(solution)/shard_map/main_product/pallas_call | solution.py:242
  53.9 2.3 %main_product.3 = (f32[512,256]{1,0:T(8,128)S(1)}, f32[512,256]{1,0:T(8,128)S(1)}) custom-call(s32[17]{0:T(128)S(1)} %concatenate.32.info, bf16[512,8192]{1,0:T(8,128)(2,1)S(1)} %bitcast.30, bf16[6144,256]{1,0:T(8,128)(2,1)S(1)} %collective-permute-done.11.refs_0_), custom_call_target="tpu_custom_call" | custom-call | tf_op jit(solution)/shard_map/main_product/pallas_call | solution.py:242
  56.3 1.3 %collective-permute-start.16 = (bf16[1024,256]{1,0:T(8,128)(2,1)S(1)}, bf16[1024,256]{1,0:T(8,128)(2,1)S(1)}, u32[]{:S(2)}, u32[]{:S(2)}) collective-permute-start(bf16[1024,256]{1,0:T(8,128)(2,1)S(1)} %collective-permute-done.9.refs_0_), channel_id=1, source_target_pairs={{0,4},{4,0},{1,5},{5,1},{2,6},{6,2},{3,7},{7,3},{8,12},{12,8},{9,1... | collective-permute-start | bytes 1572872 | tf_op jit(solution)/shard_map/ppermute | solution.py:60
  57.7 1.4 %collective-permute-start.20 = (bf16[96,2048]{1,0:T(8,128)(2,1)S(1)}, bf16[96,2048]{1,0:T(8,128)(2,1)S(1)}, u32[]{:S(2)}, u32[]{:S(2)}) collective-permute-start(bf16[96,2048]{1,0:T(8,128)(2,1)S(1)} %constant_dynamic-update-slice_fusion.13), channel_id=1, source_target_pairs={{0,8},{8,16},{16,24},{24,0},{1,9},{9,17},{17,25},{25,1},{2,10},{10... | collective-permute-start | bytes 1179656 | tf_op jit(solution)/shard_map/ppermute | solution.py:44
  59.2 2.5 %collective-permute-start.21 = (bf16[96,2048]{1,0:T(8,128)(2,1)S(1)}, bf16[96,2048]{1,0:T(8,128)(2,1)S(1)}, u32[]{:S(2)}, u32[]{:S(2)}) collective-permute-start(bf16[96,2048]{1,0:T(8,128)(2,1)S(1)} %constant_dynamic-update-slice_fusion.13), channel_id=1, source_target_pairs={{0,16},{8,24},{16,0},{24,8},{1,17},{9,25},{17,1},{25,9},{2,18},{10... | collective-permute-start | bytes 1179656 | tf_op jit(solution)/shard_map/ppermute | solution.py:44
  62.1 3.7 %finish.1 = (bf16[3,128,2,256]{3,2,1,0:T(2,128)(2,1)S(1)}, bf16[3,128,2,256]{3,2,1,0:T(2,128)(2,1)S(1)}) custom-call(s32[17]{0:T(128)S(1)} %concatenate.32.info, bf16[512,8192]{1,0:T(8,128)(2,1)S(1)} %bitcast.31, bf16[1024,256]{1,0:T(8,128)(2,1)S(1)} %collective-permute-done.9.refs_0_, bf16[1024,256]{1,0:T(8,128)(2,1)S(1)} %collective-permute-done.10.refs_1_, ...), custom_call_target="tpu_custom_call" | custom-call | tf_op jit(solution)/shard_map/finish/pallas_call | solution.py:293
  65.8 1.2 collective-permute-start.18
  67.0 1.5 %collective-permute-start.19 = (bf16[3,128,2,256]{3,2,1,0:T(2,128)(2,1)S(1)}, bf16[3,128,2,256]{3,2,1,0:T(2,128)(2,1)S(1)}, u32[]{:S(2)}, u32[]{:S(2)}) collective-permute-start(bf16[3,128,2,256]{3,2,1,0:T(2,128)(2,1)S(1)} %get-tuple-element.84), channel_id=1, source_target_pairs={{0,96},{32,64},{64,32},{96,0},{1,97},{33,65},{65,33},{97,1},{2,98}... | collective-permute-start | bytes 1179656 | tf_op jit(solution)/shard_map/ppermute | solution.py:32
  68.5 1.0 collective-permute-done.20
  69.5 9.4 %collective-permute-done.21 = bf16[96,2048]{1,0:T(8,128)(2,1)S(1)} collective-permute-done((bf16[96,2048]{1,0:T(8,128)(2,1)S(1)}, bf16[96,2048]{1,0:T(8,128)(2,1)S(1)}, u32[]{:S(2)}, u32[]{:S(2)}) %collective-permute-start.21) | collective-permute-done | bytes 393248 | tf_op jit(solution)/shard_map/ppermute | solution.py:44
  79.0 1.3 %collective-permute-start.27 = (bf16[384,2048]{1,0:T(8,128)(2,1)S(1)}, bf16[384,2048]{1,0:T(8,128)(2,1)S(1)}, u32[]{:S(2)}, u32[]{:S(2)}) collective-permute-start(bf16[384,2048]{1,0:T(8,128)(2,1)S(1)} %constant_dynamic-update-slice_fusion.15.rows_ref), channel_id=1, source_target_pairs={{0,4},{4,0},{1,5},{5,1},{2,6},{6,2},{3,7},{7,3},{8,12},{12,8},{9,1... | collective-permute-start | bytes 4718600 | tf_op jit(solution)/shard_map/ppermute | solution.py:60
  80.3 1.1 pad_maximum_fusion.refs_0_
  81.5 1.1 collective-permute-start.23
  82.5 1.7 %collective-permute-start.24 = (bf16[2,3,128,2,256]{4,3,2,1,0:T(2,128)(2,1)S(1)}, bf16[2,3,128,2,256]{4,3,2,1,0:T(2,128)(2,1)S(1)}, u32[]{:S(2)}, u32[]{:S(2)}) collective-permute-start(bf16[2,3,128,2,256]{4,3,2,1,0:T(2,128)(2,1)S(1)} %pad_maximum_fusion.refs_0_), channel_id=1, source_target_pairs={{0,24},{8,0},{16,8},{24,16},{1,25},{9,1},{17,9},{25,17},{2,26},{10... | collective-permute-start | bytes 2359304 | tf_op jit(solution)/shard_map/ppermute | solution.py:44
  84.4 3.0 %project.2.refs_0_ = bf16[384,512]{1,0:T(8,128)(2,1)S(1)} custom-call(s32[17]{0:T(128)S(1)} %concatenate.32.info, s32[768,1]{1,0:T(8,128)S(1)} %broadcast_in_dim.20.keep, bf16[128,2048]{1,0:T(8,128)(2,1)S(1)} %bitcast.32, bf16[128,512]{1,0:T(8,128)(2,1)S(1)} %bitcast.36, bf16[2048,512]{1,0:T(8,128)(2,1)S(1)} %copy-done, ...), custom_call_target="tpu_custom_call" | custom-call | tf_op jit(solution)/shard_map/project/pallas_call | solution.py:418
  87.4 3.0 %project.3 = (bf16[192,512]{1,0:T(8,128)(2,1)S(1)}, bf16[192,512]{1,0:T(8,128)(2,1)S(1)}, bf16[192,512]{1,0:T(8,128)(2,1)S(1)}, bf16[192,512]{1,0:T(8,128)(2,1)S(1)}) custom-call(s32[17]{0:T(128)S(1)} %concatenate.32.info, s32[768,1]{1,0:T(8,128)S(1)} %broadcast_in_dim.20.keep, bf16[128,2048]{1,0:T(8,128)(2,1)S(1)} %bitcast.33, ...), custom_call_target="tpu_custom_call" | custom-call | tf_op jit(solution)/shard_map/project/pallas_call | solution.py:418
  90.4 1.7 %collective-permute-start.28 = (bf16[192,512]{1,0:T(8,128)(2,1)S(1)}, bf16[192,512]{1,0:T(8,128)(2,1)S(1)}, u32[]{:S(2)}, u32[]{:S(2)}) collective-permute-start(bf16[192,512]{1,0:T(8,128)(2,1)S(1)} %get-tuple-element.96), channel_id=1, source_target_pairs={{0,1},{1,2},{2,3},{3,0},{4,5},{5,6},{6,7},{7,4},{8,9},{9,10},{10,1... | collective-permute-start | bytes 589832 | tf_op jit(solution)/shard_map/ppermute | solution.py:52
  92.2 3.3 %collective-permute-start.29 = (bf16[192,512]{1,0:T(8,128)(2,1)S(1)}, bf16[192,512]{1,0:T(8,128)(2,1)S(1)}, u32[]{:S(2)}, u32[]{:S(2)}) collective-permute-start(bf16[192,512]{1,0:T(8,128)(2,1)S(1)} %get-tuple-element.97), channel_id=1, source_target_pairs={{0,2},{1,3},{2,0},{3,1},{4,6},{5,7},{6,4},{7,5},{8,10},{9,11},{10,... | collective-permute-start | bytes 589832 | tf_op jit(solution)/shard_map/ppermute | solution.py:52
  95.5 0.7 collective-permute-start.30
  96.2 5.7 %collective-permute-done.23.refs_1_ = bf16[2,3,128,2,256]{4,3,2,1,0:T(2,128)(2,1)S(1)} collective-permute-done((bf16[2,3,128,2,256]{4,3,2,1,0:T(2,128)(2,1)S(1)}, bf16[2,3,128,2,256]{4,3,2,1,0:T(2,128)(2,1)S(1)}, u32[]{:S(2)}, u32[]{:S(2)}) %collective-permute-start.23) | collective-permute-done | bytes 786464 | tf_op jit(solution)/shard_map/ppermute | solution.py:44
  101.9 2.2 %collective-permute-done.29 = bf16[192,512]{1,0:T(8,128)(2,1)S(1)} collective-permute-done((bf16[192,512]{1,0:T(8,128)(2,1)S(1)}, bf16[192,512]{1,0:T(8,128)(2,1)S(1)}, u32[]{:S(2)}, u32[]{:S(2)}) %collective-permute-start.29) | collective-permute-done | bytes 196640 | tf_op jit(solution)/shard_map/ppermute | solution.py:52
  104.1 0.8 add_convert_fusion
  104.9 1.4 %collective-permute-start.31 = (bf16[2,3,128,2,256]{4,3,2,1,0:T(2,128)(2,1)S(1)}, bf16[2,3,128,2,256]{4,3,2,1,0:T(2,128)(2,1)S(1)}, u32[]{:S(2)}, u32[]{:S(2)}) collective-permute-start(bf16[2,3,128,2,256]{4,3,2,1,0:T(2,128)(2,1)S(1)} %pad_maximum_fusion.refs_0_), channel_id=1, source_target_pairs={{0,4},{4,0},{1,5},{5,1},{2,6},{6,2},{3,7},{7,3},{8,12},{12,8},{9,1... | collective-permute-start | bytes 2359304 | tf_op jit(solution)/shard_map/ppermute | solution.py:60
  107.4 2.7 %collective-permute-start.26 = (bf16[3,128,2,256]{3,2,1,0:T(2,128)(2,1)S(1)}, bf16[3,128,2,256]{3,2,1,0:T(2,128)(2,1)S(1)}, u32[]{:S(2)}, u32[]{:S(2)}) collective-permute-start(bf16[3,128,2,256]{3,2,1,0:T(2,128)(2,1)S(1)} %slice_bitcast_fusion), channel_id=1, source_target_pairs={{0,24},{8,0},{16,8},{24,16},{1,25},{9,1},{17,9},{25,17},{2,26},{10... | collective-permute-start | bytes 1179656 | tf_op jit(solution)/shard_map/ppermute | solution.py:44
  110.1 9.3 %collective-permute-done.25 = bf16[3,128,2,256]{3,2,1,0:T(2,128)(2,1)S(1)} collective-permute-done((bf16[3,128,2,256]{3,2,1,0:T(2,128)(2,1)S(1)}, bf16[3,128,2,256]{3,2,1,0:T(2,128)(2,1)S(1)}, u32[]{:S(2)}, u32[]{:S(2)}) %collective-permute-start.25) | collective-permute-done | bytes 393248 | tf_op jit(solution)/shard_map/ppermute | solution.py:44
  119.4 0.9 collective-permute-start.34
  120.4 2.9 %place.2.refs_4_ = bf16[1,2,2048,2,256]{4,3,2,1,0:T(2,128)(2,1)} custom-call(s32[17]{0:T(128)S(1)} %concatenate.32.info, bf16[2,3,128,2,256]{4,3,2,1,0:T(2,128)(2,1)S(1)} %pad_maximum_fusion.refs_0_, bf16[2,3,128,2,256]{4,3,2,1,0:T(2,128)(2,1)S(1)} %collective-permute-done.23.refs_1_, bf16[2,3,128,2,256]{4,3,2,1,0:T(2,128)(2,1)S(1)} %collective-permute-done.24.refs_2_, ...), custom_call_target="tpu_custom_call" | custom-call | tf_op jit(solution)/shard_map/place/pallas_call | solution.py:368
  123.3 0.9 place.3
  (90 shorter events, 4.1 us)
Async XLA Ops:
  0.6 23.6 %copy-start.5 = (s32[48]{0:T(128)S(1)}, s32[48]{0:T(128)}, u32[]{:S(2)}) copy-start(s32[48]{0:T(128)} %len_ref) | copy-start | bytes 580
  0.6 23.5 %copy-start.6 = (bf16[48,2048]{1,0:T(8,128)(2,1)S(1)}, bf16[48,2048]{1,0:T(8,128)(2,1)}, u32[]{:S(2)}) copy-start(bf16[48,2048]{1,0:T(8,128)(2,1)} %param.20) | copy-start | bytes 589828
  0.7 23.6 %copy-start.4 = (bf16[48,2,256]{2,1,0:T(2,128)(2,1)S(1)}, bf16[48,2,256]{2,1,0:T(2,128)(2,1)}, u32[]{:S(2)}) copy-start(bf16[48,2,256]{2,1,0:T(2,128)(2,1)} %cur_ref.1) | copy-start | bytes 147460
  4.2 14.1 %collective-permute-start = (bf16[512,256]{1,0:T(8,128)(2,1)S(1)}, bf16[512,256]{1,0:T(8,128)(2,1)S(1)}, u32[]{:S(2)}, u32[]{:S(2)}) collective-permute-start(bf16[512,256]{1,0:T(8,128)(2,1)S(1)} %get-tuple-element.57), channel_id=1, source_target_pairs={{0,96},{32,64},{64,32},{96,0},{1,97},{33,65},{65,33},{97,1},{2,98}... | collective-permute-start | bytes 786440 | tf_op jit(solution)/shard_map/ppermute | solution.py:32
  7.6 6.1 %collective-permute-start.1 = (bf16[320,256]{1,0:T(8,128)(2,1)S(1)}, bf16[320,256]{1,0:T(8,128)(2,1)S(1)}, u32[]{:S(2)}, u32[]{:S(2)}) collective-permute-start(bf16[320,256]{1,0:T(8,128)(2,1)S(1)} %get-tuple-element.59), channel_id=1, source_target_pairs={{0,8},{8,16},{16,24},{24,0},{1,9},{9,17},{17,25},{25,1},{2,10},{10... | collective-permute-start | bytes 491528 | tf_op jit(solution)/shard_map/ppermute | solution.py:44
  8.9 9.4 %collective-permute-start.2 = (bf16[320,256]{1,0:T(8,128)(2,1)S(1)}, bf16[320,256]{1,0:T(8,128)(2,1)S(1)}, u32[]{:S(2)}, u32[]{:S(2)}) collective-permute-start(bf16[320,256]{1,0:T(8,128)(2,1)S(1)} %get-tuple-element.59), channel_id=1, source_target_pairs={{0,16},{8,24},{16,0},{24,8},{1,17},{9,25},{17,1},{25,9},{2,18},{10... | collective-permute-start | bytes 491528 | tf_op jit(solution)/shard_map/ppermute | solution.py:44
  11.5 6.8 %collective-permute-start.3 = (bf16[320,256]{1,0:T(8,128)(2,1)S(1)}, bf16[320,256]{1,0:T(8,128)(2,1)S(1)}, u32[]{:S(2)}, u32[]{:S(2)}) collective-permute-start(bf16[320,256]{1,0:T(8,128)(2,1)S(1)} %get-tuple-element.59), channel_id=1, source_target_pairs={{0,24},{8,0},{16,8},{24,16},{1,25},{9,1},{17,9},{25,17},{2,26},{10... | collective-permute-start | bytes 491528 | tf_op jit(solution)/shard_map/ppermute | solution.py:44
  18.5 14.3 %collective-permute-start.6 = (bf16[1024,256]{1,0:T(8,128)(2,1)S(1)}, bf16[1024,256]{1,0:T(8,128)(2,1)S(1)}, u32[]{:S(2)}, u32[]{:S(2)}) collective-permute-start(bf16[1024,256]{1,0:T(8,128)(2,1)S(1)} %pad_maximum_fusion.1.refs_1_), channel_id=1, source_target_pairs={{0,64},{64,32},{32,96},{96,0},{1,65},{65,33},{33,97},{97,1},{2,66}... | collective-permute-start | bytes 1572872 | tf_op jit(solution)/shard_map/ppermute | solution.py:40
  18.5 14.3 %collective-permute-start.7 = (bf16[1024,256]{1,0:T(8,128)(2,1)S(1)}, bf16[1024,256]{1,0:T(8,128)(2,1)S(1)}, u32[]{:S(2)}, u32[]{:S(2)}) collective-permute-start(bf16[1024,256]{1,0:T(8,128)(2,1)S(1)} %pad_maximum_fusion.1.refs_1_), channel_id=1, source_target_pairs={{0,96},{64,0},{32,64},{96,32},{1,97},{65,1},{33,65},{97,33},{2,98}... | collective-permute-start | bytes 1572872 | tf_op jit(solution)/shard_map/ppermute | solution.py:40
  21.2 21.8 %slice-start = ((s8[8388608]{0:T(1024)(128)(4,1)}), s8[4194304]{0:T(1024)(128)(4,1)S(1)}, s32[]{:S(2)}) async-start(s8[8388608]{0:T(1024)(128)(4,1)} %bitcast.26), calls=%async_computation | async-start | bytes 8388608
  21.3 12.3 %collective-permute-start.4 = (bf16[1024,256]{1,0:T(8,128)(2,1)S(1)}, bf16[1024,256]{1,0:T(8,128)(2,1)S(1)}, u32[]{:S(2)}, u32[]{:S(2)}) collective-permute-start(bf16[1024,256]{1,0:T(8,128)(2,1)S(1)} %constant_dynamic-update-slice_fusion.refs_0_), channel_id=1, source_target_pairs={{0,8},{8,16},{16,24},{24,0},{1,9},{9,17},{17,25},{25,1},{2,10},{10... | collective-permute-start | bytes 1572872 | tf_op jit(solution)/shard_map/ppermute | solution.py:44
  22.7 11.2 %collective-permute-start.5 = (bf16[1024,256]{1,0:T(8,128)(2,1)S(1)}, bf16[1024,256]{1,0:T(8,128)(2,1)S(1)}, u32[]{:S(2)}, u32[]{:S(2)}) collective-permute-start(bf16[1024,256]{1,0:T(8,128)(2,1)S(1)} %constant_dynamic-update-slice_fusion.refs_0_), channel_id=1, source_target_pairs={{0,24},{8,0},{16,8},{24,16},{1,25},{9,1},{17,9},{25,17},{2,26},{10... | collective-permute-start | bytes 1572872 | tf_op jit(solution)/shard_map/ppermute | solution.py:44
  24.1 8.7 %collective-permute-start.8 = (bf16[256,256]{1,0:T(8,128)(2,1)S(1)}, bf16[256,256]{1,0:T(8,128)(2,1)S(1)}, u32[]{:S(2)}, u32[]{:S(2)}) collective-permute-start(bf16[256,256]{1,0:T(8,128)(2,1)S(1)} %pad_maximum_fusion.2), channel_id=1, source_target_pairs={{0,32},{32,0},{1,33},{33,1},{2,34},{34,2},{3,35},{35,3},{4,36},{36... | collective-permute-start | bytes 393224 | tf_op jit(solution)/shard_map/ppermute | solution.py:48
  24.2 18.8 %slice-start.1 = ((s8[8388608]{0:T(1024)(128)(4,1)}), s8[4194304]{0:T(1024)(128)(4,1)S(1)}, s32[]{:S(2)}) async-start(s8[8388608]{0:T(1024)(128)(4,1)} %bitcast.26), calls=%async_computation.1 | async-start | bytes 8388608
  34.2 19.6 %collective-permute-start.11 = (bf16[6144,256]{1,0:T(8,128)(2,1)S(1)}, bf16[6144,256]{1,0:T(8,128)(2,1)S(1)}, u32[]{:S(2)}, u32[]{:S(2)}) collective-permute-start(bf16[6144,256]{1,0:T(8,128)(2,1)S(1)} %constant_dynamic-update-slice_fusion.7), channel_id=1, source_target_pairs={{0,4},{4,0},{1,5},{5,1},{2,6},{6,2},{3,7},{7,3},{8,12},{12,8},{9,1... | collective-permute-start | bytes 9437192 | tf_op jit(solution)/shard_map/ppermute | solution.py:60
  37.4 5.7 %collective-permute-start.13 = (bf16[512,256]{1,0:T(8,128)(2,1)S(1)}, bf16[512,256]{1,0:T(8,128)(2,1)S(1)}, u32[]{:S(2)}, u32[]{:S(2)}) collective-permute-start(bf16[512,256]{1,0:T(8,128)(2,1)S(1)} %constant_dynamic-update-slice_fusion.2.own_ref), channel_id=1, source_target_pairs={{0,4},{4,0},{1,5},{5,1},{2,6},{6,2},{3,7},{7,3},{8,12},{12,8},{9,1... | collective-permute-start | bytes 786440 | tf_op jit(solution)/shard_map/ppermute | solution.py:60
  37.5 18.8 %collective-permute-start.10 = (bf16[1024,256]{1,0:T(8,128)(2,1)S(1)}, bf16[1024,256]{1,0:T(8,128)(2,1)S(1)}, u32[]{:S(2)}, u32[]{:S(2)}) collective-permute-start(bf16[1024,256]{1,0:T(8,128)(2,1)S(1)} %pad_maximum_fusion.1.refs_1_), channel_id=1, source_target_pairs={{0,32},{64,96},{32,0},{96,64},{1,33},{65,97},{33,1},{97,65},{2,34}... | collective-permute-start | bytes 1572872 | tf_op jit(solution)/shard_map/ppermute | solution.py:40
  39.5 16.8 %collective-permute-start.9 = (bf16[1024,256]{1,0:T(8,128)(2,1)S(1)}, bf16[1024,256]{1,0:T(8,128)(2,1)S(1)}, u32[]{:S(2)}, u32[]{:S(2)}) collective-permute-start(bf16[1024,256]{1,0:T(8,128)(2,1)S(1)} %constant_dynamic-update-slice_fusion.refs_0_), channel_id=1, source_target_pairs={{0,16},{8,24},{16,0},{24,8},{1,17},{9,25},{17,1},{25,9},{2,18},{10... | collective-permute-start | bytes 1572872 | tf_op jit(solution)/shard_map/ppermute | solution.py:44
  44.4 3.7 %collective-permute-start.14 = (f32[32,128]{1,0:T(8,128)S(1)}, f32[32,128]{1,0:T(8,128)S(1)}, u32[]{:S(2)}, u32[]{:S(2)}) collective-permute-start(f32[32,128]{1,0:T(8,128)S(1)} %low_rank.1), channel_id=1, source_target_pairs={{0,1},{1,0},{2,3},{3,2},{4,5},{5,4},{6,7},{7,6},{8,9},{9,8},{10,11... | collective-permute-start | bytes 49160 | tf_op jit(solution)/shard_map/ppermute | solution.py:56
  46.1 10.2 %collective-permute-start.12 = (bf16[48,2048]{1,0:T(8,128)(2,1)S(1)}, bf16[48,2048]{1,0:T(8,128)(2,1)S(1)}, u32[]{:S(2)}, u32[]{:S(2)}) collective-permute-start(bf16[48,2048]{1,0:T(8,128)(2,1)S(1)} %bitcast.42), channel_id=1, source_target_pairs={{0,32},{32,0},{1,33},{33,1},{2,34},{34,2},{3,35},{35,3},{4,36},{36... | collective-permute-start | bytes 589832 | tf_op jit(solution)/shard_map/ppermute | solution.py:48
  48.1 5.7 %collective-permute-start.15 = (f32[64,128]{1,0:T(8,128)S(1)}, f32[64,128]{1,0:T(8,128)S(1)}, u32[]{:S(2)}, u32[]{:S(2)}) collective-permute-start(f32[64,128]{1,0:T(8,128)S(1)} %pad_maximum_fusion.4), channel_id=1, source_target_pairs={{0,2},{1,3},{2,0},{3,1},{4,6},{5,7},{6,4},{7,5},{8,10},{9,11},{10,... | collective-permute-start | bytes 98312 | tf_op jit(solution)/shard_map/ppermute | solution.py:56
  53.9 8.2 %copy-start.3 = (bf16[8,2,16,256]{3,2,1,0:T(8,128)(2,1)S(1)}, bf16[8,2,16,256]{3,2,1,0:T(8,128)(2,1)}, u32[]{:S(2)}) copy-start(bf16[8,2,16,256]{3,2,1,0:T(8,128)(2,1)} %refs_9_.1) | copy-start | bytes 393220
  56.3 5.8 %collective-permute-start.16 = (bf16[1024,256]{1,0:T(8,128)(2,1)S(1)}, bf16[1024,256]{1,0:T(8,128)(2,1)S(1)}, u32[]{:S(2)}, u32[]{:S(2)}) collective-permute-start(bf16[1024,256]{1,0:T(8,128)(2,1)S(1)} %collective-permute-done.9.refs_0_), channel_id=1, source_target_pairs={{0,4},{4,0},{1,5},{5,1},{2,6},{6,2},{3,7},{7,3},{8,12},{12,8},{9,1... | collective-permute-start | bytes 1572872 | tf_op jit(solution)/shard_map/ppermute | solution.py:60
  57.6 4.5 %collective-permute-start.17 = (bf16[1024,256]{1,0:T(8,128)(2,1)S(1)}, bf16[1024,256]{1,0:T(8,128)(2,1)S(1)}, u32[]{:S(2)}, u32[]{:S(2)}) collective-permute-start(bf16[1024,256]{1,0:T(8,128)(2,1)S(1)} %collective-permute-done.10.refs_1_), channel_id=1, source_target_pairs={{0,4},{4,0},{1,5},{5,1},{2,6},{6,2},{3,7},{7,3},{8,12},{12,8},{9,1... | collective-permute-start | bytes 1572872 | tf_op jit(solution)/shard_map/ppermute | solution.py:60
  57.7 11.7 %collective-permute-start.20 = (bf16[96,2048]{1,0:T(8,128)(2,1)S(1)}, bf16[96,2048]{1,0:T(8,128)(2,1)S(1)}, u32[]{:S(2)}, u32[]{:S(2)}) collective-permute-start(bf16[96,2048]{1,0:T(8,128)(2,1)S(1)} %constant_dynamic-update-slice_fusion.13), channel_id=1, source_target_pairs={{0,8},{8,16},{16,24},{24,0},{1,9},{9,17},{17,25},{25,1},{2,10},{10... | collective-permute-start | bytes 1179656 | tf_op jit(solution)/shard_map/ppermute | solution.py:44
  59.2 19.7 %collective-permute-start.21 = (bf16[96,2048]{1,0:T(8,128)(2,1)S(1)}, bf16[96,2048]{1,0:T(8,128)(2,1)S(1)}, u32[]{:S(2)}, u32[]{:S(2)}) collective-permute-start(bf16[96,2048]{1,0:T(8,128)(2,1)S(1)} %constant_dynamic-update-slice_fusion.13), channel_id=1, source_target_pairs={{0,16},{8,24},{16,0},{24,8},{1,17},{9,25},{17,1},{25,9},{2,18},{10... | collective-permute-start | bytes 1179656 | tf_op jit(solution)/shard_map/ppermute | solution.py:44
  61.6 17.2 %collective-permute-start.22 = (bf16[96,2048]{1,0:T(8,128)(2,1)S(1)}, bf16[96,2048]{1,0:T(8,128)(2,1)S(1)}, u32[]{:S(2)}, u32[]{:S(2)}) collective-permute-start(bf16[96,2048]{1,0:T(8,128)(2,1)S(1)} %constant_dynamic-update-slice_fusion.13), channel_id=1, source_target_pairs={{0,24},{8,0},{16,8},{24,16},{1,25},{9,1},{17,9},{25,17},{2,26},{10... | collective-permute-start | bytes 1179656 | tf_op jit(solution)/shard_map/ppermute | solution.py:44
  65.8 18.4 %copy-start.7 = (s32[768]{0:T(1024)S(1)}, s32[768]{0:T(1024)}, u32[]{:S(2)}) copy-start(s32[768]{0:T(1024)} %param.24) | copy-start | bytes 9220
  65.8 18.6 %copy-start = (bf16[2048,512]{1,0:T(8,128)(2,1)S(1)}, bf16[2048,512]{1,0:T(8,128)(2,1)}, u32[]{:S(2)}) copy-start(bf16[2048,512]{1,0:T(8,128)(2,1)} %w_ref.3) | copy-start | bytes 6291460
  65.8 18.6 %copy-start.1 = (bf16[2048,8,16]{0,2,1:T(8,128)(2,1)S(1)}, bf16[2048,8,16]{0,2,1:T(8,128)(2,1)}, u32[]{:S(2)}) copy-start(bf16[2048,8,16]{0,2,1:T(8,128)(2,1)} %param.26) | copy-start | bytes 1572868
  65.8 18.6 %copy-start.2 = (bf16[8,16,512]{2,1,0:T(8,128)(2,1)S(1)}, bf16[8,16,512]{2,1,0:T(8,128)(2,1)}, u32[]{:S(2)}) copy-start(bf16[8,16,512]{2,1,0:T(8,128)(2,1)} %param.27) | copy-start | bytes 393220
  65.8 13.0 %collective-permute-start.18 = (bf16[3,128,2,256]{3,2,1,0:T(2,128)(2,1)S(1)}, bf16[3,128,2,256]{3,2,1,0:T(2,128)(2,1)S(1)}, u32[]{:S(2)}, u32[]{:S(2)}) collective-permute-start(bf16[3,128,2,256]{3,2,1,0:T(2,128)(2,1)S(1)} %get-tuple-element.83), channel_id=1, source_target_pairs={{0,64},{64,0},{1,65},{65,1},{2,66},{66,2},{3,67},{67,3},{4,68},{68... | collective-permute-start | bytes 1179656 | tf_op jit(solution)/shard_map/ppermute | solution.py:500
  67.0 11.9 %collective-permute-start.19 = (bf16[3,128,2,256]{3,2,1,0:T(2,128)(2,1)S(1)}, bf16[3,128,2,256]{3,2,1,0:T(2,128)(2,1)S(1)}, u32[]{:S(2)}, u32[]{:S(2)}) collective-permute-start(bf16[3,128,2,256]{3,2,1,0:T(2,128)(2,1)S(1)} %get-tuple-element.84), channel_id=1, source_target_pairs={{0,96},{32,64},{64,32},{96,0},{1,97},{33,65},{65,33},{97,1},{2,98}... | collective-permute-start | bytes 1179656 | tf_op jit(solution)/shard_map/ppermute | solution.py:32
  79.0 8.4 %collective-permute-start.27 = (bf16[384,2048]{1,0:T(8,128)(2,1)S(1)}, bf16[384,2048]{1,0:T(8,128)(2,1)S(1)}, u32[]{:S(2)}, u32[]{:S(2)}) collective-permute-start(bf16[384,2048]{1,0:T(8,128)(2,1)S(1)} %constant_dynamic-update-slice_fusion.15.rows_ref), channel_id=1, source_target_pairs={{0,4},{4,0},{1,5},{5,1},{2,6},{6,2},{3,7},{7,3},{8,12},{12,8},{9,1... | collective-permute-start | bytes 4718600 | tf_op jit(solution)/shard_map/ppermute | solution.py:60
  81.5 20.4 %collective-permute-start.23 = (bf16[2,3,128,2,256]{4,3,2,1,0:T(2,128)(2,1)S(1)}, bf16[2,3,128,2,256]{4,3,2,1,0:T(2,128)(2,1)S(1)}, u32[]{:S(2)}, u32[]{:S(2)}) collective-permute-start(bf16[2,3,128,2,256]{4,3,2,1,0:T(2,128)(2,1)S(1)} %pad_maximum_fusion.refs_0_), channel_id=1, source_target_pairs={{0,8},{8,16},{16,24},{24,0},{1,9},{9,17},{17,25},{25,1},{2,10},{10... | collective-permute-start | bytes 2359304 | tf_op jit(solution)/shard_map/ppermute | solution.py:44
  82.5 19.4 %collective-permute-start.24 = (bf16[2,3,128,2,256]{4,3,2,1,0:T(2,128)(2,1)S(1)}, bf16[2,3,128,2,256]{4,3,2,1,0:T(2,128)(2,1)S(1)}, u32[]{:S(2)}, u32[]{:S(2)}) collective-permute-start(bf16[2,3,128,2,256]{4,3,2,1,0:T(2,128)(2,1)S(1)} %pad_maximum_fusion.refs_0_), channel_id=1, source_target_pairs={{0,24},{8,0},{16,8},{24,16},{1,25},{9,1},{17,9},{25,17},{2,26},{10... | collective-permute-start | bytes 2359304 | tf_op jit(solution)/shard_map/ppermute | solution.py:44
  90.4 11.5 %collective-permute-start.28 = (bf16[192,512]{1,0:T(8,128)(2,1)S(1)}, bf16[192,512]{1,0:T(8,128)(2,1)S(1)}, u32[]{:S(2)}, u32[]{:S(2)}) collective-permute-start(bf16[192,512]{1,0:T(8,128)(2,1)S(1)} %get-tuple-element.96), channel_id=1, source_target_pairs={{0,1},{1,2},{2,3},{3,0},{4,5},{5,6},{6,7},{7,4},{8,9},{9,10},{10,1... | collective-permute-start | bytes 589832 | tf_op jit(solution)/shard_map/ppermute | solution.py:52
  92.2 11.9 %collective-permute-start.29 = (bf16[192,512]{1,0:T(8,128)(2,1)S(1)}, bf16[192,512]{1,0:T(8,128)(2,1)S(1)}, u32[]{:S(2)}, u32[]{:S(2)}) collective-permute-start(bf16[192,512]{1,0:T(8,128)(2,1)S(1)} %get-tuple-element.97), channel_id=1, source_target_pairs={{0,2},{1,3},{2,0},{3,1},{4,6},{5,7},{6,4},{7,5},{8,10},{9,11},{10,... | collective-permute-start | bytes 589832 | tf_op jit(solution)/shard_map/ppermute | solution.py:52
  95.5 8.6 %collective-permute-start.30 = (bf16[192,512]{1,0:T(8,128)(2,1)S(1)}, bf16[192,512]{1,0:T(8,128)(2,1)S(1)}, u32[]{:S(2)}, u32[]{:S(2)}) collective-permute-start(bf16[192,512]{1,0:T(8,128)(2,1)S(1)} %get-tuple-element.98), channel_id=1, source_target_pairs={{0,3},{1,0},{2,1},{3,2},{4,7},{5,4},{6,5},{7,6},{8,11},{9,8},{10,9... | collective-permute-start | bytes 589832 | tf_op jit(solution)/shard_map/ppermute | solution.py:52
  104.9 14.5 %collective-permute-start.31 = (bf16[2,3,128,2,256]{4,3,2,1,0:T(2,128)(2,1)S(1)}, bf16[2,3,128,2,256]{4,3,2,1,0:T(2,128)(2,1)S(1)}, u32[]{:S(2)}, u32[]{:S(2)}) collective-permute-start(bf16[2,3,128,2,256]{4,3,2,1,0:T(2,128)(2,1)S(1)} %pad_maximum_fusion.refs_0_), channel_id=1, source_target_pairs={{0,4},{4,0},{1,5},{5,1},{2,6},{6,2},{3,7},{7,3},{8,12},{12,8},{9,1... | collective-permute-start | bytes 2359304 | tf_op jit(solution)/shard_map/ppermute | solution.py:60
  106.3 13.1 %collective-permute-start.32 = (bf16[2,3,128,2,256]{4,3,2,1,0:T(2,128)(2,1)S(1)}, bf16[2,3,128,2,256]{4,3,2,1,0:T(2,128)(2,1)S(1)}, u32[]{:S(2)}, u32[]{:S(2)}) collective-permute-start(bf16[2,3,128,2,256]{4,3,2,1,0:T(2,128)(2,1)S(1)} %collective-permute-done.23.refs_1_), channel_id=1, source_target_pairs={{0,4},{4,0},{1,5},{5,1},{2,6},{6,2},{3,7},{7,3},{8,12},{12,8},{9,1... | collective-permute-start | bytes 2359304 | tf_op jit(solution)/shard_map/ppermute | solution.py:60
  106.3 13.1 %collective-permute-start.33 = (bf16[2,3,128,2,256]{4,3,2,1,0:T(2,128)(2,1)S(1)}, bf16[2,3,128,2,256]{4,3,2,1,0:T(2,128)(2,1)S(1)}, u32[]{:S(2)}, u32[]{:S(2)}) collective-permute-start(bf16[2,3,128,2,256]{4,3,2,1,0:T(2,128)(2,1)S(1)} %collective-permute-done.24.refs_2_), channel_id=1, source_target_pairs={{0,4},{4,0},{1,5},{5,1},{2,6},{6,2},{3,7},{7,3},{8,12},{12,8},{9,1... | collective-permute-start | bytes 2359304 | tf_op jit(solution)/shard_map/ppermute | solution.py:60
  107.4 12.0 %collective-permute-start.25 = (bf16[3,128,2,256]{3,2,1,0:T(2,128)(2,1)S(1)}, bf16[3,128,2,256]{3,2,1,0:T(2,128)(2,1)S(1)}, u32[]{:S(2)}, u32[]{:S(2)}) collective-permute-start(bf16[3,128,2,256]{3,2,1,0:T(2,128)(2,1)S(1)} %slice_bitcast_fusion.1), channel_id=1, source_target_pairs={{0,8},{8,16},{16,24},{24,0},{1,9},{9,17},{17,25},{25,1},{2,10},{10... | collective-permute-start | bytes 1179656 | tf_op jit(solution)/shard_map/ppermute | solution.py:44
  107.4 11.9 %collective-permute-start.26 = (bf16[3,128,2,256]{3,2,1,0:T(2,128)(2,1)S(1)}, bf16[3,128,2,256]{3,2,1,0:T(2,128)(2,1)S(1)}, u32[]{:S(2)}, u32[]{:S(2)}) collective-permute-start(bf16[3,128,2,256]{3,2,1,0:T(2,128)(2,1)S(1)} %slice_bitcast_fusion), channel_id=1, source_target_pairs={{0,24},{8,0},{16,8},{24,16},{1,25},{9,1},{17,9},{25,17},{2,26},{10... | collective-permute-start | bytes 1179656 | tf_op jit(solution)/shard_map/ppermute | solution.py:44
  119.4 3.8 %collective-permute-start.34 = (bf16[3,128,2,256]{3,2,1,0:T(2,128)(2,1)S(1)}, bf16[3,128,2,256]{3,2,1,0:T(2,128)(2,1)S(1)}, u32[]{:S(2)}, u32[]{:S(2)}) collective-permute-start(bf16[3,128,2,256]{3,2,1,0:T(2,128)(2,1)S(1)} %collective-permute-done.25), channel_id=1, source_target_pairs={{0,4},{4,0},{1,5},{5,1},{2,6},{6,2},{3,7},{7,3},{8,12},{12,8},{9,1... | collective-permute-start | bytes 1179656 | tf_op jit(solution)/shard_map/ppermute | solution.py:60
  120.3 3.0 %collective-permute-start.35 = (bf16[3,128,2,256]{3,2,1,0:T(2,128)(2,1)S(1)}, bf16[3,128,2,256]{3,2,1,0:T(2,128)(2,1)S(1)}, u32[]{:S(2)}, u32[]{:S(2)}) collective-permute-start(bf16[3,128,2,256]{3,2,1,0:T(2,128)(2,1)S(1)} %collective-permute-done.26), channel_id=1, source_target_pairs={{0,4},{4,0},{1,5},{5,1},{2,6},{6,2},{3,7},{7,3},{8,12},{12,8},{9,1... | collective-permute-start | bytes 1179656 | tf_op jit(solution)/shard_map/ppermute | solution.py:60

commit v10 on v8

--- a/solution.py
+++ b/solution.py
@@ -500,16 +500,14 @@
     down = jnp.transpose(output_down_weight, (1, 2, 0)).reshape(ranks, -1)
     up = output_up_weight.reshape(ranks, -1)
     keep = row_adapter_index[:, None]
-    shares = project(info, keep, down, up, output_weight, [mine, partner])
-    decoded = shares[0].astype(jnp.float32)
-    for k, share in ((1, shares[1]), (2, shares[2]), (-1, shares[3])):
-        decoded = decoded + z_shift(share, k).astype(jnp.float32)
-    decoded = decoded.astype(jnp.bfloat16)
-    both1, both3 = barrier((both1, both3))
+    shares = list(project(info, keep, down, up, output_weight, [mine, partner]))
+    shares[1:] = [z_shift(v, k) for v, k in zip(shares[1:], (1, 2, -1))]
+    both0, both1, both3, shares[:3] = barrier((both0, both1, both3, shares[:3]))
+    decoded = sum(v.astype(jnp.float32) for v in shares).astype(jnp.bfloat16)
     b2, a2 = y_shift(both1[0], 1), y_shift(both3[1], -1)
-    middle, decoded = barrier(([both0, both1, both3], decoded))
+    middle = [both0, both1, both3]
     theirs = [core_swap(v) for v in middle]
-    b2, a2, theirs = barrier((b2, a2, theirs))
+    b2, a2, theirs, decoded = barrier((b2, a2, theirs, decoded))
     theirs2 = [core_swap(b2), core_swap(a2)]
     kinds = ((0, 0), (1, 0), (0, 1), (1, 1), (0, 3), (1, 3))
     rest = ((0, 2), (1, 2))

time: 124 us -> 123 us (level)
  no operation moved by 1% of the time
where the time goes in v10:
time: 123 us; the launch traced here: 122 us
  starting transfers between devices  51.3 us (42%)
  waiting for transfers between devices  35.8 us (29%)
  Pallas kernels  29.8 us (24%)
  local copies, waits for them, and re-layouts  2.12 us (2%)
  other arithmetic  1.95 us (2%)
  between operations  1.34 us (1%)
    ppermute x13, waiting for transfers between devices, y_shift(): return lax.ppermute(value, 'y', [(i, (i + k) % 4) for i in range(4)])  31.9 us
    ppermute x13, starting transfers between devices, y_shift(): return lax.ppermute(value, 'y', [(i, (i + k) % 4) for i in range(4)])  18.7 us
    ppermute x10, starting transfers between devices, core_swap(): return lax.ppermute(value, 'core', [(0, 1), (1, 0)])  8.91 us
    pallas_call x1, Pallas kernels, attend(): pl.pallas_call(functools.partial(attend_kernel, first * ROWS_STEP), grid_...  8.47 us
    ppermute x3, starting transfers between devices, z_shift(): return lax.ppermute(value, 'head', [(i, (i + k) % 4) for i in range(4)])  5.75 us
    pallas_call x1, Pallas kernels, project(): pl.pallas_call(project_kernel, in_specs=[SMEM] + [VMEM] * 6, out_specs=[V...  5.15 us
    ppermute x2, starting transfers between devices, z_flip(): return lax.ppermute(value, 'head', [(i, i ^ mask) for i in range(4)])  5.02 us
    ppermute x2, starting transfers between devices, x_mirror(): return lax.ppermute(value, ('pool', 'xh'), [(i, 3 - i) for i in range(4)])  4.92 us
  transfers between devices with their start and end apart: 36, of which 11 were waited for; matrix products, arithmetic and copies ran while one was open for 2% of the time, Pallas kernels for 21%

profile of v10, /device:TPU:1, one launch (start us, length us, event | category | flops | bytes accessed | tf_op | source)
XLA Modules:
  0.0 122.4 jit_solution(12985516470430241626)
XLA Ops:
  0.7 0.8 concatenate.32.info
  1.5 2.8 %pack.1 = (bf16[512,256]{1,0:T(8,128)(2,1)S(1)}, bf16[320,256]{1,0:T(8,128)(2,1)S(1)}) custom-call(s32[17]{0:T(128)S(1)} %concatenate.32.info, bf16[512,2,256]{2,1,0:T(2,128)(2,1)} %w_hbm.1, bf16[512,256]{1,0:T(8,128)(2,1)} %d_hbm.1), custom_call_target="tpu_custom_call" | custom-call | tf_op jit(solution)/shard_map/pack/pallas_call | solution.py:86
  4.2 3.4 %collective-permute-start = (bf16[512,256]{1,0:T(8,128)(2,1)S(1)}, bf16[512,256]{1,0:T(8,128)(2,1)S(1)}, u32[]{:S(2)}, u32[]{:S(2)}) collective-permute-start(bf16[512,256]{1,0:T(8,128)(2,1)S(1)} %get-tuple-element.58), channel_id=1, source_target_pairs={{0,96},{32,64},{64,32},{96,0},{1,97},{33,65},{65,33},{97,1},{2,98}... | collective-permute-start | bytes 786440 | tf_op jit(solution)/shard_map/ppermute | solution.py:32
  7.6 1.3 %collective-permute-start.1 = (bf16[320,256]{1,0:T(8,128)(2,1)S(1)}, bf16[320,256]{1,0:T(8,128)(2,1)S(1)}, u32[]{:S(2)}, u32[]{:S(2)}) collective-permute-start(bf16[320,256]{1,0:T(8,128)(2,1)S(1)} %get-tuple-element.60), channel_id=1, source_target_pairs={{0,8},{8,16},{16,24},{24,0},{1,9},{9,17},{17,25},{25,1},{2,10},{10... | collective-permute-start | bytes 491528 | tf_op jit(solution)/shard_map/ppermute | solution.py:44
  8.9 2.6 %collective-permute-start.2 = (bf16[320,256]{1,0:T(8,128)(2,1)S(1)}, bf16[320,256]{1,0:T(8,128)(2,1)S(1)}, u32[]{:S(2)}, u32[]{:S(2)}) collective-permute-start(bf16[320,256]{1,0:T(8,128)(2,1)S(1)} %get-tuple-element.60), channel_id=1, source_target_pairs={{0,16},{8,24},{16,0},{24,8},{1,17},{9,25},{17,1},{25,9},{2,18},{10... | collective-permute-start | bytes 491528 | tf_op jit(solution)/shard_map/ppermute | solution.py:44
  11.5 1.1 collective-permute-start.3
  12.6 1.1 collective-permute-done.1
  13.7 4.6 %collective-permute-done.2 = bf16[320,256]{1,0:T(8,128)(2,1)S(1)} collective-permute-done((bf16[320,256]{1,0:T(8,128)(2,1)S(1)}, bf16[320,256]{1,0:T(8,128)(2,1)S(1)}, u32[]{:S(2)}, u32[]{:S(2)}) %collective-permute-start.2) | collective-permute-done | bytes 163872 | tf_op jit(solution)/shard_map/ppermute | solution.py:44
  18.5 2.7 %collective-permute-start.7 = (bf16[1024,256]{1,0:T(8,128)(2,1)S(1)}, bf16[1024,256]{1,0:T(8,128)(2,1)S(1)}, u32[]{:S(2)}, u32[]{:S(2)}) collective-permute-start(bf16[1024,256]{1,0:T(8,128)(2,1)S(1)} %pad_maximum_fusion.1.refs_1_), channel_id=1, source_target_pairs={{0,96},{64,0},{32,64},{96,32},{1,97},{65,1},{33,65},{97,33},{2,98}... | collective-permute-start | bytes 1572872 | tf_op jit(solution)/shard_map/ppermute | solution.py:40
  21.3 1.5 %collective-permute-start.4 = (bf16[1024,256]{1,0:T(8,128)(2,1)S(1)}, bf16[1024,256]{1,0:T(8,128)(2,1)S(1)}, u32[]{:S(2)}, u32[]{:S(2)}) collective-permute-start(bf16[1024,256]{1,0:T(8,128)(2,1)S(1)} %constant_dynamic-update-slice_fusion.refs_0_), channel_id=1, source_target_pairs={{0,8},{8,16},{16,24},{24,0},{1,9},{9,17},{17,25},{25,1},{2,10},{10... | collective-permute-start | bytes 1572872 | tf_op jit(solution)/shard_map/ppermute | solution.py:44
  22.7 1.3 %collective-permute-start.5 = (bf16[1024,256]{1,0:T(8,128)(2,1)S(1)}, bf16[1024,256]{1,0:T(8,128)(2,1)S(1)}, u32[]{:S(2)}, u32[]{:S(2)}) collective-permute-start(bf16[1024,256]{1,0:T(8,128)(2,1)S(1)} %constant_dynamic-update-slice_fusion.refs_0_), channel_id=1, source_target_pairs={{0,24},{8,0},{16,8},{24,16},{1,25},{9,1},{17,9},{25,17},{2,26},{10... | collective-permute-start | bytes 1572872 | tf_op jit(solution)/shard_map/ppermute | solution.py:44
  24.2 8.5 %attend.1 = bf16[48,16,128]{2,1,0:T(8,128)(2,1)S(1)} custom-call(s32[48]{0:T(128)S(1)} %copy-done.5, bf16[48,16,128]{2,1,0:T(8,128)(2,1)S(1)} %bitcast.33, bf16[48,128,2,256]{3,2,1,0:T(2,128)(2,1)} %kv_ref.1, bf16[48,2,256]{2,1,0:T(2,128)(2,1)S(1)} %copy-done.4), custom_call_target="tpu_custom_call" | custom-call | tf_op jit(solution)/shard_map/attend/pallas_call | solution.py:146
  32.8 0.7 collective-permute-done.4.refs_2_
  34.2 3.2 %collective-permute-start.11 = (bf16[6144,256]{1,0:T(8,128)(2,1)S(1)}, bf16[6144,256]{1,0:T(8,128)(2,1)S(1)}, u32[]{:S(2)}, u32[]{:S(2)}) collective-permute-start(bf16[6144,256]{1,0:T(8,128)(2,1)S(1)} %constant_dynamic-update-slice_fusion.7), channel_id=1, source_target_pairs={{0,4},{4,0},{1,5},{5,1},{2,6},{6,2},{3,7},{7,3},{8,12},{12,8},{9,1... | collective-permute-start | bytes 9437192 | tf_op jit(solution)/shard_map/ppermute | solution.py:60
  37.5 2.0 %collective-permute-start.10 = (bf16[1024,256]{1,0:T(8,128)(2,1)S(1)}, bf16[1024,256]{1,0:T(8,128)(2,1)S(1)}, u32[]{:S(2)}, u32[]{:S(2)}) collective-permute-start(bf16[1024,256]{1,0:T(8,128)(2,1)S(1)} %pad_maximum_fusion.1.refs_1_), channel_id=1, source_target_pairs={{0,32},{64,96},{32,0},{96,64},{1,33},{65,97},{33,1},{97,65},{2,34}... | collective-permute-start | bytes 1572872 | tf_op jit(solution)/shard_map/ppermute | solution.py:40
  39.5 1.1 collective-permute-start.9
  40.6 2.5 %collective-permute-done.13.other_ref = bf16[512,256]{1,0:T(8,128)(2,1)S(1)} collective-permute-done((bf16[512,256]{1,0:T(8,128)(2,1)S(1)}, bf16[512,256]{1,0:T(8,128)(2,1)S(1)}, u32[]{:S(2)}, u32[]{:S(2)}) %collective-permute-start.13) | collective-permute-done | bytes 262176 | tf_op jit(solution)/shard_map/ppermute | solution.py:60
  43.1 1.3 %low_rank.1 = f32[32,128]{1,0:T(8,128)S(1)} custom-call(s32[17]{0:T(128)S(1)} %concatenate.32.info, bf16[512,8192]{1,0:T(8,128)(2,1)S(1)} %bitcast.28, bf16[512,256]{1,0:T(8,128)(2,1)S(1)} %constant_dynamic-update-slice_fusion.2.own_ref, bf16[512,256]{1,0:T(8,128)(2,1)S(1)} %collective-permute-done.13.other_ref), custom_call_target="tpu_custom_call" | custom-call | tf_op jit(solution)/shard_map/low_rank/pallas_call | solution.py:199
  44.4 1.7 %collective-permute-start.14 = (f32[32,128]{1,0:T(8,128)S(1)}, f32[32,128]{1,0:T(8,128)S(1)}, u32[]{:S(2)}, u32[]{:S(2)}) collective-permute-start(f32[32,128]{1,0:T(8,128)S(1)} %low_rank.1), channel_id=1, source_target_pairs={{0,1},{1,0},{2,3},{3,2},{4,5},{5,4},{6,7},{7,6},{8,9},{9,8},{10,11... | collective-permute-start | bytes 49160 | tf_op jit(solution)/shard_map/ppermute | solution.py:56
  46.1 2.0 %collective-permute-start.12 = (bf16[48,2048]{1,0:T(8,128)(2,1)S(1)}, bf16[48,2048]{1,0:T(8,128)(2,1)S(1)}, u32[]{:S(2)}, u32[]{:S(2)}) collective-permute-start(bf16[48,2048]{1,0:T(8,128)(2,1)S(1)} %bitcast.40), channel_id=1, source_target_pairs={{0,32},{32,0},{1,33},{33,1},{2,34},{34,2},{3,35},{35,3},{4,36},{36... | collective-permute-start | bytes 589832 | tf_op jit(solution)/shard_map/ppermute | solution.py:48
  48.1 3.3 %collective-permute-start.15 = (f32[64,128]{1,0:T(8,128)S(1)}, f32[64,128]{1,0:T(8,128)S(1)}, u32[]{:S(2)}, u32[]{:S(2)}) collective-permute-start(f32[64,128]{1,0:T(8,128)S(1)} %pad_maximum_fusion.4), channel_id=1, source_target_pairs={{0,2},{1,3},{2,0},{3,1},{4,6},{5,7},{6,4},{7,5},{8,10},{9,11},{10,... | collective-permute-start | bytes 98312 | tf_op jit(solution)/shard_map/ppermute | solution.py:56
  51.4 2.4 %main_product.2 = (f32[512,256]{1,0:T(8,128)S(1)}, f32[512,256]{1,0:T(8,128)S(1)}) custom-call(s32[17]{0:T(128)S(1)} %concatenate.32.info, bf16[512,8192]{1,0:T(8,128)(2,1)S(1)} %bitcast.29, bf16[1024,256]{1,0:T(8,128)(2,1)S(1)} %constant_dynamic-update-slice_fusion.refs_0_, bf16[1024,256]{1,0:T(8,128)(2,1)S(1)} %pad_maximum_fusion.1.refs_1_, ...), custom_call_target="tpu_custom_call" | custom-call | tf_op jit(solution)/shard_map/main_product/pallas_call | solution.py:242
  53.9 2.3 %main_product.3 = (f32[512,256]{1,0:T(8,128)S(1)}, f32[512,256]{1,0:T(8,128)S(1)}) custom-call(s32[17]{0:T(128)S(1)} %concatenate.32.info, bf16[512,8192]{1,0:T(8,128)(2,1)S(1)} %bitcast.30, bf16[6144,256]{1,0:T(8,128)(2,1)S(1)} %collective-permute-done.11.refs_0_), custom_call_target="tpu_custom_call" | custom-call | tf_op jit(solution)/shard_map/main_product/pallas_call | solution.py:242
  56.3 1.3 %collective-permute-start.16 = (bf16[1024,256]{1,0:T(8,128)(2,1)S(1)}, bf16[1024,256]{1,0:T(8,128)(2,1)S(1)}, u32[]{:S(2)}, u32[]{:S(2)}) collective-permute-start(bf16[1024,256]{1,0:T(8,128)(2,1)S(1)} %collective-permute-done.9.refs_0_), channel_id=1, source_target_pairs={{0,4},{4,0},{1,5},{5,1},{2,6},{6,2},{3,7},{7,3},{8,12},{12,8},{9,1... | collective-permute-start | bytes 1572872 | tf_op jit(solution)/shard_map/ppermute | solution.py:60
  57.7 1.4 %collective-permute-start.20 = (bf16[96,2048]{1,0:T(8,128)(2,1)S(1)}, bf16[96,2048]{1,0:T(8,128)(2,1)S(1)}, u32[]{:S(2)}, u32[]{:S(2)}) collective-permute-start(bf16[96,2048]{1,0:T(8,128)(2,1)S(1)} %constant_dynamic-update-slice_fusion.13), channel_id=1, source_target_pairs={{0,8},{8,16},{16,24},{24,0},{1,9},{9,17},{17,25},{25,1},{2,10},{10... | collective-permute-start | bytes 1179656 | tf_op jit(solution)/shard_map/ppermute | solution.py:44
  59.2 2.5 %collective-permute-start.21 = (bf16[96,2048]{1,0:T(8,128)(2,1)S(1)}, bf16[96,2048]{1,0:T(8,128)(2,1)S(1)}, u32[]{:S(2)}, u32[]{:S(2)}) collective-permute-start(bf16[96,2048]{1,0:T(8,128)(2,1)S(1)} %constant_dynamic-update-slice_fusion.13), channel_id=1, source_target_pairs={{0,16},{8,24},{16,0},{24,8},{1,17},{9,25},{17,1},{25,9},{2,18},{10... | collective-permute-start | bytes 1179656 | tf_op jit(solution)/shard_map/ppermute | solution.py:44
  62.1 3.7 %finish.1 = (bf16[3,128,2,256]{3,2,1,0:T(2,128)(2,1)S(1)}, bf16[3,128,2,256]{3,2,1,0:T(2,128)(2,1)S(1)}) custom-call(s32[17]{0:T(128)S(1)} %concatenate.32.info, bf16[512,8192]{1,0:T(8,128)(2,1)S(1)} %bitcast.31, bf16[1024,256]{1,0:T(8,128)(2,1)S(1)} %collective-permute-done.9.refs_0_, bf16[1024,256]{1,0:T(8,128)(2,1)S(1)} %collective-permute-done.10.refs_1_, ...), custom_call_target="tpu_custom_call" | custom-call | tf_op jit(solution)/shard_map/finish/pallas_call | solution.py:293
  65.8 1.2 collective-permute-start.18
  67.0 1.5 %collective-permute-start.19 = (bf16[3,128,2,256]{3,2,1,0:T(2,128)(2,1)S(1)}, bf16[3,128,2,256]{3,2,1,0:T(2,128)(2,1)S(1)}, u32[]{:S(2)}, u32[]{:S(2)}) collective-permute-start(bf16[3,128,2,256]{3,2,1,0:T(2,128)(2,1)S(1)} %get-tuple-element.85), channel_id=1, source_target_pairs={{0,96},{32,64},{64,32},{96,0},{1,97},{33,65},{65,33},{97,1},{2,98}... | collective-permute-start | bytes 1179656 | tf_op jit(solution)/shard_map/ppermute | solution.py:32
  68.5 1.0 collective-permute-done.20
  69.5 9.4 %collective-permute-done.21 = bf16[96,2048]{1,0:T(8,128)(2,1)S(1)} collective-permute-done((bf16[96,2048]{1,0:T(8,128)(2,1)S(1)}, bf16[96,2048]{1,0:T(8,128)(2,1)S(1)}, u32[]{:S(2)}, u32[]{:S(2)}) %collective-permute-start.21) | collective-permute-done | bytes 393248 | tf_op jit(solution)/shard_map/ppermute | solution.py:44
  79.0 1.3 %collective-permute-start.25 = (bf16[384,2048]{1,0:T(8,128)(2,1)S(1)}, bf16[384,2048]{1,0:T(8,128)(2,1)S(1)}, u32[]{:S(2)}, u32[]{:S(2)}) collective-permute-start(bf16[384,2048]{1,0:T(8,128)(2,1)S(1)} %constant_dynamic-update-slice_fusion.15.refs_0_), channel_id=1, source_target_pairs={{0,4},{4,0},{1,5},{5,1},{2,6},{6,2},{3,7},{7,3},{8,12},{12,8},{9,1... | collective-permute-start | bytes 4718600 | tf_op jit(solution)/shard_map/ppermute | solution.py:60
  80.3 1.1 pad_maximum_fusion.refs_0_
  81.5 1.1 collective-permute-start.23
  82.5 1.7 %collective-permute-start.24 = (bf16[2,3,128,2,256]{4,3,2,1,0:T(2,128)(2,1)S(1)}, bf16[2,3,128,2,256]{4,3,2,1,0:T(2,128)(2,1)S(1)}, u32[]{:S(2)}, u32[]{:S(2)}) collective-permute-start(bf16[2,3,128,2,256]{4,3,2,1,0:T(2,128)(2,1)S(1)} %pad_maximum_fusion.refs_0_), channel_id=1, source_target_pairs={{0,24},{8,0},{16,8},{24,16},{1,25},{9,1},{17,9},{25,17},{2,26},{10... | collective-permute-start | bytes 2359304 | tf_op jit(solution)/shard_map/ppermute | solution.py:44
  84.4 5.2 %project.1 = (bf16[192,512]{1,0:T(8,128)(2,1)S(1)}, bf16[192,512]{1,0:T(8,128)(2,1)S(1)}, bf16[192,512]{1,0:T(8,128)(2,1)S(1)}, bf16[192,512]{1,0:T(8,128)(2,1)S(1)}) custom-call(s32[17]{0:T(128)S(1)} %concatenate.32.info, s32[768,1]{1,0:T(8,128)S(1)} %broadcast_in_dim.20.keep, bf16[128,2048]{1,0:T(8,128)(2,1)S(1)} %bitcast.34, ...), custom_call_target="tpu_custom_call" | custom-call | tf_op jit(solution)/shard_map/project/pallas_call | solution.py:410
  89.6 1.7 %collective-permute-start.26 = (bf16[192,512]{1,0:T(8,128)(2,1)S(1)}, bf16[192,512]{1,0:T(8,128)(2,1)S(1)}, u32[]{:S(2)}, u32[]{:S(2)}) collective-permute-start(bf16[192,512]{1,0:T(8,128)(2,1)S(1)} %get-tuple-element.95), channel_id=1, source_target_pairs={{0,1},{1,2},{2,3},{3,0},{4,5},{5,6},{6,7},{7,4},{8,9},{9,10},{10,1... | collective-permute-start | bytes 589832 | tf_op jit(solution)/shard_map/ppermute | solution.py:52
  91.3 3.3 %collective-permute-start.27 = (bf16[192,512]{1,0:T(8,128)(2,1)S(1)}, bf16[192,512]{1,0:T(8,128)(2,1)S(1)}, u32[]{:S(2)}, u32[]{:S(2)}) collective-permute-start(bf16[192,512]{1,0:T(8,128)(2,1)S(1)} %get-tuple-element.96), channel_id=1, source_target_pairs={{0,2},{1,3},{2,0},{3,1},{4,6},{5,7},{6,4},{7,5},{8,10},{9,11},{10,... | collective-permute-start | bytes 589832 | tf_op jit(solution)/shard_map/ppermute | solution.py:52
  94.6 0.7 collective-permute-start.33
  95.3 6.6 %collective-permute-done.23.refs_1_ = bf16[2,3,128,2,256]{4,3,2,1,0:T(2,128)(2,1)S(1)} collective-permute-done((bf16[2,3,128,2,256]{4,3,2,1,0:T(2,128)(2,1)S(1)}, bf16[2,3,128,2,256]{4,3,2,1,0:T(2,128)(2,1)S(1)}, u32[]{:S(2)}, u32[]{:S(2)}) %collective-permute-start.23) | collective-permute-done | bytes 786464 | tf_op jit(solution)/shard_map/ppermute | solution.py:44
  101.9 1.3 %collective-permute-done.27 = bf16[192,512]{1,0:T(8,128)(2,1)S(1)} collective-permute-done((bf16[192,512]{1,0:T(8,128)(2,1)S(1)}, bf16[192,512]{1,0:T(8,128)(2,1)S(1)}, u32[]{:S(2)}, u32[]{:S(2)}) %collective-permute-start.27) | collective-permute-done | bytes 196640 | tf_op jit(solution)/shard_map/ppermute | solution.py:52
  103.2 1.4 %collective-permute-start.30 = (bf16[2,3,128,2,256]{4,3,2,1,0:T(2,128)(2,1)S(1)}, bf16[2,3,128,2,256]{4,3,2,1,0:T(2,128)(2,1)S(1)}, u32[]{:S(2)}, u32[]{:S(2)}) collective-permute-start(bf16[2,3,128,2,256]{4,3,2,1,0:T(2,128)(2,1)S(1)} %pad_maximum_fusion.refs_0_), channel_id=1, source_target_pairs={{0,4},{4,0},{1,5},{5,1},{2,6},{6,2},{3,7},{7,3},{8,12},{12,8},{9,1... | collective-permute-start | bytes 2359304 | tf_op jit(solution)/shard_map/ppermute | solution.py:60
  105.8 2.7 %collective-permute-start.29 = (bf16[3,128,2,256]{3,2,1,0:T(2,128)(2,1)S(1)}, bf16[3,128,2,256]{3,2,1,0:T(2,128)(2,1)S(1)}, u32[]{:S(2)}, u32[]{:S(2)}) collective-permute-start(bf16[3,128,2,256]{3,2,1,0:T(2,128)(2,1)S(1)} %slice_bitcast_fusion), channel_id=1, source_target_pairs={{0,24},{8,0},{16,8},{24,16},{1,25},{9,1},{17,9},{25,17},{2,26},{10... | collective-permute-start | bytes 1179656 | tf_op jit(solution)/shard_map/ppermute | solution.py:44
  108.5 0.8 add_convert_fusion
  109.3 8.1 %collective-permute-done.28 = bf16[3,128,2,256]{3,2,1,0:T(2,128)(2,1)S(1)} collective-permute-done((bf16[3,128,2,256]{3,2,1,0:T(2,128)(2,1)S(1)}, bf16[3,128,2,256]{3,2,1,0:T(2,128)(2,1)S(1)}, u32[]{:S(2)}, u32[]{:S(2)}) %collective-permute-start.28) | collective-permute-done | bytes 393248 | tf_op jit(solution)/shard_map/ppermute | solution.py:44
  117.5 0.9 collective-permute-start.34
  118.4 2.9 %place.2.refs_4_ = bf16[1,2,2048,2,256]{4,3,2,1,0:T(2,128)(2,1)} custom-call(s32[17]{0:T(128)S(1)} %concatenate.32.info, bf16[2,3,128,2,256]{4,3,2,1,0:T(2,128)(2,1)S(1)} %pad_maximum_fusion.refs_0_, bf16[2,3,128,2,256]{4,3,2,1,0:T(2,128)(2,1)S(1)} %collective-permute-done.23.refs_1_, bf16[2,3,128,2,256]{4,3,2,1,0:T(2,128)(2,1)S(1)} %collective-permute-done.24.refs_2_, ...), custom_call_target="tpu_custom_call" | custom-call | tf_op jit(solution)/shard_map/place/pallas_call | solution.py:368
  121.3 0.9 place.3
  (89 shorter events, 3.4 us)
Async XLA Ops:
  0.6 23.6 %copy-start.5 = (s32[48]{0:T(128)S(1)}, s32[48]{0:T(128)}, u32[]{:S(2)}) copy-start(s32[48]{0:T(128)} %len_ref) | copy-start | bytes 580
  0.6 23.5 %copy-start.6 = (bf16[48,2048]{1,0:T(8,128)(2,1)S(1)}, bf16[48,2048]{1,0:T(8,128)(2,1)}, u32[]{:S(2)}) copy-start(bf16[48,2048]{1,0:T(8,128)(2,1)} %param.20) | copy-start | bytes 589828
  0.7 23.6 %copy-start.4 = (bf16[48,2,256]{2,1,0:T(2,128)(2,1)S(1)}, bf16[48,2,256]{2,1,0:T(2,128)(2,1)}, u32[]{:S(2)}) copy-start(bf16[48,2,256]{2,1,0:T(2,128)(2,1)} %cur_ref.1) | copy-start | bytes 147460
  4.2 14.1 %collective-permute-start = (bf16[512,256]{1,0:T(8,128)(2,1)S(1)}, bf16[512,256]{1,0:T(8,128)(2,1)S(1)}, u32[]{:S(2)}, u32[]{:S(2)}) collective-permute-start(bf16[512,256]{1,0:T(8,128)(2,1)S(1)} %get-tuple-element.58), channel_id=1, source_target_pairs={{0,96},{32,64},{64,32},{96,0},{1,97},{33,65},{65,33},{97,1},{2,98}... | collective-permute-start | bytes 786440 | tf_op jit(solution)/shard_map/ppermute | solution.py:32
  7.6 6.1 %collective-permute-start.1 = (bf16[320,256]{1,0:T(8,128)(2,1)S(1)}, bf16[320,256]{1,0:T(8,128)(2,1)S(1)}, u32[]{:S(2)}, u32[]{:S(2)}) collective-permute-start(bf16[320,256]{1,0:T(8,128)(2,1)S(1)} %get-tuple-element.60), channel_id=1, source_target_pairs={{0,8},{8,16},{16,24},{24,0},{1,9},{9,17},{17,25},{25,1},{2,10},{10... | collective-permute-start | bytes 491528 | tf_op jit(solution)/shard_map/ppermute | solution.py:44
  8.9 9.4 %collective-permute-start.2 = (bf16[320,256]{1,0:T(8,128)(2,1)S(1)}, bf16[320,256]{1,0:T(8,128)(2,1)S(1)}, u32[]{:S(2)}, u32[]{:S(2)}) collective-permute-start(bf16[320,256]{1,0:T(8,128)(2,1)S(1)} %get-tuple-element.60), channel_id=1, source_target_pairs={{0,16},{8,24},{16,0},{24,8},{1,17},{9,25},{17,1},{25,9},{2,18},{10... | collective-permute-start | bytes 491528 | tf_op jit(solution)/shard_map/ppermute | solution.py:44
  11.5 6.8 %collective-permute-start.3 = (bf16[320,256]{1,0:T(8,128)(2,1)S(1)}, bf16[320,256]{1,0:T(8,128)(2,1)S(1)}, u32[]{:S(2)}, u32[]{:S(2)}) collective-permute-start(bf16[320,256]{1,0:T(8,128)(2,1)S(1)} %get-tuple-element.60), channel_id=1, source_target_pairs={{0,24},{8,0},{16,8},{24,16},{1,25},{9,1},{17,9},{25,17},{2,26},{10... | collective-permute-start | bytes 491528 | tf_op jit(solution)/shard_map/ppermute | solution.py:44
  18.5 14.3 %collective-permute-start.6 = (bf16[1024,256]{1,0:T(8,128)(2,1)S(1)}, bf16[1024,256]{1,0:T(8,128)(2,1)S(1)}, u32[]{:S(2)}, u32[]{:S(2)}) collective-permute-start(bf16[1024,256]{1,0:T(8,128)(2,1)S(1)} %pad_maximum_fusion.1.refs_1_), channel_id=1, source_target_pairs={{0,64},{64,32},{32,96},{96,0},{1,65},{65,33},{33,97},{97,1},{2,66}... | collective-permute-start | bytes 1572872 | tf_op jit(solution)/shard_map/ppermute | solution.py:40
  18.5 14.3 %collective-permute-start.7 = (bf16[1024,256]{1,0:T(8,128)(2,1)S(1)}, bf16[1024,256]{1,0:T(8,128)(2,1)S(1)}, u32[]{:S(2)}, u32[]{:S(2)}) collective-permute-start(bf16[1024,256]{1,0:T(8,128)(2,1)S(1)} %pad_maximum_fusion.1.refs_1_), channel_id=1, source_target_pairs={{0,96},{64,0},{32,64},{96,32},{1,97},{65,1},{33,65},{97,33},{2,98}... | collective-permute-start | bytes 1572872 | tf_op jit(solution)/shard_map/ppermute | solution.py:40
  21.2 21.8 %slice-start = ((s8[8388608]{0:T(1024)(128)(4,1)}), s8[4194304]{0:T(1024)(128)(4,1)S(1)}, s32[]{:S(2)}) async-start(s8[8388608]{0:T(1024)(128)(4,1)} %bitcast.26), calls=%async_computation | async-start | bytes 8388608
  21.3 12.3 %collective-permute-start.4 = (bf16[1024,256]{1,0:T(8,128)(2,1)S(1)}, bf16[1024,256]{1,0:T(8,128)(2,1)S(1)}, u32[]{:S(2)}, u32[]{:S(2)}) collective-permute-start(bf16[1024,256]{1,0:T(8,128)(2,1)S(1)} %constant_dynamic-update-slice_fusion.refs_0_), channel_id=1, source_target_pairs={{0,8},{8,16},{16,24},{24,0},{1,9},{9,17},{17,25},{25,1},{2,10},{10... | collective-permute-start | bytes 1572872 | tf_op jit(solution)/shard_map/ppermute | solution.py:44
  22.7 11.2 %collective-permute-start.5 = (bf16[1024,256]{1,0:T(8,128)(2,1)S(1)}, bf16[1024,256]{1,0:T(8,128)(2,1)S(1)}, u32[]{:S(2)}, u32[]{:S(2)}) collective-permute-start(bf16[1024,256]{1,0:T(8,128)(2,1)S(1)} %constant_dynamic-update-slice_fusion.refs_0_), channel_id=1, source_target_pairs={{0,24},{8,0},{16,8},{24,16},{1,25},{9,1},{17,9},{25,17},{2,26},{10... | collective-permute-start | bytes 1572872 | tf_op jit(solution)/shard_map/ppermute | solution.py:44
  24.1 8.7 %collective-permute-start.8 = (bf16[256,256]{1,0:T(8,128)(2,1)S(1)}, bf16[256,256]{1,0:T(8,128)(2,1)S(1)}, u32[]{:S(2)}, u32[]{:S(2)}) collective-permute-start(bf16[256,256]{1,0:T(8,128)(2,1)S(1)} %pad_maximum_fusion.2), channel_id=1, source_target_pairs={{0,32},{32,0},{1,33},{33,1},{2,34},{34,2},{3,35},{35,3},{4,36},{36... | collective-permute-start | bytes 393224 | tf_op jit(solution)/shard_map/ppermute | solution.py:48
  24.2 18.8 %slice-start.1 = ((s8[8388608]{0:T(1024)(128)(4,1)}), s8[4194304]{0:T(1024)(128)(4,1)S(1)}, s32[]{:S(2)}) async-start(s8[8388608]{0:T(1024)(128)(4,1)} %bitcast.26), calls=%async_computation.1 | async-start | bytes 8388608
  34.2 19.6 %collective-permute-start.11 = (bf16[6144,256]{1,0:T(8,128)(2,1)S(1)}, bf16[6144,256]{1,0:T(8,128)(2,1)S(1)}, u32[]{:S(2)}, u32[]{:S(2)}) collective-permute-start(bf16[6144,256]{1,0:T(8,128)(2,1)S(1)} %constant_dynamic-update-slice_fusion.7), channel_id=1, source_target_pairs={{0,4},{4,0},{1,5},{5,1},{2,6},{6,2},{3,7},{7,3},{8,12},{12,8},{9,1... | collective-permute-start | bytes 9437192 | tf_op jit(solution)/shard_map/ppermute | solution.py:60
  37.4 5.7 %collective-permute-start.13 = (bf16[512,256]{1,0:T(8,128)(2,1)S(1)}, bf16[512,256]{1,0:T(8,128)(2,1)S(1)}, u32[]{:S(2)}, u32[]{:S(2)}) collective-permute-start(bf16[512,256]{1,0:T(8,128)(2,1)S(1)} %constant_dynamic-update-slice_fusion.2.own_ref), channel_id=1, source_target_pairs={{0,4},{4,0},{1,5},{5,1},{2,6},{6,2},{3,7},{7,3},{8,12},{12,8},{9,1... | collective-permute-start | bytes 786440 | tf_op jit(solution)/shard_map/ppermute | solution.py:60
  37.5 18.8 %collective-permute-start.10 = (bf16[1024,256]{1,0:T(8,128)(2,1)S(1)}, bf16[1024,256]{1,0:T(8,128)(2,1)S(1)}, u32[]{:S(2)}, u32[]{:S(2)}) collective-permute-start(bf16[1024,256]{1,0:T(8,128)(2,1)S(1)} %pad_maximum_fusion.1.refs_1_), channel_id=1, source_target_pairs={{0,32},{64,96},{32,0},{96,64},{1,33},{65,97},{33,1},{97,65},{2,34}... | collective-permute-start | bytes 1572872 | tf_op jit(solution)/shard_map/ppermute | solution.py:40
  39.5 16.8 %collective-permute-start.9 = (bf16[1024,256]{1,0:T(8,128)(2,1)S(1)}, bf16[1024,256]{1,0:T(8,128)(2,1)S(1)}, u32[]{:S(2)}, u32[]{:S(2)}) collective-permute-start(bf16[1024,256]{1,0:T(8,128)(2,1)S(1)} %constant_dynamic-update-slice_fusion.refs_0_), channel_id=1, source_target_pairs={{0,16},{8,24},{16,0},{24,8},{1,17},{9,25},{17,1},{25,9},{2,18},{10... | collective-permute-start | bytes 1572872 | tf_op jit(solution)/shard_map/ppermute | solution.py:44
  44.4 3.7 %collective-permute-start.14 = (f32[32,128]{1,0:T(8,128)S(1)}, f32[32,128]{1,0:T(8,128)S(1)}, u32[]{:S(2)}, u32[]{:S(2)}) collective-permute-start(f32[32,128]{1,0:T(8,128)S(1)} %low_rank.1), channel_id=1, source_target_pairs={{0,1},{1,0},{2,3},{3,2},{4,5},{5,4},{6,7},{7,6},{8,9},{9,8},{10,11... | collective-permute-start | bytes 49160 | tf_op jit(solution)/shard_map/ppermute | solution.py:56
  46.1 10.2 %collective-permute-start.12 = (bf16[48,2048]{1,0:T(8,128)(2,1)S(1)}, bf16[48,2048]{1,0:T(8,128)(2,1)S(1)}, u32[]{:S(2)}, u32[]{:S(2)}) collective-permute-start(bf16[48,2048]{1,0:T(8,128)(2,1)S(1)} %bitcast.40), channel_id=1, source_target_pairs={{0,32},{32,0},{1,33},{33,1},{2,34},{34,2},{3,35},{35,3},{4,36},{36... | collective-permute-start | bytes 589832 | tf_op jit(solution)/shard_map/ppermute | solution.py:48
  48.1 5.7 %collective-permute-start.15 = (f32[64,128]{1,0:T(8,128)S(1)}, f32[64,128]{1,0:T(8,128)S(1)}, u32[]{:S(2)}, u32[]{:S(2)}) collective-permute-start(f32[64,128]{1,0:T(8,128)S(1)} %pad_maximum_fusion.4), channel_id=1, source_target_pairs={{0,2},{1,3},{2,0},{3,1},{4,6},{5,7},{6,4},{7,5},{8,10},{9,11},{10,... | collective-permute-start | bytes 98312 | tf_op jit(solution)/shard_map/ppermute | solution.py:56
  53.9 8.2 %copy-start.2 = (bf16[8,2,16,256]{3,2,1,0:T(8,128)(2,1)S(1)}, bf16[8,2,16,256]{3,2,1,0:T(8,128)(2,1)}, u32[]{:S(2)}) copy-start(bf16[8,2,16,256]{3,2,1,0:T(8,128)(2,1)} %refs_9_.1) | copy-start | bytes 393220
  56.3 5.8 %collective-permute-start.16 = (bf16[1024,256]{1,0:T(8,128)(2,1)S(1)}, bf16[1024,256]{1,0:T(8,128)(2,1)S(1)}, u32[]{:S(2)}, u32[]{:S(2)}) collective-permute-start(bf16[1024,256]{1,0:T(8,128)(2,1)S(1)} %collective-permute-done.9.refs_0_), channel_id=1, source_target_pairs={{0,4},{4,0},{1,5},{5,1},{2,6},{6,2},{3,7},{7,3},{8,12},{12,8},{9,1... | collective-permute-start | bytes 1572872 | tf_op jit(solution)/shard_map/ppermute | solution.py:60
  57.6 4.5 %collective-permute-start.17 = (bf16[1024,256]{1,0:T(8,128)(2,1)S(1)}, bf16[1024,256]{1,0:T(8,128)(2,1)S(1)}, u32[]{:S(2)}, u32[]{:S(2)}) collective-permute-start(bf16[1024,256]{1,0:T(8,128)(2,1)S(1)} %collective-permute-done.10.refs_1_), channel_id=1, source_target_pairs={{0,4},{4,0},{1,5},{5,1},{2,6},{6,2},{3,7},{7,3},{8,12},{12,8},{9,1... | collective-permute-start | bytes 1572872 | tf_op jit(solution)/shard_map/ppermute | solution.py:60
  57.7 11.7 %collective-permute-start.20 = (bf16[96,2048]{1,0:T(8,128)(2,1)S(1)}, bf16[96,2048]{1,0:T(8,128)(2,1)S(1)}, u32[]{:S(2)}, u32[]{:S(2)}) collective-permute-start(bf16[96,2048]{1,0:T(8,128)(2,1)S(1)} %constant_dynamic-update-slice_fusion.13), channel_id=1, source_target_pairs={{0,8},{8,16},{16,24},{24,0},{1,9},{9,17},{17,25},{25,1},{2,10},{10... | collective-permute-start | bytes 1179656 | tf_op jit(solution)/shard_map/ppermute | solution.py:44
  59.2 19.7 %collective-permute-start.21 = (bf16[96,2048]{1,0:T(8,128)(2,1)S(1)}, bf16[96,2048]{1,0:T(8,128)(2,1)S(1)}, u32[]{:S(2)}, u32[]{:S(2)}) collective-permute-start(bf16[96,2048]{1,0:T(8,128)(2,1)S(1)} %constant_dynamic-update-slice_fusion.13), channel_id=1, source_target_pairs={{0,16},{8,24},{16,0},{24,8},{1,17},{9,25},{17,1},{25,9},{2,18},{10... | collective-permute-start | bytes 1179656 | tf_op jit(solution)/shard_map/ppermute | solution.py:44
  61.6 17.2 %collective-permute-start.22 = (bf16[96,2048]{1,0:T(8,128)(2,1)S(1)}, bf16[96,2048]{1,0:T(8,128)(2,1)S(1)}, u32[]{:S(2)}, u32[]{:S(2)}) collective-permute-start(bf16[96,2048]{1,0:T(8,128)(2,1)S(1)} %constant_dynamic-update-slice_fusion.13), channel_id=1, source_target_pairs={{0,24},{8,0},{16,8},{24,16},{1,25},{9,1},{17,9},{25,17},{2,26},{10... | collective-permute-start | bytes 1179656 | tf_op jit(solution)/shard_map/ppermute | solution.py:44
  65.8 18.4 %copy-start.7 = (s32[768]{0:T(1024)S(1)}, s32[768]{0:T(1024)}, u32[]{:S(2)}) copy-start(s32[768]{0:T(1024)} %param.24) | copy-start | bytes 9220
  65.8 18.6 %copy-start = (bf16[2048,512]{1,0:T(8,128)(2,1)S(1)}, bf16[2048,512]{1,0:T(8,128)(2,1)}, u32[]{:S(2)}) copy-start(bf16[2048,512]{1,0:T(8,128)(2,1)} %w_ref.1) | copy-start | bytes 6291460
  65.8 18.6 %copy-start.1 = (bf16[2048,8,16]{0,2,1:T(8,128)(2,1)S(1)}, bf16[2048,8,16]{0,2,1:T(8,128)(2,1)}, u32[]{:S(2)}) copy-start(bf16[2048,8,16]{0,2,1:T(8,128)(2,1)} %param.26) | copy-start | bytes 1572868
  65.8 18.6 %copy-start.3 = (bf16[8,16,512]{2,1,0:T(8,128)(2,1)S(1)}, bf16[8,16,512]{2,1,0:T(8,128)(2,1)}, u32[]{:S(2)}) copy-start(bf16[8,16,512]{2,1,0:T(8,128)(2,1)} %param.27) | copy-start | bytes 393220
  65.8 13.0 %collective-permute-start.18 = (bf16[3,128,2,256]{3,2,1,0:T(2,128)(2,1)S(1)}, bf16[3,128,2,256]{3,2,1,0:T(2,128)(2,1)S(1)}, u32[]{:S(2)}, u32[]{:S(2)}) collective-permute-start(bf16[3,128,2,256]{3,2,1,0:T(2,128)(2,1)S(1)} %get-tuple-element.84), channel_id=1, source_target_pairs={{0,64},{64,0},{1,65},{65,1},{2,66},{66,2},{3,67},{67,3},{4,68},{68... | collective-permute-start | bytes 1179656 | tf_op jit(solution)/shard_map/ppermute | solution.py:492
  67.0 11.9 %collective-permute-start.19 = (bf16[3,128,2,256]{3,2,1,0:T(2,128)(2,1)S(1)}, bf16[3,128,2,256]{3,2,1,0:T(2,128)(2,1)S(1)}, u32[]{:S(2)}, u32[]{:S(2)}) collective-permute-start(bf16[3,128,2,256]{3,2,1,0:T(2,128)(2,1)S(1)} %get-tuple-element.85), channel_id=1, source_target_pairs={{0,96},{32,64},{64,32},{96,0},{1,97},{33,65},{65,33},{97,1},{2,98}... | collective-permute-start | bytes 1179656 | tf_op jit(solution)/shard_map/ppermute | solution.py:32
  79.0 5.4 %collective-permute-start.25 = (bf16[384,2048]{1,0:T(8,128)(2,1)S(1)}, bf16[384,2048]{1,0:T(8,128)(2,1)S(1)}, u32[]{:S(2)}, u32[]{:S(2)}) collective-permute-start(bf16[384,2048]{1,0:T(8,128)(2,1)S(1)} %constant_dynamic-update-slice_fusion.15.refs_0_), channel_id=1, source_target_pairs={{0,4},{4,0},{1,5},{5,1},{2,6},{6,2},{3,7},{7,3},{8,12},{12,8},{9,1... | collective-permute-start | bytes 4718600 | tf_op jit(solution)/shard_map/ppermute | solution.py:60
  81.5 20.4 %collective-permute-start.23 = (bf16[2,3,128,2,256]{4,3,2,1,0:T(2,128)(2,1)S(1)}, bf16[2,3,128,2,256]{4,3,2,1,0:T(2,128)(2,1)S(1)}, u32[]{:S(2)}, u32[]{:S(2)}) collective-permute-start(bf16[2,3,128,2,256]{4,3,2,1,0:T(2,128)(2,1)S(1)} %pad_maximum_fusion.refs_0_), channel_id=1, source_target_pairs={{0,8},{8,16},{16,24},{24,0},{1,9},{9,17},{17,25},{25,1},{2,10},{10... | collective-permute-start | bytes 2359304 | tf_op jit(solution)/shard_map/ppermute | solution.py:44
  82.5 19.4 %collective-permute-start.24 = (bf16[2,3,128,2,256]{4,3,2,1,0:T(2,128)(2,1)S(1)}, bf16[2,3,128,2,256]{4,3,2,1,0:T(2,128)(2,1)S(1)}, u32[]{:S(2)}, u32[]{:S(2)}) collective-permute-start(bf16[2,3,128,2,256]{4,3,2,1,0:T(2,128)(2,1)S(1)} %pad_maximum_fusion.refs_0_), channel_id=1, source_target_pairs={{0,24},{8,0},{16,8},{24,16},{1,25},{9,1},{17,9},{25,17},{2,26},{10... | collective-permute-start | bytes 2359304 | tf_op jit(solution)/shard_map/ppermute | solution.py:44
  89.6 12.3 %collective-permute-start.26 = (bf16[192,512]{1,0:T(8,128)(2,1)S(1)}, bf16[192,512]{1,0:T(8,128)(2,1)S(1)}, u32[]{:S(2)}, u32[]{:S(2)}) collective-permute-start(bf16[192,512]{1,0:T(8,128)(2,1)S(1)} %get-tuple-element.95), channel_id=1, source_target_pairs={{0,1},{1,2},{2,3},{3,0},{4,5},{5,6},{6,7},{7,4},{8,9},{9,10},{10,1... | collective-permute-start | bytes 589832 | tf_op jit(solution)/shard_map/ppermute | solution.py:52
  91.3 11.9 %collective-permute-start.27 = (bf16[192,512]{1,0:T(8,128)(2,1)S(1)}, bf16[192,512]{1,0:T(8,128)(2,1)S(1)}, u32[]{:S(2)}, u32[]{:S(2)}) collective-permute-start(bf16[192,512]{1,0:T(8,128)(2,1)S(1)} %get-tuple-element.96), channel_id=1, source_target_pairs={{0,2},{1,3},{2,0},{3,1},{4,6},{5,7},{6,4},{7,5},{8,10},{9,11},{10,... | collective-permute-start | bytes 589832 | tf_op jit(solution)/shard_map/ppermute | solution.py:52
  94.6 11.2 %collective-permute-start.33 = (bf16[192,512]{1,0:T(8,128)(2,1)S(1)}, bf16[192,512]{1,0:T(8,128)(2,1)S(1)}, u32[]{:S(2)}, u32[]{:S(2)}) collective-permute-start(bf16[192,512]{1,0:T(8,128)(2,1)S(1)} %get-tuple-element.103), channel_id=1, source_target_pairs={{0,3},{1,0},{2,1},{3,2},{4,7},{5,4},{6,5},{7,6},{8,11},{9,8},{10,9... | collective-permute-start | bytes 589832 | tf_op jit(solution)/shard_map/ppermute | solution.py:52
  103.2 14.3 %collective-permute-start.30 = (bf16[2,3,128,2,256]{4,3,2,1,0:T(2,128)(2,1)S(1)}, bf16[2,3,128,2,256]{4,3,2,1,0:T(2,128)(2,1)S(1)}, u32[]{:S(2)}, u32[]{:S(2)}) collective-permute-start(bf16[2,3,128,2,256]{4,3,2,1,0:T(2,128)(2,1)S(1)} %pad_maximum_fusion.refs_0_), channel_id=1, source_target_pairs={{0,4},{4,0},{1,5},{5,1},{2,6},{6,2},{3,7},{7,3},{8,12},{12,8},{9,1... | collective-permute-start | bytes 2359304 | tf_op jit(solution)/shard_map/ppermute | solution.py:60
  104.7 12.8 %collective-permute-start.31 = (bf16[2,3,128,2,256]{4,3,2,1,0:T(2,128)(2,1)S(1)}, bf16[2,3,128,2,256]{4,3,2,1,0:T(2,128)(2,1)S(1)}, u32[]{:S(2)}, u32[]{:S(2)}) collective-permute-start(bf16[2,3,128,2,256]{4,3,2,1,0:T(2,128)(2,1)S(1)} %collective-permute-done.23.refs_1_), channel_id=1, source_target_pairs={{0,4},{4,0},{1,5},{5,1},{2,6},{6,2},{3,7},{7,3},{8,12},{12,8},{9,1... | collective-permute-start | bytes 2359304 | tf_op jit(solution)/shard_map/ppermute | solution.py:60
  104.7 12.8 %collective-permute-start.32 = (bf16[2,3,128,2,256]{4,3,2,1,0:T(2,128)(2,1)S(1)}, bf16[2,3,128,2,256]{4,3,2,1,0:T(2,128)(2,1)S(1)}, u32[]{:S(2)}, u32[]{:S(2)}) collective-permute-start(bf16[2,3,128,2,256]{4,3,2,1,0:T(2,128)(2,1)S(1)} %collective-permute-done.24.refs_2_), channel_id=1, source_target_pairs={{0,4},{4,0},{1,5},{5,1},{2,6},{6,2},{3,7},{7,3},{8,12},{12,8},{9,1... | collective-permute-start | bytes 2359304 | tf_op jit(solution)/shard_map/ppermute | solution.py:60
  105.4 12.0 %collective-permute-start.28 = (bf16[3,128,2,256]{3,2,1,0:T(2,128)(2,1)S(1)}, bf16[3,128,2,256]{3,2,1,0:T(2,128)(2,1)S(1)}, u32[]{:S(2)}, u32[]{:S(2)}) collective-permute-start(bf16[3,128,2,256]{3,2,1,0:T(2,128)(2,1)S(1)} %slice_bitcast_fusion.1), channel_id=1, source_target_pairs={{0,8},{8,16},{16,24},{24,0},{1,9},{9,17},{17,25},{25,1},{2,10},{10... | collective-permute-start | bytes 1179656 | tf_op jit(solution)/shard_map/ppermute | solution.py:44
  105.8 11.7 %collective-permute-start.29 = (bf16[3,128,2,256]{3,2,1,0:T(2,128)(2,1)S(1)}, bf16[3,128,2,256]{3,2,1,0:T(2,128)(2,1)S(1)}, u32[]{:S(2)}, u32[]{:S(2)}) collective-permute-start(bf16[3,128,2,256]{3,2,1,0:T(2,128)(2,1)S(1)} %slice_bitcast_fusion), channel_id=1, source_target_pairs={{0,24},{8,0},{16,8},{24,16},{1,25},{9,1},{17,9},{25,17},{2,26},{10... | collective-permute-start | bytes 1179656 | tf_op jit(solution)/shard_map/ppermute | solution.py:44
  117.5 3.8 %collective-permute-start.34 = (bf16[3,128,2,256]{3,2,1,0:T(2,128)(2,1)S(1)}, bf16[3,128,2,256]{3,2,1,0:T(2,128)(2,1)S(1)}, u32[]{:S(2)}, u32[]{:S(2)}) collective-permute-start(bf16[3,128,2,256]{3,2,1,0:T(2,128)(2,1)S(1)} %collective-permute-done.28), channel_id=1, source_target_pairs={{0,4},{4,0},{1,5},{5,1},{2,6},{6,2},{3,7},{7,3},{8,12},{12,8},{9,1... | collective-permute-start | bytes 1179656 | tf_op jit(solution)/shard_map/ppermute | solution.py:60
  118.4 3.0 %collective-permute-start.35 = (bf16[3,128,2,256]{3,2,1,0:T(2,128)(2,1)S(1)}, bf16[3,128,2,256]{3,2,1,0:T(2,128)(2,1)S(1)}, u32[]{:S(2)}, u32[]{:S(2)}) collective-permute-start(bf16[3,128,2,256]{3,2,1,0:T(2,128)(2,1)S(1)} %collective-permute-done.29), channel_id=1, source_target_pairs={{0,4},{4,0},{1,5},{5,1},{2,6},{6,2},{3,7},{7,3},{8,12},{12,8},{9,1... | collective-permute-start | bytes 1179656 | tf_op jit(solution)/shard_map/ppermute | solution.py:60

commit v11 on v10

--- a/solution.py
+++ b/solution.py
@@ -501,12 +501,16 @@
     up = output_up_weight.reshape(ranks, -1)
     keep = row_adapter_index[:, None]
     shares = list(project(info, keep, down, up, output_weight, [mine, partner]))
+    theirs0 = core_swap(both0)
+    shares, theirs0 = barrier((shares, theirs0))
     shares[1:] = [z_shift(v, k) for v, k in zip(shares[1:], (1, 2, -1))]
-    both0, both1, both3, shares[:3] = barrier((both0, both1, both3, shares[:3]))
+    both0, both1, both3, shares[1], shares[3] = barrier(
+        (both0, both1, both3, shares[1], shares[3])
+    )
     decoded = sum(v.astype(jnp.float32) for v in shares).astype(jnp.bfloat16)
     b2, a2 = y_shift(both1[0], 1), y_shift(both3[1], -1)
     middle = [both0, both1, both3]
-    theirs = [core_swap(v) for v in middle]
+    theirs = [theirs0, core_swap(both1), core_swap(both3)]
     b2, a2, theirs, decoded = barrier((b2, a2, theirs, decoded))
     theirs2 = [core_swap(b2), core_swap(a2)]
     kinds = ((0, 0), (1, 0), (0, 1), (1, 1), (0, 3), (1, 3))

time: 123 us -> 121 us (0.984)
  waiting for transfers between devices: 35.8 us -> 34.5 us
    ppermute x3, waiting for transfers between devices: 1.31 us -> 0.01 us  [z_shift(): return lax.ppermute(value, 'head', [(i, (i + k) % 4) for i in range(4)])]
  transfers between devices with their start and end apart: 36 -> 36, of which waited for: 11 -> 10; matrix products, arithmetic and copies ran while one was open for 2% -> 2% of each run, Pallas kernels for 21% -> 22%
where the time goes in v11:
time: 121 us; the launch traced here: 120 us
  starting transfers between devices  50.8 us (42%)
  waiting for transfers between devices  34.5 us (29%)
  Pallas kernels  29.9 us (25%)
  local copies, waits for them, and re-layouts  2.12 us (2%)
  other arithmetic  1.95 us (2%)
  between operations  1.33 us (1%)
    ppermute x13, waiting for transfers between devices, y_shift(): return lax.ppermute(value, 'y', [(i, (i + k) % 4) for i in range(4)])  31.8 us
    ppermute x13, starting transfers between devices, y_shift(): return lax.ppermute(value, 'y', [(i, (i + k) % 4) for i in range(4)])  18.6 us
    ppermute x10, starting transfers between devices, core_swap(): return lax.ppermute(value, 'core', [(0, 1), (1, 0)])  9.04 us
    pallas_call x1, Pallas kernels, attend(): pl.pallas_call(functools.partial(attend_kernel, first * ROWS_STEP), grid_...  8.47 us
    pallas_call x1, Pallas kernels, project(): pl.pallas_call(project_kernel, in_specs=[SMEM] + [VMEM] * 6, out_specs=[V...  5.15 us
    ppermute x3, starting transfers between devices, z_shift(): return lax.ppermute(value, 'head', [(i, (i + k) % 4) for i in range(4)])  5.14 us
    ppermute x2, starting transfers between devices, z_flip(): return lax.ppermute(value, 'head', [(i, i ^ mask) for i in range(4)])  5.02 us
    ppermute x2, starting transfers between devices, x_mirror(): return lax.ppermute(value, ('pool', 'xh'), [(i, 3 - i) for i in range(4)])  4.92 us
  transfers between devices with their start and end apart: 36, of which 10 were waited for; matrix products, arithmetic and copies ran while one was open for 2% of the time, Pallas kernels for 22%

profile of v11, /device:TPU:1, one launch (start us, length us, event | category | flops | bytes accessed | tf_op | source)
XLA Modules:
  0.0 120.5 jit_solution(3754491899140150288)
XLA Ops:
  0.7 0.8 concatenate.32.info
  1.5 2.8 %pack.1 = (bf16[512,256]{1,0:T(8,128)(2,1)S(1)}, bf16[320,256]{1,0:T(8,128)(2,1)S(1)}) custom-call(s32[17]{0:T(128)S(1)} %concatenate.32.info, bf16[512,2,256]{2,1,0:T(2,128)(2,1)} %w_hbm.1, bf16[512,256]{1,0:T(8,128)(2,1)} %d_hbm.1), custom_call_target="tpu_custom_call" | custom-call | tf_op jit(solution)/shard_map/pack/pallas_call | solution.py:86
  4.2 3.4 %collective-permute-start = (bf16[512,256]{1,0:T(8,128)(2,1)S(1)}, bf16[512,256]{1,0:T(8,128)(2,1)S(1)}, u32[]{:S(2)}, u32[]{:S(2)}) collective-permute-start(bf16[512,256]{1,0:T(8,128)(2,1)S(1)} %get-tuple-element.62), channel_id=1, source_target_pairs={{0,96},{32,64},{64,32},{96,0},{1,97},{33,65},{65,33},{97,1},{2,98}... | collective-permute-start | bytes 786440 | tf_op jit(solution)/shard_map/ppermute | solution.py:32
  7.6 1.3 %collective-permute-start.1 = (bf16[320,256]{1,0:T(8,128)(2,1)S(1)}, bf16[320,256]{1,0:T(8,128)(2,1)S(1)}, u32[]{:S(2)}, u32[]{:S(2)}) collective-permute-start(bf16[320,256]{1,0:T(8,128)(2,1)S(1)} %get-tuple-element.64), channel_id=1, source_target_pairs={{0,8},{8,16},{16,24},{24,0},{1,9},{9,17},{17,25},{25,1},{2,10},{10... | collective-permute-start | bytes 491528 | tf_op jit(solution)/shard_map/ppermute | solution.py:44
  8.9 2.6 %collective-permute-start.2 = (bf16[320,256]{1,0:T(8,128)(2,1)S(1)}, bf16[320,256]{1,0:T(8,128)(2,1)S(1)}, u32[]{:S(2)}, u32[]{:S(2)}) collective-permute-start(bf16[320,256]{1,0:T(8,128)(2,1)S(1)} %get-tuple-element.64), channel_id=1, source_target_pairs={{0,16},{8,24},{16,0},{24,8},{1,17},{9,25},{17,1},{25,9},{2,18},{10... | collective-permute-start | bytes 491528 | tf_op jit(solution)/shard_map/ppermute | solution.py:44
  11.5 1.1 collective-permute-start.3
  12.6 1.1 collective-permute-done.1
  13.7 4.6 %collective-permute-done.2 = bf16[320,256]{1,0:T(8,128)(2,1)S(1)} collective-permute-done((bf16[320,256]{1,0:T(8,128)(2,1)S(1)}, bf16[320,256]{1,0:T(8,128)(2,1)S(1)}, u32[]{:S(2)}, u32[]{:S(2)}) %collective-permute-start.2) | collective-permute-done | bytes 163872 | tf_op jit(solution)/shard_map/ppermute | solution.py:44
  18.5 2.7 %collective-permute-start.7 = (bf16[1024,256]{1,0:T(8,128)(2,1)S(1)}, bf16[1024,256]{1,0:T(8,128)(2,1)S(1)}, u32[]{:S(2)}, u32[]{:S(2)}) collective-permute-start(bf16[1024,256]{1,0:T(8,128)(2,1)S(1)} %pad_maximum_fusion.1.refs_1_), channel_id=1, source_target_pairs={{0,96},{64,0},{32,64},{96,32},{1,97},{65,1},{33,65},{97,33},{2,98}... | collective-permute-start | bytes 1572872 | tf_op jit(solution)/shard_map/ppermute | solution.py:40
  21.3 1.5 %collective-permute-start.4 = (bf16[1024,256]{1,0:T(8,128)(2,1)S(1)}, bf16[1024,256]{1,0:T(8,128)(2,1)S(1)}, u32[]{:S(2)}, u32[]{:S(2)}) collective-permute-start(bf16[1024,256]{1,0:T(8,128)(2,1)S(1)} %constant_dynamic-update-slice_fusion.refs_0_), channel_id=1, source_target_pairs={{0,8},{8,16},{16,24},{24,0},{1,9},{9,17},{17,25},{25,1},{2,10},{10... | collective-permute-start | bytes 1572872 | tf_op jit(solution)/shard_map/ppermute | solution.py:44
  22.7 1.3 %collective-permute-start.5 = (bf16[1024,256]{1,0:T(8,128)(2,1)S(1)}, bf16[1024,256]{1,0:T(8,128)(2,1)S(1)}, u32[]{:S(2)}, u32[]{:S(2)}) collective-permute-start(bf16[1024,256]{1,0:T(8,128)(2,1)S(1)} %constant_dynamic-update-slice_fusion.refs_0_), channel_id=1, source_target_pairs={{0,24},{8,0},{16,8},{24,16},{1,25},{9,1},{17,9},{25,17},{2,26},{10... | collective-permute-start | bytes 1572872 | tf_op jit(solution)/shard_map/ppermute | solution.py:44
  24.2 8.5 %attend.1 = bf16[48,16,128]{2,1,0:T(8,128)(2,1)S(1)} custom-call(s32[48]{0:T(128)S(1)} %copy-done.5, bf16[48,16,128]{2,1,0:T(8,128)(2,1)S(1)} %bitcast.33, bf16[48,128,2,256]{3,2,1,0:T(2,128)(2,1)} %kv_ref.1, bf16[48,2,256]{2,1,0:T(2,128)(2,1)S(1)} %copy-done.4), custom_call_target="tpu_custom_call" | custom-call | tf_op jit(solution)/shard_map/attend/pallas_call | solution.py:146
  32.8 0.7 collective-permute-done.4.refs_2_
  34.2 3.2 %collective-permute-start.11 = (bf16[6144,256]{1,0:T(8,128)(2,1)S(1)}, bf16[6144,256]{1,0:T(8,128)(2,1)S(1)}, u32[]{:S(2)}, u32[]{:S(2)}) collective-permute-start(bf16[6144,256]{1,0:T(8,128)(2,1)S(1)} %constant_dynamic-update-slice_fusion.7), channel_id=1, source_target_pairs={{0,4},{4,0},{1,5},{5,1},{2,6},{6,2},{3,7},{7,3},{8,12},{12,8},{9,1... | collective-permute-start | bytes 9437192 | tf_op jit(solution)/shard_map/ppermute | solution.py:60
  37.5 2.0 %collective-permute-start.10 = (bf16[1024,256]{1,0:T(8,128)(2,1)S(1)}, bf16[1024,256]{1,0:T(8,128)(2,1)S(1)}, u32[]{:S(2)}, u32[]{:S(2)}) collective-permute-start(bf16[1024,256]{1,0:T(8,128)(2,1)S(1)} %pad_maximum_fusion.1.refs_1_), channel_id=1, source_target_pairs={{0,32},{64,96},{32,0},{96,64},{1,33},{65,97},{33,1},{97,65},{2,34}... | collective-permute-start | bytes 1572872 | tf_op jit(solution)/shard_map/ppermute | solution.py:40
  39.5 1.1 collective-permute-start.9
  40.6 2.5 %collective-permute-done.13.other_ref = bf16[512,256]{1,0:T(8,128)(2,1)S(1)} collective-permute-done((bf16[512,256]{1,0:T(8,128)(2,1)S(1)}, bf16[512,256]{1,0:T(8,128)(2,1)S(1)}, u32[]{:S(2)}, u32[]{:S(2)}) %collective-permute-start.13) | collective-permute-done | bytes 262176 | tf_op jit(solution)/shard_map/ppermute | solution.py:60
  43.1 1.3 %low_rank.1 = f32[32,128]{1,0:T(8,128)S(1)} custom-call(s32[17]{0:T(128)S(1)} %concatenate.32.info, bf16[512,8192]{1,0:T(8,128)(2,1)S(1)} %bitcast.28, bf16[512,256]{1,0:T(8,128)(2,1)S(1)} %constant_dynamic-update-slice_fusion.2.own_ref, bf16[512,256]{1,0:T(8,128)(2,1)S(1)} %collective-permute-done.13.other_ref), custom_call_target="tpu_custom_call" | custom-call | tf_op jit(solution)/shard_map/low_rank/pallas_call | solution.py:199
  44.4 1.7 %collective-permute-start.14 = (f32[32,128]{1,0:T(8,128)S(1)}, f32[32,128]{1,0:T(8,128)S(1)}, u32[]{:S(2)}, u32[]{:S(2)}) collective-permute-start(f32[32,128]{1,0:T(8,128)S(1)} %low_rank.1), channel_id=1, source_target_pairs={{0,1},{1,0},{2,3},{3,2},{4,5},{5,4},{6,7},{7,6},{8,9},{9,8},{10,11... | collective-permute-start | bytes 49160 | tf_op jit(solution)/shard_map/ppermute | solution.py:56
  46.1 2.0 %collective-permute-start.12 = (bf16[48,2048]{1,0:T(8,128)(2,1)S(1)}, bf16[48,2048]{1,0:T(8,128)(2,1)S(1)}, u32[]{:S(2)}, u32[]{:S(2)}) collective-permute-start(bf16[48,2048]{1,0:T(8,128)(2,1)S(1)} %bitcast.40), channel_id=1, source_target_pairs={{0,32},{32,0},{1,33},{33,1},{2,34},{34,2},{3,35},{35,3},{4,36},{36... | collective-permute-start | bytes 589832 | tf_op jit(solution)/shard_map/ppermute | solution.py:48
  48.1 3.3 %collective-permute-start.15 = (f32[64,128]{1,0:T(8,128)S(1)}, f32[64,128]{1,0:T(8,128)S(1)}, u32[]{:S(2)}, u32[]{:S(2)}) collective-permute-start(f32[64,128]{1,0:T(8,128)S(1)} %pad_maximum_fusion.4), channel_id=1, source_target_pairs={{0,2},{1,3},{2,0},{3,1},{4,6},{5,7},{6,4},{7,5},{8,10},{9,11},{10,... | collective-permute-start | bytes 98312 | tf_op jit(solution)/shard_map/ppermute | solution.py:56
  51.4 2.4 %main_product.2 = (f32[512,256]{1,0:T(8,128)S(1)}, f32[512,256]{1,0:T(8,128)S(1)}) custom-call(s32[17]{0:T(128)S(1)} %concatenate.32.info, bf16[512,8192]{1,0:T(8,128)(2,1)S(1)} %bitcast.29, bf16[1024,256]{1,0:T(8,128)(2,1)S(1)} %constant_dynamic-update-slice_fusion.refs_0_, bf16[1024,256]{1,0:T(8,128)(2,1)S(1)} %pad_maximum_fusion.1.refs_1_, ...), custom_call_target="tpu_custom_call" | custom-call | tf_op jit(solution)/shard_map/main_product/pallas_call | solution.py:242
  53.9 2.3 %main_product.3 = (f32[512,256]{1,0:T(8,128)S(1)}, f32[512,256]{1,0:T(8,128)S(1)}) custom-call(s32[17]{0:T(128)S(1)} %concatenate.32.info, bf16[512,8192]{1,0:T(8,128)(2,1)S(1)} %bitcast.30, bf16[6144,256]{1,0:T(8,128)(2,1)S(1)} %collective-permute-done.11.refs_0_), custom_call_target="tpu_custom_call" | custom-call | tf_op jit(solution)/shard_map/main_product/pallas_call | solution.py:242
  56.3 1.3 %collective-permute-start.16 = (bf16[1024,256]{1,0:T(8,128)(2,1)S(1)}, bf16[1024,256]{1,0:T(8,128)(2,1)S(1)}, u32[]{:S(2)}, u32[]{:S(2)}) collective-permute-start(bf16[1024,256]{1,0:T(8,128)(2,1)S(1)} %collective-permute-done.9.refs_0_), channel_id=1, source_target_pairs={{0,4},{4,0},{1,5},{5,1},{2,6},{6,2},{3,7},{7,3},{8,12},{12,8},{9,1... | collective-permute-start | bytes 1572872 | tf_op jit(solution)/shard_map/ppermute | solution.py:60
  57.7 1.4 %collective-permute-start.20 = (bf16[96,2048]{1,0:T(8,128)(2,1)S(1)}, bf16[96,2048]{1,0:T(8,128)(2,1)S(1)}, u32[]{:S(2)}, u32[]{:S(2)}) collective-permute-start(bf16[96,2048]{1,0:T(8,128)(2,1)S(1)} %constant_dynamic-update-slice_fusion.13), channel_id=1, source_target_pairs={{0,8},{8,16},{16,24},{24,0},{1,9},{9,17},{17,25},{25,1},{2,10},{10... | collective-permute-start | bytes 1179656 | tf_op jit(solution)/shard_map/ppermute | solution.py:44
  59.2 2.5 %collective-permute-start.21 = (bf16[96,2048]{1,0:T(8,128)(2,1)S(1)}, bf16[96,2048]{1,0:T(8,128)(2,1)S(1)}, u32[]{:S(2)}, u32[]{:S(2)}) collective-permute-start(bf16[96,2048]{1,0:T(8,128)(2,1)S(1)} %constant_dynamic-update-slice_fusion.13), channel_id=1, source_target_pairs={{0,16},{8,24},{16,0},{24,8},{1,17},{9,25},{17,1},{25,9},{2,18},{10... | collective-permute-start | bytes 1179656 | tf_op jit(solution)/shard_map/ppermute | solution.py:44
  61.6 0.4 collective-permute-start.22
  62.1 3.7 %finish.1 = (bf16[3,128,2,256]{3,2,1,0:T(2,128)(2,1)S(1)}, bf16[3,128,2,256]{3,2,1,0:T(2,128)(2,1)S(1)}) custom-call(s32[17]{0:T(128)S(1)} %concatenate.32.info, bf16[512,8192]{1,0:T(8,128)(2,1)S(1)} %bitcast.31, bf16[1024,256]{1,0:T(8,128)(2,1)S(1)} %collective-permute-done.9.refs_0_, bf16[1024,256]{1,0:T(8,128)(2,1)S(1)} %collective-permute-done.10.refs_1_, ...), custom_call_target="tpu_custom_call" | custom-call | tf_op jit(solution)/shard_map/finish/pallas_call | solution.py:293
  65.8 1.2 collective-permute-start.18
  67.0 1.5 %collective-permute-start.19 = (bf16[3,128,2,256]{3,2,1,0:T(2,128)(2,1)S(1)}, bf16[3,128,2,256]{3,2,1,0:T(2,128)(2,1)S(1)}, u32[]{:S(2)}, u32[]{:S(2)}) collective-permute-start(bf16[3,128,2,256]{3,2,1,0:T(2,128)(2,1)S(1)} %get-tuple-element.89), channel_id=1, source_target_pairs={{0,96},{32,64},{64,32},{96,0},{1,97},{33,65},{65,33},{97,1},{2,98}... | collective-permute-start | bytes 1179656 | tf_op jit(solution)/shard_map/ppermute | solution.py:32
  68.5 1.0 collective-permute-done.20
  69.5 9.4 %collective-permute-done.21 = bf16[96,2048]{1,0:T(8,128)(2,1)S(1)} collective-permute-done((bf16[96,2048]{1,0:T(8,128)(2,1)S(1)}, bf16[96,2048]{1,0:T(8,128)(2,1)S(1)}, u32[]{:S(2)}, u32[]{:S(2)}) %collective-permute-start.21) | collective-permute-done | bytes 393248 | tf_op jit(solution)/shard_map/ppermute | solution.py:44
  79.0 1.3 %collective-permute-start.25 = (bf16[384,2048]{1,0:T(8,128)(2,1)S(1)}, bf16[384,2048]{1,0:T(8,128)(2,1)S(1)}, u32[]{:S(2)}, u32[]{:S(2)}) collective-permute-start(bf16[384,2048]{1,0:T(8,128)(2,1)S(1)} %constant_dynamic-update-slice_fusion.15.refs_0_), channel_id=1, source_target_pairs={{0,4},{4,0},{1,5},{5,1},{2,6},{6,2},{3,7},{7,3},{8,12},{12,8},{9,1... | collective-permute-start | bytes 4718600 | tf_op jit(solution)/shard_map/ppermute | solution.py:60
  80.3 1.1 pad_maximum_fusion.refs_0_
  81.6 1.1 collective-permute-start.23
  82.6 1.7 %collective-permute-start.24 = (bf16[2,3,128,2,256]{4,3,2,1,0:T(2,128)(2,1)S(1)}, bf16[2,3,128,2,256]{4,3,2,1,0:T(2,128)(2,1)S(1)}, u32[]{:S(2)}, u32[]{:S(2)}) collective-permute-start(bf16[2,3,128,2,256]{4,3,2,1,0:T(2,128)(2,1)S(1)} %pad_maximum_fusion.refs_0_), channel_id=1, source_target_pairs={{0,24},{8,0},{16,8},{24,16},{1,25},{9,1},{17,9},{25,17},{2,26},{10... | collective-permute-start | bytes 2359304 | tf_op jit(solution)/shard_map/ppermute | solution.py:44
  84.5 5.2 %project.1 = (bf16[192,512]{1,0:T(8,128)(2,1)S(1)}, bf16[192,512]{1,0:T(8,128)(2,1)S(1)}, bf16[192,512]{1,0:T(8,128)(2,1)S(1)}, bf16[192,512]{1,0:T(8,128)(2,1)S(1)}) custom-call(s32[17]{0:T(128)S(1)} %concatenate.32.info, s32[768,1]{1,0:T(8,128)S(1)} %broadcast_in_dim.20.keep, bf16[128,2048]{1,0:T(8,128)(2,1)S(1)} %bitcast.34, ...), custom_call_target="tpu_custom_call" | custom-call | tf_op jit(solution)/shard_map/project/pallas_call | solution.py:410
  89.7 1.7 %collective-permute-start.27 = (bf16[192,512]{1,0:T(8,128)(2,1)S(1)}, bf16[192,512]{1,0:T(8,128)(2,1)S(1)}, u32[]{:S(2)}, u32[]{:S(2)}) collective-permute-start(bf16[192,512]{1,0:T(8,128)(2,1)S(1)} %get-tuple-element.102), channel_id=1, source_target_pairs={{0,1},{1,2},{2,3},{3,0},{4,5},{5,6},{6,7},{7,4},{8,9},{9,10},{10,1... | collective-permute-start | bytes 589832 | tf_op jit(solution)/shard_map/ppermute | solution.py:52
  91.4 2.2 %collective-permute-start.28 = (bf16[192,512]{1,0:T(8,128)(2,1)S(1)}, bf16[192,512]{1,0:T(8,128)(2,1)S(1)}, u32[]{:S(2)}, u32[]{:S(2)}) collective-permute-start(bf16[192,512]{1,0:T(8,128)(2,1)S(1)} %get-tuple-element.103), channel_id=1, source_target_pairs={{0,3},{1,0},{2,1},{3,2},{4,7},{5,4},{6,5},{7,6},{8,11},{9,8},{10,9... | collective-permute-start | bytes 589832 | tf_op jit(solution)/shard_map/ppermute | solution.py:52
  93.6 1.2 %collective-permute-start.33 = (bf16[192,512]{1,0:T(8,128)(2,1)S(1)}, bf16[192,512]{1,0:T(8,128)(2,1)S(1)}, u32[]{:S(2)}, u32[]{:S(2)}) collective-permute-start(bf16[192,512]{1,0:T(8,128)(2,1)S(1)} %get-tuple-element.109), channel_id=1, source_target_pairs={{0,2},{1,3},{2,0},{3,1},{4,6},{5,7},{6,4},{7,5},{8,10},{9,11},{10,... | collective-permute-start | bytes 589832 | tf_op jit(solution)/shard_map/ppermute | solution.py:52
  94.8 6.7 %collective-permute-done.23.refs_1_ = bf16[2,3,128,2,256]{4,3,2,1,0:T(2,128)(2,1)S(1)} collective-permute-done((bf16[2,3,128,2,256]{4,3,2,1,0:T(2,128)(2,1)S(1)}, bf16[2,3,128,2,256]{4,3,2,1,0:T(2,128)(2,1)S(1)}, u32[]{:S(2)}, u32[]{:S(2)}) %collective-permute-start.23) | collective-permute-done | bytes 786464 | tf_op jit(solution)/shard_map/ppermute | solution.py:44
  101.5 1.4 %collective-permute-start.31 = (bf16[2,3,128,2,256]{4,3,2,1,0:T(2,128)(2,1)S(1)}, bf16[2,3,128,2,256]{4,3,2,1,0:T(2,128)(2,1)S(1)}, u32[]{:S(2)}, u32[]{:S(2)}) collective-permute-start(bf16[2,3,128,2,256]{4,3,2,1,0:T(2,128)(2,1)S(1)} %collective-permute-done.23.refs_1_), channel_id=1, source_target_pairs={{0,4},{4,0},{1,5},{5,1},{2,6},{6,2},{3,7},{7,3},{8,12},{12,8},{9,1... | collective-permute-start | bytes 2359304 | tf_op jit(solution)/shard_map/ppermute | solution.py:60
  103.7 2.6 %collective-permute-start.30 = (bf16[3,128,2,256]{3,2,1,0:T(2,128)(2,1)S(1)}, bf16[3,128,2,256]{3,2,1,0:T(2,128)(2,1)S(1)}, u32[]{:S(2)}, u32[]{:S(2)}) collective-permute-start(bf16[3,128,2,256]{3,2,1,0:T(2,128)(2,1)S(1)} %slice_bitcast_fusion), channel_id=1, source_target_pairs={{0,24},{8,0},{16,8},{24,16},{1,25},{9,1},{17,9},{25,17},{2,26},{10... | collective-permute-start | bytes 1179656 | tf_op jit(solution)/shard_map/ppermute | solution.py:44
  106.3 0.8 add_convert_fusion
  107.1 7.9 %collective-permute-done.29 = bf16[3,128,2,256]{3,2,1,0:T(2,128)(2,1)S(1)} collective-permute-done((bf16[3,128,2,256]{3,2,1,0:T(2,128)(2,1)S(1)}, bf16[3,128,2,256]{3,2,1,0:T(2,128)(2,1)S(1)}, u32[]{:S(2)}, u32[]{:S(2)}) %collective-permute-start.29) | collective-permute-done | bytes 393248 | tf_op jit(solution)/shard_map/ppermute | solution.py:44
  115.0 1.4 %collective-permute-start.34 = (bf16[3,128,2,256]{3,2,1,0:T(2,128)(2,1)S(1)}, bf16[3,128,2,256]{3,2,1,0:T(2,128)(2,1)S(1)}, u32[]{:S(2)}, u32[]{:S(2)}) collective-permute-start(bf16[3,128,2,256]{3,2,1,0:T(2,128)(2,1)S(1)} %collective-permute-done.29), channel_id=1, source_target_pairs={{0,4},{4,0},{1,5},{5,1},{2,6},{6,2},{3,7},{7,3},{8,12},{12,8},{9,1... | collective-permute-start | bytes 1179656 | tf_op jit(solution)/shard_map/ppermute | solution.py:60
  116.5 2.9 %place.2.refs_4_ = bf16[1,2,2048,2,256]{4,3,2,1,0:T(2,128)(2,1)} custom-call(s32[17]{0:T(128)S(1)} %concatenate.32.info, bf16[2,3,128,2,256]{4,3,2,1,0:T(2,128)(2,1)S(1)} %pad_maximum_fusion.refs_0_, bf16[2,3,128,2,256]{4,3,2,1,0:T(2,128)(2,1)S(1)} %collective-permute-done.23.refs_1_, bf16[2,3,128,2,256]{4,3,2,1,0:T(2,128)(2,1)S(1)} %collective-permute-done.24.refs_2_, ...), custom_call_target="tpu_custom_call" | custom-call | tf_op jit(solution)/shard_map/place/pallas_call | solution.py:368
  119.4 0.9 place.3
  (89 shorter events, 2.7 us)
Async XLA Ops:
  0.6 23.6 %copy-start.5 = (s32[48]{0:T(128)S(1)}, s32[48]{0:T(128)}, u32[]{:S(2)}) copy-start(s32[48]{0:T(128)} %len_ref) | copy-start | bytes 580
  0.6 23.5 %copy-start.6 = (bf16[48,2048]{1,0:T(8,128)(2,1)S(1)}, bf16[48,2048]{1,0:T(8,128)(2,1)}, u32[]{:S(2)}) copy-start(bf16[48,2048]{1,0:T(8,128)(2,1)} %param.20) | copy-start | bytes 589828
  0.7 23.6 %copy-start.4 = (bf16[48,2,256]{2,1,0:T(2,128)(2,1)S(1)}, bf16[48,2,256]{2,1,0:T(2,128)(2,1)}, u32[]{:S(2)}) copy-start(bf16[48,2,256]{2,1,0:T(2,128)(2,1)} %cur_ref.1) | copy-start | bytes 147460
  4.2 14.1 %collective-permute-start = (bf16[512,256]{1,0:T(8,128)(2,1)S(1)}, bf16[512,256]{1,0:T(8,128)(2,1)S(1)}, u32[]{:S(2)}, u32[]{:S(2)}) collective-permute-start(bf16[512,256]{1,0:T(8,128)(2,1)S(1)} %get-tuple-element.62), channel_id=1, source_target_pairs={{0,96},{32,64},{64,32},{96,0},{1,97},{33,65},{65,33},{97,1},{2,98}... | collective-permute-start | bytes 786440 | tf_op jit(solution)/shard_map/ppermute | solution.py:32
  7.6 6.1 %collective-permute-start.1 = (bf16[320,256]{1,0:T(8,128)(2,1)S(1)}, bf16[320,256]{1,0:T(8,128)(2,1)S(1)}, u32[]{:S(2)}, u32[]{:S(2)}) collective-permute-start(bf16[320,256]{1,0:T(8,128)(2,1)S(1)} %get-tuple-element.64), channel_id=1, source_target_pairs={{0,8},{8,16},{16,24},{24,0},{1,9},{9,17},{17,25},{25,1},{2,10},{10... | collective-permute-start | bytes 491528 | tf_op jit(solution)/shard_map/ppermute | solution.py:44
  8.9 9.4 %collective-permute-start.2 = (bf16[320,256]{1,0:T(8,128)(2,1)S(1)}, bf16[320,256]{1,0:T(8,128)(2,1)S(1)}, u32[]{:S(2)}, u32[]{:S(2)}) collective-permute-start(bf16[320,256]{1,0:T(8,128)(2,1)S(1)} %get-tuple-element.64), channel_id=1, source_target_pairs={{0,16},{8,24},{16,0},{24,8},{1,17},{9,25},{17,1},{25,9},{2,18},{10... | collective-permute-start | bytes 491528 | tf_op jit(solution)/shard_map/ppermute | solution.py:44
  11.5 6.8 %collective-permute-start.3 = (bf16[320,256]{1,0:T(8,128)(2,1)S(1)}, bf16[320,256]{1,0:T(8,128)(2,1)S(1)}, u32[]{:S(2)}, u32[]{:S(2)}) collective-permute-start(bf16[320,256]{1,0:T(8,128)(2,1)S(1)} %get-tuple-element.64), channel_id=1, source_target_pairs={{0,24},{8,0},{16,8},{24,16},{1,25},{9,1},{17,9},{25,17},{2,26},{10... | collective-permute-start | bytes 491528 | tf_op jit(solution)/shard_map/ppermute | solution.py:44
  18.5 14.3 %collective-permute-start.6 = (bf16[1024,256]{1,0:T(8,128)(2,1)S(1)}, bf16[1024,256]{1,0:T(8,128)(2,1)S(1)}, u32[]{:S(2)}, u32[]{:S(2)}) collective-permute-start(bf16[1024,256]{1,0:T(8,128)(2,1)S(1)} %pad_maximum_fusion.1.refs_1_), channel_id=1, source_target_pairs={{0,64},{64,32},{32,96},{96,0},{1,65},{65,33},{33,97},{97,1},{2,66}... | collective-permute-start | bytes 1572872 | tf_op jit(solution)/shard_map/ppermute | solution.py:40
  18.5 14.3 %collective-permute-start.7 = (bf16[1024,256]{1,0:T(8,128)(2,1)S(1)}, bf16[1024,256]{1,0:T(8,128)(2,1)S(1)}, u32[]{:S(2)}, u32[]{:S(2)}) collective-permute-start(bf16[1024,256]{1,0:T(8,128)(2,1)S(1)} %pad_maximum_fusion.1.refs_1_), channel_id=1, source_target_pairs={{0,96},{64,0},{32,64},{96,32},{1,97},{65,1},{33,65},{97,33},{2,98}... | collective-permute-start | bytes 1572872 | tf_op jit(solution)/shard_map/ppermute | solution.py:40
  21.2 21.8 %slice-start = ((s8[8388608]{0:T(1024)(128)(4,1)}), s8[4194304]{0:T(1024)(128)(4,1)S(1)}, s32[]{:S(2)}) async-start(s8[8388608]{0:T(1024)(128)(4,1)} %bitcast.26), calls=%async_computation | async-start | bytes 8388608
  21.3 12.3 %collective-permute-start.4 = (bf16[1024,256]{1,0:T(8,128)(2,1)S(1)}, bf16[1024,256]{1,0:T(8,128)(2,1)S(1)}, u32[]{:S(2)}, u32[]{:S(2)}) collective-permute-start(bf16[1024,256]{1,0:T(8,128)(2,1)S(1)} %constant_dynamic-update-slice_fusion.refs_0_), channel_id=1, source_target_pairs={{0,8},{8,16},{16,24},{24,0},{1,9},{9,17},{17,25},{25,1},{2,10},{10... | collective-permute-start | bytes 1572872 | tf_op jit(solution)/shard_map/ppermute | solution.py:44
  22.7 11.2 %collective-permute-start.5 = (bf16[1024,256]{1,0:T(8,128)(2,1)S(1)}, bf16[1024,256]{1,0:T(8,128)(2,1)S(1)}, u32[]{:S(2)}, u32[]{:S(2)}) collective-permute-start(bf16[1024,256]{1,0:T(8,128)(2,1)S(1)} %constant_dynamic-update-slice_fusion.refs_0_), channel_id=1, source_target_pairs={{0,24},{8,0},{16,8},{24,16},{1,25},{9,1},{17,9},{25,17},{2,26},{10... | collective-permute-start | bytes 1572872 | tf_op jit(solution)/shard_map/ppermute | solution.py:44
  24.1 8.7 %collective-permute-start.8 = (bf16[256,256]{1,0:T(8,128)(2,1)S(1)}, bf16[256,256]{1,0:T(8,128)(2,1)S(1)}, u32[]{:S(2)}, u32[]{:S(2)}) collective-permute-start(bf16[256,256]{1,0:T(8,128)(2,1)S(1)} %pad_maximum_fusion.2), channel_id=1, source_target_pairs={{0,32},{32,0},{1,33},{33,1},{2,34},{34,2},{3,35},{35,3},{4,36},{36... | collective-permute-start | bytes 393224 | tf_op jit(solution)/shard_map/ppermute | solution.py:48
  24.2 18.8 %slice-start.1 = ((s8[8388608]{0:T(1024)(128)(4,1)}), s8[4194304]{0:T(1024)(128)(4,1)S(1)}, s32[]{:S(2)}) async-start(s8[8388608]{0:T(1024)(128)(4,1)} %bitcast.26), calls=%async_computation.1 | async-start | bytes 8388608
  34.2 19.6 %collective-permute-start.11 = (bf16[6144,256]{1,0:T(8,128)(2,1)S(1)}, bf16[6144,256]{1,0:T(8,128)(2,1)S(1)}, u32[]{:S(2)}, u32[]{:S(2)}) collective-permute-start(bf16[6144,256]{1,0:T(8,128)(2,1)S(1)} %constant_dynamic-update-slice_fusion.7), channel_id=1, source_target_pairs={{0,4},{4,0},{1,5},{5,1},{2,6},{6,2},{3,7},{7,3},{8,12},{12,8},{9,1... | collective-permute-start | bytes 9437192 | tf_op jit(solution)/shard_map/ppermute | solution.py:60
  37.4 5.7 %collective-permute-start.13 = (bf16[512,256]{1,0:T(8,128)(2,1)S(1)}, bf16[512,256]{1,0:T(8,128)(2,1)S(1)}, u32[]{:S(2)}, u32[]{:S(2)}) collective-permute-start(bf16[512,256]{1,0:T(8,128)(2,1)S(1)} %constant_dynamic-update-slice_fusion.2.own_ref), channel_id=1, source_target_pairs={{0,4},{4,0},{1,5},{5,1},{2,6},{6,2},{3,7},{7,3},{8,12},{12,8},{9,1... | collective-permute-start | bytes 786440 | tf_op jit(solution)/shard_map/ppermute | solution.py:60
  37.5 18.8 %collective-permute-start.10 = (bf16[1024,256]{1,0:T(8,128)(2,1)S(1)}, bf16[1024,256]{1,0:T(8,128)(2,1)S(1)}, u32[]{:S(2)}, u32[]{:S(2)}) collective-permute-start(bf16[1024,256]{1,0:T(8,128)(2,1)S(1)} %pad_maximum_fusion.1.refs_1_), channel_id=1, source_target_pairs={{0,32},{64,96},{32,0},{96,64},{1,33},{65,97},{33,1},{97,65},{2,34}... | collective-permute-start | bytes 1572872 | tf_op jit(solution)/shard_map/ppermute | solution.py:40
  39.5 16.8 %collective-permute-start.9 = (bf16[1024,256]{1,0:T(8,128)(2,1)S(1)}, bf16[1024,256]{1,0:T(8,128)(2,1)S(1)}, u32[]{:S(2)}, u32[]{:S(2)}) collective-permute-start(bf16[1024,256]{1,0:T(8,128)(2,1)S(1)} %constant_dynamic-update-slice_fusion.refs_0_), channel_id=1, source_target_pairs={{0,16},{8,24},{16,0},{24,8},{1,17},{9,25},{17,1},{25,9},{2,18},{10... | collective-permute-start | bytes 1572872 | tf_op jit(solution)/shard_map/ppermute | solution.py:44
  44.4 3.7 %collective-permute-start.14 = (f32[32,128]{1,0:T(8,128)S(1)}, f32[32,128]{1,0:T(8,128)S(1)}, u32[]{:S(2)}, u32[]{:S(2)}) collective-permute-start(f32[32,128]{1,0:T(8,128)S(1)} %low_rank.1), channel_id=1, source_target_pairs={{0,1},{1,0},{2,3},{3,2},{4,5},{5,4},{6,7},{7,6},{8,9},{9,8},{10,11... | collective-permute-start | bytes 49160 | tf_op jit(solution)/shard_map/ppermute | solution.py:56
  46.1 10.2 %collective-permute-start.12 = (bf16[48,2048]{1,0:T(8,128)(2,1)S(1)}, bf16[48,2048]{1,0:T(8,128)(2,1)S(1)}, u32[]{:S(2)}, u32[]{:S(2)}) collective-permute-start(bf16[48,2048]{1,0:T(8,128)(2,1)S(1)} %bitcast.40), channel_id=1, source_target_pairs={{0,32},{32,0},{1,33},{33,1},{2,34},{34,2},{3,35},{35,3},{4,36},{36... | collective-permute-start | bytes 589832 | tf_op jit(solution)/shard_map/ppermute | solution.py:48
  48.1 5.7 %collective-permute-start.15 = (f32[64,128]{1,0:T(8,128)S(1)}, f32[64,128]{1,0:T(8,128)S(1)}, u32[]{:S(2)}, u32[]{:S(2)}) collective-permute-start(f32[64,128]{1,0:T(8,128)S(1)} %pad_maximum_fusion.4), channel_id=1, source_target_pairs={{0,2},{1,3},{2,0},{3,1},{4,6},{5,7},{6,4},{7,5},{8,10},{9,11},{10,... | collective-permute-start | bytes 98312 | tf_op jit(solution)/shard_map/ppermute | solution.py:56
  53.9 8.2 %copy-start.2 = (bf16[8,2,16,256]{3,2,1,0:T(8,128)(2,1)S(1)}, bf16[8,2,16,256]{3,2,1,0:T(8,128)(2,1)}, u32[]{:S(2)}) copy-start(bf16[8,2,16,256]{3,2,1,0:T(8,128)(2,1)} %refs_9_.1) | copy-start | bytes 393220
  56.3 5.8 %collective-permute-start.16 = (bf16[1024,256]{1,0:T(8,128)(2,1)S(1)}, bf16[1024,256]{1,0:T(8,128)(2,1)S(1)}, u32[]{:S(2)}, u32[]{:S(2)}) collective-permute-start(bf16[1024,256]{1,0:T(8,128)(2,1)S(1)} %collective-permute-done.9.refs_0_), channel_id=1, source_target_pairs={{0,4},{4,0},{1,5},{5,1},{2,6},{6,2},{3,7},{7,3},{8,12},{12,8},{9,1... | collective-permute-start | bytes 1572872 | tf_op jit(solution)/shard_map/ppermute | solution.py:60
  57.6 4.5 %collective-permute-start.17 = (bf16[1024,256]{1,0:T(8,128)(2,1)S(1)}, bf16[1024,256]{1,0:T(8,128)(2,1)S(1)}, u32[]{:S(2)}, u32[]{:S(2)}) collective-permute-start(bf16[1024,256]{1,0:T(8,128)(2,1)S(1)} %collective-permute-done.10.refs_1_), channel_id=1, source_target_pairs={{0,4},{4,0},{1,5},{5,1},{2,6},{6,2},{3,7},{7,3},{8,12},{12,8},{9,1... | collective-permute-start | bytes 1572872 | tf_op jit(solution)/shard_map/ppermute | solution.py:60
  57.7 11.7 %collective-permute-start.20 = (bf16[96,2048]{1,0:T(8,128)(2,1)S(1)}, bf16[96,2048]{1,0:T(8,128)(2,1)S(1)}, u32[]{:S(2)}, u32[]{:S(2)}) collective-permute-start(bf16[96,2048]{1,0:T(8,128)(2,1)S(1)} %constant_dynamic-update-slice_fusion.13), channel_id=1, source_target_pairs={{0,8},{8,16},{16,24},{24,0},{1,9},{9,17},{17,25},{25,1},{2,10},{10... | collective-permute-start | bytes 1179656 | tf_op jit(solution)/shard_map/ppermute | solution.py:44
  59.2 19.7 %collective-permute-start.21 = (bf16[96,2048]{1,0:T(8,128)(2,1)S(1)}, bf16[96,2048]{1,0:T(8,128)(2,1)S(1)}, u32[]{:S(2)}, u32[]{:S(2)}) collective-permute-start(bf16[96,2048]{1,0:T(8,128)(2,1)S(1)} %constant_dynamic-update-slice_fusion.13), channel_id=1, source_target_pairs={{0,16},{8,24},{16,0},{24,8},{1,17},{9,25},{17,1},{25,9},{2,18},{10... | collective-permute-start | bytes 1179656 | tf_op jit(solution)/shard_map/ppermute | solution.py:44
  61.6 17.2 %collective-permute-start.22 = (bf16[96,2048]{1,0:T(8,128)(2,1)S(1)}, bf16[96,2048]{1,0:T(8,128)(2,1)S(1)}, u32[]{:S(2)}, u32[]{:S(2)}) collective-permute-start(bf16[96,2048]{1,0:T(8,128)(2,1)S(1)} %constant_dynamic-update-slice_fusion.13), channel_id=1, source_target_pairs={{0,24},{8,0},{16,8},{24,16},{1,25},{9,1},{17,9},{25,17},{2,26},{10... | collective-permute-start | bytes 1179656 | tf_op jit(solution)/shard_map/ppermute | solution.py:44
  65.8 18.5 %copy-start.7 = (s32[768]{0:T(1024)S(1)}, s32[768]{0:T(1024)}, u32[]{:S(2)}) copy-start(s32[768]{0:T(1024)} %param.24) | copy-start | bytes 9220
  65.8 18.7 %copy-start = (bf16[2048,512]{1,0:T(8,128)(2,1)S(1)}, bf16[2048,512]{1,0:T(8,128)(2,1)}, u32[]{:S(2)}) copy-start(bf16[2048,512]{1,0:T(8,128)(2,1)} %w_ref.1) | copy-start | bytes 6291460
  65.8 18.7 %copy-start.1 = (bf16[2048,8,16]{0,2,1:T(8,128)(2,1)S(1)}, bf16[2048,8,16]{0,2,1:T(8,128)(2,1)}, u32[]{:S(2)}) copy-start(bf16[2048,8,16]{0,2,1:T(8,128)(2,1)} %param.26) | copy-start | bytes 1572868
  65.8 18.7 %copy-start.3 = (bf16[8,16,512]{2,1,0:T(8,128)(2,1)S(1)}, bf16[8,16,512]{2,1,0:T(8,128)(2,1)}, u32[]{:S(2)}) copy-start(bf16[8,16,512]{2,1,0:T(8,128)(2,1)} %param.27) | copy-start | bytes 393220
  65.8 13.0 %collective-permute-start.18 = (bf16[3,128,2,256]{3,2,1,0:T(2,128)(2,1)S(1)}, bf16[3,128,2,256]{3,2,1,0:T(2,128)(2,1)S(1)}, u32[]{:S(2)}, u32[]{:S(2)}) collective-permute-start(bf16[3,128,2,256]{3,2,1,0:T(2,128)(2,1)S(1)} %get-tuple-element.88), channel_id=1, source_target_pairs={{0,64},{64,0},{1,65},{65,1},{2,66},{66,2},{3,67},{67,3},{4,68},{68... | collective-permute-start | bytes 1179656 | tf_op jit(solution)/shard_map/ppermute | solution.py:492
  67.0 11.9 %collective-permute-start.19 = (bf16[3,128,2,256]{3,2,1,0:T(2,128)(2,1)S(1)}, bf16[3,128,2,256]{3,2,1,0:T(2,128)(2,1)S(1)}, u32[]{:S(2)}, u32[]{:S(2)}) collective-permute-start(bf16[3,128,2,256]{3,2,1,0:T(2,128)(2,1)S(1)} %get-tuple-element.89), channel_id=1, source_target_pairs={{0,96},{32,64},{64,32},{96,0},{1,97},{33,65},{65,33},{97,1},{2,98}... | collective-permute-start | bytes 1179656 | tf_op jit(solution)/shard_map/ppermute | solution.py:32
  79.0 5.5 %collective-permute-start.25 = (bf16[384,2048]{1,0:T(8,128)(2,1)S(1)}, bf16[384,2048]{1,0:T(8,128)(2,1)S(1)}, u32[]{:S(2)}, u32[]{:S(2)}) collective-permute-start(bf16[384,2048]{1,0:T(8,128)(2,1)S(1)} %constant_dynamic-update-slice_fusion.15.refs_0_), channel_id=1, source_target_pairs={{0,4},{4,0},{1,5},{5,1},{2,6},{6,2},{3,7},{7,3},{8,12},{12,8},{9,1... | collective-permute-start | bytes 4718600 | tf_op jit(solution)/shard_map/ppermute | solution.py:60
  81.5 8.2 %collective-permute-start.26 = (bf16[2,3,128,2,256]{4,3,2,1,0:T(2,128)(2,1)S(1)}, bf16[2,3,128,2,256]{4,3,2,1,0:T(2,128)(2,1)S(1)}, u32[]{:S(2)}, u32[]{:S(2)}) collective-permute-start(bf16[2,3,128,2,256]{4,3,2,1,0:T(2,128)(2,1)S(1)} %pad_maximum_fusion.refs_0_), channel_id=1, source_target_pairs={{0,4},{4,0},{1,5},{5,1},{2,6},{6,2},{3,7},{7,3},{8,12},{12,8},{9,1... | collective-permute-start | bytes 2359304 | tf_op jit(solution)/shard_map/ppermute | solution.py:60
  81.6 20.0 %collective-permute-start.23 = (bf16[2,3,128,2,256]{4,3,2,1,0:T(2,128)(2,1)S(1)}, bf16[2,3,128,2,256]{4,3,2,1,0:T(2,128)(2,1)S(1)}, u32[]{:S(2)}, u32[]{:S(2)}) collective-permute-start(bf16[2,3,128,2,256]{4,3,2,1,0:T(2,128)(2,1)S(1)} %pad_maximum_fusion.refs_0_), channel_id=1, source_target_pairs={{0,8},{8,16},{16,24},{24,0},{1,9},{9,17},{17,25},{25,1},{2,10},{10... | collective-permute-start | bytes 2359304 | tf_op jit(solution)/shard_map/ppermute | solution.py:44
  82.6 18.9 %collective-permute-start.24 = (bf16[2,3,128,2,256]{4,3,2,1,0:T(2,128)(2,1)S(1)}, bf16[2,3,128,2,256]{4,3,2,1,0:T(2,128)(2,1)S(1)}, u32[]{:S(2)}, u32[]{:S(2)}) collective-permute-start(bf16[2,3,128,2,256]{4,3,2,1,0:T(2,128)(2,1)S(1)} %pad_maximum_fusion.refs_0_), channel_id=1, source_target_pairs={{0,24},{8,0},{16,8},{24,16},{1,25},{9,1},{17,9},{25,17},{2,26},{10... | collective-permute-start | bytes 2359304 | tf_op jit(solution)/shard_map/ppermute | solution.py:44
  89.7 11.9 %collective-permute-start.27 = (bf16[192,512]{1,0:T(8,128)(2,1)S(1)}, bf16[192,512]{1,0:T(8,128)(2,1)S(1)}, u32[]{:S(2)}, u32[]{:S(2)}) collective-permute-start(bf16[192,512]{1,0:T(8,128)(2,1)S(1)} %get-tuple-element.102), channel_id=1, source_target_pairs={{0,1},{1,2},{2,3},{3,0},{4,5},{5,6},{6,7},{7,4},{8,9},{9,10},{10,1... | collective-permute-start | bytes 589832 | tf_op jit(solution)/shard_map/ppermute | solution.py:52
  91.4 10.1 %collective-permute-start.28 = (bf16[192,512]{1,0:T(8,128)(2,1)S(1)}, bf16[192,512]{1,0:T(8,128)(2,1)S(1)}, u32[]{:S(2)}, u32[]{:S(2)}) collective-permute-start(bf16[192,512]{1,0:T(8,128)(2,1)S(1)} %get-tuple-element.103), channel_id=1, source_target_pairs={{0,3},{1,0},{2,1},{3,2},{4,7},{5,4},{6,5},{7,6},{8,11},{9,8},{10,9... | collective-permute-start | bytes 589832 | tf_op jit(solution)/shard_map/ppermute | solution.py:52
  93.6 12.7 %collective-permute-start.33 = (bf16[192,512]{1,0:T(8,128)(2,1)S(1)}, bf16[192,512]{1,0:T(8,128)(2,1)S(1)}, u32[]{:S(2)}, u32[]{:S(2)}) collective-permute-start(bf16[192,512]{1,0:T(8,128)(2,1)S(1)} %get-tuple-element.109), channel_id=1, source_target_pairs={{0,2},{1,3},{2,0},{3,1},{4,6},{5,7},{6,4},{7,5},{8,10},{9,11},{10,... | collective-permute-start | bytes 589832 | tf_op jit(solution)/shard_map/ppermute | solution.py:52
  101.5 13.5 %collective-permute-start.31 = (bf16[2,3,128,2,256]{4,3,2,1,0:T(2,128)(2,1)S(1)}, bf16[2,3,128,2,256]{4,3,2,1,0:T(2,128)(2,1)S(1)}, u32[]{:S(2)}, u32[]{:S(2)}) collective-permute-start(bf16[2,3,128,2,256]{4,3,2,1,0:T(2,128)(2,1)S(1)} %collective-permute-done.23.refs_1_), channel_id=1, source_target_pairs={{0,4},{4,0},{1,5},{5,1},{2,6},{6,2},{3,7},{7,3},{8,12},{12,8},{9,1... | collective-permute-start | bytes 2359304 | tf_op jit(solution)/shard_map/ppermute | solution.py:60
  103.0 12.1 %collective-permute-start.32 = (bf16[2,3,128,2,256]{4,3,2,1,0:T(2,128)(2,1)S(1)}, bf16[2,3,128,2,256]{4,3,2,1,0:T(2,128)(2,1)S(1)}, u32[]{:S(2)}, u32[]{:S(2)}) collective-permute-start(bf16[2,3,128,2,256]{4,3,2,1,0:T(2,128)(2,1)S(1)} %collective-permute-done.24.refs_2_), channel_id=1, source_target_pairs={{0,4},{4,0},{1,5},{5,1},{2,6},{6,2},{3,7},{7,3},{8,12},{12,8},{9,1... | collective-permute-start | bytes 2359304 | tf_op jit(solution)/shard_map/ppermute | solution.py:60
  103.5 11.5 %collective-permute-start.29 = (bf16[3,128,2,256]{3,2,1,0:T(2,128)(2,1)S(1)}, bf16[3,128,2,256]{3,2,1,0:T(2,128)(2,1)S(1)}, u32[]{:S(2)}, u32[]{:S(2)}) collective-permute-start(bf16[3,128,2,256]{3,2,1,0:T(2,128)(2,1)S(1)} %slice_bitcast_fusion.1), channel_id=1, source_target_pairs={{0,8},{8,16},{16,24},{24,0},{1,9},{9,17},{17,25},{25,1},{2,10},{10... | collective-permute-start | bytes 1179656 | tf_op jit(solution)/shard_map/ppermute | solution.py:44
  103.7 11.3 %collective-permute-start.30 = (bf16[3,128,2,256]{3,2,1,0:T(2,128)(2,1)S(1)}, bf16[3,128,2,256]{3,2,1,0:T(2,128)(2,1)S(1)}, u32[]{:S(2)}, u32[]{:S(2)}) collective-permute-start(bf16[3,128,2,256]{3,2,1,0:T(2,128)(2,1)S(1)} %slice_bitcast_fusion), channel_id=1, source_target_pairs={{0,24},{8,0},{16,8},{24,16},{1,25},{9,1},{17,9},{25,17},{2,26},{10... | collective-permute-start | bytes 1179656 | tf_op jit(solution)/shard_map/ppermute | solution.py:44
  115.0 4.4 %collective-permute-start.34 = (bf16[3,128,2,256]{3,2,1,0:T(2,128)(2,1)S(1)}, bf16[3,128,2,256]{3,2,1,0:T(2,128)(2,1)S(1)}, u32[]{:S(2)}, u32[]{:S(2)}) collective-permute-start(bf16[3,128,2,256]{3,2,1,0:T(2,128)(2,1)S(1)} %collective-permute-done.29), channel_id=1, source_target_pairs={{0,4},{4,0},{1,5},{5,1},{2,6},{6,2},{3,7},{7,3},{8,12},{12,8},{9,1... | collective-permute-start | bytes 1179656 | tf_op jit(solution)/shard_map/ppermute | solution.py:60
  116.4 3.0 %collective-permute-start.35 = (bf16[3,128,2,256]{3,2,1,0:T(2,128)(2,1)S(1)}, bf16[3,128,2,256]{3,2,1,0:T(2,128)(2,1)S(1)}, u32[]{:S(2)}, u32[]{:S(2)}) collective-permute-start(bf16[3,128,2,256]{3,2,1,0:T(2,128)(2,1)S(1)} %collective-permute-done.30), channel_id=1, source_target_pairs={{0,4},{4,0},{1,5},{5,1},{2,6},{6,2},{3,7},{7,3},{8,12},{12,8},{9,1... | collective-permute-start | bytes 1179656 | tf_op jit(solution)/shard_map/ppermute | solution.py:60

commit v12 on v11

--- a/solution.py
+++ b/solution.py
@@ -455,9 +455,7 @@
     )
     keys_across = x_mirror(keys)
     ring_values = ring(values, y_shift)
-    keys, keys_across, ring_values, cached_length = barrier(
-        (keys, keys_across, ring_values, cached_length)
-    )
+    keys, keys_across, cached_length = barrier((keys, keys_across, cached_length))
     key0 = jnp.concatenate([keys, keys_across], 0)
     value0 = jnp.concatenate([v[:256] for v in ring_values], 0)
     down0 = jnp.concatenate([v[256:] for v in ring_values], 0)

time: 121 us -> 119 us (0.983)
    ppermute x13, waiting for transfers between devices: 31.8 us -> 29.2 us  [y_shift(): return lax.ppermute(value, 'y', [(i, (i + k) % 4) for i in range(4)])]
    ppermute x13, starting transfers between devices: 18.6 us -> 20.4 us  [y_shift(): return lax.ppermute(value, 'y', [(i, (i + k) % 4) for i in range(4)])]
    ppermute x2, starting transfers between devices: 4.92 us -> 3.35 us  [x_mirror(): return lax.ppermute(value, ('pool', 'xh'), [(i, 3 - i) for i in range(4)])]
    ppermute x2, waiting for transfers between devices: 0.08 us -> 1.35 us  [xh_swap(): return lax.ppermute(value, 'xh', [(0, 1), (1, 0)])]
  transfers between devices with their start and end apart: 36 -> 36, of which waited for: 10 -> 9; matrix products, arithmetic and copies ran while one was open for 2% -> 2% of each run, Pallas kernels for 22% -> 22%
where the time goes in v12:
time: 119 us
  starting transfers between devices  49.6 us (42%)
  waiting for transfers between devices  34 us (29%)
  Pallas kernels  29.9 us (25%)
  local copies, waits for them, and re-layouts  2.12 us (2%)
  other arithmetic  1.95 us (2%)
  between operations  1.32 us (1%)
    ppermute x13, waiting for transfers between devices, y_shift(): return lax.ppermute(value, 'y', [(i, (i + k) % 4) for i in range(4)])  29.2 us
    ppermute x13, starting transfers between devices, y_shift(): return lax.ppermute(value, 'y', [(i, (i + k) % 4) for i in range(4)])  20.4 us
    ppermute x10, starting transfers between devices, core_swap(): return lax.ppermute(value, 'core', [(0, 1), (1, 0)])  8.67 us
    pallas_call x1, Pallas kernels, attend(): pl.pallas_call(functools.partial(attend_kernel, first * ROWS_STEP), grid_...  8.47 us
    pallas_call x1, Pallas kernels, project(): pl.pallas_call(project_kernel, in_specs=[SMEM] + [VMEM] * 6, out_specs=[V...  5.15 us
    ppermute x2, starting transfers between devices, z_flip(): return lax.ppermute(value, 'head', [(i, i ^ mask) for i in range(4)])  5.15 us
    ppermute x3, starting transfers between devices, z_shift(): return lax.ppermute(value, 'head', [(i, (i + k) % 4) for i in range(4)])  5.14 us
    pallas_call x2, Pallas kernels, main_product(): pl.pallas_call(functools.partial(main_kernel, pieces), in_specs=[SMEM] +...  4.73 us
  transfers between devices with their start and end apart: 36, of which 9 were waited for; matrix products, arithmetic and copies ran while one was open for 2% of the time, Pallas kernels for 22%

profile of v12, /device:TPU:1, one launch (start us, length us, event | category | flops | bytes accessed | tf_op | source)
XLA Modules:
  0.0 118.9 jit_solution(4193970641150240816)
XLA Ops:
  0.7 0.8 concatenate.32.info
  1.5 2.8 %pack.1 = (bf16[512,256]{1,0:T(8,128)(2,1)S(1)}, bf16[320,256]{1,0:T(8,128)(2,1)S(1)}) custom-call(s32[17]{0:T(128)S(1)} %concatenate.32.info, bf16[512,2,256]{2,1,0:T(2,128)(2,1)} %w_hbm.1, bf16[512,256]{1,0:T(8,128)(2,1)} %d_hbm.1), custom_call_target="tpu_custom_call" | custom-call | tf_op jit(solution)/shard_map/pack/pallas_call | solution.py:86
  4.2 2.2 %collective-permute-start.1 = (bf16[320,256]{1,0:T(8,128)(2,1)S(1)}, bf16[320,256]{1,0:T(8,128)(2,1)S(1)}, u32[]{:S(2)}, u32[]{:S(2)}) collective-permute-start(bf16[320,256]{1,0:T(8,128)(2,1)S(1)} %get-tuple-element.59), channel_id=1, source_target_pairs={{0,8},{8,16},{16,24},{24,0},{1,9},{9,17},{17,25},{25,1},{2,10},{10... | collective-permute-start | bytes 491528 | tf_op jit(solution)/shard_map/ppermute | solution.py:44
  6.4 2.6 %collective-permute-start.2 = (bf16[320,256]{1,0:T(8,128)(2,1)S(1)}, bf16[320,256]{1,0:T(8,128)(2,1)S(1)}, u32[]{:S(2)}, u32[]{:S(2)}) collective-permute-start(bf16[320,256]{1,0:T(8,128)(2,1)S(1)} %get-tuple-element.59), channel_id=1, source_target_pairs={{0,16},{8,24},{16,0},{24,8},{1,17},{9,25},{17,1},{25,9},{2,18},{10... | collective-permute-start | bytes 491528 | tf_op jit(solution)/shard_map/ppermute | solution.py:44
  9.1 1.1 collective-permute-start.3
  10.1 2.5 %collective-permute-start = (bf16[512,256]{1,0:T(8,128)(2,1)S(1)}, bf16[512,256]{1,0:T(8,128)(2,1)S(1)}, u32[]{:S(2)}, u32[]{:S(2)}) collective-permute-start(bf16[512,256]{1,0:T(8,128)(2,1)S(1)} %get-tuple-element.57), channel_id=1, source_target_pairs={{0,96},{32,64},{64,32},{96,0},{1,97},{33,65},{65,33},{97,1},{2,98}... | collective-permute-start | bytes 786440 | tf_op jit(solution)/shard_map/ppermute | solution.py:32
  12.7 3.5 %collective-permute-done.2 = bf16[320,256]{1,0:T(8,128)(2,1)S(1)} collective-permute-done((bf16[320,256]{1,0:T(8,128)(2,1)S(1)}, bf16[320,256]{1,0:T(8,128)(2,1)S(1)}, u32[]{:S(2)}, u32[]{:S(2)}) %collective-permute-start.2) | collective-permute-done | bytes 163872 | tf_op jit(solution)/shard_map/ppermute | solution.py:44
  16.3 1.3 %collective-permute-start.6 = (bf16[1024,256]{1,0:T(8,128)(2,1)S(1)}, bf16[1024,256]{1,0:T(8,128)(2,1)S(1)}, u32[]{:S(2)}, u32[]{:S(2)}) collective-permute-start(bf16[1024,256]{1,0:T(8,128)(2,1)S(1)} %pad_maximum_fusion.1.refs_1_), channel_id=1, source_target_pairs={{0,64},{64,32},{32,96},{96,0},{1,65},{65,33},{33,97},{97,1},{2,66}... | collective-permute-start | bytes 1572872 | tf_op jit(solution)/shard_map/ppermute | solution.py:40
  17.5 1.5 %collective-permute-start.7 = (bf16[1024,256]{1,0:T(8,128)(2,1)S(1)}, bf16[1024,256]{1,0:T(8,128)(2,1)S(1)}, u32[]{:S(2)}, u32[]{:S(2)}) collective-permute-start(bf16[1024,256]{1,0:T(8,128)(2,1)S(1)} %pad_maximum_fusion.1.refs_1_), channel_id=1, source_target_pairs={{0,96},{64,0},{32,64},{96,32},{1,97},{65,1},{33,65},{97,33},{2,98}... | collective-permute-start | bytes 1572872 | tf_op jit(solution)/shard_map/ppermute | solution.py:40
  19.1 1.3 %collective-permute-start.4 = (bf16[1024,256]{1,0:T(8,128)(2,1)S(1)}, bf16[1024,256]{1,0:T(8,128)(2,1)S(1)}, u32[]{:S(2)}, u32[]{:S(2)}) collective-permute-start(bf16[1024,256]{1,0:T(8,128)(2,1)S(1)} %constant_dynamic-update-slice_fusion.refs_0_), channel_id=1, source_target_pairs={{0,8},{8,16},{16,24},{24,0},{1,9},{9,17},{17,25},{25,1},{2,10},{10... | collective-permute-start | bytes 1572872 | tf_op jit(solution)/shard_map/ppermute | solution.py:44
  20.4 1.5 %collective-permute-start.5 = (bf16[1024,256]{1,0:T(8,128)(2,1)S(1)}, bf16[1024,256]{1,0:T(8,128)(2,1)S(1)}, u32[]{:S(2)}, u32[]{:S(2)}) collective-permute-start(bf16[1024,256]{1,0:T(8,128)(2,1)S(1)} %constant_dynamic-update-slice_fusion.refs_0_), channel_id=1, source_target_pairs={{0,24},{8,0},{16,8},{24,16},{1,25},{9,1},{17,9},{25,17},{2,26},{10... | collective-permute-start | bytes 1572872 | tf_op jit(solution)/shard_map/ppermute | solution.py:44
  21.9 1.6 %collective-permute-start.8 = (bf16[256,256]{1,0:T(8,128)(2,1)S(1)}, bf16[256,256]{1,0:T(8,128)(2,1)S(1)}, u32[]{:S(2)}, u32[]{:S(2)}) collective-permute-start(bf16[256,256]{1,0:T(8,128)(2,1)S(1)} %pad_maximum_fusion.2), channel_id=1, source_target_pairs={{0,32},{32,0},{1,33},{33,1},{2,34},{34,2},{3,35},{35,3},{4,36},{36... | collective-permute-start | bytes 393224 | tf_op jit(solution)/shard_map/ppermute | solution.py:48
  23.5 8.5 %attend.1 = bf16[48,16,128]{2,1,0:T(8,128)(2,1)S(1)} custom-call(s32[48]{0:T(128)S(1)} %copy-done.5, bf16[48,16,128]{2,1,0:T(8,128)(2,1)S(1)} %bitcast.33, bf16[48,128,2,256]{3,2,1,0:T(2,128)(2,1)} %kv_ref.1, bf16[48,2,256]{2,1,0:T(2,128)(2,1)S(1)} %copy-done.4), custom_call_target="tpu_custom_call" | custom-call | tf_op jit(solution)/shard_map/attend/pallas_call | solution.py:146
  32.1 0.8 collective-permute-done.8
  33.2 2.8 %collective-permute-start.11 = (bf16[6144,256]{1,0:T(8,128)(2,1)S(1)}, bf16[6144,256]{1,0:T(8,128)(2,1)S(1)}, u32[]{:S(2)}, u32[]{:S(2)}) collective-permute-start(bf16[6144,256]{1,0:T(8,128)(2,1)S(1)} %constant_dynamic-update-slice_fusion.7), channel_id=1, source_target_pairs={{0,4},{4,0},{1,5},{5,1},{2,6},{6,2},{3,7},{7,3},{8,12},{12,8},{9,1... | collective-permute-start | bytes 9437192 | tf_op jit(solution)/shard_map/ppermute | solution.py:60
  36.1 0.8 collective-permute-start.10
  37.0 1.9 %collective-permute-start.9 = (bf16[1024,256]{1,0:T(8,128)(2,1)S(1)}, bf16[1024,256]{1,0:T(8,128)(2,1)S(1)}, u32[]{:S(2)}, u32[]{:S(2)}) collective-permute-start(bf16[1024,256]{1,0:T(8,128)(2,1)S(1)} %constant_dynamic-update-slice_fusion.refs_0_), channel_id=1, source_target_pairs={{0,16},{8,24},{16,0},{24,8},{1,17},{9,25},{17,1},{25,9},{2,18},{10... | collective-permute-start | bytes 1572872 | tf_op jit(solution)/shard_map/ppermute | solution.py:44
  38.9 2.8 %collective-permute-done.13.other_ref = bf16[512,256]{1,0:T(8,128)(2,1)S(1)} collective-permute-done((bf16[512,256]{1,0:T(8,128)(2,1)S(1)}, bf16[512,256]{1,0:T(8,128)(2,1)S(1)}, u32[]{:S(2)}, u32[]{:S(2)}) %collective-permute-start.13) | collective-permute-done | bytes 262176 | tf_op jit(solution)/shard_map/ppermute | solution.py:60
  41.7 1.3 %low_rank.1 = f32[32,128]{1,0:T(8,128)S(1)} custom-call(s32[17]{0:T(128)S(1)} %concatenate.32.info, bf16[512,8192]{1,0:T(8,128)(2,1)S(1)} %bitcast.28, bf16[512,256]{1,0:T(8,128)(2,1)S(1)} %constant_dynamic-update-slice_fusion.2.own_ref, bf16[512,256]{1,0:T(8,128)(2,1)S(1)} %collective-permute-done.13.other_ref), custom_call_target="tpu_custom_call" | custom-call | tf_op jit(solution)/shard_map/low_rank/pallas_call | solution.py:199
  43.1 1.7 %collective-permute-start.14 = (f32[32,128]{1,0:T(8,128)S(1)}, f32[32,128]{1,0:T(8,128)S(1)}, u32[]{:S(2)}, u32[]{:S(2)}) collective-permute-start(f32[32,128]{1,0:T(8,128)S(1)} %low_rank.1), channel_id=1, source_target_pairs={{0,1},{1,0},{2,3},{3,2},{4,5},{5,4},{6,7},{7,6},{8,9},{9,8},{10,11... | collective-permute-start | bytes 49160 | tf_op jit(solution)/shard_map/ppermute | solution.py:56
  44.8 0.8 collective-permute-start.12
  46.2 3.4 %collective-permute-start.15 = (f32[64,128]{1,0:T(8,128)S(1)}, f32[64,128]{1,0:T(8,128)S(1)}, u32[]{:S(2)}, u32[]{:S(2)}) collective-permute-start(f32[64,128]{1,0:T(8,128)S(1)} %pad_maximum_fusion.4), channel_id=1, source_target_pairs={{0,2},{1,3},{2,0},{3,1},{4,6},{5,7},{6,4},{7,5},{8,10},{9,11},{10,... | collective-permute-start | bytes 98312 | tf_op jit(solution)/shard_map/ppermute | solution.py:56
  49.6 2.4 %main_product.2 = (f32[512,256]{1,0:T(8,128)S(1)}, f32[512,256]{1,0:T(8,128)S(1)}) custom-call(s32[17]{0:T(128)S(1)} %concatenate.32.info, bf16[512,8192]{1,0:T(8,128)(2,1)S(1)} %bitcast.29, bf16[1024,256]{1,0:T(8,128)(2,1)S(1)} %constant_dynamic-update-slice_fusion.refs_0_, bf16[1024,256]{1,0:T(8,128)(2,1)S(1)} %pad_maximum_fusion.1.refs_1_, ...), custom_call_target="tpu_custom_call" | custom-call | tf_op jit(solution)/shard_map/main_product/pallas_call | solution.py:242
  52.1 2.3 %main_product.3 = (f32[512,256]{1,0:T(8,128)S(1)}, f32[512,256]{1,0:T(8,128)S(1)}) custom-call(s32[17]{0:T(128)S(1)} %concatenate.32.info, bf16[512,8192]{1,0:T(8,128)(2,1)S(1)} %bitcast.30, bf16[6144,256]{1,0:T(8,128)(2,1)S(1)} %collective-permute-done.11.refs_0_), custom_call_target="tpu_custom_call" | custom-call | tf_op jit(solution)/shard_map/main_product/pallas_call | solution.py:242
  55.0 1.3 %collective-permute-start.16 = (bf16[1024,256]{1,0:T(8,128)(2,1)S(1)}, bf16[1024,256]{1,0:T(8,128)(2,1)S(1)}, u32[]{:S(2)}, u32[]{:S(2)}) collective-permute-start(bf16[1024,256]{1,0:T(8,128)(2,1)S(1)} %collective-permute-done.9.refs_0_), channel_id=1, source_target_pairs={{0,4},{4,0},{1,5},{5,1},{2,6},{6,2},{3,7},{7,3},{8,12},{12,8},{9,1... | collective-permute-start | bytes 1572872 | tf_op jit(solution)/shard_map/ppermute | solution.py:60
  56.3 1.5 %collective-permute-start.20 = (bf16[96,2048]{1,0:T(8,128)(2,1)S(1)}, bf16[96,2048]{1,0:T(8,128)(2,1)S(1)}, u32[]{:S(2)}, u32[]{:S(2)}) collective-permute-start(bf16[96,2048]{1,0:T(8,128)(2,1)S(1)} %constant_dynamic-update-slice_fusion.13), channel_id=1, source_target_pairs={{0,8},{8,16},{16,24},{24,0},{1,9},{9,17},{17,25},{25,1},{2,10},{10... | collective-permute-start | bytes 1179656 | tf_op jit(solution)/shard_map/ppermute | solution.py:44
  57.8 2.2 %collective-permute-start.21 = (bf16[96,2048]{1,0:T(8,128)(2,1)S(1)}, bf16[96,2048]{1,0:T(8,128)(2,1)S(1)}, u32[]{:S(2)}, u32[]{:S(2)}) collective-permute-start(bf16[96,2048]{1,0:T(8,128)(2,1)S(1)} %constant_dynamic-update-slice_fusion.13), channel_id=1, source_target_pairs={{0,16},{8,24},{16,0},{24,8},{1,17},{9,25},{17,1},{25,9},{2,18},{10... | collective-permute-start | bytes 1179656 | tf_op jit(solution)/shard_map/ppermute | solution.py:44
  60.7 3.7 %finish.1 = (bf16[3,128,2,256]{3,2,1,0:T(2,128)(2,1)S(1)}, bf16[3,128,2,256]{3,2,1,0:T(2,128)(2,1)S(1)}) custom-call(s32[17]{0:T(128)S(1)} %concatenate.32.info, bf16[512,8192]{1,0:T(8,128)(2,1)S(1)} %bitcast.31, bf16[1024,256]{1,0:T(8,128)(2,1)S(1)} %collective-permute-done.9.refs_0_, bf16[1024,256]{1,0:T(8,128)(2,1)S(1)} %collective-permute-done.10.refs_1_, ...), custom_call_target="tpu_custom_call" | custom-call | tf_op jit(solution)/shard_map/finish/pallas_call | solution.py:293
  64.4 1.0 collective-permute-start.18
  65.4 0.9 collective-permute-start.19
  66.3 1.8 %collective-permute-done.20 = bf16[96,2048]{1,0:T(8,128)(2,1)S(1)} collective-permute-done((bf16[96,2048]{1,0:T(8,128)(2,1)S(1)}, bf16[96,2048]{1,0:T(8,128)(2,1)S(1)}, u32[]{:S(2)}, u32[]{:S(2)}) %collective-permute-start.20) | collective-permute-done | bytes 393248 | tf_op jit(solution)/shard_map/ppermute | solution.py:44
  68.1 9.2 %collective-permute-done.21 = bf16[96,2048]{1,0:T(8,128)(2,1)S(1)} collective-permute-done((bf16[96,2048]{1,0:T(8,128)(2,1)S(1)}, bf16[96,2048]{1,0:T(8,128)(2,1)S(1)}, u32[]{:S(2)}, u32[]{:S(2)}) %collective-permute-start.21) | collective-permute-done | bytes 393248 | tf_op jit(solution)/shard_map/ppermute | solution.py:44
  77.4 1.3 %collective-permute-start.25 = (bf16[384,2048]{1,0:T(8,128)(2,1)S(1)}, bf16[384,2048]{1,0:T(8,128)(2,1)S(1)}, u32[]{:S(2)}, u32[]{:S(2)}) collective-permute-start(bf16[384,2048]{1,0:T(8,128)(2,1)S(1)} %constant_dynamic-update-slice_fusion.15.refs_0_), channel_id=1, source_target_pairs={{0,4},{4,0},{1,5},{5,1},{2,6},{6,2},{3,7},{7,3},{8,12},{12,8},{9,1... | collective-permute-start | bytes 4718600 | tf_op jit(solution)/shard_map/ppermute | solution.py:60
  78.8 1.1 pad_maximum_fusion.refs_0_
  80.0 1.3 %collective-permute-start.23 = (bf16[2,3,128,2,256]{4,3,2,1,0:T(2,128)(2,1)S(1)}, bf16[2,3,128,2,256]{4,3,2,1,0:T(2,128)(2,1)S(1)}, u32[]{:S(2)}, u32[]{:S(2)}) collective-permute-start(bf16[2,3,128,2,256]{4,3,2,1,0:T(2,128)(2,1)S(1)} %pad_maximum_fusion.refs_0_), channel_id=1, source_target_pairs={{0,8},{8,16},{16,24},{24,0},{1,9},{9,17},{17,25},{25,1},{2,10},{10... | collective-permute-start | bytes 2359304 | tf_op jit(solution)/shard_map/ppermute | solution.py:44
  81.2 1.5 %collective-permute-start.24 = (bf16[2,3,128,2,256]{4,3,2,1,0:T(2,128)(2,1)S(1)}, bf16[2,3,128,2,256]{4,3,2,1,0:T(2,128)(2,1)S(1)}, u32[]{:S(2)}, u32[]{:S(2)}) collective-permute-start(bf16[2,3,128,2,256]{4,3,2,1,0:T(2,128)(2,1)S(1)} %pad_maximum_fusion.refs_0_), channel_id=1, source_target_pairs={{0,24},{8,0},{16,8},{24,16},{1,25},{9,1},{17,9},{25,17},{2,26},{10... | collective-permute-start | bytes 2359304 | tf_op jit(solution)/shard_map/ppermute | solution.py:44
  82.9 5.2 %project.1 = (bf16[192,512]{1,0:T(8,128)(2,1)S(1)}, bf16[192,512]{1,0:T(8,128)(2,1)S(1)}, bf16[192,512]{1,0:T(8,128)(2,1)S(1)}, bf16[192,512]{1,0:T(8,128)(2,1)S(1)}) custom-call(s32[17]{0:T(128)S(1)} %concatenate.32.info, s32[768,1]{1,0:T(8,128)S(1)} %broadcast_in_dim.20.keep, bf16[128,2048]{1,0:T(8,128)(2,1)S(1)} %bitcast.34, ...), custom_call_target="tpu_custom_call" | custom-call | tf_op jit(solution)/shard_map/project/pallas_call | solution.py:410
  88.1 1.7 %collective-permute-start.27 = (bf16[192,512]{1,0:T(8,128)(2,1)S(1)}, bf16[192,512]{1,0:T(8,128)(2,1)S(1)}, u32[]{:S(2)}, u32[]{:S(2)}) collective-permute-start(bf16[192,512]{1,0:T(8,128)(2,1)S(1)} %get-tuple-element.94), channel_id=1, source_target_pairs={{0,1},{1,2},{2,3},{3,0},{4,5},{5,6},{6,7},{7,4},{8,9},{9,10},{10,1... | collective-permute-start | bytes 589832 | tf_op jit(solution)/shard_map/ppermute | solution.py:52
  89.8 2.2 %collective-permute-start.28 = (bf16[192,512]{1,0:T(8,128)(2,1)S(1)}, bf16[192,512]{1,0:T(8,128)(2,1)S(1)}, u32[]{:S(2)}, u32[]{:S(2)}) collective-permute-start(bf16[192,512]{1,0:T(8,128)(2,1)S(1)} %get-tuple-element.95), channel_id=1, source_target_pairs={{0,3},{1,0},{2,1},{3,2},{4,7},{5,4},{6,5},{7,6},{8,11},{9,8},{10,9... | collective-permute-start | bytes 589832 | tf_op jit(solution)/shard_map/ppermute | solution.py:52
  92.0 1.2 %collective-permute-start.33 = (bf16[192,512]{1,0:T(8,128)(2,1)S(1)}, bf16[192,512]{1,0:T(8,128)(2,1)S(1)}, u32[]{:S(2)}, u32[]{:S(2)}) collective-permute-start(bf16[192,512]{1,0:T(8,128)(2,1)S(1)} %get-tuple-element.101), channel_id=1, source_target_pairs={{0,2},{1,3},{2,0},{3,1},{4,6},{5,7},{6,4},{7,5},{8,10},{9,11},{10,... | collective-permute-start | bytes 589832 | tf_op jit(solution)/shard_map/ppermute | solution.py:52
  93.2 6.7 %collective-permute-done.23.refs_1_ = bf16[2,3,128,2,256]{4,3,2,1,0:T(2,128)(2,1)S(1)} collective-permute-done((bf16[2,3,128,2,256]{4,3,2,1,0:T(2,128)(2,1)S(1)}, bf16[2,3,128,2,256]{4,3,2,1,0:T(2,128)(2,1)S(1)}, u32[]{:S(2)}, u32[]{:S(2)}) %collective-permute-start.23) | collective-permute-done | bytes 786464 | tf_op jit(solution)/shard_map/ppermute | solution.py:44
  100.0 1.4 %collective-permute-start.31 = (bf16[2,3,128,2,256]{4,3,2,1,0:T(2,128)(2,1)S(1)}, bf16[2,3,128,2,256]{4,3,2,1,0:T(2,128)(2,1)S(1)}, u32[]{:S(2)}, u32[]{:S(2)}) collective-permute-start(bf16[2,3,128,2,256]{4,3,2,1,0:T(2,128)(2,1)S(1)} %collective-permute-done.23.refs_1_), channel_id=1, source_target_pairs={{0,4},{4,0},{1,5},{5,1},{2,6},{6,2},{3,7},{7,3},{8,12},{12,8},{9,1... | collective-permute-start | bytes 2359304 | tf_op jit(solution)/shard_map/ppermute | solution.py:60
  102.3 2.4 %collective-permute-start.30 = (bf16[3,128,2,256]{3,2,1,0:T(2,128)(2,1)S(1)}, bf16[3,128,2,256]{3,2,1,0:T(2,128)(2,1)S(1)}, u32[]{:S(2)}, u32[]{:S(2)}) collective-permute-start(bf16[3,128,2,256]{3,2,1,0:T(2,128)(2,1)S(1)} %slice_bitcast_fusion), channel_id=1, source_target_pairs={{0,24},{8,0},{16,8},{24,16},{1,25},{9,1},{17,9},{25,17},{2,26},{10... | collective-permute-start | bytes 1179656 | tf_op jit(solution)/shard_map/ppermute | solution.py:44
  104.7 0.8 add_convert_fusion
  105.5 7.9 %collective-permute-done.29 = bf16[3,128,2,256]{3,2,1,0:T(2,128)(2,1)S(1)} collective-permute-done((bf16[3,128,2,256]{3,2,1,0:T(2,128)(2,1)S(1)}, bf16[3,128,2,256]{3,2,1,0:T(2,128)(2,1)S(1)}, u32[]{:S(2)}, u32[]{:S(2)}) %collective-permute-start.29) | collective-permute-done | bytes 393248 | tf_op jit(solution)/shard_map/ppermute | solution.py:44
  113.4 1.4 %collective-permute-start.34 = (bf16[3,128,2,256]{3,2,1,0:T(2,128)(2,1)S(1)}, bf16[3,128,2,256]{3,2,1,0:T(2,128)(2,1)S(1)}, u32[]{:S(2)}, u32[]{:S(2)}) collective-permute-start(bf16[3,128,2,256]{3,2,1,0:T(2,128)(2,1)S(1)} %collective-permute-done.29), channel_id=1, source_target_pairs={{0,4},{4,0},{1,5},{5,1},{2,6},{6,2},{3,7},{7,3},{8,12},{12,8},{9,1... | collective-permute-start | bytes 1179656 | tf_op jit(solution)/shard_map/ppermute | solution.py:60
  114.9 2.9 %place.2.refs_4_ = bf16[1,2,2048,2,256]{4,3,2,1,0:T(2,128)(2,1)} custom-call(s32[17]{0:T(128)S(1)} %concatenate.32.info, bf16[2,3,128,2,256]{4,3,2,1,0:T(2,128)(2,1)S(1)} %pad_maximum_fusion.refs_0_, bf16[2,3,128,2,256]{4,3,2,1,0:T(2,128)(2,1)S(1)} %collective-permute-done.23.refs_1_, bf16[2,3,128,2,256]{4,3,2,1,0:T(2,128)(2,1)S(1)} %collective-permute-done.24.refs_2_, ...), custom_call_target="tpu_custom_call" | custom-call | tf_op jit(solution)/shard_map/place/pallas_call | solution.py:368
  117.8 0.9 place.3
  (89 shorter events, 4.0 us)
Async XLA Ops:
  0.6 22.9 %copy-start.5 = (s32[48]{0:T(128)S(1)}, s32[48]{0:T(128)}, u32[]{:S(2)}) copy-start(s32[48]{0:T(128)} %len_ref) | copy-start | bytes 580
  0.6 22.8 %copy-start.6 = (bf16[48,2048]{1,0:T(8,128)(2,1)S(1)}, bf16[48,2048]{1,0:T(8,128)(2,1)}, u32[]{:S(2)}) copy-start(bf16[48,2048]{1,0:T(8,128)(2,1)} %param.20) | copy-start | bytes 589828
  0.7 22.9 %copy-start.4 = (bf16[48,2,256]{2,1,0:T(2,128)(2,1)S(1)}, bf16[48,2,256]{2,1,0:T(2,128)(2,1)}, u32[]{:S(2)}) copy-start(bf16[48,2,256]{2,1,0:T(2,128)(2,1)} %cur_ref.1) | copy-start | bytes 147460
  4.2 8.4 %collective-permute-start.1 = (bf16[320,256]{1,0:T(8,128)(2,1)S(1)}, bf16[320,256]{1,0:T(8,128)(2,1)S(1)}, u32[]{:S(2)}, u32[]{:S(2)}) collective-permute-start(bf16[320,256]{1,0:T(8,128)(2,1)S(1)} %get-tuple-element.59), channel_id=1, source_target_pairs={{0,8},{8,16},{16,24},{24,0},{1,9},{9,17},{17,25},{25,1},{2,10},{10... | collective-permute-start | bytes 491528 | tf_op jit(solution)/shard_map/ppermute | solution.py:44
  6.4 9.7 %collective-permute-start.2 = (bf16[320,256]{1,0:T(8,128)(2,1)S(1)}, bf16[320,256]{1,0:T(8,128)(2,1)S(1)}, u32[]{:S(2)}, u32[]{:S(2)}) collective-permute-start(bf16[320,256]{1,0:T(8,128)(2,1)S(1)} %get-tuple-element.59), channel_id=1, source_target_pairs={{0,16},{8,24},{16,0},{24,8},{1,17},{9,25},{17,1},{25,9},{2,18},{10... | collective-permute-start | bytes 491528 | tf_op jit(solution)/shard_map/ppermute | solution.py:44
  9.1 7.1 %collective-permute-start.3 = (bf16[320,256]{1,0:T(8,128)(2,1)S(1)}, bf16[320,256]{1,0:T(8,128)(2,1)S(1)}, u32[]{:S(2)}, u32[]{:S(2)}) collective-permute-start(bf16[320,256]{1,0:T(8,128)(2,1)S(1)} %get-tuple-element.59), channel_id=1, source_target_pairs={{0,24},{8,0},{16,8},{24,16},{1,25},{9,1},{17,9},{25,17},{2,26},{10... | collective-permute-start | bytes 491528 | tf_op jit(solution)/shard_map/ppermute | solution.py:44
  10.1 8.9 %collective-permute-start = (bf16[512,256]{1,0:T(8,128)(2,1)S(1)}, bf16[512,256]{1,0:T(8,128)(2,1)S(1)}, u32[]{:S(2)}, u32[]{:S(2)}) collective-permute-start(bf16[512,256]{1,0:T(8,128)(2,1)S(1)} %get-tuple-element.57), channel_id=1, source_target_pairs={{0,96},{32,64},{64,32},{96,0},{1,97},{33,65},{65,33},{97,1},{2,98}... | collective-permute-start | bytes 786440 | tf_op jit(solution)/shard_map/ppermute | solution.py:32
  16.3 16.7 %collective-permute-start.6 = (bf16[1024,256]{1,0:T(8,128)(2,1)S(1)}, bf16[1024,256]{1,0:T(8,128)(2,1)S(1)}, u32[]{:S(2)}, u32[]{:S(2)}) collective-permute-start(bf16[1024,256]{1,0:T(8,128)(2,1)S(1)} %pad_maximum_fusion.1.refs_1_), channel_id=1, source_target_pairs={{0,64},{64,32},{32,96},{96,0},{1,65},{65,33},{33,97},{97,1},{2,66}... | collective-permute-start | bytes 1572872 | tf_op jit(solution)/shard_map/ppermute | solution.py:40
  17.5 15.4 %collective-permute-start.7 = (bf16[1024,256]{1,0:T(8,128)(2,1)S(1)}, bf16[1024,256]{1,0:T(8,128)(2,1)S(1)}, u32[]{:S(2)}, u32[]{:S(2)}) collective-permute-start(bf16[1024,256]{1,0:T(8,128)(2,1)S(1)} %pad_maximum_fusion.1.refs_1_), channel_id=1, source_target_pairs={{0,96},{64,0},{32,64},{96,32},{1,97},{65,1},{33,65},{97,33},{2,98}... | collective-permute-start | bytes 1572872 | tf_op jit(solution)/shard_map/ppermute | solution.py:40
  19.0 22.7 %slice-start = ((s8[8388608]{0:T(1024)(128)(4,1)}), s8[4194304]{0:T(1024)(128)(4,1)S(1)}, s32[]{:S(2)}) async-start(s8[8388608]{0:T(1024)(128)(4,1)} %bitcast.26), calls=%async_computation | async-start | bytes 8388608
  19.1 13.8 %collective-permute-start.4 = (bf16[1024,256]{1,0:T(8,128)(2,1)S(1)}, bf16[1024,256]{1,0:T(8,128)(2,1)S(1)}, u32[]{:S(2)}, u32[]{:S(2)}) collective-permute-start(bf16[1024,256]{1,0:T(8,128)(2,1)S(1)} %constant_dynamic-update-slice_fusion.refs_0_), channel_id=1, source_target_pairs={{0,8},{8,16},{16,24},{24,0},{1,9},{9,17},{17,25},{25,1},{2,10},{10... | collective-permute-start | bytes 1572872 | tf_op jit(solution)/shard_map/ppermute | solution.py:44
  20.4 12.6 %collective-permute-start.5 = (bf16[1024,256]{1,0:T(8,128)(2,1)S(1)}, bf16[1024,256]{1,0:T(8,128)(2,1)S(1)}, u32[]{:S(2)}, u32[]{:S(2)}) collective-permute-start(bf16[1024,256]{1,0:T(8,128)(2,1)S(1)} %constant_dynamic-update-slice_fusion.refs_0_), channel_id=1, source_target_pairs={{0,24},{8,0},{16,8},{24,16},{1,25},{9,1},{17,9},{25,17},{2,26},{10... | collective-permute-start | bytes 1572872 | tf_op jit(solution)/shard_map/ppermute | solution.py:44
  21.9 11.0 %collective-permute-start.8 = (bf16[256,256]{1,0:T(8,128)(2,1)S(1)}, bf16[256,256]{1,0:T(8,128)(2,1)S(1)}, u32[]{:S(2)}, u32[]{:S(2)}) collective-permute-start(bf16[256,256]{1,0:T(8,128)(2,1)S(1)} %pad_maximum_fusion.2), channel_id=1, source_target_pairs={{0,32},{32,0},{1,33},{33,1},{2,34},{34,2},{3,35},{35,3},{4,36},{36... | collective-permute-start | bytes 393224 | tf_op jit(solution)/shard_map/ppermute | solution.py:48
  23.5 18.2 %slice-start.1 = ((s8[8388608]{0:T(1024)(128)(4,1)}), s8[4194304]{0:T(1024)(128)(4,1)S(1)}, s32[]{:S(2)}) async-start(s8[8388608]{0:T(1024)(128)(4,1)} %bitcast.26), calls=%async_computation.1 | async-start | bytes 8388608
  33.2 18.9 %collective-permute-start.11 = (bf16[6144,256]{1,0:T(8,128)(2,1)S(1)}, bf16[6144,256]{1,0:T(8,128)(2,1)S(1)}, u32[]{:S(2)}, u32[]{:S(2)}) collective-permute-start(bf16[6144,256]{1,0:T(8,128)(2,1)S(1)} %constant_dynamic-update-slice_fusion.7), channel_id=1, source_target_pairs={{0,4},{4,0},{1,5},{5,1},{2,6},{6,2},{3,7},{7,3},{8,12},{12,8},{9,1... | collective-permute-start | bytes 9437192 | tf_op jit(solution)/shard_map/ppermute | solution.py:60
  36.1 5.7 %collective-permute-start.13 = (bf16[512,256]{1,0:T(8,128)(2,1)S(1)}, bf16[512,256]{1,0:T(8,128)(2,1)S(1)}, u32[]{:S(2)}, u32[]{:S(2)}) collective-permute-start(bf16[512,256]{1,0:T(8,128)(2,1)S(1)} %constant_dynamic-update-slice_fusion.2.own_ref), channel_id=1, source_target_pairs={{0,4},{4,0},{1,5},{5,1},{2,6},{6,2},{3,7},{7,3},{8,12},{12,8},{9,1... | collective-permute-start | bytes 786440 | tf_op jit(solution)/shard_map/ppermute | solution.py:60
  36.1 18.8 %collective-permute-start.10 = (bf16[1024,256]{1,0:T(8,128)(2,1)S(1)}, bf16[1024,256]{1,0:T(8,128)(2,1)S(1)}, u32[]{:S(2)}, u32[]{:S(2)}) collective-permute-start(bf16[1024,256]{1,0:T(8,128)(2,1)S(1)} %pad_maximum_fusion.1.refs_1_), channel_id=1, source_target_pairs={{0,32},{64,96},{32,0},{96,64},{1,33},{65,97},{33,1},{97,65},{2,34}... | collective-permute-start | bytes 1572872 | tf_op jit(solution)/shard_map/ppermute | solution.py:40
  37.0 18.0 %collective-permute-start.9 = (bf16[1024,256]{1,0:T(8,128)(2,1)S(1)}, bf16[1024,256]{1,0:T(8,128)(2,1)S(1)}, u32[]{:S(2)}, u32[]{:S(2)}) collective-permute-start(bf16[1024,256]{1,0:T(8,128)(2,1)S(1)} %constant_dynamic-update-slice_fusion.refs_0_), channel_id=1, source_target_pairs={{0,16},{8,24},{16,0},{24,8},{1,17},{9,25},{17,1},{25,9},{2,18},{10... | collective-permute-start | bytes 1572872 | tf_op jit(solution)/shard_map/ppermute | solution.py:44
  43.1 3.2 %collective-permute-start.14 = (f32[32,128]{1,0:T(8,128)S(1)}, f32[32,128]{1,0:T(8,128)S(1)}, u32[]{:S(2)}, u32[]{:S(2)}) collective-permute-start(f32[32,128]{1,0:T(8,128)S(1)} %low_rank.1), channel_id=1, source_target_pairs={{0,1},{1,0},{2,3},{3,2},{4,5},{5,4},{6,7},{7,6},{8,9},{9,8},{10,11... | collective-permute-start | bytes 49160 | tf_op jit(solution)/shard_map/ppermute | solution.py:56
  44.8 10.2 %collective-permute-start.12 = (bf16[48,2048]{1,0:T(8,128)(2,1)S(1)}, bf16[48,2048]{1,0:T(8,128)(2,1)S(1)}, u32[]{:S(2)}, u32[]{:S(2)}) collective-permute-start(bf16[48,2048]{1,0:T(8,128)(2,1)S(1)} %bitcast.40), channel_id=1, source_target_pairs={{0,32},{32,0},{1,33},{33,1},{2,34},{34,2},{3,35},{35,3},{4,36},{36... | collective-permute-start | bytes 589832 | tf_op jit(solution)/shard_map/ppermute | solution.py:48
  46.2 5.8 %collective-permute-start.15 = (f32[64,128]{1,0:T(8,128)S(1)}, f32[64,128]{1,0:T(8,128)S(1)}, u32[]{:S(2)}, u32[]{:S(2)}) collective-permute-start(f32[64,128]{1,0:T(8,128)S(1)} %pad_maximum_fusion.4), channel_id=1, source_target_pairs={{0,2},{1,3},{2,0},{3,1},{4,6},{5,7},{6,4},{7,5},{8,10},{9,11},{10,... | collective-permute-start | bytes 98312 | tf_op jit(solution)/shard_map/ppermute | solution.py:56
  52.0 8.6 %copy-start.2 = (bf16[8,2,16,256]{3,2,1,0:T(8,128)(2,1)S(1)}, bf16[8,2,16,256]{3,2,1,0:T(8,128)(2,1)}, u32[]{:S(2)}) copy-start(bf16[8,2,16,256]{3,2,1,0:T(8,128)(2,1)} %refs_9_.1) | copy-start | bytes 393220
  55.0 5.7 %collective-permute-start.16 = (bf16[1024,256]{1,0:T(8,128)(2,1)S(1)}, bf16[1024,256]{1,0:T(8,128)(2,1)S(1)}, u32[]{:S(2)}, u32[]{:S(2)}) collective-permute-start(bf16[1024,256]{1,0:T(8,128)(2,1)S(1)} %collective-permute-done.9.refs_0_), channel_id=1, source_target_pairs={{0,4},{4,0},{1,5},{5,1},{2,6},{6,2},{3,7},{7,3},{8,12},{12,8},{9,1... | collective-permute-start | bytes 1572872 | tf_op jit(solution)/shard_map/ppermute | solution.py:60
  56.2 4.5 %collective-permute-start.17 = (bf16[1024,256]{1,0:T(8,128)(2,1)S(1)}, bf16[1024,256]{1,0:T(8,128)(2,1)S(1)}, u32[]{:S(2)}, u32[]{:S(2)}) collective-permute-start(bf16[1024,256]{1,0:T(8,128)(2,1)S(1)} %collective-permute-done.10.refs_1_), channel_id=1, source_target_pairs={{0,4},{4,0},{1,5},{5,1},{2,6},{6,2},{3,7},{7,3},{8,12},{12,8},{9,1... | collective-permute-start | bytes 1572872 | tf_op jit(solution)/shard_map/ppermute | solution.py:60
  56.3 11.7 %collective-permute-start.20 = (bf16[96,2048]{1,0:T(8,128)(2,1)S(1)}, bf16[96,2048]{1,0:T(8,128)(2,1)S(1)}, u32[]{:S(2)}, u32[]{:S(2)}) collective-permute-start(bf16[96,2048]{1,0:T(8,128)(2,1)S(1)} %constant_dynamic-update-slice_fusion.13), channel_id=1, source_target_pairs={{0,8},{8,16},{16,24},{24,0},{1,9},{9,17},{17,25},{25,1},{2,10},{10... | collective-permute-start | bytes 1179656 | tf_op jit(solution)/shard_map/ppermute | solution.py:44
  57.8 19.4 %collective-permute-start.21 = (bf16[96,2048]{1,0:T(8,128)(2,1)S(1)}, bf16[96,2048]{1,0:T(8,128)(2,1)S(1)}, u32[]{:S(2)}, u32[]{:S(2)}) collective-permute-start(bf16[96,2048]{1,0:T(8,128)(2,1)S(1)} %constant_dynamic-update-slice_fusion.13), channel_id=1, source_target_pairs={{0,16},{8,24},{16,0},{24,8},{1,17},{9,25},{17,1},{25,9},{2,18},{10... | collective-permute-start | bytes 1179656 | tf_op jit(solution)/shard_map/ppermute | solution.py:44
  60.0 17.2 %collective-permute-start.22 = (bf16[96,2048]{1,0:T(8,128)(2,1)S(1)}, bf16[96,2048]{1,0:T(8,128)(2,1)S(1)}, u32[]{:S(2)}, u32[]{:S(2)}) collective-permute-start(bf16[96,2048]{1,0:T(8,128)(2,1)S(1)} %constant_dynamic-update-slice_fusion.13), channel_id=1, source_target_pairs={{0,24},{8,0},{16,8},{24,16},{1,25},{9,1},{17,9},{25,17},{2,26},{10... | collective-permute-start | bytes 1179656 | tf_op jit(solution)/shard_map/ppermute | solution.py:44
  64.4 18.4 %copy-start.7 = (s32[768]{0:T(1024)S(1)}, s32[768]{0:T(1024)}, u32[]{:S(2)}) copy-start(s32[768]{0:T(1024)} %param.24) | copy-start | bytes 9220
  64.4 18.5 %copy-start = (bf16[2048,512]{1,0:T(8,128)(2,1)S(1)}, bf16[2048,512]{1,0:T(8,128)(2,1)}, u32[]{:S(2)}) copy-start(bf16[2048,512]{1,0:T(8,128)(2,1)} %w_ref.1) | copy-start | bytes 6291460
  64.4 18.5 %copy-start.1 = (bf16[2048,8,16]{0,2,1:T(8,128)(2,1)S(1)}, bf16[2048,8,16]{0,2,1:T(8,128)(2,1)}, u32[]{:S(2)}) copy-start(bf16[2048,8,16]{0,2,1:T(8,128)(2,1)} %param.26) | copy-start | bytes 1572868
  64.4 18.5 %copy-start.3 = (bf16[8,16,512]{2,1,0:T(8,128)(2,1)S(1)}, bf16[8,16,512]{2,1,0:T(8,128)(2,1)}, u32[]{:S(2)}) copy-start(bf16[8,16,512]{2,1,0:T(8,128)(2,1)} %param.27) | copy-start | bytes 393220
  64.4 12.9 %collective-permute-start.18 = (bf16[3,128,2,256]{3,2,1,0:T(2,128)(2,1)S(1)}, bf16[3,128,2,256]{3,2,1,0:T(2,128)(2,1)S(1)}, u32[]{:S(2)}, u32[]{:S(2)}) collective-permute-start(bf16[3,128,2,256]{3,2,1,0:T(2,128)(2,1)S(1)} %get-tuple-element.80), channel_id=1, source_target_pairs={{0,64},{64,0},{1,65},{65,1},{2,66},{66,2},{3,67},{67,3},{4,68},{68... | collective-permute-start | bytes 1179656 | tf_op jit(solution)/shard_map/ppermute | solution.py:490
  65.4 11.9 %collective-permute-start.19 = (bf16[3,128,2,256]{3,2,1,0:T(2,128)(2,1)S(1)}, bf16[3,128,2,256]{3,2,1,0:T(2,128)(2,1)S(1)}, u32[]{:S(2)}, u32[]{:S(2)}) collective-permute-start(bf16[3,128,2,256]{3,2,1,0:T(2,128)(2,1)S(1)} %get-tuple-element.81), channel_id=1, source_target_pairs={{0,96},{32,64},{64,32},{96,0},{1,97},{33,65},{65,33},{97,1},{2,98}... | collective-permute-start | bytes 1179656 | tf_op jit(solution)/shard_map/ppermute | solution.py:32
  77.4 5.5 %collective-permute-start.25 = (bf16[384,2048]{1,0:T(8,128)(2,1)S(1)}, bf16[384,2048]{1,0:T(8,128)(2,1)S(1)}, u32[]{:S(2)}, u32[]{:S(2)}) collective-permute-start(bf16[384,2048]{1,0:T(8,128)(2,1)S(1)} %constant_dynamic-update-slice_fusion.15.refs_0_), channel_id=1, source_target_pairs={{0,4},{4,0},{1,5},{5,1},{2,6},{6,2},{3,7},{7,3},{8,12},{12,8},{9,1... | collective-permute-start | bytes 4718600 | tf_op jit(solution)/shard_map/ppermute | solution.py:60
  79.9 8.2 %collective-permute-start.26 = (bf16[2,3,128,2,256]{4,3,2,1,0:T(2,128)(2,1)S(1)}, bf16[2,3,128,2,256]{4,3,2,1,0:T(2,128)(2,1)S(1)}, u32[]{:S(2)}, u32[]{:S(2)}) collective-permute-start(bf16[2,3,128,2,256]{4,3,2,1,0:T(2,128)(2,1)S(1)} %pad_maximum_fusion.refs_0_), channel_id=1, source_target_pairs={{0,4},{4,0},{1,5},{5,1},{2,6},{6,2},{3,7},{7,3},{8,12},{12,8},{9,1... | collective-permute-start | bytes 2359304 | tf_op jit(solution)/shard_map/ppermute | solution.py:60
  80.0 20.0 %collective-permute-start.23 = (bf16[2,3,128,2,256]{4,3,2,1,0:T(2,128)(2,1)S(1)}, bf16[2,3,128,2,256]{4,3,2,1,0:T(2,128)(2,1)S(1)}, u32[]{:S(2)}, u32[]{:S(2)}) collective-permute-start(bf16[2,3,128,2,256]{4,3,2,1,0:T(2,128)(2,1)S(1)} %pad_maximum_fusion.refs_0_), channel_id=1, source_target_pairs={{0,8},{8,16},{16,24},{24,0},{1,9},{9,17},{17,25},{25,1},{2,10},{10... | collective-permute-start | bytes 2359304 | tf_op jit(solution)/shard_map/ppermute | solution.py:44
  81.2 18.7 %collective-permute-start.24 = (bf16[2,3,128,2,256]{4,3,2,1,0:T(2,128)(2,1)S(1)}, bf16[2,3,128,2,256]{4,3,2,1,0:T(2,128)(2,1)S(1)}, u32[]{:S(2)}, u32[]{:S(2)}) collective-permute-start(bf16[2,3,128,2,256]{4,3,2,1,0:T(2,128)(2,1)S(1)} %pad_maximum_fusion.refs_0_), channel_id=1, source_target_pairs={{0,24},{8,0},{16,8},{24,16},{1,25},{9,1},{17,9},{25,17},{2,26},{10... | collective-permute-start | bytes 2359304 | tf_op jit(solution)/shard_map/ppermute | solution.py:44
  88.1 11.9 %collective-permute-start.27 = (bf16[192,512]{1,0:T(8,128)(2,1)S(1)}, bf16[192,512]{1,0:T(8,128)(2,1)S(1)}, u32[]{:S(2)}, u32[]{:S(2)}) collective-permute-start(bf16[192,512]{1,0:T(8,128)(2,1)S(1)} %get-tuple-element.94), channel_id=1, source_target_pairs={{0,1},{1,2},{2,3},{3,0},{4,5},{5,6},{6,7},{7,4},{8,9},{9,10},{10,1... | collective-permute-start | bytes 589832 | tf_op jit(solution)/shard_map/ppermute | solution.py:52
  89.8 10.1 %collective-permute-start.28 = (bf16[192,512]{1,0:T(8,128)(2,1)S(1)}, bf16[192,512]{1,0:T(8,128)(2,1)S(1)}, u32[]{:S(2)}, u32[]{:S(2)}) collective-permute-start(bf16[192,512]{1,0:T(8,128)(2,1)S(1)} %get-tuple-element.95), channel_id=1, source_target_pairs={{0,3},{1,0},{2,1},{3,2},{4,7},{5,4},{6,5},{7,6},{8,11},{9,8},{10,9... | collective-permute-start | bytes 589832 | tf_op jit(solution)/shard_map/ppermute | solution.py:52
  92.0 12.7 %collective-permute-start.33 = (bf16[192,512]{1,0:T(8,128)(2,1)S(1)}, bf16[192,512]{1,0:T(8,128)(2,1)S(1)}, u32[]{:S(2)}, u32[]{:S(2)}) collective-permute-start(bf16[192,512]{1,0:T(8,128)(2,1)S(1)} %get-tuple-element.101), channel_id=1, source_target_pairs={{0,2},{1,3},{2,0},{3,1},{4,6},{5,7},{6,4},{7,5},{8,10},{9,11},{10,... | collective-permute-start | bytes 589832 | tf_op jit(solution)/shard_map/ppermute | solution.py:52
  100.0 13.5 %collective-permute-start.31 = (bf16[2,3,128,2,256]{4,3,2,1,0:T(2,128)(2,1)S(1)}, bf16[2,3,128,2,256]{4,3,2,1,0:T(2,128)(2,1)S(1)}, u32[]{:S(2)}, u32[]{:S(2)}) collective-permute-start(bf16[2,3,128,2,256]{4,3,2,1,0:T(2,128)(2,1)S(1)} %collective-permute-done.23.refs_1_), channel_id=1, source_target_pairs={{0,4},{4,0},{1,5},{5,1},{2,6},{6,2},{3,7},{7,3},{8,12},{12,8},{9,1... | collective-permute-start | bytes 2359304 | tf_op jit(solution)/shard_map/ppermute | solution.py:60
  101.4 12.1 %collective-permute-start.32 = (bf16[2,3,128,2,256]{4,3,2,1,0:T(2,128)(2,1)S(1)}, bf16[2,3,128,2,256]{4,3,2,1,0:T(2,128)(2,1)S(1)}, u32[]{:S(2)}, u32[]{:S(2)}) collective-permute-start(bf16[2,3,128,2,256]{4,3,2,1,0:T(2,128)(2,1)S(1)} %collective-permute-done.24.refs_2_), channel_id=1, source_target_pairs={{0,4},{4,0},{1,5},{5,1},{2,6},{6,2},{3,7},{7,3},{8,12},{12,8},{9,1... | collective-permute-start | bytes 2359304 | tf_op jit(solution)/shard_map/ppermute | solution.py:60
  101.9 11.5 %collective-permute-start.29 = (bf16[3,128,2,256]{3,2,1,0:T(2,128)(2,1)S(1)}, bf16[3,128,2,256]{3,2,1,0:T(2,128)(2,1)S(1)}, u32[]{:S(2)}, u32[]{:S(2)}) collective-permute-start(bf16[3,128,2,256]{3,2,1,0:T(2,128)(2,1)S(1)} %slice_bitcast_fusion.1), channel_id=1, source_target_pairs={{0,8},{8,16},{16,24},{24,0},{1,9},{9,17},{17,25},{25,1},{2,10},{10... | collective-permute-start | bytes 1179656 | tf_op jit(solution)/shard_map/ppermute | solution.py:44
  102.3 11.1 %collective-permute-start.30 = (bf16[3,128,2,256]{3,2,1,0:T(2,128)(2,1)S(1)}, bf16[3,128,2,256]{3,2,1,0:T(2,128)(2,1)S(1)}, u32[]{:S(2)}, u32[]{:S(2)}) collective-permute-start(bf16[3,128,2,256]{3,2,1,0:T(2,128)(2,1)S(1)} %slice_bitcast_fusion), channel_id=1, source_target_pairs={{0,24},{8,0},{16,8},{24,16},{1,25},{9,1},{17,9},{25,17},{2,26},{10... | collective-permute-start | bytes 1179656 | tf_op jit(solution)/shard_map/ppermute | solution.py:44
  113.4 4.4 %collective-permute-start.34 = (bf16[3,128,2,256]{3,2,1,0:T(2,128)(2,1)S(1)}, bf16[3,128,2,256]{3,2,1,0:T(2,128)(2,1)S(1)}, u32[]{:S(2)}, u32[]{:S(2)}) collective-permute-start(bf16[3,128,2,256]{3,2,1,0:T(2,128)(2,1)S(1)} %collective-permute-done.29), channel_id=1, source_target_pairs={{0,4},{4,0},{1,5},{5,1},{2,6},{6,2},{3,7},{7,3},{8,12},{12,8},{9,1... | collective-permute-start | bytes 1179656 | tf_op jit(solution)/shard_map/ppermute | solution.py:60
  114.8 3.0 %collective-permute-start.35 = (bf16[3,128,2,256]{3,2,1,0:T(2,128)(2,1)S(1)}, bf16[3,128,2,256]{3,2,1,0:T(2,128)(2,1)S(1)}, u32[]{:S(2)}, u32[]{:S(2)}) collective-permute-start(bf16[3,128,2,256]{3,2,1,0:T(2,128)(2,1)S(1)} %collective-permute-done.30), channel_id=1, source_target_pairs={{0,4},{4,0},{1,5},{5,1},{2,6},{6,2},{3,7},{7,3},{8,12},{12,8},{9,1... | collective-permute-start | bytes 1179656 | tf_op jit(solution)/shard_map/ppermute | solution.py:60

commit v13 on v12

--- a/solution.py
+++ b/solution.py
@@ -60,7 +60,7 @@
     return lax.ppermute(value, "core", [(0, 1), (1, 0)])
 
 
-def pack_kernel(info, w_hbm, d_hbm, k_ref, v_ref, w_ref, d_ref, sems):
+def pack_kernel(info, adapter, w_hbm, d_hbm, k_ref, v_ref, w_ref, d_ref, sems):
     weight = pltpu.make_async_copy(w_hbm, w_ref, sems.at[0])
     down = pltpu.make_async_copy(d_hbm, d_ref, sems.at[1])
     weight.start()
@@ -70,7 +70,7 @@
     v_ref[0:256] = w_ref[pl.ds(pl.multiple_of(info[POOL] * 256, 256), 256), 1, :]
     column = lax.broadcasted_iota(jnp.int32, (256, 128), 0)
     lane = lax.broadcasted_iota(jnp.int32, (256, 128), 1)
-    pick = (column == info[ADAPTER + info[HEAD]] * 32 + lane) & (lane < 32)
+    pick = (column == adapter[info[HEAD]] * 32 + lane) & (lane < 32)
     down.wait()
     low = lax.dot_general(
         pick.astype(jnp.bfloat16),
@@ -82,10 +82,10 @@
     v_ref[288:320] = low[0:32, 256:512]
 
 
-def pack(info, weight, down):
+def pack(info, adapter, weight, down):
     return pl.pallas_call(
         pack_kernel,
-        in_specs=[SMEM, HBM, HBM],
+        in_specs=[SMEM, SMEM, HBM, HBM],
         out_specs=[VMEM, VMEM],
         out_shape=[
             jax.ShapeDtypeStruct((512, 256), jnp.bfloat16),
@@ -98,7 +98,7 @@
         ],
         compiler_params=params(),
         name="pack",
-    )(info, weight, down)
+    )(info, adapter, weight, down)
 
 
 ROWS_STEP = 12
@@ -449,7 +449,8 @@
 
     cache = pltpu.with_memory_space_constraint(key_value_cache, pltpu.HBM)
     keys, values = pack(
-        info,
+        place_of,
+        request_adapter_index,
         pltpu.with_memory_space_constraint(key_value_weight, pltpu.HBM),
         pltpu.with_memory_space_constraint(adapter_down_weight, pltpu.HBM),
     )

time: 119 us -> 129 us (1.084)
  local copies, waits for them, and re-layouts: 2.12 us -> 10.9 us
  Pallas kernels: 29.9 us -> 32.2 us
    unnamed x32 -> x40, local copies, waits for them, and re-layouts: 0.44 us -> 9.12 us
    pallas_call x2, Pallas kernels: 4.73 us -> 6.12 us  [main_product(): pl.pallas_call(functools.partial(main_kernel, pieces), in_specs=[SMEM] +...]
  transfers between devices with their start and end apart: 36 -> 36, of which waited for: 9 -> 8; matrix products, arithmetic and copies ran while one was open for 2% -> 3% of each run, Pallas kernels for 22% -> 22%
where the time goes in v13:
time: 129 us
  starting transfers between devices  48.8 us (38%)
  waiting for transfers between devices  33.4 us (26%)
  Pallas kernels  32.2 us (25%)
  local copies, waits for them, and re-layouts  10.9 us (8%)
  other arithmetic  1.95 us (2%)
    ppermute x13, waiting for transfers between devices, y_shift(): return lax.ppermute(value, 'y', [(i, (i + k) % 4) for i in range(4)])  29.7 us
    ppermute x13, starting transfers between devices, y_shift(): return lax.ppermute(value, 'y', [(i, (i + k) % 4) for i in range(4)])  19.8 us
    unnamed x40, local copies, waits for them, and re-layouts  9.12 us
    ppermute x10, starting transfers between devices, core_swap(): return lax.ppermute(value, 'core', [(0, 1), (1, 0)])  8.61 us
    pallas_call x1, Pallas kernels, attend(): pl.pallas_call(functools.partial(attend_kernel, first * ROWS_STEP), grid_...  8.2 us
    pallas_call x2, Pallas kernels, main_product(): pl.pallas_call(functools.partial(main_kernel, pieces), in_specs=[SMEM] +...  6.12 us
    pallas_call x1, Pallas kernels, project(): pl.pallas_call(project_kernel, in_specs=[SMEM] + [VMEM] * 6, out_specs=[V...  5.15 us
    ppermute x2, starting transfers between devices, z_flip(): return lax.ppermute(value, 'head', [(i, i ^ mask) for i in range(4)])  5.14 us
  transfers between devices with their start and end apart: 36, of which 8 were waited for; matrix products, arithmetic and copies ran while one was open for 3% of the time, Pallas kernels for 22%

profile of v13, /device:TPU:1, one launch (start us, length us, event | category | flops | bytes accessed | tf_op | source)
XLA Modules:
  0.0 128.6 jit_solution(116035983614691641)
XLA Ops:
  1.4 2.8 %pack.1 = (bf16[512,256]{1,0:T(8,128)(2,1)S(1)}, bf16[320,256]{1,0:T(8,128)(2,1)S(1)}) custom-call(s32[5]{0:T(128)S(1)} %stack.32.info, s32[4]{0:T(128)S(1)} %copy-done.7, bf16[512,2,256]{2,1,0:T(2,128)(2,1)} %w_hbm.1, bf16[512,256]{1,0:T(8,128)(2,1)} %d_hbm.1), custom_call_target="tpu_custom_call" | custom-call | tf_op jit(solution)/shard_map/pack/pallas_call | solution.py:86
  4.2 2.2 %collective-permute-start.1 = (bf16[320,256]{1,0:T(8,128)(2,1)S(1)}, bf16[320,256]{1,0:T(8,128)(2,1)S(1)}, u32[]{:S(2)}, u32[]{:S(2)}) collective-permute-start(bf16[320,256]{1,0:T(8,128)(2,1)S(1)} %get-tuple-element.59), channel_id=1, source_target_pairs={{0,8},{8,16},{16,24},{24,0},{1,9},{9,17},{17,25},{25,1},{2,10},{10... | collective-permute-start | bytes 491528 | tf_op jit(solution)/shard_map/ppermute | solution.py:44
  6.4 2.6 %collective-permute-start.2 = (bf16[320,256]{1,0:T(8,128)(2,1)S(1)}, bf16[320,256]{1,0:T(8,128)(2,1)S(1)}, u32[]{:S(2)}, u32[]{:S(2)}) collective-permute-start(bf16[320,256]{1,0:T(8,128)(2,1)S(1)} %get-tuple-element.59), channel_id=1, source_target_pairs={{0,16},{8,24},{16,0},{24,8},{1,17},{9,25},{17,1},{25,9},{2,18},{10... | collective-permute-start | bytes 491528 | tf_op jit(solution)/shard_map/ppermute | solution.py:44
  9.0 1.1 collective-permute-start.3
  10.0 2.5 %collective-permute-start = (bf16[512,256]{1,0:T(8,128)(2,1)S(1)}, bf16[512,256]{1,0:T(8,128)(2,1)S(1)}, u32[]{:S(2)}, u32[]{:S(2)}) collective-permute-start(bf16[512,256]{1,0:T(8,128)(2,1)S(1)} %get-tuple-element.57), channel_id=1, source_target_pairs={{0,96},{32,64},{64,32},{96,0},{1,97},{33,65},{65,33},{97,1},{2,98}... | collective-permute-start | bytes 786440 | tf_op jit(solution)/shard_map/ppermute | solution.py:32
  12.6 3.5 %collective-permute-done.2 = bf16[320,256]{1,0:T(8,128)(2,1)S(1)} collective-permute-done((bf16[320,256]{1,0:T(8,128)(2,1)S(1)}, bf16[320,256]{1,0:T(8,128)(2,1)S(1)}, u32[]{:S(2)}, u32[]{:S(2)}) %collective-permute-start.2) | collective-permute-done | bytes 163872 | tf_op jit(solution)/shard_map/ppermute | solution.py:44
  16.2 1.3 collective-permute-start.6
  17.4 1.5 %collective-permute-start.7 = (bf16[1024,256]{1,0:T(8,128)(2,1)S(1)}, bf16[1024,256]{1,0:T(8,128)(2,1)S(1)}, u32[]{:S(2)}, u32[]{:S(2)}) collective-permute-start(bf16[1024,256]{1,0:T(8,128)(2,1)S(1)} %pad_maximum_fusion.1.refs_1_), channel_id=1, source_target_pairs={{0,96},{64,0},{32,64},{96,32},{1,97},{65,1},{33,65},{97,33},{2,98}... | collective-permute-start | bytes 1572872 | tf_op jit(solution)/shard_map/ppermute | solution.py:40
  19.0 1.3 %collective-permute-start.4 = (bf16[1024,256]{1,0:T(8,128)(2,1)S(1)}, bf16[1024,256]{1,0:T(8,128)(2,1)S(1)}, u32[]{:S(2)}, u32[]{:S(2)}) collective-permute-start(bf16[1024,256]{1,0:T(8,128)(2,1)S(1)} %constant_dynamic-update-slice_fusion.refs_0_), channel_id=1, source_target_pairs={{0,8},{8,16},{16,24},{24,0},{1,9},{9,17},{17,25},{25,1},{2,10},{10... | collective-permute-start | bytes 1572872 | tf_op jit(solution)/shard_map/ppermute | solution.py:44
  20.3 1.5 %collective-permute-start.5 = (bf16[1024,256]{1,0:T(8,128)(2,1)S(1)}, bf16[1024,256]{1,0:T(8,128)(2,1)S(1)}, u32[]{:S(2)}, u32[]{:S(2)}) collective-permute-start(bf16[1024,256]{1,0:T(8,128)(2,1)S(1)} %constant_dynamic-update-slice_fusion.refs_0_), channel_id=1, source_target_pairs={{0,24},{8,0},{16,8},{24,16},{1,25},{9,1},{17,9},{25,17},{2,26},{10... | collective-permute-start | bytes 1572872 | tf_op jit(solution)/shard_map/ppermute | solution.py:44
  21.8 1.6 %collective-permute-start.8 = (bf16[256,256]{1,0:T(8,128)(2,1)S(1)}, bf16[256,256]{1,0:T(8,128)(2,1)S(1)}, u32[]{:S(2)}, u32[]{:S(2)}) collective-permute-start(bf16[256,256]{1,0:T(8,128)(2,1)S(1)} %pad_maximum_fusion.2), channel_id=1, source_target_pairs={{0,32},{32,0},{1,33},{33,1},{2,34},{34,2},{3,35},{35,3},{4,36},{36... | collective-permute-start | bytes 393224 | tf_op jit(solution)/shard_map/ppermute | solution.py:48
  23.4 8.2 %attend.1 = bf16[48,16,128]{2,1,0:T(8,128)(2,1)S(1)} custom-call(s32[48]{0:T(128)S(1)} %copy-done.9, bf16[48,16,128]{2,1,0:T(8,128)(2,1)S(1)} %bitcast.31, bf16[48,128,2,256]{3,2,1,0:T(2,128)(2,1)} %kv_ref.1, bf16[48,2,256]{2,1,0:T(2,128)(2,1)S(1)} %copy-done.6), custom_call_target="tpu_custom_call" | custom-call | tf_op jit(solution)/shard_map/attend/pallas_call | solution.py:146
  32.9 0.8 constant_dynamic-update-slice_fusion.12
  35.4 0.8 constant_dynamic-update-slice_fusion.9
  37.9 2.8 %collective-permute-start.11 = (bf16[6144,256]{1,0:T(8,128)(2,1)}, bf16[6144,256]{1,0:T(8,128)(2,1)}, u32[]{:S(2)}, u32[]{:S(2)}) collective-permute-start(bf16[6144,256]{1,0:T(8,128)(2,1)} %constant_dynamic-update-slice_fusion.7), channel_id=1, source_target_pairs={{0,4},{4,0},{1,5},{5,1},{2,6},{6,2},{3,7},{7,3},{8,12},{12,8},{9,1... | collective-permute-start | bytes 9437192 | tf_op jit(solution)/shard_map/ppermute | solution.py:60
  40.6 1.2 collective-permute-start.10
  41.8 1.6 %collective-permute-start.9 = (bf16[1024,256]{1,0:T(8,128)(2,1)S(1)}, bf16[1024,256]{1,0:T(8,128)(2,1)}, u32[]{:S(2)}, u32[]{:S(2)}) collective-permute-start(bf16[1024,256]{1,0:T(8,128)(2,1)S(1)} %constant_dynamic-update-slice_fusion.refs_0_), channel_id=1, source_target_pairs={{0,16},{8,24},{16,0},{24,8},{1,17},{9,25},{17,1},{25,9},{2,18},{10... | collective-permute-start | bytes 1572872 | tf_op jit(solution)/shard_map/ppermute | solution.py:44
  43.4 2.8 %collective-permute-done.13.other_ref = bf16[512,256]{1,0:T(8,128)(2,1)} collective-permute-done((bf16[512,256]{1,0:T(8,128)(2,1)S(1)}, bf16[512,256]{1,0:T(8,128)(2,1)}, u32[]{:S(2)}, u32[]{:S(2)}) %collective-permute-start.13) | collective-permute-done | bytes 262176 | tf_op jit(solution)/shard_map/ppermute | solution.py:60
  46.3 3.4 %copy-done = bf16[4,128,8192]{2,1,0:T(8,128)(2,1)S(1)} copy-done((bf16[4,128,8192]{2,1,0:T(8,128)(2,1)S(1)}, bf16[4,128,8192]{2,1,0:T(8,128)(2,1)}, u32[]{:S(2)}) %copy-start) | copy-done | bytes 8388632
  49.7 1.9 %low_rank.1 = f32[32,128]{1,0:T(8,128)S(1)} custom-call(s32[17]{0:T(128)S(1)} %concatenate.33.info, bf16[512,8192]{1,0:T(8,128)(2,1)S(1)} %bitcast.26, bf16[512,256]{1,0:T(8,128)(2,1)S(1)} %constant_dynamic-update-slice_fusion.2.own_ref, bf16[512,256]{1,0:T(8,128)(2,1)} %collective-permute-done.13.other_ref), custom_call_target="tpu_custom_call" | custom-call | tf_op jit(solution)/shard_map/low_rank/pallas_call | solution.py:199
  51.6 1.7 %collective-permute-start.14 = (f32[32,128]{1,0:T(8,128)S(1)}, f32[32,128]{1,0:T(8,128)S(1)}, u32[]{:S(2)}, u32[]{:S(2)}) collective-permute-start(f32[32,128]{1,0:T(8,128)S(1)} %low_rank.1), channel_id=1, source_target_pairs={{0,1},{1,0},{2,3},{3,2},{4,5},{5,4},{6,7},{7,6},{8,9},{9,8},{10,11... | collective-permute-start | bytes 49160 | tf_op jit(solution)/shard_map/ppermute | solution.py:56
  53.3 1.2 collective-permute-start.12
  54.8 3.4 %collective-permute-start.15 = (f32[64,128]{1,0:T(8,128)S(1)}, f32[64,128]{1,0:T(8,128)S(1)}, u32[]{:S(2)}, u32[]{:S(2)}) collective-permute-start(f32[64,128]{1,0:T(8,128)S(1)} %pad_maximum_fusion.4), channel_id=1, source_target_pairs={{0,2},{1,3},{2,0},{3,1},{4,6},{5,7},{6,4},{7,5},{8,10},{9,11},{10,... | collective-permute-start | bytes 98312 | tf_op jit(solution)/shard_map/ppermute | solution.py:56
  58.3 2.4 %main_product.2 = (f32[512,256]{1,0:T(8,128)S(1)}, f32[512,256]{1,0:T(8,128)S(1)}) custom-call(s32[17]{0:T(128)S(1)} %concatenate.33.info, bf16[512,8192]{1,0:T(8,128)(2,1)S(1)} %bitcast.27, bf16[1024,256]{1,0:T(8,128)(2,1)S(1)} %constant_dynamic-update-slice_fusion.refs_0_, bf16[1024,256]{1,0:T(8,128)(2,1)S(1)} %pad_maximum_fusion.1.refs_1_, ...), custom_call_target="tpu_custom_call" | custom-call | tf_op jit(solution)/shard_map/main_product/pallas_call | solution.py:242
  60.7 3.8 %main_product.3 = (f32[512,256]{1,0:T(8,128)S(1)}, f32[512,256]{1,0:T(8,128)S(1)}) custom-call(s32[17]{0:T(128)S(1)} %concatenate.33.info, bf16[512,8192]{1,0:T(8,128)(2,1)S(1)} %bitcast.28, bf16[6144,256]{1,0:T(8,128)(2,1)} %collective-permute-done.11.refs_0_), custom_call_target="tpu_custom_call" | custom-call | tf_op jit(solution)/shard_map/main_product/pallas_call | solution.py:242
  64.5 1.3 collective-permute-start.16
  66.0 1.3 %collective-permute-start.20 = (bf16[96,2048]{1,0:T(8,128)(2,1)S(1)}, bf16[96,2048]{1,0:T(8,128)(2,1)S(1)}, u32[]{:S(2)}, u32[]{:S(2)}) collective-permute-start(bf16[96,2048]{1,0:T(8,128)(2,1)S(1)} %constant_dynamic-update-slice_fusion.13), channel_id=1, source_target_pairs={{0,8},{8,16},{16,24},{24,0},{1,9},{9,17},{17,25},{25,1},{2,10},{10... | collective-permute-start | bytes 1179656 | tf_op jit(solution)/shard_map/ppermute | solution.py:44
  67.3 2.2 %collective-permute-start.21 = (bf16[96,2048]{1,0:T(8,128)(2,1)S(1)}, bf16[96,2048]{1,0:T(8,128)(2,1)S(1)}, u32[]{:S(2)}, u32[]{:S(2)}) collective-permute-start(bf16[96,2048]{1,0:T(8,128)(2,1)S(1)} %constant_dynamic-update-slice_fusion.13), channel_id=1, source_target_pairs={{0,16},{8,24},{16,0},{24,8},{1,17},{9,25},{17,1},{25,9},{2,18},{10... | collective-permute-start | bytes 1179656 | tf_op jit(solution)/shard_map/ppermute | solution.py:44
  70.2 4.3 %finish.1 = (bf16[3,128,2,256]{3,2,1,0:T(2,128)(2,1)S(1)}, bf16[3,128,2,256]{3,2,1,0:T(2,128)(2,1)S(1)}) custom-call(s32[17]{0:T(128)S(1)} %concatenate.33.info, bf16[512,8192]{1,0:T(8,128)(2,1)S(1)} %bitcast.29, bf16[1024,256]{1,0:T(8,128)(2,1)} %collective-permute-done.9.refs_0_, bf16[1024,256]{1,0:T(8,128)(2,1)} %collective-permute-done.10.refs_1_, ...), custom_call_target="tpu_custom_call" | custom-call | tf_op jit(solution)/shard_map/finish/pallas_call | solution.py:293
  74.6 0.9 collective-permute-start.18
  75.5 0.9 collective-permute-start.19
  76.4 1.4 %collective-permute-done.20 = bf16[96,2048]{1,0:T(8,128)(2,1)S(1)} collective-permute-done((bf16[96,2048]{1,0:T(8,128)(2,1)S(1)}, bf16[96,2048]{1,0:T(8,128)(2,1)S(1)}, u32[]{:S(2)}, u32[]{:S(2)}) %collective-permute-start.20) | collective-permute-done | bytes 393248 | tf_op jit(solution)/shard_map/ppermute | solution.py:44
  77.8 9.2 %collective-permute-done.21 = bf16[96,2048]{1,0:T(8,128)(2,1)S(1)} collective-permute-done((bf16[96,2048]{1,0:T(8,128)(2,1)S(1)}, bf16[96,2048]{1,0:T(8,128)(2,1)S(1)}, u32[]{:S(2)}, u32[]{:S(2)}) %collective-permute-start.21) | collective-permute-done | bytes 393248 | tf_op jit(solution)/shard_map/ppermute | solution.py:44
  87.2 1.4 %collective-permute-start.25 = (bf16[384,2048]{1,0:T(8,128)(2,1)S(1)}, bf16[384,2048]{1,0:T(8,128)(2,1)S(1)}, u32[]{:S(2)}, u32[]{:S(2)}) collective-permute-start(bf16[384,2048]{1,0:T(8,128)(2,1)S(1)} %constant_dynamic-update-slice_fusion.15.refs_0_), channel_id=1, source_target_pairs={{0,4},{4,0},{1,5},{5,1},{2,6},{6,2},{3,7},{7,3},{8,12},{12,8},{9,1... | collective-permute-start | bytes 4718600 | tf_op jit(solution)/shard_map/ppermute | solution.py:60
  88.5 1.1 pad_maximum_fusion.refs_0_
  89.7 1.0 collective-permute-start.23
  90.8 1.7 %collective-permute-start.24 = (bf16[2,3,128,2,256]{4,3,2,1,0:T(2,128)(2,1)S(1)}, bf16[2,3,128,2,256]{4,3,2,1,0:T(2,128)(2,1)S(1)}, u32[]{:S(2)}, u32[]{:S(2)}) collective-permute-start(bf16[2,3,128,2,256]{4,3,2,1,0:T(2,128)(2,1)S(1)} %pad_maximum_fusion.refs_0_), channel_id=1, source_target_pairs={{0,24},{8,0},{16,8},{24,16},{1,25},{9,1},{17,9},{25,17},{2,26},{10... | collective-permute-start | bytes 2359304 | tf_op jit(solution)/shard_map/ppermute | solution.py:44
  92.7 5.2 %project.1 = (bf16[192,512]{1,0:T(8,128)(2,1)S(1)}, bf16[192,512]{1,0:T(8,128)(2,1)S(1)}, bf16[192,512]{1,0:T(8,128)(2,1)S(1)}, bf16[192,512]{1,0:T(8,128)(2,1)S(1)}) custom-call(s32[17]{0:T(128)S(1)} %concatenate.33.info, s32[768,1]{1,0:T(8,128)S(1)} %broadcast_in_dim.20.keep, bf16[128,2048]{1,0:T(8,128)(2,1)S(1)} %bitcast.32, ...), custom_call_target="tpu_custom_call" | custom-call | tf_op jit(solution)/shard_map/project/pallas_call | solution.py:410
  97.8 0.9 collective-permute-start.27
  98.7 2.2 %collective-permute-start.28 = (bf16[192,512]{1,0:T(8,128)(2,1)S(1)}, bf16[192,512]{1,0:T(8,128)(2,1)S(1)}, u32[]{:S(2)}, u32[]{:S(2)}) collective-permute-start(bf16[192,512]{1,0:T(8,128)(2,1)S(1)} %get-tuple-element.95), channel_id=1, source_target_pairs={{0,3},{1,0},{2,1},{3,2},{4,7},{5,4},{6,5},{7,6},{8,11},{9,8},{10,9... | collective-permute-start | bytes 589832 | tf_op jit(solution)/shard_map/ppermute | solution.py:52
  100.9 1.2 collective-permute-start.33
  102.1 7.5 %collective-permute-done.23.refs_1_ = bf16[2,3,128,2,256]{4,3,2,1,0:T(2,128)(2,1)S(1)} collective-permute-done((bf16[2,3,128,2,256]{4,3,2,1,0:T(2,128)(2,1)S(1)}, bf16[2,3,128,2,256]{4,3,2,1,0:T(2,128)(2,1)S(1)}, u32[]{:S(2)}, u32[]{:S(2)}) %collective-permute-start.23) | collective-permute-done | bytes 786464 | tf_op jit(solution)/shard_map/ppermute | solution.py:44
  109.7 1.3 %collective-permute-start.31 = (bf16[2,3,128,2,256]{4,3,2,1,0:T(2,128)(2,1)S(1)}, bf16[2,3,128,2,256]{4,3,2,1,0:T(2,128)(2,1)S(1)}, u32[]{:S(2)}, u32[]{:S(2)}) collective-permute-start(bf16[2,3,128,2,256]{4,3,2,1,0:T(2,128)(2,1)S(1)} %collective-permute-done.23.refs_1_), channel_id=1, source_target_pairs={{0,4},{4,0},{1,5},{5,1},{2,6},{6,2},{3,7},{7,3},{8,12},{12,8},{9,1... | collective-permute-start | bytes 2359304 | tf_op jit(solution)/shard_map/ppermute | solution.py:60
  111.8 2.6 %collective-permute-start.30 = (bf16[3,128,2,256]{3,2,1,0:T(2,128)(2,1)S(1)}, bf16[3,128,2,256]{3,2,1,0:T(2,128)(2,1)S(1)}, u32[]{:S(2)}, u32[]{:S(2)}) collective-permute-start(bf16[3,128,2,256]{3,2,1,0:T(2,128)(2,1)S(1)} %slice_bitcast_fusion), channel_id=1, source_target_pairs={{0,24},{8,0},{16,8},{24,16},{1,25},{9,1},{17,9},{25,17},{2,26},{10... | collective-permute-start | bytes 1179656 | tf_op jit(solution)/shard_map/ppermute | solution.py:44
  115.2 8.0 %collective-permute-done.29 = bf16[3,128,2,256]{3,2,1,0:T(2,128)(2,1)S(1)} collective-permute-done((bf16[3,128,2,256]{3,2,1,0:T(2,128)(2,1)S(1)}, bf16[3,128,2,256]{3,2,1,0:T(2,128)(2,1)S(1)}, u32[]{:S(2)}, u32[]{:S(2)}) %collective-permute-start.29) | collective-permute-done | bytes 393248 | tf_op jit(solution)/shard_map/ppermute | solution.py:44
  123.3 1.3 %collective-permute-start.34 = (bf16[3,128,2,256]{3,2,1,0:T(2,128)(2,1)S(1)}, bf16[3,128,2,256]{3,2,1,0:T(2,128)(2,1)S(1)}, u32[]{:S(2)}, u32[]{:S(2)}) collective-permute-start(bf16[3,128,2,256]{3,2,1,0:T(2,128)(2,1)S(1)} %collective-permute-done.29), channel_id=1, source_target_pairs={{0,4},{4,0},{1,5},{5,1},{2,6},{6,2},{3,7},{7,3},{8,12},{12,8},{9,1... | collective-permute-start | bytes 1179656 | tf_op jit(solution)/shard_map/ppermute | solution.py:60
  124.7 2.9 %place.2.refs_4_ = bf16[1,2,2048,2,256]{4,3,2,1,0:T(2,128)(2,1)} custom-call(s32[17]{0:T(128)S(1)} %concatenate.33.info, bf16[2,3,128,2,256]{4,3,2,1,0:T(2,128)(2,1)S(1)} %pad_maximum_fusion.refs_0_, bf16[2,3,128,2,256]{4,3,2,1,0:T(2,128)(2,1)S(1)} %collective-permute-done.23.refs_1_, bf16[2,3,128,2,256]{4,3,2,1,0:T(2,128)(2,1)S(1)} %collective-permute-done.24.refs_2_, ...), custom_call_target="tpu_custom_call" | custom-call | tf_op jit(solution)/shard_map/place/pallas_call | solution.py:368
  127.6 0.9 place.3
  (97 shorter events, 9.0 us)
Async XLA Ops:
  0.6 22.8 %copy-start.6 = (bf16[48,2,256]{2,1,0:T(2,128)(2,1)S(1)}, bf16[48,2,256]{2,1,0:T(2,128)(2,1)}, u32[]{:S(2)}) copy-start(bf16[48,2,256]{2,1,0:T(2,128)(2,1)} %cur_ref.1) | copy-start | bytes 147460
  1.4 22.0 %copy-start.11 = (bf16[48,2048]{1,0:T(8,128)(2,1)S(1)}, bf16[48,2048]{1,0:T(8,128)(2,1)}, u32[]{:S(2)}) copy-start(bf16[48,2048]{1,0:T(8,128)(2,1)} %param.20) | copy-start | bytes 589828
  1.4 22.0 %copy-start.9 = (s32[48]{0:T(128)S(1)}, s32[48]{0:T(128)}, u32[]{:S(2)}) copy-start(s32[48]{0:T(128)} %len_ref) | copy-start | bytes 580
  4.2 8.4 %collective-permute-start.1 = (bf16[320,256]{1,0:T(8,128)(2,1)S(1)}, bf16[320,256]{1,0:T(8,128)(2,1)S(1)}, u32[]{:S(2)}, u32[]{:S(2)}) collective-permute-start(bf16[320,256]{1,0:T(8,128)(2,1)S(1)} %get-tuple-element.59), channel_id=1, source_target_pairs={{0,8},{8,16},{16,24},{24,0},{1,9},{9,17},{17,25},{25,1},{2,10},{10... | collective-permute-start | bytes 491528 | tf_op jit(solution)/shard_map/ppermute | solution.py:44
  6.4 9.7 %collective-permute-start.2 = (bf16[320,256]{1,0:T(8,128)(2,1)S(1)}, bf16[320,256]{1,0:T(8,128)(2,1)S(1)}, u32[]{:S(2)}, u32[]{:S(2)}) collective-permute-start(bf16[320,256]{1,0:T(8,128)(2,1)S(1)} %get-tuple-element.59), channel_id=1, source_target_pairs={{0,16},{8,24},{16,0},{24,8},{1,17},{9,25},{17,1},{25,9},{2,18},{10... | collective-permute-start | bytes 491528 | tf_op jit(solution)/shard_map/ppermute | solution.py:44
  9.0 7.1 %collective-permute-start.3 = (bf16[320,256]{1,0:T(8,128)(2,1)S(1)}, bf16[320,256]{1,0:T(8,128)(2,1)S(1)}, u32[]{:S(2)}, u32[]{:S(2)}) collective-permute-start(bf16[320,256]{1,0:T(8,128)(2,1)S(1)} %get-tuple-element.59), channel_id=1, source_target_pairs={{0,24},{8,0},{16,8},{24,16},{1,25},{9,1},{17,9},{25,17},{2,26},{10... | collective-permute-start | bytes 491528 | tf_op jit(solution)/shard_map/ppermute | solution.py:44
  10.0 8.9 %collective-permute-start = (bf16[512,256]{1,0:T(8,128)(2,1)S(1)}, bf16[512,256]{1,0:T(8,128)(2,1)S(1)}, u32[]{:S(2)}, u32[]{:S(2)}) collective-permute-start(bf16[512,256]{1,0:T(8,128)(2,1)S(1)} %get-tuple-element.57), channel_id=1, source_target_pairs={{0,96},{32,64},{64,32},{96,0},{1,97},{33,65},{65,33},{97,1},{2,98}... | collective-permute-start | bytes 786440 | tf_op jit(solution)/shard_map/ppermute | solution.py:32
  16.2 16.7 %collective-permute-start.6 = (bf16[1024,256]{1,0:T(8,128)(2,1)S(1)}, bf16[1024,256]{1,0:T(8,128)(2,1)S(1)}, u32[]{:S(2)}, u32[]{:S(2)}) collective-permute-start(bf16[1024,256]{1,0:T(8,128)(2,1)S(1)} %pad_maximum_fusion.1.refs_1_), channel_id=1, source_target_pairs={{0,64},{64,32},{32,96},{96,0},{1,65},{65,33},{33,97},{97,1},{2,66}... | collective-permute-start | bytes 1572872 | tf_op jit(solution)/shard_map/ppermute | solution.py:40
  17.4 15.4 %collective-permute-start.7 = (bf16[1024,256]{1,0:T(8,128)(2,1)S(1)}, bf16[1024,256]{1,0:T(8,128)(2,1)S(1)}, u32[]{:S(2)}, u32[]{:S(2)}) collective-permute-start(bf16[1024,256]{1,0:T(8,128)(2,1)S(1)} %pad_maximum_fusion.1.refs_1_), channel_id=1, source_target_pairs={{0,96},{64,0},{32,64},{96,32},{1,97},{65,1},{33,65},{97,33},{2,98}... | collective-permute-start | bytes 1572872 | tf_op jit(solution)/shard_map/ppermute | solution.py:40
  19.0 13.9 %collective-permute-start.4 = (bf16[1024,256]{1,0:T(8,128)(2,1)S(1)}, bf16[1024,256]{1,0:T(8,128)(2,1)S(1)}, u32[]{:S(2)}, u32[]{:S(2)}) collective-permute-start(bf16[1024,256]{1,0:T(8,128)(2,1)S(1)} %constant_dynamic-update-slice_fusion.refs_0_), channel_id=1, source_target_pairs={{0,8},{8,16},{16,24},{24,0},{1,9},{9,17},{17,25},{25,1},{2,10},{10... | collective-permute-start | bytes 1572872 | tf_op jit(solution)/shard_map/ppermute | solution.py:44
  20.3 12.6 %collective-permute-start.5 = (bf16[1024,256]{1,0:T(8,128)(2,1)S(1)}, bf16[1024,256]{1,0:T(8,128)(2,1)S(1)}, u32[]{:S(2)}, u32[]{:S(2)}) collective-permute-start(bf16[1024,256]{1,0:T(8,128)(2,1)S(1)} %constant_dynamic-update-slice_fusion.refs_0_), channel_id=1, source_target_pairs={{0,24},{8,0},{16,8},{24,16},{1,25},{9,1},{17,9},{25,17},{2,26},{10... | collective-permute-start | bytes 1572872 | tf_op jit(solution)/shard_map/ppermute | solution.py:44
  21.8 11.1 %collective-permute-start.8 = (bf16[256,256]{1,0:T(8,128)(2,1)S(1)}, bf16[256,256]{1,0:T(8,128)(2,1)S(1)}, u32[]{:S(2)}, u32[]{:S(2)}) collective-permute-start(bf16[256,256]{1,0:T(8,128)(2,1)S(1)} %pad_maximum_fusion.2), channel_id=1, source_target_pairs={{0,32},{32,0},{1,33},{33,1},{2,34},{34,2},{3,35},{35,3},{4,36},{36... | collective-permute-start | bytes 393224 | tf_op jit(solution)/shard_map/ppermute | solution.py:48
  32.9 10.5 %copy-start.8 = (s32[4]{0:T(128)S(1)}, s32[4]{0:T(128)}, u32[]{:S(2)}) copy-start(s32[4]{0:T(128)} %adapter.1) | copy-start | bytes 52
  32.9 10.5 %copy-start.13 = (s32[8]{0:T(128)S(1)}, s32[8]{0:T(128)}, u32[]{:S(2)}) copy-start(s32[8]{0:T(128)} %param.19) | copy-start | bytes 100
  37.9 22.8 %collective-permute-start.11 = (bf16[6144,256]{1,0:T(8,128)(2,1)}, bf16[6144,256]{1,0:T(8,128)(2,1)}, u32[]{:S(2)}, u32[]{:S(2)}) collective-permute-start(bf16[6144,256]{1,0:T(8,128)(2,1)} %constant_dynamic-update-slice_fusion.7), channel_id=1, source_target_pairs={{0,4},{4,0},{1,5},{5,1},{2,6},{6,2},{3,7},{7,3},{8,12},{12,8},{9,1... | collective-permute-start | bytes 9437192 | tf_op jit(solution)/shard_map/ppermute | solution.py:60
  40.6 5.7 %collective-permute-start.13 = (bf16[512,256]{1,0:T(8,128)(2,1)S(1)}, bf16[512,256]{1,0:T(8,128)(2,1)}, u32[]{:S(2)}, u32[]{:S(2)}) collective-permute-start(bf16[512,256]{1,0:T(8,128)(2,1)S(1)} %constant_dynamic-update-slice_fusion.2.own_ref), channel_id=1, source_target_pairs={{0,4},{4,0},{1,5},{5,1},{2,6},{6,2},{3,7},{7,3},{8,12},{12,8},{9,1... | collective-permute-start | bytes 786440 | tf_op jit(solution)/shard_map/ppermute | solution.py:60
  40.6 23.8 %collective-permute-start.10 = (bf16[1024,256]{1,0:T(8,128)(2,1)S(1)}, bf16[1024,256]{1,0:T(8,128)(2,1)}, u32[]{:S(2)}, u32[]{:S(2)}) collective-permute-start(bf16[1024,256]{1,0:T(8,128)(2,1)S(1)} %pad_maximum_fusion.1.refs_1_), channel_id=1, source_target_pairs={{0,32},{64,96},{32,0},{96,64},{1,33},{65,97},{33,1},{97,65},{2,34}... | collective-permute-start | bytes 1572872 | tf_op jit(solution)/shard_map/ppermute | solution.py:40
  41.8 22.7 %collective-permute-start.9 = (bf16[1024,256]{1,0:T(8,128)(2,1)S(1)}, bf16[1024,256]{1,0:T(8,128)(2,1)}, u32[]{:S(2)}, u32[]{:S(2)}) collective-permute-start(bf16[1024,256]{1,0:T(8,128)(2,1)S(1)} %constant_dynamic-update-slice_fusion.refs_0_), channel_id=1, source_target_pairs={{0,16},{8,24},{16,0},{24,8},{1,17},{9,25},{17,1},{25,9},{2,18},{10... | collective-permute-start | bytes 1572872 | tf_op jit(solution)/shard_map/ppermute | solution.py:44
  49.7 3.6 %copy-start.10 = (bf16[6,8,16,128]{3,1,2,0:T(8,128)(2,1)S(1)}, bf16[6,8,16,128]{3,1,2,0:T(8,128)(2,1)}, u32[]{:S(2)}) copy-start(bf16[6,8,16,128]{3,1,2,0:T(8,128)(2,1)} %copy.21) | copy-start | bytes 589828
  49.7 8.6 %copy-start.1 = (bf16[4,128,8192]{2,1,0:T(8,128)(2,1)S(1)}, bf16[4,128,8192]{2,1,0:T(8,128)(2,1)}, u32[]{:S(2)}) copy-start(bf16[4,128,8192]{2,1,0:T(8,128)(2,1)} %param.14) | copy-start | bytes 25165828
  51.6 3.2 %collective-permute-start.14 = (f32[32,128]{1,0:T(8,128)S(1)}, f32[32,128]{1,0:T(8,128)S(1)}, u32[]{:S(2)}, u32[]{:S(2)}) collective-permute-start(f32[32,128]{1,0:T(8,128)S(1)} %low_rank.1), channel_id=1, source_target_pairs={{0,1},{1,0},{2,3},{3,2},{4,5},{5,4},{6,7},{7,6},{8,9},{9,8},{10,11... | collective-permute-start | bytes 49160 | tf_op jit(solution)/shard_map/ppermute | solution.py:56
  53.3 11.1 %collective-permute-start.12 = (bf16[48,2048]{1,0:T(8,128)(2,1)S(1)}, bf16[48,2048]{1,0:T(8,128)(2,1)S(1)}, u32[]{:S(2)}, u32[]{:S(2)}) collective-permute-start(bf16[48,2048]{1,0:T(8,128)(2,1)S(1)} %bitcast.38), channel_id=1, source_target_pairs={{0,32},{32,0},{1,33},{33,1},{2,34},{34,2},{3,35},{35,3},{4,36},{36... | collective-permute-start | bytes 589832 | tf_op jit(solution)/shard_map/ppermute | solution.py:48
  54.8 5.8 %collective-permute-start.15 = (f32[64,128]{1,0:T(8,128)S(1)}, f32[64,128]{1,0:T(8,128)S(1)}, u32[]{:S(2)}, u32[]{:S(2)}) collective-permute-start(f32[64,128]{1,0:T(8,128)S(1)} %pad_maximum_fusion.4), channel_id=1, source_target_pairs={{0,2},{1,3},{2,0},{3,1},{4,6},{5,7},{6,4},{7,5},{8,10},{9,11},{10,... | collective-permute-start | bytes 98312 | tf_op jit(solution)/shard_map/ppermute | solution.py:56
  60.7 9.5 %copy-start.4 = (bf16[8,2,16,256]{3,2,1,0:T(8,128)(2,1)S(1)}, bf16[8,2,16,256]{3,2,1,0:T(8,128)(2,1)}, u32[]{:S(2)}) copy-start(bf16[8,2,16,256]{3,2,1,0:T(8,128)(2,1)} %refs_9_.1) | copy-start | bytes 393220
  64.5 5.7 %collective-permute-start.16 = (bf16[1024,256]{1,0:T(8,128)(2,1)}, bf16[1024,256]{1,0:T(8,128)(2,1)S(1)}, u32[]{:S(2)}, u32[]{:S(2)}) collective-permute-start(bf16[1024,256]{1,0:T(8,128)(2,1)} %collective-permute-done.9.refs_0_), channel_id=1, source_target_pairs={{0,4},{4,0},{1,5},{5,1},{2,6},{6,2},{3,7},{7,3},{8,12},{12,8},{9,1... | collective-permute-start | bytes 1572872 | tf_op jit(solution)/shard_map/ppermute | solution.py:60
  65.7 4.5 %collective-permute-start.17 = (bf16[1024,256]{1,0:T(8,128)(2,1)}, bf16[1024,256]{1,0:T(8,128)(2,1)S(1)}, u32[]{:S(2)}, u32[]{:S(2)}) collective-permute-start(bf16[1024,256]{1,0:T(8,128)(2,1)} %collective-permute-done.10.refs_1_), channel_id=1, source_target_pairs={{0,4},{4,0},{1,5},{5,1},{2,6},{6,2},{3,7},{7,3},{8,12},{12,8},{9,1... | collective-permute-start | bytes 1572872 | tf_op jit(solution)/shard_map/ppermute | solution.py:60
  66.0 11.8 %collective-permute-start.20 = (bf16[96,2048]{1,0:T(8,128)(2,1)S(1)}, bf16[96,2048]{1,0:T(8,128)(2,1)S(1)}, u32[]{:S(2)}, u32[]{:S(2)}) collective-permute-start(bf16[96,2048]{1,0:T(8,128)(2,1)S(1)} %constant_dynamic-update-slice_fusion.13), channel_id=1, source_target_pairs={{0,8},{8,16},{16,24},{24,0},{1,9},{9,17},{17,25},{25,1},{2,10},{10... | collective-permute-start | bytes 1179656 | tf_op jit(solution)/shard_map/ppermute | solution.py:44
  67.3 19.7 %collective-permute-start.21 = (bf16[96,2048]{1,0:T(8,128)(2,1)S(1)}, bf16[96,2048]{1,0:T(8,128)(2,1)S(1)}, u32[]{:S(2)}, u32[]{:S(2)}) collective-permute-start(bf16[96,2048]{1,0:T(8,128)(2,1)S(1)} %constant_dynamic-update-slice_fusion.13), channel_id=1, source_target_pairs={{0,16},{8,24},{16,0},{24,8},{1,17},{9,25},{17,1},{25,9},{2,18},{10... | collective-permute-start | bytes 1179656 | tf_op jit(solution)/shard_map/ppermute | solution.py:44
  69.6 17.4 %collective-permute-start.22 = (bf16[96,2048]{1,0:T(8,128)(2,1)S(1)}, bf16[96,2048]{1,0:T(8,128)(2,1)S(1)}, u32[]{:S(2)}, u32[]{:S(2)}) collective-permute-start(bf16[96,2048]{1,0:T(8,128)(2,1)S(1)} %constant_dynamic-update-slice_fusion.13), channel_id=1, source_target_pairs={{0,24},{8,0},{16,8},{24,16},{1,25},{9,1},{17,9},{25,17},{2,26},{10... | collective-permute-start | bytes 1179656 | tf_op jit(solution)/shard_map/ppermute | solution.py:44
  74.6 17.9 %copy-start.12 = (s32[768]{0:T(1024)S(1)}, s32[768]{0:T(1024)}, u32[]{:S(2)}) copy-start(s32[768]{0:T(1024)} %param.24) | copy-start | bytes 9220
  74.6 18.1 %copy-start.2 = (bf16[2048,512]{1,0:T(8,128)(2,1)S(1)}, bf16[2048,512]{1,0:T(8,128)(2,1)}, u32[]{:S(2)}) copy-start(bf16[2048,512]{1,0:T(8,128)(2,1)} %w_ref.1) | copy-start | bytes 6291460
  74.6 18.1 %copy-start.3 = (bf16[2048,8,16]{0,2,1:T(8,128)(2,1)S(1)}, bf16[2048,8,16]{0,2,1:T(8,128)(2,1)}, u32[]{:S(2)}) copy-start(bf16[2048,8,16]{0,2,1:T(8,128)(2,1)} %param.26) | copy-start | bytes 1572868
  74.6 18.1 %copy-start.5 = (bf16[8,16,512]{2,1,0:T(8,128)(2,1)S(1)}, bf16[8,16,512]{2,1,0:T(8,128)(2,1)}, u32[]{:S(2)}) copy-start(bf16[8,16,512]{2,1,0:T(8,128)(2,1)} %param.27) | copy-start | bytes 393220
  74.6 12.4 %collective-permute-start.18 = (bf16[3,128,2,256]{3,2,1,0:T(2,128)(2,1)S(1)}, bf16[3,128,2,256]{3,2,1,0:T(2,128)(2,1)S(1)}, u32[]{:S(2)}, u32[]{:S(2)}) collective-permute-start(bf16[3,128,2,256]{3,2,1,0:T(2,128)(2,1)S(1)} %get-tuple-element.80), channel_id=1, source_target_pairs={{0,64},{64,0},{1,65},{65,1},{2,66},{66,2},{3,67},{67,3},{4,68},{68... | collective-permute-start | bytes 1179656 | tf_op jit(solution)/shard_map/ppermute | solution.py:491
  75.5 11.5 %collective-permute-start.19 = (bf16[3,128,2,256]{3,2,1,0:T(2,128)(2,1)S(1)}, bf16[3,128,2,256]{3,2,1,0:T(2,128)(2,1)S(1)}, u32[]{:S(2)}, u32[]{:S(2)}) collective-permute-start(bf16[3,128,2,256]{3,2,1,0:T(2,128)(2,1)S(1)} %get-tuple-element.81), channel_id=1, source_target_pairs={{0,96},{32,64},{64,32},{96,0},{1,97},{33,65},{65,33},{97,1},{2,98}... | collective-permute-start | bytes 1179656 | tf_op jit(solution)/shard_map/ppermute | solution.py:32
  87.2 5.5 %collective-permute-start.25 = (bf16[384,2048]{1,0:T(8,128)(2,1)S(1)}, bf16[384,2048]{1,0:T(8,128)(2,1)S(1)}, u32[]{:S(2)}, u32[]{:S(2)}) collective-permute-start(bf16[384,2048]{1,0:T(8,128)(2,1)S(1)} %constant_dynamic-update-slice_fusion.15.refs_0_), channel_id=1, source_target_pairs={{0,4},{4,0},{1,5},{5,1},{2,6},{6,2},{3,7},{7,3},{8,12},{12,8},{9,1... | collective-permute-start | bytes 4718600 | tf_op jit(solution)/shard_map/ppermute | solution.py:60
  89.6 8.2 %collective-permute-start.26 = (bf16[2,3,128,2,256]{4,3,2,1,0:T(2,128)(2,1)S(1)}, bf16[2,3,128,2,256]{4,3,2,1,0:T(2,128)(2,1)S(1)}, u32[]{:S(2)}, u32[]{:S(2)}) collective-permute-start(bf16[2,3,128,2,256]{4,3,2,1,0:T(2,128)(2,1)S(1)} %pad_maximum_fusion.refs_0_), channel_id=1, source_target_pairs={{0,4},{4,0},{1,5},{5,1},{2,6},{6,2},{3,7},{7,3},{8,12},{12,8},{9,1... | collective-permute-start | bytes 2359304 | tf_op jit(solution)/shard_map/ppermute | solution.py:60
  89.7 20.0 %collective-permute-start.23 = (bf16[2,3,128,2,256]{4,3,2,1,0:T(2,128)(2,1)S(1)}, bf16[2,3,128,2,256]{4,3,2,1,0:T(2,128)(2,1)S(1)}, u32[]{:S(2)}, u32[]{:S(2)}) collective-permute-start(bf16[2,3,128,2,256]{4,3,2,1,0:T(2,128)(2,1)S(1)} %pad_maximum_fusion.refs_0_), channel_id=1, source_target_pairs={{0,8},{8,16},{16,24},{24,0},{1,9},{9,17},{17,25},{25,1},{2,10},{10... | collective-permute-start | bytes 2359304 | tf_op jit(solution)/shard_map/ppermute | solution.py:44
  90.8 18.9 %collective-permute-start.24 = (bf16[2,3,128,2,256]{4,3,2,1,0:T(2,128)(2,1)S(1)}, bf16[2,3,128,2,256]{4,3,2,1,0:T(2,128)(2,1)S(1)}, u32[]{:S(2)}, u32[]{:S(2)}) collective-permute-start(bf16[2,3,128,2,256]{4,3,2,1,0:T(2,128)(2,1)S(1)} %pad_maximum_fusion.refs_0_), channel_id=1, source_target_pairs={{0,24},{8,0},{16,8},{24,16},{1,25},{9,1},{17,9},{25,17},{2,26},{10... | collective-permute-start | bytes 2359304 | tf_op jit(solution)/shard_map/ppermute | solution.py:44
  97.8 11.9 %collective-permute-start.27 = (bf16[192,512]{1,0:T(8,128)(2,1)S(1)}, bf16[192,512]{1,0:T(8,128)(2,1)S(1)}, u32[]{:S(2)}, u32[]{:S(2)}) collective-permute-start(bf16[192,512]{1,0:T(8,128)(2,1)S(1)} %get-tuple-element.94), channel_id=1, source_target_pairs={{0,1},{1,2},{2,3},{3,0},{4,5},{5,6},{6,7},{7,4},{8,9},{9,10},{10,1... | collective-permute-start | bytes 589832 | tf_op jit(solution)/shard_map/ppermute | solution.py:52
  98.7 11.0 %collective-permute-start.28 = (bf16[192,512]{1,0:T(8,128)(2,1)S(1)}, bf16[192,512]{1,0:T(8,128)(2,1)S(1)}, u32[]{:S(2)}, u32[]{:S(2)}) collective-permute-start(bf16[192,512]{1,0:T(8,128)(2,1)S(1)} %get-tuple-element.95), channel_id=1, source_target_pairs={{0,3},{1,0},{2,1},{3,2},{4,7},{5,4},{6,5},{7,6},{8,11},{9,8},{10,9... | collective-permute-start | bytes 589832 | tf_op jit(solution)/shard_map/ppermute | solution.py:52
  100.9 13.5 %collective-permute-start.33 = (bf16[192,512]{1,0:T(8,128)(2,1)S(1)}, bf16[192,512]{1,0:T(8,128)(2,1)S(1)}, u32[]{:S(2)}, u32[]{:S(2)}) collective-permute-start(bf16[192,512]{1,0:T(8,128)(2,1)S(1)} %get-tuple-element.101), channel_id=1, source_target_pairs={{0,2},{1,3},{2,0},{3,1},{4,6},{5,7},{6,4},{7,5},{8,10},{9,11},{10,... | collective-permute-start | bytes 589832 | tf_op jit(solution)/shard_map/ppermute | solution.py:52
  109.7 13.6 %collective-permute-start.31 = (bf16[2,3,128,2,256]{4,3,2,1,0:T(2,128)(2,1)S(1)}, bf16[2,3,128,2,256]{4,3,2,1,0:T(2,128)(2,1)S(1)}, u32[]{:S(2)}, u32[]{:S(2)}) collective-permute-start(bf16[2,3,128,2,256]{4,3,2,1,0:T(2,128)(2,1)S(1)} %collective-permute-done.23.refs_1_), channel_id=1, source_target_pairs={{0,4},{4,0},{1,5},{5,1},{2,6},{6,2},{3,7},{7,3},{8,12},{12,8},{9,1... | collective-permute-start | bytes 2359304 | tf_op jit(solution)/shard_map/ppermute | solution.py:60
  111.0 12.2 %collective-permute-start.32 = (bf16[2,3,128,2,256]{4,3,2,1,0:T(2,128)(2,1)S(1)}, bf16[2,3,128,2,256]{4,3,2,1,0:T(2,128)(2,1)S(1)}, u32[]{:S(2)}, u32[]{:S(2)}) collective-permute-start(bf16[2,3,128,2,256]{4,3,2,1,0:T(2,128)(2,1)S(1)} %collective-permute-done.24.refs_2_), channel_id=1, source_target_pairs={{0,4},{4,0},{1,5},{5,1},{2,6},{6,2},{3,7},{7,3},{8,12},{12,8},{9,1... | collective-permute-start | bytes 2359304 | tf_op jit(solution)/shard_map/ppermute | solution.py:60
  111.7 11.6 %collective-permute-start.29 = (bf16[3,128,2,256]{3,2,1,0:T(2,128)(2,1)S(1)}, bf16[3,128,2,256]{3,2,1,0:T(2,128)(2,1)S(1)}, u32[]{:S(2)}, u32[]{:S(2)}) collective-permute-start(bf16[3,128,2,256]{3,2,1,0:T(2,128)(2,1)S(1)} %slice_bitcast_fusion.1), channel_id=1, source_target_pairs={{0,8},{8,16},{16,24},{24,0},{1,9},{9,17},{17,25},{25,1},{2,10},{10... | collective-permute-start | bytes 1179656 | tf_op jit(solution)/shard_map/ppermute | solution.py:44
  111.8 11.4 %collective-permute-start.30 = (bf16[3,128,2,256]{3,2,1,0:T(2,128)(2,1)S(1)}, bf16[3,128,2,256]{3,2,1,0:T(2,128)(2,1)S(1)}, u32[]{:S(2)}, u32[]{:S(2)}) collective-permute-start(bf16[3,128,2,256]{3,2,1,0:T(2,128)(2,1)S(1)} %slice_bitcast_fusion), channel_id=1, source_target_pairs={{0,24},{8,0},{16,8},{24,16},{1,25},{9,1},{17,9},{25,17},{2,26},{10... | collective-permute-start | bytes 1179656 | tf_op jit(solution)/shard_map/ppermute | solution.py:44
  123.3 4.3 %collective-permute-start.34 = (bf16[3,128,2,256]{3,2,1,0:T(2,128)(2,1)S(1)}, bf16[3,128,2,256]{3,2,1,0:T(2,128)(2,1)S(1)}, u32[]{:S(2)}, u32[]{:S(2)}) collective-permute-start(bf16[3,128,2,256]{3,2,1,0:T(2,128)(2,1)S(1)} %collective-permute-done.29), channel_id=1, source_target_pairs={{0,4},{4,0},{1,5},{5,1},{2,6},{6,2},{3,7},{7,3},{8,12},{12,8},{9,1... | collective-permute-start | bytes 1179656 | tf_op jit(solution)/shard_map/ppermute | solution.py:60
  124.6 3.0 %collective-permute-start.35 = (bf16[3,128,2,256]{3,2,1,0:T(2,128)(2,1)S(1)}, bf16[3,128,2,256]{3,2,1,0:T(2,128)(2,1)S(1)}, u32[]{:S(2)}, u32[]{:S(2)}) collective-permute-start(bf16[3,128,2,256]{3,2,1,0:T(2,128)(2,1)S(1)} %collective-permute-done.30), channel_id=1, source_target_pairs={{0,4},{4,0},{1,5},{5,1},{2,6},{6,2},{3,7},{7,3},{8,12},{12,8},{9,1... | collective-permute-start | bytes 1179656 | tf_op jit(solution)/shard_map/ppermute | solution.py:60
  (2 other events, 4.0 us)
